TPU v7x, 128 devices: a whole 4x4x4 slice. The times are simulated.
128 devices in a mesh: expert: 4 (over y), dp: 32 (over x, z, core).
Axes of the slice: x: 4, y: 4, z: 4, core: 2. Of those that a mesh axis runs over, the one named last changes fastest.
Arguments:
- pool_tokens: bfloat16 [65536, 2048], P('dp', 'expert'), may hold values from -6 to 6
- pool_cotangent: bfloat16 [65536, 2048], P('dp', 'expert'), may hold values from -6 to 6
- token_ids: int32 [4, 16384], P('expert', 'dp'), may hold values from 0 to 2047, as said below
- route_weights: float32 [4, 16384], P('expert', 'dp'), may hold values from 0.1 to 1
- gate_weight: float32 [4, 2048, 512], P('expert', 'dp'), may hold values from -0.125 to 0.125
- up_weight: float32 [4, 2048, 512], P('expert', 'dp'), may hold values from -0.125 to 0.125
- down_weight: float32 [4, 512, 2048], P('expert', 'dp'), may hold values from -0.25 to 0.25
- momentum_gate: float32 [4, 2048, 512], P('expert', 'dp'), may hold values from -0.6 to 0.6
- momentum_up: float32 [4, 2048, 512], P('expert', 'dp'), may hold values from -0.6 to 0.6
- momentum_down: float32 [4, 512, 2048], P('expert', 'dp'), may hold values from -0.6 to 0.6
Outputs:
- new_gate: float32 [4, 2048, 512], P('expert', 'dp')
- new_up: float32 [4, 2048, 512], P('expert', 'dp')
- new_down: float32 [4, 512, 2048], P('expert', 'dp')
- new_momentum_gate: float32 [4, 2048, 512], P('expert', 'dp')
- new_momentum_up: float32 [4, 2048, 512], P('expert', 'dp')
- new_momentum_down: float32 [4, 512, 2048], P('expert', 'dp')
- pool_grad: float32 [65536, 2048], P('dp', 'expert')
Inputs may be any that keep to these rules, and one draw needn't show every extreme that they name: `token_ids`: within one expert's 512 slots of one dp index the ids are distinct rows of that index's pool.
All inputs are finite; a program needn't handle non-finite values.
Results may differ from a plain program's by a relative error of at most 0.0066.
Values may be sent and summed in bfloat16 or wider, within the bound.
No kernel may reach another device: no remote copies, remote signals or barrier semaphores. Data moves between devices by JAX's collectives and lax.ppermute only.
A program may use at most 128 MiB of HBM per device.

v0:
```python
import jax
import jax.numpy as jnp
from jax import lax
from jax.sharding import PartitionSpec as P

TOK_DEV = 512
POOL = 2048


momentum_decay = 0.9
learning_rate = 0.05
epsilon = 1e-06


def sent_together(arrays, axis, dim, along):
    widths = [a.shape[along] for a in arrays]
    both = jnp.concatenate(arrays, axis=along)
    result = lax.all_gather(both, axis, axis=dim, tiled=True)
    return tuple(jnp.split(result, [sum(widths[:k]) for k in range(1, len(widths))], axis=along))


def partner(block, axis, distance):
    count = lax.axis_size(axis)
    route = []
    for low in range(count):
        high = low | 1 << distance
        if high != low and high < count:
            route += [(low, high), (high, low)]
    return lax.ppermute(block, axis, route)


def moment_terms(left_part, right_part):
    inner = jnp.sum(left_part * right_part, axis=(1, 2))
    norm_left = jnp.sum(left_part * left_part, axis=(1, 2))
    norm_right = jnp.sum(right_part * right_part, axis=(1, 2))
    return jnp.stack([inner, norm_left, norm_right], axis=1)


def adasum_merge(left_part, right_part, moments):
    coef_left = 1.0 - moments[:, 0] / (2.0 * (moments[:, 1] + epsilon))
    coef_right = 1.0 - moments[:, 0] / (2.0 * (moments[:, 2] + epsilon))
    return coef_left[:, None, None] * left_part + coef_right[:, None, None] * right_part


def local(
    pool_tokens,
    pool_cotangent,
    token_ids,
    route_weights,
    gate_weight,
    up_weight,
    down_weight,
    momentum_gate,
    momentum_up,
    momentum_down,
):
    pool_x, pool_c = sent_together((pool_tokens, pool_cotangent), "expert", 1, 0)
    gate_full, up_full, down_full = (
        *sent_together(
            (gate_weight[0].astype(jnp.bfloat16), up_weight[0].astype(jnp.bfloat16)), "dp", 0, 1
        ),
        lax.all_gather(down_weight[0].astype(jnp.bfloat16), "dp", axis=0, tiled=True),
    )
    row_ids = token_ids[0]
    route = route_weights[0]
    routed = pool_x[row_ids]
    cot_rows = pool_c[row_ids]
    gate_pre = jnp.dot(routed, gate_full, preferred_element_type=jnp.float32)
    up_pre = jnp.dot(routed, up_full, preferred_element_type=jnp.float32)
    sig = jax.nn.sigmoid(gate_pre)
    act = gate_pre * sig
    hidden = (act * up_pre).astype(jnp.bfloat16)
    scaled_cot = (route[:, None] * cot_rows.astype(jnp.float32)).astype(jnp.bfloat16)
    grad_down = (
        lax.dot_general(
            hidden, scaled_cot, (((0,), (0,)), ((), ())), preferred_element_type=jnp.float32
        )
        / TOK_DEV
    )
    hidden_grad = lax.dot_general(
        scaled_cot, down_full, (((1,), (1,)), ((), ())), preferred_element_type=jnp.float32
    )
    gate_grad = (hidden_grad * up_pre * sig * (1.0 + gate_pre * (1.0 - sig))).astype(jnp.bfloat16)
    up_grad = (hidden_grad * act).astype(jnp.bfloat16)
    grad_gate = (
        lax.dot_general(
            routed, gate_grad, (((0,), (0,)), ((), ())), preferred_element_type=jnp.float32
        )
        / TOK_DEV
    )
    grad_up = (
        lax.dot_general(
            routed, up_grad, (((0,), (0,)), ((), ())), preferred_element_type=jnp.float32
        )
        / TOK_DEV
    )
    slot_grad = lax.dot_general(
        gate_grad, gate_full, (((1,), (1,)), ((), ())), preferred_element_type=jnp.float32
    )
    slot_grad = slot_grad + lax.dot_general(
        up_grad, up_full, (((1,), (1,)), ((), ())), preferred_element_type=jnp.float32
    )
    pool_term = jax.ops.segment_sum(slot_grad, row_ids, num_segments=POOL)
    pool_grad = lax.psum_scatter(pool_term, "expert", scatter_dimension=1, tiled=True)
    block_count = lax.axis_size("dp")
    tiers = block_count.bit_length() - 1
    position = lax.axis_index("dp")
    pieces = jnp.stack([grad_gate.reshape(-1), grad_up.reshape(-1), grad_down.reshape(-1)]).reshape(
        3, block_count, -1
    )
    first_tier = 0
    for tier_index in range(first_tier, tiers):
        own_bit = position >> tier_index & 1
        paired = pieces.reshape(3, pieces.shape[1] // 2, 2, -1)
        kept_half = jnp.where(own_bit == 0, paired[:, :, 0], paired[:, :, 1])
        sent_half = jnp.where(own_bit == 0, paired[:, :, 1], paired[:, :, 0])
        received = partner(sent_half, "dp", tier_index)
        left_part = jnp.where(own_bit == 0, kept_half, received)
        right_part = jnp.where(own_bit == 0, received, kept_half)
        partial_value = moment_terms(left_part, right_part)
        summed = partial_value
        for step_bit in range(tier_index + 1):
            summed = summed + partner(summed, "dp", step_bit)
        pieces = adasum_merge(left_part, right_part, summed)
    owned = pieces[:, 0]
    next_gate = momentum_decay * momentum_gate[0] + owned[0].reshape(
        momentum_gate.shape[1], momentum_gate.shape[2]
    )
    next_up = momentum_decay * momentum_up[0] + owned[1].reshape(
        momentum_up.shape[1], momentum_up.shape[2]
    )
    next_down = momentum_decay * momentum_down[0] + owned[2].reshape(
        momentum_down.shape[1], momentum_down.shape[2]
    )
    new_gate = gate_weight[0] - learning_rate * next_gate
    new_up = up_weight[0] - learning_rate * next_up
    new_down = down_weight[0] - learning_rate * next_down
    return (
        new_gate[None],
        new_up[None],
        new_down[None],
        next_gate[None],
        next_up[None],
        next_down[None],
        pool_grad,
    )


def solution(mesh):
    in_specs = (
        P("dp", "expert"),
        P("dp", "expert"),
        P("expert", "dp"),
        P("expert", "dp"),
        P("expert", "dp", None),
        P("expert", "dp", None),
        P("expert", "dp", None),
        P("expert", "dp", None),
        P("expert", "dp", None),
        P("expert", "dp", None),
    )
    out_specs = (
        P("expert", "dp", None),
        P("expert", "dp", None),
        P("expert", "dp", None),
        P("expert", "dp", None),
        P("expert", "dp", None),
        P("expert", "dp", None),
        P("dp", "expert"),
    )
    return jax.shard_map(local, mesh=mesh, in_specs=in_specs, out_specs=out_specs, check_vma=False)
```

profile of v0, /device:TPU:1, one launch (start us, length us, event | category | flops | bytes accessed | tf_op | source)
XLA Modules:
  0.0 645.5 jit_solution(4517903335815897739)
XLA Ops:
  7.2 4.5 pad_maximum_fusion
  14.2 154.9 %all-gather.5.cloned.1.call-done = bf16[4096,2048]{1,0:T(8,128)(2,1)} async-done(((bf16[4096,512]{1,0:T(8,128)(2,1)}), bf16[4096,2048]{1,0:T(8,128)(2,1)}) %all-gather.5.cloned.1.call-update) | async-done | bytes 16777232 | tf_op jit(solution)/shard_map/all_gather | solution.py:18
  169.2 11.8 %fusion.26 = (bf16[2048,2048]{1,0:T(8,128)(2,1)}, bf16[2048,2048]{1,0:T(8,128)(2,1)}) fusion(bf16[4096,2048]{1,0:T(8,128)(2,1)} %all-gather.5.cloned.1.call-done), kind=kLoop, calls=%fused_computation.122 | loop fusion | bytes 33554432 | tf_op jit(solution)/shard_map/split | solution.py:19
  181.0 9.0 %gather_fusion = bf16[512,2048]{1,0:T(8,128)(2,1)S(1)} fusion(bf16[2048,2048]{1,0:T(8,128)(2,1)} %get-tuple-element.42, s32[1024]{0:T(1024)S(1)} %pad_clamp_fusion), kind=kCustom, calls=%fused_computation | custom fusion | bytes 4196352 | tf_op jit(solution)/shard_map/gather | solution.py:66
  190.0 9.9 %gather_fusion.1 = bf16[512,2048]{1,0:T(8,128)(2,1)} fusion(bf16[2048,2048]{1,0:T(8,128)(2,1)} %get-tuple-element.41, s32[1024]{0:T(1024)S(1)} %pad_clamp_fusion), kind=kCustom, calls=%fused_computation.1 | custom fusion | bytes 4196352 | tf_op jit(solution)/shard_map/gather | solution.py:67
  199.9 20.0 %all-gather.7.cloned.1.call-done = bf16[2048,1024]{1,0:T(8,128)(2,1)} async-done(((bf16[64,1024]{1,0:T(8,128)(2,1)}), bf16[2048,1024]{1,0:T(8,128)(2,1)}) %all-gather.7.cloned.1.call-update) | async-done | bytes 4194320 | tf_op jit(solution)/shard_map/all_gather | solution.py:18
  219.9 3.0 fusion.12
  225.1 3.5 convolution_multiply_fusion
  228.6 37.4 %all-gather.9.cloned.1.call-done = bf16[1,512,2048]{2,1,0:T(8,128)(2,1)} async-done(((bf16[1,16,2048]{2,1,0:T(8,128)(2,1)}), bf16[1,512,2048]{2,1,0:T(8,128)(2,1)}) %all-gather.9.cloned.1.call-update) | async-done | bytes 2097168 | tf_op jit(solution)/shard_map/all_gather | solution.py:62
  266.0 4.4 multiply_convert_fusion.2
  271.2 3.3 convolution_multiply_fusion.1
  274.5 6.6 %stack.70 = f32[1,16,2,32768]{3,2,1,0:T(2,128)} reshape(f32[2048,512]{1,0:T(8,128)} %convolution_multiply_fusion.1) | data formatting | bytes 8388608 | tf_op jit(solution)/shard_map/stack | solution.py:108
  281.1 3.3 convolution_multiply_fusion.2
  284.4 6.6 %stack.69 = f32[1,16,2,32768]{3,2,1,0:T(2,128)} reshape(f32[2048,512]{1,0:T(8,128)} %convolution_multiply_fusion.2) | data formatting | bytes 8388608 | tf_op jit(solution)/shard_map/stack | solution.py:108
  291.0 6.6 %copy_dynamic-update-slice_fusion.2 = f32[3,16,2,32768]{3,1,0,2:T(8,128)} fusion(f32[1,16,2,32768]{3,2,1,0:T(2,128)} %stack.69), kind=kLoop, calls=%fused_computation.17 | loop fusion | bytes 8388608
  297.7 6.8 %stack.71 = f32[1,16,2,32768]{3,2,1,0:T(2,128)} reshape(f32[512,2048]{1,0:T(8,128)} %convolution_multiply_fusion) | data formatting | bytes 8388608 | tf_op jit(solution)/shard_map/stack | solution.py:108
  304.4 6.8 %copy_dynamic-update-slice_fusion.1 = f32[3,16,2,32768]{3,1,0,2:T(8,128)} fusion(f32[3,16,2,32768]{3,1,0,2:T(8,128)} %copy_dynamic-update-slice_fusion.2, f32[1,16,2,32768]{3,2,1,0:T(2,128)} %stack.70), kind=kLoop, calls=%fused_computation.16 | loop fusion | bytes 8388608
  311.3 4.4 copy_dynamic-update-slice_fusion
  315.7 7.8 %select_bitcast_fusion = f32[3,16,32768]{2,1,0:T(8,128)} fusion(f32[3,16,2,32768]{3,1,0,2:T(8,128)} %copy_dynamic-update-slice_fusion, pred[]{:T(512)S(6)} %eq.14), kind=kLoop, calls=%fused_computation.11 | loop fusion | flops 1572864 | bytes 18874368 | tf_op jit(solution)/shard_map/jit(_where)/select_n | solution.py:116
  323.8 10.3 %collective-permute-done = f32[3,16,32768]{2,1,0:T(8,128)} collective-permute-done((f32[3,16,32768]{2,1,0:T(8,128)}, f32[3,16,32768]{2,1,0:T(8,128)}, u32[]{:S(2)}, u32[]{:S(2)}) %collective-permute-start) | collective-permute-done | bytes 6291488 | tf_op jit(solution)/shard_map/ppermute | solution.py:29
  334.0 7.9 %multiply_reduce_fusion.2 = (f32[3]{0:T(128)S(1)}, f32[3]{0:T(128)S(1)}, f32[3]{0:T(128)S(1)}, f32[3,16,32768]{2,1,0:T(8,128)S(1)}, f32[3,16,32768]{2,1,0:T(8,128)S(1)}) fusion(f32[3,16,32768]{2,1,0:T(8,128)} %collective-permute-done, f32[3,16,2,32768]{3,1,0,2:T(8,128)} %copy_dynamic-update-slice_fusion, pred[]{:T(512)S(6)} %eq.14), kind=kLoop, calls=%fused_computation.10 | loop fusion | flops 14155767 | bytes 31458340 | tf_op jit(solution)/shard_map/reduce_sum | solution.py:33
  343.3 3.4 multiply_add_fusion
  346.6 8.6 %reshape.330 = f32[3,8,2,32768]{3,2,1,0:T(2,128)} reshape(f32[3,16,32768]{2,1,0:T(8,128)} %multiply_add_fusion) | data formatting | bytes 12582912 | tf_op jit(solution)/shard_map/reshape | solution.py:114
  355.2 11.1 %fusion.27 = (f32[3,8,1,32768]{3,2,1,0:T(1,128)S(1)}, f32[3,8,1,32768]{3,2,1,0:T(1,128)S(1)}, f32[3,8,1,32768]{3,2,1,0:T(1,128)}) fusion(f32[3,8,2,32768]{3,2,1,0:T(2,128)} %reshape.330, pred[]{:T(512)S(6)} %eq.13), kind=kLoop, calls=%fused_computation.123 | loop fusion | flops 786432 | bytes 15728641 | tf_op jit(solution)/shard_map/slice | solution.py:115
  366.4 3.5 copy.141
  370.7 68.9 %collective-permute-done.2 = f32[3,8,32768]{2,1,0:T(8,128)} collective-permute-done((f32[3,8,32768]{2,1,0:T(8,128)}, f32[3,8,32768]{2,1,0:T(8,128)}, u32[]{:S(2)}, u32[]{:S(2)}) %collective-permute-start.2) | collective-permute-done | bytes 3145760 | tf_op jit(solution)/shard_map/ppermute | solution.py:29
  439.6 6.8 %multiply_reduce_fusion.5 = (f32[3]{0:T(128)S(1)}, f32[3]{0:T(128)S(1)}, f32[3]{0:T(128)S(1)}, f32[3,8,32768]{2,1,0:T(8,128)S(1)}, f32[3,8,32768]{2,1,0:T(8,128)S(1)}) fusion(f32[3,8,32768]{2,1,0:T(8,128)} %collective-permute-done.2, f32[3,8,1,32768]{3,2,1,0:T(1,128)} %get-tuple-element.45, f32[3,8,1,32768]{3,2,1,0:T(1,128)S(1)} %get-tuple-element.43, ...), kind=kLoop, calls=%fused_computation.29 | loop fusion | flops 7077879 | bytes 15728677 | tf_op jit(solution)/shard_map/reduce_sum | solution.py:33
  451.3 3.4 reshape.331
  454.7 6.0 fusion.28
  460.7 2.2 copy.142
  464.9 5.1 fusion.10
  470.1 3.3 fusion.6
  473.4 17.1 %scatter_custom_fusion = f32[2048,2048]{1,0:T(8,128)} fusion(s32[512]{0:T(512)S(1)} %bitcast.175, f32[]{:T(128)} %constant.7.clone.1, f32[512,2048]{1,0:T(8,128)} %fusion.6, f32[512,2048]{1,0:T(8,128)} %fusion.10), kind=kCustom, calls=%fused_computation.3 | custom fusion | flops 2097152 | bytes 25165828 | tf_op jit(solution)/shard_map/scatter-add | solution.py:103
  490.5 8.6 %collective-permute-done.5 = f32[3,4,32768]{2,1,0:T(4,128)} collective-permute-done((f32[3,4,32768]{2,1,0:T(4,128)}, f32[3,4,32768]{2,1,0:T(4,128)}, u32[]{:S(2)}, u32[]{:S(2)}) %collective-permute-start.5) | collective-permute-done | bytes 1572896 | tf_op jit(solution)/shard_map/ppermute | solution.py:29
  499.1 5.1 multiply_reduce_fusion.8
  504.3 2.1 collective-permute-start.6
  510.1 2.4 collective-permute-start.8
  519.6 16.0 %collective-permute-done.9 = f32[3,2,32768]{2,1,0:T(2,128)S(1)} collective-permute-done((f32[3,2,32768]{2,1,0:T(2,128)S(1)}, f32[3,2,32768]{2,1,0:T(2,128)S(1)}, u32[]{:S(2)}, u32[]{:S(2)}) %collective-permute-start.9) | collective-permute-done | bytes 786464 | tf_op jit(solution)/shard_map/ppermute | solution.py:29
  535.5 2.4 multiply_reduce_fusion.11
  537.9 3.1 collective-permute-start.10
  544.8 2.5 collective-permute-start.12
  552.6 2.3 collective-permute-start.14
  554.9 6.9 %collective-permute-done.14 = f32[3,1,32768]{2,1,0:T(1,128)S(1)} collective-permute-done((f32[3,1,32768]{2,1,0:T(1,128)S(1)}, f32[3,1,32768]{2,1,0:T(1,128)S(1)}, u32[]{:S(2)}, u32[]{:S(2)}) %collective-permute-start.14) | collective-permute-done | bytes 393248 | tf_op jit(solution)/shard_map/ppermute | solution.py:29
  561.8 2.1 multiply_reduce_fusion.14
  563.9 4.0 collective-permute-start.15
  571.9 2.7 collective-permute-start.17
  576.6 2.1 collective-permute-done.18
  586.5 52.0 %reduce-scatter.2.cloned.1.call-done = f32[2048,512]{1,0:T(8,128)} async-done(((f32[2048,2048]{1,0:T(8,128)}), f32[2048,512]{1,0:T(8,128)}) %reduce-scatter.2.cloned.1.call-update) | async-done | bytes 4194320 | tf_op jit(solution)/shard_map/reduce_scatter | solution.py:104
  (115 shorter events, 48.4 us)
Async XLA Ops:
  7.2 162.0 %all-gather.5.cloned.1.call-start = ((), (), s32[]{:S(2)}) async-start(), calls=%async_computation.1 | async-start | bytes 20971520 | tf_op jit(solution)/shard_map/all_gather | solution.py:18
  11.7 0.9 copy-start.7
  11.7 1.0 copy-start.8
  11.7 1.7 copy-start.9
  11.7 2.5 copy-start.13
  11.8 208.1 %all-gather.7.cloned.1.call-start = ((), (), s32[]{:S(2)}) async-start(), calls=%async_computation.2 | async-start | bytes 4325376 | tf_op jit(solution)/shard_map/all_gather | solution.py:18
  13.4 252.6 %all-gather.9.cloned.1.call-start = ((), (), s32[]{:S(2)}) async-start(), calls=%async_computation.4 | async-start | bytes 2162688 | tf_op jit(solution)/shard_map/all_gather | solution.py:62
  14.1 624.4 %reduce-scatter.2.cloned.1.call-start = ((), (), s32[]{:S(2)}) async-start(), calls=%async_computation.3 | async-start | bytes 20971520 | tf_op jit(solution)/shard_map/reduce_scatter | solution.py:104
  219.9 3.0 copy-start.1
  222.9 1.3 copy-start.15
  222.9 2.3 copy-start.6
  222.9 2.3 copy-start.14
  224.2 1.0 copy-start.16
  270.4 0.8 copy-start.5
  270.4 10.7 %copy-start.3 = (bf16[512,512]{1,0:T(8,128)(2,1)}, bf16[512,512]{1,0:T(8,128)(2,1)S(1)}, u32[]{:S(2)}) copy-start(bf16[512,512]{1,0:T(8,128)(2,1)S(1)} %get-tuple-element.50) | copy-start | bytes 1572868
  304.4 6.8 %copy-start = (f32[1,16,2,32768]{3,2,1,0:T(2,128)S(1)}, f32[1,16,2,32768]{3,2,1,0:T(2,128)}, u32[]{:S(2)}) copy-start(f32[1,16,2,32768]{3,2,1,0:T(2,128)} %stack.71) | copy-start | bytes 12582916
  323.5 10.5 %collective-permute-start = (f32[3,16,32768]{2,1,0:T(8,128)}, f32[3,16,32768]{2,1,0:T(8,128)}, u32[]{:S(2)}, u32[]{:S(2)}) collective-permute-start(f32[3,16,32768]{2,1,0:T(8,128)} %select_bitcast_fusion), channel_id=1, source_target_pairs={{0,1},{1,0},{2,3},{3,2},{4,5},{5,4},{6,7},{7,6},{8,9},{9,8},{10,11... | collective-permute-start | bytes 18874376 | tf_op jit(solution)/shard_map/ppermute | solution.py:29
  342.0 1.2 collective-permute-start.1
  369.8 69.8 %collective-permute-start.2 = (f32[3,8,32768]{2,1,0:T(8,128)}, f32[3,8,32768]{2,1,0:T(8,128)}, u32[]{:S(2)}, u32[]{:S(2)}) collective-permute-start(f32[3,8,32768]{2,1,0:T(8,128)} %bitcast.128), channel_id=1, source_target_pairs={{0,2},{2,0},{1,3},{3,1},{4,6},{6,4},{5,7},{7,5},{8,10},{10,8},{9,1... | collective-permute-start | bytes 9437192 | tf_op jit(solution)/shard_map/ppermute | solution.py:29
  446.4 2.0 collective-permute-start.3
  448.4 2.5 collective-permute-start.4
  462.9 36.2 %collective-permute-start.5 = (f32[3,4,32768]{2,1,0:T(4,128)}, f32[3,4,32768]{2,1,0:T(4,128)}, u32[]{:S(2)}, u32[]{:S(2)}) collective-permute-start(f32[3,4,32768]{2,1,0:T(4,128)} %bitcast.129), channel_id=1, source_target_pairs={{0,4},{4,0},{1,5},{5,1},{2,6},{6,2},{3,7},{7,3},{8,12},{12,8},{9,1... | collective-permute-start | bytes 4718600 | tf_op jit(solution)/shard_map/ppermute | solution.py:29
  464.9 5.1 copy-start.2
  464.9 5.1 copy-start.4
  504.3 2.9 collective-permute-start.6
  507.2 2.9 collective-permute-start.7
  510.1 4.3 collective-permute-start.8
  518.5 17.0 %collective-permute-start.9 = (f32[3,2,32768]{2,1,0:T(2,128)S(1)}, f32[3,2,32768]{2,1,0:T(2,128)S(1)}, u32[]{:S(2)}, u32[]{:S(2)}) collective-permute-start(f32[3,2,32768]{2,1,0:T(2,128)S(1)} %bitcast.131), channel_id=1, source_target_pairs={{0,8},{8,0},{1,9},{9,1},{2,10},{10,2},{3,11},{11,3},{4,12},{12,4},... | collective-permute-start | bytes 2359304 | tf_op jit(solution)/shard_map/ppermute | solution.py:29
  537.9 4.0 collective-permute-start.10
  541.9 2.9 collective-permute-start.11
  544.8 4.0 collective-permute-start.12
  548.8 2.8 collective-permute-start.13
  552.2 32.1 %copy-start.10 = (f32[1,64,512]{2,1,0:T(8,128)S(1)}, f32[1,64,512]{2,1,0:T(8,128)}, u32[]{:S(2)}) copy-start(f32[1,64,512]{2,1,0:T(8,128)} %param.18) | copy-start | bytes 393220
  552.2 32.9 %copy-start.11 = (f32[1,64,512]{2,1,0:T(8,128)S(1)}, f32[1,64,512]{2,1,0:T(8,128)}, u32[]{:S(2)}) copy-start(f32[1,64,512]{2,1,0:T(8,128)} %param.17) | copy-start | bytes 393220
  552.6 33.2 %copy-start.12 = (f32[1,16,2048]{2,1,0:T(8,128)S(1)}, f32[1,16,2048]{2,1,0:T(8,128)}, u32[]{:S(2)}) copy-start(f32[1,16,2048]{2,1,0:T(8,128)} %param.19) | copy-start | bytes 393220
  552.6 9.2 %collective-permute-start.14 = (f32[3,1,32768]{2,1,0:T(1,128)S(1)}, f32[3,1,32768]{2,1,0:T(1,128)S(1)}, u32[]{:S(2)}, u32[]{:S(2)}) collective-permute-start(f32[3,1,32768]{2,1,0:T(1,128)S(1)} %fusion.18), channel_id=1, source_target_pairs={{0,16},{16,0},{1,17},{17,1},{2,18},{18,2},{3,19},{19,3},{4,20},{20... | collective-permute-start | bytes 1179656 | tf_op jit(solution)/shard_map/ppermute | solution.py:29
  563.9 4.8 collective-permute-start.15
  568.8 3.1 collective-permute-start.16
  571.9 4.0 collective-permute-start.17
  575.9 2.8 collective-permute-start.18
  578.8 3.9 collective-permute-start.19
Sparse Core Ops, SparseCore 0:
  11.9 157.2 all-gather.4
  172.0 47.8 all-gather.6
  222.7 43.2 all-gather.8
  490.6 147.8 reduce-scatter.1
where the time goes:
time: 652 us; the launch traced here: 646 us
  waiting for transfers between devices  396 us (61%)
  local copies, waits for them, and re-layouts  91.8 us (14%)
  other arithmetic  82.1 us (13%)
  starting transfers between devices  33.6 us (5%)
  matrix products  27.2 us (4%)
  between operations  14.6 us (2%)
    all_gather x2, waiting for transfers between devices, sent_together(): result = lax.all_gather(both, axis, axis=dim, tiled=True)  175 us
    ppermute x20, waiting for transfers between devices, partner(): return lax.ppermute(block, axis, route)  132 us
    reduce_scatter x1, waiting for transfers between devices, local(): lax.psum_scatter(pool_term, 'expert', scatter_dimension=1, tiled=True)  52 us
    all_gather x1, waiting for transfers between devices, local(): lax.all_gather(down_weight[0].astype(jnp.bfloat16), 'dp', axis=0, tiled=T...  37.4 us
    ppermute x20, starting transfers between devices, partner(): return lax.ppermute(block, axis, route)  33.4 us
    another operation x4, local copies, waits for them, and re-layouts, local(): jnp.stack([grad_gate.reshape(-1), grad_up.reshape(-1), grad_down.reshape(...  24.4 us
    reduce_sum x5, other arithmetic, moment_terms(): inner = jnp.sum(left_part * right_part, axis=(1, 2))  24.3 us
    unnamed x39, local copies, waits for them, and re-layouts  22.4 us
  transfers between devices with their start and end apart: 24, of which 24 were waited for; matrix products, arithmetic and copies ran while one was open for 13% of the time, Pallas kernels for 0%

commit v1 on v0

v1 whole, which is shorter than its diff:
```python
import jax
import jax.numpy as jnp
from jax import lax
from jax.experimental import pallas as pl
from jax.experimental.pallas import tpu as pltpu
from jax.sharding import PartitionSpec as P

TOK_DEV = 512
POOL = 2048
D = 2048
H = 512
N_EXPERT = 4
N_CHIP = 16
SLICE = 512
ROWS = 192

momentum_decay = 0.9
learning_rate = 0.05
epsilon = 1e-06

MIB = 1 << 20
F32 = jnp.float32
BF16 = jnp.bfloat16
NT = (((1,), (1,)), ((), ()))


def vmem():
    return pl.BlockSpec(memory_space=pltpu.VMEM)


def call(body, name, n_in, out_shapes, flops, nbytes, scratch=(), limit=40):
    return pl.pallas_call(
        body,
        name=name,
        out_shape=out_shapes,
        in_specs=[vmem()] * n_in,
        out_specs=jax.tree.map(lambda _: vmem(), out_shapes),
        scratch_shapes=list(scratch),
        compiler_params=pltpu.CompilerParams(vmem_limit_bytes=limit * MIB),
        cost_estimate=pl.CostEstimate(flops=flops, bytes_accessed=nbytes, transcendentals=0),
    )


def struct(shape, dtype):
    return jax.ShapeDtypeStruct(shape, dtype)


def column(row):
    return jnp.broadcast_to(row, (128, row.shape[1])).T


def pick_rows(ids_rows, pools):
    n_ids, n_pool = len(ids_rows), len(pools)

    def body(*refs):
        ids, src = refs[:n_ids], refs[n_ids : n_ids + n_pool]
        out, hot = refs[n_ids + n_pool : -1], refs[-1]
        lane = lax.broadcasted_iota(jnp.int32, (TOK_DEV, 128), 1)
        for k in range(n_ids):
            named = column(ids[k][...])
            for j in range(POOL // 128):
                hot[:, 128 * j : 128 * (j + 1)] = jnp.where(named == lane + 128 * j, 1.0, 0.0).astype(BF16)
            for a in range(n_pool):
                rows = jnp.dot(hot[...], src[a][...], preferred_element_type=F32)
                out[k * n_pool + a][...] = rows.astype(BF16)

    shapes = [struct((TOK_DEV, SLICE), BF16)] * (n_ids * n_pool)
    return call(
        body,
        "pick_rows",
        n_ids + n_pool,
        shapes,
        2 * TOK_DEV * POOL * SLICE * n_ids * n_pool,
        (4 + 2 * n_ids) * MIB // 2,
        [pltpu.VMEM((TOK_DEV, POOL), BF16)],
    )(*ids_rows, *pools)


def slice_of(k):
    me = lax.axis_index("expert")
    return lax.rem(me + N_EXPERT - k, N_EXPERT)


def in_up_block(w, s):
    return w[pl.ds(pl.multiple_of(8 * s, 8), 8), 0:64, :].reshape(SLICE, 2 * H)


def down_block(w, s):
    row = pl.multiple_of(64 + 16 * (s // 2), 16)
    col = pl.multiple_of(SLICE * (s % 2), SLICE)
    return w[:, pl.ds(row, 16), pl.ds(col, SLICE)].reshape(H, SLICE)


def forward(tokens, weights):
    def body(x0, x1, x2, x3, w, hidden_t, gate_factor, act_out, xt, acc, hid):
        for k, x in enumerate((x0, x1, x2, x3)):
            part = jnp.dot(x[...], in_up_block(w, slice_of(k)), preferred_element_type=F32)
            if k == 0:
                acc[...] = part
            else:
                acc[...] += part
            xt[k] = x[...].T

        @pl.loop(0, TOK_DEV // 64)
        def _(i):
            rows = pl.ds(pl.multiple_of(i * 64, 64), 64)
            gate, up = acc[rows, :H], acc[rows, H:]
            sig = jax.nn.sigmoid(gate)
            act = gate * sig
            hid[rows, :] = (act * up).astype(BF16)
            gate_factor[rows, :] = up * sig * (1.0 + gate * (1.0 - sig))
            act_out[rows, :] = act

        hidden_t[...] = hid[...].T

    shapes = [
        struct((H, TOK_DEV), BF16),
        struct((TOK_DEV, H), F32),
        struct((TOK_DEV, H), F32),
        struct((N_EXPERT, SLICE, TOK_DEV), BF16),
    ]
    return call(
        body,
        "forward",
        5,
        shapes,
        2 * TOK_DEV * D * 2 * H,
        10 * MIB,
        [pltpu.VMEM((TOK_DEV, 2 * H), F32), pltpu.VMEM((TOK_DEV, H), BF16)],
    )(*tokens, weights)


def backward(cots, route, hidden_t, gate_factor, act, xt, weights):
    def body(c0, c1, c2, c3, route_ref, hid_t, factor, act_ref, xt_ref, w, keep, send, both, hg, scaled):
        first = lax.axis_index("dp") % 2 == 0
        scale = column(route_ref[...])
        for k, c in enumerate((c0, c1, c2, c3)):
            s = slice_of(k)
            for j in range(SLICE // 128):
                cols = slice(128 * j, 128 * (j + 1))
                scaled[:, cols] = (scale * c[:, cols].astype(F32)).astype(BF16)
            part = lax.dot_general(scaled[...], down_block(w, s), NT, preferred_element_type=F32)
            if k == 0:
                hg[...] = part
            else:
                hg[...] += part
            down = jnp.dot(hid_t[...], scaled[...], preferred_element_type=F32) / TOK_DEV
            down = down.astype(BF16).reshape(N_CHIP, 2, 16, SLICE)
            rows = pl.ds(pl.multiple_of(128 + 16 * s, 16), 16)
            keep[:, rows, :] = jnp.where(first, down[:, 0], down[:, 1])
            send[:, rows, :] = jnp.where(first, down[:, 1], down[:, 0])

        @pl.loop(0, TOK_DEV // 64)
        def _(i):
            rows = pl.ds(pl.multiple_of(i * 64, 64), 64)
            g = hg[rows, :]
            both[rows, :H] = (g * factor[rows, :]).astype(BF16)
            both[rows, H:] = (g * act_ref[rows, :]).astype(BF16)

        for k in range(N_EXPERT):
            chips = pl.ds(pl.multiple_of(4 * slice_of(k), 4), 4)
            grad = jnp.dot(xt_ref[k], both[...], preferred_element_type=F32) / TOK_DEV
            grad = grad.astype(BF16).reshape(4, 2, 64, 2 * H)
            for a in range(2):
                own = grad[:, 0, :, a * H : (a + 1) * H]
                other = grad[:, 1, :, a * H : (a + 1) * H]
                keep[chips, 64 * a : 64 * (a + 1), :] = jnp.where(first, own, other)
                send[chips, 64 * a : 64 * (a + 1), :] = jnp.where(first, other, own)

    shapes = [
        struct((N_CHIP, ROWS, SLICE), BF16),
        struct((N_CHIP, ROWS, SLICE), BF16),
        struct((TOK_DEV, 2 * H), BF16),
    ]
    return call(
        body,
        "backward",
        10,
        shapes,
        8 * TOK_DEV * D * H,
        20 * MIB,
        [pltpu.VMEM((TOK_DEV, H), F32), pltpu.VMEM((TOK_DEV, SLICE), BF16)],
    )(*cots, route, hidden_t, gate_factor, act, xt, weights)


def slot_gradients(both, weights):
    def body(both_ref, w, *out):
        for k in (2, 1, 3, 0):
            grad = lax.dot_general(both_ref[...], in_up_block(w, slice_of(k)), NT, preferred_element_type=F32)
            out[k][...] = grad.astype(BF16)

    shapes = [struct((TOK_DEV, SLICE), BF16)] * N_EXPERT
    return call(body, "slot_gradients", 2, shapes, 4 * TOK_DEV * D * H, 9 * MIB)(both, weights)


def pair_moments(own, other):
    def body(a_ref, b_ref, out):
        def step(q, sums):
            new = []
            for m in range(3):
                a = a_ref[q, 64 * m : 64 * (m + 1), :].astype(F32)
                b = b_ref[q, 64 * m : 64 * (m + 1), :].astype(F32)
                for t in (a * b, a * a, b * b):
                    t = jnp.sum(t.reshape(8, 8, SLICE), axis=0)
                    new.append(t[:, :128] + t[:, 128:256] + t[:, 256:384] + t[:, 384:])
            return tuple(s + n for s, n in zip(sums, new))

        sums = lax.fori_loop(0, N_CHIP, step, (jnp.zeros((8, 128), F32),) * 9)
        for j in range(9):
            out[j] = sums[j]

    return call(body, "pair_moments", 2, struct((9, 8, 128), F32), 9 * 2**20, 6 * MIB)(own, other)


def pair_merge(own, other, mine, theirs):
    def body(a_ref, b_ref, m_ref, t_ref, out):
        coefs = []
        for m in range(3):
            inner = jnp.sum(m_ref[3 * m] + t_ref[3 * m], keepdims=True)
            norm_a = jnp.sum(m_ref[3 * m + 1] + t_ref[3 * m + 2], keepdims=True)
            norm_b = jnp.sum(m_ref[3 * m + 2] + t_ref[3 * m + 1], keepdims=True)
            coef_a = 1.0 - inner / (2.0 * (norm_a + epsilon))
            coef_b = 1.0 - inner / (2.0 * (norm_b + epsilon))
            coefs.append((jnp.broadcast_to(coef_a, (64, SLICE)), jnp.broadcast_to(coef_b, (64, SLICE))))

        @pl.loop(0, N_CHIP)
        def _(q):
            for m in range(3):
                rows = slice(64 * m, 64 * (m + 1))
                a, b = a_ref[q, rows, :].astype(F32), b_ref[q, rows, :].astype(F32)
                out[q, rows, :] = (coefs[m][0] * a + coefs[m][1] * b).astype(BF16)

    return call(body, "pair_merge", 4, struct((N_CHIP, ROWS, SLICE), BF16), 9 * 2**20, 9 * MIB)(
        own, other, mine, theirs
    )


def gram(parts):
    def body(x, out):
        row = lax.broadcasted_iota(jnp.int32, (256, 256), 0)
        col = lax.broadcasted_iota(jnp.int32, (256, 256), 1)
        same = jnp.where(row % 16 == col % 16, 1.0, 0.0)
        fold = lax.broadcasted_iota(jnp.int32, (256, 128), 0) // 16
        fold = jnp.where(fold == lax.broadcasted_iota(jnp.int32, (256, 128), 1), 1.0, 0.0)
        for m in range(3):
            acc = None
            for b in range(4):
                at = 64 * m + 16 * b
                block = x[:, at : at + 16, :].reshape(256, SLICE)
                part = lax.dot_general(block, block, NT, preferred_element_type=F32)
                acc = part if acc is None else acc + part
            acc = jnp.sum((acc * same).reshape(16, 16, 256), axis=1)
            out[m] = jnp.dot(acc, fold, precision=lax.Precision.HIGHEST, preferred_element_type=F32)

    return call(body, "gram", 1, struct((3, 16, 128), F32), 12 * 2 * 256 * 256 * 512, 3 * MIB)(parts)


def finish(parts, products, gate, up, down, mom_gate, mom_up, mom_down):
    def body(x, g_ref, gate_w, up_w, down_w, gate_m, up_m, down_m, new_g, new_u, new_d, next_g, next_u, next_d):
        g = g_ref[...]
        i = lax.broadcasted_iota(jnp.int32, (3, 16, 128), 1)
        j = lax.broadcasted_iota(jnp.int32, (3, 16, 128), 2)
        c_col = jnp.ones((3, 16, 1), F32)
        c_row = jnp.ones((3, 1, 128), F32)
        for level in range(4):
            block_i, block_j = i >> level, j >> level
            same, sibling = block_i == block_j, (block_i ^ 1) == block_j
            weighted = g * c_col * c_row
            within = jnp.where(same, weighted, 0.0)
            across = jnp.where(sibling, weighted, 0.0)

            def coef(axis):
                norm = jnp.sum(jnp.where(same, jnp.sum(within, axis=3 - axis, keepdims=True), 0.0), axis=axis, keepdims=True)
                inner = jnp.sum(jnp.where(same, jnp.sum(across, axis=3 - axis, keepdims=True), 0.0), axis=axis, keepdims=True)
                return 1.0 - inner / (2.0 * (jnp.maximum(norm, 0.0) + epsilon))

            c_col, c_row = c_col * coef(2), c_row * coef(1)
        olds = ((gate_w, gate_m, new_g, next_g), (up_w, up_m, new_u, next_u))
        for m in range(3):
            merged = jnp.zeros((64, SLICE), F32)
            for q in range(16):
                scale = jnp.broadcast_to(c_col[m, q : q + 1, :], (64, SLICE))
                merged += scale * x[q, 64 * m : 64 * (m + 1), :].astype(F32)
            if m < 2:
                w, mom, new, after = olds[m]
                step = momentum_decay * mom[...] + merged
                after[...] = step
                new[...] = w[...] - learning_rate * step
            else:
                for k in range(4):
                    cols = slice(SLICE * k, SLICE * (k + 1))
                    step = momentum_decay * down_m[:, cols] + merged[16 * k : 16 * (k + 1), :]
                    next_d[:, cols] = step
                    new_d[:, cols] = down_w[:, cols] - learning_rate * step

    wide, tall = struct((64, H), F32), struct((16, D), F32)
    return call(body, "finish", 8, [wide, wide, tall, wide, wide, tall], 2**22, 6 * MIB)(
        parts, products, gate, up, down, mom_gate, mom_up, mom_down
    )


def scatter_rows(ids_rows, grads):
    block = 512

    def body(i0, i1, i2, i3, g0, g1, g2, g3, out):
        row = lax.broadcasted_iota(jnp.int32, (block, TOK_DEV), 0) + block * pl.program_id(0)
        acc = None
        for ids, g in zip((i0, i1, i2, i3), (g0, g1, g2, g3)):
            hot = jnp.where(jnp.broadcast_to(ids[...], row.shape) == row, 1.0, 0.0).astype(BF16)
            part = jnp.dot(hot, g[...], preferred_element_type=F32)
            acc = part if acc is None else acc + part
        out[...] = acc

    return pl.pallas_call(
        body,
        name="scatter_rows",
        grid=(POOL // block,),
        out_shape=struct((POOL, SLICE), F32),
        in_specs=[vmem()] * 8,
        out_specs=pl.BlockSpec((block, SLICE), lambda i: (i, 0)),
        compiler_params=pltpu.CompilerParams(vmem_limit_bytes=24 * MIB),
        cost_estimate=pl.CostEstimate(
            flops=2 * POOL * POOL * SLICE, bytes_accessed=6 * MIB, transcendentals=0
        ),
    )(*ids_rows, *grads)


def shift(block, axis, to):
    return lax.ppermute(block, axis, [(i, to(i)) for i in range(lax.axis_size(axis))])


def around_y(block, k):
    return shift(block, "expert", lambda i: (i + k) % N_EXPERT)


def around_z(block, k):
    return shift(block, "dp", lambda i: i // 8 * 8 + (i // 2 % 4 + k) % 4 * 2 + i % 2)


def around_x(block, k):
    return shift(block, "dp", lambda i: (i // 8 + k) % 4 * 8 + i % 8)


def other_core(block):
    return shift(block, "dp", lambda i: i ^ 1)


def sum_dp(value):
    for around in (around_z, around_x):
        value = value + sum(around(value, k) for k in (2, 1, 3))
    return value + other_core(value)


def local(
    pool_tokens,
    pool_cotangent,
    token_ids,
    route_weights,
    gate_weight,
    up_weight,
    down_weight,
    momentum_gate,
    momentum_up,
    momentum_down,
):
    down_halves = down_weight[0].astype(BF16)
    shard = jnp.concatenate(
        [
            jnp.concatenate([gate_weight[0].astype(BF16), up_weight[0].astype(BF16)], axis=1),
            down_halves[:, : D // 2],
            down_halves[:, D // 2 :],
        ],
        axis=0,
    )
    weights = lax.all_gather(shard, "dp", axis=0, tiled=False)

    ids = [token_ids] + [around_y(token_ids, N_EXPERT - k) for k in (1, 2, 3)]
    own_x, own_c = pick_rows(ids[:1], [pool_tokens, pool_cotangent])
    sent_x = pick_rows(ids[1:], [pool_tokens])
    sent_c = pick_rows(ids[1:], [pool_cotangent])
    tokens = [own_x] + [around_y(sent_x[k - 1], k) for k in (1, 2, 3)]
    cots = [own_c] + [around_y(sent_c[k - 1], k) for k in (1, 2, 3)]

    hidden_t, gate_factor, act, xt = forward(tokens, weights)
    keep, send, both = backward(cots, route_weights, hidden_t, gate_factor, act, xt, weights)
    received = other_core(send)
    slots = slot_gradients(both, weights)
    back = [slots[0]] + [around_y(slots[k], N_EXPERT - k) for k in (1, 2, 3)]
    received, _ = lax.optimization_barrier((received, slots))

    mine = pair_moments(keep, received)
    merged = pair_merge(keep, received, mine, other_core(mine))
    groups = [[2 * q + c for q in range(N_CHIP)] for c in range(2)]
    parts = lax.all_to_all(merged, "dp", 0, 0, tiled=True, axis_index_groups=groups)
    products = sum_dp(gram(parts))
    outs = finish(
        parts,
        products,
        gate_weight[0],
        up_weight[0],
        down_weight[0],
        momentum_gate[0],
        momentum_up[0],
        momentum_down[0],
    )
    pool_grad = scatter_rows(ids, back)
    return (*(a[None] for a in outs), pool_grad)


def solution(mesh):
    in_specs = (
        P("dp", "expert"),
        P("dp", "expert"),
        P("expert", "dp"),
        P("expert", "dp"),
        P("expert", "dp", None),
        P("expert", "dp", None),
        P("expert", "dp", None),
        P("expert", "dp", None),
        P("expert", "dp", None),
        P("expert", "dp", None),
    )
    out_specs = (
        P("expert", "dp", None),
        P("expert", "dp", None),
        P("expert", "dp", None),
        P("expert", "dp", None),
        P("expert", "dp", None),
        P("expert", "dp", None),
        P("dp", "expert"),
    )
    return jax.shard_map(local, mesh=mesh, in_specs=in_specs, out_specs=out_specs, check_vma=False)
```

time: 652 us -> 188 us (0.29)
  waiting for transfers between devices: 396 us -> 51.6 us
  local copies, waits for them, and re-layouts: 91.8 us -> 8.17 us
  other arithmetic: 82.1 us -> 2.62 us
  blocking collectives: 0 us -> 45.9 us
  Pallas kernels: 0 us -> 38.6 us
  matrix products: 27.2 us -> 0 us
  starting transfers between devices: 33.6 us -> 26.9 us
    all_gather x3 -> x1, waiting for transfers between devices: 212 us -> 13 us  [local(): weights = lax.all_gather(shard, 'dp', axis=0, tiled=False)]
    ppermute x20 -> x21, waiting for transfers between devices: 132 us -> 38.6 us  [shift(): lax.ppermute(block, axis, [(i, to(i)) for i in range(lax.axis_size(axis))])]
    reduce_scatter x1 -> x0, waiting for transfers between devices: 52 us -> none  [local(): lax.psum_scatter(pool_term, 'expert', scatter_dimension=1, tiled=True)]
    all_to_all x0 -> x1, blocking collectives: none -> 45.9 us  [local(): lax.all_to_all(merged, 'dp', 0, 0, tiled=True, axis_index_groups=groups)]
    pallas_call x0 -> x11, Pallas kernels: none -> 38.6 us  [the longest x3 10.8 us: pick_rows(): call(body, 'pick_rows', n_ids + n_pool, shapes, 2 * TOK_DEV * POOL * SLIC...]
    dot_general x8 -> x0, matrix products: 27.2 us -> none  [the longest x1 5.12 us: local(): lax.dot_general(up_grad, up_full, (((1,), (1,)), ((), ())), preferred_ele...]
    another operation x7 -> x0, local copies, waits for them, and re-layouts: 24.5 us -> none  [the longest x4 24.4 us: local(): jnp.stack([grad_gate.reshape(-1), grad_up.reshape(-1), grad_down.reshape(...]
    reduce_sum x5 -> x0, other arithmetic: 24.3 us -> none  [moment_terms(): inner = jnp.sum(left_part * right_part, axis=(1, 2))]
  transfers between devices with their start and end apart: 24 -> 22, of which waited for: 24 -> 14; matrix products, arithmetic and copies ran while one was open for 13% -> 0% of each run, Pallas kernels for 0% -> 12%
where the time goes in v1:
time: 188 us
  waiting for transfers between devices  51.6 us (27%)
  blocking collectives  45.9 us (24%)
  Pallas kernels  38.6 us (21%)
  starting transfers between devices  26.9 us (14%)
  between operations  14.2 us (8%)
  local copies, waits for them, and re-layouts  8.17 us (4%)
  other arithmetic  2.62 us (1%)
    all_to_all x1, blocking collectives, local(): lax.all_to_all(merged, 'dp', 0, 0, tiled=True, axis_index_groups=groups)  45.9 us
    ppermute x21, waiting for transfers between devices, shift(): lax.ppermute(block, axis, [(i, to(i)) for i in range(lax.axis_size(axis))])  38.6 us
    ppermute x21, starting transfers between devices, shift(): lax.ppermute(block, axis, [(i, to(i)) for i in range(lax.axis_size(axis))])  26.8 us
    all_gather x1, waiting for transfers between devices, local(): weights = lax.all_gather(shard, 'dp', axis=0, tiled=False)  13 us
    pallas_call x3, Pallas kernels, pick_rows(): call(body, 'pick_rows', n_ids + n_pool, shapes, 2 * TOK_DEV * POOL * SLIC...  10.8 us
    pallas_call x1, Pallas kernels, backward(): call(body, 'backward', 10, shapes, 8 * TOK_DEV * D * H, 20 * MIB, [pltpu....  10.2 us
    unnamed x36, local copies, waits for them, and re-layouts  8.16 us
    pallas_call x1, Pallas kernels, scatter_rows(): pl.pallas_call(body, name='scatter_rows', grid=(POOL // block,), out_shap...  5.97 us
  transfers between devices with their start and end apart: 22, of which 14 were waited for; matrix products, arithmetic and copies ran while one was open for 0% of the time, Pallas kernels for 12%

profile of v1, /device:TPU:1, one launch (start us, length us, event | category | flops | bytes accessed | tf_op | source)
XLA Modules:
  0.0 188.0 jit_solution(5014789588952785914)
XLA Ops:
  7.2 0.9 bitcast_convert_fusion
  8.1 1.0 bitcast_convert_fusion.1
  9.1 0.7 pad_maximum_fusion
  9.8 3.8 %collective-permute-start.1 = (s32[1,512]{1,0:T(1,128)}, s32[1,512]{1,0:T(1,128)S(1)}, u32[]{:S(2)}, u32[]{:S(2)}) collective-permute-start(s32[1,512]{1,0:T(1,128)} %i0.1), channel_id=1, source_target_pairs={{0,64},{32,96},{64,0},{96,32},{1,65},{33,97},{65,1},{97,33},{2,66}... | collective-permute-start | bytes 6152 | tf_op jit(solution)/shard_map/ppermute | solution.py:329
  13.7 0.8 collective-permute-start
  14.4 0.7 collective-permute-start.2
  15.1 1.2 collective-permute-done.refs_0_.i1
  16.3 2.0 %collective-permute-done.2.refs_2_.i3 = s32[1,512]{1,0:T(1,128)S(1)} collective-permute-done((s32[1,512]{1,0:T(1,128)}, s32[1,512]{1,0:T(1,128)S(1)}, u32[]{:S(2)}, u32[]{:S(2)}) %collective-permute-start.2) | collective-permute-done | bytes 2080 | tf_op jit(solution)/shard_map/ppermute | solution.py:329
  18.3 1.6 copy-done.7
  19.9 3.7 %pick_rows.5 = (bf16[512,512]{1,0:T(8,128)(2,1)S(1)}, bf16[512,512]{1,0:T(8,128)(2,1)S(1)}, bf16[512,512]{1,0:T(8,128)(2,1)S(1)}) custom-call(s32[1,512]{1,0:T(1,128)S(1)} %collective-permute-done.refs_0_.i1, s32[1,512]{1,0:T(1,128)S(1)} %collective-permute-done.1.refs_1_.i2, s32[1,512]{1,0:T(1,128)S(1)} %collective-permute-done.2.refs_2_.i3, ...), custom_call_target="tpu_custom_call" | custom-call | flops 3221225472 | bytes 5242880 | tf_op jit(solution)/shard_map/pick_rows/pallas_call | solution.py:68
  23.6 1.2 collective-permute-start.7
  24.8 1.5 collective-permute-start.8
  26.3 4.6 %pick_rows.4 = (bf16[512,512]{1,0:T(8,128)(2,1)}, bf16[512,512]{1,0:T(8,128)(2,1)}, bf16[512,512]{1,0:T(8,128)(2,1)}) custom-call(s32[1,512]{1,0:T(1,128)S(1)} %collective-permute-done.refs_0_.i1, s32[1,512]{1,0:T(1,128)S(1)} %collective-permute-done.1.refs_1_.i2, s32[1,512]{1,0:T(1,128)S(1)} %collective-permute-done.2.refs_2_.i3, ...), custom_call_target="tpu_custom_call" | custom-call | flops 3221225472 | bytes 5242880 | tf_op jit(solution)/shard_map/pick_rows/pallas_call | solution.py:68
  30.9 0.6 collective-permute-start.3
  31.5 1.8 collective-permute-start.4
  33.3 3.9 %collective-permute-done.6.x1 = bf16[512,512]{1,0:T(8,128)(2,1)S(1)} collective-permute-done((bf16[512,512]{1,0:T(8,128)(2,1)S(1)}, bf16[512,512]{1,0:T(8,128)(2,1)S(1)}, u32[]{:S(2)}, u32[]{:S(2)}) %collective-permute-start.6) | collective-permute-done | bytes 524320 | tf_op jit(solution)/shard_map/ppermute | solution.py:329
  37.2 2.6 %pick_rows.3 = (bf16[512,512]{1,0:T(8,128)(2,1)S(1)}, bf16[512,512]{1,0:T(8,128)(2,1)S(1)}) custom-call(s32[1,512]{1,0:T(1,128)S(1)} %copy-done.13, bf16[2048,512]{1,0:T(8,128)(2,1)S(1)} %copy-done.8, bf16[2048,512]{1,0:T(8,128)(2,1)S(1)} %copy-done.9), custom_call_target="tpu_custom_call" | custom-call | flops 2147483648 | bytes 3145728 | tf_op jit(solution)/shard_map/pick_rows/pallas_call | solution.py:68
  39.7 0.8 copy-done.14
  40.6 5.4 %collective-permute-done.7.x2 = bf16[512,512]{1,0:T(8,128)(2,1)S(1)} collective-permute-done((bf16[512,512]{1,0:T(8,128)(2,1)S(1)}, bf16[512,512]{1,0:T(8,128)(2,1)S(1)}, u32[]{:S(2)}, u32[]{:S(2)}) %collective-permute-start.7) | collective-permute-done | bytes 524320 | tf_op jit(solution)/shard_map/ppermute | solution.py:329
  46.0 4.7 %collective-permute-done.8.x3 = bf16[512,512]{1,0:T(8,128)(2,1)S(1)} collective-permute-done((bf16[512,512]{1,0:T(8,128)(2,1)S(1)}, bf16[512,512]{1,0:T(8,128)(2,1)S(1)}, u32[]{:S(2)}, u32[]{:S(2)}) %collective-permute-start.8) | collective-permute-done | bytes 524320 | tf_op jit(solution)/shard_map/ppermute | solution.py:329
  50.7 13.0 %all-gather.3.cloned.1.call-done = bf16[3072,1024]{1,0:T(8,128)(2,1)} async-done(((bf16[96,1024]{1,0:T(8,128)(2,1)}), bf16[3072,1024]{1,0:T(8,128)(2,1)}) %all-gather.3.cloned.1.call-update) | async-done | bytes 6291472 | tf_op jit(solution)/shard_map/all_gather | solution.py:375
  63.8 2.8 %copy-done = bf16[3072,1024]{1,0:T(8,128)(2,1)S(1)} copy-done((bf16[3072,1024]{1,0:T(8,128)(2,1)S(1)}, bf16[3072,1024]{1,0:T(8,128)(2,1)}, u32[]{:S(2)}) %copy-start) | copy-done | bytes 6291480
  66.5 3.0 %forward.1 = (bf16[512,512]{1,0:T(8,128)(2,1)S(1)}, f32[512,512]{1,0:T(8,128)S(1)}, f32[512,512]{1,0:T(8,128)S(1)}, bf16[4,512,512]{2,1,0:T(8,128)(2,1)S(1)}) custom-call(bf16[512,512]{1,0:T(8,128)(2,1)S(1)} %get-tuple-element.37.x0, bf16[512,512]{1,0:T(8,128)(2,1)S(1)} %collective-permute-done.6.x1, bf16[512,512]{1,0:T(8,128)(2,1)S(1)} %collective-permute-done.7.x2, ...), custom_call_target="tpu_custom_call" | custom-call | flops 2147483648 | bytes 10485760 | tf_op jit(solution)/shard_map/forward/pallas_call | solution.py:122
  69.5 1.3 copy-done.10
  70.9 0.6 collective-permute-done.5.c3
  71.4 1.6 copy-done.11
  73.0 10.2 %backward.1 = (bf16[16,192,512]{2,1,0:T(8,128)(2,1)S(1)}, bf16[16,192,512]{2,1,0:T(8,128)(2,1)}, bf16[512,1024]{1,0:T(8,128)(2,1)S(1)}) custom-call(bf16[512,512]{1,0:T(8,128)(2,1)S(1)} %copy-done.15, bf16[512,512]{1,0:T(8,128)(2,1)} %collective-permute-done.3.c1, bf16[512,512]{1,0:T(8,128)(2,1)} %collective-permute-done.4.c2, ...), custom_call_target="tpu_custom_call" | custom-call | flops 4294967296 | bytes 20971520 | tf_op jit(solution)/shard_map/backward/pallas_call | solution.py:175
  83.3 2.2 %collective-permute-start.9 = (bf16[16,192,512]{2,1,0:T(8,128)(2,1)}, bf16[16,192,512]{2,1,0:T(8,128)(2,1)S(1)}, u32[]{:S(2)}, u32[]{:S(2)}) collective-permute-start(bf16[16,192,512]{2,1,0:T(8,128)(2,1)} %get-tuple-element.46), channel_id=1, source_target_pairs={{0,1},{1,0},{2,3},{3,2},{4,5},{5,4},{6,7},{7,6},{8,9},{9,8},{10,11... | collective-permute-start | bytes 9437192 | tf_op jit(solution)/shard_map/ppermute | solution.py:329
  85.5 2.4 %slot_gradients.1 = (bf16[512,512]{1,0:T(8,128)(2,1)S(1)}, bf16[512,512]{1,0:T(8,128)(2,1)S(1)}, bf16[512,512]{1,0:T(8,128)(2,1)S(1)}, bf16[512,512]{1,0:T(8,128)(2,1)S(1)}) custom-call(bf16[512,1024]{1,0:T(8,128)(2,1)S(1)} %get-tuple-element.47.both_ref, bf16[32,96,1024]{2,1,0:T(8,128)(2,1)S(1)} %bitcast.20), custom_call_target="tpu_custom_call" | custom-call | flops 2147483648 | bytes 9437184 | tf_op jit(solution)/shard_map/slot_gradients/pallas_call | solution.py:193
  87.9 3.1 %collective-permute-done.9.b_ref = bf16[16,192,512]{2,1,0:T(8,128)(2,1)S(1)} collective-permute-done((bf16[16,192,512]{2,1,0:T(8,128)(2,1)}, bf16[16,192,512]{2,1,0:T(8,128)(2,1)S(1)}, u32[]{:S(2)}, u32[]{:S(2)}) %collective-permute-start.9) | collective-permute-done | bytes 3145760 | tf_op jit(solution)/shard_map/ppermute | solution.py:329
  91.0 0.8 pair_moments.1.m_ref
  92.3 0.9 collective-permute-done.10.t_ref
  93.1 1.5 pair_merge.1
  94.6 45.9 %all_to_all.5.x = bf16[16,192,512]{2,1,0:T(8,128)(2,1)S(1)} all-to-all(bf16[16,192,512]{2,1,0:T(8,128)(2,1)S(1)} %pair_merge.1), channel_id=1, replica_groups={{0,2,4,6,8,10,12,14,16,18,20,22,24,26,28,30},{1,3,5,7,9,11,13,15,17,19,..., dimensions={0} | all-to-all | bytes 6291456 | tf_op jit(solution)/shard_map/all_to_all | solution.py:394
  140.5 2.1 %gram.1 = f32[3,16,128]{2,1,0:T(8,128)S(1)} custom-call(bf16[16,192,512]{2,1,0:T(8,128)(2,1)S(1)} %all_to_all.5.x), custom_call_target="tpu_custom_call" | custom-call | flops 805306368 | bytes 3145728 | tf_op jit(solution)/shard_map/gram/pallas_call | solution.py:255
  142.6 1.0 collective-permute-start.13
  144.1 1.2 collective-permute-start.11
  145.3 2.0 %collective-permute-start.18 = (bf16[512,512]{1,0:T(8,128)(2,1)S(1)}, bf16[512,512]{1,0:T(8,128)(2,1)S(1)}, u32[]{:S(2)}, u32[]{:S(2)}) collective-permute-start(bf16[512,512]{1,0:T(8,128)(2,1)S(1)} %get-tuple-element.49), channel_id=1, source_target_pairs={{0,96},{32,0},{64,32},{96,64},{1,97},{33,1},{65,33},{97,65},{2,98}... | collective-permute-start | bytes 1572872 | tf_op jit(solution)/shard_map/ppermute | solution.py:329
  147.3 0.6 collective-permute-start.20
  148.3 1.2 collective-permute-start.16
  149.8 1.5 collective-permute-done.16
  151.3 1.1 collective-permute-start.14
  152.4 1.0 collective-permute-done.15
  153.4 2.4 %collective-permute-done.14 = f32[3,16,128]{2,1,0:T(8,128)S(1)} collective-permute-done((f32[3,16,128]{2,1,0:T(8,128)S(1)}, f32[3,16,128]{2,1,0:T(8,128)S(1)}, u32[]{:S(2)}, u32[]{:S(2)}) %collective-permute-start.14) | collective-permute-done | bytes 24608 | tf_op jit(solution)/shard_map/ppermute | solution.py:329
  155.9 5.8 %collective-permute-start.17 = (f32[3,16,128]{2,1,0:T(8,128)S(1)}, f32[3,16,128]{2,1,0:T(8,128)S(1)}, u32[]{:S(2)}, u32[]{:S(2)}) collective-permute-start(f32[3,16,128]{2,1,0:T(8,128)S(1)} %add_add_fusion), channel_id=1, source_target_pairs={{0,1},{1,0},{2,3},{3,2},{4,5},{5,4},{6,7},{7,6},{8,9},{9,8},{10,11... | collective-permute-start | bytes 73736 | tf_op jit(solution)/shard_map/ppermute | solution.py:329
  161.6 11.6 %collective-permute-done.20.g3 = bf16[512,512]{1,0:T(8,128)(2,1)S(1)} collective-permute-done((bf16[512,512]{1,0:T(8,128)(2,1)S(1)}, bf16[512,512]{1,0:T(8,128)(2,1)S(1)}, u32[]{:S(2)}, u32[]{:S(2)}) %collective-permute-start.20) | collective-permute-done | bytes 524320 | tf_op jit(solution)/shard_map/ppermute | solution.py:329
  173.3 6.0 %scatter_rows.1 = f32[2048,512]{1,0:T(8,128)} custom-call(s32[1,512]{1,0:T(1,128)S(1)} %copy-done.13, s32[1,512]{1,0:T(1,128)S(1)} %collective-permute-done.refs_0_.i1, s32[1,512]{1,0:T(1,128)S(1)} %collective-permute-done.1.refs_1_.i2, s32[1,512]{1,0:T(1,128)S(1)} %collective-permute-done.2.refs_2_.i3, bf16[512,512]{1,0:T(8,128)(2,1)S(1)} %get-tuple-element.48.g0, ...), custom_call_target="tpu_custom_call" | custom-call | flops 4294967296 | bytes 6291456 | tf_op jit(solution)/shard_map/scatter_rows/pallas_call | solution.py:314
  179.3 1.8 finish.1
  (53 shorter events, 1.9 us)
Async XLA Ops:
  7.2 56.6 %all-gather.3.cloned.1.call-start = ((), (), s32[]{:S(2)}) async-start(), calls=%async_computation.1 | async-start | bytes 6488064 | tf_op jit(solution)/shard_map/all_gather | solution.py:375
  9.8 5.3 %collective-permute-start.1 = (s32[1,512]{1,0:T(1,128)}, s32[1,512]{1,0:T(1,128)S(1)}, u32[]{:S(2)}, u32[]{:S(2)}) collective-permute-start(s32[1,512]{1,0:T(1,128)} %i0.1), channel_id=1, source_target_pairs={{0,64},{32,96},{64,0},{96,32},{1,65},{33,97},{65,1},{97,33},{2,66}... | collective-permute-start | bytes 6152 | tf_op jit(solution)/shard_map/ppermute | solution.py:329
  13.7 2.6 %collective-permute-start = (s32[1,512]{1,0:T(1,128)}, s32[1,512]{1,0:T(1,128)S(1)}, u32[]{:S(2)}, u32[]{:S(2)}) collective-permute-start(s32[1,512]{1,0:T(1,128)} %i0.1), channel_id=1, source_target_pairs={{0,96},{32,0},{64,32},{96,64},{1,97},{33,1},{65,33},{97,65},{2,98}... | collective-permute-start | bytes 6152 | tf_op jit(solution)/shard_map/ppermute | solution.py:329
  14.4 3.9 %collective-permute-start.2 = (s32[1,512]{1,0:T(1,128)}, s32[1,512]{1,0:T(1,128)S(1)}, u32[]{:S(2)}, u32[]{:S(2)}) collective-permute-start(s32[1,512]{1,0:T(1,128)} %i0.1), channel_id=1, source_target_pairs={{0,32},{32,64},{64,96},{96,0},{1,33},{33,65},{65,97},{97,1},{2,34}... | collective-permute-start | bytes 6152 | tf_op jit(solution)/shard_map/ppermute | solution.py:329
  18.3 1.6 copy-start.7
  19.9 6.4 %copy-start.9 = (bf16[2048,512]{1,0:T(8,128)(2,1)S(1)}, bf16[2048,512]{1,0:T(8,128)(2,1)}, u32[]{:S(2)}) copy-start(bf16[2048,512]{1,0:T(8,128)(2,1)} %refs_3_.2) | copy-start | bytes 6291460
  23.6 13.6 %collective-permute-start.6 = (bf16[512,512]{1,0:T(8,128)(2,1)S(1)}, bf16[512,512]{1,0:T(8,128)(2,1)S(1)}, u32[]{:S(2)}, u32[]{:S(2)}) collective-permute-start(bf16[512,512]{1,0:T(8,128)(2,1)S(1)} %get-tuple-element.38), channel_id=1, source_target_pairs={{0,32},{32,64},{64,96},{96,0},{1,33},{33,65},{65,97},{97,1},{2,34}... | collective-permute-start | bytes 1572872 | tf_op jit(solution)/shard_map/ppermute | solution.py:329
  23.6 22.3 %collective-permute-start.7 = (bf16[512,512]{1,0:T(8,128)(2,1)S(1)}, bf16[512,512]{1,0:T(8,128)(2,1)S(1)}, u32[]{:S(2)}, u32[]{:S(2)}) collective-permute-start(bf16[512,512]{1,0:T(8,128)(2,1)S(1)} %get-tuple-element.39), channel_id=1, source_target_pairs={{0,64},{32,96},{64,0},{96,32},{1,65},{33,97},{65,1},{97,33},{2,66}... | collective-permute-start | bytes 1572872 | tf_op jit(solution)/shard_map/ppermute | solution.py:329
  24.8 12.3 %copy-start.8 = (bf16[2048,512]{1,0:T(8,128)(2,1)S(1)}, bf16[2048,512]{1,0:T(8,128)(2,1)}, u32[]{:S(2)}) copy-start(bf16[2048,512]{1,0:T(8,128)(2,1)} %refs_3_.3) | copy-start | bytes 6291460
  24.8 12.3 %copy-start.13 = (s32[1,512]{1,0:T(1,128)S(1)}, s32[1,512]{1,0:T(1,128)}, u32[]{:S(2)}) copy-start(s32[1,512]{1,0:T(1,128)} %i0.1) | copy-start | bytes 6148
  24.8 25.9 %collective-permute-start.8 = (bf16[512,512]{1,0:T(8,128)(2,1)S(1)}, bf16[512,512]{1,0:T(8,128)(2,1)S(1)}, u32[]{:S(2)}, u32[]{:S(2)}) collective-permute-start(bf16[512,512]{1,0:T(8,128)(2,1)S(1)} %get-tuple-element.40), channel_id=1, source_target_pairs={{0,96},{32,0},{64,32},{96,64},{1,97},{33,1},{65,33},{97,65},{2,98}... | collective-permute-start | bytes 1572872 | tf_op jit(solution)/shard_map/ppermute | solution.py:329
  30.9 40.0 %collective-permute-start.3 = (bf16[512,512]{1,0:T(8,128)(2,1)}, bf16[512,512]{1,0:T(8,128)(2,1)}, u32[]{:S(2)}, u32[]{:S(2)}) collective-permute-start(bf16[512,512]{1,0:T(8,128)(2,1)} %get-tuple-element.34), channel_id=1, source_target_pairs={{0,32},{32,64},{64,96},{96,0},{1,33},{33,65},{65,97},{97,1},{2,34}... | collective-permute-start | bytes 1572872 | tf_op jit(solution)/shard_map/ppermute | solution.py:329
  31.5 39.4 %collective-permute-start.4 = (bf16[512,512]{1,0:T(8,128)(2,1)}, bf16[512,512]{1,0:T(8,128)(2,1)}, u32[]{:S(2)}, u32[]{:S(2)}) collective-permute-start(bf16[512,512]{1,0:T(8,128)(2,1)} %get-tuple-element.35), channel_id=1, source_target_pairs={{0,64},{32,96},{64,0},{96,32},{1,65},{33,97},{65,1},{97,33},{2,66}... | collective-permute-start | bytes 1572872 | tf_op jit(solution)/shard_map/ppermute | solution.py:329
  37.2 34.3 %collective-permute-start.5 = (bf16[512,512]{1,0:T(8,128)(2,1)}, bf16[512,512]{1,0:T(8,128)(2,1)}, u32[]{:S(2)}, u32[]{:S(2)}) collective-permute-start(bf16[512,512]{1,0:T(8,128)(2,1)} %get-tuple-element.36), channel_id=1, source_target_pairs={{0,96},{32,0},{64,32},{96,64},{1,97},{33,1},{65,33},{97,65},{2,98}... | collective-permute-start | bytes 1572872 | tf_op jit(solution)/shard_map/ppermute | solution.py:329
  39.7 0.8 copy-start.14
  63.8 2.8 %copy-start = (bf16[3072,1024]{1,0:T(8,128)(2,1)S(1)}, bf16[3072,1024]{1,0:T(8,128)(2,1)}, u32[]{:S(2)}) copy-start(bf16[3072,1024]{1,0:T(8,128)(2,1)} %all-gather.3.cloned.1.call-done) | copy-start | bytes 18874372
  66.5 4.9 %copy-start.12 = (f32[1,512]{1,0:T(1,128)S(1)}, f32[1,512]{1,0:T(1,128)}, u32[]{:S(2)}) copy-start(f32[1,512]{1,0:T(1,128)} %route_ref.1) | copy-start | bytes 6148
  66.5 4.9 %copy-start.15 = (bf16[512,512]{1,0:T(8,128)(2,1)S(1)}, bf16[512,512]{1,0:T(8,128)(2,1)}, u32[]{:S(2)}) copy-start(bf16[512,512]{1,0:T(8,128)(2,1)} %copy-done.14) | copy-start | bytes 1572868
  66.5 19.0 %slice-start = ((s8[6291456]{0:T(1024)(128)(4,1)}), s8[4194304]{0:T(1024)(128)(4,1)S(1)}, s32[]{:S(2)}) async-start(s8[6291456]{0:T(1024)(128)(4,1)} %bitcast.18), calls=%async_computation.2 | async-start | bytes 8388608
  69.5 1.3 copy-start.10
  71.4 1.6 copy-start.11
  73.0 12.5 %slice-start.1 = ((s8[6291456]{0:T(1024)(128)(4,1)}), s8[2097152]{0:T(1024)(128)(4,1)S(1)}, s32[]{:S(2)}) async-start(s8[6291456]{0:T(1024)(128)(4,1)} %bitcast.18), calls=%async_computation.3 | async-start | bytes 4194304
  83.3 7.7 %collective-permute-start.9 = (bf16[16,192,512]{2,1,0:T(8,128)(2,1)}, bf16[16,192,512]{2,1,0:T(8,128)(2,1)S(1)}, u32[]{:S(2)}, u32[]{:S(2)}) collective-permute-start(bf16[16,192,512]{2,1,0:T(8,128)(2,1)} %get-tuple-element.46), channel_id=1, source_target_pairs={{0,1},{1,0},{2,3},{3,2},{4,5},{5,4},{6,7},{7,6},{8,9},{9,8},{10,11... | collective-permute-start | bytes 9437192 | tf_op jit(solution)/shard_map/ppermute | solution.py:329
  91.8 1.3 collective-permute-start.10
  142.6 4.8 %collective-permute-start.13 = (f32[3,16,128]{2,1,0:T(8,128)S(1)}, f32[3,16,128]{2,1,0:T(8,128)S(1)}, u32[]{:S(2)}, u32[]{:S(2)}) collective-permute-start(f32[3,16,128]{2,1,0:T(8,128)S(1)} %gram.1), channel_id=1, source_target_pairs={{0,6},{1,7},{2,0},{3,1},{4,2},{5,3},{6,4},{7,5},{8,14},{9,15},{10,... | collective-permute-start | bytes 73736 | tf_op jit(solution)/shard_map/ppermute | solution.py:329
  143.6 4.4 %collective-permute-start.12 = (f32[3,16,128]{2,1,0:T(8,128)S(1)}, f32[3,16,128]{2,1,0:T(8,128)S(1)}, u32[]{:S(2)}, u32[]{:S(2)}) collective-permute-start(f32[3,16,128]{2,1,0:T(8,128)S(1)} %gram.1), channel_id=1, source_target_pairs={{0,2},{1,3},{2,4},{3,5},{4,6},{5,7},{6,0},{7,1},{8,10},{9,11},{10,... | collective-permute-start | bytes 73736 | tf_op jit(solution)/shard_map/ppermute | solution.py:329
  144.1 4.2 %collective-permute-start.11 = (f32[3,16,128]{2,1,0:T(8,128)S(1)}, f32[3,16,128]{2,1,0:T(8,128)S(1)}, u32[]{:S(2)}, u32[]{:S(2)}) collective-permute-start(f32[3,16,128]{2,1,0:T(8,128)S(1)} %gram.1), channel_id=1, source_target_pairs={{0,4},{1,5},{2,6},{3,7},{4,0},{5,1},{6,2},{7,3},{8,12},{9,13},{10,... | collective-permute-start | bytes 73736 | tf_op jit(solution)/shard_map/ppermute | solution.py:329
  145.3 16.3 %collective-permute-start.18 = (bf16[512,512]{1,0:T(8,128)(2,1)S(1)}, bf16[512,512]{1,0:T(8,128)(2,1)S(1)}, u32[]{:S(2)}, u32[]{:S(2)}) collective-permute-start(bf16[512,512]{1,0:T(8,128)(2,1)S(1)} %get-tuple-element.49), channel_id=1, source_target_pairs={{0,96},{32,0},{64,32},{96,64},{1,97},{33,1},{65,33},{97,65},{2,98}... | collective-permute-start | bytes 1572872 | tf_op jit(solution)/shard_map/ppermute | solution.py:329
  147.3 14.3 %collective-permute-start.19 = (bf16[512,512]{1,0:T(8,128)(2,1)S(1)}, bf16[512,512]{1,0:T(8,128)(2,1)S(1)}, u32[]{:S(2)}, u32[]{:S(2)}) collective-permute-start(bf16[512,512]{1,0:T(8,128)(2,1)S(1)} %get-tuple-element.50), channel_id=1, source_target_pairs={{0,64},{32,96},{64,0},{96,32},{1,65},{33,97},{65,1},{97,33},{2,66}... | collective-permute-start | bytes 1572872 | tf_op jit(solution)/shard_map/ppermute | solution.py:329
  147.3 25.9 %collective-permute-start.20 = (bf16[512,512]{1,0:T(8,128)(2,1)S(1)}, bf16[512,512]{1,0:T(8,128)(2,1)S(1)}, u32[]{:S(2)}, u32[]{:S(2)}) collective-permute-start(bf16[512,512]{1,0:T(8,128)(2,1)S(1)} %get-tuple-element.51), channel_id=1, source_target_pairs={{0,32},{32,64},{64,96},{96,0},{1,33},{33,65},{65,97},{97,1},{2,34}... | collective-permute-start | bytes 1572872 | tf_op jit(solution)/shard_map/ppermute | solution.py:329
  148.3 3.0 %collective-permute-start.16 = (f32[3,16,128]{2,1,0:T(8,128)S(1)}, f32[3,16,128]{2,1,0:T(8,128)S(1)}, u32[]{:S(2)}, u32[]{:S(2)}) collective-permute-start(f32[3,16,128]{2,1,0:T(8,128)S(1)} %add_add_fusion.1), channel_id=1, source_target_pairs={{0,24},{1,25},{2,26},{3,27},{4,28},{5,29},{6,30},{7,31},{8,0},{9,1... | collective-permute-start | bytes 73736 | tf_op jit(solution)/shard_map/ppermute | solution.py:329
  149.5 3.9 %collective-permute-start.15 = (f32[3,16,128]{2,1,0:T(8,128)S(1)}, f32[3,16,128]{2,1,0:T(8,128)S(1)}, u32[]{:S(2)}, u32[]{:S(2)}) collective-permute-start(f32[3,16,128]{2,1,0:T(8,128)S(1)} %add_add_fusion.1), channel_id=1, source_target_pairs={{0,8},{1,9},{2,10},{3,11},{4,12},{5,13},{6,14},{7,15},{8,16},{9,17... | collective-permute-start | bytes 73736 | tf_op jit(solution)/shard_map/ppermute | solution.py:329
  151.3 4.5 %collective-permute-start.14 = (f32[3,16,128]{2,1,0:T(8,128)S(1)}, f32[3,16,128]{2,1,0:T(8,128)S(1)}, u32[]{:S(2)}, u32[]{:S(2)}) collective-permute-start(f32[3,16,128]{2,1,0:T(8,128)S(1)} %add_add_fusion.1), channel_id=1, source_target_pairs={{0,16},{1,17},{2,18},{3,19},{4,20},{5,21},{6,22},{7,23},{8,24},{9,... | collective-permute-start | bytes 73736 | tf_op jit(solution)/shard_map/ppermute | solution.py:329
  155.8 23.4 %copy-start.1 = (f32[1,64,512]{2,1,0:T(8,128)S(1)}, f32[1,64,512]{2,1,0:T(8,128)}, u32[]{:S(2)}) copy-start(f32[1,64,512]{2,1,0:T(8,128)} %param.15) | copy-start | bytes 393220
  155.8 23.4 %copy-start.2 = (f32[1,64,512]{2,1,0:T(8,128)S(1)}, f32[1,64,512]{2,1,0:T(8,128)}, u32[]{:S(2)}) copy-start(f32[1,64,512]{2,1,0:T(8,128)} %param.14) | copy-start | bytes 393220
  155.8 23.4 %copy-start.3 = (f32[1,16,2048]{2,1,0:T(8,128)S(1)}, f32[1,16,2048]{2,1,0:T(8,128)}, u32[]{:S(2)}) copy-start(f32[1,16,2048]{2,1,0:T(8,128)} %param.16) | copy-start | bytes 393220
  155.8 23.4 %copy-start.4 = (f32[1,64,512]{2,1,0:T(8,128)S(1)}, f32[1,64,512]{2,1,0:T(8,128)}, u32[]{:S(2)}) copy-start(f32[1,64,512]{2,1,0:T(8,128)} %param.17) | copy-start | bytes 393220
  155.9 23.4 %copy-start.5 = (f32[1,64,512]{2,1,0:T(8,128)S(1)}, f32[1,64,512]{2,1,0:T(8,128)}, u32[]{:S(2)}) copy-start(f32[1,64,512]{2,1,0:T(8,128)} %param.18) | copy-start | bytes 393220
  155.9 23.4 %copy-start.6 = (f32[1,16,2048]{2,1,0:T(8,128)S(1)}, f32[1,16,2048]{2,1,0:T(8,128)}, u32[]{:S(2)}) copy-start(f32[1,16,2048]{2,1,0:T(8,128)} %param.19) | copy-start | bytes 393220
  155.9 23.4 %collective-permute-start.17 = (f32[3,16,128]{2,1,0:T(8,128)S(1)}, f32[3,16,128]{2,1,0:T(8,128)S(1)}, u32[]{:S(2)}, u32[]{:S(2)}) collective-permute-start(f32[3,16,128]{2,1,0:T(8,128)S(1)} %add_add_fusion), channel_id=1, source_target_pairs={{0,1},{1,0},{2,3},{3,2},{4,5},{5,4},{6,7},{7,6},{8,9},{9,8},{10,11... | collective-permute-start | bytes 73736 | tf_op jit(solution)/shard_map/ppermute | solution.py:329
Sparse Core Ops, SparseCore 0:
  10.8 52.8 all-gather.2

commit v2 on v1

--- a/solution.py
+++ b/solution.py
@@ -28,7 +28,7 @@
     return pl.BlockSpec(memory_space=pltpu.VMEM)
 
 
-def call(body, name, n_in, out_shapes, flops, nbytes, scratch=(), limit=40):
+def call(body, name, n_in, out_shapes, flops, nbytes, scratch=(), limit=20):
     return pl.pallas_call(
         body,
         name=name,
@@ -213,6 +213,8 @@
 
 
 def pair_merge(own, other, mine, theirs):
+    step = 4
+
     def body(a_ref, b_ref, m_ref, t_ref, out):
         coefs = []
         for m in range(3):
@@ -223,16 +225,23 @@
             coef_b = 1.0 - inner / (2.0 * (norm_b + epsilon))
             coefs.append((jnp.broadcast_to(coef_a, (64, SLICE)), jnp.broadcast_to(coef_b, (64, SLICE))))
 
-        @pl.loop(0, N_CHIP)
-        def _(q):
+        for i in range(step):
+            q = pl.program_id(0) * step + i
             for m in range(3):
                 rows = slice(64 * m, 64 * (m + 1))
                 a, b = a_ref[q, rows, :].astype(F32), b_ref[q, rows, :].astype(F32)
-                out[q, rows, :] = (coefs[m][0] * a + coefs[m][1] * b).astype(BF16)
-
-    return call(body, "pair_merge", 4, struct((N_CHIP, ROWS, SLICE), BF16), 9 * 2**20, 9 * MIB)(
-        own, other, mine, theirs
-    )
+                out[i, rows, :] = (coefs[m][0] * a + coefs[m][1] * b).astype(BF16)
+
+    return pl.pallas_call(
+        body,
+        name="pair_merge",
+        grid=(N_CHIP // step,),
+        out_shape=struct((N_CHIP, ROWS, SLICE), BF16),
+        in_specs=[vmem()] * 4,
+        out_specs=pl.BlockSpec((step, ROWS, SLICE), lambda i: (i, 0, 0)),
+        compiler_params=pltpu.CompilerParams(vmem_limit_bytes=20 * MIB),
+        cost_estimate=pl.CostEstimate(flops=9 * 2**20, bytes_accessed=9 * MIB, transcendentals=0),
+    )(own, other, mine, theirs)
 
 
 def gram(parts):
@@ -376,8 +385,11 @@
 
     ids = [token_ids] + [around_y(token_ids, N_EXPERT - k) for k in (1, 2, 3)]
     own_x, own_c = pick_rows(ids[:1], [pool_tokens, pool_cotangent])
-    sent_x = pick_rows(ids[1:], [pool_tokens])
-    sent_c = pick_rows(ids[1:], [pool_cotangent])
+    ids, own_x, own_c = lax.optimization_barrier((ids, own_x, own_c))
+    sent_x, sent_c = [None] * 3, [None] * 3
+    for sent, pool in ((sent_x, pool_tokens), (sent_c, pool_cotangent)):
+        for k in (2, 1, 3):
+            (sent[k - 1],) = pick_rows(ids[k : k + 1], [pool])
     tokens = [own_x] + [around_y(sent_x[k - 1], k) for k in (1, 2, 3)]
     cots = [own_c] + [around_y(sent_c[k - 1], k) for k in (1, 2, 3)]
 
@@ -392,6 +404,8 @@
     merged = pair_merge(keep, received, mine, other_core(mine))
     groups = [[2 * q + c for q in range(N_CHIP)] for c in range(2)]
     parts = lax.all_to_all(merged, "dp", 0, 0, tiled=True, axis_index_groups=groups)
+    pool_grad = scatter_rows(ids, back)
+    parts, pool_grad = lax.optimization_barrier((parts, pool_grad))
     products = sum_dp(gram(parts))
     outs = finish(
         parts,
@@ -403,7 +417,6 @@
         momentum_up[0],
         momentum_down[0],
     )
-    pool_grad = scatter_rows(ids, back)
     return (*(a[None] for a in outs), pool_grad)
 
 

time: 188 us -> 174 us (0.926)
  blocking collectives: 45.9 us -> 0 us
  waiting for transfers between devices: 51.6 us -> 68.1 us
  starting transfers between devices: 26.9 us -> 41.7 us
    all_to_all x1 -> x0, blocking collectives: 45.9 us -> none  [local(): lax.all_to_all(merged, 'dp', 0, 0, tiled=True, axis_index_groups=groups)]
    ppermute x21, waiting for transfers between devices: 38.6 us -> 52.3 us  [shift(): lax.ppermute(block, axis, [(i, to(i)) for i in range(lax.axis_size(axis))])]
    all_to_all x0 -> x1, starting transfers between devices: none -> 7.71 us  [local(): lax.all_to_all(merged, 'dp', 0, 0, tiled=True, axis_index_groups=groups)]
    ppermute x21, starting transfers between devices: 26.8 us -> 34 us  [shift(): lax.ppermute(block, axis, [(i, to(i)) for i in range(lax.axis_size(axis))])]
    all_to_all x0 -> x1, waiting for transfers between devices: none -> 6.37 us  [local(): lax.all_to_all(merged, 'dp', 0, 0, tiled=True, axis_index_groups=groups)]
    pallas_call x1, Pallas kernels: 10.2 us -> 6.19 us  [backward(): call(body, 'backward', 10, shapes, 8 * TOK_DEV * D * H, 20 * MIB, [pltpu....]
    all_gather x1, waiting for transfers between devices: 13 us -> 9.4 us  [local(): weights = lax.all_gather(shard, 'dp', axis=0, tiled=False)]
    pallas_call x3 -> x7, Pallas kernels: 10.8 us -> 13.5 us  [pick_rows(): call(body, 'pick_rows', n_ids + n_pool, shapes, 2 * TOK_DEV * POOL * SLIC...]
  transfers between devices with their start and end apart: 22 -> 23, of which waited for: 14 -> 13; matrix products, arithmetic and copies ran while one was open for 0% -> 0% of each run, Pallas kernels for 12% -> 14%
where the time goes in v2:
time: 174 us; the launch traced here: 173 us
  waiting for transfers between devices  68.1 us (39%)
  starting transfers between devices  41.7 us (24%)
  Pallas kernels  37.3 us (21%)
  between operations  14.3 us (8%)
  local copies, waits for them, and re-layouts  9.38 us (5%)
  other arithmetic  2.64 us (2%)
    ppermute x21, waiting for transfers between devices, shift(): lax.ppermute(block, axis, [(i, to(i)) for i in range(lax.axis_size(axis))])  52.3 us
    ppermute x21, starting transfers between devices, shift(): lax.ppermute(block, axis, [(i, to(i)) for i in range(lax.axis_size(axis))])  34 us
    pallas_call x7, Pallas kernels, pick_rows(): call(body, 'pick_rows', n_ids + n_pool, shapes, 2 * TOK_DEV * POOL * SLIC...  13.5 us
    all_gather x1, waiting for transfers between devices, local(): weights = lax.all_gather(shard, 'dp', axis=0, tiled=False)  9.4 us
    unnamed x42, local copies, waits for them, and re-layouts  9.37 us
    all_to_all x1, starting transfers between devices, local(): lax.all_to_all(merged, 'dp', 0, 0, tiled=True, axis_index_groups=groups)  7.71 us
    all_to_all x1, waiting for transfers between devices, local(): lax.all_to_all(merged, 'dp', 0, 0, tiled=True, axis_index_groups=groups)  6.37 us
    pallas_call x1, Pallas kernels, backward(): call(body, 'backward', 10, shapes, 8 * TOK_DEV * D * H, 20 * MIB, [pltpu....  6.19 us
  transfers between devices with their start and end apart: 23, of which 13 were waited for; matrix products, arithmetic and copies ran while one was open for 0% of the time, Pallas kernels for 14%

profile of v2, /device:TPU:1, one launch (start us, length us, event | category | flops | bytes accessed | tf_op | source)
XLA Modules:
  0.0 173.5 jit_solution(7239013068850222872)
XLA Ops:
  7.2 0.9 bitcast_convert_fusion
  8.1 1.0 bitcast_convert_fusion.1
  9.1 0.7 pad_maximum_fusion
  9.9 2.2 %collective-permute-start.2 = (s32[1,512]{1,0:T(1,128)}, s32[1,512]{1,0:T(1,128)S(1)}, u32[]{:S(2)}, u32[]{:S(2)}) collective-permute-start(s32[1,512]{1,0:T(1,128)} %i0), channel_id=1, source_target_pairs={{0,32},{32,64},{64,96},{96,0},{1,33},{33,65},{65,97},{97,1},{2,34}... | collective-permute-start | bytes 6152 | tf_op jit(solution)/shard_map/ppermute | solution.py:338
  12.1 2.6 %collective-permute-start.1 = (s32[1,512]{1,0:T(1,128)}, s32[1,512]{1,0:T(1,128)S(1)}, u32[]{:S(2)}, u32[]{:S(2)}) collective-permute-start(s32[1,512]{1,0:T(1,128)} %i0), channel_id=1, source_target_pairs={{0,64},{32,96},{64,0},{96,32},{1,65},{33,97},{65,1},{97,33},{2,66}... | collective-permute-start | bytes 6152 | tf_op jit(solution)/shard_map/ppermute | solution.py:338
  14.7 1.1 collective-permute-start
  15.7 1.6 copy-done.8
  17.3 1.6 copy-done.9
  19.6 2.5 %pick_rows.7 = (bf16[512,512]{1,0:T(8,128)(2,1)S(1)}, bf16[512,512]{1,0:T(8,128)(2,1)S(1)}) custom-call(s32[1,512]{1,0:T(1,128)S(1)} %copy-done.15, bf16[2048,512]{1,0:T(8,128)(2,1)S(1)} %copy-done.8, bf16[2048,512]{1,0:T(8,128)(2,1)S(1)} %copy-done.9), custom_call_target="tpu_custom_call" | custom-call | flops 2147483648 | bytes 3145728 | tf_op jit(solution)/shard_map/pick_rows/pallas_call | solution.py:68
  22.1 1.4 pick_rows.13
  23.7 1.4 pick_rows.12
  25.1 2.3 %collective-permute-start.7 = (bf16[512,512]{1,0:T(8,128)(2,1)S(1)}, bf16[512,512]{1,0:T(8,128)(2,1)S(1)}, u32[]{:S(2)}, u32[]{:S(2)}) collective-permute-start(bf16[512,512]{1,0:T(8,128)(2,1)S(1)} %pick_rows.12), channel_id=1, source_target_pairs={{0,64},{32,96},{64,0},{96,32},{1,65},{33,97},{65,1},{97,33},{2,66}... | collective-permute-start | bytes 1572872 | tf_op jit(solution)/shard_map/ppermute | solution.py:338
  27.3 1.4 pick_rows.11
  28.8 2.2 %pick_rows.10 = bf16[512,512]{1,0:T(8,128)(2,1)} custom-call(s32[1,512]{1,0:T(1,128)S(1)} %collective-permute-done.2.refs_0_.i3, bf16[2048,512]{1,0:T(8,128)(2,1)S(1)} %copy-done.10), custom_call_target="tpu_custom_call" | custom-call | flops 1073741824 | bytes 3145728 | tf_op jit(solution)/shard_map/pick_rows/pallas_call | solution.py:68
  31.1 2.7 %collective-permute-start.5 = (bf16[512,512]{1,0:T(8,128)(2,1)}, bf16[512,512]{1,0:T(8,128)(2,1)S(1)}, u32[]{:S(2)}, u32[]{:S(2)}) collective-permute-start(bf16[512,512]{1,0:T(8,128)(2,1)} %pick_rows.10), channel_id=1, source_target_pairs={{0,96},{32,0},{64,32},{96,64},{1,97},{33,1},{65,33},{97,65},{2,98}... | collective-permute-start | bytes 1572872 | tf_op jit(solution)/shard_map/ppermute | solution.py:338
  33.8 2.2 %pick_rows.8 = bf16[512,512]{1,0:T(8,128)(2,1)} custom-call(s32[1,512]{1,0:T(1,128)S(1)} %collective-permute-done.refs_0_.i1, bf16[2048,512]{1,0:T(8,128)(2,1)S(1)} %copy-done.10), custom_call_target="tpu_custom_call" | custom-call | flops 1073741824 | bytes 3145728 | tf_op jit(solution)/shard_map/pick_rows/pallas_call | solution.py:68
  36.0 2.3 %pick_rows.9 = bf16[512,512]{1,0:T(8,128)(2,1)} custom-call(s32[1,512]{1,0:T(1,128)S(1)} %collective-permute-done.1.refs_0_.i2, bf16[2048,512]{1,0:T(8,128)(2,1)S(1)} %copy-done.10), custom_call_target="tpu_custom_call" | custom-call | flops 1073741824 | bytes 3145728 | tf_op jit(solution)/shard_map/pick_rows/pallas_call | solution.py:68
  38.5 0.8 collective-permute-start.3
  39.3 14.5 %collective-permute-done.6.x1 = bf16[512,512]{1,0:T(8,128)(2,1)S(1)} collective-permute-done((bf16[512,512]{1,0:T(8,128)(2,1)S(1)}, bf16[512,512]{1,0:T(8,128)(2,1)S(1)}, u32[]{:S(2)}, u32[]{:S(2)}) %collective-permute-start.6) | collective-permute-done | bytes 524320 | tf_op jit(solution)/shard_map/ppermute | solution.py:338
  53.8 9.4 %all-gather.3.cloned.1.call-done = bf16[3072,1024]{1,0:T(8,128)(2,1)} async-done(((bf16[96,1024]{1,0:T(8,128)(2,1)}), bf16[3072,1024]{1,0:T(8,128)(2,1)}) %all-gather.3.cloned.1.call-update) | async-done | bytes 6291472 | tf_op jit(solution)/shard_map/all_gather | solution.py:384
  63.2 2.8 %copy-done.1 = bf16[3072,1024]{1,0:T(8,128)(2,1)S(1)} copy-done((bf16[3072,1024]{1,0:T(8,128)(2,1)S(1)}, bf16[3072,1024]{1,0:T(8,128)(2,1)}, u32[]{:S(2)}) %copy-start.1) | copy-done | bytes 6291480
  66.0 3.0 %forward.1 = (bf16[512,512]{1,0:T(8,128)(2,1)S(1)}, f32[512,512]{1,0:T(8,128)S(1)}, f32[512,512]{1,0:T(8,128)S(1)}, bf16[4,512,512]{2,1,0:T(8,128)(2,1)S(1)}) custom-call(bf16[512,512]{1,0:T(8,128)(2,1)S(1)} %get-tuple-element.41.x0, bf16[512,512]{1,0:T(8,128)(2,1)S(1)} %collective-permute-done.6.x1, bf16[512,512]{1,0:T(8,128)(2,1)S(1)} %collective-permute-done.7.x2, ...), custom_call_target="tpu_custom_call" | custom-call | flops 2147483648 | bytes 10485760 | tf_op jit(solution)/shard_map/forward/pallas_call | solution.py:122
  69.0 5.4 %collective-permute-done.3.c1 = bf16[512,512]{1,0:T(8,128)(2,1)} collective-permute-done((bf16[512,512]{1,0:T(8,128)(2,1)}, bf16[512,512]{1,0:T(8,128)(2,1)}, u32[]{:S(2)}, u32[]{:S(2)}) %collective-permute-start.3) | collective-permute-done | bytes 524320 | tf_op jit(solution)/shard_map/ppermute | solution.py:338
  74.3 6.2 %backward.1 = (bf16[16,192,512]{2,1,0:T(8,128)(2,1)S(1)}, bf16[16,192,512]{2,1,0:T(8,128)(2,1)S(1)}, bf16[512,1024]{1,0:T(8,128)(2,1)S(1)}) custom-call(bf16[512,512]{1,0:T(8,128)(2,1)S(1)} %copy-done.20, bf16[512,512]{1,0:T(8,128)(2,1)} %collective-permute-done.3.c1, bf16[512,512]{1,0:T(8,128)(2,1)S(1)} %collective-permute-done.4.c2, ...), custom_call_target="tpu_custom_call" | custom-call | flops 4294967296 | bytes 20971520 | tf_op jit(solution)/shard_map/backward/pallas_call | solution.py:175
  81.1 2.4 %slot_gradients.1 = (bf16[512,512]{1,0:T(8,128)(2,1)S(1)}, bf16[512,512]{1,0:T(8,128)(2,1)S(1)}, bf16[512,512]{1,0:T(8,128)(2,1)S(1)}, bf16[512,512]{1,0:T(8,128)(2,1)S(1)}) custom-call(bf16[512,1024]{1,0:T(8,128)(2,1)S(1)} %get-tuple-element.48.both_ref, bf16[32,96,1024]{2,1,0:T(8,128)(2,1)S(1)} %bitcast.18), custom_call_target="tpu_custom_call" | custom-call | flops 2147483648 | bytes 9437184 | tf_op jit(solution)/shard_map/slot_gradients/pallas_call | solution.py:193
  83.5 2.9 %collective-permute-done.9.b_ref = bf16[16,192,512]{2,1,0:T(8,128)(2,1)S(1)} collective-permute-done((bf16[16,192,512]{2,1,0:T(8,128)(2,1)S(1)}, bf16[16,192,512]{2,1,0:T(8,128)(2,1)S(1)}, u32[]{:S(2)}, u32[]{:S(2)}) %collective-permute-start.9) | collective-permute-done | bytes 3145760 | tf_op jit(solution)/shard_map/ppermute | solution.py:338
  86.4 0.8 pair_moments.1.m_ref
  87.7 0.9 collective-permute-done.10.t_ref
  88.5 1.7 pair_merge.1
  90.3 1.6 copy-done
  91.9 7.7 %all-to-all-start = ((bf16[16,192,512]{2,1,0:T(8,128)(2,1)}), bf16[16,192,512]{2,1,0:T(8,128)(2,1)S(1)}, u32[]{:S(2)}, u32[]{:S(2)}) async-start(bf16[16,192,512]{2,1,0:T(8,128)(2,1)} %copy-done), calls=%async_computation | async-start | bytes 6291456 | tf_op jit(solution)/shard_map/all_to_all | solution.py:406
  100.0 2.2 %collective-permute-start.12 = (bf16[512,512]{1,0:T(8,128)(2,1)}, bf16[512,512]{1,0:T(8,128)(2,1)S(1)}, u32[]{:S(2)}, u32[]{:S(2)}) collective-permute-start(bf16[512,512]{1,0:T(8,128)(2,1)} %copy-done.12), channel_id=1, source_target_pairs={{0,64},{32,96},{64,0},{96,32},{1,65},{33,97},{65,1},{97,33},{2,66}... | collective-permute-start | bytes 1572872 | tf_op jit(solution)/shard_map/ppermute | solution.py:338
  102.7 10.0 %collective-permute-done.11.g1 = bf16[512,512]{1,0:T(8,128)(2,1)S(1)} collective-permute-done((bf16[512,512]{1,0:T(8,128)(2,1)}, bf16[512,512]{1,0:T(8,128)(2,1)S(1)}, u32[]{:S(2)}, u32[]{:S(2)}) %collective-permute-start.11) | collective-permute-done | bytes 524320 | tf_op jit(solution)/shard_map/ppermute | solution.py:338
  112.7 1.6 collective-permute-done.12.g2
  114.3 12.5 %collective-permute-done.13.g3 = bf16[512,512]{1,0:T(8,128)(2,1)S(1)} collective-permute-done((bf16[512,512]{1,0:T(8,128)(2,1)}, bf16[512,512]{1,0:T(8,128)(2,1)S(1)}, u32[]{:S(2)}, u32[]{:S(2)}) %collective-permute-start.13) | collective-permute-done | bytes 524320 | tf_op jit(solution)/shard_map/ppermute | solution.py:338
  126.8 1.0 copy-done.18
  127.9 6.0 %scatter_rows.1 = f32[2048,512]{1,0:T(8,128)} custom-call(s32[1,512]{1,0:T(1,128)S(1)} %copy-done.16, s32[1,512]{1,0:T(1,128)S(1)} %collective-permute-done.refs_0_.i1, s32[1,512]{1,0:T(1,128)S(1)} %collective-permute-done.1.refs_0_.i2, s32[1,512]{1,0:T(1,128)S(1)} %collective-permute-done.2.refs_0_.i3, bf16[512,512]{1,0:T(8,128)(2,1)S(1)} %copy-done.18, ...), custom_call_target="tpu_custom_call" | custom-call | flops 4294967296 | bytes 6291456 | tf_op jit(solution)/shard_map/scatter_rows/pallas_call | solution.py:323
  133.9 6.4 %all-to-all-done.x = bf16[16,192,512]{2,1,0:T(8,128)(2,1)S(1)} async-done(((bf16[16,192,512]{2,1,0:T(8,128)(2,1)}), bf16[16,192,512]{2,1,0:T(8,128)(2,1)S(1)}, u32[]{:S(2)}, u32[]{:S(2)}) %all-to-all-start) | async-done | bytes 3145760 | tf_op jit(solution)/shard_map/all_to_all | solution.py:406
  140.2 2.1 %gram.1 = f32[3,16,128]{2,1,0:T(8,128)S(1)} custom-call(bf16[16,192,512]{2,1,0:T(8,128)(2,1)S(1)} %all-to-all-done.x), custom_call_target="tpu_custom_call" | custom-call | flops 805306368 | bytes 3145728 | tf_op jit(solution)/shard_map/gram/pallas_call | solution.py:264
  142.3 4.5 %collective-permute-start.16 = (f32[3,16,128]{2,1,0:T(8,128)S(1)}, f32[3,16,128]{2,1,0:T(8,128)S(1)}, u32[]{:S(2)}, u32[]{:S(2)}) collective-permute-start(f32[3,16,128]{2,1,0:T(8,128)S(1)} %gram.1), channel_id=1, source_target_pairs={{0,6},{1,7},{2,0},{3,1},{4,2},{5,3},{6,4},{7,5},{8,14},{9,15},{10,... | collective-permute-start | bytes 73736 | tf_op jit(solution)/shard_map/ppermute | solution.py:338
  146.8 1.9 %collective-permute-start.14 = (f32[3,16,128]{2,1,0:T(8,128)S(1)}, f32[3,16,128]{2,1,0:T(8,128)S(1)}, u32[]{:S(2)}, u32[]{:S(2)}) collective-permute-start(f32[3,16,128]{2,1,0:T(8,128)S(1)} %gram.1), channel_id=1, source_target_pairs={{0,4},{1,5},{2,6},{3,7},{4,0},{5,1},{6,2},{7,3},{8,12},{9,13},{10,... | collective-permute-start | bytes 73736 | tf_op jit(solution)/shard_map/ppermute | solution.py:338
  148.7 2.0 %collective-permute-done.15 = f32[3,16,128]{2,1,0:T(8,128)S(1)} collective-permute-done((f32[3,16,128]{2,1,0:T(8,128)S(1)}, f32[3,16,128]{2,1,0:T(8,128)S(1)}, u32[]{:S(2)}, u32[]{:S(2)}) %collective-permute-start.15) | collective-permute-done | bytes 24608 | tf_op jit(solution)/shard_map/ppermute | solution.py:338
  151.0 2.8 %collective-permute-start.19 = (f32[3,16,128]{2,1,0:T(8,128)S(1)}, f32[3,16,128]{2,1,0:T(8,128)S(1)}, u32[]{:S(2)}, u32[]{:S(2)}) collective-permute-start(f32[3,16,128]{2,1,0:T(8,128)S(1)} %add_add_fusion.1), channel_id=1, source_target_pairs={{0,24},{1,25},{2,26},{3,27},{4,28},{5,29},{6,30},{7,31},{8,0},{9,1... | collective-permute-start | bytes 73736 | tf_op jit(solution)/shard_map/ppermute | solution.py:338
  153.8 4.2 %collective-permute-start.17 = (f32[3,16,128]{2,1,0:T(8,128)S(1)}, f32[3,16,128]{2,1,0:T(8,128)S(1)}, u32[]{:S(2)}, u32[]{:S(2)}) collective-permute-start(f32[3,16,128]{2,1,0:T(8,128)S(1)} %add_add_fusion.1), channel_id=1, source_target_pairs={{0,16},{1,17},{2,18},{3,19},{4,20},{5,21},{6,22},{7,23},{8,24},{9,... | collective-permute-start | bytes 73736 | tf_op jit(solution)/shard_map/ppermute | solution.py:338
  158.1 1.4 collective-permute-done.17
  159.5 4.4 %collective-permute-start.20 = (f32[3,16,128]{2,1,0:T(8,128)S(1)}, f32[3,16,128]{2,1,0:T(8,128)S(1)}, u32[]{:S(2)}, u32[]{:S(2)}) collective-permute-start(f32[3,16,128]{2,1,0:T(8,128)S(1)} %add_add_fusion), channel_id=1, source_target_pairs={{0,1},{1,0},{2,3},{3,2},{4,5},{5,4},{6,7},{7,6},{8,9},{9,8},{10,11... | collective-permute-start | bytes 73736 | tf_op jit(solution)/shard_map/ppermute | solution.py:338
  164.0 0.8 collective-permute-done.20
  164.9 1.8 %finish.1 = (f32[64,512]{1,0:T(8,128)}, f32[64,512]{1,0:T(8,128)}, f32[16,2048]{1,0:T(8,128)}, f32[64,512]{1,0:T(8,128)}, f32[64,512]{1,0:T(8,128)}, /*index=5*/f32[16,2048]{1,0:T(8,128)}) custom-call(bf16[16,192,512]{2,1,0:T(8,128)(2,1)S(1)} %all-to-all-done.x, f32[3,16,128]{2,1,0:T(8,128)S(1)} %add.27.g_ref, f32[64,512]{1,0:T(8,128)S(1)} %bitcast.20, ...), custom_call_target="tpu_custom_call" | custom-call | flops 4194304 | bytes 6291456 | tf_op jit(solution)/shard_map/finish/pallas_call | solution.py:306
  (63 shorter events, 3.5 us)
Async XLA Ops:
  7.2 56.0 %all-gather.3.cloned.1.call-start = ((), (), s32[]{:S(2)}) async-start(), calls=%async_computation.1 | async-start | bytes 6488064 | tf_op jit(solution)/shard_map/all_gather | solution.py:384
  9.9 12.3 %collective-permute-start.2 = (s32[1,512]{1,0:T(1,128)}, s32[1,512]{1,0:T(1,128)S(1)}, u32[]{:S(2)}, u32[]{:S(2)}) collective-permute-start(s32[1,512]{1,0:T(1,128)} %i0), channel_id=1, source_target_pairs={{0,32},{32,64},{64,96},{96,0},{1,33},{33,65},{65,97},{97,1},{2,34}... | collective-permute-start | bytes 6152 | tf_op jit(solution)/shard_map/ppermute | solution.py:338
  12.1 10.1 %collective-permute-start.1 = (s32[1,512]{1,0:T(1,128)}, s32[1,512]{1,0:T(1,128)S(1)}, u32[]{:S(2)}, u32[]{:S(2)}) collective-permute-start(s32[1,512]{1,0:T(1,128)} %i0), channel_id=1, source_target_pairs={{0,64},{32,96},{64,0},{96,32},{1,65},{33,97},{65,1},{97,33},{2,66}... | collective-permute-start | bytes 6152 | tf_op jit(solution)/shard_map/ppermute | solution.py:338
  14.7 7.5 %collective-permute-start = (s32[1,512]{1,0:T(1,128)}, s32[1,512]{1,0:T(1,128)S(1)}, u32[]{:S(2)}, u32[]{:S(2)}) collective-permute-start(s32[1,512]{1,0:T(1,128)} %i0), channel_id=1, source_target_pairs={{0,96},{32,0},{64,32},{96,64},{1,97},{33,1},{65,33},{97,65},{2,98}... | collective-permute-start | bytes 6152 | tf_op jit(solution)/shard_map/ppermute | solution.py:338
  15.7 1.6 copy-start.8
  17.3 1.6 copy-start.9
  18.9 0.7 copy-start.15
  22.1 1.5 copy-start.19
  23.6 5.3 %copy-start.10 = (bf16[2048,512]{1,0:T(8,128)(2,1)S(1)}, bf16[2048,512]{1,0:T(8,128)(2,1)}, u32[]{:S(2)}) copy-start(bf16[2048,512]{1,0:T(8,128)(2,1)} %refs_1_.10) | copy-start | bytes 6291460
  23.6 14.9 %collective-permute-start.8 = (bf16[512,512]{1,0:T(8,128)(2,1)S(1)}, bf16[512,512]{1,0:T(8,128)(2,1)S(1)}, u32[]{:S(2)}, u32[]{:S(2)}) collective-permute-start(bf16[512,512]{1,0:T(8,128)(2,1)S(1)} %pick_rows.13), channel_id=1, source_target_pairs={{0,96},{32,0},{64,32},{96,64},{1,97},{33,1},{65,33},{97,65},{2,98}... | collective-permute-start | bytes 1572872 | tf_op jit(solution)/shard_map/ppermute | solution.py:338
  25.1 14.2 %collective-permute-start.7 = (bf16[512,512]{1,0:T(8,128)(2,1)S(1)}, bf16[512,512]{1,0:T(8,128)(2,1)S(1)}, u32[]{:S(2)}, u32[]{:S(2)}) collective-permute-start(bf16[512,512]{1,0:T(8,128)(2,1)S(1)} %pick_rows.12), channel_id=1, source_target_pairs={{0,64},{32,96},{64,0},{96,32},{1,65},{33,97},{65,1},{97,33},{2,66}... | collective-permute-start | bytes 1572872 | tf_op jit(solution)/shard_map/ppermute | solution.py:338
  28.8 25.0 %collective-permute-start.6 = (bf16[512,512]{1,0:T(8,128)(2,1)S(1)}, bf16[512,512]{1,0:T(8,128)(2,1)S(1)}, u32[]{:S(2)}, u32[]{:S(2)}) collective-permute-start(bf16[512,512]{1,0:T(8,128)(2,1)S(1)} %pick_rows.11), channel_id=1, source_target_pairs={{0,32},{32,64},{64,96},{96,0},{1,33},{33,65},{65,97},{97,1},{2,34}... | collective-permute-start | bytes 1572872 | tf_op jit(solution)/shard_map/ppermute | solution.py:338
  31.1 37.9 %collective-permute-start.5 = (bf16[512,512]{1,0:T(8,128)(2,1)}, bf16[512,512]{1,0:T(8,128)(2,1)S(1)}, u32[]{:S(2)}, u32[]{:S(2)}) collective-permute-start(bf16[512,512]{1,0:T(8,128)(2,1)} %pick_rows.10), channel_id=1, source_target_pairs={{0,96},{32,0},{64,32},{96,64},{1,97},{33,1},{65,33},{97,65},{2,98}... | collective-permute-start | bytes 1572872 | tf_op jit(solution)/shard_map/ppermute | solution.py:338
  38.3 30.7 %collective-permute-start.4 = (bf16[512,512]{1,0:T(8,128)(2,1)}, bf16[512,512]{1,0:T(8,128)(2,1)S(1)}, u32[]{:S(2)}, u32[]{:S(2)}) collective-permute-start(bf16[512,512]{1,0:T(8,128)(2,1)} %pick_rows.9), channel_id=1, source_target_pairs={{0,64},{32,96},{64,0},{96,32},{1,65},{33,97},{65,1},{97,33},{2,66}... | collective-permute-start | bytes 1572872 | tf_op jit(solution)/shard_map/ppermute | solution.py:338
  38.5 35.9 %collective-permute-start.3 = (bf16[512,512]{1,0:T(8,128)(2,1)}, bf16[512,512]{1,0:T(8,128)(2,1)}, u32[]{:S(2)}, u32[]{:S(2)}) collective-permute-start(bf16[512,512]{1,0:T(8,128)(2,1)} %pick_rows.8), channel_id=1, source_target_pairs={{0,32},{32,64},{64,96},{96,0},{1,33},{33,65},{65,97},{97,1},{2,34}... | collective-permute-start | bytes 1572872 | tf_op jit(solution)/shard_map/ppermute | solution.py:338
  63.2 2.8 %copy-start.1 = (bf16[3072,1024]{1,0:T(8,128)(2,1)S(1)}, bf16[3072,1024]{1,0:T(8,128)(2,1)}, u32[]{:S(2)}) copy-start(bf16[3072,1024]{1,0:T(8,128)(2,1)} %all-gather.3.cloned.1.call-done) | copy-start | bytes 18874372
  66.0 8.4 %copy-start.14 = (f32[1,512]{1,0:T(1,128)S(1)}, f32[1,512]{1,0:T(1,128)}, u32[]{:S(2)}) copy-start(f32[1,512]{1,0:T(1,128)} %route_ref.1) | copy-start | bytes 6148
  66.0 8.4 %copy-start.20 = (bf16[512,512]{1,0:T(8,128)(2,1)S(1)}, bf16[512,512]{1,0:T(8,128)(2,1)}, u32[]{:S(2)}) copy-start(bf16[512,512]{1,0:T(8,128)(2,1)} %copy-done.19) | copy-start | bytes 1572868
  80.5 5.9 %collective-permute-start.9 = (bf16[16,192,512]{2,1,0:T(8,128)(2,1)S(1)}, bf16[16,192,512]{2,1,0:T(8,128)(2,1)S(1)}, u32[]{:S(2)}, u32[]{:S(2)}) collective-permute-start(bf16[16,192,512]{2,1,0:T(8,128)(2,1)S(1)} %get-tuple-element.47), channel_id=1, source_target_pairs={{0,1},{1,0},{2,3},{3,2},{4,5},{5,4},{6,7},{7,6},{8,9},{9,8},{10,11... | collective-permute-start | bytes 9437192 | tf_op jit(solution)/shard_map/ppermute | solution.py:338
  83.5 3.7 %copy-start.11 = (bf16[512,512]{1,0:T(8,128)(2,1)}, bf16[512,512]{1,0:T(8,128)(2,1)S(1)}, u32[]{:S(2)}) copy-start(bf16[512,512]{1,0:T(8,128)(2,1)S(1)} %get-tuple-element.52) | copy-start | bytes 1572868
  83.5 3.7 %copy-start.12 = (bf16[512,512]{1,0:T(8,128)(2,1)}, bf16[512,512]{1,0:T(8,128)(2,1)S(1)}, u32[]{:S(2)}) copy-start(bf16[512,512]{1,0:T(8,128)(2,1)S(1)} %get-tuple-element.51) | copy-start | bytes 1572868
  83.5 3.7 %copy-start.13 = (bf16[512,512]{1,0:T(8,128)(2,1)}, bf16[512,512]{1,0:T(8,128)(2,1)S(1)}, u32[]{:S(2)}) copy-start(bf16[512,512]{1,0:T(8,128)(2,1)S(1)} %get-tuple-element.50) | copy-start | bytes 1572868
  83.5 3.7 %copy-start.17 = (bf16[512,512]{1,0:T(8,128)(2,1)}, bf16[512,512]{1,0:T(8,128)(2,1)S(1)}, u32[]{:S(2)}) copy-start(bf16[512,512]{1,0:T(8,128)(2,1)S(1)} %get-tuple-element.49.g0) | copy-start | bytes 1572868
  87.2 1.3 collective-permute-start.10
  90.3 1.6 copy-start
  91.9 35.0 %copy-start.16 = (s32[1,512]{1,0:T(1,128)S(1)}, s32[1,512]{1,0:T(1,128)}, u32[]{:S(2)}) copy-start(s32[1,512]{1,0:T(1,128)} %i0) | copy-start | bytes 6148
  91.9 48.4 %all-to-all-start = ((bf16[16,192,512]{2,1,0:T(8,128)(2,1)}), bf16[16,192,512]{2,1,0:T(8,128)(2,1)S(1)}, u32[]{:S(2)}, u32[]{:S(2)}) async-start(bf16[16,192,512]{2,1,0:T(8,128)(2,1)} %copy-done), calls=%async_computation | async-start | bytes 6291456 | tf_op jit(solution)/shard_map/all_to_all | solution.py:406
  99.6 13.1 %collective-permute-start.11 = (bf16[512,512]{1,0:T(8,128)(2,1)}, bf16[512,512]{1,0:T(8,128)(2,1)S(1)}, u32[]{:S(2)}, u32[]{:S(2)}) collective-permute-start(bf16[512,512]{1,0:T(8,128)(2,1)} %copy-done.13), channel_id=1, source_target_pairs={{0,96},{32,0},{64,32},{96,64},{1,97},{33,1},{65,33},{97,65},{2,98}... | collective-permute-start | bytes 1572872 | tf_op jit(solution)/shard_map/ppermute | solution.py:338
  100.0 14.3 %collective-permute-start.12 = (bf16[512,512]{1,0:T(8,128)(2,1)}, bf16[512,512]{1,0:T(8,128)(2,1)S(1)}, u32[]{:S(2)}, u32[]{:S(2)}) collective-permute-start(bf16[512,512]{1,0:T(8,128)(2,1)} %copy-done.12), channel_id=1, source_target_pairs={{0,64},{32,96},{64,0},{96,32},{1,65},{33,97},{65,1},{97,33},{2,66}... | collective-permute-start | bytes 1572872 | tf_op jit(solution)/shard_map/ppermute | solution.py:338
  102.2 24.6 %collective-permute-start.13 = (bf16[512,512]{1,0:T(8,128)(2,1)}, bf16[512,512]{1,0:T(8,128)(2,1)S(1)}, u32[]{:S(2)}, u32[]{:S(2)}) collective-permute-start(bf16[512,512]{1,0:T(8,128)(2,1)} %copy-done.11), channel_id=1, source_target_pairs={{0,32},{32,64},{64,96},{96,0},{1,33},{33,65},{65,97},{97,1},{2,34}... | collective-permute-start | bytes 1572872 | tf_op jit(solution)/shard_map/ppermute | solution.py:338
  126.8 1.0 copy-start.18
  133.9 31.0 %copy-start.2 = (f32[1,64,512]{2,1,0:T(8,128)S(1)}, f32[1,64,512]{2,1,0:T(8,128)}, u32[]{:S(2)}) copy-start(f32[1,64,512]{2,1,0:T(8,128)} %param.15) | copy-start | bytes 393220
  133.9 31.0 %copy-start.3 = (f32[1,64,512]{2,1,0:T(8,128)S(1)}, f32[1,64,512]{2,1,0:T(8,128)}, u32[]{:S(2)}) copy-start(f32[1,64,512]{2,1,0:T(8,128)} %param.14) | copy-start | bytes 393220
  133.9 31.0 %copy-start.4 = (f32[1,16,2048]{2,1,0:T(8,128)S(1)}, f32[1,16,2048]{2,1,0:T(8,128)}, u32[]{:S(2)}) copy-start(f32[1,16,2048]{2,1,0:T(8,128)} %param.16) | copy-start | bytes 393220
  140.2 24.6 %copy-start.5 = (f32[1,64,512]{2,1,0:T(8,128)S(1)}, f32[1,64,512]{2,1,0:T(8,128)}, u32[]{:S(2)}) copy-start(f32[1,64,512]{2,1,0:T(8,128)} %param.17) | copy-start | bytes 393220
  140.2 24.6 %copy-start.6 = (f32[1,64,512]{2,1,0:T(8,128)S(1)}, f32[1,64,512]{2,1,0:T(8,128)}, u32[]{:S(2)}) copy-start(f32[1,64,512]{2,1,0:T(8,128)} %param.18) | copy-start | bytes 393220
  140.2 24.6 %copy-start.7 = (f32[1,16,2048]{2,1,0:T(8,128)S(1)}, f32[1,16,2048]{2,1,0:T(8,128)}, u32[]{:S(2)}) copy-start(f32[1,16,2048]{2,1,0:T(8,128)} %param.19) | copy-start | bytes 393220
  142.3 6.4 %collective-permute-start.16 = (f32[3,16,128]{2,1,0:T(8,128)S(1)}, f32[3,16,128]{2,1,0:T(8,128)S(1)}, u32[]{:S(2)}, u32[]{:S(2)}) collective-permute-start(f32[3,16,128]{2,1,0:T(8,128)S(1)} %gram.1), channel_id=1, source_target_pairs={{0,6},{1,7},{2,0},{3,1},{4,2},{5,3},{6,4},{7,5},{8,14},{9,15},{10,... | collective-permute-start | bytes 73736 | tf_op jit(solution)/shard_map/ppermute | solution.py:338
  146.8 3.9 %collective-permute-start.15 = (f32[3,16,128]{2,1,0:T(8,128)S(1)}, f32[3,16,128]{2,1,0:T(8,128)S(1)}, u32[]{:S(2)}, u32[]{:S(2)}) collective-permute-start(f32[3,16,128]{2,1,0:T(8,128)S(1)} %gram.1), channel_id=1, source_target_pairs={{0,2},{1,3},{2,4},{3,5},{4,6},{5,7},{6,0},{7,1},{8,10},{9,11},{10,... | collective-permute-start | bytes 73736 | tf_op jit(solution)/shard_map/ppermute | solution.py:338
  146.8 4.2 %collective-permute-start.14 = (f32[3,16,128]{2,1,0:T(8,128)S(1)}, f32[3,16,128]{2,1,0:T(8,128)S(1)}, u32[]{:S(2)}, u32[]{:S(2)}) collective-permute-start(f32[3,16,128]{2,1,0:T(8,128)S(1)} %gram.1), channel_id=1, source_target_pairs={{0,4},{1,5},{2,6},{3,7},{4,0},{5,1},{6,2},{7,3},{8,12},{9,13},{10,... | collective-permute-start | bytes 73736 | tf_op jit(solution)/shard_map/ppermute | solution.py:338
  151.0 7.0 %collective-permute-start.19 = (f32[3,16,128]{2,1,0:T(8,128)S(1)}, f32[3,16,128]{2,1,0:T(8,128)S(1)}, u32[]{:S(2)}, u32[]{:S(2)}) collective-permute-start(f32[3,16,128]{2,1,0:T(8,128)S(1)} %add_add_fusion.1), channel_id=1, source_target_pairs={{0,24},{1,25},{2,26},{3,27},{4,28},{5,29},{6,30},{7,31},{8,0},{9,1... | collective-permute-start | bytes 73736 | tf_op jit(solution)/shard_map/ppermute | solution.py:338
  153.8 4.2 %collective-permute-start.18 = (f32[3,16,128]{2,1,0:T(8,128)S(1)}, f32[3,16,128]{2,1,0:T(8,128)S(1)}, u32[]{:S(2)}, u32[]{:S(2)}) collective-permute-start(f32[3,16,128]{2,1,0:T(8,128)S(1)} %add_add_fusion.1), channel_id=1, source_target_pairs={{0,8},{1,9},{2,10},{3,11},{4,12},{5,13},{6,14},{7,15},{8,16},{9,17... | collective-permute-start | bytes 73736 | tf_op jit(solution)/shard_map/ppermute | solution.py:338
  153.8 5.7 %collective-permute-start.17 = (f32[3,16,128]{2,1,0:T(8,128)S(1)}, f32[3,16,128]{2,1,0:T(8,128)S(1)}, u32[]{:S(2)}, u32[]{:S(2)}) collective-permute-start(f32[3,16,128]{2,1,0:T(8,128)S(1)} %add_add_fusion.1), channel_id=1, source_target_pairs={{0,16},{1,17},{2,18},{3,19},{4,20},{5,21},{6,22},{7,23},{8,24},{9,... | collective-permute-start | bytes 73736 | tf_op jit(solution)/shard_map/ppermute | solution.py:338
  159.5 5.3 %collective-permute-start.20 = (f32[3,16,128]{2,1,0:T(8,128)S(1)}, f32[3,16,128]{2,1,0:T(8,128)S(1)}, u32[]{:S(2)}, u32[]{:S(2)}) collective-permute-start(f32[3,16,128]{2,1,0:T(8,128)S(1)} %add_add_fusion), channel_id=1, source_target_pairs={{0,1},{1,0},{2,3},{3,2},{4,5},{5,4},{6,7},{7,6},{8,9},{9,8},{10,11... | collective-permute-start | bytes 73736 | tf_op jit(solution)/shard_map/ppermute | solution.py:338
Sparse Core Ops, SparseCore 0:
  10.3 52.8 all-gather.2

commit v3 on v2

--- a/solution.py
+++ b/solution.py
@@ -13,6 +13,7 @@
 N_CHIP = 16
 SLICE = 512
 ROWS = 192
+EARLY = 160
 
 momentum_decay = 0.9
 learning_rate = 0.05
@@ -131,14 +132,17 @@
 
 
 def backward(cots, route, hidden_t, gate_factor, act, xt, weights):
-    def body(c0, c1, c2, c3, route_ref, hid_t, factor, act_ref, xt_ref, w, keep, send, both, hg, scaled):
+    def body(*refs):
+        early, late = refs[:4], refs[4:8]
+        route_ref, hid_t, factor, act_ref, xt_ref, w, keep, send, both, hg, scaled = refs[8:]
         first = lax.axis_index("dp") % 2 == 0
         scale = column(route_ref[...])
-        for k, c in enumerate((c0, c1, c2, c3)):
+        for k in range(N_EXPERT):
             s = slice_of(k)
             for j in range(SLICE // 128):
                 cols = slice(128 * j, 128 * (j + 1))
-                scaled[:, cols] = (scale * c[:, cols].astype(F32)).astype(BF16)
+                scaled[:EARLY, cols] = (scale[:EARLY] * early[k][:, cols].astype(F32)).astype(BF16)
+                scaled[EARLY:, cols] = (scale[EARLY:] * late[k][:, cols].astype(F32)).astype(BF16)
             part = lax.dot_general(scaled[...], down_block(w, s), NT, preferred_element_type=F32)
             if k == 0:
                 hg[...] = part
@@ -175,7 +179,7 @@
     return call(
         body,
         "backward",
-        10,
+        14,
         shapes,
         8 * TOK_DEV * D * H,
         20 * MIB,
@@ -360,6 +364,80 @@
     return value + other_core(value)
 
 
+def pack(gate, up, down):
+    def body(g, u, d, out):
+        out[0:64, 0:H] = g[...].astype(BF16)
+        out[0:64, H:] = u[...].astype(BF16)
+        out[64:80, :] = d[:, : D // 2].astype(BF16)
+        out[80:96, :] = d[:, D // 2 :].astype(BF16)
+
+    return call(body, "pack", 3, struct((96, 1024), BF16), 2**17, MIB)(gate, up, down)
+
+
+def along(turn, step):
+    def to(i):
+        x, z, c = i // 8, i // 2 % 4, i % 2
+        return x * 8 + (z + step) % 4 * 2 + c if c == turn else (x + step) % 4 * 8 + z * 2 + c
+
+    return to
+
+
+def ring_near(block, turn):
+    return shift(block, "dp", along(turn, 1)), shift(block, "dp", along(turn, 3))
+
+
+def ring_far(before, after, turn):
+    half = before.shape[0] // 2
+    return shift(before[:half], "dp", along(turn, 1)), shift(after[half:], "dp", along(turn, 3))
+
+
+def place(turn):
+    at = lax.axis_index("dp")
+    x, z, c = at // 8, lax.rem(at // 2, 4), lax.rem(at, 2)
+    return c, jnp.where(c == turn, z, x)
+
+
+def bundle(blocks):
+    def body(own, before, after, low, high, out):
+        _, at = place(0)
+        out[at] = own[...]
+        out[lax.rem(at + 3, 4)] = before[...]
+        out[lax.rem(at + 1, 4)] = after[...]
+        far = lax.rem(at + 2, 4)
+        out[far, 0:48, :] = low[...]
+        out[far, 48:96, :] = high[...]
+
+    return call(body, "bundle", 5, struct((4, 96, 1024), BF16), 2**10, 2 * MIB)(*blocks)
+
+
+def half_of_weights(bundles):
+    def body(own, before, after, low, high, out):
+        c, at = place(1)
+
+        def put(j, other, value):
+            out[jnp.where(c == 0, other * 4 + j, j * 4 + other)] = value
+
+        for j in range(4):
+            put(j, at, own[j])
+            put(j, lax.rem(at + 3, 4), before[j])
+            put(j, lax.rem(at + 1, 4), after[j])
+            put(j, lax.rem(at + 2, 4), (low, high)[j // 2][j % 2])
+
+    return call(body, "half_of_weights", 5, struct((N_CHIP, 96, 1024), BF16), 2**10, 6 * MIB)(*bundles)
+
+
+def whole_weights(own, other):
+    def body(a, b, out):
+        c = lax.rem(lax.axis_index("dp"), 2)
+
+        @pl.loop(0, N_CHIP)
+        def _(q):
+            out[2 * q + c] = a[q]
+            out[2 * q + 1 - c] = b[q]
+
+    return call(body, "whole_weights", 2, struct((2 * N_CHIP, 96, 1024), BF16), 2**10, 12 * MIB)(own, other)
+
+
 def local(
     pool_tokens,
     pool_cotangent,
@@ -372,26 +450,33 @@
     momentum_up,
     momentum_down,
 ):
-    down_halves = down_weight[0].astype(BF16)
-    shard = jnp.concatenate(
-        [
-            jnp.concatenate([gate_weight[0].astype(BF16), up_weight[0].astype(BF16)], axis=1),
-            down_halves[:, : D // 2],
-            down_halves[:, D // 2 :],
-        ],
-        axis=0,
-    )
-    weights = lax.all_gather(shard, "dp", axis=0, tiled=False)
-
+    tie = lax.optimization_barrier
     ids = [token_ids] + [around_y(token_ids, N_EXPERT - k) for k in (1, 2, 3)]
+    packed = pack(gate_weight[0], up_weight[0], down_weight[0])
+    near = ring_near(packed, 0)
     own_x, own_c = pick_rows(ids[:1], [pool_tokens, pool_cotangent])
-    ids, own_x, own_c = lax.optimization_barrier((ids, own_x, own_c))
-    sent_x, sent_c = [None] * 3, [None] * 3
-    for sent, pool in ((sent_x, pool_tokens), (sent_c, pool_cotangent)):
-        for k in (2, 1, 3):
-            (sent[k - 1],) = pick_rows(ids[k : k + 1], [pool])
-    tokens = [own_x] + [around_y(sent_x[k - 1], k) for k in (1, 2, 3)]
-    cots = [own_c] + [around_y(sent_c[k - 1], k) for k in (1, 2, 3)]
+    ids, own_x, own_c, near = tie((ids, own_x, own_c, near))
+
+    far = ring_far(*near, 0)
+    sent_x = [pick_rows(ids[k : k + 1], [pool_tokens])[0] for k in (1, 2, 3)]
+    far, sent_x = tie((far, sent_x))
+
+    tokens = [around_y(sent_x[k - 1], k) for k in (1, 2, 3)]
+    block = bundle((packed, *near, *far))
+    near = ring_near(block, 1)
+    sent_c = [pick_rows(ids[k : k + 1], [pool_cotangent])[0] for k in (1, 2, 3)]
+    near, tokens, sent_c = tie((near, tokens, sent_c))
+    tokens = [own_x, *tokens]
+
+    far = ring_far(*near, 1)
+    early = [around_y(sent_c[k - 1][:EARLY], k) for k in (1, 2, 3)]
+    late = [sent_c[k - 1][EARLY:] for k in (1, 2, 3)]
+    far, early, late = tie((far, early, late))
+
+    late = [around_y(late[k - 1], k) for k in (1, 2, 3)]
+    cots = [own_c[:EARLY], *early, own_c[EARLY:], *late]
+    mine = half_of_weights((block, *near, *far))
+    weights = whole_weights(mine, other_core(mine))
 
     hidden_t, gate_factor, act, xt = forward(tokens, weights)
     keep, send, both = backward(cots, route_weights, hidden_t, gate_factor, act, xt, weights)

time: 174 us -> 183 us (1.052)
  starting transfers between devices: 41.7 us -> 57.1 us
  between operations: 14.3 us -> 1.05 us
  waiting for transfers between devices: 68.1 us -> 80.9 us
  Pallas kernels: 37.3 us -> 34.5 us
  other arithmetic: 2.64 us -> 0.02 us
    ppermute x21 -> x33, waiting for transfers between devices: 52.3 us -> 75.5 us  [shift(): lax.ppermute(block, axis, [(i, to(i)) for i in range(lax.axis_size(axis))])]
    ppermute x21 -> x33, starting transfers between devices: 34 us -> 51.2 us  [shift(): lax.ppermute(block, axis, [(i, to(i)) for i in range(lax.axis_size(axis))])]
    all_gather x1 -> x0, waiting for transfers between devices: 9.4 us -> none  [local(): weights = lax.all_gather(shard, 'dp', axis=0, tiled=False)]
    pallas_call x7, Pallas kernels: 13.5 us -> 10.9 us  [pick_rows(): call(body, 'pick_rows', n_ids + n_pool, shapes, 2 * TOK_DEV * POOL * SLIC...]
    convert_element_type x2 -> x0, other arithmetic: 1.9 us -> none  [the longest x1 0.99 us: local(): up_weight[0].astype(BF16)]
    pallas_call x1 -> x5, Pallas kernels: 6.19 us -> 5.92 us  [the longest x1 5.13 us: backward(): call(body, 'backward', 14, shapes, 8 * TOK_DEV * D * H, 20 * MIB, [pltpu....]
  transfers between devices with their start and end apart: 23 -> 34, of which waited for: 13 -> 19; matrix products, arithmetic and copies ran while one was open for 0% -> 0% of each run, Pallas kernels for 14% -> 12%
where the time goes in v3:
time: 183 us
  waiting for transfers between devices  80.9 us (44%)
  starting transfers between devices  57.1 us (31%)
  Pallas kernels  34.5 us (19%)
  local copies, waits for them, and re-layouts  9.51 us (5%)
    ppermute x33, waiting for transfers between devices, shift(): lax.ppermute(block, axis, [(i, to(i)) for i in range(lax.axis_size(axis))])  75.5 us
    ppermute x33, starting transfers between devices, shift(): lax.ppermute(block, axis, [(i, to(i)) for i in range(lax.axis_size(axis))])  51.2 us
    pallas_call x7, Pallas kernels, pick_rows(): call(body, 'pick_rows', n_ids + n_pool, shapes, 2 * TOK_DEV * POOL * SLIC...  10.9 us
    unnamed x42, local copies, waits for them, and re-layouts  9.29 us
    pallas_call x1, Pallas kernels, scatter_rows(): pl.pallas_call(body, name='scatter_rows', grid=(POOL // block,), out_shap...  5.97 us
    all_to_all x1, starting transfers between devices, local(): lax.all_to_all(merged, 'dp', 0, 0, tiled=True, axis_index_groups=groups)  5.96 us
    all_to_all x1, waiting for transfers between devices, local(): lax.all_to_all(merged, 'dp', 0, 0, tiled=True, axis_index_groups=groups)  5.31 us
    pallas_call x1, Pallas kernels, backward(): call(body, 'backward', 14, shapes, 8 * TOK_DEV * D * H, 20 * MIB, [pltpu....  5.13 us
  transfers between devices with their start and end apart: 34, of which 19 were waited for; matrix products, arithmetic and copies ran while one was open for 0% of the time, Pallas kernels for 12%

profile of v3, /device:TPU:1, one launch (start us, length us, event | category | flops | bytes accessed | tf_op | source)
XLA Modules:
  0.0 183.0 jit_solution(1183621510139777249)
XLA Ops:
  0.6 2.2 %collective-permute-start.2 = (s32[1,512]{1,0:T(1,128)}, s32[1,512]{1,0:T(1,128)S(1)}, u32[]{:S(2)}, u32[]{:S(2)}) collective-permute-start(s32[1,512]{1,0:T(1,128)} %i0), channel_id=1, source_target_pairs={{0,32},{32,64},{64,96},{96,0},{1,33},{33,65},{65,97},{97,1},{2,34}... | collective-permute-start | bytes 6152 | tf_op jit(solution)/shard_map/ppermute | solution.py:342
  2.8 2.6 %collective-permute-start.1 = (s32[1,512]{1,0:T(1,128)}, s32[1,512]{1,0:T(1,128)S(1)}, u32[]{:S(2)}, u32[]{:S(2)}) collective-permute-start(s32[1,512]{1,0:T(1,128)} %i0), channel_id=1, source_target_pairs={{0,64},{32,96},{64,0},{96,32},{1,65},{33,97},{65,1},{97,33},{2,66}... | collective-permute-start | bytes 6152 | tf_op jit(solution)/shard_map/ppermute | solution.py:342
  9.3 2.5 %collective-permute-start.4 = (bf16[96,1024]{1,0:T(8,128)(2,1)S(1)}, bf16[96,1024]{1,0:T(8,128)(2,1)S(1)}, u32[]{:S(2)}, u32[]{:S(2)}) collective-permute-start(bf16[96,1024]{1,0:T(8,128)(2,1)S(1)} %pack.1.own), channel_id=1, source_target_pairs={{0,6},{1,25},{2,0},{3,27},{4,2},{5,29},{6,4},{7,31},{8,14},{9,1},{... | collective-permute-start | bytes 589832 | tf_op jit(solution)/shard_map/ppermute | solution.py:342
  11.8 1.6 copy-done.10
  13.4 1.6 copy-done.11
  15.7 2.5 %pick_rows.7 = (bf16[512,512]{1,0:T(8,128)(2,1)S(1)}, bf16[512,512]{1,0:T(8,128)(2,1)S(1)}) custom-call(s32[1,512]{1,0:T(1,128)S(1)} %copy-done.17, bf16[2048,512]{1,0:T(8,128)(2,1)S(1)} %copy-done.10, bf16[2048,512]{1,0:T(8,128)(2,1)S(1)} %copy-done.11), custom_call_target="tpu_custom_call" | custom-call | flops 2147483648 | bytes 3145728 | tf_op jit(solution)/shard_map/pick_rows/pallas_call | solution.py:69
  18.3 2.7 %collective-permute-start.6 = (bf16[48,1024]{1,0:T(8,128)(2,1)S(1)}, bf16[48,1024]{1,0:T(8,128)(2,1)S(1)}, u32[]{:S(2)}, u32[]{:S(2)}) collective-permute-start(bf16[48,1024]{1,0:T(8,128)(2,1)S(1)} %slice.38), channel_id=1, source_target_pairs={{0,6},{1,25},{2,0},{3,27},{4,2},{5,29},{6,4},{7,31},{8,14},{9,1},{... | collective-permute-start | bytes 294920 | tf_op jit(solution)/shard_map/ppermute | solution.py:342
  21.0 1.4 pick_rows.8
  22.4 1.4 pick_rows.9
  23.8 1.4 pick_rows.10
  25.8 4.1 %collective-permute-start.8 = (bf16[4,96,1024]{2,1,0:T(8,128)(2,1)S(1)}, bf16[4,96,1024]{2,1,0:T(8,128)(2,1)S(1)}, u32[]{:S(2)}, u32[]{:S(2)}) collective-permute-start(bf16[4,96,1024]{2,1,0:T(8,128)(2,1)S(1)} %bundle.1.own), channel_id=1, source_target_pairs={{0,24},{1,7},{2,26},{3,1},{4,28},{5,3},{6,30},{7,5},{8,0},{9,15},{... | collective-permute-start | bytes 2359304 | tf_op jit(solution)/shard_map/ppermute | solution.py:342
  30.8 1.8 %collective-permute-start.11 = (bf16[512,512]{1,0:T(8,128)(2,1)S(1)}, bf16[512,512]{1,0:T(8,128)(2,1)S(1)}, u32[]{:S(2)}, u32[]{:S(2)}) collective-permute-start(bf16[512,512]{1,0:T(8,128)(2,1)S(1)} %pick_rows.10), channel_id=1, source_target_pairs={{0,96},{32,0},{64,32},{96,64},{1,97},{33,1},{65,33},{97,65},{2,98}... | collective-permute-start | bytes 1572872 | tf_op jit(solution)/shard_map/ppermute | solution.py:342
  32.7 1.4 pick_rows.11
  34.1 1.4 pick_rows.12
  35.5 1.4 pick_rows.13
  36.9 5.9 %collective-permute-done.9.x1 = bf16[512,512]{1,0:T(8,128)(2,1)S(1)} collective-permute-done((bf16[512,512]{1,0:T(8,128)(2,1)S(1)}, bf16[512,512]{1,0:T(8,128)(2,1)S(1)}, u32[]{:S(2)}, u32[]{:S(2)}) %collective-permute-start.9) | collective-permute-done | bytes 524320 | tf_op jit(solution)/shard_map/ppermute | solution.py:342
  42.7 7.9 %collective-permute-done.10.x2 = bf16[512,512]{1,0:T(8,128)(2,1)S(1)} collective-permute-done((bf16[512,512]{1,0:T(8,128)(2,1)S(1)}, bf16[512,512]{1,0:T(8,128)(2,1)S(1)}, u32[]{:S(2)}, u32[]{:S(2)}) %collective-permute-start.10) | collective-permute-done | bytes 524320 | tf_op jit(solution)/shard_map/ppermute | solution.py:342
  50.6 4.7 %collective-permute-done.11.x3 = bf16[512,512]{1,0:T(8,128)(2,1)S(1)} collective-permute-done((bf16[512,512]{1,0:T(8,128)(2,1)S(1)}, bf16[512,512]{1,0:T(8,128)(2,1)S(1)}, u32[]{:S(2)}, u32[]{:S(2)}) %collective-permute-start.11) | collective-permute-done | bytes 524320 | tf_op jit(solution)/shard_map/ppermute | solution.py:342
  55.4 2.7 %collective-permute-start.13 = (bf16[2,96,1024]{2,1,0:T(8,128)(2,1)S(1)}, bf16[2,96,1024]{2,1,0:T(8,128)(2,1)S(1)}, u32[]{:S(2)}, u32[]{:S(2)}) collective-permute-start(bf16[2,96,1024]{2,1,0:T(8,128)(2,1)S(1)} %slice.40), channel_id=1, source_target_pairs={{0,24},{1,7},{2,26},{3,1},{4,28},{5,3},{6,30},{7,5},{8,0},{9,15},{... | collective-permute-start | bytes 1179656 | tf_op jit(solution)/shard_map/ppermute | solution.py:342
  58.2 3.5 %collective-permute-start.16 = (bf16[160,512]{1,0:T(8,128)(2,1)S(1)}, bf16[160,512]{1,0:T(8,128)(2,1)S(1)}, u32[]{:S(2)}, u32[]{:S(2)}) collective-permute-start(bf16[160,512]{1,0:T(8,128)(2,1)S(1)} %slice.43), channel_id=1, source_target_pairs={{0,96},{32,0},{64,32},{96,64},{1,97},{33,1},{65,33},{97,65},{2,98}... | collective-permute-start | bytes 491528 | tf_op jit(solution)/shard_map/ppermute | solution.py:342
  62.5 6.2 %collective-permute-done.16.refs_3_ = bf16[160,512]{1,0:T(8,128)(2,1)S(1)} collective-permute-done((bf16[160,512]{1,0:T(8,128)(2,1)S(1)}, bf16[160,512]{1,0:T(8,128)(2,1)S(1)}, u32[]{:S(2)}, u32[]{:S(2)}) %collective-permute-start.16) | collective-permute-done | bytes 163872 | tf_op jit(solution)/shard_map/ppermute | solution.py:342
  68.7 3.5 %collective-permute-done.14.refs_1_ = bf16[160,512]{1,0:T(8,128)(2,1)S(1)} collective-permute-done((bf16[160,512]{1,0:T(8,128)(2,1)S(1)}, bf16[160,512]{1,0:T(8,128)(2,1)S(1)}, u32[]{:S(2)}, u32[]{:S(2)}) %collective-permute-start.14) | collective-permute-done | bytes 163872 | tf_op jit(solution)/shard_map/ppermute | solution.py:342
  73.4 1.8 collective-permute-start.18
  76.1 2.5 %collective-permute-done.20.b = bf16[16,96,1024]{2,1,0:T(8,128)(2,1)S(1)} collective-permute-done((bf16[16,96,1024]{2,1,0:T(8,128)(2,1)S(1)}, bf16[16,96,1024]{2,1,0:T(8,128)(2,1)S(1)}, u32[]{:S(2)}, u32[]{:S(2)}) %collective-permute-start.20) | collective-permute-done | bytes 3145760 | tf_op jit(solution)/shard_map/ppermute | solution.py:342
  79.1 3.0 %forward.1 = (bf16[512,512]{1,0:T(8,128)(2,1)S(1)}, f32[512,512]{1,0:T(8,128)S(1)}, f32[512,512]{1,0:T(8,128)S(1)}, bf16[4,512,512]{2,1,0:T(8,128)(2,1)S(1)}) custom-call(bf16[512,512]{1,0:T(8,128)(2,1)S(1)} %get-tuple-element.82.x0, bf16[512,512]{1,0:T(8,128)(2,1)S(1)} %collective-permute-done.9.x1, bf16[512,512]{1,0:T(8,128)(2,1)S(1)} %collective-permute-done.10.x2, ...), custom_call_target="tpu_custom_call" | custom-call | flops 2147483648 | bytes 10485760 | tf_op jit(solution)/shard_map/forward/pallas_call | solution.py:123
  82.2 10.2 %collective-permute-done.17.refs_5_ = bf16[352,512]{1,0:T(8,128)(2,1)S(1)} collective-permute-done((bf16[352,512]{1,0:T(8,128)(2,1)S(1)}, bf16[352,512]{1,0:T(8,128)(2,1)S(1)}, u32[]{:S(2)}, u32[]{:S(2)}) %collective-permute-start.17) | collective-permute-done | bytes 360480 | tf_op jit(solution)/shard_map/ppermute | solution.py:342
  92.6 5.1 %backward.1 = (bf16[16,192,512]{2,1,0:T(8,128)(2,1)S(1)}, bf16[16,192,512]{2,1,0:T(8,128)(2,1)S(1)}, bf16[512,1024]{1,0:T(8,128)(2,1)S(1)}) custom-call(bf16[160,512]{1,0:T(8,128)(2,1)S(1)} %slice.36.refs_0_, bf16[160,512]{1,0:T(8,128)(2,1)S(1)} %collective-permute-done.14.refs_1_, bf16[160,512]{1,0:T(8,128)(2,1)S(1)} %collective-permute-done.15.refs_2_, ...), custom_call_target="tpu_custom_call" | custom-call | flops 4294967296 | bytes 20971520 | tf_op jit(solution)/shard_map/backward/pallas_call | solution.py:179
  97.8 1.3 collective-permute-start.21
  99.0 2.4 %slot_gradients.1 = (bf16[512,512]{1,0:T(8,128)(2,1)S(1)}, bf16[512,512]{1,0:T(8,128)(2,1)S(1)}, bf16[512,512]{1,0:T(8,128)(2,1)S(1)}, bf16[512,512]{1,0:T(8,128)(2,1)S(1)}) custom-call(bf16[512,1024]{1,0:T(8,128)(2,1)S(1)} %get-tuple-element.94.both_ref, bf16[32,96,1024]{2,1,0:T(8,128)(2,1)S(1)} %whole_weights.1.w.refs_13_), custom_call_target="tpu_custom_call" | custom-call | flops 2147483648 | bytes 9437184 | tf_op jit(solution)/shard_map/slot_gradients/pallas_call | solution.py:197
  101.4 2.9 %collective-permute-done.21.b_ref = bf16[16,192,512]{2,1,0:T(8,128)(2,1)S(1)} collective-permute-done((bf16[16,192,512]{2,1,0:T(8,128)(2,1)S(1)}, bf16[16,192,512]{2,1,0:T(8,128)(2,1)S(1)}, u32[]{:S(2)}, u32[]{:S(2)}) %collective-permute-start.21) | collective-permute-done | bytes 3145760 | tf_op jit(solution)/shard_map/ppermute | solution.py:342
  106.4 1.7 pair_merge.1
  108.2 1.6 copy-done
  109.8 6.0 %all-to-all-start = ((bf16[16,192,512]{2,1,0:T(8,128)(2,1)}), bf16[16,192,512]{2,1,0:T(8,128)(2,1)S(1)}, u32[]{:S(2)}, u32[]{:S(2)}) async-start(bf16[16,192,512]{2,1,0:T(8,128)(2,1)} %copy-done), calls=%async_computation | async-start | bytes 6291456 | tf_op jit(solution)/shard_map/all_to_all | solution.py:491
  115.8 2.1 %collective-permute-start.23 = (bf16[512,512]{1,0:T(8,128)(2,1)}, bf16[512,512]{1,0:T(8,128)(2,1)S(1)}, u32[]{:S(2)}, u32[]{:S(2)}) collective-permute-start(bf16[512,512]{1,0:T(8,128)(2,1)} %copy-done.15), channel_id=1, source_target_pairs={{0,96},{32,0},{64,32},{96,64},{1,97},{33,1},{65,33},{97,65},{2,98}... | collective-permute-start | bytes 1572872 | tf_op jit(solution)/shard_map/ppermute | solution.py:342
  118.6 10.7 %collective-permute-done.23.g1 = bf16[512,512]{1,0:T(8,128)(2,1)S(1)} collective-permute-done((bf16[512,512]{1,0:T(8,128)(2,1)}, bf16[512,512]{1,0:T(8,128)(2,1)S(1)}, u32[]{:S(2)}, u32[]{:S(2)}) %collective-permute-start.23) | collective-permute-done | bytes 524320 | tf_op jit(solution)/shard_map/ppermute | solution.py:342
  129.2 3.0 %collective-permute-done.24.g2 = bf16[512,512]{1,0:T(8,128)(2,1)S(1)} collective-permute-done((bf16[512,512]{1,0:T(8,128)(2,1)}, bf16[512,512]{1,0:T(8,128)(2,1)S(1)}, u32[]{:S(2)}, u32[]{:S(2)}) %collective-permute-start.24) | collective-permute-done | bytes 524320 | tf_op jit(solution)/shard_map/ppermute | solution.py:342
  132.2 11.8 %collective-permute-done.25.g3 = bf16[512,512]{1,0:T(8,128)(2,1)S(1)} collective-permute-done((bf16[512,512]{1,0:T(8,128)(2,1)}, bf16[512,512]{1,0:T(8,128)(2,1)S(1)}, u32[]{:S(2)}, u32[]{:S(2)}) %collective-permute-start.25) | collective-permute-done | bytes 524320 | tf_op jit(solution)/shard_map/ppermute | solution.py:342
  145.1 6.0 %scatter_rows.1 = f32[2048,512]{1,0:T(8,128)} custom-call(s32[1,512]{1,0:T(1,128)S(1)} %copy-done.18, s32[1,512]{1,0:T(1,128)S(1)} %collective-permute-done.refs_0_.i1, s32[1,512]{1,0:T(1,128)S(1)} %collective-permute-done.1.refs_0_.i2, s32[1,512]{1,0:T(1,128)S(1)} %collective-permute-done.2.refs_0_.i3, bf16[512,512]{1,0:T(8,128)(2,1)S(1)} %copy-done.20, ...), custom_call_target="tpu_custom_call" | custom-call | flops 4294967296 | bytes 6291456 | tf_op jit(solution)/shard_map/scatter_rows/pallas_call | solution.py:327
  151.1 5.3 %all-to-all-done.x = bf16[16,192,512]{2,1,0:T(8,128)(2,1)S(1)} async-done(((bf16[16,192,512]{2,1,0:T(8,128)(2,1)}), bf16[16,192,512]{2,1,0:T(8,128)(2,1)S(1)}, u32[]{:S(2)}, u32[]{:S(2)}) %all-to-all-start) | async-done | bytes 3145760 | tf_op jit(solution)/shard_map/all_to_all | solution.py:491
  156.4 2.1 %gram.1 = f32[3,16,128]{2,1,0:T(8,128)S(1)} custom-call(bf16[16,192,512]{2,1,0:T(8,128)(2,1)S(1)} %all-to-all-done.x), custom_call_target="tpu_custom_call" | custom-call | flops 805306368 | bytes 3145728 | tf_op jit(solution)/shard_map/gram/pallas_call | solution.py:268
  158.4 4.7 %collective-permute-start.28 = (f32[3,16,128]{2,1,0:T(8,128)S(1)}, f32[3,16,128]{2,1,0:T(8,128)S(1)}, u32[]{:S(2)}, u32[]{:S(2)}) collective-permute-start(f32[3,16,128]{2,1,0:T(8,128)S(1)} %gram.1), channel_id=1, source_target_pairs={{0,6},{1,7},{2,0},{3,1},{4,2},{5,3},{6,4},{7,5},{8,14},{9,15},{10,... | collective-permute-start | bytes 73736 | tf_op jit(solution)/shard_map/ppermute | solution.py:342
  163.2 1.9 %collective-permute-start.26 = (f32[3,16,128]{2,1,0:T(8,128)S(1)}, f32[3,16,128]{2,1,0:T(8,128)S(1)}, u32[]{:S(2)}, u32[]{:S(2)}) collective-permute-start(f32[3,16,128]{2,1,0:T(8,128)S(1)} %gram.1), channel_id=1, source_target_pairs={{0,4},{1,5},{2,6},{3,7},{4,0},{5,1},{6,2},{7,3},{8,12},{9,13},{10,... | collective-permute-start | bytes 73736 | tf_op jit(solution)/shard_map/ppermute | solution.py:342
  165.1 2.0 %collective-permute-done.27 = f32[3,16,128]{2,1,0:T(8,128)S(1)} collective-permute-done((f32[3,16,128]{2,1,0:T(8,128)S(1)}, f32[3,16,128]{2,1,0:T(8,128)S(1)}, u32[]{:S(2)}, u32[]{:S(2)}) %collective-permute-start.27) | collective-permute-done | bytes 24608 | tf_op jit(solution)/shard_map/ppermute | solution.py:342
  167.4 2.8 %collective-permute-start.31 = (f32[3,16,128]{2,1,0:T(8,128)S(1)}, f32[3,16,128]{2,1,0:T(8,128)S(1)}, u32[]{:S(2)}, u32[]{:S(2)}) collective-permute-start(f32[3,16,128]{2,1,0:T(8,128)S(1)} %add_add_fusion.1), channel_id=1, source_target_pairs={{0,24},{1,25},{2,26},{3,27},{4,28},{5,29},{6,30},{7,31},{8,0},{9,1... | collective-permute-start | bytes 73736 | tf_op jit(solution)/shard_map/ppermute | solution.py:342
  170.2 4.2 %collective-permute-start.29 = (f32[3,16,128]{2,1,0:T(8,128)S(1)}, f32[3,16,128]{2,1,0:T(8,128)S(1)}, u32[]{:S(2)}, u32[]{:S(2)}) collective-permute-start(f32[3,16,128]{2,1,0:T(8,128)S(1)} %add_add_fusion.1), channel_id=1, source_target_pairs={{0,16},{1,17},{2,18},{3,19},{4,20},{5,21},{6,22},{7,23},{8,24},{9,... | collective-permute-start | bytes 73736 | tf_op jit(solution)/shard_map/ppermute | solution.py:342
  174.5 1.4 collective-permute-done.29
  175.9 4.4 %collective-permute-start.32 = (f32[3,16,128]{2,1,0:T(8,128)S(1)}, f32[3,16,128]{2,1,0:T(8,128)S(1)}, u32[]{:S(2)}, u32[]{:S(2)}) collective-permute-start(f32[3,16,128]{2,1,0:T(8,128)S(1)} %add_add_fusion), channel_id=1, source_target_pairs={{0,1},{1,0},{2,3},{3,2},{4,5},{5,4},{6,7},{7,6},{8,9},{9,8},{10,11... | collective-permute-start | bytes 73736 | tf_op jit(solution)/shard_map/ppermute | solution.py:342
  181.3 1.8 finish.1
  (96 shorter events, 14.7 us)
Async XLA Ops:
  0.6 17.6 %collective-permute-start.2 = (s32[1,512]{1,0:T(1,128)}, s32[1,512]{1,0:T(1,128)S(1)}, u32[]{:S(2)}, u32[]{:S(2)}) collective-permute-start(s32[1,512]{1,0:T(1,128)} %i0), channel_id=1, source_target_pairs={{0,32},{32,64},{64,96},{96,0},{1,33},{33,65},{65,97},{97,1},{2,34}... | collective-permute-start | bytes 6152 | tf_op jit(solution)/shard_map/ppermute | solution.py:342
  2.8 15.4 %collective-permute-start.1 = (s32[1,512]{1,0:T(1,128)}, s32[1,512]{1,0:T(1,128)S(1)}, u32[]{:S(2)}, u32[]{:S(2)}) collective-permute-start(s32[1,512]{1,0:T(1,128)} %i0), channel_id=1, source_target_pairs={{0,64},{32,96},{64,0},{96,32},{1,65},{33,97},{65,1},{97,33},{2,66}... | collective-permute-start | bytes 6152 | tf_op jit(solution)/shard_map/ppermute | solution.py:342
  5.4 12.8 %collective-permute-start = (s32[1,512]{1,0:T(1,128)}, s32[1,512]{1,0:T(1,128)S(1)}, u32[]{:S(2)}, u32[]{:S(2)}) collective-permute-start(s32[1,512]{1,0:T(1,128)} %i0), channel_id=1, source_target_pairs={{0,96},{32,0},{64,32},{96,64},{1,97},{33,1},{65,33},{97,65},{2,98}... | collective-permute-start | bytes 6152 | tf_op jit(solution)/shard_map/ppermute | solution.py:342
  9.3 9.0 %collective-permute-start.4 = (bf16[96,1024]{1,0:T(8,128)(2,1)S(1)}, bf16[96,1024]{1,0:T(8,128)(2,1)S(1)}, u32[]{:S(2)}, u32[]{:S(2)}) collective-permute-start(bf16[96,1024]{1,0:T(8,128)(2,1)S(1)} %pack.1.own), channel_id=1, source_target_pairs={{0,6},{1,25},{2,0},{3,27},{4,2},{5,29},{6,4},{7,31},{8,14},{9,1},{... | collective-permute-start | bytes 589832 | tf_op jit(solution)/shard_map/ppermute | solution.py:342
  11.8 6.4 %collective-permute-start.3 = (bf16[96,1024]{1,0:T(8,128)(2,1)S(1)}, bf16[96,1024]{1,0:T(8,128)(2,1)S(1)}, u32[]{:S(2)}, u32[]{:S(2)}) collective-permute-start(bf16[96,1024]{1,0:T(8,128)(2,1)S(1)} %pack.1.own), channel_id=1, source_target_pairs={{0,2},{1,9},{2,4},{3,11},{4,6},{5,13},{6,0},{7,15},{8,10},{9,17},{... | collective-permute-start | bytes 589832 | tf_op jit(solution)/shard_map/ppermute | solution.py:342
  18.3 7.0 %collective-permute-start.6 = (bf16[48,1024]{1,0:T(8,128)(2,1)S(1)}, bf16[48,1024]{1,0:T(8,128)(2,1)S(1)}, u32[]{:S(2)}, u32[]{:S(2)}) collective-permute-start(bf16[48,1024]{1,0:T(8,128)(2,1)S(1)} %slice.38), channel_id=1, source_target_pairs={{0,6},{1,25},{2,0},{3,27},{4,2},{5,29},{6,4},{7,31},{8,14},{9,1},{... | collective-permute-start | bytes 294920 | tf_op jit(solution)/shard_map/ppermute | solution.py:342
  21.0 4.7 %collective-permute-start.5 = (bf16[48,1024]{1,0:T(8,128)(2,1)S(1)}, bf16[48,1024]{1,0:T(8,128)(2,1)S(1)}, u32[]{:S(2)}, u32[]{:S(2)}) collective-permute-start(bf16[48,1024]{1,0:T(8,128)(2,1)S(1)} %slice.37), channel_id=1, source_target_pairs={{0,2},{1,9},{2,4},{3,11},{4,6},{5,13},{6,0},{7,15},{8,10},{9,17},{... | collective-permute-start | bytes 294920 | tf_op jit(solution)/shard_map/ppermute | solution.py:342
  23.8 8.8 %copy-start.12 = (bf16[2048,512]{1,0:T(8,128)(2,1)S(1)}, bf16[2048,512]{1,0:T(8,128)(2,1)}, u32[]{:S(2)}) copy-start(bf16[2048,512]{1,0:T(8,128)(2,1)} %refs_1_.13) | copy-start | bytes 6291460
  25.8 29.6 %collective-permute-start.8 = (bf16[4,96,1024]{2,1,0:T(8,128)(2,1)S(1)}, bf16[4,96,1024]{2,1,0:T(8,128)(2,1)S(1)}, u32[]{:S(2)}, u32[]{:S(2)}) collective-permute-start(bf16[4,96,1024]{2,1,0:T(8,128)(2,1)S(1)} %bundle.1.own), channel_id=1, source_target_pairs={{0,24},{1,7},{2,26},{3,1},{4,28},{5,3},{6,30},{7,5},{8,0},{9,15},{... | collective-permute-start | bytes 2359304 | tf_op jit(solution)/shard_map/ppermute | solution.py:342
  29.9 25.5 %collective-permute-start.7 = (bf16[4,96,1024]{2,1,0:T(8,128)(2,1)S(1)}, bf16[4,96,1024]{2,1,0:T(8,128)(2,1)S(1)}, u32[]{:S(2)}, u32[]{:S(2)}) collective-permute-start(bf16[4,96,1024]{2,1,0:T(8,128)(2,1)S(1)} %bundle.1.own), channel_id=1, source_target_pairs={{0,8},{1,3},{2,10},{3,5},{4,12},{5,7},{6,14},{7,1},{8,16},{9,11},{... | collective-permute-start | bytes 2359304 | tf_op jit(solution)/shard_map/ppermute | solution.py:342
  29.9 12.9 %collective-permute-start.9 = (bf16[512,512]{1,0:T(8,128)(2,1)S(1)}, bf16[512,512]{1,0:T(8,128)(2,1)S(1)}, u32[]{:S(2)}, u32[]{:S(2)}) collective-permute-start(bf16[512,512]{1,0:T(8,128)(2,1)S(1)} %pick_rows.8), channel_id=1, source_target_pairs={{0,32},{32,64},{64,96},{96,0},{1,33},{33,65},{65,97},{97,1},{2,34}... | collective-permute-start | bytes 1572872 | tf_op jit(solution)/shard_map/ppermute | solution.py:342
  30.3 20.4 %collective-permute-start.10 = (bf16[512,512]{1,0:T(8,128)(2,1)S(1)}, bf16[512,512]{1,0:T(8,128)(2,1)S(1)}, u32[]{:S(2)}, u32[]{:S(2)}) collective-permute-start(bf16[512,512]{1,0:T(8,128)(2,1)S(1)} %pick_rows.9), channel_id=1, source_target_pairs={{0,64},{32,96},{64,0},{96,32},{1,65},{33,97},{65,1},{97,33},{2,66}... | collective-permute-start | bytes 1572872 | tf_op jit(solution)/shard_map/ppermute | solution.py:342
  30.8 24.5 %collective-permute-start.11 = (bf16[512,512]{1,0:T(8,128)(2,1)S(1)}, bf16[512,512]{1,0:T(8,128)(2,1)S(1)}, u32[]{:S(2)}, u32[]{:S(2)}) collective-permute-start(bf16[512,512]{1,0:T(8,128)(2,1)S(1)} %pick_rows.10), channel_id=1, source_target_pairs={{0,96},{32,0},{64,32},{96,64},{1,97},{33,1},{65,33},{97,65},{2,98}... | collective-permute-start | bytes 1572872 | tf_op jit(solution)/shard_map/ppermute | solution.py:342
  55.4 16.8 %collective-permute-start.13 = (bf16[2,96,1024]{2,1,0:T(8,128)(2,1)S(1)}, bf16[2,96,1024]{2,1,0:T(8,128)(2,1)S(1)}, u32[]{:S(2)}, u32[]{:S(2)}) collective-permute-start(bf16[2,96,1024]{2,1,0:T(8,128)(2,1)S(1)} %slice.40), channel_id=1, source_target_pairs={{0,24},{1,7},{2,26},{3,1},{4,28},{5,3},{6,30},{7,5},{8,0},{9,15},{... | collective-permute-start | bytes 1179656 | tf_op jit(solution)/shard_map/ppermute | solution.py:342
  58.2 14.1 %collective-permute-start.12 = (bf16[2,96,1024]{2,1,0:T(8,128)(2,1)S(1)}, bf16[2,96,1024]{2,1,0:T(8,128)(2,1)S(1)}, u32[]{:S(2)}, u32[]{:S(2)}) collective-permute-start(bf16[2,96,1024]{2,1,0:T(8,128)(2,1)S(1)} %slice.39), channel_id=1, source_target_pairs={{0,8},{1,3},{2,10},{3,5},{4,12},{5,7},{6,14},{7,1},{8,16},{9,11},{... | collective-permute-start | bytes 1179656 | tf_op jit(solution)/shard_map/ppermute | solution.py:342
  58.2 10.5 %collective-permute-start.16 = (bf16[160,512]{1,0:T(8,128)(2,1)S(1)}, bf16[160,512]{1,0:T(8,128)(2,1)S(1)}, u32[]{:S(2)}, u32[]{:S(2)}) collective-permute-start(bf16[160,512]{1,0:T(8,128)(2,1)S(1)} %slice.43), channel_id=1, source_target_pairs={{0,96},{32,0},{64,32},{96,64},{1,97},{33,1},{65,33},{97,65},{2,98}... | collective-permute-start | bytes 491528 | tf_op jit(solution)/shard_map/ppermute | solution.py:342
  61.7 7.0 %collective-permute-start.15 = (bf16[160,512]{1,0:T(8,128)(2,1)S(1)}, bf16[160,512]{1,0:T(8,128)(2,1)S(1)}, u32[]{:S(2)}, u32[]{:S(2)}) collective-permute-start(bf16[160,512]{1,0:T(8,128)(2,1)S(1)} %slice.42), channel_id=1, source_target_pairs={{0,64},{32,96},{64,0},{96,32},{1,65},{33,97},{65,1},{97,33},{2,66}... | collective-permute-start | bytes 491528 | tf_op jit(solution)/shard_map/ppermute | solution.py:342
  61.7 10.5 %collective-permute-start.14 = (bf16[160,512]{1,0:T(8,128)(2,1)S(1)}, bf16[160,512]{1,0:T(8,128)(2,1)S(1)}, u32[]{:S(2)}, u32[]{:S(2)}) collective-permute-start(bf16[160,512]{1,0:T(8,128)(2,1)S(1)} %slice.41), channel_id=1, source_target_pairs={{0,32},{32,64},{64,96},{96,0},{1,33},{33,65},{65,97},{97,1},{2,34}... | collective-permute-start | bytes 491528 | tf_op jit(solution)/shard_map/ppermute | solution.py:342
  72.5 6.2 %collective-permute-start.20 = (bf16[16,96,1024]{2,1,0:T(8,128)(2,1)S(1)}, bf16[16,96,1024]{2,1,0:T(8,128)(2,1)S(1)}, u32[]{:S(2)}, u32[]{:S(2)}) collective-permute-start(bf16[16,96,1024]{2,1,0:T(8,128)(2,1)S(1)} %half_of_weights.1.a), channel_id=1, source_target_pairs={{0,1},{1,0},{2,3},{3,2},{4,5},{5,4},{6,7},{7,6},{8,9},{9,8},{10,11... | collective-permute-start | bytes 9437192 | tf_op jit(solution)/shard_map/ppermute | solution.py:342
  73.4 18.9 %collective-permute-start.17 = (bf16[352,512]{1,0:T(8,128)(2,1)S(1)}, bf16[352,512]{1,0:T(8,128)(2,1)S(1)}, u32[]{:S(2)}, u32[]{:S(2)}) collective-permute-start(bf16[352,512]{1,0:T(8,128)(2,1)S(1)} %slice.44), channel_id=1, source_target_pairs={{0,32},{32,64},{64,96},{96,0},{1,33},{33,65},{65,97},{97,1},{2,34}... | collective-permute-start | bytes 1081352 | tf_op jit(solution)/shard_map/ppermute | solution.py:342
  73.4 18.9 %collective-permute-start.18 = (bf16[352,512]{1,0:T(8,128)(2,1)S(1)}, bf16[352,512]{1,0:T(8,128)(2,1)S(1)}, u32[]{:S(2)}, u32[]{:S(2)}) collective-permute-start(bf16[352,512]{1,0:T(8,128)(2,1)S(1)} %slice.45), channel_id=1, source_target_pairs={{0,64},{32,96},{64,0},{96,32},{1,65},{33,97},{65,1},{97,33},{2,66}... | collective-permute-start | bytes 1081352 | tf_op jit(solution)/shard_map/ppermute | solution.py:342
  75.2 17.4 %collective-permute-start.19 = (bf16[352,512]{1,0:T(8,128)(2,1)S(1)}, bf16[352,512]{1,0:T(8,128)(2,1)S(1)}, u32[]{:S(2)}, u32[]{:S(2)}) collective-permute-start(bf16[352,512]{1,0:T(8,128)(2,1)S(1)} %slice.46), channel_id=1, source_target_pairs={{0,96},{32,0},{64,32},{96,64},{1,97},{33,1},{65,33},{97,65},{2,98}... | collective-permute-start | bytes 1081352 | tf_op jit(solution)/shard_map/ppermute | solution.py:342
  79.1 13.5 %copy-start.16 = (f32[1,512]{1,0:T(1,128)S(1)}, f32[1,512]{1,0:T(1,128)}, u32[]{:S(2)}) copy-start(f32[1,512]{1,0:T(1,128)} %refs_8_.1) | copy-start | bytes 6148
  97.8 6.5 %collective-permute-start.21 = (bf16[16,192,512]{2,1,0:T(8,128)(2,1)S(1)}, bf16[16,192,512]{2,1,0:T(8,128)(2,1)S(1)}, u32[]{:S(2)}, u32[]{:S(2)}) collective-permute-start(bf16[16,192,512]{2,1,0:T(8,128)(2,1)S(1)} %get-tuple-element.93), channel_id=1, source_target_pairs={{0,1},{1,0},{2,3},{3,2},{4,5},{5,4},{6,7},{7,6},{8,9},{9,8},{10,11... | collective-permute-start | bytes 9437192 | tf_op jit(solution)/shard_map/ppermute | solution.py:342
  101.4 3.7 %copy-start.13 = (bf16[512,512]{1,0:T(8,128)(2,1)}, bf16[512,512]{1,0:T(8,128)(2,1)S(1)}, u32[]{:S(2)}) copy-start(bf16[512,512]{1,0:T(8,128)(2,1)S(1)} %get-tuple-element.98) | copy-start | bytes 1572868
  101.4 3.7 %copy-start.14 = (bf16[512,512]{1,0:T(8,128)(2,1)}, bf16[512,512]{1,0:T(8,128)(2,1)S(1)}, u32[]{:S(2)}) copy-start(bf16[512,512]{1,0:T(8,128)(2,1)S(1)} %get-tuple-element.97) | copy-start | bytes 1572868
  101.4 3.7 %copy-start.15 = (bf16[512,512]{1,0:T(8,128)(2,1)}, bf16[512,512]{1,0:T(8,128)(2,1)S(1)}, u32[]{:S(2)}) copy-start(bf16[512,512]{1,0:T(8,128)(2,1)S(1)} %get-tuple-element.96) | copy-start | bytes 1572868
  101.4 3.7 %copy-start.19 = (bf16[512,512]{1,0:T(8,128)(2,1)}, bf16[512,512]{1,0:T(8,128)(2,1)S(1)}, u32[]{:S(2)}) copy-start(bf16[512,512]{1,0:T(8,128)(2,1)S(1)} %get-tuple-element.95.g0) | copy-start | bytes 1572868
  105.1 1.3 collective-permute-start.22
  108.2 1.6 copy-start
  109.8 34.3 %copy-start.18 = (s32[1,512]{1,0:T(1,128)S(1)}, s32[1,512]{1,0:T(1,128)}, u32[]{:S(2)}) copy-start(s32[1,512]{1,0:T(1,128)} %i0) | copy-start | bytes 6148
  109.8 46.6 %all-to-all-start = ((bf16[16,192,512]{2,1,0:T(8,128)(2,1)}), bf16[16,192,512]{2,1,0:T(8,128)(2,1)S(1)}, u32[]{:S(2)}, u32[]{:S(2)}) async-start(bf16[16,192,512]{2,1,0:T(8,128)(2,1)} %copy-done), calls=%async_computation | async-start | bytes 6291456 | tf_op jit(solution)/shard_map/all_to_all | solution.py:491
  115.8 13.5 %collective-permute-start.23 = (bf16[512,512]{1,0:T(8,128)(2,1)}, bf16[512,512]{1,0:T(8,128)(2,1)S(1)}, u32[]{:S(2)}, u32[]{:S(2)}) collective-permute-start(bf16[512,512]{1,0:T(8,128)(2,1)} %copy-done.15), channel_id=1, source_target_pairs={{0,96},{32,0},{64,32},{96,64},{1,97},{33,1},{65,33},{97,65},{2,98}... | collective-permute-start | bytes 1572872 | tf_op jit(solution)/shard_map/ppermute | solution.py:342
  117.9 14.3 %collective-permute-start.24 = (bf16[512,512]{1,0:T(8,128)(2,1)}, bf16[512,512]{1,0:T(8,128)(2,1)S(1)}, u32[]{:S(2)}, u32[]{:S(2)}) collective-permute-start(bf16[512,512]{1,0:T(8,128)(2,1)} %copy-done.14), channel_id=1, source_target_pairs={{0,64},{32,96},{64,0},{96,32},{1,65},{33,97},{65,1},{97,33},{2,66}... | collective-permute-start | bytes 1572872 | tf_op jit(solution)/shard_map/ppermute | solution.py:342
  117.9 26.2 %collective-permute-start.25 = (bf16[512,512]{1,0:T(8,128)(2,1)}, bf16[512,512]{1,0:T(8,128)(2,1)S(1)}, u32[]{:S(2)}, u32[]{:S(2)}) collective-permute-start(bf16[512,512]{1,0:T(8,128)(2,1)} %copy-done.13), channel_id=1, source_target_pairs={{0,32},{32,64},{64,96},{96,0},{1,33},{33,65},{65,97},{97,1},{2,34}... | collective-permute-start | bytes 1572872 | tf_op jit(solution)/shard_map/ppermute | solution.py:342
  151.1 30.1 %copy-start.2 = (f32[1,64,512]{2,1,0:T(8,128)S(1)}, f32[1,64,512]{2,1,0:T(8,128)}, u32[]{:S(2)}) copy-start(f32[1,64,512]{2,1,0:T(8,128)} %param.14) | copy-start | bytes 393220
  151.1 30.1 %copy-start.4 = (f32[1,64,512]{2,1,0:T(8,128)S(1)}, f32[1,64,512]{2,1,0:T(8,128)}, u32[]{:S(2)}) copy-start(f32[1,64,512]{2,1,0:T(8,128)} %param.15) | copy-start | bytes 393220
  151.1 30.2 %copy-start.6 = (f32[1,16,2048]{2,1,0:T(8,128)S(1)}, f32[1,16,2048]{2,1,0:T(8,128)}, u32[]{:S(2)}) copy-start(f32[1,16,2048]{2,1,0:T(8,128)} %param.16) | copy-start | bytes 393220
  156.4 24.9 %copy-start.7 = (f32[1,64,512]{2,1,0:T(8,128)S(1)}, f32[1,64,512]{2,1,0:T(8,128)}, u32[]{:S(2)}) copy-start(f32[1,64,512]{2,1,0:T(8,128)} %param.17) | copy-start | bytes 393220
  156.4 24.9 %copy-start.8 = (f32[1,64,512]{2,1,0:T(8,128)S(1)}, f32[1,64,512]{2,1,0:T(8,128)}, u32[]{:S(2)}) copy-start(f32[1,64,512]{2,1,0:T(8,128)} %param.18) | copy-start | bytes 393220
  156.4 24.9 %copy-start.9 = (f32[1,16,2048]{2,1,0:T(8,128)S(1)}, f32[1,16,2048]{2,1,0:T(8,128)}, u32[]{:S(2)}) copy-start(f32[1,16,2048]{2,1,0:T(8,128)} %param.19) | copy-start | bytes 393220
  158.4 6.6 %collective-permute-start.28 = (f32[3,16,128]{2,1,0:T(8,128)S(1)}, f32[3,16,128]{2,1,0:T(8,128)S(1)}, u32[]{:S(2)}, u32[]{:S(2)}) collective-permute-start(f32[3,16,128]{2,1,0:T(8,128)S(1)} %gram.1), channel_id=1, source_target_pairs={{0,6},{1,7},{2,0},{3,1},{4,2},{5,3},{6,4},{7,5},{8,14},{9,15},{10,... | collective-permute-start | bytes 73736 | tf_op jit(solution)/shard_map/ppermute | solution.py:342
  163.2 3.9 %collective-permute-start.27 = (f32[3,16,128]{2,1,0:T(8,128)S(1)}, f32[3,16,128]{2,1,0:T(8,128)S(1)}, u32[]{:S(2)}, u32[]{:S(2)}) collective-permute-start(f32[3,16,128]{2,1,0:T(8,128)S(1)} %gram.1), channel_id=1, source_target_pairs={{0,2},{1,3},{2,4},{3,5},{4,6},{5,7},{6,0},{7,1},{8,10},{9,11},{10,... | collective-permute-start | bytes 73736 | tf_op jit(solution)/shard_map/ppermute | solution.py:342
  163.2 4.2 %collective-permute-start.26 = (f32[3,16,128]{2,1,0:T(8,128)S(1)}, f32[3,16,128]{2,1,0:T(8,128)S(1)}, u32[]{:S(2)}, u32[]{:S(2)}) collective-permute-start(f32[3,16,128]{2,1,0:T(8,128)S(1)} %gram.1), channel_id=1, source_target_pairs={{0,4},{1,5},{2,6},{3,7},{4,0},{5,1},{6,2},{7,3},{8,12},{9,13},{10,... | collective-permute-start | bytes 73736 | tf_op jit(solution)/shard_map/ppermute | solution.py:342
  167.4 7.0 %collective-permute-start.31 = (f32[3,16,128]{2,1,0:T(8,128)S(1)}, f32[3,16,128]{2,1,0:T(8,128)S(1)}, u32[]{:S(2)}, u32[]{:S(2)}) collective-permute-start(f32[3,16,128]{2,1,0:T(8,128)S(1)} %add_add_fusion.1), channel_id=1, source_target_pairs={{0,24},{1,25},{2,26},{3,27},{4,28},{5,29},{6,30},{7,31},{8,0},{9,1... | collective-permute-start | bytes 73736 | tf_op jit(solution)/shard_map/ppermute | solution.py:342
  170.2 4.2 %collective-permute-start.30 = (f32[3,16,128]{2,1,0:T(8,128)S(1)}, f32[3,16,128]{2,1,0:T(8,128)S(1)}, u32[]{:S(2)}, u32[]{:S(2)}) collective-permute-start(f32[3,16,128]{2,1,0:T(8,128)S(1)} %add_add_fusion.1), channel_id=1, source_target_pairs={{0,8},{1,9},{2,10},{3,11},{4,12},{5,13},{6,14},{7,15},{8,16},{9,17... | collective-permute-start | bytes 73736 | tf_op jit(solution)/shard_map/ppermute | solution.py:342
  170.2 5.7 %collective-permute-start.29 = (f32[3,16,128]{2,1,0:T(8,128)S(1)}, f32[3,16,128]{2,1,0:T(8,128)S(1)}, u32[]{:S(2)}, u32[]{:S(2)}) collective-permute-start(f32[3,16,128]{2,1,0:T(8,128)S(1)} %add_add_fusion.1), channel_id=1, source_target_pairs={{0,16},{1,17},{2,18},{3,19},{4,20},{5,21},{6,22},{7,23},{8,24},{9,... | collective-permute-start | bytes 73736 | tf_op jit(solution)/shard_map/ppermute | solution.py:342
  175.9 5.3 %collective-permute-start.32 = (f32[3,16,128]{2,1,0:T(8,128)S(1)}, f32[3,16,128]{2,1,0:T(8,128)S(1)}, u32[]{:S(2)}, u32[]{:S(2)}) collective-permute-start(f32[3,16,128]{2,1,0:T(8,128)S(1)} %add_add_fusion), channel_id=1, source_target_pairs={{0,1},{1,0},{2,3},{3,2},{4,5},{5,4},{6,7},{7,6},{8,9},{9,8},{10,11... | collective-permute-start | bytes 73736 | tf_op jit(solution)/shard_map/ppermute | solution.py:342
  (7 other events, 7.6 us)

commit v4 on v2

--- a/solution.py
+++ b/solution.py
@@ -360,6 +360,88 @@
     return value + other_core(value)
 
 
+def pack(gate, up, down, pool):
+    def body(gate_hbm, up_hbm, down_hbm, pool_ref, out, g, u, d, sems):
+        copies = [
+            pltpu.make_async_copy(src, dst, sems.at[j])
+            for j, (src, dst) in enumerate(((gate_hbm, g), (up_hbm, u), (down_hbm, d)))
+        ]
+        for copy in copies:
+            copy.start()
+        for copy in copies:
+            copy.wait()
+        out[0:64, 0:H] = g[...].astype(BF16)
+        out[0:64, H:] = u[...].astype(BF16)
+        out[64:80, :] = d[:, : D // 2].astype(BF16)
+        out[80:96, :] = d[:, D // 2 :].astype(BF16)
+
+    return pl.pallas_call(
+        body,
+        name="pack",
+        out_shape=struct((96, 1024), BF16),
+        in_specs=[pl.BlockSpec(memory_space=pltpu.HBM)] * 3 + [vmem()],
+        out_specs=vmem(),
+        scratch_shapes=[
+            pltpu.VMEM((64, H), F32),
+            pltpu.VMEM((64, H), F32),
+            pltpu.VMEM((16, D), F32),
+            pltpu.SemaphoreType.DMA((3,)),
+        ],
+        compiler_params=pltpu.CompilerParams(vmem_limit_bytes=8 * MIB),
+        cost_estimate=pl.CostEstimate(flops=2**17, bytes_accessed=MIB, transcendentals=0),
+    )(gate, up, down, pool)
+
+
+def along(turn, step):
+    def to(i):
+        x, z, c = i // 8, i // 2 % 4, i % 2
+        return x * 8 + (z + step) % 4 * 2 + c if c == turn else (x + step) % 4 * 8 + z * 2 + c
+
+    return to
+
+
+def spread(block, turn):
+    return [shift(block, "dp", along(turn, k)) for k in (1, 2, 3)]
+
+
+def place(turn):
+    at = lax.axis_index("dp")
+    x, z, c = at // 8, lax.rem(at // 2, 4), lax.rem(at, 2)
+    return c, jnp.where(c == turn, z, x)
+
+
+def bundle(blocks):
+    def body(*refs):
+        _, at = place(0)
+        for k in range(4):
+            refs[4][lax.rem(at + 4 - k, 4)] = refs[k][...]
+
+    return call(body, "bundle", 4, struct((4, 96, 1024), BF16), 2**10, 2 * MIB)(*blocks)
+
+
+def half_of_weights(bundles):
+    def body(*refs):
+        c, at = place(1)
+        for k in range(4):
+            other = lax.rem(at + 4 - k, 4)
+            for j in range(4):
+                refs[4][jnp.where(c == 0, other * 4 + j, j * 4 + other)] = refs[k][j]
+
+    return call(body, "half_of_weights", 4, struct((N_CHIP, 96, 1024), BF16), 2**10, 6 * MIB)(*bundles)
+
+
+def whole_weights(own, other):
+    def body(a, b, out):
+        c = lax.rem(lax.axis_index("dp"), 2)
+
+        @pl.loop(0, N_CHIP)
+        def _(q):
+            out[2 * q + c] = a[q]
+            out[2 * q + 1 - c] = b[q]
+
+    return call(body, "whole_weights", 2, struct((2 * N_CHIP, 96, 1024), BF16), 2**10, 12 * MIB)(own, other)
+
+
 def local(
     pool_tokens,
     pool_cotangent,
@@ -372,26 +454,33 @@
     momentum_up,
     momentum_down,
 ):
-    down_halves = down_weight[0].astype(BF16)
-    shard = jnp.concatenate(
-        [
-            jnp.concatenate([gate_weight[0].astype(BF16), up_weight[0].astype(BF16)], axis=1),
-            down_halves[:, : D // 2],
-            down_halves[:, D // 2 :],
-        ],
-        axis=0,
-    )
-    weights = lax.all_gather(shard, "dp", axis=0, tiled=False)
+    tie = lax.optimization_barrier
+
+    def picked(k, pool):
+        return pick_rows(ids[k : k + 1], [pool])[0]
 
     ids = [token_ids] + [around_y(token_ids, N_EXPERT - k) for k in (1, 2, 3)]
-    own_x, own_c = pick_rows(ids[:1], [pool_tokens, pool_cotangent])
-    ids, own_x, own_c = lax.optimization_barrier((ids, own_x, own_c))
-    sent_x, sent_c = [None] * 3, [None] * 3
-    for sent, pool in ((sent_x, pool_tokens), (sent_c, pool_cotangent)):
-        for k in (2, 1, 3):
-            (sent[k - 1],) = pick_rows(ids[k : k + 1], [pool])
-    tokens = [own_x] + [around_y(sent_x[k - 1], k) for k in (1, 2, 3)]
-    cots = [own_c] + [around_y(sent_c[k - 1], k) for k in (1, 2, 3)]
+    packed = pack(gate_weight[0], up_weight[0], down_weight[0], pool_tokens)
+    x, c = [None] * 4, [None] * 4
+    x[1], x[3] = picked(1, pool_tokens), picked(3, pool_tokens)
+    packed, x[1], x[3] = tie((packed, x[1], x[3]))
+
+    x[1], x[3] = around_y(x[1], 1), around_y(x[3], 3)
+    blocks = spread(packed, 0)
+    x[2], c[2] = picked(2, pool_tokens), picked(2, pool_cotangent)
+    x[0], c[0] = pick_rows(ids[:1], [pool_tokens, pool_cotangent])
+    blocks, x, c[2], c[0] = tie((blocks, x, c[2], c[0]))
+
+    x[2], c[2] = around_y(x[2], 2), around_y(c[2], 2)
+    block = bundle((packed, *blocks))
+    blocks = spread(block, 1)
+    c[1], c[3] = picked(1, pool_cotangent), picked(3, pool_cotangent)
+    blocks, x, c = tie((blocks, x, c))
+
+    c[1], c[3] = around_y(c[1], 1), around_y(c[3], 3)
+    mine = half_of_weights((block, *blocks))
+    weights = whole_weights(mine, other_core(mine))
+    tokens, cots = x, c
 
     hidden_t, gate_factor, act, xt = forward(tokens, weights)
     keep, send, both = backward(cots, route_weights, hidden_t, gate_factor, act, xt, weights)

time: 174 us -> 170 us (0.977)
  starting transfers between devices: 41.7 us -> 55.2 us
  between operations: 14.3 us -> 0.98 us
  other arithmetic: 2.64 us -> 0.02 us
  Pallas kernels: 37.3 us -> 35.1 us
    ppermute x21 -> x28, starting transfers between devices: 34 us -> 50.3 us  [shift(): lax.ppermute(block, axis, [(i, to(i)) for i in range(lax.axis_size(axis))])]
    ppermute x21 -> x28, waiting for transfers between devices: 52.3 us -> 65.2 us  [shift(): lax.ppermute(block, axis, [(i, to(i)) for i in range(lax.axis_size(axis))])]
    all_gather x1 -> x0, waiting for transfers between devices: 9.4 us -> none  [local(): weights = lax.all_gather(shard, 'dp', axis=0, tiled=False)]
    all_to_all x1, starting transfers between devices: 7.71 us -> 4.93 us  [local(): lax.all_to_all(merged, 'dp', 0, 0, tiled=True, axis_index_groups=groups)]
    pallas_call x7, Pallas kernels: 13.5 us -> 11 us  [pick_rows(): call(body, 'pick_rows', n_ids + n_pool, shapes, 2 * TOK_DEV * POOL * SLIC...]
    convert_element_type x2 -> x0, other arithmetic: 1.9 us -> none  [the longest x1 0.99 us: local(): up_weight[0].astype(BF16)]
    all_to_all x1, waiting for transfers between devices: 6.37 us -> 4.47 us  [local(): lax.all_to_all(merged, 'dp', 0, 0, tiled=True, axis_index_groups=groups)]
  transfers between devices with their start and end apart: 23 -> 29, of which waited for: 13 -> 16; matrix products, arithmetic and copies ran while one was open for 0% -> 0% of each run, Pallas kernels for 14% -> 13%
where the time goes in v4:
time: 170 us
  waiting for transfers between devices  69.6 us (41%)
  starting transfers between devices  55.2 us (32%)
  Pallas kernels  35.1 us (21%)
  local copies, waits for them, and re-layouts  8.62 us (5%)
    ppermute x28, waiting for transfers between devices, shift(): lax.ppermute(block, axis, [(i, to(i)) for i in range(lax.axis_size(axis))])  65.2 us
    ppermute x28, starting transfers between devices, shift(): lax.ppermute(block, axis, [(i, to(i)) for i in range(lax.axis_size(axis))])  50.3 us
    pallas_call x7, Pallas kernels, pick_rows(): call(body, 'pick_rows', n_ids + n_pool, shapes, 2 * TOK_DEV * POOL * SLIC...  11 us
    unnamed x42, local copies, waits for them, and re-layouts  8.62 us
    pallas_call x1, Pallas kernels, scatter_rows(): pl.pallas_call(body, name='scatter_rows', grid=(POOL // block,), out_shap...  5.97 us
    pallas_call x1, Pallas kernels, backward(): call(body, 'backward', 10, shapes, 8 * TOK_DEV * D * H, 20 * MIB, [pltpu....  5.23 us
    all_to_all x1, starting transfers between devices, local(): lax.all_to_all(merged, 'dp', 0, 0, tiled=True, axis_index_groups=groups)  4.93 us
    all_to_all x1, waiting for transfers between devices, local(): lax.all_to_all(merged, 'dp', 0, 0, tiled=True, axis_index_groups=groups)  4.47 us
  transfers between devices with their start and end apart: 29, of which 16 were waited for; matrix products, arithmetic and copies ran while one was open for 0% of the time, Pallas kernels for 13%

profile of v4, /device:TPU:1, one launch (start us, length us, event | category | flops | bytes accessed | tf_op | source)
XLA Modules:
  0.0 169.6 jit_solution(18120074322079936228)
XLA Ops:
  0.6 3.6 %collective-permute-start = (s32[1,512]{1,0:T(1,128)}, s32[1,512]{1,0:T(1,128)S(1)}, u32[]{:S(2)}, u32[]{:S(2)}) collective-permute-start(s32[1,512]{1,0:T(1,128)} %i0.1), channel_id=1, source_target_pairs={{0,96},{32,0},{64,32},{96,64},{1,97},{33,1},{65,33},{97,65},{2,98}... | collective-permute-start | bytes 6152 | tf_op jit(solution)/shard_map/ppermute | solution.py:338
  4.3 1.6 copy-done.1
  9.1 1.6 copy-done.2
  10.7 1.4 pick_rows.7
  12.2 1.4 pick_rows.8
  13.7 2.7 %collective-permute-start.7 = (bf16[512,512]{1,0:T(8,128)(2,1)S(1)}, bf16[512,512]{1,0:T(8,128)(2,1)S(1)}, u32[]{:S(2)}, u32[]{:S(2)}) collective-permute-start(bf16[512,512]{1,0:T(8,128)(2,1)S(1)} %pick_rows.8), channel_id=1, source_target_pairs={{0,96},{32,0},{64,32},{96,64},{1,97},{33,1},{65,33},{97,65},{2,98}... | collective-permute-start | bytes 1572872 | tf_op jit(solution)/shard_map/ppermute | solution.py:338
  16.4 1.1 collective-permute-start.6
  17.5 2.5 %pick_rows.9 = (bf16[512,512]{1,0:T(8,128)(2,1)S(1)}, bf16[512,512]{1,0:T(8,128)(2,1)S(1)}) custom-call(s32[1,512]{1,0:T(1,128)S(1)} %copy-done.18, bf16[2048,512]{1,0:T(8,128)(2,1)S(1)} %copy-done.2, bf16[2048,512]{1,0:T(8,128)(2,1)S(1)} %copy-done.13), custom_call_target="tpu_custom_call" | custom-call | flops 2147483648 | bytes 3145728 | tf_op jit(solution)/shard_map/pick_rows/pallas_call | solution.py:68
  20.0 2.6 %collective-permute-start.4 = (bf16[96,1024]{1,0:T(8,128)(2,1)S(1)}, bf16[96,1024]{1,0:T(8,128)(2,1)S(1)}, u32[]{:S(2)}, u32[]{:S(2)}) collective-permute-start(bf16[96,1024]{1,0:T(8,128)(2,1)S(1)} %pack.1.refs_0_), channel_id=1, source_target_pairs={{0,6},{1,25},{2,0},{3,27},{4,2},{5,29},{6,4},{7,31},{8,14},{9,1},{... | collective-permute-start | bytes 589832 | tf_op jit(solution)/shard_map/ppermute | solution.py:338
  23.1 4.9 %collective-permute-done.6.refs_0_.i2 = s32[1,512]{1,0:T(1,128)S(1)} collective-permute-done((s32[1,512]{1,0:T(1,128)S(1)}, s32[1,512]{1,0:T(1,128)S(1)}, u32[]{:S(2)}, u32[]{:S(2)}) %collective-permute-start.6) | collective-permute-done | bytes 2080 | tf_op jit(solution)/shard_map/ppermute | solution.py:338
  27.9 1.2 collective-permute-start.2
  29.1 1.4 pick_rows.11
  30.6 1.4 pick_rows.10
  32.0 1.7 collective-permute-done.2.refs_1_
  33.7 4.1 %collective-permute-start.10 = (bf16[4,96,1024]{2,1,0:T(8,128)(2,1)S(1)}, bf16[4,96,1024]{2,1,0:T(8,128)(2,1)S(1)}, u32[]{:S(2)}, u32[]{:S(2)}) collective-permute-start(bf16[4,96,1024]{2,1,0:T(8,128)(2,1)S(1)} %bundle.1.refs_0_), channel_id=1, source_target_pairs={{0,24},{1,7},{2,26},{3,1},{4,28},{5,3},{6,30},{7,5},{8,0},{9,15},{... | collective-permute-start | bytes 2359304 | tf_op jit(solution)/shard_map/ppermute | solution.py:338
  38.5 3.0 %collective-permute-start.12 = (bf16[512,512]{1,0:T(8,128)(2,1)S(1)}, bf16[512,512]{1,0:T(8,128)(2,1)S(1)}, u32[]{:S(2)}, u32[]{:S(2)}) collective-permute-start(bf16[512,512]{1,0:T(8,128)(2,1)S(1)} %pick_rows.11), channel_id=1, source_target_pairs={{0,64},{32,96},{64,0},{96,32},{1,65},{33,97},{65,1},{97,33},{2,66}... | collective-permute-start | bytes 1572872 | tf_op jit(solution)/shard_map/ppermute | solution.py:338
  41.5 1.4 pick_rows.12
  42.9 1.4 pick_rows.13
  44.4 5.0 %collective-permute-done.11.x2 = bf16[512,512]{1,0:T(8,128)(2,1)S(1)} collective-permute-done((bf16[512,512]{1,0:T(8,128)(2,1)S(1)}, bf16[512,512]{1,0:T(8,128)(2,1)S(1)}, u32[]{:S(2)}, u32[]{:S(2)}) %collective-permute-start.11) | collective-permute-done | bytes 524320 | tf_op jit(solution)/shard_map/ppermute | solution.py:338
  49.3 11.2 %collective-permute-done.12.c2 = bf16[512,512]{1,0:T(8,128)(2,1)S(1)} collective-permute-done((bf16[512,512]{1,0:T(8,128)(2,1)S(1)}, bf16[512,512]{1,0:T(8,128)(2,1)S(1)}, u32[]{:S(2)}, u32[]{:S(2)}) %collective-permute-start.12) | collective-permute-done | bytes 524320 | tf_op jit(solution)/shard_map/ppermute | solution.py:338
  60.8 5.1 %collective-permute-start.15 = (bf16[16,96,1024]{2,1,0:T(8,128)(2,1)S(1)}, bf16[16,96,1024]{2,1,0:T(8,128)(2,1)S(1)}, u32[]{:S(2)}, u32[]{:S(2)}) collective-permute-start(bf16[16,96,1024]{2,1,0:T(8,128)(2,1)S(1)} %half_of_weights.1.a), channel_id=1, source_target_pairs={{0,1},{1,0},{2,3},{3,2},{4,5},{5,4},{6,7},{7,6},{8,9},{9,8},{10,11... | collective-permute-start | bytes 9437192 | tf_op jit(solution)/shard_map/ppermute | solution.py:338
  66.6 2.0 %collective-permute-start.14 = (bf16[512,512]{1,0:T(8,128)(2,1)S(1)}, bf16[512,512]{1,0:T(8,128)(2,1)S(1)}, u32[]{:S(2)}, u32[]{:S(2)}) collective-permute-start(bf16[512,512]{1,0:T(8,128)(2,1)S(1)} %pick_rows.13), channel_id=1, source_target_pairs={{0,96},{32,0},{64,32},{96,64},{1,97},{33,1},{65,33},{97,65},{2,98}... | collective-permute-start | bytes 1572872 | tf_op jit(solution)/shard_map/ppermute | solution.py:338
  68.7 2.6 %collective-permute-done.15.b = bf16[16,96,1024]{2,1,0:T(8,128)(2,1)S(1)} collective-permute-done((bf16[16,96,1024]{2,1,0:T(8,128)(2,1)S(1)}, bf16[16,96,1024]{2,1,0:T(8,128)(2,1)S(1)}, u32[]{:S(2)}, u32[]{:S(2)}) %collective-permute-start.15) | collective-permute-done | bytes 3145760 | tf_op jit(solution)/shard_map/ppermute | solution.py:338
  71.7 3.0 %forward.1 = (bf16[512,512]{1,0:T(8,128)(2,1)S(1)}, f32[512,512]{1,0:T(8,128)S(1)}, f32[512,512]{1,0:T(8,128)S(1)}, bf16[4,512,512]{2,1,0:T(8,128)(2,1)S(1)}) custom-call(bf16[512,512]{1,0:T(8,128)(2,1)S(1)} %get-tuple-element.70.x0, bf16[512,512]{1,0:T(8,128)(2,1)S(1)} %collective-permute-done.5.x1, bf16[512,512]{1,0:T(8,128)(2,1)S(1)} %collective-permute-done.11.x2, ...), custom_call_target="tpu_custom_call" | custom-call | flops 2147483648 | bytes 10485760 | tf_op jit(solution)/shard_map/forward/pallas_call | solution.py:122
  74.7 5.9 %collective-permute-done.13.c1 = bf16[512,512]{1,0:T(8,128)(2,1)S(1)} collective-permute-done((bf16[512,512]{1,0:T(8,128)(2,1)S(1)}, bf16[512,512]{1,0:T(8,128)(2,1)S(1)}, u32[]{:S(2)}, u32[]{:S(2)}) %collective-permute-start.13) | collective-permute-done | bytes 524320 | tf_op jit(solution)/shard_map/ppermute | solution.py:338
  80.7 5.2 %backward.1 = (bf16[16,192,512]{2,1,0:T(8,128)(2,1)S(1)}, bf16[16,192,512]{2,1,0:T(8,128)(2,1)S(1)}, bf16[512,1024]{1,0:T(8,128)(2,1)S(1)}) custom-call(bf16[512,512]{1,0:T(8,128)(2,1)S(1)} %get-tuple-element.66.c0, bf16[512,512]{1,0:T(8,128)(2,1)S(1)} %collective-permute-done.13.c1, bf16[512,512]{1,0:T(8,128)(2,1)S(1)} %collective-permute-done.12.c2, ...), custom_call_target="tpu_custom_call" | custom-call | flops 4294967296 | bytes 20971520 | tf_op jit(solution)/shard_map/backward/pallas_call | solution.py:175
  85.9 0.9 collective-permute-start.16
  86.8 2.4 %slot_gradients.1 = (bf16[512,512]{1,0:T(8,128)(2,1)S(1)}, bf16[512,512]{1,0:T(8,128)(2,1)S(1)}, bf16[512,512]{1,0:T(8,128)(2,1)S(1)}, bf16[512,512]{1,0:T(8,128)(2,1)S(1)}) custom-call(bf16[512,1024]{1,0:T(8,128)(2,1)S(1)} %get-tuple-element.83.both_ref, bf16[32,96,1024]{2,1,0:T(8,128)(2,1)S(1)} %whole_weights.1.w), custom_call_target="tpu_custom_call" | custom-call | flops 2147483648 | bytes 9437184 | tf_op jit(solution)/shard_map/slot_gradients/pallas_call | solution.py:193
  89.3 2.8 %collective-permute-done.16.b_ref = bf16[16,192,512]{2,1,0:T(8,128)(2,1)S(1)} collective-permute-done((bf16[16,192,512]{2,1,0:T(8,128)(2,1)S(1)}, bf16[16,192,512]{2,1,0:T(8,128)(2,1)S(1)}, u32[]{:S(2)}, u32[]{:S(2)}) %collective-permute-start.16) | collective-permute-done | bytes 3145760 | tf_op jit(solution)/shard_map/ppermute | solution.py:338
  94.3 1.7 %pair_merge.1 = bf16[16,192,512]{2,1,0:T(8,128)(2,1)S(1)} custom-call(bf16[16,192,512]{2,1,0:T(8,128)(2,1)S(1)} %get-tuple-element.81.a_ref, bf16[16,192,512]{2,1,0:T(8,128)(2,1)S(1)} %collective-permute-done.16.b_ref, f32[9,8,128]{2,1,0:T(8,128)S(1)} %pair_moments.1.m_ref, f32[9,8,128]{2,1,0:T(8,128)S(1)} %collective-permute-done.17.t_ref), custom_call_target="tpu_custom_call" | custom-call | flops 9437184 | bytes 9437184 | tf_op jit(solution)/shard_map/pair_merge/pallas_call | solution.py:235
  96.0 1.6 copy-done
  97.6 4.9 %all-to-all-start = ((bf16[16,192,512]{2,1,0:T(8,128)(2,1)}), bf16[16,192,512]{2,1,0:T(8,128)(2,1)S(1)}, u32[]{:S(2)}, u32[]{:S(2)}) async-start(bf16[16,192,512]{2,1,0:T(8,128)(2,1)} %copy-done), calls=%async_computation | async-start | bytes 6291456 | tf_op jit(solution)/shard_map/all_to_all | solution.py:495
  102.6 3.0 %collective-permute-start.18 = (bf16[512,512]{1,0:T(8,128)(2,1)}, bf16[512,512]{1,0:T(8,128)(2,1)S(1)}, u32[]{:S(2)}, u32[]{:S(2)}) collective-permute-start(bf16[512,512]{1,0:T(8,128)(2,1)} %copy-done.16), channel_id=1, source_target_pairs={{0,96},{32,0},{64,32},{96,64},{1,97},{33,1},{65,33},{97,65},{2,98}... | collective-permute-start | bytes 1572872 | tf_op jit(solution)/shard_map/ppermute | solution.py:338
  106.2 11.3 %collective-permute-done.18.g1 = bf16[512,512]{1,0:T(8,128)(2,1)S(1)} collective-permute-done((bf16[512,512]{1,0:T(8,128)(2,1)}, bf16[512,512]{1,0:T(8,128)(2,1)S(1)}, u32[]{:S(2)}, u32[]{:S(2)}) %collective-permute-start.18) | collective-permute-done | bytes 524320 | tf_op jit(solution)/shard_map/ppermute | solution.py:338
  117.5 2.4 %collective-permute-done.19.g2 = bf16[512,512]{1,0:T(8,128)(2,1)S(1)} collective-permute-done((bf16[512,512]{1,0:T(8,128)(2,1)}, bf16[512,512]{1,0:T(8,128)(2,1)S(1)}, u32[]{:S(2)}, u32[]{:S(2)}) %collective-permute-start.19) | collective-permute-done | bytes 524320 | tf_op jit(solution)/shard_map/ppermute | solution.py:338
  119.9 11.8 %collective-permute-done.20.g3 = bf16[512,512]{1,0:T(8,128)(2,1)S(1)} collective-permute-done((bf16[512,512]{1,0:T(8,128)(2,1)}, bf16[512,512]{1,0:T(8,128)(2,1)S(1)}, u32[]{:S(2)}, u32[]{:S(2)}) %collective-permute-start.20) | collective-permute-done | bytes 524320 | tf_op jit(solution)/shard_map/ppermute | solution.py:338
  131.7 1.0 copy-done.20
  132.7 6.0 %scatter_rows.1 = f32[2048,512]{1,0:T(8,128)} custom-call(s32[1,512]{1,0:T(1,128)S(1)} %copy-done.18, s32[1,512]{1,0:T(1,128)S(1)} %collective-permute-done.refs_0_.i1, s32[1,512]{1,0:T(1,128)S(1)} %collective-permute-done.6.refs_0_.i2, s32[1,512]{1,0:T(1,128)S(1)} %collective-permute-done.1.refs_0_.i3, bf16[512,512]{1,0:T(8,128)(2,1)S(1)} %copy-done.20, ...), custom_call_target="tpu_custom_call" | custom-call | flops 4294967296 | bytes 6291456 | tf_op jit(solution)/shard_map/scatter_rows/pallas_call | solution.py:323
  138.7 4.5 %all-to-all-done.x = bf16[16,192,512]{2,1,0:T(8,128)(2,1)S(1)} async-done(((bf16[16,192,512]{2,1,0:T(8,128)(2,1)}), bf16[16,192,512]{2,1,0:T(8,128)(2,1)S(1)}, u32[]{:S(2)}, u32[]{:S(2)}) %all-to-all-start) | async-done | bytes 3145760 | tf_op jit(solution)/shard_map/all_to_all | solution.py:495
  143.2 2.1 %gram.1 = f32[3,16,128]{2,1,0:T(8,128)S(1)} custom-call(bf16[16,192,512]{2,1,0:T(8,128)(2,1)S(1)} %all-to-all-done.x), custom_call_target="tpu_custom_call" | custom-call | flops 805306368 | bytes 3145728 | tf_op jit(solution)/shard_map/gram/pallas_call | solution.py:264
  145.3 4.5 %collective-permute-start.23 = (f32[3,16,128]{2,1,0:T(8,128)S(1)}, f32[3,16,128]{2,1,0:T(8,128)S(1)}, u32[]{:S(2)}, u32[]{:S(2)}) collective-permute-start(f32[3,16,128]{2,1,0:T(8,128)S(1)} %gram.1), channel_id=1, source_target_pairs={{0,6},{1,7},{2,0},{3,1},{4,2},{5,3},{6,4},{7,5},{8,14},{9,15},{10,... | collective-permute-start | bytes 73736 | tf_op jit(solution)/shard_map/ppermute | solution.py:338
  149.7 1.9 %collective-permute-start.21 = (f32[3,16,128]{2,1,0:T(8,128)S(1)}, f32[3,16,128]{2,1,0:T(8,128)S(1)}, u32[]{:S(2)}, u32[]{:S(2)}) collective-permute-start(f32[3,16,128]{2,1,0:T(8,128)S(1)} %gram.1), channel_id=1, source_target_pairs={{0,4},{1,5},{2,6},{3,7},{4,0},{5,1},{6,2},{7,3},{8,12},{9,13},{10,... | collective-permute-start | bytes 73736 | tf_op jit(solution)/shard_map/ppermute | solution.py:338
  151.6 2.0 %collective-permute-done.22 = f32[3,16,128]{2,1,0:T(8,128)S(1)} collective-permute-done((f32[3,16,128]{2,1,0:T(8,128)S(1)}, f32[3,16,128]{2,1,0:T(8,128)S(1)}, u32[]{:S(2)}, u32[]{:S(2)}) %collective-permute-start.22) | collective-permute-done | bytes 24608 | tf_op jit(solution)/shard_map/ppermute | solution.py:338
  153.9 2.8 %collective-permute-start.26 = (f32[3,16,128]{2,1,0:T(8,128)S(1)}, f32[3,16,128]{2,1,0:T(8,128)S(1)}, u32[]{:S(2)}, u32[]{:S(2)}) collective-permute-start(f32[3,16,128]{2,1,0:T(8,128)S(1)} %add_add_fusion.1), channel_id=1, source_target_pairs={{0,24},{1,25},{2,26},{3,27},{4,28},{5,29},{6,30},{7,31},{8,0},{9,1... | collective-permute-start | bytes 73736 | tf_op jit(solution)/shard_map/ppermute | solution.py:338
  156.8 4.2 %collective-permute-start.24 = (f32[3,16,128]{2,1,0:T(8,128)S(1)}, f32[3,16,128]{2,1,0:T(8,128)S(1)}, u32[]{:S(2)}, u32[]{:S(2)}) collective-permute-start(f32[3,16,128]{2,1,0:T(8,128)S(1)} %add_add_fusion.1), channel_id=1, source_target_pairs={{0,16},{1,17},{2,18},{3,19},{4,20},{5,21},{6,22},{7,23},{8,24},{9,... | collective-permute-start | bytes 73736 | tf_op jit(solution)/shard_map/ppermute | solution.py:338
  161.0 1.4 collective-permute-done.24
  162.5 4.4 %collective-permute-start.27 = (f32[3,16,128]{2,1,0:T(8,128)S(1)}, f32[3,16,128]{2,1,0:T(8,128)S(1)}, u32[]{:S(2)}, u32[]{:S(2)}) collective-permute-start(f32[3,16,128]{2,1,0:T(8,128)S(1)} %add_add_fusion), channel_id=1, source_target_pairs={{0,1},{1,0},{2,3},{3,2},{4,5},{5,4},{6,7},{7,6},{8,9},{9,8},{10,11... | collective-permute-start | bytes 73736 | tf_op jit(solution)/shard_map/ppermute | solution.py:338
  167.8 1.8 %finish.1 = (f32[64,512]{1,0:T(8,128)}, f32[64,512]{1,0:T(8,128)}, f32[16,2048]{1,0:T(8,128)}, f32[64,512]{1,0:T(8,128)}, f32[64,512]{1,0:T(8,128)}, /*index=5*/f32[16,2048]{1,0:T(8,128)}) custom-call(bf16[16,192,512]{2,1,0:T(8,128)(2,1)S(1)} %all-to-all-done.x, f32[3,16,128]{2,1,0:T(8,128)S(1)} %add.27.g_ref, f32[64,512]{1,0:T(8,128)S(1)} %bitcast.13, ...), custom_call_target="tpu_custom_call" | custom-call | flops 4194304 | bytes 6291456 | tf_op jit(solution)/shard_map/finish/pallas_call | solution.py:306
  (74 shorter events, 10.0 us)
Async XLA Ops:
  0.6 8.5 %collective-permute-start = (s32[1,512]{1,0:T(1,128)}, s32[1,512]{1,0:T(1,128)S(1)}, u32[]{:S(2)}, u32[]{:S(2)}) collective-permute-start(s32[1,512]{1,0:T(1,128)} %i0.1), channel_id=1, source_target_pairs={{0,96},{32,0},{64,32},{96,64},{1,97},{33,1},{65,33},{97,65},{2,98}... | collective-permute-start | bytes 6152 | tf_op jit(solution)/shard_map/ppermute | solution.py:338
  4.3 7.9 %collective-permute-start.1 = (s32[1,512]{1,0:T(1,128)}, s32[1,512]{1,0:T(1,128)S(1)}, u32[]{:S(2)}, u32[]{:S(2)}) collective-permute-start(s32[1,512]{1,0:T(1,128)} %i0.1), channel_id=1, source_target_pairs={{0,32},{32,64},{64,96},{96,0},{1,33},{33,65},{65,97},{97,1},{2,34}... | collective-permute-start | bytes 6152 | tf_op jit(solution)/shard_map/ppermute | solution.py:338
  4.3 1.6 copy-start.1
  6.8 0.9 copy-start.6
  9.1 1.6 copy-start.2
  10.7 5.7 %copy-start.18 = (s32[1,512]{1,0:T(1,128)S(1)}, s32[1,512]{1,0:T(1,128)}, u32[]{:S(2)}) copy-start(s32[1,512]{1,0:T(1,128)} %i0.1) | copy-start | bytes 6148
  10.7 6.8 %copy-start.13 = (bf16[2048,512]{1,0:T(8,128)(2,1)S(1)}, bf16[2048,512]{1,0:T(8,128)(2,1)}, u32[]{:S(2)}) copy-start(bf16[2048,512]{1,0:T(8,128)(2,1)} %refs_1_.13) | copy-start | bytes 6291460
  13.6 20.1 %collective-permute-start.5 = (bf16[512,512]{1,0:T(8,128)(2,1)S(1)}, bf16[512,512]{1,0:T(8,128)(2,1)S(1)}, u32[]{:S(2)}, u32[]{:S(2)}) collective-permute-start(bf16[512,512]{1,0:T(8,128)(2,1)S(1)} %pick_rows.7), channel_id=1, source_target_pairs={{0,32},{32,64},{64,96},{96,0},{1,33},{33,65},{65,97},{97,1},{2,34}... | collective-permute-start | bytes 1572872 | tf_op jit(solution)/shard_map/ppermute | solution.py:338
  13.7 20.0 %collective-permute-start.7 = (bf16[512,512]{1,0:T(8,128)(2,1)S(1)}, bf16[512,512]{1,0:T(8,128)(2,1)S(1)}, u32[]{:S(2)}, u32[]{:S(2)}) collective-permute-start(bf16[512,512]{1,0:T(8,128)(2,1)S(1)} %pick_rows.8), channel_id=1, source_target_pairs={{0,96},{32,0},{64,32},{96,64},{1,97},{33,1},{65,33},{97,65},{2,98}... | collective-permute-start | bytes 1572872 | tf_op jit(solution)/shard_map/ppermute | solution.py:338
  16.4 11.6 %collective-permute-start.6 = (s32[1,512]{1,0:T(1,128)S(1)}, s32[1,512]{1,0:T(1,128)S(1)}, u32[]{:S(2)}, u32[]{:S(2)}) collective-permute-start(s32[1,512]{1,0:T(1,128)S(1)} %copy-done.18), channel_id=1, source_target_pairs={{0,64},{32,96},{64,0},{96,32},{1,65},{33,97},{65,1},{97,33},{2,66}... | collective-permute-start | bytes 6152 | tf_op jit(solution)/shard_map/ppermute | solution.py:338
  20.0 10.6 %copy-start.3 = (bf16[2048,512]{1,0:T(8,128)(2,1)S(1)}, bf16[2048,512]{1,0:T(8,128)(2,1)}, u32[]{:S(2)}) copy-start(bf16[2048,512]{1,0:T(8,128)(2,1)} %refs_1_.10) | copy-start | bytes 6291460
  20.0 12.0 %collective-permute-start.4 = (bf16[96,1024]{1,0:T(8,128)(2,1)S(1)}, bf16[96,1024]{1,0:T(8,128)(2,1)S(1)}, u32[]{:S(2)}, u32[]{:S(2)}) collective-permute-start(bf16[96,1024]{1,0:T(8,128)(2,1)S(1)} %pack.1.refs_0_), channel_id=1, source_target_pairs={{0,6},{1,25},{2,0},{3,27},{4,2},{5,29},{6,4},{7,31},{8,14},{9,1},{... | collective-permute-start | bytes 589832 | tf_op jit(solution)/shard_map/ppermute | solution.py:338
  22.5 9.4 %collective-permute-start.3 = (bf16[96,1024]{1,0:T(8,128)(2,1)S(1)}, bf16[96,1024]{1,0:T(8,128)(2,1)S(1)}, u32[]{:S(2)}, u32[]{:S(2)}) collective-permute-start(bf16[96,1024]{1,0:T(8,128)(2,1)S(1)} %pack.1.refs_0_), channel_id=1, source_target_pairs={{0,4},{1,17},{2,6},{3,19},{4,0},{5,21},{6,2},{7,23},{8,12},{9,25},... | collective-permute-start | bytes 589832 | tf_op jit(solution)/shard_map/ppermute | solution.py:338
  27.9 5.7 %collective-permute-start.2 = (bf16[96,1024]{1,0:T(8,128)(2,1)S(1)}, bf16[96,1024]{1,0:T(8,128)(2,1)S(1)}, u32[]{:S(2)}, u32[]{:S(2)}) collective-permute-start(bf16[96,1024]{1,0:T(8,128)(2,1)S(1)} %pack.1.refs_0_), channel_id=1, source_target_pairs={{0,2},{1,9},{2,4},{3,11},{4,6},{5,13},{6,0},{7,15},{8,10},{9,17},{... | collective-permute-start | bytes 589832 | tf_op jit(solution)/shard_map/ppermute | solution.py:338
  33.7 26.8 %collective-permute-start.10 = (bf16[4,96,1024]{2,1,0:T(8,128)(2,1)S(1)}, bf16[4,96,1024]{2,1,0:T(8,128)(2,1)S(1)}, u32[]{:S(2)}, u32[]{:S(2)}) collective-permute-start(bf16[4,96,1024]{2,1,0:T(8,128)(2,1)S(1)} %bundle.1.refs_0_), channel_id=1, source_target_pairs={{0,24},{1,7},{2,26},{3,1},{4,28},{5,3},{6,30},{7,5},{8,0},{9,15},{... | collective-permute-start | bytes 2359304 | tf_op jit(solution)/shard_map/ppermute | solution.py:338
  37.9 22.7 %collective-permute-start.9 = (bf16[4,96,1024]{2,1,0:T(8,128)(2,1)S(1)}, bf16[4,96,1024]{2,1,0:T(8,128)(2,1)S(1)}, u32[]{:S(2)}, u32[]{:S(2)}) collective-permute-start(bf16[4,96,1024]{2,1,0:T(8,128)(2,1)S(1)} %bundle.1.refs_0_), channel_id=1, source_target_pairs={{0,16},{1,5},{2,18},{3,7},{4,20},{5,1},{6,22},{7,3},{8,24},{9,13},... | collective-permute-start | bytes 2359304 | tf_op jit(solution)/shard_map/ppermute | solution.py:338
  37.9 22.7 %collective-permute-start.8 = (bf16[4,96,1024]{2,1,0:T(8,128)(2,1)S(1)}, bf16[4,96,1024]{2,1,0:T(8,128)(2,1)S(1)}, u32[]{:S(2)}, u32[]{:S(2)}) collective-permute-start(bf16[4,96,1024]{2,1,0:T(8,128)(2,1)S(1)} %bundle.1.refs_0_), channel_id=1, source_target_pairs={{0,8},{1,3},{2,10},{3,5},{4,12},{5,7},{6,14},{7,1},{8,16},{9,11},{... | collective-permute-start | bytes 2359304 | tf_op jit(solution)/shard_map/ppermute | solution.py:338
  38.5 10.8 %collective-permute-start.11 = (bf16[512,512]{1,0:T(8,128)(2,1)S(1)}, bf16[512,512]{1,0:T(8,128)(2,1)S(1)}, u32[]{:S(2)}, u32[]{:S(2)}) collective-permute-start(bf16[512,512]{1,0:T(8,128)(2,1)S(1)} %pick_rows.10), channel_id=1, source_target_pairs={{0,64},{32,96},{64,0},{96,32},{1,65},{33,97},{65,1},{97,33},{2,66}... | collective-permute-start | bytes 1572872 | tf_op jit(solution)/shard_map/ppermute | solution.py:338
  38.5 22.0 %collective-permute-start.12 = (bf16[512,512]{1,0:T(8,128)(2,1)S(1)}, bf16[512,512]{1,0:T(8,128)(2,1)S(1)}, u32[]{:S(2)}, u32[]{:S(2)}) collective-permute-start(bf16[512,512]{1,0:T(8,128)(2,1)S(1)} %pick_rows.11), channel_id=1, source_target_pairs={{0,64},{32,96},{64,0},{96,32},{1,65},{33,97},{65,1},{97,33},{2,66}... | collective-permute-start | bytes 1572872 | tf_op jit(solution)/shard_map/ppermute | solution.py:338
  60.8 10.4 %collective-permute-start.15 = (bf16[16,96,1024]{2,1,0:T(8,128)(2,1)S(1)}, bf16[16,96,1024]{2,1,0:T(8,128)(2,1)S(1)}, u32[]{:S(2)}, u32[]{:S(2)}) collective-permute-start(bf16[16,96,1024]{2,1,0:T(8,128)(2,1)S(1)} %half_of_weights.1.a), channel_id=1, source_target_pairs={{0,1},{1,0},{2,3},{3,2},{4,5},{5,4},{6,7},{7,6},{8,9},{9,8},{10,11... | collective-permute-start | bytes 9437192 | tf_op jit(solution)/shard_map/ppermute | solution.py:338
  66.0 14.7 %collective-permute-start.13 = (bf16[512,512]{1,0:T(8,128)(2,1)S(1)}, bf16[512,512]{1,0:T(8,128)(2,1)S(1)}, u32[]{:S(2)}, u32[]{:S(2)}) collective-permute-start(bf16[512,512]{1,0:T(8,128)(2,1)S(1)} %pick_rows.12), channel_id=1, source_target_pairs={{0,32},{32,64},{64,96},{96,0},{1,33},{33,65},{65,97},{97,1},{2,34}... | collective-permute-start | bytes 1572872 | tf_op jit(solution)/shard_map/ppermute | solution.py:338
  66.6 14.0 %collective-permute-start.14 = (bf16[512,512]{1,0:T(8,128)(2,1)S(1)}, bf16[512,512]{1,0:T(8,128)(2,1)S(1)}, u32[]{:S(2)}, u32[]{:S(2)}) collective-permute-start(bf16[512,512]{1,0:T(8,128)(2,1)S(1)} %pick_rows.13), channel_id=1, source_target_pairs={{0,96},{32,0},{64,32},{96,64},{1,97},{33,1},{65,33},{97,65},{2,98}... | collective-permute-start | bytes 1572872 | tf_op jit(solution)/shard_map/ppermute | solution.py:338
  71.7 9.0 %copy-start.17 = (f32[1,512]{1,0:T(1,128)S(1)}, f32[1,512]{1,0:T(1,128)}, u32[]{:S(2)}) copy-start(f32[1,512]{1,0:T(1,128)} %route_ref.1) | copy-start | bytes 6148
  85.9 6.2 %collective-permute-start.16 = (bf16[16,192,512]{2,1,0:T(8,128)(2,1)S(1)}, bf16[16,192,512]{2,1,0:T(8,128)(2,1)S(1)}, u32[]{:S(2)}, u32[]{:S(2)}) collective-permute-start(bf16[16,192,512]{2,1,0:T(8,128)(2,1)S(1)} %get-tuple-element.82), channel_id=1, source_target_pairs={{0,1},{1,0},{2,3},{3,2},{4,5},{5,4},{6,7},{7,6},{8,9},{9,8},{10,11... | collective-permute-start | bytes 9437192 | tf_op jit(solution)/shard_map/ppermute | solution.py:338
  89.3 3.7 %copy-start.14 = (bf16[512,512]{1,0:T(8,128)(2,1)}, bf16[512,512]{1,0:T(8,128)(2,1)S(1)}, u32[]{:S(2)}) copy-start(bf16[512,512]{1,0:T(8,128)(2,1)S(1)} %get-tuple-element.87) | copy-start | bytes 1572868
  89.3 3.7 %copy-start.15 = (bf16[512,512]{1,0:T(8,128)(2,1)}, bf16[512,512]{1,0:T(8,128)(2,1)S(1)}, u32[]{:S(2)}) copy-start(bf16[512,512]{1,0:T(8,128)(2,1)S(1)} %get-tuple-element.86) | copy-start | bytes 1572868
  89.3 3.7 %copy-start.16 = (bf16[512,512]{1,0:T(8,128)(2,1)}, bf16[512,512]{1,0:T(8,128)(2,1)S(1)}, u32[]{:S(2)}) copy-start(bf16[512,512]{1,0:T(8,128)(2,1)S(1)} %get-tuple-element.85) | copy-start | bytes 1572868
  89.3 3.7 %copy-start.19 = (bf16[512,512]{1,0:T(8,128)(2,1)}, bf16[512,512]{1,0:T(8,128)(2,1)S(1)}, u32[]{:S(2)}) copy-start(bf16[512,512]{1,0:T(8,128)(2,1)S(1)} %get-tuple-element.84.g0) | copy-start | bytes 1572868
  93.0 1.3 collective-permute-start.17
  96.0 1.6 copy-start
  97.6 45.6 %all-to-all-start = ((bf16[16,192,512]{2,1,0:T(8,128)(2,1)}), bf16[16,192,512]{2,1,0:T(8,128)(2,1)S(1)}, u32[]{:S(2)}, u32[]{:S(2)}) async-start(bf16[16,192,512]{2,1,0:T(8,128)(2,1)} %copy-done), calls=%async_computation | async-start | bytes 6291456 | tf_op jit(solution)/shard_map/all_to_all | solution.py:495
  102.6 14.9 %collective-permute-start.18 = (bf16[512,512]{1,0:T(8,128)(2,1)}, bf16[512,512]{1,0:T(8,128)(2,1)S(1)}, u32[]{:S(2)}, u32[]{:S(2)}) collective-permute-start(bf16[512,512]{1,0:T(8,128)(2,1)} %copy-done.16), channel_id=1, source_target_pairs={{0,96},{32,0},{64,32},{96,64},{1,97},{33,1},{65,33},{97,65},{2,98}... | collective-permute-start | bytes 1572872 | tf_op jit(solution)/shard_map/ppermute | solution.py:338
  105.5 14.3 %collective-permute-start.19 = (bf16[512,512]{1,0:T(8,128)(2,1)}, bf16[512,512]{1,0:T(8,128)(2,1)S(1)}, u32[]{:S(2)}, u32[]{:S(2)}) collective-permute-start(bf16[512,512]{1,0:T(8,128)(2,1)} %copy-done.15), channel_id=1, source_target_pairs={{0,64},{32,96},{64,0},{96,32},{1,65},{33,97},{65,1},{97,33},{2,66}... | collective-permute-start | bytes 1572872 | tf_op jit(solution)/shard_map/ppermute | solution.py:338
  105.5 26.2 %collective-permute-start.20 = (bf16[512,512]{1,0:T(8,128)(2,1)}, bf16[512,512]{1,0:T(8,128)(2,1)S(1)}, u32[]{:S(2)}, u32[]{:S(2)}) collective-permute-start(bf16[512,512]{1,0:T(8,128)(2,1)} %copy-done.14), channel_id=1, source_target_pairs={{0,32},{32,64},{64,96},{96,0},{1,33},{33,65},{65,97},{97,1},{2,34}... | collective-permute-start | bytes 1572872 | tf_op jit(solution)/shard_map/ppermute | solution.py:338
  131.7 1.0 copy-start.20
  138.7 29.1 %copy-start.5 = (f32[1,64,512]{2,1,0:T(8,128)S(1)}, f32[1,64,512]{2,1,0:T(8,128)}, u32[]{:S(2)}) copy-start(f32[1,64,512]{2,1,0:T(8,128)} %param.14) | copy-start | bytes 393220
  138.7 29.1 %copy-start.7 = (f32[1,64,512]{2,1,0:T(8,128)S(1)}, f32[1,64,512]{2,1,0:T(8,128)}, u32[]{:S(2)}) copy-start(f32[1,64,512]{2,1,0:T(8,128)} %param.15) | copy-start | bytes 393220
  138.7 29.1 %copy-start.9 = (f32[1,16,2048]{2,1,0:T(8,128)S(1)}, f32[1,16,2048]{2,1,0:T(8,128)}, u32[]{:S(2)}) copy-start(f32[1,16,2048]{2,1,0:T(8,128)} %param.16) | copy-start | bytes 393220
  143.2 24.6 %copy-start.10 = (f32[1,64,512]{2,1,0:T(8,128)S(1)}, f32[1,64,512]{2,1,0:T(8,128)}, u32[]{:S(2)}) copy-start(f32[1,64,512]{2,1,0:T(8,128)} %param.17) | copy-start | bytes 393220
  143.2 24.6 %copy-start.11 = (f32[1,64,512]{2,1,0:T(8,128)S(1)}, f32[1,64,512]{2,1,0:T(8,128)}, u32[]{:S(2)}) copy-start(f32[1,64,512]{2,1,0:T(8,128)} %param.18) | copy-start | bytes 393220
  143.2 24.6 %copy-start.12 = (f32[1,16,2048]{2,1,0:T(8,128)S(1)}, f32[1,16,2048]{2,1,0:T(8,128)}, u32[]{:S(2)}) copy-start(f32[1,16,2048]{2,1,0:T(8,128)} %param.19) | copy-start | bytes 393220
  145.3 6.4 %collective-permute-start.23 = (f32[3,16,128]{2,1,0:T(8,128)S(1)}, f32[3,16,128]{2,1,0:T(8,128)S(1)}, u32[]{:S(2)}, u32[]{:S(2)}) collective-permute-start(f32[3,16,128]{2,1,0:T(8,128)S(1)} %gram.1), channel_id=1, source_target_pairs={{0,6},{1,7},{2,0},{3,1},{4,2},{5,3},{6,4},{7,5},{8,14},{9,15},{10,... | collective-permute-start | bytes 73736 | tf_op jit(solution)/shard_map/ppermute | solution.py:338
  149.7 3.9 %collective-permute-start.22 = (f32[3,16,128]{2,1,0:T(8,128)S(1)}, f32[3,16,128]{2,1,0:T(8,128)S(1)}, u32[]{:S(2)}, u32[]{:S(2)}) collective-permute-start(f32[3,16,128]{2,1,0:T(8,128)S(1)} %gram.1), channel_id=1, source_target_pairs={{0,2},{1,3},{2,4},{3,5},{4,6},{5,7},{6,0},{7,1},{8,10},{9,11},{10,... | collective-permute-start | bytes 73736 | tf_op jit(solution)/shard_map/ppermute | solution.py:338
  149.7 4.2 %collective-permute-start.21 = (f32[3,16,128]{2,1,0:T(8,128)S(1)}, f32[3,16,128]{2,1,0:T(8,128)S(1)}, u32[]{:S(2)}, u32[]{:S(2)}) collective-permute-start(f32[3,16,128]{2,1,0:T(8,128)S(1)} %gram.1), channel_id=1, source_target_pairs={{0,4},{1,5},{2,6},{3,7},{4,0},{5,1},{6,2},{7,3},{8,12},{9,13},{10,... | collective-permute-start | bytes 73736 | tf_op jit(solution)/shard_map/ppermute | solution.py:338
  153.9 7.0 %collective-permute-start.26 = (f32[3,16,128]{2,1,0:T(8,128)S(1)}, f32[3,16,128]{2,1,0:T(8,128)S(1)}, u32[]{:S(2)}, u32[]{:S(2)}) collective-permute-start(f32[3,16,128]{2,1,0:T(8,128)S(1)} %add_add_fusion.1), channel_id=1, source_target_pairs={{0,24},{1,25},{2,26},{3,27},{4,28},{5,29},{6,30},{7,31},{8,0},{9,1... | collective-permute-start | bytes 73736 | tf_op jit(solution)/shard_map/ppermute | solution.py:338
  156.8 4.2 %collective-permute-start.25 = (f32[3,16,128]{2,1,0:T(8,128)S(1)}, f32[3,16,128]{2,1,0:T(8,128)S(1)}, u32[]{:S(2)}, u32[]{:S(2)}) collective-permute-start(f32[3,16,128]{2,1,0:T(8,128)S(1)} %add_add_fusion.1), channel_id=1, source_target_pairs={{0,8},{1,9},{2,10},{3,11},{4,12},{5,13},{6,14},{7,15},{8,16},{9,17... | collective-permute-start | bytes 73736 | tf_op jit(solution)/shard_map/ppermute | solution.py:338
  156.8 5.7 %collective-permute-start.24 = (f32[3,16,128]{2,1,0:T(8,128)S(1)}, f32[3,16,128]{2,1,0:T(8,128)S(1)}, u32[]{:S(2)}, u32[]{:S(2)}) collective-permute-start(f32[3,16,128]{2,1,0:T(8,128)S(1)} %add_add_fusion.1), channel_id=1, source_target_pairs={{0,16},{1,17},{2,18},{3,19},{4,20},{5,21},{6,22},{7,23},{8,24},{9,... | collective-permute-start | bytes 73736 | tf_op jit(solution)/shard_map/ppermute | solution.py:338
  162.5 5.3 %collective-permute-start.27 = (f32[3,16,128]{2,1,0:T(8,128)S(1)}, f32[3,16,128]{2,1,0:T(8,128)S(1)}, u32[]{:S(2)}, u32[]{:S(2)}) collective-permute-start(f32[3,16,128]{2,1,0:T(8,128)S(1)} %add_add_fusion), channel_id=1, source_target_pairs={{0,1},{1,0},{2,3},{3,2},{4,5},{5,4},{6,7},{7,6},{8,9},{9,8},{10,11... | collective-permute-start | bytes 73736 | tf_op jit(solution)/shard_map/ppermute | solution.py:338
  (2 other events, 1.8 us)

commit v5 on v4

--- a/solution.py
+++ b/solution.py
@@ -360,8 +360,8 @@
     return value + other_core(value)
 
 
-def pack(gate, up, down, pool):
-    def body(gate_hbm, up_hbm, down_hbm, pool_ref, out, g, u, d, sems):
+def pack(gate, up, down):
+    def body(gate_hbm, up_hbm, down_hbm, out, g, u, d, sems):
         copies = [
             pltpu.make_async_copy(src, dst, sems.at[j])
             for j, (src, dst) in enumerate(((gate_hbm, g), (up_hbm, u), (down_hbm, d)))
@@ -379,7 +379,7 @@
         body,
         name="pack",
         out_shape=struct((96, 1024), BF16),
-        in_specs=[pl.BlockSpec(memory_space=pltpu.HBM)] * 3 + [vmem()],
+        in_specs=[pl.BlockSpec(memory_space=pl.ANY)] * 3,
         out_specs=vmem(),
         scratch_shapes=[
             pltpu.VMEM((64, H), F32),
@@ -389,7 +389,7 @@
         ],
         compiler_params=pltpu.CompilerParams(vmem_limit_bytes=8 * MIB),
         cost_estimate=pl.CostEstimate(flops=2**17, bytes_accessed=MIB, transcendentals=0),
-    )(gate, up, down, pool)
+    )(gate, up, down)
 
 
 def along(turn, step):
@@ -460,26 +460,26 @@
         return pick_rows(ids[k : k + 1], [pool])[0]
 
     ids = [token_ids] + [around_y(token_ids, N_EXPERT - k) for k in (1, 2, 3)]
-    packed = pack(gate_weight[0], up_weight[0], down_weight[0], pool_tokens)
+    packed = pack(gate_weight[0], up_weight[0], down_weight[0])
     x, c = [None] * 4, [None] * 4
     x[1], x[3] = picked(1, pool_tokens), picked(3, pool_tokens)
-    packed, x[1], x[3] = tie((packed, x[1], x[3]))
-
+    ids, packed, x[1], x[3] = tie((ids, packed, x[1], x[3]))
+
+    blocks = spread(packed, 0)
     x[1], x[3] = around_y(x[1], 1), around_y(x[3], 3)
-    blocks = spread(packed, 0)
     x[2], c[2] = picked(2, pool_tokens), picked(2, pool_cotangent)
-    x[0], c[0] = pick_rows(ids[:1], [pool_tokens, pool_cotangent])
-    blocks, x, c[2], c[0] = tie((blocks, x, c[2], c[0]))
-
-    x[2], c[2] = around_y(x[2], 2), around_y(c[2], 2)
+    ids, blocks, x[1:], c[2] = tie((ids, blocks, x[1:], c[2]))
+
     block = bundle((packed, *blocks))
     blocks = spread(block, 1)
+    x[2], c[2] = around_y(x[2], 2), around_y(c[2], 2)
     c[1], c[3] = picked(1, pool_cotangent), picked(3, pool_cotangent)
+    x[0], c[0] = pick_rows(ids[:1], [pool_tokens, pool_cotangent])
     blocks, x, c = tie((blocks, x, c))
 
-    c[1], c[3] = around_y(c[1], 1), around_y(c[3], 3)
     mine = half_of_weights((block, *blocks))
     weights = whole_weights(mine, other_core(mine))
+    c[1], c[3] = around_y(c[1], 1), around_y(c[3], 3)
     tokens, cots = x, c
 
     hidden_t, gate_factor, act, xt = forward(tokens, weights)
@@ -491,6 +491,7 @@
 
     mine = pair_moments(keep, received)
     merged = pair_merge(keep, received, mine, other_core(mine))
+    merged = pltpu.with_memory_space_constraint(merged, pltpu.HBM)
     groups = [[2 * q + c for q in range(N_CHIP)] for c in range(2)]
     parts = lax.all_to_all(merged, "dp", 0, 0, tiled=True, axis_index_groups=groups)
     pool_grad = scatter_rows(ids, back)

time: 170 us -> 168 us (0.988)
  Pallas kernels: 35.1 us -> 40.3 us
  local copies, waits for them, and re-layouts: 8.62 us -> 4.35 us
  waiting for transfers between devices: 69.6 us -> 66.2 us
    ppermute x28, waiting for transfers between devices: 65.2 us -> 60.3 us  [shift(): lax.ppermute(block, axis, [(i, to(i)) for i in range(lax.axis_size(axis))])]
    unnamed x42 -> x28, local copies, waits for them, and re-layouts: 8.62 us -> 4.35 us
    pallas_call x1, Pallas kernels: 1.77 us -> 3.66 us  [finish(): call(body, 'finish', 8, [wide, wide, tall, wide, wide, tall], 2 ** 22, 6...]
    pallas_call x1, Pallas kernels: 2.05 us -> 3.94 us  [gram(): call(body, 'gram', 1, struct((3, 16, 128), F32), 12 * 2 * 256 * 256 * 512...]
  transfers between devices with their start and end apart: 29 -> 29, of which waited for: 16 -> 17; matrix products, arithmetic and copies ran while one was open for 0% -> 0% of each run, Pallas kernels for 13% -> 14%
where the time goes in v5:
time: 168 us
  waiting for transfers between devices  66.2 us (39%)
  starting transfers between devices  56.2 us (33%)
  Pallas kernels  40.3 us (24%)
  local copies, waits for them, and re-layouts  4.35 us (3%)
    ppermute x28, waiting for transfers between devices, shift(): lax.ppermute(block, axis, [(i, to(i)) for i in range(lax.axis_size(axis))])  60.3 us
    ppermute x28, starting transfers between devices, shift(): lax.ppermute(block, axis, [(i, to(i)) for i in range(lax.axis_size(axis))])  50.6 us
    pallas_call x7, Pallas kernels, pick_rows(): call(body, 'pick_rows', n_ids + n_pool, shapes, 2 * TOK_DEV * POOL * SLIC...  10.9 us
    all_to_all x1, waiting for transfers between devices, local(): lax.all_to_all(merged, 'dp', 0, 0, tiled=True, axis_index_groups=groups)  5.98 us
    pallas_call x1, Pallas kernels, scatter_rows(): pl.pallas_call(body, name='scatter_rows', grid=(POOL // block,), out_shap...  5.97 us
    all_to_all x1, starting transfers between devices, local(): lax.all_to_all(merged, 'dp', 0, 0, tiled=True, axis_index_groups=groups)  5.6 us
    pallas_call x1, Pallas kernels, backward(): call(body, 'backward', 10, shapes, 8 * TOK_DEV * D * H, 20 * MIB, [pltpu....  5.14 us
    unnamed x28, local copies, waits for them, and re-layouts  4.35 us
  transfers between devices with their start and end apart: 29, of which 17 were waited for; matrix products, arithmetic and copies ran while one was open for 0% of the time, Pallas kernels for 14%

profile of v5, /device:TPU:1, one launch (start us, length us, event | category | flops | bytes accessed | tf_op | source)
XLA Modules:
  0.0 168.0 jit_solution(10253012457853689434)
XLA Ops:
  0.6 2.2 %collective-permute-start.2 = (s32[1,512]{1,0:T(1,128)}, s32[1,512]{1,0:T(1,128)S(1)}, u32[]{:S(2)}, u32[]{:S(2)}) collective-permute-start(s32[1,512]{1,0:T(1,128)} %i0), channel_id=1, source_target_pairs={{0,32},{32,64},{64,96},{96,0},{1,33},{33,65},{65,97},{97,1},{2,34}... | collective-permute-start | bytes 6152 | tf_op jit(solution)/shard_map/ppermute | solution.py:338
  2.8 2.6 %collective-permute-start.1 = (s32[1,512]{1,0:T(1,128)}, s32[1,512]{1,0:T(1,128)S(1)}, u32[]{:S(2)}, u32[]{:S(2)}) collective-permute-start(s32[1,512]{1,0:T(1,128)} %i0), channel_id=1, source_target_pairs={{0,64},{32,96},{64,0},{96,32},{1,65},{33,97},{65,1},{97,33},{2,66}... | collective-permute-start | bytes 6152 | tf_op jit(solution)/shard_map/ppermute | solution.py:338
  5.4 1.1 collective-permute-start
  6.5 0.9 copy-done
  7.4 0.9 copy-done.2
  8.3 0.9 copy-done.4
  9.8 1.6 copy-done.9
  11.4 1.4 pick_rows.8
  12.8 1.4 pick_rows.7
  14.7 2.3 %collective-permute-start.7 = (bf16[512,512]{1,0:T(8,128)(2,1)S(1)}, bf16[512,512]{1,0:T(8,128)(2,1)S(1)}, u32[]{:S(2)}, u32[]{:S(2)}) collective-permute-start(bf16[512,512]{1,0:T(8,128)(2,1)S(1)} %pick_rows.8), channel_id=1, source_target_pairs={{0,96},{32,0},{64,32},{96,64},{1,97},{33,1},{65,33},{97,65},{2,98}... | collective-permute-start | bytes 1572872 | tf_op jit(solution)/shard_map/ppermute | solution.py:338
  17.0 2.5 %collective-permute-start.5 = (bf16[96,1024]{1,0:T(8,128)(2,1)S(1)}, bf16[96,1024]{1,0:T(8,128)(2,1)S(1)}, u32[]{:S(2)}, u32[]{:S(2)}) collective-permute-start(bf16[96,1024]{1,0:T(8,128)(2,1)S(1)} %pack.1.refs_0_), channel_id=1, source_target_pairs={{0,6},{1,25},{2,0},{3,27},{4,2},{5,29},{6,4},{7,31},{8,14},{9,1},{... | collective-permute-start | bytes 589832 | tf_op jit(solution)/shard_map/ppermute | solution.py:338
  20.6 1.4 pick_rows.9
  22.0 1.4 pick_rows.10
  24.2 1.4 collective-permute-done.4.refs_2_
  25.6 2.3 %collective-permute-done.3.refs_1_ = bf16[96,1024]{1,0:T(8,128)(2,1)S(1)} collective-permute-done((bf16[96,1024]{1,0:T(8,128)(2,1)S(1)}, bf16[96,1024]{1,0:T(8,128)(2,1)S(1)}, u32[]{:S(2)}, u32[]{:S(2)}) %collective-permute-start.3) | collective-permute-done | bytes 196640 | tf_op jit(solution)/shard_map/ppermute | solution.py:338
  28.0 3.8 %collective-permute-start.10 = (bf16[4,96,1024]{2,1,0:T(8,128)(2,1)S(1)}, bf16[4,96,1024]{2,1,0:T(8,128)(2,1)S(1)}, u32[]{:S(2)}, u32[]{:S(2)}) collective-permute-start(bf16[4,96,1024]{2,1,0:T(8,128)(2,1)S(1)} %bundle.1.refs_0_), channel_id=1, source_target_pairs={{0,24},{1,7},{2,26},{3,1},{4,28},{5,3},{6,30},{7,5},{8,0},{9,15},{... | collective-permute-start | bytes 2359304 | tf_op jit(solution)/shard_map/ppermute | solution.py:338
  33.2 2.3 %collective-permute-start.12 = (bf16[512,512]{1,0:T(8,128)(2,1)S(1)}, bf16[512,512]{1,0:T(8,128)(2,1)S(1)}, u32[]{:S(2)}, u32[]{:S(2)}) collective-permute-start(bf16[512,512]{1,0:T(8,128)(2,1)S(1)} %pick_rows.10), channel_id=1, source_target_pairs={{0,64},{32,96},{64,0},{96,32},{1,65},{33,97},{65,1},{97,33},{2,66}... | collective-permute-start | bytes 1572872 | tf_op jit(solution)/shard_map/ppermute | solution.py:338
  35.5 1.4 pick_rows.12
  36.9 1.4 pick_rows.13
  38.4 2.5 %pick_rows.11 = (bf16[512,512]{1,0:T(8,128)(2,1)S(1)}, bf16[512,512]{1,0:T(8,128)(2,1)S(1)}) custom-call(s32[1,512]{1,0:T(1,128)S(1)} %copy-done.13, bf16[2048,512]{1,0:T(8,128)(2,1)S(1)} %copy-done.10, bf16[2048,512]{1,0:T(8,128)(2,1)S(1)} %copy-done.11), custom_call_target="tpu_custom_call" | custom-call | flops 2147483648 | bytes 3145728 | tf_op jit(solution)/shard_map/pick_rows/pallas_call | solution.py:68
  40.9 2.4 %collective-permute-done.11.x2 = bf16[512,512]{1,0:T(8,128)(2,1)S(1)} collective-permute-done((bf16[512,512]{1,0:T(8,128)(2,1)S(1)}, bf16[512,512]{1,0:T(8,128)(2,1)S(1)}, u32[]{:S(2)}, u32[]{:S(2)}) %collective-permute-start.11) | collective-permute-done | bytes 524320 | tf_op jit(solution)/shard_map/ppermute | solution.py:338
  43.3 11.2 %collective-permute-done.12.c2 = bf16[512,512]{1,0:T(8,128)(2,1)S(1)} collective-permute-done((bf16[512,512]{1,0:T(8,128)(2,1)S(1)}, bf16[512,512]{1,0:T(8,128)(2,1)S(1)}, u32[]{:S(2)}, u32[]{:S(2)}) %collective-permute-start.12) | collective-permute-done | bytes 524320 | tf_op jit(solution)/shard_map/ppermute | solution.py:338
  54.8 5.2 %collective-permute-start.15 = (bf16[16,96,1024]{2,1,0:T(8,128)(2,1)S(1)}, bf16[16,96,1024]{2,1,0:T(8,128)(2,1)S(1)}, u32[]{:S(2)}, u32[]{:S(2)}) collective-permute-start(bf16[16,96,1024]{2,1,0:T(8,128)(2,1)S(1)} %half_of_weights.1.a), channel_id=1, source_target_pairs={{0,1},{1,0},{2,3},{3,2},{4,5},{5,4},{6,7},{7,6},{8,9},{9,8},{10,11... | collective-permute-start | bytes 9437192 | tf_op jit(solution)/shard_map/ppermute | solution.py:338
  60.0 2.7 %collective-permute-start.14 = (bf16[512,512]{1,0:T(8,128)(2,1)S(1)}, bf16[512,512]{1,0:T(8,128)(2,1)S(1)}, u32[]{:S(2)}, u32[]{:S(2)}) collective-permute-start(bf16[512,512]{1,0:T(8,128)(2,1)S(1)} %pick_rows.13), channel_id=1, source_target_pairs={{0,96},{32,0},{64,32},{96,64},{1,97},{33,1},{65,33},{97,65},{2,98}... | collective-permute-start | bytes 1572872 | tf_op jit(solution)/shard_map/ppermute | solution.py:338
  62.7 2.6 %collective-permute-done.15.b = bf16[16,96,1024]{2,1,0:T(8,128)(2,1)S(1)} collective-permute-done((bf16[16,96,1024]{2,1,0:T(8,128)(2,1)S(1)}, bf16[16,96,1024]{2,1,0:T(8,128)(2,1)S(1)}, u32[]{:S(2)}, u32[]{:S(2)}) %collective-permute-start.15) | collective-permute-done | bytes 3145760 | tf_op jit(solution)/shard_map/ppermute | solution.py:338
  65.7 3.0 %forward.1 = (bf16[512,512]{1,0:T(8,128)(2,1)S(1)}, f32[512,512]{1,0:T(8,128)S(1)}, f32[512,512]{1,0:T(8,128)S(1)}, bf16[4,512,512]{2,1,0:T(8,128)(2,1)S(1)}) custom-call(bf16[512,512]{1,0:T(8,128)(2,1)S(1)} %get-tuple-element.81.x0, bf16[512,512]{1,0:T(8,128)(2,1)S(1)} %collective-permute-done.6.x1, bf16[512,512]{1,0:T(8,128)(2,1)S(1)} %collective-permute-done.11.x2, ...), custom_call_target="tpu_custom_call" | custom-call | flops 2147483648 | bytes 10485760 | tf_op jit(solution)/shard_map/forward/pallas_call | solution.py:122
  68.8 5.9 %collective-permute-done.13.c1 = bf16[512,512]{1,0:T(8,128)(2,1)S(1)} collective-permute-done((bf16[512,512]{1,0:T(8,128)(2,1)S(1)}, bf16[512,512]{1,0:T(8,128)(2,1)S(1)}, u32[]{:S(2)}, u32[]{:S(2)}) %collective-permute-start.13) | collective-permute-done | bytes 524320 | tf_op jit(solution)/shard_map/ppermute | solution.py:338
  74.7 5.1 %backward.1 = (bf16[16,192,512]{2,1,0:T(8,128)(2,1)S(1)}, bf16[16,192,512]{2,1,0:T(8,128)(2,1)S(1)}, bf16[512,1024]{1,0:T(8,128)(2,1)S(1)}) custom-call(bf16[512,512]{1,0:T(8,128)(2,1)S(1)} %get-tuple-element.77.c0, bf16[512,512]{1,0:T(8,128)(2,1)S(1)} %collective-permute-done.13.c1, bf16[512,512]{1,0:T(8,128)(2,1)S(1)} %collective-permute-done.12.c2, ...), custom_call_target="tpu_custom_call" | custom-call | flops 4294967296 | bytes 20971520 | tf_op jit(solution)/shard_map/backward/pallas_call | solution.py:175
  79.8 1.2 collective-permute-start.16
  81.0 2.4 %slot_gradients.1 = (bf16[512,512]{1,0:T(8,128)(2,1)S(1)}, bf16[512,512]{1,0:T(8,128)(2,1)S(1)}, bf16[512,512]{1,0:T(8,128)(2,1)S(1)}, bf16[512,512]{1,0:T(8,128)(2,1)S(1)}) custom-call(bf16[512,1024]{1,0:T(8,128)(2,1)S(1)} %get-tuple-element.94.both_ref, bf16[32,96,1024]{2,1,0:T(8,128)(2,1)S(1)} %whole_weights.1.w), custom_call_target="tpu_custom_call" | custom-call | flops 2147483648 | bytes 9437184 | tf_op jit(solution)/shard_map/slot_gradients/pallas_call | solution.py:193
  83.4 2.9 %collective-permute-done.16.b_ref = bf16[16,192,512]{2,1,0:T(8,128)(2,1)S(1)} collective-permute-done((bf16[16,192,512]{2,1,0:T(8,128)(2,1)S(1)}, bf16[16,192,512]{2,1,0:T(8,128)(2,1)S(1)}, u32[]{:S(2)}, u32[]{:S(2)}) %collective-permute-start.16) | collective-permute-done | bytes 3145760 | tf_op jit(solution)/shard_map/ppermute | solution.py:338
  88.4 3.1 %pair_merge.1 = bf16[16,192,512]{2,1,0:T(8,128)(2,1)} custom-call(bf16[16,192,512]{2,1,0:T(8,128)(2,1)S(1)} %get-tuple-element.92.a_ref, bf16[16,192,512]{2,1,0:T(8,128)(2,1)S(1)} %collective-permute-done.16.b_ref, f32[9,8,128]{2,1,0:T(8,128)S(1)} %pair_moments.1.m_ref, f32[9,8,128]{2,1,0:T(8,128)S(1)} %collective-permute-done.17.t_ref), custom_call_target="tpu_custom_call" | custom-call | flops 9437184 | bytes 9437184 | tf_op jit(solution)/shard_map/pair_merge/pallas_call | solution.py:235
  91.5 5.6 %all-to-all-start = ((bf16[16,192,512]{2,1,0:T(8,128)(2,1)}), bf16[16,192,512]{2,1,0:T(8,128)(2,1)}, u32[]{:S(2)}, u32[]{:S(2)}) async-start(bf16[16,192,512]{2,1,0:T(8,128)(2,1)} %pair_merge.1), calls=%async_computation | async-start | bytes 6291456 | tf_op jit(solution)/shard_map/all_to_all | solution.py:496
  97.1 2.7 %collective-permute-start.18 = (bf16[512,512]{1,0:T(8,128)(2,1)S(1)}, bf16[512,512]{1,0:T(8,128)(2,1)S(1)}, u32[]{:S(2)}, u32[]{:S(2)}) collective-permute-start(bf16[512,512]{1,0:T(8,128)(2,1)S(1)} %get-tuple-element.96), channel_id=1, source_target_pairs={{0,96},{32,0},{64,32},{96,64},{1,97},{33,1},{65,33},{97,65},{2,98}... | collective-permute-start | bytes 1572872 | tf_op jit(solution)/shard_map/ppermute | solution.py:338
  100.5 10.9 %collective-permute-done.18.g1 = bf16[512,512]{1,0:T(8,128)(2,1)S(1)} collective-permute-done((bf16[512,512]{1,0:T(8,128)(2,1)S(1)}, bf16[512,512]{1,0:T(8,128)(2,1)S(1)}, u32[]{:S(2)}, u32[]{:S(2)}) %collective-permute-start.18) | collective-permute-done | bytes 524320 | tf_op jit(solution)/shard_map/ppermute | solution.py:338
  111.5 2.6 %collective-permute-done.19.g2 = bf16[512,512]{1,0:T(8,128)(2,1)S(1)} collective-permute-done((bf16[512,512]{1,0:T(8,128)(2,1)S(1)}, bf16[512,512]{1,0:T(8,128)(2,1)S(1)}, u32[]{:S(2)}, u32[]{:S(2)}) %collective-permute-start.19) | collective-permute-done | bytes 524320 | tf_op jit(solution)/shard_map/ppermute | solution.py:338
  114.1 11.7 %collective-permute-done.20.g3 = bf16[512,512]{1,0:T(8,128)(2,1)S(1)} collective-permute-done((bf16[512,512]{1,0:T(8,128)(2,1)S(1)}, bf16[512,512]{1,0:T(8,128)(2,1)S(1)}, u32[]{:S(2)}, u32[]{:S(2)}) %collective-permute-start.20) | collective-permute-done | bytes 524320 | tf_op jit(solution)/shard_map/ppermute | solution.py:338
  125.8 6.0 %scatter_rows.1 = f32[2048,512]{1,0:T(8,128)} custom-call(s32[1,512]{1,0:T(1,128)S(1)} %copy-done.13, s32[1,512]{1,0:T(1,128)S(1)} %collective-permute-done.refs_0_.i1, s32[1,512]{1,0:T(1,128)S(1)} %collective-permute-done.1.refs_0_.i2, s32[1,512]{1,0:T(1,128)S(1)} %collective-permute-done.2.refs_0_.i3, bf16[512,512]{1,0:T(8,128)(2,1)S(1)} %get-tuple-element.95.g0, ...), custom_call_target="tpu_custom_call" | custom-call | flops 4294967296 | bytes 6291456 | tf_op jit(solution)/shard_map/scatter_rows/pallas_call | solution.py:323
  131.8 6.0 %all-to-all-done.x = bf16[16,192,512]{2,1,0:T(8,128)(2,1)} async-done(((bf16[16,192,512]{2,1,0:T(8,128)(2,1)}), bf16[16,192,512]{2,1,0:T(8,128)(2,1)}, u32[]{:S(2)}, u32[]{:S(2)}) %all-to-all-start) | async-done | bytes 3145760 | tf_op jit(solution)/shard_map/all_to_all | solution.py:496
  137.8 3.9 %gram.1 = f32[3,16,128]{2,1,0:T(8,128)S(1)} custom-call(bf16[16,192,512]{2,1,0:T(8,128)(2,1)} %all-to-all-done.x), custom_call_target="tpu_custom_call" | custom-call | flops 805306368 | bytes 3145728 | tf_op jit(solution)/shard_map/gram/pallas_call | solution.py:264
  141.8 4.5 %collective-permute-start.23 = (f32[3,16,128]{2,1,0:T(8,128)S(1)}, f32[3,16,128]{2,1,0:T(8,128)S(1)}, u32[]{:S(2)}, u32[]{:S(2)}) collective-permute-start(f32[3,16,128]{2,1,0:T(8,128)S(1)} %gram.1), channel_id=1, source_target_pairs={{0,6},{1,7},{2,0},{3,1},{4,2},{5,3},{6,4},{7,5},{8,14},{9,15},{10,... | collective-permute-start | bytes 73736 | tf_op jit(solution)/shard_map/ppermute | solution.py:338
  146.2 1.9 %collective-permute-start.21 = (f32[3,16,128]{2,1,0:T(8,128)S(1)}, f32[3,16,128]{2,1,0:T(8,128)S(1)}, u32[]{:S(2)}, u32[]{:S(2)}) collective-permute-start(f32[3,16,128]{2,1,0:T(8,128)S(1)} %gram.1), channel_id=1, source_target_pairs={{0,4},{1,5},{2,6},{3,7},{4,0},{5,1},{6,2},{7,3},{8,12},{9,13},{10,... | collective-permute-start | bytes 73736 | tf_op jit(solution)/shard_map/ppermute | solution.py:338
  148.1 2.0 %collective-permute-done.22 = f32[3,16,128]{2,1,0:T(8,128)S(1)} collective-permute-done((f32[3,16,128]{2,1,0:T(8,128)S(1)}, f32[3,16,128]{2,1,0:T(8,128)S(1)}, u32[]{:S(2)}, u32[]{:S(2)}) %collective-permute-start.22) | collective-permute-done | bytes 24608 | tf_op jit(solution)/shard_map/ppermute | solution.py:338
  150.4 2.7 %collective-permute-start.26 = (f32[3,16,128]{2,1,0:T(8,128)S(1)}, f32[3,16,128]{2,1,0:T(8,128)S(1)}, u32[]{:S(2)}, u32[]{:S(2)}) collective-permute-start(f32[3,16,128]{2,1,0:T(8,128)S(1)} %add_add_fusion.1), channel_id=1, source_target_pairs={{0,24},{1,25},{2,26},{3,27},{4,28},{5,29},{6,30},{7,31},{8,0},{9,1... | collective-permute-start | bytes 73736 | tf_op jit(solution)/shard_map/ppermute | solution.py:338
  153.2 4.3 %collective-permute-start.24 = (f32[3,16,128]{2,1,0:T(8,128)S(1)}, f32[3,16,128]{2,1,0:T(8,128)S(1)}, u32[]{:S(2)}, u32[]{:S(2)}) collective-permute-start(f32[3,16,128]{2,1,0:T(8,128)S(1)} %add_add_fusion.1), channel_id=1, source_target_pairs={{0,16},{1,17},{2,18},{3,19},{4,20},{5,21},{6,22},{7,23},{8,24},{9,... | collective-permute-start | bytes 73736 | tf_op jit(solution)/shard_map/ppermute | solution.py:338
  157.5 1.4 collective-permute-done.24
  159.0 4.4 %collective-permute-start.27 = (f32[3,16,128]{2,1,0:T(8,128)S(1)}, f32[3,16,128]{2,1,0:T(8,128)S(1)}, u32[]{:S(2)}, u32[]{:S(2)}) collective-permute-start(f32[3,16,128]{2,1,0:T(8,128)S(1)} %add_add_fusion), channel_id=1, source_target_pairs={{0,1},{1,0},{2,3},{3,2},{4,5},{5,4},{6,7},{7,6},{8,9},{9,8},{10,11... | collective-permute-start | bytes 73736 | tf_op jit(solution)/shard_map/ppermute | solution.py:338
  164.3 3.7 %finish.1 = (f32[64,512]{1,0:T(8,128)}, f32[64,512]{1,0:T(8,128)}, f32[16,2048]{1,0:T(8,128)}, f32[64,512]{1,0:T(8,128)}, f32[64,512]{1,0:T(8,128)}, /*index=5*/f32[16,2048]{1,0:T(8,128)}) custom-call(bf16[16,192,512]{2,1,0:T(8,128)(2,1)} %all-to-all-done.x, f32[3,16,128]{2,1,0:T(8,128)S(1)} %add.27.g_ref, f32[64,512]{1,0:T(8,128)S(1)} %bitcast.13, ...), custom_call_target="tpu_custom_call" | custom-call | flops 4194304 | bytes 6291456 | tf_op jit(solution)/shard_map/finish/pallas_call | solution.py:306
  (60 shorter events, 9.2 us)
Async XLA Ops:
  0.6 9.1 %collective-permute-start.2 = (s32[1,512]{1,0:T(1,128)}, s32[1,512]{1,0:T(1,128)S(1)}, u32[]{:S(2)}, u32[]{:S(2)}) collective-permute-start(s32[1,512]{1,0:T(1,128)} %i0), channel_id=1, source_target_pairs={{0,32},{32,64},{64,96},{96,0},{1,33},{33,65},{65,97},{97,1},{2,34}... | collective-permute-start | bytes 6152 | tf_op jit(solution)/shard_map/ppermute | solution.py:338
  2.8 11.4 %collective-permute-start.1 = (s32[1,512]{1,0:T(1,128)}, s32[1,512]{1,0:T(1,128)S(1)}, u32[]{:S(2)}, u32[]{:S(2)}) collective-permute-start(s32[1,512]{1,0:T(1,128)} %i0), channel_id=1, source_target_pairs={{0,64},{32,96},{64,0},{96,32},{1,65},{33,97},{65,1},{97,33},{2,66}... | collective-permute-start | bytes 6152 | tf_op jit(solution)/shard_map/ppermute | solution.py:338
  5.4 7.3 %collective-permute-start = (s32[1,512]{1,0:T(1,128)}, s32[1,512]{1,0:T(1,128)S(1)}, u32[]{:S(2)}, u32[]{:S(2)}) collective-permute-start(s32[1,512]{1,0:T(1,128)} %i0), channel_id=1, source_target_pairs={{0,96},{32,0},{64,32},{96,64},{1,97},{33,1},{65,33},{97,65},{2,98}... | collective-permute-start | bytes 6152 | tf_op jit(solution)/shard_map/ppermute | solution.py:338
  6.5 0.9 copy-start
  7.4 0.9 copy-start.2
  8.3 0.9 copy-start.4
  9.8 1.6 copy-start.9
  12.8 9.2 %copy-start.11 = (bf16[2048,512]{1,0:T(8,128)(2,1)S(1)}, bf16[2048,512]{1,0:T(8,128)(2,1)}, u32[]{:S(2)}) copy-start(bf16[2048,512]{1,0:T(8,128)(2,1)} %refs_1_.13) | copy-start | bytes 6291460
  14.2 13.7 %collective-permute-start.6 = (bf16[512,512]{1,0:T(8,128)(2,1)S(1)}, bf16[512,512]{1,0:T(8,128)(2,1)S(1)}, u32[]{:S(2)}, u32[]{:S(2)}) collective-permute-start(bf16[512,512]{1,0:T(8,128)(2,1)S(1)} %pick_rows.7), channel_id=1, source_target_pairs={{0,32},{32,64},{64,96},{96,0},{1,33},{33,65},{65,97},{97,1},{2,34}... | collective-permute-start | bytes 1572872 | tf_op jit(solution)/shard_map/ppermute | solution.py:338
  14.7 13.2 %collective-permute-start.7 = (bf16[512,512]{1,0:T(8,128)(2,1)S(1)}, bf16[512,512]{1,0:T(8,128)(2,1)S(1)}, u32[]{:S(2)}, u32[]{:S(2)}) collective-permute-start(bf16[512,512]{1,0:T(8,128)(2,1)S(1)} %pick_rows.8), channel_id=1, source_target_pairs={{0,96},{32,0},{64,32},{96,64},{1,97},{33,1},{65,33},{97,65},{2,98}... | collective-permute-start | bytes 1572872 | tf_op jit(solution)/shard_map/ppermute | solution.py:338
  17.0 7.2 %collective-permute-start.5 = (bf16[96,1024]{1,0:T(8,128)(2,1)S(1)}, bf16[96,1024]{1,0:T(8,128)(2,1)S(1)}, u32[]{:S(2)}, u32[]{:S(2)}) collective-permute-start(bf16[96,1024]{1,0:T(8,128)(2,1)S(1)} %pack.1.refs_0_), channel_id=1, source_target_pairs={{0,6},{1,25},{2,0},{3,27},{4,2},{5,29},{6,4},{7,31},{8,14},{9,1},{... | collective-permute-start | bytes 589832 | tf_op jit(solution)/shard_map/ppermute | solution.py:338
  19.4 6.1 %collective-permute-start.4 = (bf16[96,1024]{1,0:T(8,128)(2,1)S(1)}, bf16[96,1024]{1,0:T(8,128)(2,1)S(1)}, u32[]{:S(2)}, u32[]{:S(2)}) collective-permute-start(bf16[96,1024]{1,0:T(8,128)(2,1)S(1)} %pack.1.refs_0_), channel_id=1, source_target_pairs={{0,4},{1,17},{2,6},{3,19},{4,0},{5,21},{6,2},{7,23},{8,12},{9,25},... | collective-permute-start | bytes 589832 | tf_op jit(solution)/shard_map/ppermute | solution.py:338
  20.0 7.9 %collective-permute-start.3 = (bf16[96,1024]{1,0:T(8,128)(2,1)S(1)}, bf16[96,1024]{1,0:T(8,128)(2,1)S(1)}, u32[]{:S(2)}, u32[]{:S(2)}) collective-permute-start(bf16[96,1024]{1,0:T(8,128)(2,1)S(1)} %pack.1.refs_0_), channel_id=1, source_target_pairs={{0,2},{1,9},{2,4},{3,11},{4,6},{5,13},{6,0},{7,15},{8,10},{9,17},{... | collective-permute-start | bytes 589832 | tf_op jit(solution)/shard_map/ppermute | solution.py:338
  28.0 10.4 %copy-start.10 = (bf16[2048,512]{1,0:T(8,128)(2,1)S(1)}, bf16[2048,512]{1,0:T(8,128)(2,1)}, u32[]{:S(2)}) copy-start(bf16[2048,512]{1,0:T(8,128)(2,1)} %refs_1_.11) | copy-start | bytes 6291460
  28.0 10.4 %copy-start.13 = (s32[1,512]{1,0:T(1,128)S(1)}, s32[1,512]{1,0:T(1,128)}, u32[]{:S(2)}) copy-start(s32[1,512]{1,0:T(1,128)} %i0) | copy-start | bytes 6148
  28.0 26.5 %collective-permute-start.10 = (bf16[4,96,1024]{2,1,0:T(8,128)(2,1)S(1)}, bf16[4,96,1024]{2,1,0:T(8,128)(2,1)S(1)}, u32[]{:S(2)}, u32[]{:S(2)}) collective-permute-start(bf16[4,96,1024]{2,1,0:T(8,128)(2,1)S(1)} %bundle.1.refs_0_), channel_id=1, source_target_pairs={{0,24},{1,7},{2,26},{3,1},{4,28},{5,3},{6,30},{7,5},{8,0},{9,15},{... | collective-permute-start | bytes 2359304 | tf_op jit(solution)/shard_map/ppermute | solution.py:338
  31.8 22.7 %collective-permute-start.9 = (bf16[4,96,1024]{2,1,0:T(8,128)(2,1)S(1)}, bf16[4,96,1024]{2,1,0:T(8,128)(2,1)S(1)}, u32[]{:S(2)}, u32[]{:S(2)}) collective-permute-start(bf16[4,96,1024]{2,1,0:T(8,128)(2,1)S(1)} %bundle.1.refs_0_), channel_id=1, source_target_pairs={{0,16},{1,5},{2,18},{3,7},{4,20},{5,1},{6,22},{7,3},{8,24},{9,13},... | collective-permute-start | bytes 2359304 | tf_op jit(solution)/shard_map/ppermute | solution.py:338
  31.8 22.7 %collective-permute-start.8 = (bf16[4,96,1024]{2,1,0:T(8,128)(2,1)S(1)}, bf16[4,96,1024]{2,1,0:T(8,128)(2,1)S(1)}, u32[]{:S(2)}, u32[]{:S(2)}) collective-permute-start(bf16[4,96,1024]{2,1,0:T(8,128)(2,1)S(1)} %bundle.1.refs_0_), channel_id=1, source_target_pairs={{0,8},{1,3},{2,10},{3,5},{4,12},{5,7},{6,14},{7,1},{8,16},{9,11},{... | collective-permute-start | bytes 2359304 | tf_op jit(solution)/shard_map/ppermute | solution.py:338
  32.5 10.7 %collective-permute-start.11 = (bf16[512,512]{1,0:T(8,128)(2,1)S(1)}, bf16[512,512]{1,0:T(8,128)(2,1)S(1)}, u32[]{:S(2)}, u32[]{:S(2)}) collective-permute-start(bf16[512,512]{1,0:T(8,128)(2,1)S(1)} %pick_rows.9), channel_id=1, source_target_pairs={{0,64},{32,96},{64,0},{96,32},{1,65},{33,97},{65,1},{97,33},{2,66}... | collective-permute-start | bytes 1572872 | tf_op jit(solution)/shard_map/ppermute | solution.py:338
  33.2 21.3 %collective-permute-start.12 = (bf16[512,512]{1,0:T(8,128)(2,1)S(1)}, bf16[512,512]{1,0:T(8,128)(2,1)S(1)}, u32[]{:S(2)}, u32[]{:S(2)}) collective-permute-start(bf16[512,512]{1,0:T(8,128)(2,1)S(1)} %pick_rows.10), channel_id=1, source_target_pairs={{0,64},{32,96},{64,0},{96,32},{1,65},{33,97},{65,1},{97,33},{2,66}... | collective-permute-start | bytes 1572872 | tf_op jit(solution)/shard_map/ppermute | solution.py:338
  54.8 10.5 %collective-permute-start.15 = (bf16[16,96,1024]{2,1,0:T(8,128)(2,1)S(1)}, bf16[16,96,1024]{2,1,0:T(8,128)(2,1)S(1)}, u32[]{:S(2)}, u32[]{:S(2)}) collective-permute-start(bf16[16,96,1024]{2,1,0:T(8,128)(2,1)S(1)} %half_of_weights.1.a), channel_id=1, source_target_pairs={{0,1},{1,0},{2,3},{3,2},{4,5},{5,4},{6,7},{7,6},{8,9},{9,8},{10,11... | collective-permute-start | bytes 9437192 | tf_op jit(solution)/shard_map/ppermute | solution.py:338
  60.0 14.7 %collective-permute-start.13 = (bf16[512,512]{1,0:T(8,128)(2,1)S(1)}, bf16[512,512]{1,0:T(8,128)(2,1)S(1)}, u32[]{:S(2)}, u32[]{:S(2)}) collective-permute-start(bf16[512,512]{1,0:T(8,128)(2,1)S(1)} %pick_rows.12), channel_id=1, source_target_pairs={{0,32},{32,64},{64,96},{96,0},{1,33},{33,65},{65,97},{97,1},{2,34}... | collective-permute-start | bytes 1572872 | tf_op jit(solution)/shard_map/ppermute | solution.py:338
  60.0 14.7 %collective-permute-start.14 = (bf16[512,512]{1,0:T(8,128)(2,1)S(1)}, bf16[512,512]{1,0:T(8,128)(2,1)S(1)}, u32[]{:S(2)}, u32[]{:S(2)}) collective-permute-start(bf16[512,512]{1,0:T(8,128)(2,1)S(1)} %pick_rows.13), channel_id=1, source_target_pairs={{0,96},{32,0},{64,32},{96,64},{1,97},{33,1},{65,33},{97,65},{2,98}... | collective-permute-start | bytes 1572872 | tf_op jit(solution)/shard_map/ppermute | solution.py:338
  65.7 9.0 %copy-start.12 = (f32[1,512]{1,0:T(1,128)S(1)}, f32[1,512]{1,0:T(1,128)}, u32[]{:S(2)}) copy-start(f32[1,512]{1,0:T(1,128)} %route_ref.1) | copy-start | bytes 6148
  79.8 6.5 %collective-permute-start.16 = (bf16[16,192,512]{2,1,0:T(8,128)(2,1)S(1)}, bf16[16,192,512]{2,1,0:T(8,128)(2,1)S(1)}, u32[]{:S(2)}, u32[]{:S(2)}) collective-permute-start(bf16[16,192,512]{2,1,0:T(8,128)(2,1)S(1)} %get-tuple-element.93), channel_id=1, source_target_pairs={{0,1},{1,0},{2,3},{3,2},{4,5},{5,4},{6,7},{7,6},{8,9},{9,8},{10,11... | collective-permute-start | bytes 9437192 | tf_op jit(solution)/shard_map/ppermute | solution.py:338
  87.1 1.3 collective-permute-start.17
  91.5 46.3 %all-to-all-start = ((bf16[16,192,512]{2,1,0:T(8,128)(2,1)}), bf16[16,192,512]{2,1,0:T(8,128)(2,1)}, u32[]{:S(2)}, u32[]{:S(2)}) async-start(bf16[16,192,512]{2,1,0:T(8,128)(2,1)} %pair_merge.1), calls=%async_computation | async-start | bytes 6291456 | tf_op jit(solution)/shard_map/all_to_all | solution.py:496
  97.1 14.4 %collective-permute-start.18 = (bf16[512,512]{1,0:T(8,128)(2,1)S(1)}, bf16[512,512]{1,0:T(8,128)(2,1)S(1)}, u32[]{:S(2)}, u32[]{:S(2)}) collective-permute-start(bf16[512,512]{1,0:T(8,128)(2,1)S(1)} %get-tuple-element.96), channel_id=1, source_target_pairs={{0,96},{32,0},{64,32},{96,64},{1,97},{33,1},{65,33},{97,65},{2,98}... | collective-permute-start | bytes 1572872 | tf_op jit(solution)/shard_map/ppermute | solution.py:338
  99.9 14.2 %collective-permute-start.19 = (bf16[512,512]{1,0:T(8,128)(2,1)S(1)}, bf16[512,512]{1,0:T(8,128)(2,1)S(1)}, u32[]{:S(2)}, u32[]{:S(2)}) collective-permute-start(bf16[512,512]{1,0:T(8,128)(2,1)S(1)} %get-tuple-element.97), channel_id=1, source_target_pairs={{0,64},{32,96},{64,0},{96,32},{1,65},{33,97},{65,1},{97,33},{2,66}... | collective-permute-start | bytes 1572872 | tf_op jit(solution)/shard_map/ppermute | solution.py:338
  99.9 26.0 %collective-permute-start.20 = (bf16[512,512]{1,0:T(8,128)(2,1)S(1)}, bf16[512,512]{1,0:T(8,128)(2,1)S(1)}, u32[]{:S(2)}, u32[]{:S(2)}) collective-permute-start(bf16[512,512]{1,0:T(8,128)(2,1)S(1)} %get-tuple-element.98), channel_id=1, source_target_pairs={{0,32},{32,64},{64,96},{96,0},{1,33},{33,65},{65,97},{97,1},{2,34}... | collective-permute-start | bytes 1572872 | tf_op jit(solution)/shard_map/ppermute | solution.py:338
  131.8 32.5 %copy-start.1 = (f32[1,64,512]{2,1,0:T(8,128)S(1)}, f32[1,64,512]{2,1,0:T(8,128)}, u32[]{:S(2)}) copy-start(f32[1,64,512]{2,1,0:T(8,128)} %param.14) | copy-start | bytes 393220
  131.8 32.5 %copy-start.3 = (f32[1,64,512]{2,1,0:T(8,128)S(1)}, f32[1,64,512]{2,1,0:T(8,128)}, u32[]{:S(2)}) copy-start(f32[1,64,512]{2,1,0:T(8,128)} %param.15) | copy-start | bytes 393220
  131.8 32.5 %copy-start.5 = (f32[1,16,2048]{2,1,0:T(8,128)S(1)}, f32[1,16,2048]{2,1,0:T(8,128)}, u32[]{:S(2)}) copy-start(f32[1,16,2048]{2,1,0:T(8,128)} %param.16) | copy-start | bytes 393220
  131.8 32.5 %copy-start.6 = (f32[1,64,512]{2,1,0:T(8,128)S(1)}, f32[1,64,512]{2,1,0:T(8,128)}, u32[]{:S(2)}) copy-start(f32[1,64,512]{2,1,0:T(8,128)} %param.17) | copy-start | bytes 393220
  131.8 32.5 %copy-start.7 = (f32[1,64,512]{2,1,0:T(8,128)S(1)}, f32[1,64,512]{2,1,0:T(8,128)}, u32[]{:S(2)}) copy-start(f32[1,64,512]{2,1,0:T(8,128)} %param.18) | copy-start | bytes 393220
  131.8 32.5 %copy-start.8 = (f32[1,16,2048]{2,1,0:T(8,128)S(1)}, f32[1,16,2048]{2,1,0:T(8,128)}, u32[]{:S(2)}) copy-start(f32[1,16,2048]{2,1,0:T(8,128)} %param.19) | copy-start | bytes 393220
  141.8 6.4 %collective-permute-start.23 = (f32[3,16,128]{2,1,0:T(8,128)S(1)}, f32[3,16,128]{2,1,0:T(8,128)S(1)}, u32[]{:S(2)}, u32[]{:S(2)}) collective-permute-start(f32[3,16,128]{2,1,0:T(8,128)S(1)} %gram.1), channel_id=1, source_target_pairs={{0,6},{1,7},{2,0},{3,1},{4,2},{5,3},{6,4},{7,5},{8,14},{9,15},{10,... | collective-permute-start | bytes 73736 | tf_op jit(solution)/shard_map/ppermute | solution.py:338
  146.2 3.9 %collective-permute-start.22 = (f32[3,16,128]{2,1,0:T(8,128)S(1)}, f32[3,16,128]{2,1,0:T(8,128)S(1)}, u32[]{:S(2)}, u32[]{:S(2)}) collective-permute-start(f32[3,16,128]{2,1,0:T(8,128)S(1)} %gram.1), channel_id=1, source_target_pairs={{0,2},{1,3},{2,4},{3,5},{4,6},{5,7},{6,0},{7,1},{8,10},{9,11},{10,... | collective-permute-start | bytes 73736 | tf_op jit(solution)/shard_map/ppermute | solution.py:338
  146.2 4.2 %collective-permute-start.21 = (f32[3,16,128]{2,1,0:T(8,128)S(1)}, f32[3,16,128]{2,1,0:T(8,128)S(1)}, u32[]{:S(2)}, u32[]{:S(2)}) collective-permute-start(f32[3,16,128]{2,1,0:T(8,128)S(1)} %gram.1), channel_id=1, source_target_pairs={{0,4},{1,5},{2,6},{3,7},{4,0},{5,1},{6,2},{7,3},{8,12},{9,13},{10,... | collective-permute-start | bytes 73736 | tf_op jit(solution)/shard_map/ppermute | solution.py:338
  150.4 7.1 %collective-permute-start.26 = (f32[3,16,128]{2,1,0:T(8,128)S(1)}, f32[3,16,128]{2,1,0:T(8,128)S(1)}, u32[]{:S(2)}, u32[]{:S(2)}) collective-permute-start(f32[3,16,128]{2,1,0:T(8,128)S(1)} %add_add_fusion.1), channel_id=1, source_target_pairs={{0,24},{1,25},{2,26},{3,27},{4,28},{5,29},{6,30},{7,31},{8,0},{9,1... | collective-permute-start | bytes 73736 | tf_op jit(solution)/shard_map/ppermute | solution.py:338
  153.2 4.3 %collective-permute-start.25 = (f32[3,16,128]{2,1,0:T(8,128)S(1)}, f32[3,16,128]{2,1,0:T(8,128)S(1)}, u32[]{:S(2)}, u32[]{:S(2)}) collective-permute-start(f32[3,16,128]{2,1,0:T(8,128)S(1)} %add_add_fusion.1), channel_id=1, source_target_pairs={{0,8},{1,9},{2,10},{3,11},{4,12},{5,13},{6,14},{7,15},{8,16},{9,17... | collective-permute-start | bytes 73736 | tf_op jit(solution)/shard_map/ppermute | solution.py:338
  153.2 5.8 %collective-permute-start.24 = (f32[3,16,128]{2,1,0:T(8,128)S(1)}, f32[3,16,128]{2,1,0:T(8,128)S(1)}, u32[]{:S(2)}, u32[]{:S(2)}) collective-permute-start(f32[3,16,128]{2,1,0:T(8,128)S(1)} %add_add_fusion.1), channel_id=1, source_target_pairs={{0,16},{1,17},{2,18},{3,19},{4,20},{5,21},{6,22},{7,23},{8,24},{9,... | collective-permute-start | bytes 73736 | tf_op jit(solution)/shard_map/ppermute | solution.py:338
  159.0 5.3 %collective-permute-start.27 = (f32[3,16,128]{2,1,0:T(8,128)S(1)}, f32[3,16,128]{2,1,0:T(8,128)S(1)}, u32[]{:S(2)}, u32[]{:S(2)}) collective-permute-start(f32[3,16,128]{2,1,0:T(8,128)S(1)} %add_add_fusion), channel_id=1, source_target_pairs={{0,1},{1,0},{2,3},{3,2},{4,5},{5,4},{6,7},{7,6},{8,9},{9,8},{10,11... | collective-permute-start | bytes 73736 | tf_op jit(solution)/shard_map/ppermute | solution.py:338

commit v6 on v5

--- a/solution.py
+++ b/solution.py
@@ -213,9 +213,7 @@
 
 
 def pair_merge(own, other, mine, theirs):
-    step = 4
-
-    def body(a_ref, b_ref, m_ref, t_ref, out):
+    def body(a_ref, b_ref, m_ref, t_ref, *out):
         coefs = []
         for m in range(3):
             inner = jnp.sum(m_ref[3 * m] + t_ref[3 * m], keepdims=True)
@@ -224,48 +222,65 @@
             coef_a = 1.0 - inner / (2.0 * (norm_a + epsilon))
             coef_b = 1.0 - inner / (2.0 * (norm_b + epsilon))
             coefs.append((jnp.broadcast_to(coef_a, (64, SLICE)), jnp.broadcast_to(coef_b, (64, SLICE))))
-
-        for i in range(step):
-            q = pl.program_id(0) * step + i
-            for m in range(3):
-                rows = slice(64 * m, 64 * (m + 1))
-                a, b = a_ref[q, rows, :].astype(F32), b_ref[q, rows, :].astype(F32)
-                out[i, rows, :] = (coefs[m][0] * a + coefs[m][1] * b).astype(BF16)
-
-    return pl.pallas_call(
-        body,
-        name="pair_merge",
-        grid=(N_CHIP // step,),
-        out_shape=struct((N_CHIP, ROWS, SLICE), BF16),
-        in_specs=[vmem()] * 4,
-        out_specs=pl.BlockSpec((step, ROWS, SLICE), lambda i: (i, 0, 0)),
-        compiler_params=pltpu.CompilerParams(vmem_limit_bytes=20 * MIB),
-        cost_estimate=pl.CostEstimate(flops=9 * 2**20, bytes_accessed=9 * MIB, transcendentals=0),
-    )(own, other, mine, theirs)
+        c, at = place(0)
+
+        @pl.loop(0, 4)
+        def _(j):
+            for k in range(4):
+                first = lax.rem(at + k, 4)
+                q = jnp.where(c == 0, 4 * j + first, 4 * first + j)
+                for m in range(3):
+                    rows = slice(64 * m, 64 * (m + 1))
+                    a, b = a_ref[q, rows, :].astype(F32), b_ref[q, rows, :].astype(F32)
+                    out[k][j, rows, :] = (coefs[m][0] * a + coefs[m][1] * b).astype(BF16)
+
+    return call(body, "pair_merge", 4, [struct((4, ROWS, SLICE), BF16)] * 4, 9 * 2**20, 9 * MIB)(
+        own, other, mine, theirs
+    )
+
+
+def turn_over(parts):
+    def body(*refs):
+        (_, first), (_, second) = place(0), place(1)
+        for k in range(4):
+            for m in range(4):
+                refs[4 + k][lax.rem(first + 4 - m, 4)] = refs[m][lax.rem(second + k, 4)]
+
+    return call(body, "turn_over", 4, [struct((4, ROWS, SLICE), BF16)] * 4, 2**10, 6 * MIB)(*parts)
+
+
+def origin(index):
+    c, second = place(1)
+    other = (second + 4 - (index >> 2)) & 3
+    return jnp.where(c == 0, other * 4 + (index & 3), (index & 3) * 4 + other)
 
 
 def gram(parts):
-    def body(x, out):
+    def body(*refs):
+        x, out = refs[:4], refs[4]
         row = lax.broadcasted_iota(jnp.int32, (256, 256), 0)
         col = lax.broadcasted_iota(jnp.int32, (256, 256), 1)
         same = jnp.where(row % 16 == col % 16, 1.0, 0.0)
-        fold = lax.broadcasted_iota(jnp.int32, (256, 128), 0) // 16
+        fold = origin(lax.broadcasted_iota(jnp.int32, (256, 128), 0) // 16)
         fold = jnp.where(fold == lax.broadcasted_iota(jnp.int32, (256, 128), 1), 1.0, 0.0)
+        order = origin(lax.broadcasted_iota(jnp.int32, (16, 16), 1))
+        order = jnp.where(order == lax.broadcasted_iota(jnp.int32, (16, 16), 0), 1.0, 0.0)
+        exact = dict(precision=lax.Precision.HIGHEST, preferred_element_type=F32)
         for m in range(3):
             acc = None
             for b in range(4):
                 at = 64 * m + 16 * b
-                block = x[:, at : at + 16, :].reshape(256, SLICE)
+                block = jnp.concatenate([r[:, at : at + 16, :].reshape(64, SLICE) for r in x], axis=0)
                 part = lax.dot_general(block, block, NT, preferred_element_type=F32)
                 acc = part if acc is None else acc + part
             acc = jnp.sum((acc * same).reshape(16, 16, 256), axis=1)
-            out[m] = jnp.dot(acc, fold, precision=lax.Precision.HIGHEST, preferred_element_type=F32)
-
-    return call(body, "gram", 1, struct((3, 16, 128), F32), 12 * 2 * 256 * 256 * 512, 3 * MIB)(parts)
+            out[m] = jnp.dot(order, jnp.dot(acc, fold, **exact), **exact)
+
+    return call(body, "gram", 4, struct((3, 16, 128), F32), 12 * 2 * 256 * 256 * 512, 3 * MIB)(*parts)
 
 
 def finish(parts, products, gate, up, down, mom_gate, mom_up, mom_down):
-    def body(x, g_ref, gate_w, up_w, down_w, gate_m, up_m, down_m, new_g, new_u, new_d, next_g, next_u, next_d):
+    def body(x0, x1, x2, x3, g_ref, gate_w, up_w, down_w, gate_m, up_m, down_m, new_g, new_u, new_d, next_g, next_u, next_d):
         g = g_ref[...]
         i = lax.broadcasted_iota(jnp.int32, (3, 16, 128), 1)
         j = lax.broadcasted_iota(jnp.int32, (3, 16, 128), 2)
@@ -284,12 +299,16 @@
                 return 1.0 - inner / (2.0 * (jnp.maximum(norm, 0.0) + epsilon))
 
             c_col, c_row = c_col * coef(2), c_row * coef(1)
+        chip = origin(lax.broadcasted_iota(jnp.int32, (16, 128), 0))
+        chip = chip == lax.broadcasted_iota(jnp.int32, (16, 128), 1)
+        c_col = jnp.sum(jnp.where(chip, c_row, 0.0), axis=2, keepdims=True)
         olds = ((gate_w, gate_m, new_g, next_g), (up_w, up_m, new_u, next_u))
         for m in range(3):
             merged = jnp.zeros((64, SLICE), F32)
             for q in range(16):
                 scale = jnp.broadcast_to(c_col[m, q : q + 1, :], (64, SLICE))
-                merged += scale * x[q, 64 * m : 64 * (m + 1), :].astype(F32)
+                x = (x0, x1, x2, x3)[q // 4]
+                merged += scale * x[q % 4, 64 * m : 64 * (m + 1), :].astype(F32)
             if m < 2:
                 w, mom, new, after = olds[m]
                 step = momentum_decay * mom[...] + merged
@@ -303,8 +322,8 @@
                     new_d[:, cols] = down_w[:, cols] - learning_rate * step
 
     wide, tall = struct((64, H), F32), struct((16, D), F32)
-    return call(body, "finish", 8, [wide, wide, tall, wide, wide, tall], 2**22, 6 * MIB)(
-        parts, products, gate, up, down, mom_gate, mom_up, mom_down
+    return call(body, "finish", 11, [wide, wide, tall, wide, wide, tall], 2**22, 6 * MIB)(
+        *parts, products, gate, up, down, mom_gate, mom_up, mom_down
     )
 
 
@@ -486,16 +505,17 @@
     keep, send, both = backward(cots, route_weights, hidden_t, gate_factor, act, xt, weights)
     received = other_core(send)
     slots = slot_gradients(both, weights)
+    received, slots = lax.optimization_barrier((received, slots))
+
+    mine = pair_moments(keep, received)
+    sent = pair_merge(keep, received, mine, other_core(mine))
+    parts = [sent[0]] + [shift(sent[k], "dp", along(0, k)) for k in (1, 2, 3)]
     back = [slots[0]] + [around_y(slots[k], N_EXPERT - k) for k in (1, 2, 3)]
-    received, _ = lax.optimization_barrier((received, slots))
-
-    mine = pair_moments(keep, received)
-    merged = pair_merge(keep, received, mine, other_core(mine))
-    merged = pltpu.with_memory_space_constraint(merged, pltpu.HBM)
-    groups = [[2 * q + c for q in range(N_CHIP)] for c in range(2)]
-    parts = lax.all_to_all(merged, "dp", 0, 0, tiled=True, axis_index_groups=groups)
+    parts, back[1], back[3] = tie((parts, back[1], back[3]))
+    sent = turn_over(parts)
+    parts = [sent[0]] + [shift(sent[k], "dp", along(1, k)) for k in (1, 2, 3)]
     pool_grad = scatter_rows(ids, back)
-    parts, pool_grad = lax.optimization_barrier((parts, pool_grad))
+    parts, pool_grad = tie((parts, pool_grad))
     products = sum_dp(gram(parts))
     outs = finish(
         parts,

time: 168 us -> 167 us (level)
  starting transfers between devices: 56.2 us -> 67.2 us
  waiting for transfers between devices: 66.2 us -> 59.4 us
  Pallas kernels: 40.3 us -> 35.3 us
    ppermute x28 -> x34, starting transfers between devices: 50.6 us -> 67.2 us  [shift(): lax.ppermute(block, axis, [(i, to(i)) for i in range(lax.axis_size(axis))])]
    all_to_all x1 -> x0, waiting for transfers between devices: 5.98 us -> none  [local(): lax.all_to_all(merged, 'dp', 0, 0, tiled=True, axis_index_groups=groups)]
    all_to_all x1 -> x0, starting transfers between devices: 5.6 us -> none  [local(): lax.all_to_all(merged, 'dp', 0, 0, tiled=True, axis_index_groups=groups)]
    pallas_call x3 -> x4, Pallas kernels: 10.7 us -> 5.69 us  [the longest x1 2.35 us: gram(): call(body, 'gram', 4, struct((3, 16, 128), F32), 12 * 2 * 256 * 256 * 512...]
    ppermute x28 -> x34, waiting for transfers between devices: 60.3 us -> 59.4 us  [shift(): lax.ppermute(block, axis, [(i, to(i)) for i in range(lax.axis_size(axis))])]
  transfers between devices with their start and end apart: 29 -> 34, of which waited for: 17 -> 21; matrix products, arithmetic and copies ran while one was open for 0% -> 0% of each run, Pallas kernels for 14% -> 14%
where the time goes in v6:
time: 167 us
  starting transfers between devices  67.2 us (40%)
  waiting for transfers between devices  59.4 us (36%)
  Pallas kernels  35.3 us (21%)
  local copies, waits for them, and re-layouts  4.35 us (3%)
    ppermute x34, starting transfers between devices, shift(): lax.ppermute(block, axis, [(i, to(i)) for i in range(lax.axis_size(axis))])  67.2 us
    ppermute x34, waiting for transfers between devices, shift(): lax.ppermute(block, axis, [(i, to(i)) for i in range(lax.axis_size(axis))])  59.4 us
    pallas_call x7, Pallas kernels, pick_rows(): call(body, 'pick_rows', n_ids + n_pool, shapes, 2 * TOK_DEV * POOL * SLIC...  10.9 us
    pallas_call x1, Pallas kernels, scatter_rows(): pl.pallas_call(body, name='scatter_rows', grid=(POOL // block,), out_shap...  5.98 us
    pallas_call x1, Pallas kernels, backward(): call(body, 'backward', 10, shapes, 8 * TOK_DEV * D * H, 20 * MIB, [pltpu....  5.14 us
    unnamed x28, local copies, waits for them, and re-layouts  4.35 us
  transfers between devices with their start and end apart: 34, of which 21 were waited for; matrix products, arithmetic and copies ran while one was open for 0% of the time, Pallas kernels for 14%

profile of v6, /device:TPU:1, one launch (start us, length us, event | category | flops | bytes accessed | tf_op | source)
XLA Modules:
  0.0 167.2 jit_solution(13508797645548101336)
XLA Ops:
  0.6 2.2 %collective-permute-start.2 = (s32[1,512]{1,0:T(1,128)}, s32[1,512]{1,0:T(1,128)S(1)}, u32[]{:S(2)}, u32[]{:S(2)}) collective-permute-start(s32[1,512]{1,0:T(1,128)} %i0), channel_id=1, source_target_pairs={{0,32},{32,64},{64,96},{96,0},{1,33},{33,65},{65,97},{97,1},{2,34}... | collective-permute-start | bytes 6152 | tf_op jit(solution)/shard_map/ppermute | solution.py:357
  2.8 2.6 %collective-permute-start.1 = (s32[1,512]{1,0:T(1,128)}, s32[1,512]{1,0:T(1,128)S(1)}, u32[]{:S(2)}, u32[]{:S(2)}) collective-permute-start(s32[1,512]{1,0:T(1,128)} %i0), channel_id=1, source_target_pairs={{0,64},{32,96},{64,0},{96,32},{1,65},{33,97},{65,1},{97,33},{2,66}... | collective-permute-start | bytes 6152 | tf_op jit(solution)/shard_map/ppermute | solution.py:357
  9.8 1.6 copy-done.9
  11.4 1.4 pick_rows.8
  12.8 1.4 pick_rows.7
  14.7 2.3 %collective-permute-start.7 = (bf16[512,512]{1,0:T(8,128)(2,1)S(1)}, bf16[512,512]{1,0:T(8,128)(2,1)S(1)}, u32[]{:S(2)}, u32[]{:S(2)}) collective-permute-start(bf16[512,512]{1,0:T(8,128)(2,1)S(1)} %pick_rows.8), channel_id=1, source_target_pairs={{0,96},{32,0},{64,32},{96,64},{1,97},{33,1},{65,33},{97,65},{2,98}... | collective-permute-start | bytes 1572872 | tf_op jit(solution)/shard_map/ppermute | solution.py:357
  17.0 2.5 %collective-permute-start.5 = (bf16[96,1024]{1,0:T(8,128)(2,1)S(1)}, bf16[96,1024]{1,0:T(8,128)(2,1)S(1)}, u32[]{:S(2)}, u32[]{:S(2)}) collective-permute-start(bf16[96,1024]{1,0:T(8,128)(2,1)S(1)} %pack.1.refs_0_), channel_id=1, source_target_pairs={{0,6},{1,25},{2,0},{3,27},{4,2},{5,29},{6,4},{7,31},{8,14},{9,1},{... | collective-permute-start | bytes 589832 | tf_op jit(solution)/shard_map/ppermute | solution.py:357
  20.6 1.4 pick_rows.9
  22.0 1.4 pick_rows.10
  24.2 1.4 collective-permute-done.4.refs_2_
  25.6 2.3 %collective-permute-done.3.refs_1_ = bf16[96,1024]{1,0:T(8,128)(2,1)S(1)} collective-permute-done((bf16[96,1024]{1,0:T(8,128)(2,1)S(1)}, bf16[96,1024]{1,0:T(8,128)(2,1)S(1)}, u32[]{:S(2)}, u32[]{:S(2)}) %collective-permute-start.3) | collective-permute-done | bytes 196640 | tf_op jit(solution)/shard_map/ppermute | solution.py:357
  28.0 3.8 %collective-permute-start.10 = (bf16[4,96,1024]{2,1,0:T(8,128)(2,1)S(1)}, bf16[4,96,1024]{2,1,0:T(8,128)(2,1)S(1)}, u32[]{:S(2)}, u32[]{:S(2)}) collective-permute-start(bf16[4,96,1024]{2,1,0:T(8,128)(2,1)S(1)} %bundle.1.refs_0_), channel_id=1, source_target_pairs={{0,24},{1,7},{2,26},{3,1},{4,28},{5,3},{6,30},{7,5},{8,0},{9,15},{... | collective-permute-start | bytes 2359304 | tf_op jit(solution)/shard_map/ppermute | solution.py:357
  33.2 2.3 %collective-permute-start.12 = (bf16[512,512]{1,0:T(8,128)(2,1)S(1)}, bf16[512,512]{1,0:T(8,128)(2,1)S(1)}, u32[]{:S(2)}, u32[]{:S(2)}) collective-permute-start(bf16[512,512]{1,0:T(8,128)(2,1)S(1)} %pick_rows.10), channel_id=1, source_target_pairs={{0,64},{32,96},{64,0},{96,32},{1,65},{33,97},{65,1},{97,33},{2,66}... | collective-permute-start | bytes 1572872 | tf_op jit(solution)/shard_map/ppermute | solution.py:357
  35.5 1.4 pick_rows.12
  36.9 1.4 pick_rows.13
  38.4 2.5 %pick_rows.11 = (bf16[512,512]{1,0:T(8,128)(2,1)S(1)}, bf16[512,512]{1,0:T(8,128)(2,1)S(1)}) custom-call(s32[1,512]{1,0:T(1,128)S(1)} %copy-done.13, bf16[2048,512]{1,0:T(8,128)(2,1)S(1)} %copy-done.10, bf16[2048,512]{1,0:T(8,128)(2,1)S(1)} %copy-done.11), custom_call_target="tpu_custom_call" | custom-call | flops 2147483648 | bytes 3145728 | tf_op jit(solution)/shard_map/pick_rows/pallas_call | solution.py:68
  40.9 2.4 %collective-permute-done.11.x2 = bf16[512,512]{1,0:T(8,128)(2,1)S(1)} collective-permute-done((bf16[512,512]{1,0:T(8,128)(2,1)S(1)}, bf16[512,512]{1,0:T(8,128)(2,1)S(1)}, u32[]{:S(2)}, u32[]{:S(2)}) %collective-permute-start.11) | collective-permute-done | bytes 524320 | tf_op jit(solution)/shard_map/ppermute | solution.py:357
  43.3 11.2 %collective-permute-done.12.c2 = bf16[512,512]{1,0:T(8,128)(2,1)S(1)} collective-permute-done((bf16[512,512]{1,0:T(8,128)(2,1)S(1)}, bf16[512,512]{1,0:T(8,128)(2,1)S(1)}, u32[]{:S(2)}, u32[]{:S(2)}) %collective-permute-start.12) | collective-permute-done | bytes 524320 | tf_op jit(solution)/shard_map/ppermute | solution.py:357
  54.8 5.2 %collective-permute-start.15 = (bf16[16,96,1024]{2,1,0:T(8,128)(2,1)S(1)}, bf16[16,96,1024]{2,1,0:T(8,128)(2,1)S(1)}, u32[]{:S(2)}, u32[]{:S(2)}) collective-permute-start(bf16[16,96,1024]{2,1,0:T(8,128)(2,1)S(1)} %half_of_weights.1.a), channel_id=1, source_target_pairs={{0,1},{1,0},{2,3},{3,2},{4,5},{5,4},{6,7},{7,6},{8,9},{9,8},{10,11... | collective-permute-start | bytes 9437192 | tf_op jit(solution)/shard_map/ppermute | solution.py:357
  60.0 2.7 %collective-permute-start.14 = (bf16[512,512]{1,0:T(8,128)(2,1)S(1)}, bf16[512,512]{1,0:T(8,128)(2,1)S(1)}, u32[]{:S(2)}, u32[]{:S(2)}) collective-permute-start(bf16[512,512]{1,0:T(8,128)(2,1)S(1)} %pick_rows.13), channel_id=1, source_target_pairs={{0,96},{32,0},{64,32},{96,64},{1,97},{33,1},{65,33},{97,65},{2,98}... | collective-permute-start | bytes 1572872 | tf_op jit(solution)/shard_map/ppermute | solution.py:357
  62.7 2.6 %collective-permute-done.15.b = bf16[16,96,1024]{2,1,0:T(8,128)(2,1)S(1)} collective-permute-done((bf16[16,96,1024]{2,1,0:T(8,128)(2,1)S(1)}, bf16[16,96,1024]{2,1,0:T(8,128)(2,1)S(1)}, u32[]{:S(2)}, u32[]{:S(2)}) %collective-permute-start.15) | collective-permute-done | bytes 3145760 | tf_op jit(solution)/shard_map/ppermute | solution.py:357
  65.7 3.0 %forward.1 = (bf16[512,512]{1,0:T(8,128)(2,1)S(1)}, f32[512,512]{1,0:T(8,128)S(1)}, f32[512,512]{1,0:T(8,128)S(1)}, bf16[4,512,512]{2,1,0:T(8,128)(2,1)S(1)}) custom-call(bf16[512,512]{1,0:T(8,128)(2,1)S(1)} %get-tuple-element.102.x0, bf16[512,512]{1,0:T(8,128)(2,1)S(1)} %collective-permute-done.6.x1, bf16[512,512]{1,0:T(8,128)(2,1)S(1)} %collective-permute-done.11.x2, ...), custom_call_target="tpu_custom_call" | custom-call | flops 2147483648 | bytes 10485760 | tf_op jit(solution)/shard_map/forward/pallas_call | solution.py:122
  68.8 5.9 %collective-permute-done.13.c1 = bf16[512,512]{1,0:T(8,128)(2,1)S(1)} collective-permute-done((bf16[512,512]{1,0:T(8,128)(2,1)S(1)}, bf16[512,512]{1,0:T(8,128)(2,1)S(1)}, u32[]{:S(2)}, u32[]{:S(2)}) %collective-permute-start.13) | collective-permute-done | bytes 524320 | tf_op jit(solution)/shard_map/ppermute | solution.py:357
  74.7 5.1 %backward.1 = (bf16[16,192,512]{2,1,0:T(8,128)(2,1)S(1)}, bf16[16,192,512]{2,1,0:T(8,128)(2,1)S(1)}, bf16[512,1024]{1,0:T(8,128)(2,1)S(1)}) custom-call(bf16[512,512]{1,0:T(8,128)(2,1)S(1)} %get-tuple-element.98.c0, bf16[512,512]{1,0:T(8,128)(2,1)S(1)} %collective-permute-done.13.c1, bf16[512,512]{1,0:T(8,128)(2,1)S(1)} %collective-permute-done.12.c2, ...), custom_call_target="tpu_custom_call" | custom-call | flops 4294967296 | bytes 20971520 | tf_op jit(solution)/shard_map/backward/pallas_call | solution.py:175
  79.8 1.2 collective-permute-start.16
  81.0 2.4 %slot_gradients.1 = (bf16[512,512]{1,0:T(8,128)(2,1)S(1)}, bf16[512,512]{1,0:T(8,128)(2,1)S(1)}, bf16[512,512]{1,0:T(8,128)(2,1)S(1)}, bf16[512,512]{1,0:T(8,128)(2,1)S(1)}) custom-call(bf16[512,1024]{1,0:T(8,128)(2,1)S(1)} %get-tuple-element.115.both_ref, bf16[32,96,1024]{2,1,0:T(8,128)(2,1)S(1)} %whole_weights.1.w), custom_call_target="tpu_custom_call" | custom-call | flops 2147483648 | bytes 9437184 | tf_op jit(solution)/shard_map/slot_gradients/pallas_call | solution.py:193
  83.4 2.9 %collective-permute-done.16.b_ref = bf16[16,192,512]{2,1,0:T(8,128)(2,1)S(1)} collective-permute-done((bf16[16,192,512]{2,1,0:T(8,128)(2,1)S(1)}, bf16[16,192,512]{2,1,0:T(8,128)(2,1)S(1)}, u32[]{:S(2)}, u32[]{:S(2)}) %collective-permute-start.16) | collective-permute-done | bytes 3145760 | tf_op jit(solution)/shard_map/ppermute | solution.py:357
  88.4 1.3 pair_merge.1
  90.5 2.5 %collective-permute-start.19 = (bf16[4,192,512]{2,1,0:T(8,128)(2,1)S(1)}, bf16[4,192,512]{2,1,0:T(8,128)(2,1)S(1)}, u32[]{:S(2)}, u32[]{:S(2)}) collective-permute-start(bf16[4,192,512]{2,1,0:T(8,128)(2,1)S(1)} %get-tuple-element.123), channel_id=1, source_target_pairs={{0,4},{1,17},{2,6},{3,19},{4,0},{5,21},{6,2},{7,23},{8,12},{9,25},... | collective-permute-start | bytes 2359304 | tf_op jit(solution)/shard_map/ppermute | solution.py:357
  93.0 1.1 collective-permute-start.20
  94.1 2.7 %collective-permute-start.21 = (bf16[512,512]{1,0:T(8,128)(2,1)S(1)}, bf16[512,512]{1,0:T(8,128)(2,1)S(1)}, u32[]{:S(2)}, u32[]{:S(2)}) collective-permute-start(bf16[512,512]{1,0:T(8,128)(2,1)S(1)} %get-tuple-element.125), channel_id=1, source_target_pairs={{0,96},{32,0},{64,32},{96,64},{1,97},{33,1},{65,33},{97,65},{2,98}... | collective-permute-start | bytes 1572872 | tf_op jit(solution)/shard_map/ppermute | solution.py:357
  96.8 10.0 %collective-permute-done.21.g1 = bf16[512,512]{1,0:T(8,128)(2,1)S(1)} collective-permute-done((bf16[512,512]{1,0:T(8,128)(2,1)S(1)}, bf16[512,512]{1,0:T(8,128)(2,1)S(1)}, u32[]{:S(2)}, u32[]{:S(2)}) %collective-permute-start.21) | collective-permute-done | bytes 524320 | tf_op jit(solution)/shard_map/ppermute | solution.py:357
  106.8 2.2 %collective-permute-start.26 = (bf16[512,512]{1,0:T(8,128)(2,1)S(1)}, bf16[512,512]{1,0:T(8,128)(2,1)S(1)}, u32[]{:S(2)}, u32[]{:S(2)}) collective-permute-start(bf16[512,512]{1,0:T(8,128)(2,1)S(1)} %get-tuple-element.138), channel_id=1, source_target_pairs={{0,64},{32,96},{64,0},{96,32},{1,65},{33,97},{65,1},{97,33},{2,66}... | collective-permute-start | bytes 1572872 | tf_op jit(solution)/shard_map/ppermute | solution.py:357
  109.9 1.2 collective-permute-done.19.refs_2_
  111.4 2.4 %collective-permute-start.23 = (bf16[4,192,512]{2,1,0:T(8,128)(2,1)S(1)}, bf16[4,192,512]{2,1,0:T(8,128)(2,1)S(1)}, u32[]{:S(2)}, u32[]{:S(2)}) collective-permute-start(bf16[4,192,512]{2,1,0:T(8,128)(2,1)S(1)} %get-tuple-element.132), channel_id=1, source_target_pairs={{0,8},{1,3},{2,10},{3,5},{4,12},{5,7},{6,14},{7,1},{8,16},{9,11},{... | collective-permute-start | bytes 2359304 | tf_op jit(solution)/shard_map/ppermute | solution.py:357
  114.6 1.7 %collective-permute-start.25 = (bf16[4,192,512]{2,1,0:T(8,128)(2,1)S(1)}, bf16[4,192,512]{2,1,0:T(8,128)(2,1)S(1)}, u32[]{:S(2)}, u32[]{:S(2)}) collective-permute-start(bf16[4,192,512]{2,1,0:T(8,128)(2,1)S(1)} %get-tuple-element.134), channel_id=1, source_target_pairs={{0,24},{1,7},{2,26},{3,1},{4,28},{5,3},{6,30},{7,5},{8,0},{9,15},{... | collective-permute-start | bytes 2359304 | tf_op jit(solution)/shard_map/ppermute | solution.py:357
  116.3 3.3 %collective-permute-done.26.g2 = bf16[512,512]{1,0:T(8,128)(2,1)S(1)} collective-permute-done((bf16[512,512]{1,0:T(8,128)(2,1)S(1)}, bf16[512,512]{1,0:T(8,128)(2,1)S(1)}, u32[]{:S(2)}, u32[]{:S(2)}) %collective-permute-start.26) | collective-permute-done | bytes 524320 | tf_op jit(solution)/shard_map/ppermute | solution.py:357
  119.7 6.0 %scatter_rows.1 = f32[2048,512]{1,0:T(8,128)} custom-call(s32[1,512]{1,0:T(1,128)S(1)} %copy-done.13, s32[1,512]{1,0:T(1,128)S(1)} %collective-permute-done.refs_0_.i1, s32[1,512]{1,0:T(1,128)S(1)} %collective-permute-done.1.refs_0_.i2, s32[1,512]{1,0:T(1,128)S(1)} %collective-permute-done.2.refs_0_.i3, bf16[512,512]{1,0:T(8,128)(2,1)S(1)} %get-tuple-element.136.g0, ...), custom_call_target="tpu_custom_call" | custom-call | flops 4294967296 | bytes 6291456 | tf_op jit(solution)/shard_map/scatter_rows/pallas_call | solution.py:342
  125.7 6.7 %collective-permute-done.24.refs_2_.x2 = bf16[4,192,512]{2,1,0:T(8,128)(2,1)S(1)} collective-permute-done((bf16[4,192,512]{2,1,0:T(8,128)(2,1)S(1)}, bf16[4,192,512]{2,1,0:T(8,128)(2,1)S(1)}, u32[]{:S(2)}, u32[]{:S(2)}) %collective-permute-start.24) | collective-permute-done | bytes 786464 | tf_op jit(solution)/shard_map/ppermute | solution.py:357
  132.9 2.3 %gram.1 = f32[3,16,128]{2,1,0:T(8,128)S(1)} custom-call(bf16[4,192,512]{2,1,0:T(8,128)(2,1)S(1)} %get-tuple-element.140.refs_0_.x0, bf16[4,192,512]{2,1,0:T(8,128)(2,1)S(1)} %collective-permute-done.23.refs_1_.x1, bf16[4,192,512]{2,1,0:T(8,128)(2,1)S(1)} %collective-permute-done.24.refs_2_.x2, bf16[4,192,512]{2,1,0:T(8,128)(2,1)S(1)} %collective-permute-done.25.refs_3_.x3), custom_call_target="tpu_custom_call" | custom-call | flops 805306368 | bytes 3145728 | tf_op jit(solution)/shard_map/gram/pallas_call | solution.py:279
  135.2 2.4 %collective-permute-start.29 = (f32[3,16,128]{2,1,0:T(8,128)S(1)}, f32[3,16,128]{2,1,0:T(8,128)S(1)}, u32[]{:S(2)}, u32[]{:S(2)}) collective-permute-start(f32[3,16,128]{2,1,0:T(8,128)S(1)} %gram.1), channel_id=1, source_target_pairs={{0,6},{1,7},{2,0},{3,1},{4,2},{5,3},{6,4},{7,5},{8,14},{9,15},{10,... | collective-permute-start | bytes 73736 | tf_op jit(solution)/shard_map/ppermute | solution.py:357
  137.6 1.9 %collective-permute-start.27 = (f32[3,16,128]{2,1,0:T(8,128)S(1)}, f32[3,16,128]{2,1,0:T(8,128)S(1)}, u32[]{:S(2)}, u32[]{:S(2)}) collective-permute-start(f32[3,16,128]{2,1,0:T(8,128)S(1)} %gram.1), channel_id=1, source_target_pairs={{0,4},{1,5},{2,6},{3,7},{4,0},{5,1},{6,2},{7,3},{8,12},{9,13},{10,... | collective-permute-start | bytes 73736 | tf_op jit(solution)/shard_map/ppermute | solution.py:357
  139.5 2.3 %collective-permute-done.28 = f32[3,16,128]{2,1,0:T(8,128)S(1)} collective-permute-done((f32[3,16,128]{2,1,0:T(8,128)S(1)}, f32[3,16,128]{2,1,0:T(8,128)S(1)}, u32[]{:S(2)}, u32[]{:S(2)}) %collective-permute-start.28) | collective-permute-done | bytes 24608 | tf_op jit(solution)/shard_map/ppermute | solution.py:357
  142.1 2.1 %collective-permute-start.32 = (f32[3,16,128]{2,1,0:T(8,128)S(1)}, f32[3,16,128]{2,1,0:T(8,128)S(1)}, u32[]{:S(2)}, u32[]{:S(2)}) collective-permute-start(f32[3,16,128]{2,1,0:T(8,128)S(1)} %add_add_fusion.1), channel_id=1, source_target_pairs={{0,24},{1,25},{2,26},{3,27},{4,28},{5,29},{6,30},{7,31},{8,0},{9,1... | collective-permute-start | bytes 73736 | tf_op jit(solution)/shard_map/ppermute | solution.py:357
  144.2 1.3 collective-permute-start.30
  145.5 2.6 %collective-permute-done.31 = f32[3,16,128]{2,1,0:T(8,128)S(1)} collective-permute-done((f32[3,16,128]{2,1,0:T(8,128)S(1)}, f32[3,16,128]{2,1,0:T(8,128)S(1)}, u32[]{:S(2)}, u32[]{:S(2)}) %collective-permute-start.31) | collective-permute-done | bytes 24608 | tf_op jit(solution)/shard_map/ppermute | solution.py:357
  148.4 16.0 %collective-permute-start.33 = (f32[3,16,128]{2,1,0:T(8,128)S(1)}, f32[3,16,128]{2,1,0:T(8,128)S(1)}, u32[]{:S(2)}, u32[]{:S(2)}) collective-permute-start(f32[3,16,128]{2,1,0:T(8,128)S(1)} %add_add_fusion), channel_id=1, source_target_pairs={{0,1},{1,0},{2,3},{3,2},{4,5},{5,4},{6,7},{7,6},{8,9},{9,8},{10,11... | collective-permute-start | bytes 73736 | tf_op jit(solution)/shard_map/ppermute | solution.py:357
  165.3 1.9 %finish.1 = (f32[64,512]{1,0:T(8,128)}, f32[64,512]{1,0:T(8,128)}, f32[16,2048]{1,0:T(8,128)}, f32[64,512]{1,0:T(8,128)}, f32[64,512]{1,0:T(8,128)}, /*index=5*/f32[16,2048]{1,0:T(8,128)}) custom-call(bf16[4,192,512]{2,1,0:T(8,128)(2,1)S(1)} %get-tuple-element.140.refs_0_.x0, bf16[4,192,512]{2,1,0:T(8,128)(2,1)S(1)} %collective-permute-done.23.refs_1_.x1, ...), custom_call_target="tpu_custom_call" | custom-call | flops 4194304 | bytes 6291456 | tf_op jit(solution)/shard_map/finish/pallas_call | solution.py:325
  (71 shorter events, 15.8 us)
Async XLA Ops:
  0.6 9.1 %collective-permute-start.2 = (s32[1,512]{1,0:T(1,128)}, s32[1,512]{1,0:T(1,128)S(1)}, u32[]{:S(2)}, u32[]{:S(2)}) collective-permute-start(s32[1,512]{1,0:T(1,128)} %i0), channel_id=1, source_target_pairs={{0,32},{32,64},{64,96},{96,0},{1,33},{33,65},{65,97},{97,1},{2,34}... | collective-permute-start | bytes 6152 | tf_op jit(solution)/shard_map/ppermute | solution.py:357
  2.8 11.4 %collective-permute-start.1 = (s32[1,512]{1,0:T(1,128)}, s32[1,512]{1,0:T(1,128)S(1)}, u32[]{:S(2)}, u32[]{:S(2)}) collective-permute-start(s32[1,512]{1,0:T(1,128)} %i0), channel_id=1, source_target_pairs={{0,64},{32,96},{64,0},{96,32},{1,65},{33,97},{65,1},{97,33},{2,66}... | collective-permute-start | bytes 6152 | tf_op jit(solution)/shard_map/ppermute | solution.py:357
  5.4 7.3 %collective-permute-start = (s32[1,512]{1,0:T(1,128)}, s32[1,512]{1,0:T(1,128)S(1)}, u32[]{:S(2)}, u32[]{:S(2)}) collective-permute-start(s32[1,512]{1,0:T(1,128)} %i0), channel_id=1, source_target_pairs={{0,96},{32,0},{64,32},{96,64},{1,97},{33,1},{65,33},{97,65},{2,98}... | collective-permute-start | bytes 6152 | tf_op jit(solution)/shard_map/ppermute | solution.py:357
  6.5 0.9 copy-start
  7.4 0.9 copy-start.2
  8.3 0.9 copy-start.4
  9.8 1.6 copy-start.9
  12.8 9.2 %copy-start.11 = (bf16[2048,512]{1,0:T(8,128)(2,1)S(1)}, bf16[2048,512]{1,0:T(8,128)(2,1)}, u32[]{:S(2)}) copy-start(bf16[2048,512]{1,0:T(8,128)(2,1)} %refs_1_.13) | copy-start | bytes 6291460
  14.2 13.7 %collective-permute-start.6 = (bf16[512,512]{1,0:T(8,128)(2,1)S(1)}, bf16[512,512]{1,0:T(8,128)(2,1)S(1)}, u32[]{:S(2)}, u32[]{:S(2)}) collective-permute-start(bf16[512,512]{1,0:T(8,128)(2,1)S(1)} %pick_rows.7), channel_id=1, source_target_pairs={{0,32},{32,64},{64,96},{96,0},{1,33},{33,65},{65,97},{97,1},{2,34}... | collective-permute-start | bytes 1572872 | tf_op jit(solution)/shard_map/ppermute | solution.py:357
  14.7 13.2 %collective-permute-start.7 = (bf16[512,512]{1,0:T(8,128)(2,1)S(1)}, bf16[512,512]{1,0:T(8,128)(2,1)S(1)}, u32[]{:S(2)}, u32[]{:S(2)}) collective-permute-start(bf16[512,512]{1,0:T(8,128)(2,1)S(1)} %pick_rows.8), channel_id=1, source_target_pairs={{0,96},{32,0},{64,32},{96,64},{1,97},{33,1},{65,33},{97,65},{2,98}... | collective-permute-start | bytes 1572872 | tf_op jit(solution)/shard_map/ppermute | solution.py:357
  17.0 7.2 %collective-permute-start.5 = (bf16[96,1024]{1,0:T(8,128)(2,1)S(1)}, bf16[96,1024]{1,0:T(8,128)(2,1)S(1)}, u32[]{:S(2)}, u32[]{:S(2)}) collective-permute-start(bf16[96,1024]{1,0:T(8,128)(2,1)S(1)} %pack.1.refs_0_), channel_id=1, source_target_pairs={{0,6},{1,25},{2,0},{3,27},{4,2},{5,29},{6,4},{7,31},{8,14},{9,1},{... | collective-permute-start | bytes 589832 | tf_op jit(solution)/shard_map/ppermute | solution.py:357
  19.4 6.1 %collective-permute-start.4 = (bf16[96,1024]{1,0:T(8,128)(2,1)S(1)}, bf16[96,1024]{1,0:T(8,128)(2,1)S(1)}, u32[]{:S(2)}, u32[]{:S(2)}) collective-permute-start(bf16[96,1024]{1,0:T(8,128)(2,1)S(1)} %pack.1.refs_0_), channel_id=1, source_target_pairs={{0,4},{1,17},{2,6},{3,19},{4,0},{5,21},{6,2},{7,23},{8,12},{9,25},... | collective-permute-start | bytes 589832 | tf_op jit(solution)/shard_map/ppermute | solution.py:357
  20.0 7.9 %collective-permute-start.3 = (bf16[96,1024]{1,0:T(8,128)(2,1)S(1)}, bf16[96,1024]{1,0:T(8,128)(2,1)S(1)}, u32[]{:S(2)}, u32[]{:S(2)}) collective-permute-start(bf16[96,1024]{1,0:T(8,128)(2,1)S(1)} %pack.1.refs_0_), channel_id=1, source_target_pairs={{0,2},{1,9},{2,4},{3,11},{4,6},{5,13},{6,0},{7,15},{8,10},{9,17},{... | collective-permute-start | bytes 589832 | tf_op jit(solution)/shard_map/ppermute | solution.py:357
  28.0 10.4 %copy-start.10 = (bf16[2048,512]{1,0:T(8,128)(2,1)S(1)}, bf16[2048,512]{1,0:T(8,128)(2,1)}, u32[]{:S(2)}) copy-start(bf16[2048,512]{1,0:T(8,128)(2,1)} %refs_1_.11) | copy-start | bytes 6291460
  28.0 10.4 %copy-start.13 = (s32[1,512]{1,0:T(1,128)S(1)}, s32[1,512]{1,0:T(1,128)}, u32[]{:S(2)}) copy-start(s32[1,512]{1,0:T(1,128)} %i0) | copy-start | bytes 6148
  28.0 26.5 %collective-permute-start.10 = (bf16[4,96,1024]{2,1,0:T(8,128)(2,1)S(1)}, bf16[4,96,1024]{2,1,0:T(8,128)(2,1)S(1)}, u32[]{:S(2)}, u32[]{:S(2)}) collective-permute-start(bf16[4,96,1024]{2,1,0:T(8,128)(2,1)S(1)} %bundle.1.refs_0_), channel_id=1, source_target_pairs={{0,24},{1,7},{2,26},{3,1},{4,28},{5,3},{6,30},{7,5},{8,0},{9,15},{... | collective-permute-start | bytes 2359304 | tf_op jit(solution)/shard_map/ppermute | solution.py:357
  31.8 22.7 %collective-permute-start.9 = (bf16[4,96,1024]{2,1,0:T(8,128)(2,1)S(1)}, bf16[4,96,1024]{2,1,0:T(8,128)(2,1)S(1)}, u32[]{:S(2)}, u32[]{:S(2)}) collective-permute-start(bf16[4,96,1024]{2,1,0:T(8,128)(2,1)S(1)} %bundle.1.refs_0_), channel_id=1, source_target_pairs={{0,16},{1,5},{2,18},{3,7},{4,20},{5,1},{6,22},{7,3},{8,24},{9,13},... | collective-permute-start | bytes 2359304 | tf_op jit(solution)/shard_map/ppermute | solution.py:357
  31.8 22.7 %collective-permute-start.8 = (bf16[4,96,1024]{2,1,0:T(8,128)(2,1)S(1)}, bf16[4,96,1024]{2,1,0:T(8,128)(2,1)S(1)}, u32[]{:S(2)}, u32[]{:S(2)}) collective-permute-start(bf16[4,96,1024]{2,1,0:T(8,128)(2,1)S(1)} %bundle.1.refs_0_), channel_id=1, source_target_pairs={{0,8},{1,3},{2,10},{3,5},{4,12},{5,7},{6,14},{7,1},{8,16},{9,11},{... | collective-permute-start | bytes 2359304 | tf_op jit(solution)/shard_map/ppermute | solution.py:357
  32.5 10.7 %collective-permute-start.11 = (bf16[512,512]{1,0:T(8,128)(2,1)S(1)}, bf16[512,512]{1,0:T(8,128)(2,1)S(1)}, u32[]{:S(2)}, u32[]{:S(2)}) collective-permute-start(bf16[512,512]{1,0:T(8,128)(2,1)S(1)} %pick_rows.9), channel_id=1, source_target_pairs={{0,64},{32,96},{64,0},{96,32},{1,65},{33,97},{65,1},{97,33},{2,66}... | collective-permute-start | bytes 1572872 | tf_op jit(solution)/shard_map/ppermute | solution.py:357
  33.2 21.3 %collective-permute-start.12 = (bf16[512,512]{1,0:T(8,128)(2,1)S(1)}, bf16[512,512]{1,0:T(8,128)(2,1)S(1)}, u32[]{:S(2)}, u32[]{:S(2)}) collective-permute-start(bf16[512,512]{1,0:T(8,128)(2,1)S(1)} %pick_rows.10), channel_id=1, source_target_pairs={{0,64},{32,96},{64,0},{96,32},{1,65},{33,97},{65,1},{97,33},{2,66}... | collective-permute-start | bytes 1572872 | tf_op jit(solution)/shard_map/ppermute | solution.py:357
  54.8 10.5 %collective-permute-start.15 = (bf16[16,96,1024]{2,1,0:T(8,128)(2,1)S(1)}, bf16[16,96,1024]{2,1,0:T(8,128)(2,1)S(1)}, u32[]{:S(2)}, u32[]{:S(2)}) collective-permute-start(bf16[16,96,1024]{2,1,0:T(8,128)(2,1)S(1)} %half_of_weights.1.a), channel_id=1, source_target_pairs={{0,1},{1,0},{2,3},{3,2},{4,5},{5,4},{6,7},{7,6},{8,9},{9,8},{10,11... | collective-permute-start | bytes 9437192 | tf_op jit(solution)/shard_map/ppermute | solution.py:357
  60.0 14.7 %collective-permute-start.13 = (bf16[512,512]{1,0:T(8,128)(2,1)S(1)}, bf16[512,512]{1,0:T(8,128)(2,1)S(1)}, u32[]{:S(2)}, u32[]{:S(2)}) collective-permute-start(bf16[512,512]{1,0:T(8,128)(2,1)S(1)} %pick_rows.12), channel_id=1, source_target_pairs={{0,32},{32,64},{64,96},{96,0},{1,33},{33,65},{65,97},{97,1},{2,34}... | collective-permute-start | bytes 1572872 | tf_op jit(solution)/shard_map/ppermute | solution.py:357
  60.0 14.7 %collective-permute-start.14 = (bf16[512,512]{1,0:T(8,128)(2,1)S(1)}, bf16[512,512]{1,0:T(8,128)(2,1)S(1)}, u32[]{:S(2)}, u32[]{:S(2)}) collective-permute-start(bf16[512,512]{1,0:T(8,128)(2,1)S(1)} %pick_rows.13), channel_id=1, source_target_pairs={{0,96},{32,0},{64,32},{96,64},{1,97},{33,1},{65,33},{97,65},{2,98}... | collective-permute-start | bytes 1572872 | tf_op jit(solution)/shard_map/ppermute | solution.py:357
  65.7 9.0 %copy-start.12 = (f32[1,512]{1,0:T(1,128)S(1)}, f32[1,512]{1,0:T(1,128)}, u32[]{:S(2)}) copy-start(f32[1,512]{1,0:T(1,128)} %route_ref.1) | copy-start | bytes 6148
  79.8 6.5 %collective-permute-start.16 = (bf16[16,192,512]{2,1,0:T(8,128)(2,1)S(1)}, bf16[16,192,512]{2,1,0:T(8,128)(2,1)S(1)}, u32[]{:S(2)}, u32[]{:S(2)}) collective-permute-start(bf16[16,192,512]{2,1,0:T(8,128)(2,1)S(1)} %get-tuple-element.114), channel_id=1, source_target_pairs={{0,1},{1,0},{2,3},{3,2},{4,5},{5,4},{6,7},{7,6},{8,9},{9,8},{10,11... | collective-permute-start | bytes 9437192 | tf_op jit(solution)/shard_map/ppermute | solution.py:357
  87.1 1.3 collective-permute-start.17
  89.7 20.2 %collective-permute-start.18 = (bf16[4,192,512]{2,1,0:T(8,128)(2,1)S(1)}, bf16[4,192,512]{2,1,0:T(8,128)(2,1)S(1)}, u32[]{:S(2)}, u32[]{:S(2)}) collective-permute-start(bf16[4,192,512]{2,1,0:T(8,128)(2,1)S(1)} %get-tuple-element.122), channel_id=1, source_target_pairs={{0,2},{1,9},{2,4},{3,11},{4,6},{5,13},{6,0},{7,15},{8,10},{9,17},{... | collective-permute-start | bytes 2359304 | tf_op jit(solution)/shard_map/ppermute | solution.py:357
  90.5 20.6 %collective-permute-start.19 = (bf16[4,192,512]{2,1,0:T(8,128)(2,1)S(1)}, bf16[4,192,512]{2,1,0:T(8,128)(2,1)S(1)}, u32[]{:S(2)}, u32[]{:S(2)}) collective-permute-start(bf16[4,192,512]{2,1,0:T(8,128)(2,1)S(1)} %get-tuple-element.123), channel_id=1, source_target_pairs={{0,4},{1,17},{2,6},{3,19},{4,0},{5,21},{6,2},{7,23},{8,12},{9,25},... | collective-permute-start | bytes 2359304 | tf_op jit(solution)/shard_map/ppermute | solution.py:357
  93.0 18.2 %collective-permute-start.20 = (bf16[4,192,512]{2,1,0:T(8,128)(2,1)S(1)}, bf16[4,192,512]{2,1,0:T(8,128)(2,1)S(1)}, u32[]{:S(2)}, u32[]{:S(2)}) collective-permute-start(bf16[4,192,512]{2,1,0:T(8,128)(2,1)S(1)} %get-tuple-element.124), channel_id=1, source_target_pairs={{0,6},{1,25},{2,0},{3,27},{4,2},{5,29},{6,4},{7,31},{8,14},{9,1},{... | collective-permute-start | bytes 2359304 | tf_op jit(solution)/shard_map/ppermute | solution.py:357
  94.1 12.7 %collective-permute-start.21 = (bf16[512,512]{1,0:T(8,128)(2,1)S(1)}, bf16[512,512]{1,0:T(8,128)(2,1)S(1)}, u32[]{:S(2)}, u32[]{:S(2)}) collective-permute-start(bf16[512,512]{1,0:T(8,128)(2,1)S(1)} %get-tuple-element.125), channel_id=1, source_target_pairs={{0,96},{32,0},{64,32},{96,64},{1,97},{33,1},{65,33},{97,65},{2,98}... | collective-permute-start | bytes 1572872 | tf_op jit(solution)/shard_map/ppermute | solution.py:357
  96.8 13.1 %collective-permute-start.22 = (bf16[512,512]{1,0:T(8,128)(2,1)S(1)}, bf16[512,512]{1,0:T(8,128)(2,1)S(1)}, u32[]{:S(2)}, u32[]{:S(2)}) collective-permute-start(bf16[512,512]{1,0:T(8,128)(2,1)S(1)} %get-tuple-element.126), channel_id=1, source_target_pairs={{0,32},{32,64},{64,96},{96,0},{1,33},{33,65},{65,97},{97,1},{2,34}... | collective-permute-start | bytes 1572872 | tf_op jit(solution)/shard_map/ppermute | solution.py:357
  106.8 12.9 %collective-permute-start.26 = (bf16[512,512]{1,0:T(8,128)(2,1)S(1)}, bf16[512,512]{1,0:T(8,128)(2,1)S(1)}, u32[]{:S(2)}, u32[]{:S(2)}) collective-permute-start(bf16[512,512]{1,0:T(8,128)(2,1)S(1)} %get-tuple-element.138), channel_id=1, source_target_pairs={{0,64},{32,96},{64,0},{96,32},{1,65},{33,97},{65,1},{97,33},{2,66}... | collective-permute-start | bytes 1572872 | tf_op jit(solution)/shard_map/ppermute | solution.py:357
  111.4 14.3 %collective-permute-start.23 = (bf16[4,192,512]{2,1,0:T(8,128)(2,1)S(1)}, bf16[4,192,512]{2,1,0:T(8,128)(2,1)S(1)}, u32[]{:S(2)}, u32[]{:S(2)}) collective-permute-start(bf16[4,192,512]{2,1,0:T(8,128)(2,1)S(1)} %get-tuple-element.132), channel_id=1, source_target_pairs={{0,8},{1,3},{2,10},{3,5},{4,12},{5,7},{6,14},{7,1},{8,16},{9,11},{... | collective-permute-start | bytes 2359304 | tf_op jit(solution)/shard_map/ppermute | solution.py:357
  113.9 18.6 %collective-permute-start.24 = (bf16[4,192,512]{2,1,0:T(8,128)(2,1)S(1)}, bf16[4,192,512]{2,1,0:T(8,128)(2,1)S(1)}, u32[]{:S(2)}, u32[]{:S(2)}) collective-permute-start(bf16[4,192,512]{2,1,0:T(8,128)(2,1)S(1)} %get-tuple-element.133), channel_id=1, source_target_pairs={{0,16},{1,5},{2,18},{3,7},{4,20},{5,1},{6,22},{7,3},{8,24},{9,13},... | collective-permute-start | bytes 2359304 | tf_op jit(solution)/shard_map/ppermute | solution.py:357
  114.6 18.3 %collective-permute-start.25 = (bf16[4,192,512]{2,1,0:T(8,128)(2,1)S(1)}, bf16[4,192,512]{2,1,0:T(8,128)(2,1)S(1)}, u32[]{:S(2)}, u32[]{:S(2)}) collective-permute-start(bf16[4,192,512]{2,1,0:T(8,128)(2,1)S(1)} %get-tuple-element.134), channel_id=1, source_target_pairs={{0,24},{1,7},{2,26},{3,1},{4,28},{5,3},{6,30},{7,5},{8,0},{9,15},{... | collective-permute-start | bytes 2359304 | tf_op jit(solution)/shard_map/ppermute | solution.py:357
  125.7 39.6 %copy-start.1 = (f32[1,64,512]{2,1,0:T(8,128)S(1)}, f32[1,64,512]{2,1,0:T(8,128)}, u32[]{:S(2)}) copy-start(f32[1,64,512]{2,1,0:T(8,128)} %param.14) | copy-start | bytes 393220
  125.7 39.6 %copy-start.3 = (f32[1,64,512]{2,1,0:T(8,128)S(1)}, f32[1,64,512]{2,1,0:T(8,128)}, u32[]{:S(2)}) copy-start(f32[1,64,512]{2,1,0:T(8,128)} %param.15) | copy-start | bytes 393220
  125.7 39.6 %copy-start.5 = (f32[1,16,2048]{2,1,0:T(8,128)S(1)}, f32[1,16,2048]{2,1,0:T(8,128)}, u32[]{:S(2)}) copy-start(f32[1,16,2048]{2,1,0:T(8,128)} %param.16) | copy-start | bytes 393220
  125.7 39.7 %copy-start.6 = (f32[1,64,512]{2,1,0:T(8,128)S(1)}, f32[1,64,512]{2,1,0:T(8,128)}, u32[]{:S(2)}) copy-start(f32[1,64,512]{2,1,0:T(8,128)} %param.17) | copy-start | bytes 393220
  125.7 39.7 %copy-start.7 = (f32[1,64,512]{2,1,0:T(8,128)S(1)}, f32[1,64,512]{2,1,0:T(8,128)}, u32[]{:S(2)}) copy-start(f32[1,64,512]{2,1,0:T(8,128)} %param.18) | copy-start | bytes 393220
  125.7 39.7 %copy-start.8 = (f32[1,16,2048]{2,1,0:T(8,128)S(1)}, f32[1,16,2048]{2,1,0:T(8,128)}, u32[]{:S(2)}) copy-start(f32[1,16,2048]{2,1,0:T(8,128)} %param.19) | copy-start | bytes 393220
  135.2 4.3 %collective-permute-start.29 = (f32[3,16,128]{2,1,0:T(8,128)S(1)}, f32[3,16,128]{2,1,0:T(8,128)S(1)}, u32[]{:S(2)}, u32[]{:S(2)}) collective-permute-start(f32[3,16,128]{2,1,0:T(8,128)S(1)} %gram.1), channel_id=1, source_target_pairs={{0,6},{1,7},{2,0},{3,1},{4,2},{5,3},{6,4},{7,5},{8,14},{9,15},{10,... | collective-permute-start | bytes 73736 | tf_op jit(solution)/shard_map/ppermute | solution.py:357
  137.6 4.2 %collective-permute-start.28 = (f32[3,16,128]{2,1,0:T(8,128)S(1)}, f32[3,16,128]{2,1,0:T(8,128)S(1)}, u32[]{:S(2)}, u32[]{:S(2)}) collective-permute-start(f32[3,16,128]{2,1,0:T(8,128)S(1)} %gram.1), channel_id=1, source_target_pairs={{0,2},{1,3},{2,4},{3,5},{4,6},{5,7},{6,0},{7,1},{8,10},{9,11},{10,... | collective-permute-start | bytes 73736 | tf_op jit(solution)/shard_map/ppermute | solution.py:357
  137.6 4.5 %collective-permute-start.27 = (f32[3,16,128]{2,1,0:T(8,128)S(1)}, f32[3,16,128]{2,1,0:T(8,128)S(1)}, u32[]{:S(2)}, u32[]{:S(2)}) collective-permute-start(f32[3,16,128]{2,1,0:T(8,128)S(1)} %gram.1), channel_id=1, source_target_pairs={{0,4},{1,5},{2,6},{3,7},{4,0},{5,1},{6,2},{7,3},{8,12},{9,13},{10,... | collective-permute-start | bytes 73736 | tf_op jit(solution)/shard_map/ppermute | solution.py:357
  142.1 3.4 %collective-permute-start.32 = (f32[3,16,128]{2,1,0:T(8,128)S(1)}, f32[3,16,128]{2,1,0:T(8,128)S(1)}, u32[]{:S(2)}, u32[]{:S(2)}) collective-permute-start(f32[3,16,128]{2,1,0:T(8,128)S(1)} %add_add_fusion.1), channel_id=1, source_target_pairs={{0,24},{1,25},{2,26},{3,27},{4,28},{5,29},{6,30},{7,31},{8,0},{9,1... | collective-permute-start | bytes 73736 | tf_op jit(solution)/shard_map/ppermute | solution.py:357
  144.2 3.9 %collective-permute-start.31 = (f32[3,16,128]{2,1,0:T(8,128)S(1)}, f32[3,16,128]{2,1,0:T(8,128)S(1)}, u32[]{:S(2)}, u32[]{:S(2)}) collective-permute-start(f32[3,16,128]{2,1,0:T(8,128)S(1)} %add_add_fusion.1), channel_id=1, source_target_pairs={{0,8},{1,9},{2,10},{3,11},{4,12},{5,13},{6,14},{7,15},{8,16},{9,17... | collective-permute-start | bytes 73736 | tf_op jit(solution)/shard_map/ppermute | solution.py:357
  144.2 4.2 %collective-permute-start.30 = (f32[3,16,128]{2,1,0:T(8,128)S(1)}, f32[3,16,128]{2,1,0:T(8,128)S(1)}, u32[]{:S(2)}, u32[]{:S(2)}) collective-permute-start(f32[3,16,128]{2,1,0:T(8,128)S(1)} %add_add_fusion.1), channel_id=1, source_target_pairs={{0,16},{1,17},{2,18},{3,19},{4,20},{5,21},{6,22},{7,23},{8,24},{9,... | collective-permute-start | bytes 73736 | tf_op jit(solution)/shard_map/ppermute | solution.py:357
  148.4 16.9 %collective-permute-start.33 = (f32[3,16,128]{2,1,0:T(8,128)S(1)}, f32[3,16,128]{2,1,0:T(8,128)S(1)}, u32[]{:S(2)}, u32[]{:S(2)}) collective-permute-start(f32[3,16,128]{2,1,0:T(8,128)S(1)} %add_add_fusion), channel_id=1, source_target_pairs={{0,1},{1,0},{2,3},{3,2},{4,5},{5,4},{6,7},{7,6},{8,9},{9,8},{10,11... | collective-permute-start | bytes 73736 | tf_op jit(solution)/shard_map/ppermute | solution.py:357

commit v7 on v6

--- a/solution.py
+++ b/solution.py
@@ -130,25 +130,49 @@
     )(*tokens, weights)
 
 
-def backward(cots, route, hidden_t, gate_factor, act, xt, weights):
-    def body(c0, c1, c2, c3, route_ref, hid_t, factor, act_ref, xt_ref, w, keep, send, both, hg, scaled):
+def of_cotangents(first, ks, cots, route, hid_t, w, hg, scaled, put):
+    scale = column(route[...])
+    for k, c in zip(ks, cots):
+        for j in range(SLICE // 128):
+            cols = slice(128 * j, 128 * (j + 1))
+            scaled[:, cols] = (scale * c[:, cols].astype(F32)).astype(BF16)
+        part = lax.dot_general(scaled[...], down_block(w, slice_of(k)), NT, preferred_element_type=F32)
+        if first and k == ks[0]:
+            hg[...] = part
+        else:
+            hg[...] += part
+        down = jnp.dot(hid_t[...], scaled[...], preferred_element_type=F32) / TOK_DEV
+        put(k, down.astype(BF16))
+
+
+def backward_early(cots, route, hidden_t, weights):
+    def body(c0, c2, route_ref, hid_t, w, hg, downs, scaled):
+        def put(k, down):
+            downs[k // 2] = down
+
+        of_cotangents(True, (0, 2), (c0, c2), route_ref, hid_t, w, hg, scaled, put)
+
+    shapes = [struct((TOK_DEV, H), F32), struct((2, H, SLICE), BF16)]
+    scratch = [pltpu.VMEM((TOK_DEV, SLICE), BF16)]
+    return call(body, "backward_early", 5, shapes, 2 * TOK_DEV * D * H, 8 * MIB, scratch)(
+        *cots, route, hidden_t, weights
+    )
+
+
+def backward(cots, route, hidden_t, early, downs, gate_factor, act, xt, weights):
+    def body(c1, c3, route_ref, hid_t, hg0, down_ref, factor, act_ref, xt_ref, w, keep, send, both, hg, scaled):
         first = lax.axis_index("dp") % 2 == 0
-        scale = column(route_ref[...])
-        for k, c in enumerate((c0, c1, c2, c3)):
-            s = slice_of(k)
-            for j in range(SLICE // 128):
-                cols = slice(128 * j, 128 * (j + 1))
-                scaled[:, cols] = (scale * c[:, cols].astype(F32)).astype(BF16)
-            part = lax.dot_general(scaled[...], down_block(w, s), NT, preferred_element_type=F32)
-            if k == 0:
-                hg[...] = part
-            else:
-                hg[...] += part
-            down = jnp.dot(hid_t[...], scaled[...], preferred_element_type=F32) / TOK_DEV
-            down = down.astype(BF16).reshape(N_CHIP, 2, 16, SLICE)
-            rows = pl.ds(pl.multiple_of(128 + 16 * s, 16), 16)
+
+        def put(k, down):
+            down = down.reshape(N_CHIP, 2, 16, SLICE)
+            rows = pl.ds(pl.multiple_of(128 + 16 * slice_of(k), 16), 16)
             keep[:, rows, :] = jnp.where(first, down[:, 0], down[:, 1])
             send[:, rows, :] = jnp.where(first, down[:, 1], down[:, 0])
+
+        hg[...] = hg0[...]
+        of_cotangents(False, (1, 3), (c1, c3), route_ref, hid_t, w, hg, scaled, put)
+        put(0, down_ref[0])
+        put(2, down_ref[1])
 
         @pl.loop(0, TOK_DEV // 64)
         def _(i):
@@ -177,10 +201,10 @@
         "backward",
         10,
         shapes,
-        8 * TOK_DEV * D * H,
+        6 * TOK_DEV * D * H,
         20 * MIB,
         [pltpu.VMEM((TOK_DEV, H), F32), pltpu.VMEM((TOK_DEV, SLICE), BF16)],
-    )(*cots, route, hidden_t, gate_factor, act, xt, weights)
+    )(*cots, route, hidden_t, early, downs, gate_factor, act, xt, weights)
 
 
 def slot_gradients(both, weights):
@@ -479,11 +503,11 @@
         return pick_rows(ids[k : k + 1], [pool])[0]
 
     ids = [token_ids] + [around_y(token_ids, N_EXPERT - k) for k in (1, 2, 3)]
-    packed = pack(gate_weight[0], up_weight[0], down_weight[0])
     x, c = [None] * 4, [None] * 4
     x[1], x[3] = picked(1, pool_tokens), picked(3, pool_tokens)
-    ids, packed, x[1], x[3] = tie((ids, packed, x[1], x[3]))
-
+    ids, x[1], x[3], shards = tie((ids, x[1], x[3], (gate_weight[0], up_weight[0], down_weight[0])))
+
+    packed = pack(*shards)
     blocks = spread(packed, 0)
     x[1], x[3] = around_y(x[1], 1), around_y(x[3], 3)
     x[2], c[2] = picked(2, pool_tokens), picked(2, pool_cotangent)
@@ -499,19 +523,22 @@
     mine = half_of_weights((block, *blocks))
     weights = whole_weights(mine, other_core(mine))
     c[1], c[3] = around_y(c[1], 1), around_y(c[3], 3)
-    tokens, cots = x, c
-
-    hidden_t, gate_factor, act, xt = forward(tokens, weights)
-    keep, send, both = backward(cots, route_weights, hidden_t, gate_factor, act, xt, weights)
+
+    hidden_t, gate_factor, act, xt = forward(x, weights)
+    early, downs = backward_early((c[0], c[2]), route_weights, hidden_t, weights)
+    keep, send, both = backward(
+        (c[1], c[3]), route_weights, hidden_t, early, downs, gate_factor, act, xt, weights
+    )
     received = other_core(send)
     slots = slot_gradients(both, weights)
-    received, slots = lax.optimization_barrier((received, slots))
+    received, slots = lax.optimization_barrier((received, list(slots)))
 
     mine = pair_moments(keep, received)
     sent = pair_merge(keep, received, mine, other_core(mine))
     parts = [sent[0]] + [shift(sent[k], "dp", along(0, k)) for k in (1, 2, 3)]
-    back = [slots[0]] + [around_y(slots[k], N_EXPERT - k) for k in (1, 2, 3)]
-    parts, back[1], back[3] = tie((parts, back[1], back[3]))
+    back = [slots[0], around_y(slots[1], 3), None, around_y(slots[3], 1)]
+    parts, back[1], back[3], slots[2] = tie((parts, back[1], back[3], slots[2]))
+    back[2] = around_y(slots[2], 2)
     sent = turn_over(parts)
     parts = [sent[0]] + [shift(sent[k], "dp", along(1, k)) for k in (1, 2, 3)]
     pool_grad = scatter_rows(ids, back)

time: 167 us -> 155 us (0.928)
  starting transfers between devices: 67.2 us -> 54.7 us
  local copies, waits for them, and re-layouts: 4.35 us -> 1.64 us
  waiting for transfers between devices: 59.4 us -> 61.4 us
    ppermute x34, starting transfers between devices: 67.2 us -> 54.7 us  [shift(): lax.ppermute(block, axis, [(i, to(i)) for i in range(lax.axis_size(axis))])]
    unnamed x28 -> x22, local copies, waits for them, and re-layouts: 4.35 us -> 1.64 us
    ppermute x34, waiting for transfers between devices: 59.4 us -> 61.4 us  [shift(): lax.ppermute(block, axis, [(i, to(i)) for i in range(lax.axis_size(axis))])]
    pallas_call x1 -> x2, Pallas kernels: 5.14 us -> 5.52 us  [the longest x1 4.1 us: backward(): call(body, 'backward', 10, shapes, 6 * TOK_DEV * D * H, 20 * MIB, [pltpu....]
  transfers between devices with their start and end apart: 34 -> 34, of which waited for: 21 -> 21; matrix products, arithmetic and copies ran while one was open for 0% -> 0% of each run, Pallas kernels for 14% -> 16%
where the time goes in v7:
time: 155 us
  waiting for transfers between devices  61.4 us (40%)
  starting transfers between devices  54.7 us (35%)
  Pallas kernels  35.9 us (23%)
  local copies, waits for them, and re-layouts  1.64 us (1%)
    ppermute x34, waiting for transfers between devices, shift(): lax.ppermute(block, axis, [(i, to(i)) for i in range(lax.axis_size(axis))])  61.4 us
    ppermute x34, starting transfers between devices, shift(): lax.ppermute(block, axis, [(i, to(i)) for i in range(lax.axis_size(axis))])  54.7 us
    pallas_call x7, Pallas kernels, pick_rows(): call(body, 'pick_rows', n_ids + n_pool, shapes, 2 * TOK_DEV * POOL * SLIC...  11.1 us
    pallas_call x1, Pallas kernels, scatter_rows(): pl.pallas_call(body, name='scatter_rows', grid=(POOL // block,), out_shap...  5.97 us
    pallas_call x1, Pallas kernels, backward(): call(body, 'backward', 10, shapes, 6 * TOK_DEV * D * H, 20 * MIB, [pltpu....  4.1 us
  transfers between devices with their start and end apart: 34, of which 21 were waited for; matrix products, arithmetic and copies ran while one was open for 0% of the time, Pallas kernels for 16%

profile of v7, /device:TPU:1, one launch (start us, length us, event | category | flops | bytes accessed | tf_op | source)
XLA Modules:
  0.0 154.6 jit_solution(12789005146860894409)
XLA Ops:
  0.7 2.2 %collective-permute-start.2 = (s32[1,512]{1,0:T(1,128)}, s32[1,512]{1,0:T(1,128)S(1)}, u32[]{:S(2)}, u32[]{:S(2)}) collective-permute-start(s32[1,512]{1,0:T(1,128)} %i0), channel_id=1, source_target_pairs={{0,32},{32,64},{64,96},{96,0},{1,33},{33,65},{65,97},{97,1},{2,34}... | collective-permute-start | bytes 6152 | tf_op jit(solution)/shard_map/ppermute | solution.py:381
  2.9 2.6 %collective-permute-start.1 = (s32[1,512]{1,0:T(1,128)}, s32[1,512]{1,0:T(1,128)S(1)}, u32[]{:S(2)}, u32[]{:S(2)}) collective-permute-start(s32[1,512]{1,0:T(1,128)} %i0), channel_id=1, source_target_pairs={{0,64},{32,96},{64,0},{96,32},{1,65},{33,97},{65,1},{97,33},{2,66}... | collective-permute-start | bytes 6152 | tf_op jit(solution)/shard_map/ppermute | solution.py:381
  6.6 1.6 %copy-done.8 = bf16[2048,512]{1,0:T(8,128)(2,1)S(1)} copy-done((bf16[2048,512]{1,0:T(8,128)(2,1)S(1)}, bf16[2048,512]{1,0:T(8,128)(2,1)}, u32[]{:S(2)}) %copy-start.8) | copy-done | bytes 2097176
  8.1 1.4 pick_rows.8
  9.6 1.4 pick_rows.7
  11.6 2.3 %collective-permute-start.7 = (bf16[512,512]{1,0:T(8,128)(2,1)S(1)}, bf16[512,512]{1,0:T(8,128)(2,1)S(1)}, u32[]{:S(2)}, u32[]{:S(2)}) collective-permute-start(bf16[512,512]{1,0:T(8,128)(2,1)S(1)} %pick_rows.8), channel_id=1, source_target_pairs={{0,96},{32,0},{64,32},{96,64},{1,97},{33,1},{65,33},{97,65},{2,98}... | collective-permute-start | bytes 1572872 | tf_op jit(solution)/shard_map/ppermute | solution.py:381
  14.4 2.5 %collective-permute-start.5 = (bf16[96,1024]{1,0:T(8,128)(2,1)S(1)}, bf16[96,1024]{1,0:T(8,128)(2,1)S(1)}, u32[]{:S(2)}, u32[]{:S(2)}) collective-permute-start(bf16[96,1024]{1,0:T(8,128)(2,1)S(1)} %pack.1.refs_0_), channel_id=1, source_target_pairs={{0,6},{1,25},{2,0},{3,27},{4,2},{5,29},{6,4},{7,31},{8,14},{9,1},{... | collective-permute-start | bytes 589832 | tf_op jit(solution)/shard_map/ppermute | solution.py:381
  18.1 1.4 pick_rows.9
  19.5 1.4 pick_rows.10
  21.7 1.4 collective-permute-done.4.refs_2_
  23.1 2.3 %collective-permute-done.3.refs_1_ = bf16[96,1024]{1,0:T(8,128)(2,1)S(1)} collective-permute-done((bf16[96,1024]{1,0:T(8,128)(2,1)S(1)}, bf16[96,1024]{1,0:T(8,128)(2,1)S(1)}, u32[]{:S(2)}, u32[]{:S(2)}) %collective-permute-start.3) | collective-permute-done | bytes 196640 | tf_op jit(solution)/shard_map/ppermute | solution.py:381
  25.5 3.8 %collective-permute-start.10 = (bf16[4,96,1024]{2,1,0:T(8,128)(2,1)S(1)}, bf16[4,96,1024]{2,1,0:T(8,128)(2,1)S(1)}, u32[]{:S(2)}, u32[]{:S(2)}) collective-permute-start(bf16[4,96,1024]{2,1,0:T(8,128)(2,1)S(1)} %bundle.1.refs_0_), channel_id=1, source_target_pairs={{0,24},{1,7},{2,26},{3,1},{4,28},{5,3},{6,30},{7,5},{8,0},{9,15},{... | collective-permute-start | bytes 2359304 | tf_op jit(solution)/shard_map/ppermute | solution.py:381
  30.0 3.0 %collective-permute-start.12 = (bf16[512,512]{1,0:T(8,128)(2,1)S(1)}, bf16[512,512]{1,0:T(8,128)(2,1)S(1)}, u32[]{:S(2)}, u32[]{:S(2)}) collective-permute-start(bf16[512,512]{1,0:T(8,128)(2,1)S(1)} %pick_rows.10), channel_id=1, source_target_pairs={{0,64},{32,96},{64,0},{96,32},{1,65},{33,97},{65,1},{97,33},{2,66}... | collective-permute-start | bytes 1572872 | tf_op jit(solution)/shard_map/ppermute | solution.py:381
  33.0 1.4 pick_rows.12
  34.4 1.4 pick_rows.13
  35.9 2.5 %pick_rows.11 = (bf16[512,512]{1,0:T(8,128)(2,1)S(1)}, bf16[512,512]{1,0:T(8,128)(2,1)S(1)}) custom-call(s32[1,512]{1,0:T(1,128)S(1)} %copy-done.10, bf16[2048,512]{1,0:T(8,128)(2,1)S(1)} %copy-done.9, bf16[2048,512]{1,0:T(8,128)(2,1)S(1)} %copy-done.7), custom_call_target="tpu_custom_call" | custom-call | flops 2147483648 | bytes 3145728 | tf_op jit(solution)/shard_map/pick_rows/pallas_call | solution.py:68
  38.4 2.3 %collective-permute-done.11.x2 = bf16[512,512]{1,0:T(8,128)(2,1)S(1)} collective-permute-done((bf16[512,512]{1,0:T(8,128)(2,1)S(1)}, bf16[512,512]{1,0:T(8,128)(2,1)S(1)}, u32[]{:S(2)}, u32[]{:S(2)}) %collective-permute-start.11) | collective-permute-done | bytes 524320 | tf_op jit(solution)/shard_map/ppermute | solution.py:381
  40.7 11.2 %collective-permute-done.12.c2 = bf16[512,512]{1,0:T(8,128)(2,1)S(1)} collective-permute-done((bf16[512,512]{1,0:T(8,128)(2,1)S(1)}, bf16[512,512]{1,0:T(8,128)(2,1)S(1)}, u32[]{:S(2)}, u32[]{:S(2)}) %collective-permute-start.12) | collective-permute-done | bytes 524320 | tf_op jit(solution)/shard_map/ppermute | solution.py:381
  52.2 5.2 %collective-permute-start.15 = (bf16[16,96,1024]{2,1,0:T(8,128)(2,1)S(1)}, bf16[16,96,1024]{2,1,0:T(8,128)(2,1)S(1)}, u32[]{:S(2)}, u32[]{:S(2)}) collective-permute-start(bf16[16,96,1024]{2,1,0:T(8,128)(2,1)S(1)} %half_of_weights.1.a), channel_id=1, source_target_pairs={{0,1},{1,0},{2,3},{3,2},{4,5},{5,4},{6,7},{7,6},{8,9},{9,8},{10,11... | collective-permute-start | bytes 9437192 | tf_op jit(solution)/shard_map/ppermute | solution.py:381
  57.4 2.7 %collective-permute-start.14 = (bf16[512,512]{1,0:T(8,128)(2,1)S(1)}, bf16[512,512]{1,0:T(8,128)(2,1)S(1)}, u32[]{:S(2)}, u32[]{:S(2)}) collective-permute-start(bf16[512,512]{1,0:T(8,128)(2,1)S(1)} %pick_rows.13), channel_id=1, source_target_pairs={{0,96},{32,0},{64,32},{96,64},{1,97},{33,1},{65,33},{97,65},{2,98}... | collective-permute-start | bytes 1572872 | tf_op jit(solution)/shard_map/ppermute | solution.py:381
  60.1 2.6 %collective-permute-done.15.b = bf16[16,96,1024]{2,1,0:T(8,128)(2,1)S(1)} collective-permute-done((bf16[16,96,1024]{2,1,0:T(8,128)(2,1)S(1)}, bf16[16,96,1024]{2,1,0:T(8,128)(2,1)S(1)}, u32[]{:S(2)}, u32[]{:S(2)}) %collective-permute-start.15) | collective-permute-done | bytes 3145760 | tf_op jit(solution)/shard_map/ppermute | solution.py:381
  63.2 3.1 %forward.1 = (bf16[512,512]{1,0:T(8,128)(2,1)S(1)}, f32[512,512]{1,0:T(8,128)S(1)}, f32[512,512]{1,0:T(8,128)S(1)}, bf16[4,512,512]{2,1,0:T(8,128)(2,1)S(1)}) custom-call(bf16[512,512]{1,0:T(8,128)(2,1)S(1)} %get-tuple-element.107.x0, bf16[512,512]{1,0:T(8,128)(2,1)S(1)} %collective-permute-done.6.x1, bf16[512,512]{1,0:T(8,128)(2,1)S(1)} %collective-permute-done.11.x2, ...), custom_call_target="tpu_custom_call" | custom-call | flops 2147483648 | bytes 10485760 | tf_op jit(solution)/shard_map/forward/pallas_call | solution.py:122
  66.2 1.4 backward_early.1
  67.7 4.5 %collective-permute-done.13.c1 = bf16[512,512]{1,0:T(8,128)(2,1)S(1)} collective-permute-done((bf16[512,512]{1,0:T(8,128)(2,1)S(1)}, bf16[512,512]{1,0:T(8,128)(2,1)S(1)}, u32[]{:S(2)}, u32[]{:S(2)}) %collective-permute-start.13) | collective-permute-done | bytes 524320 | tf_op jit(solution)/shard_map/ppermute | solution.py:381
  72.1 4.1 %backward.1 = (bf16[16,192,512]{2,1,0:T(8,128)(2,1)S(1)}, bf16[16,192,512]{2,1,0:T(8,128)(2,1)S(1)}, bf16[512,1024]{1,0:T(8,128)(2,1)S(1)}) custom-call(bf16[512,512]{1,0:T(8,128)(2,1)S(1)} %collective-permute-done.13.c1, bf16[512,512]{1,0:T(8,128)(2,1)S(1)} %collective-permute-done.14.c3, f32[1,512]{1,0:T(1,128)S(1)} %copy-done.6, ...), custom_call_target="tpu_custom_call" | custom-call | flops 3221225472 | bytes 20971520 | tf_op jit(solution)/shard_map/backward/pallas_call | solution.py:199
  77.4 2.4 %slot_gradients.1 = (bf16[512,512]{1,0:T(8,128)(2,1)S(1)}, bf16[512,512]{1,0:T(8,128)(2,1)S(1)}, bf16[512,512]{1,0:T(8,128)(2,1)S(1)}, bf16[512,512]{1,0:T(8,128)(2,1)S(1)}) custom-call(bf16[512,1024]{1,0:T(8,128)(2,1)S(1)} %get-tuple-element.124.both_ref, bf16[32,96,1024]{2,1,0:T(8,128)(2,1)S(1)} %whole_weights.1.w), custom_call_target="tpu_custom_call" | custom-call | flops 2147483648 | bytes 9437184 | tf_op jit(solution)/shard_map/slot_gradients/pallas_call | solution.py:217
  79.8 2.9 %collective-permute-done.16.b_ref = bf16[16,192,512]{2,1,0:T(8,128)(2,1)S(1)} collective-permute-done((bf16[16,192,512]{2,1,0:T(8,128)(2,1)S(1)}, bf16[16,192,512]{2,1,0:T(8,128)(2,1)S(1)}, u32[]{:S(2)}, u32[]{:S(2)}) %collective-permute-start.16) | collective-permute-done | bytes 3145760 | tf_op jit(solution)/shard_map/ppermute | solution.py:381
  84.9 1.3 pair_merge.1
  86.3 2.4 %collective-permute-start.19 = (bf16[4,192,512]{2,1,0:T(8,128)(2,1)S(1)}, bf16[4,192,512]{2,1,0:T(8,128)(2,1)S(1)}, u32[]{:S(2)}, u32[]{:S(2)}) collective-permute-start(bf16[4,192,512]{2,1,0:T(8,128)(2,1)S(1)} %get-tuple-element.132), channel_id=1, source_target_pairs={{0,4},{1,17},{2,6},{3,19},{4,0},{5,21},{6,2},{7,23},{8,12},{9,25},... | collective-permute-start | bytes 2359304 | tf_op jit(solution)/shard_map/ppermute | solution.py:381
  89.9 2.7 %collective-permute-start.21 = (bf16[512,512]{1,0:T(8,128)(2,1)S(1)}, bf16[512,512]{1,0:T(8,128)(2,1)S(1)}, u32[]{:S(2)}, u32[]{:S(2)}) collective-permute-start(bf16[512,512]{1,0:T(8,128)(2,1)S(1)} %get-tuple-element.134), channel_id=1, source_target_pairs={{0,96},{32,0},{64,32},{96,64},{1,97},{33,1},{65,33},{97,65},{2,98}... | collective-permute-start | bytes 1572872 | tf_op jit(solution)/shard_map/ppermute | solution.py:381
  92.6 9.4 %collective-permute-done.21.g1 = bf16[512,512]{1,0:T(8,128)(2,1)S(1)} collective-permute-done((bf16[512,512]{1,0:T(8,128)(2,1)S(1)}, bf16[512,512]{1,0:T(8,128)(2,1)S(1)}, u32[]{:S(2)}, u32[]{:S(2)}) %collective-permute-start.21) | collective-permute-done | bytes 524320 | tf_op jit(solution)/shard_map/ppermute | solution.py:381
  102.0 3.1 %collective-permute-done.22.g3 = bf16[512,512]{1,0:T(8,128)(2,1)S(1)} collective-permute-done((bf16[512,512]{1,0:T(8,128)(2,1)S(1)}, bf16[512,512]{1,0:T(8,128)(2,1)S(1)}, u32[]{:S(2)}, u32[]{:S(2)}) %collective-permute-start.22) | collective-permute-done | bytes 524320 | tf_op jit(solution)/shard_map/ppermute | solution.py:381
  105.1 1.9 %collective-permute-done.18.refs_1_ = bf16[4,192,512]{2,1,0:T(8,128)(2,1)S(1)} collective-permute-done((bf16[4,192,512]{2,1,0:T(8,128)(2,1)S(1)}, bf16[4,192,512]{2,1,0:T(8,128)(2,1)S(1)}, u32[]{:S(2)}, u32[]{:S(2)}) %collective-permute-start.18) | collective-permute-done | bytes 786464 | tf_op jit(solution)/shard_map/ppermute | solution.py:381
  107.6 1.6 %collective-permute-start.26 = (bf16[512,512]{1,0:T(8,128)(2,1)S(1)}, bf16[512,512]{1,0:T(8,128)(2,1)S(1)}, u32[]{:S(2)}, u32[]{:S(2)}) collective-permute-start(bf16[512,512]{1,0:T(8,128)(2,1)S(1)} %get-tuple-element.148), channel_id=1, source_target_pairs={{0,64},{32,96},{64,0},{96,32},{1,65},{33,97},{65,1},{97,33},{2,66}... | collective-permute-start | bytes 1572872 | tf_op jit(solution)/shard_map/ppermute | solution.py:381
  109.4 1.7 %collective-permute-start.23 = (bf16[4,192,512]{2,1,0:T(8,128)(2,1)S(1)}, bf16[4,192,512]{2,1,0:T(8,128)(2,1)S(1)}, u32[]{:S(2)}, u32[]{:S(2)}) collective-permute-start(bf16[4,192,512]{2,1,0:T(8,128)(2,1)S(1)} %get-tuple-element.142), channel_id=1, source_target_pairs={{0,8},{1,3},{2,10},{3,5},{4,12},{5,7},{6,14},{7,1},{8,16},{9,11},{... | collective-permute-start | bytes 2359304 | tf_op jit(solution)/shard_map/ppermute | solution.py:381
  111.2 1.2 collective-permute-start.24
  112.4 1.3 collective-permute-start.25
  113.6 7.4 %collective-permute-done.26.g2 = bf16[512,512]{1,0:T(8,128)(2,1)S(1)} collective-permute-done((bf16[512,512]{1,0:T(8,128)(2,1)S(1)}, bf16[512,512]{1,0:T(8,128)(2,1)S(1)}, u32[]{:S(2)}, u32[]{:S(2)}) %collective-permute-start.26) | collective-permute-done | bytes 524320 | tf_op jit(solution)/shard_map/ppermute | solution.py:381
  121.0 6.0 %scatter_rows.1 = f32[2048,512]{1,0:T(8,128)} custom-call(s32[1,512]{1,0:T(1,128)S(1)} %copy-done.10, s32[1,512]{1,0:T(1,128)S(1)} %collective-permute-done.refs_0_.i1, s32[1,512]{1,0:T(1,128)S(1)} %collective-permute-done.1.refs_0_.i2, s32[1,512]{1,0:T(1,128)S(1)} %collective-permute-done.2.refs_0_.i3, bf16[512,512]{1,0:T(8,128)(2,1)S(1)} %get-tuple-element.146.g0, ...), custom_call_target="tpu_custom_call" | custom-call | flops 4294967296 | bytes 6291456 | tf_op jit(solution)/shard_map/scatter_rows/pallas_call | solution.py:366
  127.0 3.4 %collective-permute-done.24.refs_2_.x2 = bf16[4,192,512]{2,1,0:T(8,128)(2,1)S(1)} collective-permute-done((bf16[4,192,512]{2,1,0:T(8,128)(2,1)S(1)}, bf16[4,192,512]{2,1,0:T(8,128)(2,1)S(1)}, u32[]{:S(2)}, u32[]{:S(2)}) %collective-permute-start.24) | collective-permute-done | bytes 786464 | tf_op jit(solution)/shard_map/ppermute | solution.py:381
  130.9 2.3 %gram.1 = f32[3,16,128]{2,1,0:T(8,128)S(1)} custom-call(bf16[4,192,512]{2,1,0:T(8,128)(2,1)S(1)} %get-tuple-element.150.refs_0_.x0, bf16[4,192,512]{2,1,0:T(8,128)(2,1)S(1)} %collective-permute-done.23.refs_1_.x1, bf16[4,192,512]{2,1,0:T(8,128)(2,1)S(1)} %collective-permute-done.24.refs_2_.x2, bf16[4,192,512]{2,1,0:T(8,128)(2,1)S(1)} %collective-permute-done.25.refs_3_.x3), custom_call_target="tpu_custom_call" | custom-call | flops 805306368 | bytes 3145728 | tf_op jit(solution)/shard_map/gram/pallas_call | solution.py:303
  133.2 2.4 %collective-permute-start.29 = (f32[3,16,128]{2,1,0:T(8,128)S(1)}, f32[3,16,128]{2,1,0:T(8,128)S(1)}, u32[]{:S(2)}, u32[]{:S(2)}) collective-permute-start(f32[3,16,128]{2,1,0:T(8,128)S(1)} %gram.1), channel_id=1, source_target_pairs={{0,6},{1,7},{2,0},{3,1},{4,2},{5,3},{6,4},{7,5},{8,14},{9,15},{10,... | collective-permute-start | bytes 73736 | tf_op jit(solution)/shard_map/ppermute | solution.py:381
  136.8 2.7 %collective-permute-done.28 = f32[3,16,128]{2,1,0:T(8,128)S(1)} collective-permute-done((f32[3,16,128]{2,1,0:T(8,128)S(1)}, f32[3,16,128]{2,1,0:T(8,128)S(1)}, u32[]{:S(2)}, u32[]{:S(2)}) %collective-permute-start.28) | collective-permute-done | bytes 24608 | tf_op jit(solution)/shard_map/ppermute | solution.py:381
  139.8 2.1 %collective-permute-start.32 = (f32[3,16,128]{2,1,0:T(8,128)S(1)}, f32[3,16,128]{2,1,0:T(8,128)S(1)}, u32[]{:S(2)}, u32[]{:S(2)}) collective-permute-start(f32[3,16,128]{2,1,0:T(8,128)S(1)} %add_add_fusion.1), channel_id=1, source_target_pairs={{0,24},{1,25},{2,26},{3,27},{4,28},{5,29},{6,30},{7,31},{8,0},{9,1... | collective-permute-start | bytes 73736 | tf_op jit(solution)/shard_map/ppermute | solution.py:381
  141.9 1.7 %collective-permute-start.30 = (f32[3,16,128]{2,1,0:T(8,128)S(1)}, f32[3,16,128]{2,1,0:T(8,128)S(1)}, u32[]{:S(2)}, u32[]{:S(2)}) collective-permute-start(f32[3,16,128]{2,1,0:T(8,128)S(1)} %add_add_fusion.1), channel_id=1, source_target_pairs={{0,16},{1,17},{2,18},{3,19},{4,20},{5,21},{6,22},{7,23},{8,24},{9,... | collective-permute-start | bytes 73736 | tf_op jit(solution)/shard_map/ppermute | solution.py:381
  143.6 2.2 %collective-permute-done.31 = f32[3,16,128]{2,1,0:T(8,128)S(1)} collective-permute-done((f32[3,16,128]{2,1,0:T(8,128)S(1)}, f32[3,16,128]{2,1,0:T(8,128)S(1)}, u32[]{:S(2)}, u32[]{:S(2)}) %collective-permute-start.31) | collective-permute-done | bytes 24608 | tf_op jit(solution)/shard_map/ppermute | solution.py:381
  146.1 5.8 %collective-permute-start.33 = (f32[3,16,128]{2,1,0:T(8,128)S(1)}, f32[3,16,128]{2,1,0:T(8,128)S(1)}, u32[]{:S(2)}, u32[]{:S(2)}) collective-permute-start(f32[3,16,128]{2,1,0:T(8,128)S(1)} %add_add_fusion), channel_id=1, source_target_pairs={{0,1},{1,0},{2,3},{3,2},{4,5},{5,4},{6,7},{7,6},{8,9},{9,8},{10,11... | collective-permute-start | bytes 73736 | tf_op jit(solution)/shard_map/ppermute | solution.py:381
  152.8 1.9 %finish.1 = (f32[64,512]{1,0:T(8,128)}, f32[64,512]{1,0:T(8,128)}, f32[16,2048]{1,0:T(8,128)}, f32[64,512]{1,0:T(8,128)}, f32[64,512]{1,0:T(8,128)}, /*index=5*/f32[16,2048]{1,0:T(8,128)}) custom-call(bf16[4,192,512]{2,1,0:T(8,128)(2,1)S(1)} %get-tuple-element.150.refs_0_.x0, bf16[4,192,512]{2,1,0:T(8,128)(2,1)S(1)} %collective-permute-done.23.refs_1_.x1, ...), custom_call_target="tpu_custom_call" | custom-call | flops 4194304 | bytes 6291456 | tf_op jit(solution)/shard_map/finish/pallas_call | solution.py:349
  (66 shorter events, 14.0 us)
Async XLA Ops:
  0.6 13.2 %copy-start.2 = (f32[1,16,2048]{2,1,0:T(8,128)S(1)}, f32[1,16,2048]{2,1,0:T(8,128)}, u32[]{:S(2)}) copy-start(f32[1,16,2048]{2,1,0:T(8,128)} %param.16) | copy-start | bytes 393220
  0.6 13.2 %copy-start.1 = (f32[1,64,512]{2,1,0:T(8,128)S(1)}, f32[1,64,512]{2,1,0:T(8,128)}, u32[]{:S(2)}) copy-start(f32[1,64,512]{2,1,0:T(8,128)} %param.15) | copy-start | bytes 393220
  0.7 13.2 %copy-start = (f32[1,64,512]{2,1,0:T(8,128)S(1)}, f32[1,64,512]{2,1,0:T(8,128)}, u32[]{:S(2)}) copy-start(f32[1,64,512]{2,1,0:T(8,128)} %param.14) | copy-start | bytes 393220
  0.7 5.9 %collective-permute-start.2 = (s32[1,512]{1,0:T(1,128)}, s32[1,512]{1,0:T(1,128)S(1)}, u32[]{:S(2)}, u32[]{:S(2)}) collective-permute-start(s32[1,512]{1,0:T(1,128)} %i0), channel_id=1, source_target_pairs={{0,32},{32,64},{64,96},{96,0},{1,33},{33,65},{65,97},{97,1},{2,34}... | collective-permute-start | bytes 6152 | tf_op jit(solution)/shard_map/ppermute | solution.py:381
  2.9 8.2 %collective-permute-start.1 = (s32[1,512]{1,0:T(1,128)}, s32[1,512]{1,0:T(1,128)S(1)}, u32[]{:S(2)}, u32[]{:S(2)}) collective-permute-start(s32[1,512]{1,0:T(1,128)} %i0), channel_id=1, source_target_pairs={{0,64},{32,96},{64,0},{96,32},{1,65},{33,97},{65,1},{97,33},{2,66}... | collective-permute-start | bytes 6152 | tf_op jit(solution)/shard_map/ppermute | solution.py:381
  5.5 4.1 %collective-permute-start = (s32[1,512]{1,0:T(1,128)}, s32[1,512]{1,0:T(1,128)S(1)}, u32[]{:S(2)}, u32[]{:S(2)}) collective-permute-start(s32[1,512]{1,0:T(1,128)} %i0), channel_id=1, source_target_pairs={{0,96},{32,0},{64,32},{96,64},{1,97},{33,1},{65,33},{97,65},{2,98}... | collective-permute-start | bytes 6152 | tf_op jit(solution)/shard_map/ppermute | solution.py:381
  6.6 1.6 %copy-start.8 = (bf16[2048,512]{1,0:T(8,128)(2,1)S(1)}, bf16[2048,512]{1,0:T(8,128)(2,1)}, u32[]{:S(2)}) copy-start(bf16[2048,512]{1,0:T(8,128)(2,1)} %refs_1_.11) | copy-start | bytes 6291460
  9.6 8.5 %copy-start.9 = (bf16[2048,512]{1,0:T(8,128)(2,1)S(1)}, bf16[2048,512]{1,0:T(8,128)(2,1)}, u32[]{:S(2)}) copy-start(bf16[2048,512]{1,0:T(8,128)(2,1)} %refs_1_.11) | copy-start | bytes 6291460
  11.1 8.4 %copy-start.7 = (bf16[2048,512]{1,0:T(8,128)(2,1)S(1)}, bf16[2048,512]{1,0:T(8,128)(2,1)}, u32[]{:S(2)}) copy-start(bf16[2048,512]{1,0:T(8,128)(2,1)} %refs_1_.13) | copy-start | bytes 6291460
  11.1 14.3 %collective-permute-start.6 = (bf16[512,512]{1,0:T(8,128)(2,1)S(1)}, bf16[512,512]{1,0:T(8,128)(2,1)S(1)}, u32[]{:S(2)}, u32[]{:S(2)}) collective-permute-start(bf16[512,512]{1,0:T(8,128)(2,1)S(1)} %pick_rows.7), channel_id=1, source_target_pairs={{0,32},{32,64},{64,96},{96,0},{1,33},{33,65},{65,97},{97,1},{2,34}... | collective-permute-start | bytes 1572872 | tf_op jit(solution)/shard_map/ppermute | solution.py:381
  11.6 13.8 %collective-permute-start.7 = (bf16[512,512]{1,0:T(8,128)(2,1)S(1)}, bf16[512,512]{1,0:T(8,128)(2,1)S(1)}, u32[]{:S(2)}, u32[]{:S(2)}) collective-permute-start(bf16[512,512]{1,0:T(8,128)(2,1)S(1)} %pick_rows.8), channel_id=1, source_target_pairs={{0,96},{32,0},{64,32},{96,64},{1,97},{33,1},{65,33},{97,65},{2,98}... | collective-permute-start | bytes 1572872 | tf_op jit(solution)/shard_map/ppermute | solution.py:381
  14.4 7.3 %collective-permute-start.5 = (bf16[96,1024]{1,0:T(8,128)(2,1)S(1)}, bf16[96,1024]{1,0:T(8,128)(2,1)S(1)}, u32[]{:S(2)}, u32[]{:S(2)}) collective-permute-start(bf16[96,1024]{1,0:T(8,128)(2,1)S(1)} %pack.1.refs_0_), channel_id=1, source_target_pairs={{0,6},{1,25},{2,0},{3,27},{4,2},{5,29},{6,4},{7,31},{8,14},{9,1},{... | collective-permute-start | bytes 589832 | tf_op jit(solution)/shard_map/ppermute | solution.py:381
  17.0 6.1 %collective-permute-start.4 = (bf16[96,1024]{1,0:T(8,128)(2,1)S(1)}, bf16[96,1024]{1,0:T(8,128)(2,1)S(1)}, u32[]{:S(2)}, u32[]{:S(2)}) collective-permute-start(bf16[96,1024]{1,0:T(8,128)(2,1)S(1)} %pack.1.refs_0_), channel_id=1, source_target_pairs={{0,4},{1,17},{2,6},{3,19},{4,0},{5,21},{6,2},{7,23},{8,12},{9,25},... | collective-permute-start | bytes 589832 | tf_op jit(solution)/shard_map/ppermute | solution.py:381
  17.5 7.9 %collective-permute-start.3 = (bf16[96,1024]{1,0:T(8,128)(2,1)S(1)}, bf16[96,1024]{1,0:T(8,128)(2,1)S(1)}, u32[]{:S(2)}, u32[]{:S(2)}) collective-permute-start(bf16[96,1024]{1,0:T(8,128)(2,1)S(1)} %pack.1.refs_0_), channel_id=1, source_target_pairs={{0,2},{1,9},{2,4},{3,11},{4,6},{5,13},{6,0},{7,15},{8,10},{9,17},{... | collective-permute-start | bytes 589832 | tf_op jit(solution)/shard_map/ppermute | solution.py:381
  25.5 10.4 %copy-start.10 = (s32[1,512]{1,0:T(1,128)S(1)}, s32[1,512]{1,0:T(1,128)}, u32[]{:S(2)}) copy-start(s32[1,512]{1,0:T(1,128)} %i0) | copy-start | bytes 6148
  25.5 26.5 %collective-permute-start.10 = (bf16[4,96,1024]{2,1,0:T(8,128)(2,1)S(1)}, bf16[4,96,1024]{2,1,0:T(8,128)(2,1)S(1)}, u32[]{:S(2)}, u32[]{:S(2)}) collective-permute-start(bf16[4,96,1024]{2,1,0:T(8,128)(2,1)S(1)} %bundle.1.refs_0_), channel_id=1, source_target_pairs={{0,24},{1,7},{2,26},{3,1},{4,28},{5,3},{6,30},{7,5},{8,0},{9,15},{... | collective-permute-start | bytes 2359304 | tf_op jit(solution)/shard_map/ppermute | solution.py:381
  29.3 22.7 %collective-permute-start.9 = (bf16[4,96,1024]{2,1,0:T(8,128)(2,1)S(1)}, bf16[4,96,1024]{2,1,0:T(8,128)(2,1)S(1)}, u32[]{:S(2)}, u32[]{:S(2)}) collective-permute-start(bf16[4,96,1024]{2,1,0:T(8,128)(2,1)S(1)} %bundle.1.refs_0_), channel_id=1, source_target_pairs={{0,16},{1,5},{2,18},{3,7},{4,20},{5,1},{6,22},{7,3},{8,24},{9,13},... | collective-permute-start | bytes 2359304 | tf_op jit(solution)/shard_map/ppermute | solution.py:381
  29.3 22.7 %collective-permute-start.8 = (bf16[4,96,1024]{2,1,0:T(8,128)(2,1)S(1)}, bf16[4,96,1024]{2,1,0:T(8,128)(2,1)S(1)}, u32[]{:S(2)}, u32[]{:S(2)}) collective-permute-start(bf16[4,96,1024]{2,1,0:T(8,128)(2,1)S(1)} %bundle.1.refs_0_), channel_id=1, source_target_pairs={{0,8},{1,3},{2,10},{3,5},{4,12},{5,7},{6,14},{7,1},{8,16},{9,11},{... | collective-permute-start | bytes 2359304 | tf_op jit(solution)/shard_map/ppermute | solution.py:381
  30.0 10.7 %collective-permute-start.11 = (bf16[512,512]{1,0:T(8,128)(2,1)S(1)}, bf16[512,512]{1,0:T(8,128)(2,1)S(1)}, u32[]{:S(2)}, u32[]{:S(2)}) collective-permute-start(bf16[512,512]{1,0:T(8,128)(2,1)S(1)} %pick_rows.9), channel_id=1, source_target_pairs={{0,64},{32,96},{64,0},{96,32},{1,65},{33,97},{65,1},{97,33},{2,66}... | collective-permute-start | bytes 1572872 | tf_op jit(solution)/shard_map/ppermute | solution.py:381
  30.0 22.0 %collective-permute-start.12 = (bf16[512,512]{1,0:T(8,128)(2,1)S(1)}, bf16[512,512]{1,0:T(8,128)(2,1)S(1)}, u32[]{:S(2)}, u32[]{:S(2)}) collective-permute-start(bf16[512,512]{1,0:T(8,128)(2,1)S(1)} %pick_rows.10), channel_id=1, source_target_pairs={{0,64},{32,96},{64,0},{96,32},{1,65},{33,97},{65,1},{97,33},{2,66}... | collective-permute-start | bytes 1572872 | tf_op jit(solution)/shard_map/ppermute | solution.py:381
  52.2 10.5 %collective-permute-start.15 = (bf16[16,96,1024]{2,1,0:T(8,128)(2,1)S(1)}, bf16[16,96,1024]{2,1,0:T(8,128)(2,1)S(1)}, u32[]{:S(2)}, u32[]{:S(2)}) collective-permute-start(bf16[16,96,1024]{2,1,0:T(8,128)(2,1)S(1)} %half_of_weights.1.a), channel_id=1, source_target_pairs={{0,1},{1,0},{2,3},{3,2},{4,5},{5,4},{6,7},{7,6},{8,9},{9,8},{10,11... | collective-permute-start | bytes 9437192 | tf_op jit(solution)/shard_map/ppermute | solution.py:381
  57.4 14.7 %collective-permute-start.13 = (bf16[512,512]{1,0:T(8,128)(2,1)S(1)}, bf16[512,512]{1,0:T(8,128)(2,1)S(1)}, u32[]{:S(2)}, u32[]{:S(2)}) collective-permute-start(bf16[512,512]{1,0:T(8,128)(2,1)S(1)} %pick_rows.12), channel_id=1, source_target_pairs={{0,32},{32,64},{64,96},{96,0},{1,33},{33,65},{65,97},{97,1},{2,34}... | collective-permute-start | bytes 1572872 | tf_op jit(solution)/shard_map/ppermute | solution.py:381
  57.4 14.7 %collective-permute-start.14 = (bf16[512,512]{1,0:T(8,128)(2,1)S(1)}, bf16[512,512]{1,0:T(8,128)(2,1)S(1)}, u32[]{:S(2)}, u32[]{:S(2)}) collective-permute-start(bf16[512,512]{1,0:T(8,128)(2,1)S(1)} %pick_rows.13), channel_id=1, source_target_pairs={{0,96},{32,0},{64,32},{96,64},{1,97},{33,1},{65,33},{97,65},{2,98}... | collective-permute-start | bytes 1572872 | tf_op jit(solution)/shard_map/ppermute | solution.py:381
  63.2 3.1 %copy-start.6 = (f32[1,512]{1,0:T(1,128)S(1)}, f32[1,512]{1,0:T(1,128)}, u32[]{:S(2)}) copy-start(f32[1,512]{1,0:T(1,128)} %route_ref.3) | copy-start | bytes 6148
  76.2 6.5 %collective-permute-start.16 = (bf16[16,192,512]{2,1,0:T(8,128)(2,1)S(1)}, bf16[16,192,512]{2,1,0:T(8,128)(2,1)S(1)}, u32[]{:S(2)}, u32[]{:S(2)}) collective-permute-start(bf16[16,192,512]{2,1,0:T(8,128)(2,1)S(1)} %get-tuple-element.123), channel_id=1, source_target_pairs={{0,1},{1,0},{2,3},{3,2},{4,5},{5,4},{6,7},{7,6},{8,9},{9,8},{10,11... | collective-permute-start | bytes 9437192 | tf_op jit(solution)/shard_map/ppermute | solution.py:381
  83.5 1.3 collective-permute-start.17
  86.1 20.8 %collective-permute-start.18 = (bf16[4,192,512]{2,1,0:T(8,128)(2,1)S(1)}, bf16[4,192,512]{2,1,0:T(8,128)(2,1)S(1)}, u32[]{:S(2)}, u32[]{:S(2)}) collective-permute-start(bf16[4,192,512]{2,1,0:T(8,128)(2,1)S(1)} %get-tuple-element.131), channel_id=1, source_target_pairs={{0,2},{1,9},{2,4},{3,11},{4,6},{5,13},{6,0},{7,15},{8,10},{9,17},{... | collective-permute-start | bytes 2359304 | tf_op jit(solution)/shard_map/ppermute | solution.py:381
  86.3 20.7 %collective-permute-start.19 = (bf16[4,192,512]{2,1,0:T(8,128)(2,1)S(1)}, bf16[4,192,512]{2,1,0:T(8,128)(2,1)S(1)}, u32[]{:S(2)}, u32[]{:S(2)}) collective-permute-start(bf16[4,192,512]{2,1,0:T(8,128)(2,1)S(1)} %get-tuple-element.132), channel_id=1, source_target_pairs={{0,4},{1,17},{2,6},{3,19},{4,0},{5,21},{6,2},{7,23},{8,12},{9,25},... | collective-permute-start | bytes 2359304 | tf_op jit(solution)/shard_map/ppermute | solution.py:381
  88.8 18.8 %collective-permute-start.20 = (bf16[4,192,512]{2,1,0:T(8,128)(2,1)S(1)}, bf16[4,192,512]{2,1,0:T(8,128)(2,1)S(1)}, u32[]{:S(2)}, u32[]{:S(2)}) collective-permute-start(bf16[4,192,512]{2,1,0:T(8,128)(2,1)S(1)} %get-tuple-element.133), channel_id=1, source_target_pairs={{0,6},{1,25},{2,0},{3,27},{4,2},{5,29},{6,4},{7,31},{8,14},{9,1},{... | collective-permute-start | bytes 2359304 | tf_op jit(solution)/shard_map/ppermute | solution.py:381
  89.9 12.0 %collective-permute-start.21 = (bf16[512,512]{1,0:T(8,128)(2,1)S(1)}, bf16[512,512]{1,0:T(8,128)(2,1)S(1)}, u32[]{:S(2)}, u32[]{:S(2)}) collective-permute-start(bf16[512,512]{1,0:T(8,128)(2,1)S(1)} %get-tuple-element.134), channel_id=1, source_target_pairs={{0,96},{32,0},{64,32},{96,64},{1,97},{33,1},{65,33},{97,65},{2,98}... | collective-permute-start | bytes 1572872 | tf_op jit(solution)/shard_map/ppermute | solution.py:381
  92.6 12.5 %collective-permute-start.22 = (bf16[512,512]{1,0:T(8,128)(2,1)S(1)}, bf16[512,512]{1,0:T(8,128)(2,1)S(1)}, u32[]{:S(2)}, u32[]{:S(2)}) collective-permute-start(bf16[512,512]{1,0:T(8,128)(2,1)S(1)} %get-tuple-element.135), channel_id=1, source_target_pairs={{0,32},{32,64},{64,96},{96,0},{1,33},{33,65},{65,97},{97,1},{2,34}... | collective-permute-start | bytes 1572872 | tf_op jit(solution)/shard_map/ppermute | solution.py:381
  107.6 13.4 %collective-permute-start.26 = (bf16[512,512]{1,0:T(8,128)(2,1)S(1)}, bf16[512,512]{1,0:T(8,128)(2,1)S(1)}, u32[]{:S(2)}, u32[]{:S(2)}) collective-permute-start(bf16[512,512]{1,0:T(8,128)(2,1)S(1)} %get-tuple-element.148), channel_id=1, source_target_pairs={{0,64},{32,96},{64,0},{96,32},{1,65},{33,97},{65,1},{97,33},{2,66}... | collective-permute-start | bytes 1572872 | tf_op jit(solution)/shard_map/ppermute | solution.py:381
  109.4 17.6 %collective-permute-start.23 = (bf16[4,192,512]{2,1,0:T(8,128)(2,1)S(1)}, bf16[4,192,512]{2,1,0:T(8,128)(2,1)S(1)}, u32[]{:S(2)}, u32[]{:S(2)}) collective-permute-start(bf16[4,192,512]{2,1,0:T(8,128)(2,1)S(1)} %get-tuple-element.142), channel_id=1, source_target_pairs={{0,8},{1,3},{2,10},{3,5},{4,12},{5,7},{6,14},{7,1},{8,16},{9,11},{... | collective-permute-start | bytes 2359304 | tf_op jit(solution)/shard_map/ppermute | solution.py:381
  111.2 19.3 %collective-permute-start.24 = (bf16[4,192,512]{2,1,0:T(8,128)(2,1)S(1)}, bf16[4,192,512]{2,1,0:T(8,128)(2,1)S(1)}, u32[]{:S(2)}, u32[]{:S(2)}) collective-permute-start(bf16[4,192,512]{2,1,0:T(8,128)(2,1)S(1)} %get-tuple-element.143), channel_id=1, source_target_pairs={{0,16},{1,5},{2,18},{3,7},{4,20},{5,1},{6,22},{7,3},{8,24},{9,13},... | collective-permute-start | bytes 2359304 | tf_op jit(solution)/shard_map/ppermute | solution.py:381
  112.4 18.5 %collective-permute-start.25 = (bf16[4,192,512]{2,1,0:T(8,128)(2,1)S(1)}, bf16[4,192,512]{2,1,0:T(8,128)(2,1)S(1)}, u32[]{:S(2)}, u32[]{:S(2)}) collective-permute-start(bf16[4,192,512]{2,1,0:T(8,128)(2,1)S(1)} %get-tuple-element.144), channel_id=1, source_target_pairs={{0,24},{1,7},{2,26},{3,1},{4,28},{5,3},{6,30},{7,5},{8,0},{9,15},{... | collective-permute-start | bytes 2359304 | tf_op jit(solution)/shard_map/ppermute | solution.py:381
  127.0 25.8 %copy-start.3 = (f32[1,64,512]{2,1,0:T(8,128)S(1)}, f32[1,64,512]{2,1,0:T(8,128)}, u32[]{:S(2)}) copy-start(f32[1,64,512]{2,1,0:T(8,128)} %param.17) | copy-start | bytes 393220
  127.0 25.8 %copy-start.4 = (f32[1,64,512]{2,1,0:T(8,128)S(1)}, f32[1,64,512]{2,1,0:T(8,128)}, u32[]{:S(2)}) copy-start(f32[1,64,512]{2,1,0:T(8,128)} %param.18) | copy-start | bytes 393220
  127.0 25.8 %copy-start.5 = (f32[1,16,2048]{2,1,0:T(8,128)S(1)}, f32[1,16,2048]{2,1,0:T(8,128)}, u32[]{:S(2)}) copy-start(f32[1,16,2048]{2,1,0:T(8,128)} %param.19) | copy-start | bytes 393220
  133.2 3.6 %collective-permute-start.29 = (f32[3,16,128]{2,1,0:T(8,128)S(1)}, f32[3,16,128]{2,1,0:T(8,128)S(1)}, u32[]{:S(2)}, u32[]{:S(2)}) collective-permute-start(f32[3,16,128]{2,1,0:T(8,128)S(1)} %gram.1), channel_id=1, source_target_pairs={{0,6},{1,7},{2,0},{3,1},{4,2},{5,3},{6,4},{7,5},{8,14},{9,15},{10,... | collective-permute-start | bytes 73736 | tf_op jit(solution)/shard_map/ppermute | solution.py:381
  135.6 3.9 %collective-permute-start.28 = (f32[3,16,128]{2,1,0:T(8,128)S(1)}, f32[3,16,128]{2,1,0:T(8,128)S(1)}, u32[]{:S(2)}, u32[]{:S(2)}) collective-permute-start(f32[3,16,128]{2,1,0:T(8,128)S(1)} %gram.1), channel_id=1, source_target_pairs={{0,2},{1,3},{2,4},{3,5},{4,6},{5,7},{6,0},{7,1},{8,10},{9,11},{10,... | collective-permute-start | bytes 73736 | tf_op jit(solution)/shard_map/ppermute | solution.py:381
  135.6 4.2 %collective-permute-start.27 = (f32[3,16,128]{2,1,0:T(8,128)S(1)}, f32[3,16,128]{2,1,0:T(8,128)S(1)}, u32[]{:S(2)}, u32[]{:S(2)}) collective-permute-start(f32[3,16,128]{2,1,0:T(8,128)S(1)} %gram.1), channel_id=1, source_target_pairs={{0,4},{1,5},{2,6},{3,7},{4,0},{5,1},{6,2},{7,3},{8,12},{9,13},{10,... | collective-permute-start | bytes 73736 | tf_op jit(solution)/shard_map/ppermute | solution.py:381
  139.8 3.8 %collective-permute-start.32 = (f32[3,16,128]{2,1,0:T(8,128)S(1)}, f32[3,16,128]{2,1,0:T(8,128)S(1)}, u32[]{:S(2)}, u32[]{:S(2)}) collective-permute-start(f32[3,16,128]{2,1,0:T(8,128)S(1)} %add_add_fusion.1), channel_id=1, source_target_pairs={{0,24},{1,25},{2,26},{3,27},{4,28},{5,29},{6,30},{7,31},{8,0},{9,1... | collective-permute-start | bytes 73736 | tf_op jit(solution)/shard_map/ppermute | solution.py:381
  141.9 3.9 %collective-permute-start.31 = (f32[3,16,128]{2,1,0:T(8,128)S(1)}, f32[3,16,128]{2,1,0:T(8,128)S(1)}, u32[]{:S(2)}, u32[]{:S(2)}) collective-permute-start(f32[3,16,128]{2,1,0:T(8,128)S(1)} %add_add_fusion.1), channel_id=1, source_target_pairs={{0,8},{1,9},{2,10},{3,11},{4,12},{5,13},{6,14},{7,15},{8,16},{9,17... | collective-permute-start | bytes 73736 | tf_op jit(solution)/shard_map/ppermute | solution.py:381
  141.9 4.2 %collective-permute-start.30 = (f32[3,16,128]{2,1,0:T(8,128)S(1)}, f32[3,16,128]{2,1,0:T(8,128)S(1)}, u32[]{:S(2)}, u32[]{:S(2)}) collective-permute-start(f32[3,16,128]{2,1,0:T(8,128)S(1)} %add_add_fusion.1), channel_id=1, source_target_pairs={{0,16},{1,17},{2,18},{3,19},{4,20},{5,21},{6,22},{7,23},{8,24},{9,... | collective-permute-start | bytes 73736 | tf_op jit(solution)/shard_map/ppermute | solution.py:381
  146.1 6.7 %collective-permute-start.33 = (f32[3,16,128]{2,1,0:T(8,128)S(1)}, f32[3,16,128]{2,1,0:T(8,128)S(1)}, u32[]{:S(2)}, u32[]{:S(2)}) collective-permute-start(f32[3,16,128]{2,1,0:T(8,128)S(1)} %add_add_fusion), channel_id=1, source_target_pairs={{0,1},{1,0},{2,3},{3,2},{4,5},{5,4},{6,7},{7,6},{8,9},{9,8},{10,11... | collective-permute-start | bytes 73736 | tf_op jit(solution)/shard_map/ppermute | solution.py:381

commit v8 on v7

--- a/solution.py
+++ b/solution.py
@@ -49,7 +49,7 @@
     return jnp.broadcast_to(row, (128, row.shape[1])).T
 
 
-def pick_rows(ids_rows, pools):
+def pick_rows(ids_rows, pools, stacked=False):
     n_ids, n_pool = len(ids_rows), len(pools)
 
     def body(*refs):
@@ -61,10 +61,15 @@
             for j in range(POOL // 128):
                 hot[:, 128 * j : 128 * (j + 1)] = jnp.where(named == lane + 128 * j, 1.0, 0.0).astype(BF16)
             for a in range(n_pool):
-                rows = jnp.dot(hot[...], src[a][...], preferred_element_type=F32)
-                out[k * n_pool + a][...] = rows.astype(BF16)
+                rows = jnp.dot(hot[...], src[a][...], preferred_element_type=F32).astype(BF16)
+                if stacked:
+                    out[k][TOK_DEV * a : TOK_DEV * (a + 1), :] = rows
+                else:
+                    out[k * n_pool + a][...] = rows
 
     shapes = [struct((TOK_DEV, SLICE), BF16)] * (n_ids * n_pool)
+    if stacked:
+        shapes = [struct((n_pool * TOK_DEV, SLICE), BF16)] * n_ids
     return call(
         body,
         "pick_rows",
@@ -94,12 +99,12 @@
 def forward(tokens, weights):
     def body(x0, x1, x2, x3, w, hidden_t, gate_factor, act_out, xt, acc, hid):
         for k, x in enumerate((x0, x1, x2, x3)):
-            part = jnp.dot(x[...], in_up_block(w, slice_of(k)), preferred_element_type=F32)
+            part = jnp.dot(x[0:TOK_DEV, :], in_up_block(w, slice_of(k)), preferred_element_type=F32)
             if k == 0:
                 acc[...] = part
             else:
                 acc[...] += part
-            xt[k] = x[...].T
+            xt[k] = x[0:TOK_DEV, :].T
 
         @pl.loop(0, TOK_DEV // 64)
         def _(i):
@@ -135,7 +140,8 @@
     for k, c in zip(ks, cots):
         for j in range(SLICE // 128):
             cols = slice(128 * j, 128 * (j + 1))
-            scaled[:, cols] = (scale * c[:, cols].astype(F32)).astype(BF16)
+            rows = slice(c.shape[0] - TOK_DEV, c.shape[0])
+            scaled[:, cols] = (scale * c[rows, cols].astype(F32)).astype(BF16)
         part = lax.dot_general(scaled[...], down_block(w, slice_of(k)), NT, preferred_element_type=F32)
         if first and k == ks[0]:
             hg[...] = part
@@ -159,13 +165,13 @@
     )
 
 
-def backward(cots, route, hidden_t, early, downs, gate_factor, act, xt, weights):
-    def body(c1, c3, route_ref, hid_t, hg0, down_ref, factor, act_ref, xt_ref, w, keep, send, both, hg, scaled):
+def backward_down(cots, route, hidden_t, early, downs, weights):
+    def body(c1, c3, route_ref, hid_t, hg0, down_ref, w, keep, send, hg, scaled):
         first = lax.axis_index("dp") % 2 == 0
 
         def put(k, down):
             down = down.reshape(N_CHIP, 2, 16, SLICE)
-            rows = pl.ds(pl.multiple_of(128 + 16 * slice_of(k), 16), 16)
+            rows = pl.ds(pl.multiple_of(16 * slice_of(k), 16), 16)
             keep[:, rows, :] = jnp.where(first, down[:, 0], down[:, 1])
             send[:, rows, :] = jnp.where(first, down[:, 1], down[:, 0])
 
@@ -173,6 +179,18 @@
         of_cotangents(False, (1, 3), (c1, c3), route_ref, hid_t, w, hg, scaled, put)
         put(0, down_ref[0])
         put(2, down_ref[1])
+
+    half = struct((N_CHIP, 64, SLICE), BF16)
+    shapes = [half, half, struct((TOK_DEV, H), F32)]
+    scratch = [pltpu.VMEM((TOK_DEV, SLICE), BF16)]
+    return call(body, "backward_down", 7, shapes, 2 * TOK_DEV * D * H, 10 * MIB, scratch)(
+        *cots, route, hidden_t, early, downs, weights
+    )
+
+
+def backward_in(hidden_grad, gate_factor, act, xt):
+    def body(hg, factor, act_ref, xt_ref, keep, send, both):
+        first = lax.axis_index("dp") % 2 == 0
 
         @pl.loop(0, TOK_DEV // 64)
         def _(i):
@@ -191,20 +209,9 @@
                 keep[chips, 64 * a : 64 * (a + 1), :] = jnp.where(first, own, other)
                 send[chips, 64 * a : 64 * (a + 1), :] = jnp.where(first, other, own)
 
-    shapes = [
-        struct((N_CHIP, ROWS, SLICE), BF16),
-        struct((N_CHIP, ROWS, SLICE), BF16),
-        struct((TOK_DEV, 2 * H), BF16),
-    ]
-    return call(
-        body,
-        "backward",
-        10,
-        shapes,
-        6 * TOK_DEV * D * H,
-        20 * MIB,
-        [pltpu.VMEM((TOK_DEV, H), F32), pltpu.VMEM((TOK_DEV, SLICE), BF16)],
-    )(*cots, route, hidden_t, early, downs, gate_factor, act, xt, weights)
+    half = struct((N_CHIP, 128, SLICE), BF16)
+    shapes = [half, half, struct((TOK_DEV, 2 * H), BF16)]
+    return call(body, "backward_in", 4, shapes, 4 * TOK_DEV * D * H, 10 * MIB)(hidden_grad, gate_factor, act, xt)
 
 
 def slot_gradients(both, weights):
@@ -217,13 +224,17 @@
     return call(body, "slot_gradients", 2, shapes, 4 * TOK_DEV * D * H, 9 * MIB)(both, weights)
 
 
+def rows_of(of_in, of_down, q, m):
+    return of_down[q] if m == 2 else of_in[q, 64 * m : 64 * (m + 1), :]
+
+
 def pair_moments(own, other):
-    def body(a_ref, b_ref, out):
+    def body(a_in, a_down, b_in, b_down, out):
         def step(q, sums):
             new = []
             for m in range(3):
-                a = a_ref[q, 64 * m : 64 * (m + 1), :].astype(F32)
-                b = b_ref[q, 64 * m : 64 * (m + 1), :].astype(F32)
+                a = rows_of(a_in, a_down, q, m).astype(F32)
+                b = rows_of(b_in, b_down, q, m).astype(F32)
                 for t in (a * b, a * a, b * b):
                     t = jnp.sum(t.reshape(8, 8, SLICE), axis=0)
                     new.append(t[:, :128] + t[:, 128:256] + t[:, 256:384] + t[:, 384:])
@@ -233,11 +244,11 @@
         for j in range(9):
             out[j] = sums[j]
 
-    return call(body, "pair_moments", 2, struct((9, 8, 128), F32), 9 * 2**20, 6 * MIB)(own, other)
+    return call(body, "pair_moments", 4, struct((9, 8, 128), F32), 9 * 2**20, 6 * MIB)(*own, *other)
 
 
 def pair_merge(own, other, mine, theirs):
-    def body(a_ref, b_ref, m_ref, t_ref, *out):
+    def body(a_in, a_down, b_in, b_down, m_ref, t_ref, *out):
         coefs = []
         for m in range(3):
             inner = jnp.sum(m_ref[3 * m] + t_ref[3 * m], keepdims=True)
@@ -255,11 +266,12 @@
                 q = jnp.where(c == 0, 4 * j + first, 4 * first + j)
                 for m in range(3):
                     rows = slice(64 * m, 64 * (m + 1))
-                    a, b = a_ref[q, rows, :].astype(F32), b_ref[q, rows, :].astype(F32)
+                    a = rows_of(a_in, a_down, q, m).astype(F32)
+                    b = rows_of(b_in, b_down, q, m).astype(F32)
                     out[k][j, rows, :] = (coefs[m][0] * a + coefs[m][1] * b).astype(BF16)
 
-    return call(body, "pair_merge", 4, [struct((4, ROWS, SLICE), BF16)] * 4, 9 * 2**20, 9 * MIB)(
-        own, other, mine, theirs
+    return call(body, "pair_merge", 6, [struct((4, ROWS, SLICE), BF16)] * 4, 9 * 2**20, 9 * MIB)(
+        *own, *other, mine, theirs
     )
 
 
@@ -443,8 +455,13 @@
     return to
 
 
+def to_others(blocks, turn):
+    out = {k: shift(blocks[k], "dp", along(turn, k)) for k in (2, 1, 3)}
+    return [out[1], out[2], out[3]]
+
+
 def spread(block, turn):
-    return [shift(block, "dp", along(turn, k)) for k in (1, 2, 3)]
+    return to_others([block] * 4, turn)
 
 
 def place(turn):
@@ -510,15 +527,16 @@
     packed = pack(*shards)
     blocks = spread(packed, 0)
     x[1], x[3] = around_y(x[1], 1), around_y(x[3], 3)
-    x[2], c[2] = picked(2, pool_tokens), picked(2, pool_cotangent)
-    ids, blocks, x[1:], c[2] = tie((ids, blocks, x[1:], c[2]))
+    (x[2],) = pick_rows(ids[2:3], [pool_tokens, pool_cotangent], stacked=True)
+    ids, blocks, x[1:] = tie((ids, blocks, x[1:]))
 
     block = bundle((packed, *blocks))
     blocks = spread(block, 1)
-    x[2], c[2] = around_y(x[2], 2), around_y(c[2], 2)
+    x[2] = c[2] = around_y(x[2], 2)
     c[1], c[3] = picked(1, pool_cotangent), picked(3, pool_cotangent)
     x[0], c[0] = pick_rows(ids[:1], [pool_tokens, pool_cotangent])
-    blocks, x, c = tie((blocks, x, c))
+    blocks, x, c = tie((blocks, x, [c[0], c[1], c[3]]))
+    c = [c[0], c[1], x[2], c[2]]
 
     mine = half_of_weights((block, *blocks))
     weights = whole_weights(mine, other_core(mine))
@@ -526,21 +544,21 @@
 
     hidden_t, gate_factor, act, xt = forward(x, weights)
     early, downs = backward_early((c[0], c[2]), route_weights, hidden_t, weights)
-    keep, send, both = backward(
-        (c[1], c[3]), route_weights, hidden_t, early, downs, gate_factor, act, xt, weights
-    )
-    received = other_core(send)
+    keep_down, send_down, hidden_grad = backward_down((c[1], c[3]), route_weights, hidden_t, early, downs, weights)
+    keep_in, send_in, both = backward_in(hidden_grad, gate_factor, act, xt)
+    received_down, both = tie((other_core(send_down), both))
+    keep, received = (keep_in, keep_down), (other_core(send_in), received_down)
     slots = slot_gradients(both, weights)
     received, slots = lax.optimization_barrier((received, list(slots)))
 
     mine = pair_moments(keep, received)
     sent = pair_merge(keep, received, mine, other_core(mine))
-    parts = [sent[0]] + [shift(sent[k], "dp", along(0, k)) for k in (1, 2, 3)]
+    parts = [sent[0], *to_others(sent, 0)]
     back = [slots[0], around_y(slots[1], 3), None, around_y(slots[3], 1)]
-    parts, back[1], back[3], slots[2] = tie((parts, back[1], back[3], slots[2]))
+    parts, back[1], back[3] = tie((parts, back[1], back[3]))
+    sent, slots[2] = tie((turn_over(parts), slots[2]))
+    parts = [sent[0], *to_others(sent, 1)]
     back[2] = around_y(slots[2], 2)
-    sent = turn_over(parts)
-    parts = [sent[0]] + [shift(sent[k], "dp", along(1, k)) for k in (1, 2, 3)]
     pool_grad = scatter_rows(ids, back)
     parts, pool_grad = tie((parts, pool_grad))
     products = sum_dp(gram(parts))

time: 155 us -> 155 us (level)
  waiting for transfers between devices: 61.4 us -> 67.3 us
  starting transfers between devices: 54.7 us -> 49.7 us
    ppermute x34, waiting for transfers between devices: 61.4 us -> 67.3 us  [shift(): lax.ppermute(block, axis, [(i, to(i)) for i in range(lax.axis_size(axis))])]
    ppermute x34, starting transfers between devices: 54.7 us -> 49.7 us  [shift(): lax.ppermute(block, axis, [(i, to(i)) for i in range(lax.axis_size(axis))])]
    pallas_call x7 -> x6, Pallas kernels: 11.1 us -> 10.8 us  [pick_rows(): call(body, 'pick_rows', n_ids + n_pool, shapes, 2 * TOK_DEV * POOL * SLIC...]
    pallas_call x3 -> x4, Pallas kernels: 6.24 us -> 6.1 us  [the longest x1 2.56 us: backward_in(): call(body, 'backward_in', 4, shapes, 4 * TOK_DEV * D * H, 10 * MIB)]
where the time goes in v8:
time: 155 us
  waiting for transfers between devices  67.3 us (43%)
  starting transfers between devices  49.7 us (32%)
  Pallas kernels  35.4 us (23%)
  local copies, waits for them, and re-layouts  1.76 us (1%)
    ppermute x34, waiting for transfers between devices, shift(): lax.ppermute(block, axis, [(i, to(i)) for i in range(lax.axis_size(axis))])  67.3 us
    ppermute x34, starting transfers between devices, shift(): lax.ppermute(block, axis, [(i, to(i)) for i in range(lax.axis_size(axis))])  49.7 us
    pallas_call x6, Pallas kernels, pick_rows(): call(body, 'pick_rows', n_ids + n_pool, shapes, 2 * TOK_DEV * POOL * SLIC...  10.8 us
    pallas_call x1, Pallas kernels, scatter_rows(): pl.pallas_call(body, name='scatter_rows', grid=(POOL // block,), out_shap...  5.97 us
  transfers between devices with their start and end apart: 34, of which 21 were waited for; matrix products, arithmetic and copies ran while one was open for 0% of the time, Pallas kernels for 16%

profile of v8, /device:TPU:1, one launch (start us, length us, event | category | flops | bytes accessed | tf_op | source)
XLA Modules:
  0.0 155.2 jit_solution(10104755545525415664)
XLA Ops:
  0.6 2.2 %collective-permute-start.2 = (s32[1,512]{1,0:T(1,128)}, s32[1,512]{1,0:T(1,128)S(1)}, u32[]{:S(2)}, u32[]{:S(2)}) collective-permute-start(s32[1,512]{1,0:T(1,128)} %i0), channel_id=1, source_target_pairs={{0,32},{32,64},{64,96},{96,0},{1,33},{33,65},{65,97},{97,1},{2,34}... | collective-permute-start | bytes 6152 | tf_op jit(solution)/shard_map/ppermute | solution.py:393
  2.8 2.6 %collective-permute-start.1 = (s32[1,512]{1,0:T(1,128)}, s32[1,512]{1,0:T(1,128)S(1)}, u32[]{:S(2)}, u32[]{:S(2)}) collective-permute-start(s32[1,512]{1,0:T(1,128)} %i0), channel_id=1, source_target_pairs={{0,64},{32,96},{64,0},{96,32},{1,65},{33,97},{65,1},{97,33},{2,66}... | collective-permute-start | bytes 6152 | tf_op jit(solution)/shard_map/ppermute | solution.py:393
  6.5 1.6 %copy-done.8 = bf16[2048,512]{1,0:T(8,128)(2,1)S(1)} copy-done((bf16[2048,512]{1,0:T(8,128)(2,1)S(1)}, bf16[2048,512]{1,0:T(8,128)(2,1)}, u32[]{:S(2)}) %copy-start.8) | copy-done | bytes 2097176
  8.1 1.4 pick_rows.7
  9.6 1.4 pick_rows.6
  11.6 2.3 %collective-permute-start.7 = (bf16[512,512]{1,0:T(8,128)(2,1)S(1)}, bf16[512,512]{1,0:T(8,128)(2,1)S(1)}, u32[]{:S(2)}, u32[]{:S(2)}) collective-permute-start(bf16[512,512]{1,0:T(8,128)(2,1)S(1)} %pick_rows.7), channel_id=1, source_target_pairs={{0,96},{32,0},{64,32},{96,64},{1,97},{33,1},{65,33},{97,65},{2,98}... | collective-permute-start | bytes 1572872 | tf_op jit(solution)/shard_map/ppermute | solution.py:393
  14.4 2.5 %collective-permute-start.5 = (bf16[96,1024]{1,0:T(8,128)(2,1)S(1)}, bf16[96,1024]{1,0:T(8,128)(2,1)S(1)}, u32[]{:S(2)}, u32[]{:S(2)}) collective-permute-start(bf16[96,1024]{1,0:T(8,128)(2,1)S(1)} %pack.1.refs_0_), channel_id=1, source_target_pairs={{0,6},{1,25},{2,0},{3,27},{4,2},{5,29},{6,4},{7,31},{8,14},{9,1},{... | collective-permute-start | bytes 589832 | tf_op jit(solution)/shard_map/ppermute | solution.py:393
  18.1 2.5 %pick_rows.8 = bf16[1024,512]{1,0:T(8,128)(2,1)S(1)} custom-call(s32[1,512]{1,0:T(1,128)S(1)} %collective-permute-done.1.refs_0_.i2, bf16[2048,512]{1,0:T(8,128)(2,1)S(1)} %copy-done.8, bf16[2048,512]{1,0:T(8,128)(2,1)S(1)} %copy-done.7), custom_call_target="tpu_custom_call" | custom-call | flops 2147483648 | bytes 3145728 | tf_op jit(solution)/shard_map/pick_rows/pallas_call | solution.py:73
  21.7 1.4 collective-permute-done.4.refs_2_
  23.1 2.3 %collective-permute-done.3.refs_1_ = bf16[96,1024]{1,0:T(8,128)(2,1)S(1)} collective-permute-done((bf16[96,1024]{1,0:T(8,128)(2,1)S(1)}, bf16[96,1024]{1,0:T(8,128)(2,1)S(1)}, u32[]{:S(2)}, u32[]{:S(2)}) %collective-permute-start.3) | collective-permute-done | bytes 196640 | tf_op jit(solution)/shard_map/ppermute | solution.py:393
  25.5 3.8 %collective-permute-start.10 = (bf16[4,96,1024]{2,1,0:T(8,128)(2,1)S(1)}, bf16[4,96,1024]{2,1,0:T(8,128)(2,1)S(1)}, u32[]{:S(2)}, u32[]{:S(2)}) collective-permute-start(bf16[4,96,1024]{2,1,0:T(8,128)(2,1)S(1)} %bundle.1.refs_0_), channel_id=1, source_target_pairs={{0,24},{1,7},{2,26},{3,1},{4,28},{5,3},{6,30},{7,5},{8,0},{9,15},{... | collective-permute-start | bytes 2359304 | tf_op jit(solution)/shard_map/ppermute | solution.py:393
  30.0 1.4 pick_rows.10
  31.5 1.4 pick_rows.11
  33.0 2.5 %pick_rows.9 = (bf16[512,512]{1,0:T(8,128)(2,1)S(1)}, bf16[512,512]{1,0:T(8,128)(2,1)S(1)}) custom-call(s32[1,512]{1,0:T(1,128)S(1)} %copy-done.10, bf16[2048,512]{1,0:T(8,128)(2,1)S(1)} %copy-done.9, bf16[2048,512]{1,0:T(8,128)(2,1)S(1)} %copy-done.7), custom_call_target="tpu_custom_call" | custom-call | flops 2147483648 | bytes 3145728 | tf_op jit(solution)/shard_map/pick_rows/pallas_call | solution.py:73
  35.6 11.1 %collective-permute-done.10.refs_3_ = bf16[4,96,1024]{2,1,0:T(8,128)(2,1)S(1)} collective-permute-done((bf16[4,96,1024]{2,1,0:T(8,128)(2,1)S(1)}, bf16[4,96,1024]{2,1,0:T(8,128)(2,1)S(1)}, u32[]{:S(2)}, u32[]{:S(2)}) %collective-permute-start.10) | collective-permute-done | bytes 786464 | tf_op jit(solution)/shard_map/ppermute | solution.py:393
  46.7 3.4 %collective-permute-done.8.refs_1_ = bf16[4,96,1024]{2,1,0:T(8,128)(2,1)S(1)} collective-permute-done((bf16[4,96,1024]{2,1,0:T(8,128)(2,1)S(1)}, bf16[4,96,1024]{2,1,0:T(8,128)(2,1)S(1)}, u32[]{:S(2)}, u32[]{:S(2)}) %collective-permute-start.8) | collective-permute-done | bytes 786464 | tf_op jit(solution)/shard_map/ppermute | solution.py:393
  50.3 4.7 %collective-permute-start.14 = (bf16[16,96,1024]{2,1,0:T(8,128)(2,1)S(1)}, bf16[16,96,1024]{2,1,0:T(8,128)(2,1)S(1)}, u32[]{:S(2)}, u32[]{:S(2)}) collective-permute-start(bf16[16,96,1024]{2,1,0:T(8,128)(2,1)S(1)} %half_of_weights.1.a), channel_id=1, source_target_pairs={{0,1},{1,0},{2,3},{3,2},{4,5},{5,4},{6,7},{7,6},{8,9},{9,8},{10,11... | collective-permute-start | bytes 9437192 | tf_op jit(solution)/shard_map/ppermute | solution.py:393
  55.1 1.1 collective-permute-start.12
  56.2 1.6 %collective-permute-start.13 = (bf16[512,512]{1,0:T(8,128)(2,1)S(1)}, bf16[512,512]{1,0:T(8,128)(2,1)S(1)}, u32[]{:S(2)}, u32[]{:S(2)}) collective-permute-start(bf16[512,512]{1,0:T(8,128)(2,1)S(1)} %pick_rows.11), channel_id=1, source_target_pairs={{0,96},{32,0},{64,32},{96,64},{1,97},{33,1},{65,33},{97,65},{2,98}... | collective-permute-start | bytes 1572872 | tf_op jit(solution)/shard_map/ppermute | solution.py:393
  57.7 2.6 %collective-permute-done.14.b = bf16[16,96,1024]{2,1,0:T(8,128)(2,1)S(1)} collective-permute-done((bf16[16,96,1024]{2,1,0:T(8,128)(2,1)S(1)}, bf16[16,96,1024]{2,1,0:T(8,128)(2,1)S(1)}, u32[]{:S(2)}, u32[]{:S(2)}) %collective-permute-start.14) | collective-permute-done | bytes 3145760 | tf_op jit(solution)/shard_map/ppermute | solution.py:393
  60.8 3.0 %forward.1 = (bf16[512,512]{1,0:T(8,128)(2,1)S(1)}, f32[512,512]{1,0:T(8,128)S(1)}, f32[512,512]{1,0:T(8,128)S(1)}, bf16[4,512,512]{2,1,0:T(8,128)(2,1)S(1)}) custom-call(bf16[512,512]{1,0:T(8,128)(2,1)S(1)} %get-tuple-element.114.x0, bf16[512,512]{1,0:T(8,128)(2,1)S(1)} %collective-permute-done.6.x1, bf16[1024,512]{1,0:T(8,128)(2,1)S(1)} %collective-permute-done.11.x2.c2, ...), custom_call_target="tpu_custom_call" | custom-call | flops 2147483648 | bytes 10485760 | tf_op jit(solution)/shard_map/forward/pallas_call | solution.py:127
  63.8 1.4 backward_early.1
  65.3 4.5 %collective-permute-done.12.c1 = bf16[512,512]{1,0:T(8,128)(2,1)S(1)} collective-permute-done((bf16[512,512]{1,0:T(8,128)(2,1)S(1)}, bf16[512,512]{1,0:T(8,128)(2,1)S(1)}, u32[]{:S(2)}, u32[]{:S(2)}) %collective-permute-start.12) | collective-permute-done | bytes 524320 | tf_op jit(solution)/shard_map/ppermute | solution.py:393
  69.8 1.5 backward_down.1
  71.3 2.6 %backward_in.1 = (bf16[16,128,512]{2,1,0:T(8,128)(2,1)S(1)}, bf16[16,128,512]{2,1,0:T(8,128)(2,1)S(1)}, bf16[512,1024]{1,0:T(8,128)(2,1)S(1)}) custom-call(f32[512,512]{1,0:T(8,128)S(1)} %get-tuple-element.125.hg, f32[512,512]{1,0:T(8,128)S(1)} %get-tuple-element.126.factor, f32[512,512]{1,0:T(8,128)S(1)} %get-tuple-element.127.act_ref, ...), custom_call_target="tpu_custom_call" | custom-call | flops 2147483648 | bytes 10485760 | tf_op jit(solution)/shard_map/backward_in/pallas_call | solution.py:214
  75.0 5.2 %collective-permute-done.16.b_down = bf16[16,64,512]{2,1,0:T(8,128)(2,1)S(1)} collective-permute-done((bf16[16,64,512]{2,1,0:T(8,128)(2,1)S(1)}, bf16[16,64,512]{2,1,0:T(8,128)(2,1)S(1)}, u32[]{:S(2)}, u32[]{:S(2)}) %collective-permute-start.16) | collective-permute-done | bytes 1048608 | tf_op jit(solution)/shard_map/ppermute | solution.py:393
  80.2 2.4 %slot_gradients.1 = (bf16[512,512]{1,0:T(8,128)(2,1)S(1)}, bf16[512,512]{1,0:T(8,128)(2,1)S(1)}, bf16[512,512]{1,0:T(8,128)(2,1)S(1)}, bf16[512,512]{1,0:T(8,128)(2,1)S(1)}) custom-call(bf16[512,1024]{1,0:T(8,128)(2,1)S(1)} %get-tuple-element.135.both_ref, bf16[32,96,1024]{2,1,0:T(8,128)(2,1)S(1)} %whole_weights.1.w), custom_call_target="tpu_custom_call" | custom-call | flops 2147483648 | bytes 9437184 | tf_op jit(solution)/shard_map/slot_gradients/pallas_call | solution.py:224
  84.6 1.3 pair_merge.1
  86.0 1.5 collective-permute-start.19
  87.5 1.2 collective-permute-start.20
  88.7 2.6 %collective-permute-start.21 = (bf16[512,512]{1,0:T(8,128)(2,1)S(1)}, bf16[512,512]{1,0:T(8,128)(2,1)S(1)}, u32[]{:S(2)}, u32[]{:S(2)}) collective-permute-start(bf16[512,512]{1,0:T(8,128)(2,1)S(1)} %get-tuple-element.146), channel_id=1, source_target_pairs={{0,96},{32,0},{64,32},{96,64},{1,97},{33,1},{65,33},{97,65},{2,98}... | collective-permute-start | bytes 1572872 | tf_op jit(solution)/shard_map/ppermute | solution.py:393
  91.2 8.6 %collective-permute-done.21.g1 = bf16[512,512]{1,0:T(8,128)(2,1)S(1)} collective-permute-done((bf16[512,512]{1,0:T(8,128)(2,1)S(1)}, bf16[512,512]{1,0:T(8,128)(2,1)S(1)}, u32[]{:S(2)}, u32[]{:S(2)}) %collective-permute-start.21) | collective-permute-done | bytes 524320 | tf_op jit(solution)/shard_map/ppermute | solution.py:393
  99.8 3.1 %collective-permute-done.22.g3 = bf16[512,512]{1,0:T(8,128)(2,1)S(1)} collective-permute-done((bf16[512,512]{1,0:T(8,128)(2,1)S(1)}, bf16[512,512]{1,0:T(8,128)(2,1)S(1)}, u32[]{:S(2)}, u32[]{:S(2)}) %collective-permute-start.22) | collective-permute-done | bytes 524320 | tf_op jit(solution)/shard_map/ppermute | solution.py:393
  103.0 3.8 %collective-permute-done.18.refs_1_ = bf16[4,192,512]{2,1,0:T(8,128)(2,1)S(1)} collective-permute-done((bf16[4,192,512]{2,1,0:T(8,128)(2,1)S(1)}, bf16[4,192,512]{2,1,0:T(8,128)(2,1)S(1)}, u32[]{:S(2)}, u32[]{:S(2)}) %collective-permute-start.18) | collective-permute-done | bytes 786464 | tf_op jit(solution)/shard_map/ppermute | solution.py:393
  107.6 2.1 %collective-permute-start.26 = (bf16[512,512]{1,0:T(8,128)(2,1)S(1)}, bf16[512,512]{1,0:T(8,128)(2,1)S(1)}, u32[]{:S(2)}, u32[]{:S(2)}) collective-permute-start(bf16[512,512]{1,0:T(8,128)(2,1)S(1)} %get-tuple-element.164), channel_id=1, source_target_pairs={{0,64},{32,96},{64,0},{96,32},{1,65},{33,97},{65,1},{97,33},{2,66}... | collective-permute-start | bytes 1572872 | tf_op jit(solution)/shard_map/ppermute | solution.py:393
  109.7 2.7 %collective-permute-start.24 = (bf16[4,192,512]{2,1,0:T(8,128)(2,1)S(1)}, bf16[4,192,512]{2,1,0:T(8,128)(2,1)S(1)}, u32[]{:S(2)}, u32[]{:S(2)}) collective-permute-start(bf16[4,192,512]{2,1,0:T(8,128)(2,1)S(1)} %get-tuple-element.159), channel_id=1, source_target_pairs={{0,16},{1,5},{2,18},{3,7},{4,20},{5,1},{6,22},{7,3},{8,24},{9,13},... | collective-permute-start | bytes 2359304 | tf_op jit(solution)/shard_map/ppermute | solution.py:393
  113.1 7.7 %collective-permute-done.26.g2 = bf16[512,512]{1,0:T(8,128)(2,1)S(1)} collective-permute-done((bf16[512,512]{1,0:T(8,128)(2,1)S(1)}, bf16[512,512]{1,0:T(8,128)(2,1)S(1)}, u32[]{:S(2)}, u32[]{:S(2)}) %collective-permute-start.26) | collective-permute-done | bytes 524320 | tf_op jit(solution)/shard_map/ppermute | solution.py:393
  120.8 6.0 %scatter_rows.1 = f32[2048,512]{1,0:T(8,128)} custom-call(s32[1,512]{1,0:T(1,128)S(1)} %copy-done.10, s32[1,512]{1,0:T(1,128)S(1)} %collective-permute-done.refs_0_.i1, s32[1,512]{1,0:T(1,128)S(1)} %collective-permute-done.1.refs_0_.i2, s32[1,512]{1,0:T(1,128)S(1)} %collective-permute-done.2.refs_0_.i3, bf16[512,512]{1,0:T(8,128)(2,1)S(1)} %get-tuple-element.162.g0, ...), custom_call_target="tpu_custom_call" | custom-call | flops 4294967296 | bytes 6291456 | tf_op jit(solution)/shard_map/scatter_rows/pallas_call | solution.py:378
  126.8 3.7 %collective-permute-done.24.refs_2_.x2 = bf16[4,192,512]{2,1,0:T(8,128)(2,1)S(1)} collective-permute-done((bf16[4,192,512]{2,1,0:T(8,128)(2,1)S(1)}, bf16[4,192,512]{2,1,0:T(8,128)(2,1)S(1)}, u32[]{:S(2)}, u32[]{:S(2)}) %collective-permute-start.24) | collective-permute-done | bytes 786464 | tf_op jit(solution)/shard_map/ppermute | solution.py:393
  131.1 2.3 %gram.1 = f32[3,16,128]{2,1,0:T(8,128)S(1)} custom-call(bf16[4,192,512]{2,1,0:T(8,128)(2,1)S(1)} %get-tuple-element.166.refs_0_.x0, bf16[4,192,512]{2,1,0:T(8,128)(2,1)S(1)} %collective-permute-done.23.refs_1_.x1, bf16[4,192,512]{2,1,0:T(8,128)(2,1)S(1)} %collective-permute-done.24.refs_2_.x2, bf16[4,192,512]{2,1,0:T(8,128)(2,1)S(1)} %collective-permute-done.25.refs_3_.x3), custom_call_target="tpu_custom_call" | custom-call | flops 805306368 | bytes 3145728 | tf_op jit(solution)/shard_map/gram/pallas_call | solution.py:315
  133.4 2.4 %collective-permute-start.29 = (f32[3,16,128]{2,1,0:T(8,128)S(1)}, f32[3,16,128]{2,1,0:T(8,128)S(1)}, u32[]{:S(2)}, u32[]{:S(2)}) collective-permute-start(f32[3,16,128]{2,1,0:T(8,128)S(1)} %gram.1), channel_id=1, source_target_pairs={{0,6},{1,7},{2,0},{3,1},{4,2},{5,3},{6,4},{7,5},{8,14},{9,15},{10,... | collective-permute-start | bytes 73736 | tf_op jit(solution)/shard_map/ppermute | solution.py:393
  135.8 1.2 collective-permute-start.27
  137.0 2.7 %collective-permute-done.28 = f32[3,16,128]{2,1,0:T(8,128)S(1)} collective-permute-done((f32[3,16,128]{2,1,0:T(8,128)S(1)}, f32[3,16,128]{2,1,0:T(8,128)S(1)}, u32[]{:S(2)}, u32[]{:S(2)}) %collective-permute-start.28) | collective-permute-done | bytes 24608 | tf_op jit(solution)/shard_map/ppermute | solution.py:393
  140.0 2.1 %collective-permute-start.32 = (f32[3,16,128]{2,1,0:T(8,128)S(1)}, f32[3,16,128]{2,1,0:T(8,128)S(1)}, u32[]{:S(2)}, u32[]{:S(2)}) collective-permute-start(f32[3,16,128]{2,1,0:T(8,128)S(1)} %add_add_fusion.1), channel_id=1, source_target_pairs={{0,24},{1,25},{2,26},{3,27},{4,28},{5,29},{6,30},{7,31},{8,0},{9,1... | collective-permute-start | bytes 73736 | tf_op jit(solution)/shard_map/ppermute | solution.py:393
  142.1 1.3 collective-permute-start.30
  143.4 2.6 %collective-permute-done.31 = f32[3,16,128]{2,1,0:T(8,128)S(1)} collective-permute-done((f32[3,16,128]{2,1,0:T(8,128)S(1)}, f32[3,16,128]{2,1,0:T(8,128)S(1)}, u32[]{:S(2)}, u32[]{:S(2)}) %collective-permute-start.31) | collective-permute-done | bytes 24608 | tf_op jit(solution)/shard_map/ppermute | solution.py:393
  146.3 6.1 %collective-permute-start.33 = (f32[3,16,128]{2,1,0:T(8,128)S(1)}, f32[3,16,128]{2,1,0:T(8,128)S(1)}, u32[]{:S(2)}, u32[]{:S(2)}) collective-permute-start(f32[3,16,128]{2,1,0:T(8,128)S(1)} %add_add_fusion), channel_id=1, source_target_pairs={{0,1},{1,0},{2,3},{3,2},{4,5},{5,4},{6,7},{7,6},{8,9},{9,8},{10,11... | collective-permute-start | bytes 73736 | tf_op jit(solution)/shard_map/ppermute | solution.py:393
  153.3 1.9 %finish.1 = (f32[64,512]{1,0:T(8,128)}, f32[64,512]{1,0:T(8,128)}, f32[16,2048]{1,0:T(8,128)}, f32[64,512]{1,0:T(8,128)}, f32[64,512]{1,0:T(8,128)}, /*index=5*/f32[16,2048]{1,0:T(8,128)}) custom-call(bf16[4,192,512]{2,1,0:T(8,128)(2,1)S(1)} %get-tuple-element.166.refs_0_.x0, bf16[4,192,512]{2,1,0:T(8,128)(2,1)S(1)} %collective-permute-done.23.refs_1_.x1, ...), custom_call_target="tpu_custom_call" | custom-call | flops 4194304 | bytes 6291456 | tf_op jit(solution)/shard_map/finish/pallas_call | solution.py:361
  (66 shorter events, 12.8 us)
Async XLA Ops:
  0.6 5.9 %collective-permute-start.2 = (s32[1,512]{1,0:T(1,128)}, s32[1,512]{1,0:T(1,128)S(1)}, u32[]{:S(2)}, u32[]{:S(2)}) collective-permute-start(s32[1,512]{1,0:T(1,128)} %i0), channel_id=1, source_target_pairs={{0,32},{32,64},{64,96},{96,0},{1,33},{33,65},{65,97},{97,1},{2,34}... | collective-permute-start | bytes 6152 | tf_op jit(solution)/shard_map/ppermute | solution.py:393
  2.8 8.3 %collective-permute-start.1 = (s32[1,512]{1,0:T(1,128)}, s32[1,512]{1,0:T(1,128)S(1)}, u32[]{:S(2)}, u32[]{:S(2)}) collective-permute-start(s32[1,512]{1,0:T(1,128)} %i0), channel_id=1, source_target_pairs={{0,64},{32,96},{64,0},{96,32},{1,65},{33,97},{65,1},{97,33},{2,66}... | collective-permute-start | bytes 6152 | tf_op jit(solution)/shard_map/ppermute | solution.py:393
  5.4 4.2 %collective-permute-start = (s32[1,512]{1,0:T(1,128)}, s32[1,512]{1,0:T(1,128)S(1)}, u32[]{:S(2)}, u32[]{:S(2)}) collective-permute-start(s32[1,512]{1,0:T(1,128)} %i0), channel_id=1, source_target_pairs={{0,96},{32,0},{64,32},{96,64},{1,97},{33,1},{65,33},{97,65},{2,98}... | collective-permute-start | bytes 6152 | tf_op jit(solution)/shard_map/ppermute | solution.py:393
  6.5 1.6 %copy-start.8 = (bf16[2048,512]{1,0:T(8,128)(2,1)S(1)}, bf16[2048,512]{1,0:T(8,128)(2,1)}, u32[]{:S(2)}) copy-start(bf16[2048,512]{1,0:T(8,128)(2,1)} %refs_1_.9) | copy-start | bytes 6291460
  9.6 4.3 %copy-start = (f32[1,64,512]{2,1,0:T(8,128)S(1)}, f32[1,64,512]{2,1,0:T(8,128)}, u32[]{:S(2)}) copy-start(f32[1,64,512]{2,1,0:T(8,128)} %param.14) | copy-start | bytes 393220
  9.6 4.3 %copy-start.1 = (f32[1,64,512]{2,1,0:T(8,128)S(1)}, f32[1,64,512]{2,1,0:T(8,128)}, u32[]{:S(2)}) copy-start(f32[1,64,512]{2,1,0:T(8,128)} %param.15) | copy-start | bytes 393220
  9.6 4.3 %copy-start.2 = (f32[1,16,2048]{2,1,0:T(8,128)S(1)}, f32[1,16,2048]{2,1,0:T(8,128)}, u32[]{:S(2)}) copy-start(f32[1,16,2048]{2,1,0:T(8,128)} %param.16) | copy-start | bytes 393220
  9.6 8.5 %copy-start.7 = (bf16[2048,512]{1,0:T(8,128)(2,1)S(1)}, bf16[2048,512]{1,0:T(8,128)(2,1)}, u32[]{:S(2)}) copy-start(bf16[2048,512]{1,0:T(8,128)(2,1)} %refs_1_.11) | copy-start | bytes 6291460
  11.1 14.3 %collective-permute-start.6 = (bf16[512,512]{1,0:T(8,128)(2,1)S(1)}, bf16[512,512]{1,0:T(8,128)(2,1)S(1)}, u32[]{:S(2)}, u32[]{:S(2)}) collective-permute-start(bf16[512,512]{1,0:T(8,128)(2,1)S(1)} %pick_rows.6), channel_id=1, source_target_pairs={{0,32},{32,64},{64,96},{96,0},{1,33},{33,65},{65,97},{97,1},{2,34}... | collective-permute-start | bytes 1572872 | tf_op jit(solution)/shard_map/ppermute | solution.py:393
  11.6 13.8 %collective-permute-start.7 = (bf16[512,512]{1,0:T(8,128)(2,1)S(1)}, bf16[512,512]{1,0:T(8,128)(2,1)S(1)}, u32[]{:S(2)}, u32[]{:S(2)}) collective-permute-start(bf16[512,512]{1,0:T(8,128)(2,1)S(1)} %pick_rows.7), channel_id=1, source_target_pairs={{0,96},{32,0},{64,32},{96,64},{1,97},{33,1},{65,33},{97,65},{2,98}... | collective-permute-start | bytes 1572872 | tf_op jit(solution)/shard_map/ppermute | solution.py:393
  14.4 7.3 %collective-permute-start.5 = (bf16[96,1024]{1,0:T(8,128)(2,1)S(1)}, bf16[96,1024]{1,0:T(8,128)(2,1)S(1)}, u32[]{:S(2)}, u32[]{:S(2)}) collective-permute-start(bf16[96,1024]{1,0:T(8,128)(2,1)S(1)} %pack.1.refs_0_), channel_id=1, source_target_pairs={{0,6},{1,25},{2,0},{3,27},{4,2},{5,29},{6,4},{7,31},{8,14},{9,1},{... | collective-permute-start | bytes 589832 | tf_op jit(solution)/shard_map/ppermute | solution.py:393
  17.0 6.1 %collective-permute-start.4 = (bf16[96,1024]{1,0:T(8,128)(2,1)S(1)}, bf16[96,1024]{1,0:T(8,128)(2,1)S(1)}, u32[]{:S(2)}, u32[]{:S(2)}) collective-permute-start(bf16[96,1024]{1,0:T(8,128)(2,1)S(1)} %pack.1.refs_0_), channel_id=1, source_target_pairs={{0,4},{1,17},{2,6},{3,19},{4,0},{5,21},{6,2},{7,23},{8,12},{9,25},... | collective-permute-start | bytes 589832 | tf_op jit(solution)/shard_map/ppermute | solution.py:393
  17.5 7.9 %collective-permute-start.3 = (bf16[96,1024]{1,0:T(8,128)(2,1)S(1)}, bf16[96,1024]{1,0:T(8,128)(2,1)S(1)}, u32[]{:S(2)}, u32[]{:S(2)}) collective-permute-start(bf16[96,1024]{1,0:T(8,128)(2,1)S(1)} %pack.1.refs_0_), channel_id=1, source_target_pairs={{0,2},{1,9},{2,4},{3,11},{4,6},{5,13},{6,0},{7,15},{8,10},{9,17},{... | collective-permute-start | bytes 589832 | tf_op jit(solution)/shard_map/ppermute | solution.py:393
  25.4 24.7 %collective-permute-start.11 = (bf16[1024,512]{1,0:T(8,128)(2,1)S(1)}, bf16[1024,512]{1,0:T(8,128)(2,1)S(1)}, u32[]{:S(2)}, u32[]{:S(2)}) collective-permute-start(bf16[1024,512]{1,0:T(8,128)(2,1)S(1)} %pick_rows.8), channel_id=1, source_target_pairs={{0,64},{32,96},{64,0},{96,32},{1,65},{33,97},{65,1},{97,33},{2,66}... | collective-permute-start | bytes 3145736 | tf_op jit(solution)/shard_map/ppermute | solution.py:393
  25.5 21.2 %collective-permute-start.10 = (bf16[4,96,1024]{2,1,0:T(8,128)(2,1)S(1)}, bf16[4,96,1024]{2,1,0:T(8,128)(2,1)S(1)}, u32[]{:S(2)}, u32[]{:S(2)}) collective-permute-start(bf16[4,96,1024]{2,1,0:T(8,128)(2,1)S(1)} %bundle.1.refs_0_), channel_id=1, source_target_pairs={{0,24},{1,7},{2,26},{3,1},{4,28},{5,3},{6,30},{7,5},{8,0},{9,15},{... | collective-permute-start | bytes 2359304 | tf_op jit(solution)/shard_map/ppermute | solution.py:393
  29.3 17.4 %collective-permute-start.9 = (bf16[4,96,1024]{2,1,0:T(8,128)(2,1)S(1)}, bf16[4,96,1024]{2,1,0:T(8,128)(2,1)S(1)}, u32[]{:S(2)}, u32[]{:S(2)}) collective-permute-start(bf16[4,96,1024]{2,1,0:T(8,128)(2,1)S(1)} %bundle.1.refs_0_), channel_id=1, source_target_pairs={{0,16},{1,5},{2,18},{3,7},{4,20},{5,1},{6,22},{7,3},{8,24},{9,13},... | collective-permute-start | bytes 2359304 | tf_op jit(solution)/shard_map/ppermute | solution.py:393
  29.3 20.8 %collective-permute-start.8 = (bf16[4,96,1024]{2,1,0:T(8,128)(2,1)S(1)}, bf16[4,96,1024]{2,1,0:T(8,128)(2,1)S(1)}, u32[]{:S(2)}, u32[]{:S(2)}) collective-permute-start(bf16[4,96,1024]{2,1,0:T(8,128)(2,1)S(1)} %bundle.1.refs_0_), channel_id=1, source_target_pairs={{0,8},{1,3},{2,10},{3,5},{4,12},{5,7},{6,14},{7,1},{8,16},{9,11},{... | collective-permute-start | bytes 2359304 | tf_op jit(solution)/shard_map/ppermute | solution.py:393
  31.5 1.6 %copy-start.9 = (bf16[2048,512]{1,0:T(8,128)(2,1)S(1)}, bf16[2048,512]{1,0:T(8,128)(2,1)}, u32[]{:S(2)}) copy-start(bf16[2048,512]{1,0:T(8,128)(2,1)} %refs_1_.9) | copy-start | bytes 6291460
  31.5 1.6 %copy-start.10 = (s32[1,512]{1,0:T(1,128)S(1)}, s32[1,512]{1,0:T(1,128)}, u32[]{:S(2)}) copy-start(s32[1,512]{1,0:T(1,128)} %i0) | copy-start | bytes 6148
  50.3 10.0 %collective-permute-start.14 = (bf16[16,96,1024]{2,1,0:T(8,128)(2,1)S(1)}, bf16[16,96,1024]{2,1,0:T(8,128)(2,1)S(1)}, u32[]{:S(2)}, u32[]{:S(2)}) collective-permute-start(bf16[16,96,1024]{2,1,0:T(8,128)(2,1)S(1)} %half_of_weights.1.a), channel_id=1, source_target_pairs={{0,1},{1,0},{2,3},{3,2},{4,5},{5,4},{6,7},{7,6},{8,9},{9,8},{10,11... | collective-permute-start | bytes 9437192 | tf_op jit(solution)/shard_map/ppermute | solution.py:393
  55.1 14.7 %collective-permute-start.12 = (bf16[512,512]{1,0:T(8,128)(2,1)S(1)}, bf16[512,512]{1,0:T(8,128)(2,1)S(1)}, u32[]{:S(2)}, u32[]{:S(2)}) collective-permute-start(bf16[512,512]{1,0:T(8,128)(2,1)S(1)} %pick_rows.10), channel_id=1, source_target_pairs={{0,32},{32,64},{64,96},{96,0},{1,33},{33,65},{65,97},{97,1},{2,34}... | collective-permute-start | bytes 1572872 | tf_op jit(solution)/shard_map/ppermute | solution.py:393
  56.2 13.6 %collective-permute-start.13 = (bf16[512,512]{1,0:T(8,128)(2,1)S(1)}, bf16[512,512]{1,0:T(8,128)(2,1)S(1)}, u32[]{:S(2)}, u32[]{:S(2)}) collective-permute-start(bf16[512,512]{1,0:T(8,128)(2,1)S(1)} %pick_rows.11), channel_id=1, source_target_pairs={{0,96},{32,0},{64,32},{96,64},{1,97},{33,1},{65,33},{97,65},{2,98}... | collective-permute-start | bytes 1572872 | tf_op jit(solution)/shard_map/ppermute | solution.py:393
  60.8 3.0 %copy-start.6 = (f32[1,512]{1,0:T(1,128)S(1)}, f32[1,512]{1,0:T(1,128)}, u32[]{:S(2)}) copy-start(f32[1,512]{1,0:T(1,128)} %route_ref.3) | copy-start | bytes 6148
  73.8 8.7 %collective-permute-start.15 = (bf16[16,128,512]{2,1,0:T(8,128)(2,1)S(1)}, bf16[16,128,512]{2,1,0:T(8,128)(2,1)S(1)}, u32[]{:S(2)}, u32[]{:S(2)}) collective-permute-start(bf16[16,128,512]{2,1,0:T(8,128)(2,1)S(1)} %get-tuple-element.131), channel_id=1, source_target_pairs={{0,1},{1,0},{2,3},{3,2},{4,5},{5,4},{6,7},{7,6},{8,9},{9,8},{10,11... | collective-permute-start | bytes 6291464 | tf_op jit(solution)/shard_map/ppermute | solution.py:393
  74.9 5.3 %collective-permute-start.16 = (bf16[16,64,512]{2,1,0:T(8,128)(2,1)S(1)}, bf16[16,64,512]{2,1,0:T(8,128)(2,1)S(1)}, u32[]{:S(2)}, u32[]{:S(2)}) collective-permute-start(bf16[16,64,512]{2,1,0:T(8,128)(2,1)S(1)} %get-tuple-element.132), channel_id=1, source_target_pairs={{0,1},{1,0},{2,3},{3,2},{4,5},{5,4},{6,7},{7,6},{8,9},{9,8},{10,11... | collective-permute-start | bytes 3145736 | tf_op jit(solution)/shard_map/ppermute | solution.py:393
  83.3 1.3 collective-permute-start.17
  85.9 20.8 %collective-permute-start.18 = (bf16[4,192,512]{2,1,0:T(8,128)(2,1)S(1)}, bf16[4,192,512]{2,1,0:T(8,128)(2,1)S(1)}, u32[]{:S(2)}, u32[]{:S(2)}) collective-permute-start(bf16[4,192,512]{2,1,0:T(8,128)(2,1)S(1)} %get-tuple-element.143), channel_id=1, source_target_pairs={{0,2},{1,9},{2,4},{3,11},{4,6},{5,13},{6,0},{7,15},{8,10},{9,17},{... | collective-permute-start | bytes 2359304 | tf_op jit(solution)/shard_map/ppermute | solution.py:393
  86.0 20.8 %collective-permute-start.19 = (bf16[4,192,512]{2,1,0:T(8,128)(2,1)S(1)}, bf16[4,192,512]{2,1,0:T(8,128)(2,1)S(1)}, u32[]{:S(2)}, u32[]{:S(2)}) collective-permute-start(bf16[4,192,512]{2,1,0:T(8,128)(2,1)S(1)} %get-tuple-element.144), channel_id=1, source_target_pairs={{0,4},{1,17},{2,6},{3,19},{4,0},{5,21},{6,2},{7,23},{8,12},{9,25},... | collective-permute-start | bytes 2359304 | tf_op jit(solution)/shard_map/ppermute | solution.py:393
  87.5 19.9 %collective-permute-start.20 = (bf16[4,192,512]{2,1,0:T(8,128)(2,1)S(1)}, bf16[4,192,512]{2,1,0:T(8,128)(2,1)S(1)}, u32[]{:S(2)}, u32[]{:S(2)}) collective-permute-start(bf16[4,192,512]{2,1,0:T(8,128)(2,1)S(1)} %get-tuple-element.145), channel_id=1, source_target_pairs={{0,6},{1,25},{2,0},{3,27},{4,2},{5,29},{6,4},{7,31},{8,14},{9,1},{... | collective-permute-start | bytes 2359304 | tf_op jit(solution)/shard_map/ppermute | solution.py:393
  88.7 11.2 %collective-permute-start.21 = (bf16[512,512]{1,0:T(8,128)(2,1)S(1)}, bf16[512,512]{1,0:T(8,128)(2,1)S(1)}, u32[]{:S(2)}, u32[]{:S(2)}) collective-permute-start(bf16[512,512]{1,0:T(8,128)(2,1)S(1)} %get-tuple-element.146), channel_id=1, source_target_pairs={{0,96},{32,0},{64,32},{96,64},{1,97},{33,1},{65,33},{97,65},{2,98}... | collective-permute-start | bytes 1572872 | tf_op jit(solution)/shard_map/ppermute | solution.py:393
  91.2 11.7 %collective-permute-start.22 = (bf16[512,512]{1,0:T(8,128)(2,1)S(1)}, bf16[512,512]{1,0:T(8,128)(2,1)S(1)}, u32[]{:S(2)}, u32[]{:S(2)}) collective-permute-start(bf16[512,512]{1,0:T(8,128)(2,1)S(1)} %get-tuple-element.147), channel_id=1, source_target_pairs={{0,32},{32,64},{64,96},{96,0},{1,33},{33,65},{65,97},{97,1},{2,34}... | collective-permute-start | bytes 1572872 | tf_op jit(solution)/shard_map/ppermute | solution.py:393
  107.6 13.2 %collective-permute-start.26 = (bf16[512,512]{1,0:T(8,128)(2,1)S(1)}, bf16[512,512]{1,0:T(8,128)(2,1)S(1)}, u32[]{:S(2)}, u32[]{:S(2)}) collective-permute-start(bf16[512,512]{1,0:T(8,128)(2,1)S(1)} %get-tuple-element.164), channel_id=1, source_target_pairs={{0,64},{32,96},{64,0},{96,32},{1,65},{33,97},{65,1},{97,33},{2,66}... | collective-permute-start | bytes 1572872 | tf_op jit(solution)/shard_map/ppermute | solution.py:393
  109.7 17.1 %collective-permute-start.23 = (bf16[4,192,512]{2,1,0:T(8,128)(2,1)S(1)}, bf16[4,192,512]{2,1,0:T(8,128)(2,1)S(1)}, u32[]{:S(2)}, u32[]{:S(2)}) collective-permute-start(bf16[4,192,512]{2,1,0:T(8,128)(2,1)S(1)} %get-tuple-element.158), channel_id=1, source_target_pairs={{0,8},{1,3},{2,10},{3,5},{4,12},{5,7},{6,14},{7,1},{8,16},{9,11},{... | collective-permute-start | bytes 2359304 | tf_op jit(solution)/shard_map/ppermute | solution.py:393
  109.7 20.8 %collective-permute-start.24 = (bf16[4,192,512]{2,1,0:T(8,128)(2,1)S(1)}, bf16[4,192,512]{2,1,0:T(8,128)(2,1)S(1)}, u32[]{:S(2)}, u32[]{:S(2)}) collective-permute-start(bf16[4,192,512]{2,1,0:T(8,128)(2,1)S(1)} %get-tuple-element.159), channel_id=1, source_target_pairs={{0,16},{1,5},{2,18},{3,7},{4,20},{5,1},{6,22},{7,3},{8,24},{9,13},... | collective-permute-start | bytes 2359304 | tf_op jit(solution)/shard_map/ppermute | solution.py:393
  112.4 18.7 %collective-permute-start.25 = (bf16[4,192,512]{2,1,0:T(8,128)(2,1)S(1)}, bf16[4,192,512]{2,1,0:T(8,128)(2,1)S(1)}, u32[]{:S(2)}, u32[]{:S(2)}) collective-permute-start(bf16[4,192,512]{2,1,0:T(8,128)(2,1)S(1)} %get-tuple-element.160), channel_id=1, source_target_pairs={{0,24},{1,7},{2,26},{3,1},{4,28},{5,3},{6,30},{7,5},{8,0},{9,15},{... | collective-permute-start | bytes 2359304 | tf_op jit(solution)/shard_map/ppermute | solution.py:393
  126.8 26.5 %copy-start.3 = (f32[1,64,512]{2,1,0:T(8,128)S(1)}, f32[1,64,512]{2,1,0:T(8,128)}, u32[]{:S(2)}) copy-start(f32[1,64,512]{2,1,0:T(8,128)} %param.17) | copy-start | bytes 393220
  126.8 26.5 %copy-start.4 = (f32[1,64,512]{2,1,0:T(8,128)S(1)}, f32[1,64,512]{2,1,0:T(8,128)}, u32[]{:S(2)}) copy-start(f32[1,64,512]{2,1,0:T(8,128)} %param.18) | copy-start | bytes 393220
  126.8 26.5 %copy-start.5 = (f32[1,16,2048]{2,1,0:T(8,128)S(1)}, f32[1,16,2048]{2,1,0:T(8,128)}, u32[]{:S(2)}) copy-start(f32[1,16,2048]{2,1,0:T(8,128)} %param.19) | copy-start | bytes 393220
  133.4 3.6 %collective-permute-start.29 = (f32[3,16,128]{2,1,0:T(8,128)S(1)}, f32[3,16,128]{2,1,0:T(8,128)S(1)}, u32[]{:S(2)}, u32[]{:S(2)}) collective-permute-start(f32[3,16,128]{2,1,0:T(8,128)S(1)} %gram.1), channel_id=1, source_target_pairs={{0,6},{1,7},{2,0},{3,1},{4,2},{5,3},{6,4},{7,5},{8,14},{9,15},{10,... | collective-permute-start | bytes 73736 | tf_op jit(solution)/shard_map/ppermute | solution.py:393
  135.8 3.9 %collective-permute-start.28 = (f32[3,16,128]{2,1,0:T(8,128)S(1)}, f32[3,16,128]{2,1,0:T(8,128)S(1)}, u32[]{:S(2)}, u32[]{:S(2)}) collective-permute-start(f32[3,16,128]{2,1,0:T(8,128)S(1)} %gram.1), channel_id=1, source_target_pairs={{0,2},{1,3},{2,4},{3,5},{4,6},{5,7},{6,0},{7,1},{8,10},{9,11},{10,... | collective-permute-start | bytes 73736 | tf_op jit(solution)/shard_map/ppermute | solution.py:393
  135.8 4.2 %collective-permute-start.27 = (f32[3,16,128]{2,1,0:T(8,128)S(1)}, f32[3,16,128]{2,1,0:T(8,128)S(1)}, u32[]{:S(2)}, u32[]{:S(2)}) collective-permute-start(f32[3,16,128]{2,1,0:T(8,128)S(1)} %gram.1), channel_id=1, source_target_pairs={{0,4},{1,5},{2,6},{3,7},{4,0},{5,1},{6,2},{7,3},{8,12},{9,13},{10,... | collective-permute-start | bytes 73736 | tf_op jit(solution)/shard_map/ppermute | solution.py:393
  140.0 3.4 %collective-permute-start.32 = (f32[3,16,128]{2,1,0:T(8,128)S(1)}, f32[3,16,128]{2,1,0:T(8,128)S(1)}, u32[]{:S(2)}, u32[]{:S(2)}) collective-permute-start(f32[3,16,128]{2,1,0:T(8,128)S(1)} %add_add_fusion.1), channel_id=1, source_target_pairs={{0,24},{1,25},{2,26},{3,27},{4,28},{5,29},{6,30},{7,31},{8,0},{9,1... | collective-permute-start | bytes 73736 | tf_op jit(solution)/shard_map/ppermute | solution.py:393
  142.1 3.9 %collective-permute-start.31 = (f32[3,16,128]{2,1,0:T(8,128)S(1)}, f32[3,16,128]{2,1,0:T(8,128)S(1)}, u32[]{:S(2)}, u32[]{:S(2)}) collective-permute-start(f32[3,16,128]{2,1,0:T(8,128)S(1)} %add_add_fusion.1), channel_id=1, source_target_pairs={{0,8},{1,9},{2,10},{3,11},{4,12},{5,13},{6,14},{7,15},{8,16},{9,17... | collective-permute-start | bytes 73736 | tf_op jit(solution)/shard_map/ppermute | solution.py:393
  142.1 4.2 %collective-permute-start.30 = (f32[3,16,128]{2,1,0:T(8,128)S(1)}, f32[3,16,128]{2,1,0:T(8,128)S(1)}, u32[]{:S(2)}, u32[]{:S(2)}) collective-permute-start(f32[3,16,128]{2,1,0:T(8,128)S(1)} %add_add_fusion.1), channel_id=1, source_target_pairs={{0,16},{1,17},{2,18},{3,19},{4,20},{5,21},{6,22},{7,23},{8,24},{9,... | collective-permute-start | bytes 73736 | tf_op jit(solution)/shard_map/ppermute | solution.py:393
  146.3 7.0 %collective-permute-start.33 = (f32[3,16,128]{2,1,0:T(8,128)S(1)}, f32[3,16,128]{2,1,0:T(8,128)S(1)}, u32[]{:S(2)}, u32[]{:S(2)}) collective-permute-start(f32[3,16,128]{2,1,0:T(8,128)S(1)} %add_add_fusion), channel_id=1, source_target_pairs={{0,1},{1,0},{2,3},{3,2},{4,5},{5,4},{6,7},{7,6},{8,9},{9,8},{10,11... | collective-permute-start | bytes 73736 | tf_op jit(solution)/shard_map/ppermute | solution.py:393

commit v9 on v8

--- a/solution.py
+++ b/solution.py
@@ -460,6 +460,12 @@
     return [out[1], out[2], out[3]]
 
 
+def tie_far(items, others, last=False):
+    order = (3, 1, 2, 0) if last else (2, 1, 3, 0)
+    tied, others = lax.optimization_barrier(([items[k] for k in order], others))
+    return [tied[order.index(k)] for k in range(4)], others
+
+
 def spread(block, turn):
     return to_others([block] * 4, turn)
 
@@ -528,17 +534,17 @@
     blocks = spread(packed, 0)
     x[1], x[3] = around_y(x[1], 1), around_y(x[3], 3)
     (x[2],) = pick_rows(ids[2:3], [pool_tokens, pool_cotangent], stacked=True)
-    ids, blocks, x[1:] = tie((ids, blocks, x[1:]))
-
-    block = bundle((packed, *blocks))
+    blocks, (ids, x[1:]) = tie_far([packed, *blocks], (ids, x[1:]), last=True)
+
+    block = bundle(blocks)
     blocks = spread(block, 1)
     x[2] = c[2] = around_y(x[2], 2)
     c[1], c[3] = picked(1, pool_cotangent), picked(3, pool_cotangent)
     x[0], c[0] = pick_rows(ids[:1], [pool_tokens, pool_cotangent])
-    blocks, x, c = tie((blocks, x, [c[0], c[1], c[3]]))
+    blocks, (x, c) = tie_far([block, *blocks], (x, [c[0], c[1], c[3]]), last=True)
     c = [c[0], c[1], x[2], c[2]]
 
-    mine = half_of_weights((block, *blocks))
+    mine = half_of_weights(blocks)
     weights = whole_weights(mine, other_core(mine))
     c[1], c[3] = around_y(c[1], 1), around_y(c[3], 3)
 
@@ -546,7 +552,7 @@
     early, downs = backward_early((c[0], c[2]), route_weights, hidden_t, weights)
     keep_down, send_down, hidden_grad = backward_down((c[1], c[3]), route_weights, hidden_t, early, downs, weights)
     keep_in, send_in, both = backward_in(hidden_grad, gate_factor, act, xt)
-    received_down, both = tie((other_core(send_down), both))
+    received_down, send_in = tie((other_core(send_down), send_in))
     keep, received = (keep_in, keep_down), (other_core(send_in), received_down)
     slots = slot_gradients(both, weights)
     received, slots = lax.optimization_barrier((received, list(slots)))
@@ -555,12 +561,12 @@
     sent = pair_merge(keep, received, mine, other_core(mine))
     parts = [sent[0], *to_others(sent, 0)]
     back = [slots[0], around_y(slots[1], 3), None, around_y(slots[3], 1)]
-    parts, back[1], back[3] = tie((parts, back[1], back[3]))
+    parts, (back[1], back[3]) = tie_far(parts, (back[1], back[3]))
     sent, slots[2] = tie((turn_over(parts), slots[2]))
     parts = [sent[0], *to_others(sent, 1)]
     back[2] = around_y(slots[2], 2)
     pool_grad = scatter_rows(ids, back)
-    parts, pool_grad = tie((parts, pool_grad))
+    parts, pool_grad = tie_far(parts, pool_grad)
     products = sum_dp(gram(parts))
     outs = finish(
         parts,

time: 155 us -> 149 us (0.961)
  waiting for transfers between devices: 67.3 us -> 52.4 us
  starting transfers between devices: 49.7 us -> 58.6 us
    ppermute x34, waiting for transfers between devices: 67.3 us -> 52.4 us  [shift(): lax.ppermute(block, axis, [(i, to(i)) for i in range(lax.axis_size(axis))])]
    ppermute x34, starting transfers between devices: 49.7 us -> 58.6 us  [shift(): lax.ppermute(block, axis, [(i, to(i)) for i in range(lax.axis_size(axis))])]
  transfers between devices with their start and end apart: 34 -> 34, of which waited for: 21 -> 21; matrix products, arithmetic and copies ran while one was open for 0% -> 0% of each run, Pallas kernels for 16% -> 18%
where the time goes in v9:
time: 149 us
  starting transfers between devices  58.6 us (39%)
  waiting for transfers between devices  52.4 us (35%)
  Pallas kernels  35.4 us (24%)
  local copies, waits for them, and re-layouts  1.77 us (1%)
    ppermute x34, starting transfers between devices, shift(): lax.ppermute(block, axis, [(i, to(i)) for i in range(lax.axis_size(axis))])  58.6 us
    ppermute x34, waiting for transfers between devices, shift(): lax.ppermute(block, axis, [(i, to(i)) for i in range(lax.axis_size(axis))])  52.4 us
    pallas_call x6, Pallas kernels, pick_rows(): call(body, 'pick_rows', n_ids + n_pool, shapes, 2 * TOK_DEV * POOL * SLIC...  10.8 us
    pallas_call x1, Pallas kernels, scatter_rows(): pl.pallas_call(body, name='scatter_rows', grid=(POOL // block,), out_shap...  5.97 us
    pallas_call x1, Pallas kernels, forward(): call(body, 'forward', 5, shapes, 2 * TOK_DEV * D * 2 * H, 10 * MIB, [pltp...  3.02 us
  transfers between devices with their start and end apart: 34, of which 21 were waited for; matrix products, arithmetic and copies ran while one was open for 0% of the time, Pallas kernels for 18%

profile of v9, /device:TPU:1, one launch (start us, length us, event | category | flops | bytes accessed | tf_op | source)
XLA Modules:
  0.0 149.1 jit_solution(3922017317611332328)
XLA Ops:
  0.6 2.2 %collective-permute-start.2 = (s32[1,512]{1,0:T(1,128)}, s32[1,512]{1,0:T(1,128)S(1)}, u32[]{:S(2)}, u32[]{:S(2)}) collective-permute-start(s32[1,512]{1,0:T(1,128)} %i0), channel_id=1, source_target_pairs={{0,32},{32,64},{64,96},{96,0},{1,33},{33,65},{65,97},{97,1},{2,34}... | collective-permute-start | bytes 6152 | tf_op jit(solution)/shard_map/ppermute | solution.py:393
  2.8 2.6 %collective-permute-start.1 = (s32[1,512]{1,0:T(1,128)}, s32[1,512]{1,0:T(1,128)S(1)}, u32[]{:S(2)}, u32[]{:S(2)}) collective-permute-start(s32[1,512]{1,0:T(1,128)} %i0), channel_id=1, source_target_pairs={{0,64},{32,96},{64,0},{96,32},{1,65},{33,97},{65,1},{97,33},{2,66}... | collective-permute-start | bytes 6152 | tf_op jit(solution)/shard_map/ppermute | solution.py:393
  6.5 1.6 %copy-done.8 = bf16[2048,512]{1,0:T(8,128)(2,1)S(1)} copy-done((bf16[2048,512]{1,0:T(8,128)(2,1)S(1)}, bf16[2048,512]{1,0:T(8,128)(2,1)}, u32[]{:S(2)}) %copy-start.8) | copy-done | bytes 2097176
  8.1 1.4 pick_rows.7
  9.6 1.4 pick_rows.6
  11.6 2.3 %collective-permute-start.7 = (bf16[512,512]{1,0:T(8,128)(2,1)S(1)}, bf16[512,512]{1,0:T(8,128)(2,1)S(1)}, u32[]{:S(2)}, u32[]{:S(2)}) collective-permute-start(bf16[512,512]{1,0:T(8,128)(2,1)S(1)} %pick_rows.7), channel_id=1, source_target_pairs={{0,96},{32,0},{64,32},{96,64},{1,97},{33,1},{65,33},{97,65},{2,98}... | collective-permute-start | bytes 1572872 | tf_op jit(solution)/shard_map/ppermute | solution.py:393
  14.4 2.8 %collective-permute-start.5 = (bf16[96,1024]{1,0:T(8,128)(2,1)S(1)}, bf16[96,1024]{1,0:T(8,128)(2,1)S(1)}, u32[]{:S(2)}, u32[]{:S(2)}) collective-permute-start(bf16[96,1024]{1,0:T(8,128)(2,1)S(1)} %pack.1.refs_0_), channel_id=1, source_target_pairs={{0,4},{1,17},{2,6},{3,19},{4,0},{5,21},{6,2},{7,23},{8,12},{9,25},... | collective-permute-start | bytes 589832 | tf_op jit(solution)/shard_map/ppermute | solution.py:393
  17.5 2.4 %collective-permute-start.3 = (bf16[96,1024]{1,0:T(8,128)(2,1)S(1)}, bf16[96,1024]{1,0:T(8,128)(2,1)S(1)}, u32[]{:S(2)}, u32[]{:S(2)}) collective-permute-start(bf16[96,1024]{1,0:T(8,128)(2,1)S(1)} %pack.1.refs_0_), channel_id=1, source_target_pairs={{0,6},{1,25},{2,0},{3,27},{4,2},{5,29},{6,4},{7,31},{8,14},{9,1},{... | collective-permute-start | bytes 589832 | tf_op jit(solution)/shard_map/ppermute | solution.py:393
  19.9 2.5 %pick_rows.8 = bf16[1024,512]{1,0:T(8,128)(2,1)S(1)} custom-call(s32[1,512]{1,0:T(1,128)S(1)} %collective-permute-done.1.refs_0_.i2, bf16[2048,512]{1,0:T(8,128)(2,1)S(1)} %copy-done.8, bf16[2048,512]{1,0:T(8,128)(2,1)S(1)} %copy-done.7), custom_call_target="tpu_custom_call" | custom-call | flops 2147483648 | bytes 3145728 | tf_op jit(solution)/shard_map/pick_rows/pallas_call | solution.py:73
  24.8 3.7 %collective-permute-start.10 = (bf16[4,96,1024]{2,1,0:T(8,128)(2,1)S(1)}, bf16[4,96,1024]{2,1,0:T(8,128)(2,1)S(1)}, u32[]{:S(2)}, u32[]{:S(2)}) collective-permute-start(bf16[4,96,1024]{2,1,0:T(8,128)(2,1)S(1)} %bundle.1.refs_0_), channel_id=1, source_target_pairs={{0,16},{1,5},{2,18},{3,7},{4,20},{5,1},{6,22},{7,3},{8,24},{9,13},... | collective-permute-start | bytes 2359304 | tf_op jit(solution)/shard_map/ppermute | solution.py:393
  29.2 1.9 %collective-permute-start.8 = (bf16[4,96,1024]{2,1,0:T(8,128)(2,1)S(1)}, bf16[4,96,1024]{2,1,0:T(8,128)(2,1)S(1)}, u32[]{:S(2)}, u32[]{:S(2)}) collective-permute-start(bf16[4,96,1024]{2,1,0:T(8,128)(2,1)S(1)} %bundle.1.refs_0_), channel_id=1, source_target_pairs={{0,24},{1,7},{2,26},{3,1},{4,28},{5,3},{6,30},{7,5},{8,0},{9,15},{... | collective-permute-start | bytes 2359304 | tf_op jit(solution)/shard_map/ppermute | solution.py:393
  31.2 1.4 pick_rows.10
  32.7 1.4 pick_rows.11
  34.2 2.5 %pick_rows.9 = (bf16[512,512]{1,0:T(8,128)(2,1)S(1)}, bf16[512,512]{1,0:T(8,128)(2,1)S(1)}) custom-call(s32[1,512]{1,0:T(1,128)S(1)} %copy-done.10, bf16[2048,512]{1,0:T(8,128)(2,1)S(1)} %copy-done.9, bf16[2048,512]{1,0:T(8,128)(2,1)S(1)} %copy-done.7), custom_call_target="tpu_custom_call" | custom-call | flops 2147483648 | bytes 3145728 | tf_op jit(solution)/shard_map/pick_rows/pallas_call | solution.py:73
  36.7 1.5 collective-permute-done.10.refs_2_
  38.2 8.4 %collective-permute-done.9.refs_1_ = bf16[4,96,1024]{2,1,0:T(8,128)(2,1)S(1)} collective-permute-done((bf16[4,96,1024]{2,1,0:T(8,128)(2,1)S(1)}, bf16[4,96,1024]{2,1,0:T(8,128)(2,1)S(1)}, u32[]{:S(2)}, u32[]{:S(2)}) %collective-permute-start.9) | collective-permute-done | bytes 786464 | tf_op jit(solution)/shard_map/ppermute | solution.py:393
  47.6 4.2 %collective-permute-start.14 = (bf16[16,96,1024]{2,1,0:T(8,128)(2,1)S(1)}, bf16[16,96,1024]{2,1,0:T(8,128)(2,1)S(1)}, u32[]{:S(2)}, u32[]{:S(2)}) collective-permute-start(bf16[16,96,1024]{2,1,0:T(8,128)(2,1)S(1)} %half_of_weights.1.a), channel_id=1, source_target_pairs={{0,1},{1,0},{2,3},{3,2},{4,5},{5,4},{6,7},{7,6},{8,9},{9,8},{10,11... | collective-permute-start | bytes 9437192 | tf_op jit(solution)/shard_map/ppermute | solution.py:393
  51.8 1.1 collective-permute-start.12
  53.0 1.6 %collective-permute-start.13 = (bf16[512,512]{1,0:T(8,128)(2,1)S(1)}, bf16[512,512]{1,0:T(8,128)(2,1)S(1)}, u32[]{:S(2)}, u32[]{:S(2)}) collective-permute-start(bf16[512,512]{1,0:T(8,128)(2,1)S(1)} %pick_rows.11), channel_id=1, source_target_pairs={{0,96},{32,0},{64,32},{96,64},{1,97},{33,1},{65,33},{97,65},{2,98}... | collective-permute-start | bytes 1572872 | tf_op jit(solution)/shard_map/ppermute | solution.py:393
  54.5 2.6 %collective-permute-done.14.b = bf16[16,96,1024]{2,1,0:T(8,128)(2,1)S(1)} collective-permute-done((bf16[16,96,1024]{2,1,0:T(8,128)(2,1)S(1)}, bf16[16,96,1024]{2,1,0:T(8,128)(2,1)S(1)}, u32[]{:S(2)}, u32[]{:S(2)}) %collective-permute-start.14) | collective-permute-done | bytes 3145760 | tf_op jit(solution)/shard_map/ppermute | solution.py:393
  57.6 3.0 %forward.1 = (bf16[512,512]{1,0:T(8,128)(2,1)S(1)}, f32[512,512]{1,0:T(8,128)S(1)}, f32[512,512]{1,0:T(8,128)S(1)}, bf16[4,512,512]{2,1,0:T(8,128)(2,1)S(1)}) custom-call(bf16[512,512]{1,0:T(8,128)(2,1)S(1)} %get-tuple-element.117.x0, bf16[512,512]{1,0:T(8,128)(2,1)S(1)} %collective-permute-done.6.x1, bf16[1024,512]{1,0:T(8,128)(2,1)S(1)} %collective-permute-done.11.x2.c2, ...), custom_call_target="tpu_custom_call" | custom-call | flops 2147483648 | bytes 10485760 | tf_op jit(solution)/shard_map/forward/pallas_call | solution.py:127
  60.6 1.4 backward_early.1
  62.1 4.5 %collective-permute-done.12.c1 = bf16[512,512]{1,0:T(8,128)(2,1)S(1)} collective-permute-done((bf16[512,512]{1,0:T(8,128)(2,1)S(1)}, bf16[512,512]{1,0:T(8,128)(2,1)S(1)}, u32[]{:S(2)}, u32[]{:S(2)}) %collective-permute-start.12) | collective-permute-done | bytes 524320 | tf_op jit(solution)/shard_map/ppermute | solution.py:393
  66.6 1.5 backward_down.1
  69.0 2.5 %backward_in.1 = (bf16[16,128,512]{2,1,0:T(8,128)(2,1)S(1)}, bf16[16,128,512]{2,1,0:T(8,128)(2,1)S(1)}, bf16[512,1024]{1,0:T(8,128)(2,1)S(1)}) custom-call(f32[512,512]{1,0:T(8,128)S(1)} %get-tuple-element.129.hg, f32[512,512]{1,0:T(8,128)S(1)} %get-tuple-element.130.factor, f32[512,512]{1,0:T(8,128)S(1)} %get-tuple-element.131.act_ref, ...), custom_call_target="tpu_custom_call" | custom-call | flops 2147483648 | bytes 10485760 | tf_op jit(solution)/shard_map/backward_in/pallas_call | solution.py:214
  71.7 2.4 %slot_gradients.1 = (bf16[512,512]{1,0:T(8,128)(2,1)S(1)}, bf16[512,512]{1,0:T(8,128)(2,1)S(1)}, bf16[512,512]{1,0:T(8,128)(2,1)S(1)}, bf16[512,512]{1,0:T(8,128)(2,1)S(1)}) custom-call(bf16[512,1024]{1,0:T(8,128)(2,1)S(1)} %get-tuple-element.139.both_ref, bf16[32,96,1024]{2,1,0:T(8,128)(2,1)S(1)} %whole_weights.1.w), custom_call_target="tpu_custom_call" | custom-call | flops 2147483648 | bytes 9437184 | tf_op jit(solution)/shard_map/slot_gradients/pallas_call | solution.py:224
  74.0 1.8 %collective-permute-done.16.b_in = bf16[16,128,512]{2,1,0:T(8,128)(2,1)S(1)} collective-permute-done((bf16[16,128,512]{2,1,0:T(8,128)(2,1)S(1)}, bf16[16,128,512]{2,1,0:T(8,128)(2,1)S(1)}, u32[]{:S(2)}, u32[]{:S(2)}) %collective-permute-start.16) | collective-permute-done | bytes 2097184 | tf_op jit(solution)/shard_map/ppermute | solution.py:393
  77.9 1.3 pair_merge.1
  79.1 2.8 %collective-permute-start.18 = (bf16[4,192,512]{2,1,0:T(8,128)(2,1)S(1)}, bf16[4,192,512]{2,1,0:T(8,128)(2,1)S(1)}, u32[]{:S(2)}, u32[]{:S(2)}) collective-permute-start(bf16[4,192,512]{2,1,0:T(8,128)(2,1)S(1)} %get-tuple-element.146), channel_id=1, source_target_pairs={{0,4},{1,17},{2,6},{3,19},{4,0},{5,21},{6,2},{7,23},{8,12},{9,25},... | collective-permute-start | bytes 2359304 | tf_op jit(solution)/shard_map/ppermute | solution.py:393
  82.3 2.4 %collective-permute-start.20 = (bf16[4,192,512]{2,1,0:T(8,128)(2,1)S(1)}, bf16[4,192,512]{2,1,0:T(8,128)(2,1)S(1)}, u32[]{:S(2)}, u32[]{:S(2)}) collective-permute-start(bf16[4,192,512]{2,1,0:T(8,128)(2,1)S(1)} %get-tuple-element.148), channel_id=1, source_target_pairs={{0,6},{1,25},{2,0},{3,27},{4,2},{5,29},{6,4},{7,31},{8,14},{9,1},{... | collective-permute-start | bytes 2359304 | tf_op jit(solution)/shard_map/ppermute | solution.py:393
  84.6 2.7 %collective-permute-start.21 = (bf16[512,512]{1,0:T(8,128)(2,1)S(1)}, bf16[512,512]{1,0:T(8,128)(2,1)S(1)}, u32[]{:S(2)}, u32[]{:S(2)}) collective-permute-start(bf16[512,512]{1,0:T(8,128)(2,1)S(1)} %get-tuple-element.150), channel_id=1, source_target_pairs={{0,96},{32,0},{64,32},{96,64},{1,97},{33,1},{65,33},{97,65},{2,98}... | collective-permute-start | bytes 1572872 | tf_op jit(solution)/shard_map/ppermute | solution.py:393
  87.3 9.4 %collective-permute-done.21.g1 = bf16[512,512]{1,0:T(8,128)(2,1)S(1)} collective-permute-done((bf16[512,512]{1,0:T(8,128)(2,1)S(1)}, bf16[512,512]{1,0:T(8,128)(2,1)S(1)}, u32[]{:S(2)}, u32[]{:S(2)}) %collective-permute-start.21) | collective-permute-done | bytes 524320 | tf_op jit(solution)/shard_map/ppermute | solution.py:393
  96.7 3.1 %collective-permute-done.22.g3 = bf16[512,512]{1,0:T(8,128)(2,1)S(1)} collective-permute-done((bf16[512,512]{1,0:T(8,128)(2,1)S(1)}, bf16[512,512]{1,0:T(8,128)(2,1)S(1)}, u32[]{:S(2)}, u32[]{:S(2)}) %collective-permute-start.22) | collective-permute-done | bytes 524320 | tf_op jit(solution)/shard_map/ppermute | solution.py:393
  100.6 2.7 %collective-permute-start.26 = (bf16[512,512]{1,0:T(8,128)(2,1)S(1)}, bf16[512,512]{1,0:T(8,128)(2,1)S(1)}, u32[]{:S(2)}, u32[]{:S(2)}) collective-permute-start(bf16[512,512]{1,0:T(8,128)(2,1)S(1)} %get-tuple-element.168), channel_id=1, source_target_pairs={{0,64},{32,96},{64,0},{96,32},{1,65},{33,97},{65,1},{97,33},{2,66}... | collective-permute-start | bytes 1572872 | tf_op jit(solution)/shard_map/ppermute | solution.py:393
  103.3 3.6 %collective-permute-start.23 = (bf16[4,192,512]{2,1,0:T(8,128)(2,1)S(1)}, bf16[4,192,512]{2,1,0:T(8,128)(2,1)S(1)}, u32[]{:S(2)}, u32[]{:S(2)}) collective-permute-start(bf16[4,192,512]{2,1,0:T(8,128)(2,1)S(1)} %get-tuple-element.161), channel_id=1, source_target_pairs={{0,16},{1,5},{2,18},{3,7},{4,20},{5,1},{6,22},{7,3},{8,24},{9,13},... | collective-permute-start | bytes 2359304 | tf_op jit(solution)/shard_map/ppermute | solution.py:393
  107.6 1.9 %collective-permute-start.25 = (bf16[4,192,512]{2,1,0:T(8,128)(2,1)S(1)}, bf16[4,192,512]{2,1,0:T(8,128)(2,1)S(1)}, u32[]{:S(2)}, u32[]{:S(2)}) collective-permute-start(bf16[4,192,512]{2,1,0:T(8,128)(2,1)S(1)} %get-tuple-element.163), channel_id=1, source_target_pairs={{0,24},{1,7},{2,26},{3,1},{4,28},{5,3},{6,30},{7,5},{8,0},{9,15},{... | collective-permute-start | bytes 2359304 | tf_op jit(solution)/shard_map/ppermute | solution.py:393
  109.6 3.8 %collective-permute-done.26.g2 = bf16[512,512]{1,0:T(8,128)(2,1)S(1)} collective-permute-done((bf16[512,512]{1,0:T(8,128)(2,1)S(1)}, bf16[512,512]{1,0:T(8,128)(2,1)S(1)}, u32[]{:S(2)}, u32[]{:S(2)}) %collective-permute-start.26) | collective-permute-done | bytes 524320 | tf_op jit(solution)/shard_map/ppermute | solution.py:393
  113.4 6.0 %scatter_rows.1 = f32[2048,512]{1,0:T(8,128)} custom-call(s32[1,512]{1,0:T(1,128)S(1)} %copy-done.10, s32[1,512]{1,0:T(1,128)S(1)} %collective-permute-done.refs_0_.i1, s32[1,512]{1,0:T(1,128)S(1)} %collective-permute-done.1.refs_0_.i2, s32[1,512]{1,0:T(1,128)S(1)} %collective-permute-done.2.refs_0_.i3, bf16[512,512]{1,0:T(8,128)(2,1)S(1)} %get-tuple-element.166.g0, ...), custom_call_target="tpu_custom_call" | custom-call | flops 4294967296 | bytes 6291456 | tf_op jit(solution)/shard_map/scatter_rows/pallas_call | solution.py:378
  119.4 5.6 %collective-permute-done.24.refs_1_.x1 = bf16[4,192,512]{2,1,0:T(8,128)(2,1)S(1)} collective-permute-done((bf16[4,192,512]{2,1,0:T(8,128)(2,1)S(1)}, bf16[4,192,512]{2,1,0:T(8,128)(2,1)S(1)}, u32[]{:S(2)}, u32[]{:S(2)}) %collective-permute-start.24) | collective-permute-done | bytes 786464 | tf_op jit(solution)/shard_map/ppermute | solution.py:393
  125.8 2.3 %gram.1 = f32[3,16,128]{2,1,0:T(8,128)S(1)} custom-call(bf16[4,192,512]{2,1,0:T(8,128)(2,1)S(1)} %get-tuple-element.170.refs_0_.x0, bf16[4,192,512]{2,1,0:T(8,128)(2,1)S(1)} %collective-permute-done.24.refs_1_.x1, bf16[4,192,512]{2,1,0:T(8,128)(2,1)S(1)} %collective-permute-done.23.refs_2_.x2, bf16[4,192,512]{2,1,0:T(8,128)(2,1)S(1)} %collective-permute-done.25.refs_3_.x3), custom_call_target="tpu_custom_call" | custom-call | flops 805306368 | bytes 3145728 | tf_op jit(solution)/shard_map/gram/pallas_call | solution.py:315
  128.1 2.4 %collective-permute-start.29 = (f32[3,16,128]{2,1,0:T(8,128)S(1)}, f32[3,16,128]{2,1,0:T(8,128)S(1)}, u32[]{:S(2)}, u32[]{:S(2)}) collective-permute-start(f32[3,16,128]{2,1,0:T(8,128)S(1)} %gram.1), channel_id=1, source_target_pairs={{0,6},{1,7},{2,0},{3,1},{4,2},{5,3},{6,4},{7,5},{8,14},{9,15},{10,... | collective-permute-start | bytes 73736 | tf_op jit(solution)/shard_map/ppermute | solution.py:393
  130.5 1.2 collective-permute-start.27
  131.7 2.7 %collective-permute-done.28 = f32[3,16,128]{2,1,0:T(8,128)S(1)} collective-permute-done((f32[3,16,128]{2,1,0:T(8,128)S(1)}, f32[3,16,128]{2,1,0:T(8,128)S(1)}, u32[]{:S(2)}, u32[]{:S(2)}) %collective-permute-start.28) | collective-permute-done | bytes 24608 | tf_op jit(solution)/shard_map/ppermute | solution.py:393
  134.7 2.4 %collective-permute-start.32 = (f32[3,16,128]{2,1,0:T(8,128)S(1)}, f32[3,16,128]{2,1,0:T(8,128)S(1)}, u32[]{:S(2)}, u32[]{:S(2)}) collective-permute-start(f32[3,16,128]{2,1,0:T(8,128)S(1)} %add_add_fusion.1), channel_id=1, source_target_pairs={{0,24},{1,25},{2,26},{3,27},{4,28},{5,29},{6,30},{7,31},{8,0},{9,1... | collective-permute-start | bytes 73736 | tf_op jit(solution)/shard_map/ppermute | solution.py:393
  137.1 1.3 collective-permute-start.30
  138.4 2.6 %collective-permute-done.31 = f32[3,16,128]{2,1,0:T(8,128)S(1)} collective-permute-done((f32[3,16,128]{2,1,0:T(8,128)S(1)}, f32[3,16,128]{2,1,0:T(8,128)S(1)}, u32[]{:S(2)}, u32[]{:S(2)}) %collective-permute-start.31) | collective-permute-done | bytes 24608 | tf_op jit(solution)/shard_map/ppermute | solution.py:393
  141.3 5.1 %collective-permute-start.33 = (f32[3,16,128]{2,1,0:T(8,128)S(1)}, f32[3,16,128]{2,1,0:T(8,128)S(1)}, u32[]{:S(2)}, u32[]{:S(2)}) collective-permute-start(f32[3,16,128]{2,1,0:T(8,128)S(1)} %add_add_fusion), channel_id=1, source_target_pairs={{0,1},{1,0},{2,3},{3,2},{4,5},{5,4},{6,7},{7,6},{8,9},{9,8},{10,11... | collective-permute-start | bytes 73736 | tf_op jit(solution)/shard_map/ppermute | solution.py:393
  147.2 1.9 %finish.1 = (f32[64,512]{1,0:T(8,128)}, f32[64,512]{1,0:T(8,128)}, f32[16,2048]{1,0:T(8,128)}, f32[64,512]{1,0:T(8,128)}, f32[64,512]{1,0:T(8,128)}, /*index=5*/f32[16,2048]{1,0:T(8,128)}) custom-call(bf16[4,192,512]{2,1,0:T(8,128)(2,1)S(1)} %get-tuple-element.170.refs_0_.x0, bf16[4,192,512]{2,1,0:T(8,128)(2,1)S(1)} %collective-permute-done.24.refs_1_.x1, ...), custom_call_target="tpu_custom_call" | custom-call | flops 4194304 | bytes 6291456 | tf_op jit(solution)/shard_map/finish/pallas_call | solution.py:361
  (66 shorter events, 14.4 us)
Async XLA Ops:
  0.6 5.9 %collective-permute-start.2 = (s32[1,512]{1,0:T(1,128)}, s32[1,512]{1,0:T(1,128)S(1)}, u32[]{:S(2)}, u32[]{:S(2)}) collective-permute-start(s32[1,512]{1,0:T(1,128)} %i0), channel_id=1, source_target_pairs={{0,32},{32,64},{64,96},{96,0},{1,33},{33,65},{65,97},{97,1},{2,34}... | collective-permute-start | bytes 6152 | tf_op jit(solution)/shard_map/ppermute | solution.py:393
  2.8 8.3 %collective-permute-start.1 = (s32[1,512]{1,0:T(1,128)}, s32[1,512]{1,0:T(1,128)S(1)}, u32[]{:S(2)}, u32[]{:S(2)}) collective-permute-start(s32[1,512]{1,0:T(1,128)} %i0), channel_id=1, source_target_pairs={{0,64},{32,96},{64,0},{96,32},{1,65},{33,97},{65,1},{97,33},{2,66}... | collective-permute-start | bytes 6152 | tf_op jit(solution)/shard_map/ppermute | solution.py:393
  5.4 4.2 %collective-permute-start = (s32[1,512]{1,0:T(1,128)}, s32[1,512]{1,0:T(1,128)S(1)}, u32[]{:S(2)}, u32[]{:S(2)}) collective-permute-start(s32[1,512]{1,0:T(1,128)} %i0), channel_id=1, source_target_pairs={{0,96},{32,0},{64,32},{96,64},{1,97},{33,1},{65,33},{97,65},{2,98}... | collective-permute-start | bytes 6152 | tf_op jit(solution)/shard_map/ppermute | solution.py:393
  6.5 1.6 %copy-start.8 = (bf16[2048,512]{1,0:T(8,128)(2,1)S(1)}, bf16[2048,512]{1,0:T(8,128)(2,1)}, u32[]{:S(2)}) copy-start(bf16[2048,512]{1,0:T(8,128)(2,1)} %refs_1_.9) | copy-start | bytes 6291460
  9.6 4.3 %copy-start = (f32[1,64,512]{2,1,0:T(8,128)S(1)}, f32[1,64,512]{2,1,0:T(8,128)}, u32[]{:S(2)}) copy-start(f32[1,64,512]{2,1,0:T(8,128)} %param.14) | copy-start | bytes 393220
  9.6 4.3 %copy-start.1 = (f32[1,64,512]{2,1,0:T(8,128)S(1)}, f32[1,64,512]{2,1,0:T(8,128)}, u32[]{:S(2)}) copy-start(f32[1,64,512]{2,1,0:T(8,128)} %param.15) | copy-start | bytes 393220
  9.6 4.3 %copy-start.2 = (f32[1,16,2048]{2,1,0:T(8,128)S(1)}, f32[1,16,2048]{2,1,0:T(8,128)}, u32[]{:S(2)}) copy-start(f32[1,16,2048]{2,1,0:T(8,128)} %param.16) | copy-start | bytes 393220
  9.6 10.3 %copy-start.7 = (bf16[2048,512]{1,0:T(8,128)(2,1)S(1)}, bf16[2048,512]{1,0:T(8,128)(2,1)}, u32[]{:S(2)}) copy-start(bf16[2048,512]{1,0:T(8,128)(2,1)} %refs_1_.11) | copy-start | bytes 6291460
  11.1 13.2 %collective-permute-start.6 = (bf16[512,512]{1,0:T(8,128)(2,1)S(1)}, bf16[512,512]{1,0:T(8,128)(2,1)S(1)}, u32[]{:S(2)}, u32[]{:S(2)}) collective-permute-start(bf16[512,512]{1,0:T(8,128)(2,1)S(1)} %pick_rows.6), channel_id=1, source_target_pairs={{0,32},{32,64},{64,96},{96,0},{1,33},{33,65},{65,97},{97,1},{2,34}... | collective-permute-start | bytes 1572872 | tf_op jit(solution)/shard_map/ppermute | solution.py:393
  11.6 12.7 %collective-permute-start.7 = (bf16[512,512]{1,0:T(8,128)(2,1)S(1)}, bf16[512,512]{1,0:T(8,128)(2,1)S(1)}, u32[]{:S(2)}, u32[]{:S(2)}) collective-permute-start(bf16[512,512]{1,0:T(8,128)(2,1)S(1)} %pick_rows.7), channel_id=1, source_target_pairs={{0,96},{32,0},{64,32},{96,64},{1,97},{33,1},{65,33},{97,65},{2,98}... | collective-permute-start | bytes 1572872 | tf_op jit(solution)/shard_map/ppermute | solution.py:393
  14.4 8.1 %collective-permute-start.5 = (bf16[96,1024]{1,0:T(8,128)(2,1)S(1)}, bf16[96,1024]{1,0:T(8,128)(2,1)S(1)}, u32[]{:S(2)}, u32[]{:S(2)}) collective-permute-start(bf16[96,1024]{1,0:T(8,128)(2,1)S(1)} %pack.1.refs_0_), channel_id=1, source_target_pairs={{0,4},{1,17},{2,6},{3,19},{4,0},{5,21},{6,2},{7,23},{8,12},{9,25},... | collective-permute-start | bytes 589832 | tf_op jit(solution)/shard_map/ppermute | solution.py:393
  17.2 6.0 %collective-permute-start.4 = (bf16[96,1024]{1,0:T(8,128)(2,1)S(1)}, bf16[96,1024]{1,0:T(8,128)(2,1)S(1)}, u32[]{:S(2)}, u32[]{:S(2)}) collective-permute-start(bf16[96,1024]{1,0:T(8,128)(2,1)S(1)} %pack.1.refs_0_), channel_id=1, source_target_pairs={{0,2},{1,9},{2,4},{3,11},{4,6},{5,13},{6,0},{7,15},{8,10},{9,17},{... | collective-permute-start | bytes 589832 | tf_op jit(solution)/shard_map/ppermute | solution.py:393
  17.5 5.7 %collective-permute-start.3 = (bf16[96,1024]{1,0:T(8,128)(2,1)S(1)}, bf16[96,1024]{1,0:T(8,128)(2,1)S(1)}, u32[]{:S(2)}, u32[]{:S(2)}) collective-permute-start(bf16[96,1024]{1,0:T(8,128)(2,1)S(1)} %pack.1.refs_0_), channel_id=1, source_target_pairs={{0,6},{1,25},{2,0},{3,27},{4,2},{5,29},{6,4},{7,31},{8,14},{9,1},{... | collective-permute-start | bytes 589832 | tf_op jit(solution)/shard_map/ppermute | solution.py:393
  24.3 23.1 %collective-permute-start.11 = (bf16[1024,512]{1,0:T(8,128)(2,1)S(1)}, bf16[1024,512]{1,0:T(8,128)(2,1)S(1)}, u32[]{:S(2)}, u32[]{:S(2)}) collective-permute-start(bf16[1024,512]{1,0:T(8,128)(2,1)S(1)} %pick_rows.8), channel_id=1, source_target_pairs={{0,64},{32,96},{64,0},{96,32},{1,65},{33,97},{65,1},{97,33},{2,66}... | collective-permute-start | bytes 3145736 | tf_op jit(solution)/shard_map/ppermute | solution.py:393
  24.8 13.4 %collective-permute-start.10 = (bf16[4,96,1024]{2,1,0:T(8,128)(2,1)S(1)}, bf16[4,96,1024]{2,1,0:T(8,128)(2,1)S(1)}, u32[]{:S(2)}, u32[]{:S(2)}) collective-permute-start(bf16[4,96,1024]{2,1,0:T(8,128)(2,1)S(1)} %bundle.1.refs_0_), channel_id=1, source_target_pairs={{0,16},{1,5},{2,18},{3,7},{4,20},{5,1},{6,22},{7,3},{8,24},{9,13},... | collective-permute-start | bytes 2359304 | tf_op jit(solution)/shard_map/ppermute | solution.py:393
  28.5 18.1 %collective-permute-start.9 = (bf16[4,96,1024]{2,1,0:T(8,128)(2,1)S(1)}, bf16[4,96,1024]{2,1,0:T(8,128)(2,1)S(1)}, u32[]{:S(2)}, u32[]{:S(2)}) collective-permute-start(bf16[4,96,1024]{2,1,0:T(8,128)(2,1)S(1)} %bundle.1.refs_0_), channel_id=1, source_target_pairs={{0,8},{1,3},{2,10},{3,5},{4,12},{5,7},{6,14},{7,1},{8,16},{9,11},{... | collective-permute-start | bytes 2359304 | tf_op jit(solution)/shard_map/ppermute | solution.py:393
  29.2 18.1 %collective-permute-start.8 = (bf16[4,96,1024]{2,1,0:T(8,128)(2,1)S(1)}, bf16[4,96,1024]{2,1,0:T(8,128)(2,1)S(1)}, u32[]{:S(2)}, u32[]{:S(2)}) collective-permute-start(bf16[4,96,1024]{2,1,0:T(8,128)(2,1)S(1)} %bundle.1.refs_0_), channel_id=1, source_target_pairs={{0,24},{1,7},{2,26},{3,1},{4,28},{5,3},{6,30},{7,5},{8,0},{9,15},{... | collective-permute-start | bytes 2359304 | tf_op jit(solution)/shard_map/ppermute | solution.py:393
  32.6 1.6 %copy-start.9 = (bf16[2048,512]{1,0:T(8,128)(2,1)S(1)}, bf16[2048,512]{1,0:T(8,128)(2,1)}, u32[]{:S(2)}) copy-start(bf16[2048,512]{1,0:T(8,128)(2,1)} %refs_1_.9) | copy-start | bytes 6291460
  32.6 1.6 %copy-start.10 = (s32[1,512]{1,0:T(1,128)S(1)}, s32[1,512]{1,0:T(1,128)}, u32[]{:S(2)}) copy-start(s32[1,512]{1,0:T(1,128)} %i0) | copy-start | bytes 6148
  47.6 9.5 %collective-permute-start.14 = (bf16[16,96,1024]{2,1,0:T(8,128)(2,1)S(1)}, bf16[16,96,1024]{2,1,0:T(8,128)(2,1)S(1)}, u32[]{:S(2)}, u32[]{:S(2)}) collective-permute-start(bf16[16,96,1024]{2,1,0:T(8,128)(2,1)S(1)} %half_of_weights.1.a), channel_id=1, source_target_pairs={{0,1},{1,0},{2,3},{3,2},{4,5},{5,4},{6,7},{7,6},{8,9},{9,8},{10,11... | collective-permute-start | bytes 9437192 | tf_op jit(solution)/shard_map/ppermute | solution.py:393
  51.8 14.7 %collective-permute-start.12 = (bf16[512,512]{1,0:T(8,128)(2,1)S(1)}, bf16[512,512]{1,0:T(8,128)(2,1)S(1)}, u32[]{:S(2)}, u32[]{:S(2)}) collective-permute-start(bf16[512,512]{1,0:T(8,128)(2,1)S(1)} %pick_rows.10), channel_id=1, source_target_pairs={{0,32},{32,64},{64,96},{96,0},{1,33},{33,65},{65,97},{97,1},{2,34}... | collective-permute-start | bytes 1572872 | tf_op jit(solution)/shard_map/ppermute | solution.py:393
  53.0 13.6 %collective-permute-start.13 = (bf16[512,512]{1,0:T(8,128)(2,1)S(1)}, bf16[512,512]{1,0:T(8,128)(2,1)S(1)}, u32[]{:S(2)}, u32[]{:S(2)}) collective-permute-start(bf16[512,512]{1,0:T(8,128)(2,1)S(1)} %pick_rows.11), channel_id=1, source_target_pairs={{0,96},{32,0},{64,32},{96,64},{1,97},{33,1},{65,33},{97,65},{2,98}... | collective-permute-start | bytes 1572872 | tf_op jit(solution)/shard_map/ppermute | solution.py:393
  57.6 3.0 %copy-start.6 = (f32[1,512]{1,0:T(1,128)S(1)}, f32[1,512]{1,0:T(1,128)}, u32[]{:S(2)}) copy-start(f32[1,512]{1,0:T(1,128)} %route_ref.3) | copy-start | bytes 6148
  68.0 3.5 %collective-permute-start.15 = (bf16[16,64,512]{2,1,0:T(8,128)(2,1)S(1)}, bf16[16,64,512]{2,1,0:T(8,128)(2,1)S(1)}, u32[]{:S(2)}, u32[]{:S(2)}) collective-permute-start(bf16[16,64,512]{2,1,0:T(8,128)(2,1)S(1)} %get-tuple-element.135), channel_id=1, source_target_pairs={{0,1},{1,0},{2,3},{3,2},{4,5},{5,4},{6,7},{7,6},{8,9},{9,8},{10,11... | collective-permute-start | bytes 3145736 | tf_op jit(solution)/shard_map/ppermute | solution.py:393
  71.5 4.2 %collective-permute-start.16 = (bf16[16,128,512]{2,1,0:T(8,128)(2,1)S(1)}, bf16[16,128,512]{2,1,0:T(8,128)(2,1)S(1)}, u32[]{:S(2)}, u32[]{:S(2)}) collective-permute-start(bf16[16,128,512]{2,1,0:T(8,128)(2,1)S(1)} %get-tuple-element.137), channel_id=1, source_target_pairs={{0,1},{1,0},{2,3},{3,2},{4,5},{5,4},{6,7},{7,6},{8,9},{9,8},{10,11... | collective-permute-start | bytes 6291464 | tf_op jit(solution)/shard_map/ppermute | solution.py:393
  76.6 1.3 collective-permute-start.17
  79.1 20.7 %collective-permute-start.18 = (bf16[4,192,512]{2,1,0:T(8,128)(2,1)S(1)}, bf16[4,192,512]{2,1,0:T(8,128)(2,1)S(1)}, u32[]{:S(2)}, u32[]{:S(2)}) collective-permute-start(bf16[4,192,512]{2,1,0:T(8,128)(2,1)S(1)} %get-tuple-element.146), channel_id=1, source_target_pairs={{0,4},{1,17},{2,6},{3,19},{4,0},{5,21},{6,2},{7,23},{8,12},{9,25},... | collective-permute-start | bytes 2359304 | tf_op jit(solution)/shard_map/ppermute | solution.py:393
  82.0 18.3 %collective-permute-start.19 = (bf16[4,192,512]{2,1,0:T(8,128)(2,1)S(1)}, bf16[4,192,512]{2,1,0:T(8,128)(2,1)S(1)}, u32[]{:S(2)}, u32[]{:S(2)}) collective-permute-start(bf16[4,192,512]{2,1,0:T(8,128)(2,1)S(1)} %get-tuple-element.147), channel_id=1, source_target_pairs={{0,2},{1,9},{2,4},{3,11},{4,6},{5,13},{6,0},{7,15},{8,10},{9,17},{... | collective-permute-start | bytes 2359304 | tf_op jit(solution)/shard_map/ppermute | solution.py:393
  82.3 18.1 %collective-permute-start.20 = (bf16[4,192,512]{2,1,0:T(8,128)(2,1)S(1)}, bf16[4,192,512]{2,1,0:T(8,128)(2,1)S(1)}, u32[]{:S(2)}, u32[]{:S(2)}) collective-permute-start(bf16[4,192,512]{2,1,0:T(8,128)(2,1)S(1)} %get-tuple-element.148), channel_id=1, source_target_pairs={{0,6},{1,25},{2,0},{3,27},{4,2},{5,29},{6,4},{7,31},{8,14},{9,1},{... | collective-permute-start | bytes 2359304 | tf_op jit(solution)/shard_map/ppermute | solution.py:393
  84.6 12.0 %collective-permute-start.21 = (bf16[512,512]{1,0:T(8,128)(2,1)S(1)}, bf16[512,512]{1,0:T(8,128)(2,1)S(1)}, u32[]{:S(2)}, u32[]{:S(2)}) collective-permute-start(bf16[512,512]{1,0:T(8,128)(2,1)S(1)} %get-tuple-element.150), channel_id=1, source_target_pairs={{0,96},{32,0},{64,32},{96,64},{1,97},{33,1},{65,33},{97,65},{2,98}... | collective-permute-start | bytes 1572872 | tf_op jit(solution)/shard_map/ppermute | solution.py:393
  87.3 12.5 %collective-permute-start.22 = (bf16[512,512]{1,0:T(8,128)(2,1)S(1)}, bf16[512,512]{1,0:T(8,128)(2,1)S(1)}, u32[]{:S(2)}, u32[]{:S(2)}) collective-permute-start(bf16[512,512]{1,0:T(8,128)(2,1)S(1)} %get-tuple-element.151), channel_id=1, source_target_pairs={{0,32},{32,64},{64,96},{96,0},{1,33},{33,65},{65,97},{97,1},{2,34}... | collective-permute-start | bytes 1572872 | tf_op jit(solution)/shard_map/ppermute | solution.py:393
  100.6 12.7 %collective-permute-start.26 = (bf16[512,512]{1,0:T(8,128)(2,1)S(1)}, bf16[512,512]{1,0:T(8,128)(2,1)S(1)}, u32[]{:S(2)}, u32[]{:S(2)}) collective-permute-start(bf16[512,512]{1,0:T(8,128)(2,1)S(1)} %get-tuple-element.168), channel_id=1, source_target_pairs={{0,64},{32,96},{64,0},{96,32},{1,65},{33,97},{65,1},{97,33},{2,66}... | collective-permute-start | bytes 1572872 | tf_op jit(solution)/shard_map/ppermute | solution.py:393
  103.3 16.1 %collective-permute-start.23 = (bf16[4,192,512]{2,1,0:T(8,128)(2,1)S(1)}, bf16[4,192,512]{2,1,0:T(8,128)(2,1)S(1)}, u32[]{:S(2)}, u32[]{:S(2)}) collective-permute-start(bf16[4,192,512]{2,1,0:T(8,128)(2,1)S(1)} %get-tuple-element.161), channel_id=1, source_target_pairs={{0,16},{1,5},{2,18},{3,7},{4,20},{5,1},{6,22},{7,3},{8,24},{9,13},... | collective-permute-start | bytes 2359304 | tf_op jit(solution)/shard_map/ppermute | solution.py:393
  106.9 18.1 %collective-permute-start.24 = (bf16[4,192,512]{2,1,0:T(8,128)(2,1)S(1)}, bf16[4,192,512]{2,1,0:T(8,128)(2,1)S(1)}, u32[]{:S(2)}, u32[]{:S(2)}) collective-permute-start(bf16[4,192,512]{2,1,0:T(8,128)(2,1)S(1)} %get-tuple-element.162), channel_id=1, source_target_pairs={{0,8},{1,3},{2,10},{3,5},{4,12},{5,7},{6,14},{7,1},{8,16},{9,11},{... | collective-permute-start | bytes 2359304 | tf_op jit(solution)/shard_map/ppermute | solution.py:393
  107.6 18.1 %collective-permute-start.25 = (bf16[4,192,512]{2,1,0:T(8,128)(2,1)S(1)}, bf16[4,192,512]{2,1,0:T(8,128)(2,1)S(1)}, u32[]{:S(2)}, u32[]{:S(2)}) collective-permute-start(bf16[4,192,512]{2,1,0:T(8,128)(2,1)S(1)} %get-tuple-element.163), channel_id=1, source_target_pairs={{0,24},{1,7},{2,26},{3,1},{4,28},{5,3},{6,30},{7,5},{8,0},{9,15},{... | collective-permute-start | bytes 2359304 | tf_op jit(solution)/shard_map/ppermute | solution.py:393
  119.3 27.9 %copy-start.3 = (f32[1,64,512]{2,1,0:T(8,128)S(1)}, f32[1,64,512]{2,1,0:T(8,128)}, u32[]{:S(2)}) copy-start(f32[1,64,512]{2,1,0:T(8,128)} %param.17) | copy-start | bytes 393220
  119.3 27.9 %copy-start.4 = (f32[1,64,512]{2,1,0:T(8,128)S(1)}, f32[1,64,512]{2,1,0:T(8,128)}, u32[]{:S(2)}) copy-start(f32[1,64,512]{2,1,0:T(8,128)} %param.18) | copy-start | bytes 393220
  119.4 27.9 %copy-start.5 = (f32[1,16,2048]{2,1,0:T(8,128)S(1)}, f32[1,16,2048]{2,1,0:T(8,128)}, u32[]{:S(2)}) copy-start(f32[1,16,2048]{2,1,0:T(8,128)} %param.19) | copy-start | bytes 393220
  128.1 3.6 %collective-permute-start.29 = (f32[3,16,128]{2,1,0:T(8,128)S(1)}, f32[3,16,128]{2,1,0:T(8,128)S(1)}, u32[]{:S(2)}, u32[]{:S(2)}) collective-permute-start(f32[3,16,128]{2,1,0:T(8,128)S(1)} %gram.1), channel_id=1, source_target_pairs={{0,6},{1,7},{2,0},{3,1},{4,2},{5,3},{6,4},{7,5},{8,14},{9,15},{10,... | collective-permute-start | bytes 73736 | tf_op jit(solution)/shard_map/ppermute | solution.py:393
  130.5 3.9 %collective-permute-start.28 = (f32[3,16,128]{2,1,0:T(8,128)S(1)}, f32[3,16,128]{2,1,0:T(8,128)S(1)}, u32[]{:S(2)}, u32[]{:S(2)}) collective-permute-start(f32[3,16,128]{2,1,0:T(8,128)S(1)} %gram.1), channel_id=1, source_target_pairs={{0,2},{1,3},{2,4},{3,5},{4,6},{5,7},{6,0},{7,1},{8,10},{9,11},{10,... | collective-permute-start | bytes 73736 | tf_op jit(solution)/shard_map/ppermute | solution.py:393
  130.5 4.2 %collective-permute-start.27 = (f32[3,16,128]{2,1,0:T(8,128)S(1)}, f32[3,16,128]{2,1,0:T(8,128)S(1)}, u32[]{:S(2)}, u32[]{:S(2)}) collective-permute-start(f32[3,16,128]{2,1,0:T(8,128)S(1)} %gram.1), channel_id=1, source_target_pairs={{0,4},{1,5},{2,6},{3,7},{4,0},{5,1},{6,2},{7,3},{8,12},{9,13},{10,... | collective-permute-start | bytes 73736 | tf_op jit(solution)/shard_map/ppermute | solution.py:393
  134.7 3.7 %collective-permute-start.32 = (f32[3,16,128]{2,1,0:T(8,128)S(1)}, f32[3,16,128]{2,1,0:T(8,128)S(1)}, u32[]{:S(2)}, u32[]{:S(2)}) collective-permute-start(f32[3,16,128]{2,1,0:T(8,128)S(1)} %add_add_fusion.1), channel_id=1, source_target_pairs={{0,24},{1,25},{2,26},{3,27},{4,28},{5,29},{6,30},{7,31},{8,0},{9,1... | collective-permute-start | bytes 73736 | tf_op jit(solution)/shard_map/ppermute | solution.py:393
  137.1 3.9 %collective-permute-start.31 = (f32[3,16,128]{2,1,0:T(8,128)S(1)}, f32[3,16,128]{2,1,0:T(8,128)S(1)}, u32[]{:S(2)}, u32[]{:S(2)}) collective-permute-start(f32[3,16,128]{2,1,0:T(8,128)S(1)} %add_add_fusion.1), channel_id=1, source_target_pairs={{0,8},{1,9},{2,10},{3,11},{4,12},{5,13},{6,14},{7,15},{8,16},{9,17... | collective-permute-start | bytes 73736 | tf_op jit(solution)/shard_map/ppermute | solution.py:393
  137.1 4.2 %collective-permute-start.30 = (f32[3,16,128]{2,1,0:T(8,128)S(1)}, f32[3,16,128]{2,1,0:T(8,128)S(1)}, u32[]{:S(2)}, u32[]{:S(2)}) collective-permute-start(f32[3,16,128]{2,1,0:T(8,128)S(1)} %add_add_fusion.1), channel_id=1, source_target_pairs={{0,16},{1,17},{2,18},{3,19},{4,20},{5,21},{6,22},{7,23},{8,24},{9,... | collective-permute-start | bytes 73736 | tf_op jit(solution)/shard_map/ppermute | solution.py:393
  141.3 5.9 %collective-permute-start.33 = (f32[3,16,128]{2,1,0:T(8,128)S(1)}, f32[3,16,128]{2,1,0:T(8,128)S(1)}, u32[]{:S(2)}, u32[]{:S(2)}) collective-permute-start(f32[3,16,128]{2,1,0:T(8,128)S(1)} %add_add_fusion), channel_id=1, source_target_pairs={{0,1},{1,0},{2,3},{3,2},{4,5},{5,4},{6,7},{7,6},{8,9},{9,8},{10,11... | collective-permute-start | bytes 73736 | tf_op jit(solution)/shard_map/ppermute | solution.py:393

commit v10 on v9

--- a/solution.py
+++ b/solution.py
@@ -363,30 +363,30 @@
     )
 
 
-def scatter_rows(ids_rows, grads):
-    block = 512
-
-    def body(i0, i1, i2, i3, g0, g1, g2, g3, out):
-        row = lax.broadcasted_iota(jnp.int32, (block, TOK_DEV), 0) + block * pl.program_id(0)
+def scatter_rows(ids_rows, grads, half, into=()):
+    block, steps = 512, POOL // 1024
+
+    def body(*refs):
+        row = lax.broadcasted_iota(jnp.int32, (block, TOK_DEV), 0)
+        row += block * (pl.program_id(0) + steps * half)
         acc = None
-        for ids, g in zip((i0, i1, i2, i3), (g0, g1, g2, g3)):
+        for ids, g in zip(refs[:4], refs[4:8]):
             hot = jnp.where(jnp.broadcast_to(ids[...], row.shape) == row, 1.0, 0.0).astype(BF16)
             part = jnp.dot(hot, g[...], preferred_element_type=F32)
             acc = part if acc is None else acc + part
-        out[...] = acc
+        refs[-1][...] = acc
 
     return pl.pallas_call(
         body,
         name="scatter_rows",
-        grid=(POOL // block,),
+        grid=(steps,),
         out_shape=struct((POOL, SLICE), F32),
-        in_specs=[vmem()] * 8,
-        out_specs=pl.BlockSpec((block, SLICE), lambda i: (i, 0)),
+        in_specs=[vmem()] * 8 + [pl.BlockSpec(memory_space=pl.ANY)] * len(into),
+        out_specs=pl.BlockSpec((block, SLICE), lambda i: (i + steps * half, 0)),
+        input_output_aliases={8: 0} if into else {},
         compiler_params=pltpu.CompilerParams(vmem_limit_bytes=24 * MIB),
-        cost_estimate=pl.CostEstimate(
-            flops=2 * POOL * POOL * SLICE, bytes_accessed=6 * MIB, transcendentals=0
-        ),
-    )(*ids_rows, *grads)
+        cost_estimate=pl.CostEstimate(flops=POOL * POOL * SLICE, bytes_accessed=4 * MIB, transcendentals=0),
+    )(*ids_rows, *grads, *into)
 
 
 def shift(block, axis, to):
@@ -409,10 +409,13 @@
     return shift(block, "dp", lambda i: i ^ 1)
 
 
-def sum_dp(value):
-    for around in (around_z, around_x):
-        value = value + sum(around(value, k) for k in (2, 1, 3))
-    return value + other_core(value)
+def sum_dp(value, ids, grads):
+    pool = ()
+    for half, around in enumerate((around_z, around_x)):
+        others = [around(value, k) for k in (1, 3, 2)]
+        others, pool = lax.optimization_barrier((others, (scatter_rows(ids, grads, half, pool),)))
+        value = value + sum(others)
+    return value + other_core(value), pool[0]
 
 
 def pack(gate, up, down):
@@ -565,9 +568,8 @@
     sent, slots[2] = tie((turn_over(parts), slots[2]))
     parts = [sent[0], *to_others(sent, 1)]
     back[2] = around_y(slots[2], 2)
-    pool_grad = scatter_rows(ids, back)
-    parts, pool_grad = tie_far(parts, pool_grad)
-    products = sum_dp(gram(parts))
+    parts, back[2] = tie_far(parts, back[2])
+    products, pool_grad = sum_dp(gram(parts), ids, back)
     outs = finish(
         parts,
         products,

time: 149 us -> 149 us (level)
    pallas_call x1 -> x2, Pallas kernels: 5.97 us -> 6.94 us  [scatter_rows(): pl.pallas_call(body, name='scatter_rows', grid=(steps,), out_shape=struct...]
  transfers between devices with their start and end apart: 34 -> 34, of which waited for: 21 -> 19; matrix products, arithmetic and copies ran while one was open for 0% -> 0% of each run, Pallas kernels for 18% -> 19%
where the time goes in v10:
time: 149 us; the launch traced here: 148 us
  starting transfers between devices  57.8 us (39%)
  waiting for transfers between devices  51.7 us (35%)
  Pallas kernels  36.2 us (24%)
  local copies, waits for them, and re-layouts  1.65 us (1%)
    ppermute x34, starting transfers between devices, shift(): lax.ppermute(block, axis, [(i, to(i)) for i in range(lax.axis_size(axis))])  57.8 us
    ppermute x34, waiting for transfers between devices, shift(): lax.ppermute(block, axis, [(i, to(i)) for i in range(lax.axis_size(axis))])  51.7 us
    pallas_call x6, Pallas kernels, pick_rows(): call(body, 'pick_rows', n_ids + n_pool, shapes, 2 * TOK_DEV * POOL * SLIC...  10.7 us
    pallas_call x2, Pallas kernels, scatter_rows(): pl.pallas_call(body, name='scatter_rows', grid=(steps,), out_shape=struct...  6.94 us
    pallas_call x1, Pallas kernels, forward(): call(body, 'forward', 5, shapes, 2 * TOK_DEV * D * 2 * H, 10 * MIB, [pltp...  3.02 us
  transfers between devices with their start and end apart: 34, of which 19 were waited for; matrix products, arithmetic and copies ran while one was open for 0% of the time, Pallas kernels for 19%

profile of v10, /device:TPU:1, one launch (start us, length us, event | category | flops | bytes accessed | tf_op | source)
XLA Modules:
  0.0 148.4 jit_solution(3966268195988899101)
XLA Ops:
  0.6 2.2 %collective-permute-start.2 = (s32[1,512]{1,0:T(1,128)}, s32[1,512]{1,0:T(1,128)S(1)}, u32[]{:S(2)}, u32[]{:S(2)}) collective-permute-start(s32[1,512]{1,0:T(1,128)} %refs_0_.2), channel_id=1, source_target_pairs={{0,32},{32,64},{64,96},{96,0},{1,33},{33,65},{65,97},{97,1},{2,34}... | collective-permute-start | bytes 6152 | tf_op jit(solution)/shard_map/ppermute | solution.py:393
  2.8 2.6 %collective-permute-start.1 = (s32[1,512]{1,0:T(1,128)}, s32[1,512]{1,0:T(1,128)S(1)}, u32[]{:S(2)}, u32[]{:S(2)}) collective-permute-start(s32[1,512]{1,0:T(1,128)} %refs_0_.2), channel_id=1, source_target_pairs={{0,64},{32,96},{64,0},{96,32},{1,65},{33,97},{65,1},{97,33},{2,66}... | collective-permute-start | bytes 6152 | tf_op jit(solution)/shard_map/ppermute | solution.py:393
  5.4 1.1 collective-permute-start
  6.5 1.6 %copy-done.9 = bf16[2048,512]{1,0:T(8,128)(2,1)S(1)} copy-done((bf16[2048,512]{1,0:T(8,128)(2,1)S(1)}, bf16[2048,512]{1,0:T(8,128)(2,1)}, u32[]{:S(2)}) %copy-start.9) | copy-done | bytes 2097176
  8.1 1.4 pick_rows.7
  9.6 1.4 pick_rows.6
  11.5 2.3 %collective-permute-start.7 = (bf16[512,512]{1,0:T(8,128)(2,1)S(1)}, bf16[512,512]{1,0:T(8,128)(2,1)S(1)}, u32[]{:S(2)}, u32[]{:S(2)}) collective-permute-start(bf16[512,512]{1,0:T(8,128)(2,1)S(1)} %pick_rows.7), channel_id=1, source_target_pairs={{0,96},{32,0},{64,32},{96,64},{1,97},{33,1},{65,33},{97,65},{2,98}... | collective-permute-start | bytes 1572872 | tf_op jit(solution)/shard_map/ppermute | solution.py:393
  14.3 2.8 %collective-permute-start.5 = (bf16[96,1024]{1,0:T(8,128)(2,1)S(1)}, bf16[96,1024]{1,0:T(8,128)(2,1)S(1)}, u32[]{:S(2)}, u32[]{:S(2)}) collective-permute-start(bf16[96,1024]{1,0:T(8,128)(2,1)S(1)} %pack.1.refs_0_), channel_id=1, source_target_pairs={{0,4},{1,17},{2,6},{3,19},{4,0},{5,21},{6,2},{7,23},{8,12},{9,25},... | collective-permute-start | bytes 589832 | tf_op jit(solution)/shard_map/ppermute | solution.py:393
  17.5 2.3 %collective-permute-start.3 = (bf16[96,1024]{1,0:T(8,128)(2,1)S(1)}, bf16[96,1024]{1,0:T(8,128)(2,1)S(1)}, u32[]{:S(2)}, u32[]{:S(2)}) collective-permute-start(bf16[96,1024]{1,0:T(8,128)(2,1)S(1)} %pack.1.refs_0_), channel_id=1, source_target_pairs={{0,6},{1,25},{2,0},{3,27},{4,2},{5,29},{6,4},{7,31},{8,14},{9,1},{... | collective-permute-start | bytes 589832 | tf_op jit(solution)/shard_map/ppermute | solution.py:393
  19.8 2.5 %pick_rows.8 = bf16[1024,512]{1,0:T(8,128)(2,1)S(1)} custom-call(s32[1,512]{1,0:T(1,128)S(1)} %collective-permute-done.1.refs_0_.refs_2_, bf16[2048,512]{1,0:T(8,128)(2,1)S(1)} %copy-done.9, bf16[2048,512]{1,0:T(8,128)(2,1)S(1)} %copy-done.8), custom_call_target="tpu_custom_call" | custom-call | flops 2147483648 | bytes 3145728 | tf_op jit(solution)/shard_map/pick_rows/pallas_call | solution.py:73
  24.7 3.7 %collective-permute-start.10 = (bf16[4,96,1024]{2,1,0:T(8,128)(2,1)S(1)}, bf16[4,96,1024]{2,1,0:T(8,128)(2,1)S(1)}, u32[]{:S(2)}, u32[]{:S(2)}) collective-permute-start(bf16[4,96,1024]{2,1,0:T(8,128)(2,1)S(1)} %bundle.1.refs_0_), channel_id=1, source_target_pairs={{0,16},{1,5},{2,18},{3,7},{4,20},{5,1},{6,22},{7,3},{8,24},{9,13},... | collective-permute-start | bytes 2359304 | tf_op jit(solution)/shard_map/ppermute | solution.py:393
  29.2 1.9 %collective-permute-start.8 = (bf16[4,96,1024]{2,1,0:T(8,128)(2,1)S(1)}, bf16[4,96,1024]{2,1,0:T(8,128)(2,1)S(1)}, u32[]{:S(2)}, u32[]{:S(2)}) collective-permute-start(bf16[4,96,1024]{2,1,0:T(8,128)(2,1)S(1)} %bundle.1.refs_0_), channel_id=1, source_target_pairs={{0,24},{1,7},{2,26},{3,1},{4,28},{5,3},{6,30},{7,5},{8,0},{9,15},{... | collective-permute-start | bytes 2359304 | tf_op jit(solution)/shard_map/ppermute | solution.py:393
  31.1 1.4 pick_rows.10
  32.6 1.4 pick_rows.11
  34.0 2.5 %pick_rows.9 = (bf16[512,512]{1,0:T(8,128)(2,1)S(1)}, bf16[512,512]{1,0:T(8,128)(2,1)S(1)}) custom-call(s32[1,512]{1,0:T(1,128)S(1)} %copy-done.7, bf16[2048,512]{1,0:T(8,128)(2,1)S(1)} %copy-done.9, bf16[2048,512]{1,0:T(8,128)(2,1)S(1)} %copy-done.8), custom_call_target="tpu_custom_call" | custom-call | flops 2147483648 | bytes 3145728 | tf_op jit(solution)/shard_map/pick_rows/pallas_call | solution.py:73
  36.5 1.6 %collective-permute-done.10.refs_2_ = bf16[4,96,1024]{2,1,0:T(8,128)(2,1)S(1)} collective-permute-done((bf16[4,96,1024]{2,1,0:T(8,128)(2,1)S(1)}, bf16[4,96,1024]{2,1,0:T(8,128)(2,1)S(1)}, u32[]{:S(2)}, u32[]{:S(2)}) %collective-permute-start.10) | collective-permute-done | bytes 786464 | tf_op jit(solution)/shard_map/ppermute | solution.py:393
  38.1 8.4 %collective-permute-done.9.refs_1_ = bf16[4,96,1024]{2,1,0:T(8,128)(2,1)S(1)} collective-permute-done((bf16[4,96,1024]{2,1,0:T(8,128)(2,1)S(1)}, bf16[4,96,1024]{2,1,0:T(8,128)(2,1)S(1)}, u32[]{:S(2)}, u32[]{:S(2)}) %collective-permute-start.9) | collective-permute-done | bytes 786464 | tf_op jit(solution)/shard_map/ppermute | solution.py:393
  47.5 4.2 %collective-permute-start.14 = (bf16[16,96,1024]{2,1,0:T(8,128)(2,1)S(1)}, bf16[16,96,1024]{2,1,0:T(8,128)(2,1)S(1)}, u32[]{:S(2)}, u32[]{:S(2)}) collective-permute-start(bf16[16,96,1024]{2,1,0:T(8,128)(2,1)S(1)} %half_of_weights.1.a), channel_id=1, source_target_pairs={{0,1},{1,0},{2,3},{3,2},{4,5},{5,4},{6,7},{7,6},{8,9},{9,8},{10,11... | collective-permute-start | bytes 9437192 | tf_op jit(solution)/shard_map/ppermute | solution.py:393
  51.8 1.1 collective-permute-start.12
  52.9 1.5 %collective-permute-start.13 = (bf16[512,512]{1,0:T(8,128)(2,1)S(1)}, bf16[512,512]{1,0:T(8,128)(2,1)S(1)}, u32[]{:S(2)}, u32[]{:S(2)}) collective-permute-start(bf16[512,512]{1,0:T(8,128)(2,1)S(1)} %pick_rows.11), channel_id=1, source_target_pairs={{0,96},{32,0},{64,32},{96,64},{1,97},{33,1},{65,33},{97,65},{2,98}... | collective-permute-start | bytes 1572872 | tf_op jit(solution)/shard_map/ppermute | solution.py:393
  54.4 2.6 %collective-permute-done.14.b = bf16[16,96,1024]{2,1,0:T(8,128)(2,1)S(1)} collective-permute-done((bf16[16,96,1024]{2,1,0:T(8,128)(2,1)S(1)}, bf16[16,96,1024]{2,1,0:T(8,128)(2,1)S(1)}, u32[]{:S(2)}, u32[]{:S(2)}) %collective-permute-start.14) | collective-permute-done | bytes 3145760 | tf_op jit(solution)/shard_map/ppermute | solution.py:393
  57.5 3.0 %forward.1 = (bf16[512,512]{1,0:T(8,128)(2,1)S(1)}, f32[512,512]{1,0:T(8,128)S(1)}, f32[512,512]{1,0:T(8,128)S(1)}, bf16[4,512,512]{2,1,0:T(8,128)(2,1)S(1)}) custom-call(bf16[512,512]{1,0:T(8,128)(2,1)S(1)} %get-tuple-element.125.x0, bf16[512,512]{1,0:T(8,128)(2,1)S(1)} %collective-permute-done.6.x1, bf16[1024,512]{1,0:T(8,128)(2,1)S(1)} %collective-permute-done.11.x2.c2, ...), custom_call_target="tpu_custom_call" | custom-call | flops 2147483648 | bytes 10485760 | tf_op jit(solution)/shard_map/forward/pallas_call | solution.py:127
  60.5 1.4 backward_early.1
  62.0 4.5 %collective-permute-done.12.c1 = bf16[512,512]{1,0:T(8,128)(2,1)S(1)} collective-permute-done((bf16[512,512]{1,0:T(8,128)(2,1)S(1)}, bf16[512,512]{1,0:T(8,128)(2,1)S(1)}, u32[]{:S(2)}, u32[]{:S(2)}) %collective-permute-start.12) | collective-permute-done | bytes 524320 | tf_op jit(solution)/shard_map/ppermute | solution.py:393
  66.5 1.5 backward_down.1
  68.9 2.5 %backward_in.1 = (bf16[16,128,512]{2,1,0:T(8,128)(2,1)S(1)}, bf16[16,128,512]{2,1,0:T(8,128)(2,1)S(1)}, bf16[512,1024]{1,0:T(8,128)(2,1)S(1)}) custom-call(f32[512,512]{1,0:T(8,128)S(1)} %get-tuple-element.137.hg, f32[512,512]{1,0:T(8,128)S(1)} %get-tuple-element.138.factor, f32[512,512]{1,0:T(8,128)S(1)} %get-tuple-element.139.act_ref, ...), custom_call_target="tpu_custom_call" | custom-call | flops 2147483648 | bytes 10485760 | tf_op jit(solution)/shard_map/backward_in/pallas_call | solution.py:214
  71.6 2.4 %slot_gradients.1 = (bf16[512,512]{1,0:T(8,128)(2,1)S(1)}, bf16[512,512]{1,0:T(8,128)(2,1)S(1)}, bf16[512,512]{1,0:T(8,128)(2,1)S(1)}, bf16[512,512]{1,0:T(8,128)(2,1)S(1)}) custom-call(bf16[512,1024]{1,0:T(8,128)(2,1)S(1)} %get-tuple-element.147.both_ref, bf16[32,96,1024]{2,1,0:T(8,128)(2,1)S(1)} %whole_weights.1.w), custom_call_target="tpu_custom_call" | custom-call | flops 2147483648 | bytes 9437184 | tf_op jit(solution)/shard_map/slot_gradients/pallas_call | solution.py:224
  73.9 1.8 %collective-permute-done.16.b_in = bf16[16,128,512]{2,1,0:T(8,128)(2,1)S(1)} collective-permute-done((bf16[16,128,512]{2,1,0:T(8,128)(2,1)S(1)}, bf16[16,128,512]{2,1,0:T(8,128)(2,1)S(1)}, u32[]{:S(2)}, u32[]{:S(2)}) %collective-permute-start.16) | collective-permute-done | bytes 2097184 | tf_op jit(solution)/shard_map/ppermute | solution.py:393
  76.7 1.1 collective-permute-done.17.t_ref
  77.8 1.3 pair_merge.1
  79.1 2.8 %collective-permute-start.18 = (bf16[4,192,512]{2,1,0:T(8,128)(2,1)S(1)}, bf16[4,192,512]{2,1,0:T(8,128)(2,1)S(1)}, u32[]{:S(2)}, u32[]{:S(2)}) collective-permute-start(bf16[4,192,512]{2,1,0:T(8,128)(2,1)S(1)} %get-tuple-element.154), channel_id=1, source_target_pairs={{0,4},{1,17},{2,6},{3,19},{4,0},{5,21},{6,2},{7,23},{8,12},{9,25},... | collective-permute-start | bytes 2359304 | tf_op jit(solution)/shard_map/ppermute | solution.py:393
  82.2 2.3 %collective-permute-start.20 = (bf16[4,192,512]{2,1,0:T(8,128)(2,1)S(1)}, bf16[4,192,512]{2,1,0:T(8,128)(2,1)S(1)}, u32[]{:S(2)}, u32[]{:S(2)}) collective-permute-start(bf16[4,192,512]{2,1,0:T(8,128)(2,1)S(1)} %get-tuple-element.156), channel_id=1, source_target_pairs={{0,6},{1,25},{2,0},{3,27},{4,2},{5,29},{6,4},{7,31},{8,14},{9,1},{... | collective-permute-start | bytes 2359304 | tf_op jit(solution)/shard_map/ppermute | solution.py:393
  84.6 2.7 %collective-permute-start.21 = (bf16[512,512]{1,0:T(8,128)(2,1)S(1)}, bf16[512,512]{1,0:T(8,128)(2,1)S(1)}, u32[]{:S(2)}, u32[]{:S(2)}) collective-permute-start(bf16[512,512]{1,0:T(8,128)(2,1)S(1)} %get-tuple-element.158), channel_id=1, source_target_pairs={{0,96},{32,0},{64,32},{96,64},{1,97},{33,1},{65,33},{97,65},{2,98}... | collective-permute-start | bytes 1572872 | tf_op jit(solution)/shard_map/ppermute | solution.py:393
  87.2 9.3 %collective-permute-done.21.refs_5_ = bf16[512,512]{1,0:T(8,128)(2,1)S(1)} collective-permute-done((bf16[512,512]{1,0:T(8,128)(2,1)S(1)}, bf16[512,512]{1,0:T(8,128)(2,1)S(1)}, u32[]{:S(2)}, u32[]{:S(2)}) %collective-permute-start.21) | collective-permute-done | bytes 524320 | tf_op jit(solution)/shard_map/ppermute | solution.py:393
  96.5 3.1 %collective-permute-done.22.refs_7_ = bf16[512,512]{1,0:T(8,128)(2,1)S(1)} collective-permute-done((bf16[512,512]{1,0:T(8,128)(2,1)S(1)}, bf16[512,512]{1,0:T(8,128)(2,1)S(1)}, u32[]{:S(2)}, u32[]{:S(2)}) %collective-permute-start.22) | collective-permute-done | bytes 524320 | tf_op jit(solution)/shard_map/ppermute | solution.py:393
  100.6 4.3 %collective-permute-start.23 = (bf16[4,192,512]{2,1,0:T(8,128)(2,1)S(1)}, bf16[4,192,512]{2,1,0:T(8,128)(2,1)S(1)}, u32[]{:S(2)}, u32[]{:S(2)}) collective-permute-start(bf16[4,192,512]{2,1,0:T(8,128)(2,1)S(1)} %get-tuple-element.169), channel_id=1, source_target_pairs={{0,16},{1,5},{2,18},{3,7},{4,20},{5,1},{6,22},{7,3},{8,24},{9,13},... | collective-permute-start | bytes 2359304 | tf_op jit(solution)/shard_map/ppermute | solution.py:393
  105.8 1.8 %collective-permute-start.25 = (bf16[4,192,512]{2,1,0:T(8,128)(2,1)S(1)}, bf16[4,192,512]{2,1,0:T(8,128)(2,1)S(1)}, u32[]{:S(2)}, u32[]{:S(2)}) collective-permute-start(bf16[4,192,512]{2,1,0:T(8,128)(2,1)S(1)} %get-tuple-element.171), channel_id=1, source_target_pairs={{0,24},{1,7},{2,26},{3,1},{4,28},{5,3},{6,30},{7,5},{8,0},{9,15},{... | collective-permute-start | bytes 2359304 | tf_op jit(solution)/shard_map/ppermute | solution.py:393
  107.5 2.0 %collective-permute-start.26 = (bf16[512,512]{1,0:T(8,128)(2,1)S(1)}, bf16[512,512]{1,0:T(8,128)(2,1)S(1)}, u32[]{:S(2)}, u32[]{:S(2)}) collective-permute-start(bf16[512,512]{1,0:T(8,128)(2,1)S(1)} %get-tuple-element.173), channel_id=1, source_target_pairs={{0,64},{32,96},{64,0},{96,32},{1,65},{33,97},{65,1},{97,33},{2,66}... | collective-permute-start | bytes 1572872 | tf_op jit(solution)/shard_map/ppermute | solution.py:393
  109.5 11.1 %collective-permute-done.26.refs_6_ = bf16[512,512]{1,0:T(8,128)(2,1)S(1)} collective-permute-done((bf16[512,512]{1,0:T(8,128)(2,1)S(1)}, bf16[512,512]{1,0:T(8,128)(2,1)S(1)}, u32[]{:S(2)}, u32[]{:S(2)}) %collective-permute-start.26) | collective-permute-done | bytes 524320 | tf_op jit(solution)/shard_map/ppermute | solution.py:393
  120.6 2.4 %collective-permute-done.24.refs_1_.x1 = bf16[4,192,512]{2,1,0:T(8,128)(2,1)S(1)} collective-permute-done((bf16[4,192,512]{2,1,0:T(8,128)(2,1)S(1)}, bf16[4,192,512]{2,1,0:T(8,128)(2,1)S(1)}, u32[]{:S(2)}, u32[]{:S(2)}) %collective-permute-start.24) | collective-permute-done | bytes 786464 | tf_op jit(solution)/shard_map/ppermute | solution.py:393
  123.9 2.3 %gram.1 = f32[3,16,128]{2,1,0:T(8,128)S(1)} custom-call(bf16[4,192,512]{2,1,0:T(8,128)(2,1)S(1)} %get-tuple-element.174.refs_0_.x0, bf16[4,192,512]{2,1,0:T(8,128)(2,1)S(1)} %collective-permute-done.24.refs_1_.x1, bf16[4,192,512]{2,1,0:T(8,128)(2,1)S(1)} %collective-permute-done.23.refs_2_.x2, bf16[4,192,512]{2,1,0:T(8,128)(2,1)S(1)} %collective-permute-done.25.refs_3_.x3), custom_call_target="tpu_custom_call" | custom-call | flops 805306368 | bytes 3145728 | tf_op jit(solution)/shard_map/gram/pallas_call | solution.py:315
  126.2 2.0 %collective-permute-start.29 = (f32[3,16,128]{2,1,0:T(8,128)S(1)}, f32[3,16,128]{2,1,0:T(8,128)S(1)}, u32[]{:S(2)}, u32[]{:S(2)}) collective-permute-start(f32[3,16,128]{2,1,0:T(8,128)S(1)} %gram.1), channel_id=1, source_target_pairs={{0,4},{1,5},{2,6},{3,7},{4,0},{5,1},{6,2},{7,3},{8,12},{9,13},{10,... | collective-permute-start | bytes 73736 | tf_op jit(solution)/shard_map/ppermute | solution.py:393
  128.2 1.7 %collective-permute-start.28 = (f32[3,16,128]{2,1,0:T(8,128)S(1)}, f32[3,16,128]{2,1,0:T(8,128)S(1)}, u32[]{:S(2)}, u32[]{:S(2)}) collective-permute-start(f32[3,16,128]{2,1,0:T(8,128)S(1)} %gram.1), channel_id=1, source_target_pairs={{0,6},{1,7},{2,0},{3,1},{4,2},{5,3},{6,4},{7,5},{8,14},{9,15},{10,... | collective-permute-start | bytes 73736 | tf_op jit(solution)/shard_map/ppermute | solution.py:393
  130.0 3.5 %scatter_rows.2.refs_8_ = f32[2048,512]{1,0:T(8,128)} custom-call(s32[1,512]{1,0:T(1,128)S(1)} %copy-done.7, s32[1,512]{1,0:T(1,128)S(1)} %collective-permute-done.refs_0_.refs_1_, s32[1,512]{1,0:T(1,128)S(1)} %collective-permute-done.1.refs_0_.refs_2_, s32[1,512]{1,0:T(1,128)S(1)} %collective-permute-done.2.refs_0_.refs_3_, ...), custom_call_target="tpu_custom_call" | custom-call | flops 2147483648 | bytes 4194304 | tf_op jit(solution)/shard_map/scatter_rows/pallas_call | solution.py:379
  134.6 1.8 %collective-permute-start.31 = (f32[3,16,128]{2,1,0:T(8,128)S(1)}, f32[3,16,128]{2,1,0:T(8,128)S(1)}, u32[]{:S(2)}, u32[]{:S(2)}) collective-permute-start(f32[3,16,128]{2,1,0:T(8,128)S(1)} %add_add_fusion.1), channel_id=1, source_target_pairs={{0,24},{1,25},{2,26},{3,27},{4,28},{5,29},{6,30},{7,31},{8,0},{9,1... | collective-permute-start | bytes 73736 | tf_op jit(solution)/shard_map/ppermute | solution.py:393
  136.4 3.5 %scatter_rows.3 = f32[2048,512]{1,0:T(8,128)} custom-call(s32[1,512]{1,0:T(1,128)S(1)} %copy-done.7, s32[1,512]{1,0:T(1,128)S(1)} %collective-permute-done.refs_0_.refs_1_, s32[1,512]{1,0:T(1,128)S(1)} %collective-permute-done.1.refs_0_.refs_2_, s32[1,512]{1,0:T(1,128)S(1)} %collective-permute-done.2.refs_0_.refs_3_, ...), custom_call_target="tpu_custom_call", output_to_operand_aliasing={{}: (8, {})} | custom-call | flops 2147483648 | bytes 4194304 | tf_op jit(solution)/shard_map/scatter_rows/pallas_call | solution.py:379
  140.3 5.4 %collective-permute-start.33 = (f32[3,16,128]{2,1,0:T(8,128)S(1)}, f32[3,16,128]{2,1,0:T(8,128)S(1)}, u32[]{:S(2)}, u32[]{:S(2)}) collective-permute-start(f32[3,16,128]{2,1,0:T(8,128)S(1)} %add_add_fusion), channel_id=1, source_target_pairs={{0,1},{1,0},{2,3},{3,2},{4,5},{5,4},{6,7},{7,6},{8,9},{9,8},{10,11... | collective-permute-start | bytes 73736 | tf_op jit(solution)/shard_map/ppermute | solution.py:393
  146.5 1.8 %finish.1 = (f32[64,512]{1,0:T(8,128)}, f32[64,512]{1,0:T(8,128)}, f32[16,2048]{1,0:T(8,128)}, f32[64,512]{1,0:T(8,128)}, f32[64,512]{1,0:T(8,128)}, /*index=5*/f32[16,2048]{1,0:T(8,128)}) custom-call(bf16[4,192,512]{2,1,0:T(8,128)(2,1)S(1)} %get-tuple-element.174.refs_0_.x0, bf16[4,192,512]{2,1,0:T(8,128)(2,1)S(1)} %collective-permute-done.24.refs_1_.x1, ...), custom_call_target="tpu_custom_call" | custom-call | flops 4194304 | bytes 6291456 | tf_op jit(solution)/shard_map/finish/pallas_call | solution.py:361
  (65 shorter events, 13.5 us)
Async XLA Ops:
  0.6 5.9 %collective-permute-start.2 = (s32[1,512]{1,0:T(1,128)}, s32[1,512]{1,0:T(1,128)S(1)}, u32[]{:S(2)}, u32[]{:S(2)}) collective-permute-start(s32[1,512]{1,0:T(1,128)} %refs_0_.2), channel_id=1, source_target_pairs={{0,32},{32,64},{64,96},{96,0},{1,33},{33,65},{65,97},{97,1},{2,34}... | collective-permute-start | bytes 6152 | tf_op jit(solution)/shard_map/ppermute | solution.py:393
  2.8 8.2 %collective-permute-start.1 = (s32[1,512]{1,0:T(1,128)}, s32[1,512]{1,0:T(1,128)S(1)}, u32[]{:S(2)}, u32[]{:S(2)}) collective-permute-start(s32[1,512]{1,0:T(1,128)} %refs_0_.2), channel_id=1, source_target_pairs={{0,64},{32,96},{64,0},{96,32},{1,65},{33,97},{65,1},{97,33},{2,66}... | collective-permute-start | bytes 6152 | tf_op jit(solution)/shard_map/ppermute | solution.py:393
  5.4 4.1 %collective-permute-start = (s32[1,512]{1,0:T(1,128)}, s32[1,512]{1,0:T(1,128)S(1)}, u32[]{:S(2)}, u32[]{:S(2)}) collective-permute-start(s32[1,512]{1,0:T(1,128)} %refs_0_.2), channel_id=1, source_target_pairs={{0,96},{32,0},{64,32},{96,64},{1,97},{33,1},{65,33},{97,65},{2,98}... | collective-permute-start | bytes 6152 | tf_op jit(solution)/shard_map/ppermute | solution.py:393
  6.5 1.6 %copy-start.9 = (bf16[2048,512]{1,0:T(8,128)(2,1)S(1)}, bf16[2048,512]{1,0:T(8,128)(2,1)}, u32[]{:S(2)}) copy-start(bf16[2048,512]{1,0:T(8,128)(2,1)} %refs_1_.9) | copy-start | bytes 6291460
  9.5 4.2 %copy-start = (f32[1,64,512]{2,1,0:T(8,128)S(1)}, f32[1,64,512]{2,1,0:T(8,128)}, u32[]{:S(2)}) copy-start(f32[1,64,512]{2,1,0:T(8,128)} %param.14) | copy-start | bytes 393220
  9.5 4.2 %copy-start.1 = (f32[1,64,512]{2,1,0:T(8,128)S(1)}, f32[1,64,512]{2,1,0:T(8,128)}, u32[]{:S(2)}) copy-start(f32[1,64,512]{2,1,0:T(8,128)} %param.15) | copy-start | bytes 393220
  9.5 4.2 %copy-start.2 = (f32[1,16,2048]{2,1,0:T(8,128)S(1)}, f32[1,16,2048]{2,1,0:T(8,128)}, u32[]{:S(2)}) copy-start(f32[1,16,2048]{2,1,0:T(8,128)} %param.16) | copy-start | bytes 393220
  9.6 10.3 %copy-start.8 = (bf16[2048,512]{1,0:T(8,128)(2,1)S(1)}, bf16[2048,512]{1,0:T(8,128)(2,1)}, u32[]{:S(2)}) copy-start(bf16[2048,512]{1,0:T(8,128)(2,1)} %refs_1_.11) | copy-start | bytes 6291460
  11.0 13.2 %collective-permute-start.6 = (bf16[512,512]{1,0:T(8,128)(2,1)S(1)}, bf16[512,512]{1,0:T(8,128)(2,1)S(1)}, u32[]{:S(2)}, u32[]{:S(2)}) collective-permute-start(bf16[512,512]{1,0:T(8,128)(2,1)S(1)} %pick_rows.6), channel_id=1, source_target_pairs={{0,32},{32,64},{64,96},{96,0},{1,33},{33,65},{65,97},{97,1},{2,34}... | collective-permute-start | bytes 1572872 | tf_op jit(solution)/shard_map/ppermute | solution.py:393
  11.5 12.7 %collective-permute-start.7 = (bf16[512,512]{1,0:T(8,128)(2,1)S(1)}, bf16[512,512]{1,0:T(8,128)(2,1)S(1)}, u32[]{:S(2)}, u32[]{:S(2)}) collective-permute-start(bf16[512,512]{1,0:T(8,128)(2,1)S(1)} %pick_rows.7), channel_id=1, source_target_pairs={{0,96},{32,0},{64,32},{96,64},{1,97},{33,1},{65,33},{97,65},{2,98}... | collective-permute-start | bytes 1572872 | tf_op jit(solution)/shard_map/ppermute | solution.py:393
  14.3 8.0 %collective-permute-start.5 = (bf16[96,1024]{1,0:T(8,128)(2,1)S(1)}, bf16[96,1024]{1,0:T(8,128)(2,1)S(1)}, u32[]{:S(2)}, u32[]{:S(2)}) collective-permute-start(bf16[96,1024]{1,0:T(8,128)(2,1)S(1)} %pack.1.refs_0_), channel_id=1, source_target_pairs={{0,4},{1,17},{2,6},{3,19},{4,0},{5,21},{6,2},{7,23},{8,12},{9,25},... | collective-permute-start | bytes 589832 | tf_op jit(solution)/shard_map/ppermute | solution.py:393
  17.1 6.0 %collective-permute-start.4 = (bf16[96,1024]{1,0:T(8,128)(2,1)S(1)}, bf16[96,1024]{1,0:T(8,128)(2,1)S(1)}, u32[]{:S(2)}, u32[]{:S(2)}) collective-permute-start(bf16[96,1024]{1,0:T(8,128)(2,1)S(1)} %pack.1.refs_0_), channel_id=1, source_target_pairs={{0,2},{1,9},{2,4},{3,11},{4,6},{5,13},{6,0},{7,15},{8,10},{9,17},{... | collective-permute-start | bytes 589832 | tf_op jit(solution)/shard_map/ppermute | solution.py:393
  17.5 5.7 %collective-permute-start.3 = (bf16[96,1024]{1,0:T(8,128)(2,1)S(1)}, bf16[96,1024]{1,0:T(8,128)(2,1)S(1)}, u32[]{:S(2)}, u32[]{:S(2)}) collective-permute-start(bf16[96,1024]{1,0:T(8,128)(2,1)S(1)} %pack.1.refs_0_), channel_id=1, source_target_pairs={{0,6},{1,25},{2,0},{3,27},{4,2},{5,29},{6,4},{7,31},{8,14},{9,1},{... | collective-permute-start | bytes 589832 | tf_op jit(solution)/shard_map/ppermute | solution.py:393
  24.2 23.1 %collective-permute-start.11 = (bf16[1024,512]{1,0:T(8,128)(2,1)S(1)}, bf16[1024,512]{1,0:T(8,128)(2,1)S(1)}, u32[]{:S(2)}, u32[]{:S(2)}) collective-permute-start(bf16[1024,512]{1,0:T(8,128)(2,1)S(1)} %pick_rows.8), channel_id=1, source_target_pairs={{0,64},{32,96},{64,0},{96,32},{1,65},{33,97},{65,1},{97,33},{2,66}... | collective-permute-start | bytes 3145736 | tf_op jit(solution)/shard_map/ppermute | solution.py:393
  24.7 13.5 %collective-permute-start.10 = (bf16[4,96,1024]{2,1,0:T(8,128)(2,1)S(1)}, bf16[4,96,1024]{2,1,0:T(8,128)(2,1)S(1)}, u32[]{:S(2)}, u32[]{:S(2)}) collective-permute-start(bf16[4,96,1024]{2,1,0:T(8,128)(2,1)S(1)} %bundle.1.refs_0_), channel_id=1, source_target_pairs={{0,16},{1,5},{2,18},{3,7},{4,20},{5,1},{6,22},{7,3},{8,24},{9,13},... | collective-permute-start | bytes 2359304 | tf_op jit(solution)/shard_map/ppermute | solution.py:393
  28.4 18.1 %collective-permute-start.9 = (bf16[4,96,1024]{2,1,0:T(8,128)(2,1)S(1)}, bf16[4,96,1024]{2,1,0:T(8,128)(2,1)S(1)}, u32[]{:S(2)}, u32[]{:S(2)}) collective-permute-start(bf16[4,96,1024]{2,1,0:T(8,128)(2,1)S(1)} %bundle.1.refs_0_), channel_id=1, source_target_pairs={{0,8},{1,3},{2,10},{3,5},{4,12},{5,7},{6,14},{7,1},{8,16},{9,11},{... | collective-permute-start | bytes 2359304 | tf_op jit(solution)/shard_map/ppermute | solution.py:393
  29.2 18.1 %collective-permute-start.8 = (bf16[4,96,1024]{2,1,0:T(8,128)(2,1)S(1)}, bf16[4,96,1024]{2,1,0:T(8,128)(2,1)S(1)}, u32[]{:S(2)}, u32[]{:S(2)}) collective-permute-start(bf16[4,96,1024]{2,1,0:T(8,128)(2,1)S(1)} %bundle.1.refs_0_), channel_id=1, source_target_pairs={{0,24},{1,7},{2,26},{3,1},{4,28},{5,3},{6,30},{7,5},{8,0},{9,15},{... | collective-permute-start | bytes 2359304 | tf_op jit(solution)/shard_map/ppermute | solution.py:393
  32.5 1.5 copy-start.7
  47.5 9.5 %collective-permute-start.14 = (bf16[16,96,1024]{2,1,0:T(8,128)(2,1)S(1)}, bf16[16,96,1024]{2,1,0:T(8,128)(2,1)S(1)}, u32[]{:S(2)}, u32[]{:S(2)}) collective-permute-start(bf16[16,96,1024]{2,1,0:T(8,128)(2,1)S(1)} %half_of_weights.1.a), channel_id=1, source_target_pairs={{0,1},{1,0},{2,3},{3,2},{4,5},{5,4},{6,7},{7,6},{8,9},{9,8},{10,11... | collective-permute-start | bytes 9437192 | tf_op jit(solution)/shard_map/ppermute | solution.py:393
  51.8 14.7 %collective-permute-start.12 = (bf16[512,512]{1,0:T(8,128)(2,1)S(1)}, bf16[512,512]{1,0:T(8,128)(2,1)S(1)}, u32[]{:S(2)}, u32[]{:S(2)}) collective-permute-start(bf16[512,512]{1,0:T(8,128)(2,1)S(1)} %pick_rows.10), channel_id=1, source_target_pairs={{0,32},{32,64},{64,96},{96,0},{1,33},{33,65},{65,97},{97,1},{2,34}... | collective-permute-start | bytes 1572872 | tf_op jit(solution)/shard_map/ppermute | solution.py:393
  52.9 13.6 %collective-permute-start.13 = (bf16[512,512]{1,0:T(8,128)(2,1)S(1)}, bf16[512,512]{1,0:T(8,128)(2,1)S(1)}, u32[]{:S(2)}, u32[]{:S(2)}) collective-permute-start(bf16[512,512]{1,0:T(8,128)(2,1)S(1)} %pick_rows.11), channel_id=1, source_target_pairs={{0,96},{32,0},{64,32},{96,64},{1,97},{33,1},{65,33},{97,65},{2,98}... | collective-permute-start | bytes 1572872 | tf_op jit(solution)/shard_map/ppermute | solution.py:393
  57.5 3.0 %copy-start.6 = (f32[1,512]{1,0:T(1,128)S(1)}, f32[1,512]{1,0:T(1,128)}, u32[]{:S(2)}) copy-start(f32[1,512]{1,0:T(1,128)} %route_ref.3) | copy-start | bytes 6148
  68.0 3.5 %collective-permute-start.15 = (bf16[16,64,512]{2,1,0:T(8,128)(2,1)S(1)}, bf16[16,64,512]{2,1,0:T(8,128)(2,1)S(1)}, u32[]{:S(2)}, u32[]{:S(2)}) collective-permute-start(bf16[16,64,512]{2,1,0:T(8,128)(2,1)S(1)} %get-tuple-element.143), channel_id=1, source_target_pairs={{0,1},{1,0},{2,3},{3,2},{4,5},{5,4},{6,7},{7,6},{8,9},{9,8},{10,11... | collective-permute-start | bytes 3145736 | tf_op jit(solution)/shard_map/ppermute | solution.py:393
  71.4 4.2 %collective-permute-start.16 = (bf16[16,128,512]{2,1,0:T(8,128)(2,1)S(1)}, bf16[16,128,512]{2,1,0:T(8,128)(2,1)S(1)}, u32[]{:S(2)}, u32[]{:S(2)}) collective-permute-start(bf16[16,128,512]{2,1,0:T(8,128)(2,1)S(1)} %get-tuple-element.145), channel_id=1, source_target_pairs={{0,1},{1,0},{2,3},{3,2},{4,5},{5,4},{6,7},{7,6},{8,9},{9,8},{10,11... | collective-permute-start | bytes 6291464 | tf_op jit(solution)/shard_map/ppermute | solution.py:393
  76.5 1.3 collective-permute-start.17
  79.1 20.6 %collective-permute-start.18 = (bf16[4,192,512]{2,1,0:T(8,128)(2,1)S(1)}, bf16[4,192,512]{2,1,0:T(8,128)(2,1)S(1)}, u32[]{:S(2)}, u32[]{:S(2)}) collective-permute-start(bf16[4,192,512]{2,1,0:T(8,128)(2,1)S(1)} %get-tuple-element.154), channel_id=1, source_target_pairs={{0,4},{1,17},{2,6},{3,19},{4,0},{5,21},{6,2},{7,23},{8,12},{9,25},... | collective-permute-start | bytes 2359304 | tf_op jit(solution)/shard_map/ppermute | solution.py:393
  81.9 18.3 %collective-permute-start.19 = (bf16[4,192,512]{2,1,0:T(8,128)(2,1)S(1)}, bf16[4,192,512]{2,1,0:T(8,128)(2,1)S(1)}, u32[]{:S(2)}, u32[]{:S(2)}) collective-permute-start(bf16[4,192,512]{2,1,0:T(8,128)(2,1)S(1)} %get-tuple-element.155), channel_id=1, source_target_pairs={{0,2},{1,9},{2,4},{3,11},{4,6},{5,13},{6,0},{7,15},{8,10},{9,17},{... | collective-permute-start | bytes 2359304 | tf_op jit(solution)/shard_map/ppermute | solution.py:393
  82.2 18.1 %collective-permute-start.20 = (bf16[4,192,512]{2,1,0:T(8,128)(2,1)S(1)}, bf16[4,192,512]{2,1,0:T(8,128)(2,1)S(1)}, u32[]{:S(2)}, u32[]{:S(2)}) collective-permute-start(bf16[4,192,512]{2,1,0:T(8,128)(2,1)S(1)} %get-tuple-element.156), channel_id=1, source_target_pairs={{0,6},{1,25},{2,0},{3,27},{4,2},{5,29},{6,4},{7,31},{8,14},{9,1},{... | collective-permute-start | bytes 2359304 | tf_op jit(solution)/shard_map/ppermute | solution.py:393
  84.6 12.0 %collective-permute-start.21 = (bf16[512,512]{1,0:T(8,128)(2,1)S(1)}, bf16[512,512]{1,0:T(8,128)(2,1)S(1)}, u32[]{:S(2)}, u32[]{:S(2)}) collective-permute-start(bf16[512,512]{1,0:T(8,128)(2,1)S(1)} %get-tuple-element.158), channel_id=1, source_target_pairs={{0,96},{32,0},{64,32},{96,64},{1,97},{33,1},{65,33},{97,65},{2,98}... | collective-permute-start | bytes 1572872 | tf_op jit(solution)/shard_map/ppermute | solution.py:393
  87.2 12.4 %collective-permute-start.22 = (bf16[512,512]{1,0:T(8,128)(2,1)S(1)}, bf16[512,512]{1,0:T(8,128)(2,1)S(1)}, u32[]{:S(2)}, u32[]{:S(2)}) collective-permute-start(bf16[512,512]{1,0:T(8,128)(2,1)S(1)} %get-tuple-element.159), channel_id=1, source_target_pairs={{0,32},{32,64},{64,96},{96,0},{1,33},{33,65},{65,97},{97,1},{2,34}... | collective-permute-start | bytes 1572872 | tf_op jit(solution)/shard_map/ppermute | solution.py:393
  100.6 20.0 %collective-permute-start.23 = (bf16[4,192,512]{2,1,0:T(8,128)(2,1)S(1)}, bf16[4,192,512]{2,1,0:T(8,128)(2,1)S(1)}, u32[]{:S(2)}, u32[]{:S(2)}) collective-permute-start(bf16[4,192,512]{2,1,0:T(8,128)(2,1)S(1)} %get-tuple-element.169), channel_id=1, source_target_pairs={{0,16},{1,5},{2,18},{3,7},{4,20},{5,1},{6,22},{7,3},{8,24},{9,13},... | collective-permute-start | bytes 2359304 | tf_op jit(solution)/shard_map/ppermute | solution.py:393
  104.8 18.1 %collective-permute-start.24 = (bf16[4,192,512]{2,1,0:T(8,128)(2,1)S(1)}, bf16[4,192,512]{2,1,0:T(8,128)(2,1)S(1)}, u32[]{:S(2)}, u32[]{:S(2)}) collective-permute-start(bf16[4,192,512]{2,1,0:T(8,128)(2,1)S(1)} %get-tuple-element.170), channel_id=1, source_target_pairs={{0,8},{1,3},{2,10},{3,5},{4,12},{5,7},{6,14},{7,1},{8,16},{9,11},{... | collective-permute-start | bytes 2359304 | tf_op jit(solution)/shard_map/ppermute | solution.py:393
  105.8 18.1 %collective-permute-start.25 = (bf16[4,192,512]{2,1,0:T(8,128)(2,1)S(1)}, bf16[4,192,512]{2,1,0:T(8,128)(2,1)S(1)}, u32[]{:S(2)}, u32[]{:S(2)}) collective-permute-start(bf16[4,192,512]{2,1,0:T(8,128)(2,1)S(1)} %get-tuple-element.171), channel_id=1, source_target_pairs={{0,24},{1,7},{2,26},{3,1},{4,28},{5,3},{6,30},{7,5},{8,0},{9,15},{... | collective-permute-start | bytes 2359304 | tf_op jit(solution)/shard_map/ppermute | solution.py:393
  107.5 13.1 %collective-permute-start.26 = (bf16[512,512]{1,0:T(8,128)(2,1)S(1)}, bf16[512,512]{1,0:T(8,128)(2,1)S(1)}, u32[]{:S(2)}, u32[]{:S(2)}) collective-permute-start(bf16[512,512]{1,0:T(8,128)(2,1)S(1)} %get-tuple-element.173), channel_id=1, source_target_pairs={{0,64},{32,96},{64,0},{96,32},{1,65},{33,97},{65,1},{97,33},{2,66}... | collective-permute-start | bytes 1572872 | tf_op jit(solution)/shard_map/ppermute | solution.py:393
  126.2 7.2 %collective-permute-start.29 = (f32[3,16,128]{2,1,0:T(8,128)S(1)}, f32[3,16,128]{2,1,0:T(8,128)S(1)}, u32[]{:S(2)}, u32[]{:S(2)}) collective-permute-start(f32[3,16,128]{2,1,0:T(8,128)S(1)} %gram.1), channel_id=1, source_target_pairs={{0,4},{1,5},{2,6},{3,7},{4,0},{5,1},{6,2},{7,3},{8,12},{9,13},{10,... | collective-permute-start | bytes 73736 | tf_op jit(solution)/shard_map/ppermute | solution.py:393
  128.2 5.2 %collective-permute-start.28 = (f32[3,16,128]{2,1,0:T(8,128)S(1)}, f32[3,16,128]{2,1,0:T(8,128)S(1)}, u32[]{:S(2)}, u32[]{:S(2)}) collective-permute-start(f32[3,16,128]{2,1,0:T(8,128)S(1)} %gram.1), channel_id=1, source_target_pairs={{0,6},{1,7},{2,0},{3,1},{4,2},{5,3},{6,4},{7,5},{8,14},{9,15},{10,... | collective-permute-start | bytes 73736 | tf_op jit(solution)/shard_map/ppermute | solution.py:393
  130.0 3.9 %collective-permute-start.27 = (f32[3,16,128]{2,1,0:T(8,128)S(1)}, f32[3,16,128]{2,1,0:T(8,128)S(1)}, u32[]{:S(2)}, u32[]{:S(2)}) collective-permute-start(f32[3,16,128]{2,1,0:T(8,128)S(1)} %gram.1), channel_id=1, source_target_pairs={{0,2},{1,3},{2,4},{3,5},{4,6},{5,7},{6,0},{7,1},{8,10},{9,11},{10,... | collective-permute-start | bytes 73736 | tf_op jit(solution)/shard_map/ppermute | solution.py:393
  133.9 12.6 %copy-start.3 = (f32[1,64,512]{2,1,0:T(8,128)S(1)}, f32[1,64,512]{2,1,0:T(8,128)}, u32[]{:S(2)}) copy-start(f32[1,64,512]{2,1,0:T(8,128)} %param.17) | copy-start | bytes 393220
  133.9 12.6 %copy-start.4 = (f32[1,64,512]{2,1,0:T(8,128)S(1)}, f32[1,64,512]{2,1,0:T(8,128)}, u32[]{:S(2)}) copy-start(f32[1,64,512]{2,1,0:T(8,128)} %param.18) | copy-start | bytes 393220
  133.9 12.6 %copy-start.5 = (f32[1,16,2048]{2,1,0:T(8,128)S(1)}, f32[1,16,2048]{2,1,0:T(8,128)}, u32[]{:S(2)}) copy-start(f32[1,16,2048]{2,1,0:T(8,128)} %param.19) | copy-start | bytes 393220
  133.9 6.0 %collective-permute-start.32 = (f32[3,16,128]{2,1,0:T(8,128)S(1)}, f32[3,16,128]{2,1,0:T(8,128)S(1)}, u32[]{:S(2)}, u32[]{:S(2)}) collective-permute-start(f32[3,16,128]{2,1,0:T(8,128)S(1)} %add_add_fusion.1), channel_id=1, source_target_pairs={{0,16},{1,17},{2,18},{3,19},{4,20},{5,21},{6,22},{7,23},{8,24},{9,... | collective-permute-start | bytes 73736 | tf_op jit(solution)/shard_map/ppermute | solution.py:393
  134.6 5.3 %collective-permute-start.31 = (f32[3,16,128]{2,1,0:T(8,128)S(1)}, f32[3,16,128]{2,1,0:T(8,128)S(1)}, u32[]{:S(2)}, u32[]{:S(2)}) collective-permute-start(f32[3,16,128]{2,1,0:T(8,128)S(1)} %add_add_fusion.1), channel_id=1, source_target_pairs={{0,24},{1,25},{2,26},{3,27},{4,28},{5,29},{6,30},{7,31},{8,0},{9,1... | collective-permute-start | bytes 73736 | tf_op jit(solution)/shard_map/ppermute | solution.py:393
  136.4 3.9 %collective-permute-start.30 = (f32[3,16,128]{2,1,0:T(8,128)S(1)}, f32[3,16,128]{2,1,0:T(8,128)S(1)}, u32[]{:S(2)}, u32[]{:S(2)}) collective-permute-start(f32[3,16,128]{2,1,0:T(8,128)S(1)} %add_add_fusion.1), channel_id=1, source_target_pairs={{0,8},{1,9},{2,10},{3,11},{4,12},{5,13},{6,14},{7,15},{8,16},{9,17... | collective-permute-start | bytes 73736 | tf_op jit(solution)/shard_map/ppermute | solution.py:393
  140.3 6.2 %collective-permute-start.33 = (f32[3,16,128]{2,1,0:T(8,128)S(1)}, f32[3,16,128]{2,1,0:T(8,128)S(1)}, u32[]{:S(2)}, u32[]{:S(2)}) collective-permute-start(f32[3,16,128]{2,1,0:T(8,128)S(1)} %add_add_fusion), channel_id=1, source_target_pairs={{0,1},{1,0},{2,3},{3,2},{4,5},{5,4},{6,7},{7,6},{8,9},{9,8},{10,11... | collective-permute-start | bytes 73736 | tf_op jit(solution)/shard_map/ppermute | solution.py:393

commit v11 on v10

--- a/solution.py
+++ b/solution.py
@@ -79,6 +79,53 @@
         (4 + 2 * n_ids) * MIB // 2,
         [pltpu.VMEM((TOK_DEV, POOL), BF16)],
     )(*ids_rows, *pools)
+
+
+def pick_two(ids_a, ids_b, pool):
+    block = 512
+
+    def body(a_ref, b_ref, src, out_a, out_b, hot, acc, named):
+        i = pl.program_id(0)
+        both = slice(0, TOK_DEV), slice(TOK_DEV, 2 * TOK_DEV)
+
+        @pl.when(i == 0)
+        def _():
+            for rows, ids in zip(both, (a_ref, b_ref)):
+                named[rows, :] = column(ids[...])
+
+        lane = lax.broadcasted_iota(jnp.int32, (2 * TOK_DEV, 128), 1) + block * i
+        for j in range(block // 128):
+            hot[:, 128 * j : 128 * (j + 1)] = jnp.where(named[...] == lane + 128 * j, 1.0, 0.0).astype(BF16)
+        part = jnp.dot(hot[...], src[...], preferred_element_type=F32)
+
+        @pl.when(i == 0)
+        def _():
+            acc[...] = part
+
+        @pl.when(i > 0)
+        def _():
+            acc[...] += part
+
+        @pl.when(i == POOL // block - 1)
+        def _():
+            for rows, out in zip(both, (out_a, out_b)):
+                out[...] = acc[rows, :].astype(BF16)
+
+    return pl.pallas_call(
+        body,
+        name="pick_two",
+        grid=(POOL // block,),
+        out_shape=[struct((TOK_DEV, SLICE), BF16)] * 2,
+        in_specs=[vmem(), vmem(), pl.BlockSpec((block, SLICE), lambda i: (i, 0))],
+        out_specs=[vmem(), vmem()],
+        scratch_shapes=[
+            pltpu.VMEM((2 * TOK_DEV, block), BF16),
+            pltpu.VMEM((2 * TOK_DEV, SLICE), F32),
+            pltpu.VMEM((2 * TOK_DEV, 128), jnp.int32),
+        ],
+        compiler_params=pltpu.CompilerParams(vmem_limit_bytes=20 * MIB),
+        cost_estimate=pl.CostEstimate(flops=4 * TOK_DEV * POOL * SLICE, bytes_accessed=3 * MIB, transcendentals=0),
+    )(ids_a, ids_b, pltpu.with_memory_space_constraint(pool, pltpu.HBM))
 
 
 def slice_of(k):
@@ -463,8 +510,8 @@
     return [out[1], out[2], out[3]]
 
 
-def tie_far(items, others, last=False):
-    order = (3, 1, 2, 0) if last else (2, 1, 3, 0)
+def tie_in_order(items, others, last=False):
+    order = (3, 1, 2, 0) if last else (1, 3, 2, 0)
     tied, others = lax.optimization_barrier(([items[k] for k in order], others))
     return [tied[order.index(k)] for k in range(4)], others
 
@@ -530,21 +577,21 @@
 
     ids = [token_ids] + [around_y(token_ids, N_EXPERT - k) for k in (1, 2, 3)]
     x, c = [None] * 4, [None] * 4
-    x[1], x[3] = picked(1, pool_tokens), picked(3, pool_tokens)
+    x[1], x[3] = pick_two(ids[1], ids[3], pool_tokens)
     ids, x[1], x[3], shards = tie((ids, x[1], x[3], (gate_weight[0], up_weight[0], down_weight[0])))
 
     packed = pack(*shards)
     blocks = spread(packed, 0)
     x[1], x[3] = around_y(x[1], 1), around_y(x[3], 3)
     (x[2],) = pick_rows(ids[2:3], [pool_tokens, pool_cotangent], stacked=True)
-    blocks, (ids, x[1:]) = tie_far([packed, *blocks], (ids, x[1:]), last=True)
+    blocks, (ids, x[1:]) = tie_in_order([packed, *blocks], (ids, x[1:]), last=True)
 
     block = bundle(blocks)
     blocks = spread(block, 1)
     x[2] = c[2] = around_y(x[2], 2)
     c[1], c[3] = picked(1, pool_cotangent), picked(3, pool_cotangent)
     x[0], c[0] = pick_rows(ids[:1], [pool_tokens, pool_cotangent])
-    blocks, (x, c) = tie_far([block, *blocks], (x, [c[0], c[1], c[3]]), last=True)
+    blocks, (x, c) = tie_in_order([block, *blocks], (x, [c[0], c[1], c[3]]), last=True)
     c = [c[0], c[1], x[2], c[2]]
 
     mine = half_of_weights(blocks)
@@ -564,11 +611,11 @@
     sent = pair_merge(keep, received, mine, other_core(mine))
     parts = [sent[0], *to_others(sent, 0)]
     back = [slots[0], around_y(slots[1], 3), None, around_y(slots[3], 1)]
-    parts, (back[1], back[3]) = tie_far(parts, (back[1], back[3]))
+    parts, (back[1], back[3]) = tie_in_order(parts, (back[1], back[3]))
     sent, slots[2] = tie((turn_over(parts), slots[2]))
     parts = [sent[0], *to_others(sent, 1)]
     back[2] = around_y(slots[2], 2)
-    parts, back[2] = tie_far(parts, back[2])
+    parts, back[2] = tie_in_order(parts, back[2])
     products, pool_grad = sum_dp(gram(parts), ids, back)
     outs = finish(
         parts,

time: 149 us -> 152 us (1.020)
  waiting for transfers between devices: 51.7 us -> 57.1 us
  starting transfers between devices: 57.8 us -> 54.8 us
  Pallas kernels: 36.2 us -> 38.5 us
  local copies, waits for them, and re-layouts: 1.65 us -> 0.05 us
    ppermute x34, waiting for transfers between devices: 51.7 us -> 57.1 us  [shift(): lax.ppermute(block, axis, [(i, to(i)) for i in range(lax.axis_size(axis))])]
    pallas_call x0 -> x1, Pallas kernels: none -> 5.06 us  [pick_two(): pl.pallas_call(body, name='pick_two', grid=(POOL // block,), out_shape=[s...]
    ppermute x34, starting transfers between devices: 57.8 us -> 54.8 us  [shift(): lax.ppermute(block, axis, [(i, to(i)) for i in range(lax.axis_size(axis))])]
    pallas_call x6 -> x4, Pallas kernels: 10.7 us -> 7.9 us  [pick_rows(): call(body, 'pick_rows', n_ids + n_pool, shapes, 2 * TOK_DEV * POOL * SLIC...]
    unnamed x20, local copies, waits for them, and re-layouts: 1.65 us -> 0.05 us
  transfers between devices with their start and end apart: 34 -> 34, of which waited for: 19 -> 21; matrix products, arithmetic and copies ran while one was open for 0% -> 0% of each run, Pallas kernels for 19% -> 20%
where the time goes in v11:
time: 152 us; the launch traced here: 151 us
  waiting for transfers between devices  57.1 us (38%)
  starting transfers between devices  54.8 us (36%)
  Pallas kernels  38.5 us (25%)
    ppermute x34, waiting for transfers between devices, shift(): lax.ppermute(block, axis, [(i, to(i)) for i in range(lax.axis_size(axis))])  57.1 us
    ppermute x34, starting transfers between devices, shift(): lax.ppermute(block, axis, [(i, to(i)) for i in range(lax.axis_size(axis))])  54.8 us
    pallas_call x4, Pallas kernels, pick_rows(): call(body, 'pick_rows', n_ids + n_pool, shapes, 2 * TOK_DEV * POOL * SLIC...  7.9 us
    pallas_call x2, Pallas kernels, scatter_rows(): pl.pallas_call(body, name='scatter_rows', grid=(steps,), out_shape=struct...  6.94 us
    pallas_call x1, Pallas kernels, pick_two(): pl.pallas_call(body, name='pick_two', grid=(POOL // block,), out_shape=[s...  5.06 us
  transfers between devices with their start and end apart: 34, of which 21 were waited for; matrix products, arithmetic and copies ran while one was open for 0% of the time, Pallas kernels for 20%

profile of v11, /device:TPU:1, one launch (start us, length us, event | category | flops | bytes accessed | tf_op | source)
XLA Modules:
  0.0 151.5 jit_solution(16802903332976186451)
XLA Ops:
  0.7 3.6 %collective-permute-start = (s32[1,512]{1,0:T(1,128)}, s32[1,512]{1,0:T(1,128)S(1)}, u32[]{:S(2)}, u32[]{:S(2)}) collective-permute-start(s32[1,512]{1,0:T(1,128)} %refs_0_.2), channel_id=1, source_target_pairs={{0,96},{32,0},{64,32},{96,64},{1,97},{33,1},{65,33},{97,65},{2,98}... | collective-permute-start | bytes 6152 | tf_op jit(solution)/shard_map/ppermute | solution.py:440
  4.3 1.6 %collective-permute-start.1 = (s32[1,512]{1,0:T(1,128)}, s32[1,512]{1,0:T(1,128)S(1)}, u32[]{:S(2)}, u32[]{:S(2)}) collective-permute-start(s32[1,512]{1,0:T(1,128)} %refs_0_.2), channel_id=1, source_target_pairs={{0,64},{32,96},{64,0},{96,32},{1,65},{33,97},{65,1},{97,33},{2,66}... | collective-permute-start | bytes 6152 | tf_op jit(solution)/shard_map/ppermute | solution.py:440
  6.0 2.2 %collective-permute-done.2.b_ref.refs_0_.refs_3_ = s32[1,512]{1,0:T(1,128)S(1)} collective-permute-done((s32[1,512]{1,0:T(1,128)}, s32[1,512]{1,0:T(1,128)S(1)}, u32[]{:S(2)}, u32[]{:S(2)}) %collective-permute-start.2) | collective-permute-done | bytes 2080 | tf_op jit(solution)/shard_map/ppermute | solution.py:440
  8.2 5.1 %pick_two.1 = (bf16[512,512]{1,0:T(8,128)(2,1)S(1)}, bf16[512,512]{1,0:T(8,128)(2,1)S(1)}) custom-call(s32[1,512]{1,0:T(1,128)S(1)} %collective-permute-done.a_ref.refs_0_.refs_1_, s32[1,512]{1,0:T(1,128)S(1)} %collective-permute-done.2.b_ref.refs_0_.refs_3_, bf16[2048,512]{1,0:T(8,128)(2,1)} %refs_1_.5), custom_call_target="tpu_custom_call" | custom-call | flops 2147483648 | bytes 3145728 | tf_op jit(solution)/shard_map/pick_two/pallas_call | solution.py:114
  13.3 2.7 %collective-permute-start.7 = (bf16[512,512]{1,0:T(8,128)(2,1)S(1)}, bf16[512,512]{1,0:T(8,128)(2,1)S(1)}, u32[]{:S(2)}, u32[]{:S(2)}) collective-permute-start(bf16[512,512]{1,0:T(8,128)(2,1)S(1)} %get-tuple-element.114), channel_id=1, source_target_pairs={{0,96},{32,0},{64,32},{96,64},{1,97},{33,1},{65,33},{97,65},{2,98}... | collective-permute-start | bytes 1572872 | tf_op jit(solution)/shard_map/ppermute | solution.py:440
  16.6 2.8 %collective-permute-start.5 = (bf16[96,1024]{1,0:T(8,128)(2,1)S(1)}, bf16[96,1024]{1,0:T(8,128)(2,1)S(1)}, u32[]{:S(2)}, u32[]{:S(2)}) collective-permute-start(bf16[96,1024]{1,0:T(8,128)(2,1)S(1)} %pack.1.refs_0_), channel_id=1, source_target_pairs={{0,4},{1,17},{2,6},{3,19},{4,0},{5,21},{6,2},{7,23},{8,12},{9,25},... | collective-permute-start | bytes 589832 | tf_op jit(solution)/shard_map/ppermute | solution.py:440
  19.7 2.4 %collective-permute-start.3 = (bf16[96,1024]{1,0:T(8,128)(2,1)S(1)}, bf16[96,1024]{1,0:T(8,128)(2,1)S(1)}, u32[]{:S(2)}, u32[]{:S(2)}) collective-permute-start(bf16[96,1024]{1,0:T(8,128)(2,1)S(1)} %pack.1.refs_0_), channel_id=1, source_target_pairs={{0,6},{1,25},{2,0},{3,27},{4,2},{5,29},{6,4},{7,31},{8,14},{9,1},{... | collective-permute-start | bytes 589832 | tf_op jit(solution)/shard_map/ppermute | solution.py:440
  22.1 2.5 %pick_rows.4 = bf16[1024,512]{1,0:T(8,128)(2,1)S(1)} custom-call(s32[1,512]{1,0:T(1,128)S(1)} %collective-permute-done.1.refs_0_.refs_2_, bf16[2048,512]{1,0:T(8,128)(2,1)S(1)} %copy-done.9, bf16[2048,512]{1,0:T(8,128)(2,1)S(1)} %copy-done.8), custom_call_target="tpu_custom_call" | custom-call | flops 2147483648 | bytes 3145728 | tf_op jit(solution)/shard_map/pick_rows/pallas_call | solution.py:73
  27.1 3.7 %collective-permute-start.10 = (bf16[4,96,1024]{2,1,0:T(8,128)(2,1)S(1)}, bf16[4,96,1024]{2,1,0:T(8,128)(2,1)S(1)}, u32[]{:S(2)}, u32[]{:S(2)}) collective-permute-start(bf16[4,96,1024]{2,1,0:T(8,128)(2,1)S(1)} %bundle.1.refs_0_), channel_id=1, source_target_pairs={{0,16},{1,5},{2,18},{3,7},{4,20},{5,1},{6,22},{7,3},{8,24},{9,13},... | collective-permute-start | bytes 2359304 | tf_op jit(solution)/shard_map/ppermute | solution.py:440
  31.5 2.0 %collective-permute-start.8 = (bf16[4,96,1024]{2,1,0:T(8,128)(2,1)S(1)}, bf16[4,96,1024]{2,1,0:T(8,128)(2,1)S(1)}, u32[]{:S(2)}, u32[]{:S(2)}) collective-permute-start(bf16[4,96,1024]{2,1,0:T(8,128)(2,1)S(1)} %bundle.1.refs_0_), channel_id=1, source_target_pairs={{0,24},{1,7},{2,26},{3,1},{4,28},{5,3},{6,30},{7,5},{8,0},{9,15},{... | collective-permute-start | bytes 2359304 | tf_op jit(solution)/shard_map/ppermute | solution.py:440
  33.5 1.4 pick_rows.6
  34.9 1.4 pick_rows.7
  36.4 2.5 %pick_rows.5 = (bf16[512,512]{1,0:T(8,128)(2,1)S(1)}, bf16[512,512]{1,0:T(8,128)(2,1)S(1)}) custom-call(s32[1,512]{1,0:T(1,128)S(1)} %copy-done.7, bf16[2048,512]{1,0:T(8,128)(2,1)S(1)} %copy-done.9, bf16[2048,512]{1,0:T(8,128)(2,1)S(1)} %copy-done.8), custom_call_target="tpu_custom_call" | custom-call | flops 2147483648 | bytes 3145728 | tf_op jit(solution)/shard_map/pick_rows/pallas_call | solution.py:73
  38.9 1.6 %collective-permute-done.10.refs_2_ = bf16[4,96,1024]{2,1,0:T(8,128)(2,1)S(1)} collective-permute-done((bf16[4,96,1024]{2,1,0:T(8,128)(2,1)S(1)}, bf16[4,96,1024]{2,1,0:T(8,128)(2,1)S(1)}, u32[]{:S(2)}, u32[]{:S(2)}) %collective-permute-start.10) | collective-permute-done | bytes 786464 | tf_op jit(solution)/shard_map/ppermute | solution.py:440
  40.5 8.4 %collective-permute-done.9.refs_1_ = bf16[4,96,1024]{2,1,0:T(8,128)(2,1)S(1)} collective-permute-done((bf16[4,96,1024]{2,1,0:T(8,128)(2,1)S(1)}, bf16[4,96,1024]{2,1,0:T(8,128)(2,1)S(1)}, u32[]{:S(2)}, u32[]{:S(2)}) %collective-permute-start.9) | collective-permute-done | bytes 786464 | tf_op jit(solution)/shard_map/ppermute | solution.py:440
  49.9 3.4 %collective-permute-start.14 = (bf16[16,96,1024]{2,1,0:T(8,128)(2,1)S(1)}, bf16[16,96,1024]{2,1,0:T(8,128)(2,1)S(1)}, u32[]{:S(2)}, u32[]{:S(2)}) collective-permute-start(bf16[16,96,1024]{2,1,0:T(8,128)(2,1)S(1)} %half_of_weights.1.a), channel_id=1, source_target_pairs={{0,1},{1,0},{2,3},{3,2},{4,5},{5,4},{6,7},{7,6},{8,9},{9,8},{10,11... | collective-permute-start | bytes 9437192 | tf_op jit(solution)/shard_map/ppermute | solution.py:440
  53.2 1.7 %collective-permute-start.12 = (bf16[512,512]{1,0:T(8,128)(2,1)S(1)}, bf16[512,512]{1,0:T(8,128)(2,1)S(1)}, u32[]{:S(2)}, u32[]{:S(2)}) collective-permute-start(bf16[512,512]{1,0:T(8,128)(2,1)S(1)} %pick_rows.6), channel_id=1, source_target_pairs={{0,32},{32,64},{64,96},{96,0},{1,33},{33,65},{65,97},{97,1},{2,34}... | collective-permute-start | bytes 1572872 | tf_op jit(solution)/shard_map/ppermute | solution.py:440
  55.9 2.6 %collective-permute-done.14.b = bf16[16,96,1024]{2,1,0:T(8,128)(2,1)S(1)} collective-permute-done((bf16[16,96,1024]{2,1,0:T(8,128)(2,1)S(1)}, bf16[16,96,1024]{2,1,0:T(8,128)(2,1)S(1)}, u32[]{:S(2)}, u32[]{:S(2)}) %collective-permute-start.14) | collective-permute-done | bytes 3145760 | tf_op jit(solution)/shard_map/ppermute | solution.py:440
  59.0 3.0 %forward.1 = (bf16[512,512]{1,0:T(8,128)(2,1)S(1)}, f32[512,512]{1,0:T(8,128)S(1)}, f32[512,512]{1,0:T(8,128)S(1)}, bf16[4,512,512]{2,1,0:T(8,128)(2,1)S(1)}) custom-call(bf16[512,512]{1,0:T(8,128)(2,1)S(1)} %get-tuple-element.129.x0, bf16[512,512]{1,0:T(8,128)(2,1)S(1)} %collective-permute-done.6.x1, bf16[1024,512]{1,0:T(8,128)(2,1)S(1)} %collective-permute-done.11.x2.c2, ...), custom_call_target="tpu_custom_call" | custom-call | flops 2147483648 | bytes 10485760 | tf_op jit(solution)/shard_map/forward/pallas_call | solution.py:174
  62.0 1.4 backward_early.1
  63.5 4.5 %collective-permute-done.12.c1 = bf16[512,512]{1,0:T(8,128)(2,1)S(1)} collective-permute-done((bf16[512,512]{1,0:T(8,128)(2,1)S(1)}, bf16[512,512]{1,0:T(8,128)(2,1)S(1)}, u32[]{:S(2)}, u32[]{:S(2)}) %collective-permute-start.12) | collective-permute-done | bytes 524320 | tf_op jit(solution)/shard_map/ppermute | solution.py:440
  68.1 1.5 backward_down.1
  69.6 1.3 collective-permute-start.15
  70.9 2.5 %backward_in.1 = (bf16[16,128,512]{2,1,0:T(8,128)(2,1)S(1)}, bf16[16,128,512]{2,1,0:T(8,128)(2,1)S(1)}, bf16[512,1024]{1,0:T(8,128)(2,1)S(1)}) custom-call(f32[512,512]{1,0:T(8,128)S(1)} %get-tuple-element.141.hg, f32[512,512]{1,0:T(8,128)S(1)} %get-tuple-element.142.factor, f32[512,512]{1,0:T(8,128)S(1)} %get-tuple-element.143.act_ref, ...), custom_call_target="tpu_custom_call" | custom-call | flops 2147483648 | bytes 10485760 | tf_op jit(solution)/shard_map/backward_in/pallas_call | solution.py:261
  73.5 2.4 %slot_gradients.1 = (bf16[512,512]{1,0:T(8,128)(2,1)S(1)}, bf16[512,512]{1,0:T(8,128)(2,1)S(1)}, bf16[512,512]{1,0:T(8,128)(2,1)S(1)}, bf16[512,512]{1,0:T(8,128)(2,1)S(1)}) custom-call(bf16[512,1024]{1,0:T(8,128)(2,1)S(1)} %get-tuple-element.151.both_ref, bf16[32,96,1024]{2,1,0:T(8,128)(2,1)S(1)} %whole_weights.1.w), custom_call_target="tpu_custom_call" | custom-call | flops 2147483648 | bytes 9437184 | tf_op jit(solution)/shard_map/slot_gradients/pallas_call | solution.py:271
  75.9 1.7 %collective-permute-done.16.b_in = bf16[16,128,512]{2,1,0:T(8,128)(2,1)S(1)} collective-permute-done((bf16[16,128,512]{2,1,0:T(8,128)(2,1)S(1)}, bf16[16,128,512]{2,1,0:T(8,128)(2,1)S(1)}, u32[]{:S(2)}, u32[]{:S(2)}) %collective-permute-start.16) | collective-permute-done | bytes 2097184 | tf_op jit(solution)/shard_map/ppermute | solution.py:440
  79.7 1.3 pair_merge.1
  81.0 1.2 collective-permute-start.18
  82.2 1.5 %collective-permute-start.19 = (bf16[4,192,512]{2,1,0:T(8,128)(2,1)S(1)}, bf16[4,192,512]{2,1,0:T(8,128)(2,1)S(1)}, u32[]{:S(2)}, u32[]{:S(2)}) collective-permute-start(bf16[4,192,512]{2,1,0:T(8,128)(2,1)S(1)} %get-tuple-element.159), channel_id=1, source_target_pairs={{0,6},{1,25},{2,0},{3,27},{4,2},{5,29},{6,4},{7,31},{8,14},{9,1},{... | collective-permute-start | bytes 2359304 | tf_op jit(solution)/shard_map/ppermute | solution.py:440
  84.8 2.7 %collective-permute-start.21 = (bf16[512,512]{1,0:T(8,128)(2,1)S(1)}, bf16[512,512]{1,0:T(8,128)(2,1)S(1)}, u32[]{:S(2)}, u32[]{:S(2)}) collective-permute-start(bf16[512,512]{1,0:T(8,128)(2,1)S(1)} %get-tuple-element.162), channel_id=1, source_target_pairs={{0,96},{32,0},{64,32},{96,64},{1,97},{33,1},{65,33},{97,65},{2,98}... | collective-permute-start | bytes 1572872 | tf_op jit(solution)/shard_map/ppermute | solution.py:440
  87.5 9.4 %collective-permute-done.21.refs_5_ = bf16[512,512]{1,0:T(8,128)(2,1)S(1)} collective-permute-done((bf16[512,512]{1,0:T(8,128)(2,1)S(1)}, bf16[512,512]{1,0:T(8,128)(2,1)S(1)}, u32[]{:S(2)}, u32[]{:S(2)}) %collective-permute-start.21) | collective-permute-done | bytes 524320 | tf_op jit(solution)/shard_map/ppermute | solution.py:440
  96.9 3.1 %collective-permute-done.22.refs_7_ = bf16[512,512]{1,0:T(8,128)(2,1)S(1)} collective-permute-done((bf16[512,512]{1,0:T(8,128)(2,1)S(1)}, bf16[512,512]{1,0:T(8,128)(2,1)S(1)}, u32[]{:S(2)}, u32[]{:S(2)}) %collective-permute-start.22) | collective-permute-done | bytes 524320 | tf_op jit(solution)/shard_map/ppermute | solution.py:440
  101.1 1.6 %collective-permute-done.20.refs_2_ = bf16[4,192,512]{2,1,0:T(8,128)(2,1)S(1)} collective-permute-done((bf16[4,192,512]{2,1,0:T(8,128)(2,1)S(1)}, bf16[4,192,512]{2,1,0:T(8,128)(2,1)S(1)}, u32[]{:S(2)}, u32[]{:S(2)}) %collective-permute-start.20) | collective-permute-done | bytes 786464 | tf_op jit(solution)/shard_map/ppermute | solution.py:440
  102.9 1.4 collective-permute-start.23
  104.3 2.2 %collective-permute-start.24 = (bf16[4,192,512]{2,1,0:T(8,128)(2,1)S(1)}, bf16[4,192,512]{2,1,0:T(8,128)(2,1)S(1)}, u32[]{:S(2)}, u32[]{:S(2)}) collective-permute-start(bf16[4,192,512]{2,1,0:T(8,128)(2,1)S(1)} %get-tuple-element.174), channel_id=1, source_target_pairs={{0,24},{1,7},{2,26},{3,1},{4,28},{5,3},{6,30},{7,5},{8,0},{9,15},{... | collective-permute-start | bytes 2359304 | tf_op jit(solution)/shard_map/ppermute | solution.py:440
  106.5 1.2 collective-permute-start.25
  107.8 2.0 %collective-permute-start.26 = (bf16[512,512]{1,0:T(8,128)(2,1)S(1)}, bf16[512,512]{1,0:T(8,128)(2,1)S(1)}, u32[]{:S(2)}, u32[]{:S(2)}) collective-permute-start(bf16[512,512]{1,0:T(8,128)(2,1)S(1)} %get-tuple-element.177), channel_id=1, source_target_pairs={{0,64},{32,96},{64,0},{96,32},{1,65},{33,97},{65,1},{97,33},{2,66}... | collective-permute-start | bytes 1572872 | tf_op jit(solution)/shard_map/ppermute | solution.py:440
  109.8 10.7 %collective-permute-done.26.refs_6_ = bf16[512,512]{1,0:T(8,128)(2,1)S(1)} collective-permute-done((bf16[512,512]{1,0:T(8,128)(2,1)S(1)}, bf16[512,512]{1,0:T(8,128)(2,1)S(1)}, u32[]{:S(2)}, u32[]{:S(2)}) %collective-permute-start.26) | collective-permute-done | bytes 524320 | tf_op jit(solution)/shard_map/ppermute | solution.py:440
  120.4 3.5 %collective-permute-done.24.refs_3_.x3 = bf16[4,192,512]{2,1,0:T(8,128)(2,1)S(1)} collective-permute-done((bf16[4,192,512]{2,1,0:T(8,128)(2,1)S(1)}, bf16[4,192,512]{2,1,0:T(8,128)(2,1)S(1)}, u32[]{:S(2)}, u32[]{:S(2)}) %collective-permute-start.24) | collective-permute-done | bytes 786464 | tf_op jit(solution)/shard_map/ppermute | solution.py:440
  123.9 1.8 %collective-permute-done.25.refs_2_.x2 = bf16[4,192,512]{2,1,0:T(8,128)(2,1)S(1)} collective-permute-done((bf16[4,192,512]{2,1,0:T(8,128)(2,1)S(1)}, bf16[4,192,512]{2,1,0:T(8,128)(2,1)S(1)}, u32[]{:S(2)}, u32[]{:S(2)}) %collective-permute-start.25) | collective-permute-done | bytes 786464 | tf_op jit(solution)/shard_map/ppermute | solution.py:440
  125.7 2.3 %gram.1 = f32[3,16,128]{2,1,0:T(8,128)S(1)} custom-call(bf16[4,192,512]{2,1,0:T(8,128)(2,1)S(1)} %get-tuple-element.178.refs_0_.x0, bf16[4,192,512]{2,1,0:T(8,128)(2,1)S(1)} %collective-permute-done.23.refs_1_.x1, bf16[4,192,512]{2,1,0:T(8,128)(2,1)S(1)} %collective-permute-done.25.refs_2_.x2, bf16[4,192,512]{2,1,0:T(8,128)(2,1)S(1)} %collective-permute-done.24.refs_3_.x3), custom_call_target="tpu_custom_call" | custom-call | flops 805306368 | bytes 3145728 | tf_op jit(solution)/shard_map/gram/pallas_call | solution.py:362
  128.2 3.1 %collective-permute-start.28 = (f32[3,16,128]{2,1,0:T(8,128)S(1)}, f32[3,16,128]{2,1,0:T(8,128)S(1)}, u32[]{:S(2)}, u32[]{:S(2)}) collective-permute-start(f32[3,16,128]{2,1,0:T(8,128)S(1)} %gram.1), channel_id=1, source_target_pairs={{0,6},{1,7},{2,0},{3,1},{4,2},{5,3},{6,4},{7,5},{8,14},{9,15},{10,... | collective-permute-start | bytes 73736 | tf_op jit(solution)/shard_map/ppermute | solution.py:440
  131.4 3.5 %scatter_rows.2.refs_8_ = f32[2048,512]{1,0:T(8,128)} custom-call(s32[1,512]{1,0:T(1,128)S(1)} %copy-done.7, s32[1,512]{1,0:T(1,128)S(1)} %collective-permute-done.a_ref.refs_0_.refs_1_, s32[1,512]{1,0:T(1,128)S(1)} %collective-permute-done.1.refs_0_.refs_2_, s32[1,512]{1,0:T(1,128)S(1)} %collective-permute-done.2.b_ref.refs_0_.refs_3_, ...), custom_call_target="tpu_custom_call" | custom-call | flops 2147483648 | bytes 4194304 | tf_op jit(solution)/shard_map/scatter_rows/pallas_call | solution.py:426
  135.3 1.2 collective-permute-start.32
  136.5 2.4 %collective-permute-start.31 = (f32[3,16,128]{2,1,0:T(8,128)S(1)}, f32[3,16,128]{2,1,0:T(8,128)S(1)}, u32[]{:S(2)}, u32[]{:S(2)}) collective-permute-start(f32[3,16,128]{2,1,0:T(8,128)S(1)} %add_add_fusion.1), channel_id=1, source_target_pairs={{0,24},{1,25},{2,26},{3,27},{4,28},{5,29},{6,30},{7,31},{8,0},{9,1... | collective-permute-start | bytes 73736 | tf_op jit(solution)/shard_map/ppermute | solution.py:440
  138.9 3.5 %scatter_rows.3 = f32[2048,512]{1,0:T(8,128)} custom-call(s32[1,512]{1,0:T(1,128)S(1)} %copy-done.7, s32[1,512]{1,0:T(1,128)S(1)} %collective-permute-done.a_ref.refs_0_.refs_1_, s32[1,512]{1,0:T(1,128)S(1)} %collective-permute-done.1.refs_0_.refs_2_, s32[1,512]{1,0:T(1,128)S(1)} %collective-permute-done.2.b_ref.refs_0_.refs_3_, ...), custom_call_target="tpu_custom_call", output_to_operand_aliasing={{}: (8, {})} | custom-call | flops 2147483648 | bytes 4194304 | tf_op jit(solution)/shard_map/scatter_rows/pallas_call | solution.py:426
  142.8 5.9 %collective-permute-start.33 = (f32[3,16,128]{2,1,0:T(8,128)S(1)}, f32[3,16,128]{2,1,0:T(8,128)S(1)}, u32[]{:S(2)}, u32[]{:S(2)}) collective-permute-start(f32[3,16,128]{2,1,0:T(8,128)S(1)} %add_add_fusion), channel_id=1, source_target_pairs={{0,1},{1,0},{2,3},{3,2},{4,5},{5,4},{6,7},{7,6},{8,9},{9,8},{10,11... | collective-permute-start | bytes 73736 | tf_op jit(solution)/shard_map/ppermute | solution.py:440
  149.6 1.8 %finish.1 = (f32[64,512]{1,0:T(8,128)}, f32[64,512]{1,0:T(8,128)}, f32[16,2048]{1,0:T(8,128)}, f32[64,512]{1,0:T(8,128)}, f32[64,512]{1,0:T(8,128)}, /*index=5*/f32[16,2048]{1,0:T(8,128)}) custom-call(bf16[4,192,512]{2,1,0:T(8,128)(2,1)S(1)} %get-tuple-element.178.refs_0_.x0, bf16[4,192,512]{2,1,0:T(8,128)(2,1)S(1)} %collective-permute-done.23.refs_1_.x1, ...), custom_call_target="tpu_custom_call" | custom-call | flops 4194304 | bytes 6291456 | tf_op jit(solution)/shard_map/finish/pallas_call | solution.py:408
  (64 shorter events, 13.2 us)
Async XLA Ops:
  0.6 21.4 %copy-start.9 = (bf16[2048,512]{1,0:T(8,128)(2,1)S(1)}, bf16[2048,512]{1,0:T(8,128)(2,1)}, u32[]{:S(2)}) copy-start(bf16[2048,512]{1,0:T(8,128)(2,1)} %refs_1_.5) | copy-start | bytes 6291460
  0.6 15.4 %copy-start.2 = (f32[1,16,2048]{2,1,0:T(8,128)S(1)}, f32[1,16,2048]{2,1,0:T(8,128)}, u32[]{:S(2)}) copy-start(f32[1,16,2048]{2,1,0:T(8,128)} %param.16) | copy-start | bytes 393220
  0.7 15.3 %copy-start.1 = (f32[1,64,512]{2,1,0:T(8,128)S(1)}, f32[1,64,512]{2,1,0:T(8,128)}, u32[]{:S(2)}) copy-start(f32[1,64,512]{2,1,0:T(8,128)} %param.15) | copy-start | bytes 393220
  0.7 15.3 %copy-start = (f32[1,64,512]{2,1,0:T(8,128)S(1)}, f32[1,64,512]{2,1,0:T(8,128)}, u32[]{:S(2)}) copy-start(f32[1,64,512]{2,1,0:T(8,128)} %param.14) | copy-start | bytes 393220
  0.7 21.4 %copy-start.8 = (bf16[2048,512]{1,0:T(8,128)(2,1)S(1)}, bf16[2048,512]{1,0:T(8,128)(2,1)}, u32[]{:S(2)}) copy-start(bf16[2048,512]{1,0:T(8,128)(2,1)} %refs_1_.7) | copy-start | bytes 6291460
  0.7 5.3 %collective-permute-start = (s32[1,512]{1,0:T(1,128)}, s32[1,512]{1,0:T(1,128)S(1)}, u32[]{:S(2)}, u32[]{:S(2)}) collective-permute-start(s32[1,512]{1,0:T(1,128)} %refs_0_.2), channel_id=1, source_target_pairs={{0,96},{32,0},{64,32},{96,64},{1,97},{33,1},{65,33},{97,65},{2,98}... | collective-permute-start | bytes 6152 | tf_op jit(solution)/shard_map/ppermute | solution.py:440
  4.3 3.9 %collective-permute-start.2 = (s32[1,512]{1,0:T(1,128)}, s32[1,512]{1,0:T(1,128)S(1)}, u32[]{:S(2)}, u32[]{:S(2)}) collective-permute-start(s32[1,512]{1,0:T(1,128)} %refs_0_.2), channel_id=1, source_target_pairs={{0,32},{32,64},{64,96},{96,0},{1,33},{33,65},{65,97},{97,1},{2,34}... | collective-permute-start | bytes 6152 | tf_op jit(solution)/shard_map/ppermute | solution.py:440
  4.3 8.9 %collective-permute-start.1 = (s32[1,512]{1,0:T(1,128)}, s32[1,512]{1,0:T(1,128)S(1)}, u32[]{:S(2)}, u32[]{:S(2)}) collective-permute-start(s32[1,512]{1,0:T(1,128)} %refs_0_.2), channel_id=1, source_target_pairs={{0,64},{32,96},{64,0},{96,32},{1,65},{33,97},{65,1},{97,33},{2,66}... | collective-permute-start | bytes 6152 | tf_op jit(solution)/shard_map/ppermute | solution.py:440
  13.3 12.6 %collective-permute-start.6 = (bf16[512,512]{1,0:T(8,128)(2,1)S(1)}, bf16[512,512]{1,0:T(8,128)(2,1)S(1)}, u32[]{:S(2)}, u32[]{:S(2)}) collective-permute-start(bf16[512,512]{1,0:T(8,128)(2,1)S(1)} %get-tuple-element.113), channel_id=1, source_target_pairs={{0,32},{32,64},{64,96},{96,0},{1,33},{33,65},{65,97},{97,1},{2,34}... | collective-permute-start | bytes 1572872 | tf_op jit(solution)/shard_map/ppermute | solution.py:440
  13.3 12.5 %collective-permute-start.7 = (bf16[512,512]{1,0:T(8,128)(2,1)S(1)}, bf16[512,512]{1,0:T(8,128)(2,1)S(1)}, u32[]{:S(2)}, u32[]{:S(2)}) collective-permute-start(bf16[512,512]{1,0:T(8,128)(2,1)S(1)} %get-tuple-element.114), channel_id=1, source_target_pairs={{0,96},{32,0},{64,32},{96,64},{1,97},{33,1},{65,33},{97,65},{2,98}... | collective-permute-start | bytes 1572872 | tf_op jit(solution)/shard_map/ppermute | solution.py:440
  16.6 8.0 %collective-permute-start.5 = (bf16[96,1024]{1,0:T(8,128)(2,1)S(1)}, bf16[96,1024]{1,0:T(8,128)(2,1)S(1)}, u32[]{:S(2)}, u32[]{:S(2)}) collective-permute-start(bf16[96,1024]{1,0:T(8,128)(2,1)S(1)} %pack.1.refs_0_), channel_id=1, source_target_pairs={{0,4},{1,17},{2,6},{3,19},{4,0},{5,21},{6,2},{7,23},{8,12},{9,25},... | collective-permute-start | bytes 589832 | tf_op jit(solution)/shard_map/ppermute | solution.py:440
  19.4 6.0 %collective-permute-start.4 = (bf16[96,1024]{1,0:T(8,128)(2,1)S(1)}, bf16[96,1024]{1,0:T(8,128)(2,1)S(1)}, u32[]{:S(2)}, u32[]{:S(2)}) collective-permute-start(bf16[96,1024]{1,0:T(8,128)(2,1)S(1)} %pack.1.refs_0_), channel_id=1, source_target_pairs={{0,2},{1,9},{2,4},{3,11},{4,6},{5,13},{6,0},{7,15},{8,10},{9,17},{... | collective-permute-start | bytes 589832 | tf_op jit(solution)/shard_map/ppermute | solution.py:440
  19.7 5.7 %collective-permute-start.3 = (bf16[96,1024]{1,0:T(8,128)(2,1)S(1)}, bf16[96,1024]{1,0:T(8,128)(2,1)S(1)}, u32[]{:S(2)}, u32[]{:S(2)}) collective-permute-start(bf16[96,1024]{1,0:T(8,128)(2,1)S(1)} %pack.1.refs_0_), channel_id=1, source_target_pairs={{0,6},{1,25},{2,0},{3,27},{4,2},{5,29},{6,4},{7,31},{8,14},{9,1},{... | collective-permute-start | bytes 589832 | tf_op jit(solution)/shard_map/ppermute | solution.py:440
  25.8 23.8 %collective-permute-start.11 = (bf16[1024,512]{1,0:T(8,128)(2,1)S(1)}, bf16[1024,512]{1,0:T(8,128)(2,1)S(1)}, u32[]{:S(2)}, u32[]{:S(2)}) collective-permute-start(bf16[1024,512]{1,0:T(8,128)(2,1)S(1)} %pick_rows.4), channel_id=1, source_target_pairs={{0,64},{32,96},{64,0},{96,32},{1,65},{33,97},{65,1},{97,33},{2,66}... | collective-permute-start | bytes 3145736 | tf_op jit(solution)/shard_map/ppermute | solution.py:440
  27.1 13.4 %collective-permute-start.10 = (bf16[4,96,1024]{2,1,0:T(8,128)(2,1)S(1)}, bf16[4,96,1024]{2,1,0:T(8,128)(2,1)S(1)}, u32[]{:S(2)}, u32[]{:S(2)}) collective-permute-start(bf16[4,96,1024]{2,1,0:T(8,128)(2,1)S(1)} %bundle.1.refs_0_), channel_id=1, source_target_pairs={{0,16},{1,5},{2,18},{3,7},{4,20},{5,1},{6,22},{7,3},{8,24},{9,13},... | collective-permute-start | bytes 2359304 | tf_op jit(solution)/shard_map/ppermute | solution.py:440
  30.8 18.1 %collective-permute-start.9 = (bf16[4,96,1024]{2,1,0:T(8,128)(2,1)S(1)}, bf16[4,96,1024]{2,1,0:T(8,128)(2,1)S(1)}, u32[]{:S(2)}, u32[]{:S(2)}) collective-permute-start(bf16[4,96,1024]{2,1,0:T(8,128)(2,1)S(1)} %bundle.1.refs_0_), channel_id=1, source_target_pairs={{0,8},{1,3},{2,10},{3,5},{4,12},{5,7},{6,14},{7,1},{8,16},{9,11},{... | collective-permute-start | bytes 2359304 | tf_op jit(solution)/shard_map/ppermute | solution.py:440
  31.5 18.1 %collective-permute-start.8 = (bf16[4,96,1024]{2,1,0:T(8,128)(2,1)S(1)}, bf16[4,96,1024]{2,1,0:T(8,128)(2,1)S(1)}, u32[]{:S(2)}, u32[]{:S(2)}) collective-permute-start(bf16[4,96,1024]{2,1,0:T(8,128)(2,1)S(1)} %bundle.1.refs_0_), channel_id=1, source_target_pairs={{0,24},{1,7},{2,26},{3,1},{4,28},{5,3},{6,30},{7,5},{8,0},{9,15},{... | collective-permute-start | bytes 2359304 | tf_op jit(solution)/shard_map/ppermute | solution.py:440
  34.9 1.5 copy-start.7
  49.9 8.6 %collective-permute-start.14 = (bf16[16,96,1024]{2,1,0:T(8,128)(2,1)S(1)}, bf16[16,96,1024]{2,1,0:T(8,128)(2,1)S(1)}, u32[]{:S(2)}, u32[]{:S(2)}) collective-permute-start(bf16[16,96,1024]{2,1,0:T(8,128)(2,1)S(1)} %half_of_weights.1.a), channel_id=1, source_target_pairs={{0,1},{1,0},{2,3},{3,2},{4,5},{5,4},{6,7},{7,6},{8,9},{9,8},{10,11... | collective-permute-start | bytes 9437192 | tf_op jit(solution)/shard_map/ppermute | solution.py:440
  53.2 14.7 %collective-permute-start.12 = (bf16[512,512]{1,0:T(8,128)(2,1)S(1)}, bf16[512,512]{1,0:T(8,128)(2,1)S(1)}, u32[]{:S(2)}, u32[]{:S(2)}) collective-permute-start(bf16[512,512]{1,0:T(8,128)(2,1)S(1)} %pick_rows.6), channel_id=1, source_target_pairs={{0,32},{32,64},{64,96},{96,0},{1,33},{33,65},{65,97},{97,1},{2,34}... | collective-permute-start | bytes 1572872 | tf_op jit(solution)/shard_map/ppermute | solution.py:440
  55.0 13.2 %collective-permute-start.13 = (bf16[512,512]{1,0:T(8,128)(2,1)S(1)}, bf16[512,512]{1,0:T(8,128)(2,1)S(1)}, u32[]{:S(2)}, u32[]{:S(2)}) collective-permute-start(bf16[512,512]{1,0:T(8,128)(2,1)S(1)} %pick_rows.7), channel_id=1, source_target_pairs={{0,96},{32,0},{64,32},{96,64},{1,97},{33,1},{65,33},{97,65},{2,98}... | collective-permute-start | bytes 1572872 | tf_op jit(solution)/shard_map/ppermute | solution.py:440
  59.0 3.0 %copy-start.6 = (f32[1,512]{1,0:T(1,128)S(1)}, f32[1,512]{1,0:T(1,128)}, u32[]{:S(2)}) copy-start(f32[1,512]{1,0:T(1,128)} %route_ref.3) | copy-start | bytes 6148
  69.6 3.8 %collective-permute-start.15 = (bf16[16,64,512]{2,1,0:T(8,128)(2,1)S(1)}, bf16[16,64,512]{2,1,0:T(8,128)(2,1)S(1)}, u32[]{:S(2)}, u32[]{:S(2)}) collective-permute-start(bf16[16,64,512]{2,1,0:T(8,128)(2,1)S(1)} %get-tuple-element.147), channel_id=1, source_target_pairs={{0,1},{1,0},{2,3},{3,2},{4,5},{5,4},{6,7},{7,6},{8,9},{9,8},{10,11... | collective-permute-start | bytes 3145736 | tf_op jit(solution)/shard_map/ppermute | solution.py:440
  73.4 4.2 %collective-permute-start.16 = (bf16[16,128,512]{2,1,0:T(8,128)(2,1)S(1)}, bf16[16,128,512]{2,1,0:T(8,128)(2,1)S(1)}, u32[]{:S(2)}, u32[]{:S(2)}) collective-permute-start(bf16[16,128,512]{2,1,0:T(8,128)(2,1)S(1)} %get-tuple-element.149), channel_id=1, source_target_pairs={{0,1},{1,0},{2,3},{3,2},{4,5},{5,4},{6,7},{7,6},{8,9},{9,8},{10,11... | collective-permute-start | bytes 6291464 | tf_op jit(solution)/shard_map/ppermute | solution.py:440
  78.4 1.3 collective-permute-start.17
  81.0 19.0 %collective-permute-start.18 = (bf16[4,192,512]{2,1,0:T(8,128)(2,1)S(1)}, bf16[4,192,512]{2,1,0:T(8,128)(2,1)S(1)}, u32[]{:S(2)}, u32[]{:S(2)}) collective-permute-start(bf16[4,192,512]{2,1,0:T(8,128)(2,1)S(1)} %get-tuple-element.158), channel_id=1, source_target_pairs={{0,2},{1,9},{2,4},{3,11},{4,6},{5,13},{6,0},{7,15},{8,10},{9,17},{... | collective-permute-start | bytes 2359304 | tf_op jit(solution)/shard_map/ppermute | solution.py:440
  82.2 18.9 %collective-permute-start.19 = (bf16[4,192,512]{2,1,0:T(8,128)(2,1)S(1)}, bf16[4,192,512]{2,1,0:T(8,128)(2,1)S(1)}, u32[]{:S(2)}, u32[]{:S(2)}) collective-permute-start(bf16[4,192,512]{2,1,0:T(8,128)(2,1)S(1)} %get-tuple-element.159), channel_id=1, source_target_pairs={{0,6},{1,25},{2,0},{3,27},{4,2},{5,29},{6,4},{7,31},{8,14},{9,1},{... | collective-permute-start | bytes 2359304 | tf_op jit(solution)/shard_map/ppermute | solution.py:440
  83.8 19.0 %collective-permute-start.20 = (bf16[4,192,512]{2,1,0:T(8,128)(2,1)S(1)}, bf16[4,192,512]{2,1,0:T(8,128)(2,1)S(1)}, u32[]{:S(2)}, u32[]{:S(2)}) collective-permute-start(bf16[4,192,512]{2,1,0:T(8,128)(2,1)S(1)} %get-tuple-element.160), channel_id=1, source_target_pairs={{0,4},{1,17},{2,6},{3,19},{4,0},{5,21},{6,2},{7,23},{8,12},{9,25},... | collective-permute-start | bytes 2359304 | tf_op jit(solution)/shard_map/ppermute | solution.py:440
  84.8 12.0 %collective-permute-start.21 = (bf16[512,512]{1,0:T(8,128)(2,1)S(1)}, bf16[512,512]{1,0:T(8,128)(2,1)S(1)}, u32[]{:S(2)}, u32[]{:S(2)}) collective-permute-start(bf16[512,512]{1,0:T(8,128)(2,1)S(1)} %get-tuple-element.162), channel_id=1, source_target_pairs={{0,96},{32,0},{64,32},{96,64},{1,97},{33,1},{65,33},{97,65},{2,98}... | collective-permute-start | bytes 1572872 | tf_op jit(solution)/shard_map/ppermute | solution.py:440
  87.5 12.5 %collective-permute-start.22 = (bf16[512,512]{1,0:T(8,128)(2,1)S(1)}, bf16[512,512]{1,0:T(8,128)(2,1)S(1)}, u32[]{:S(2)}, u32[]{:S(2)}) collective-permute-start(bf16[512,512]{1,0:T(8,128)(2,1)S(1)} %get-tuple-element.163), channel_id=1, source_target_pairs={{0,32},{32,64},{64,96},{96,0},{1,33},{33,65},{65,97},{97,1},{2,34}... | collective-permute-start | bytes 1572872 | tf_op jit(solution)/shard_map/ppermute | solution.py:440
  102.9 17.5 %collective-permute-start.23 = (bf16[4,192,512]{2,1,0:T(8,128)(2,1)S(1)}, bf16[4,192,512]{2,1,0:T(8,128)(2,1)S(1)}, u32[]{:S(2)}, u32[]{:S(2)}) collective-permute-start(bf16[4,192,512]{2,1,0:T(8,128)(2,1)S(1)} %get-tuple-element.173), channel_id=1, source_target_pairs={{0,8},{1,3},{2,10},{3,5},{4,12},{5,7},{6,14},{7,1},{8,16},{9,11},{... | collective-permute-start | bytes 2359304 | tf_op jit(solution)/shard_map/ppermute | solution.py:440
  104.3 19.6 %collective-permute-start.24 = (bf16[4,192,512]{2,1,0:T(8,128)(2,1)S(1)}, bf16[4,192,512]{2,1,0:T(8,128)(2,1)S(1)}, u32[]{:S(2)}, u32[]{:S(2)}) collective-permute-start(bf16[4,192,512]{2,1,0:T(8,128)(2,1)S(1)} %get-tuple-element.174), channel_id=1, source_target_pairs={{0,24},{1,7},{2,26},{3,1},{4,28},{5,3},{6,30},{7,5},{8,0},{9,15},{... | collective-permute-start | bytes 2359304 | tf_op jit(solution)/shard_map/ppermute | solution.py:440
  106.5 19.2 %collective-permute-start.25 = (bf16[4,192,512]{2,1,0:T(8,128)(2,1)S(1)}, bf16[4,192,512]{2,1,0:T(8,128)(2,1)S(1)}, u32[]{:S(2)}, u32[]{:S(2)}) collective-permute-start(bf16[4,192,512]{2,1,0:T(8,128)(2,1)S(1)} %get-tuple-element.175), channel_id=1, source_target_pairs={{0,16},{1,5},{2,18},{3,7},{4,20},{5,1},{6,22},{7,3},{8,24},{9,13},... | collective-permute-start | bytes 2359304 | tf_op jit(solution)/shard_map/ppermute | solution.py:440
  107.8 12.7 %collective-permute-start.26 = (bf16[512,512]{1,0:T(8,128)(2,1)S(1)}, bf16[512,512]{1,0:T(8,128)(2,1)S(1)}, u32[]{:S(2)}, u32[]{:S(2)}) collective-permute-start(bf16[512,512]{1,0:T(8,128)(2,1)S(1)} %get-tuple-element.177), channel_id=1, source_target_pairs={{0,64},{32,96},{64,0},{96,32},{1,65},{33,97},{65,1},{97,33},{2,66}... | collective-permute-start | bytes 1572872 | tf_op jit(solution)/shard_map/ppermute | solution.py:440
  128.1 6.7 %collective-permute-start.29 = (f32[3,16,128]{2,1,0:T(8,128)S(1)}, f32[3,16,128]{2,1,0:T(8,128)S(1)}, u32[]{:S(2)}, u32[]{:S(2)}) collective-permute-start(f32[3,16,128]{2,1,0:T(8,128)S(1)} %gram.1), channel_id=1, source_target_pairs={{0,4},{1,5},{2,6},{3,7},{4,0},{5,1},{6,2},{7,3},{8,12},{9,13},{10,... | collective-permute-start | bytes 73736 | tf_op jit(solution)/shard_map/ppermute | solution.py:440
  128.2 6.6 %collective-permute-start.28 = (f32[3,16,128]{2,1,0:T(8,128)S(1)}, f32[3,16,128]{2,1,0:T(8,128)S(1)}, u32[]{:S(2)}, u32[]{:S(2)}) collective-permute-start(f32[3,16,128]{2,1,0:T(8,128)S(1)} %gram.1), channel_id=1, source_target_pairs={{0,6},{1,7},{2,0},{3,1},{4,2},{5,3},{6,4},{7,5},{8,14},{9,15},{10,... | collective-permute-start | bytes 73736 | tf_op jit(solution)/shard_map/ppermute | solution.py:440
  131.4 3.9 %collective-permute-start.27 = (f32[3,16,128]{2,1,0:T(8,128)S(1)}, f32[3,16,128]{2,1,0:T(8,128)S(1)}, u32[]{:S(2)}, u32[]{:S(2)}) collective-permute-start(f32[3,16,128]{2,1,0:T(8,128)S(1)} %gram.1), channel_id=1, source_target_pairs={{0,2},{1,3},{2,4},{3,5},{4,6},{5,7},{6,0},{7,1},{8,10},{9,11},{10,... | collective-permute-start | bytes 73736 | tf_op jit(solution)/shard_map/ppermute | solution.py:440
  135.3 14.4 %copy-start.3 = (f32[1,64,512]{2,1,0:T(8,128)S(1)}, f32[1,64,512]{2,1,0:T(8,128)}, u32[]{:S(2)}) copy-start(f32[1,64,512]{2,1,0:T(8,128)} %param.17) | copy-start | bytes 393220
  135.3 14.3 %copy-start.4 = (f32[1,64,512]{2,1,0:T(8,128)S(1)}, f32[1,64,512]{2,1,0:T(8,128)}, u32[]{:S(2)}) copy-start(f32[1,64,512]{2,1,0:T(8,128)} %param.18) | copy-start | bytes 393220
  135.3 14.3 %copy-start.5 = (f32[1,16,2048]{2,1,0:T(8,128)S(1)}, f32[1,16,2048]{2,1,0:T(8,128)}, u32[]{:S(2)}) copy-start(f32[1,16,2048]{2,1,0:T(8,128)} %param.19) | copy-start | bytes 393220
  135.3 7.1 %collective-permute-start.32 = (f32[3,16,128]{2,1,0:T(8,128)S(1)}, f32[3,16,128]{2,1,0:T(8,128)S(1)}, u32[]{:S(2)}, u32[]{:S(2)}) collective-permute-start(f32[3,16,128]{2,1,0:T(8,128)S(1)} %add_add_fusion.1), channel_id=1, source_target_pairs={{0,16},{1,17},{2,18},{3,19},{4,20},{5,21},{6,22},{7,23},{8,24},{9,... | collective-permute-start | bytes 73736 | tf_op jit(solution)/shard_map/ppermute | solution.py:440
  136.5 5.9 %collective-permute-start.31 = (f32[3,16,128]{2,1,0:T(8,128)S(1)}, f32[3,16,128]{2,1,0:T(8,128)S(1)}, u32[]{:S(2)}, u32[]{:S(2)}) collective-permute-start(f32[3,16,128]{2,1,0:T(8,128)S(1)} %add_add_fusion.1), channel_id=1, source_target_pairs={{0,24},{1,25},{2,26},{3,27},{4,28},{5,29},{6,30},{7,31},{8,0},{9,1... | collective-permute-start | bytes 73736 | tf_op jit(solution)/shard_map/ppermute | solution.py:440
  138.9 3.9 %collective-permute-start.30 = (f32[3,16,128]{2,1,0:T(8,128)S(1)}, f32[3,16,128]{2,1,0:T(8,128)S(1)}, u32[]{:S(2)}, u32[]{:S(2)}) collective-permute-start(f32[3,16,128]{2,1,0:T(8,128)S(1)} %add_add_fusion.1), channel_id=1, source_target_pairs={{0,8},{1,9},{2,10},{3,11},{4,12},{5,13},{6,14},{7,15},{8,16},{9,17... | collective-permute-start | bytes 73736 | tf_op jit(solution)/shard_map/ppermute | solution.py:440
  142.8 6.8 %collective-permute-start.33 = (f32[3,16,128]{2,1,0:T(8,128)S(1)}, f32[3,16,128]{2,1,0:T(8,128)S(1)}, u32[]{:S(2)}, u32[]{:S(2)}) collective-permute-start(f32[3,16,128]{2,1,0:T(8,128)S(1)} %add_add_fusion), channel_id=1, source_target_pairs={{0,1},{1,0},{2,3},{3,2},{4,5},{5,4},{6,7},{7,6},{8,9},{9,8},{10,11... | collective-permute-start | bytes 73736 | tf_op jit(solution)/shard_map/ppermute | solution.py:440

commit v12 on v10

--- a/solution.py
+++ b/solution.py
@@ -316,8 +316,8 @@
 
 
 def finish(parts, products, gate, up, down, mom_gate, mom_up, mom_down):
-    def body(x0, x1, x2, x3, g_ref, gate_w, up_w, down_w, gate_m, up_m, down_m, new_g, new_u, new_d, next_g, next_u, next_d):
-        g = g_ref[...]
+    def body(x0, x1, x2, x3, g_ref, g_other, gate_w, up_w, down_w, gate_m, up_m, down_m, new_g, new_u, new_d, next_g, next_u, next_d):
+        g = g_ref[...] + g_other[...]
         i = lax.broadcasted_iota(jnp.int32, (3, 16, 128), 1)
         j = lax.broadcasted_iota(jnp.int32, (3, 16, 128), 2)
         c_col = jnp.ones((3, 16, 1), F32)
@@ -358,8 +358,8 @@
                     new_d[:, cols] = down_w[:, cols] - learning_rate * step
 
     wide, tall = struct((64, H), F32), struct((16, D), F32)
-    return call(body, "finish", 11, [wide, wide, tall, wide, wide, tall], 2**22, 6 * MIB)(
-        *parts, products, gate, up, down, mom_gate, mom_up, mom_down
+    return call(body, "finish", 12, [wide, wide, tall, wide, wide, tall], 2**22, 6 * MIB)(
+        *parts, *products, gate, up, down, mom_gate, mom_up, mom_down
     )
 
 
@@ -412,10 +412,10 @@
 def sum_dp(value, ids, grads):
     pool = ()
     for half, around in enumerate((around_z, around_x)):
-        others = [around(value, k) for k in (1, 3, 2)]
+        others = [around(value, k) for k in (2, 1, 3)]
         others, pool = lax.optimization_barrier((others, (scatter_rows(ids, grads, half, pool),)))
         value = value + sum(others)
-    return value + other_core(value), pool[0]
+    return (value, other_core(value)), pool[0]
 
 
 def pack(gate, up, down):

time: 149 us -> 147 us (0.987)
  transfers between devices with their start and end apart: 34 -> 34, of which waited for: 19 -> 17; matrix products, arithmetic and copies ran while one was open for 0% -> 0% of each run, Pallas kernels for 19% -> 19%
where the time goes in v12:
time: 147 us; the launch traced here: 146 us
  starting transfers between devices  56.6 us (39%)
  waiting for transfers between devices  50.9 us (35%)
  Pallas kernels  36.2 us (25%)
  local copies, waits for them, and re-layouts  1.65 us (1%)
    ppermute x34, starting transfers between devices, shift(): lax.ppermute(block, axis, [(i, to(i)) for i in range(lax.axis_size(axis))])  56.6 us
    ppermute x34, waiting for transfers between devices, shift(): lax.ppermute(block, axis, [(i, to(i)) for i in range(lax.axis_size(axis))])  50.9 us
    pallas_call x6, Pallas kernels, pick_rows(): call(body, 'pick_rows', n_ids + n_pool, shapes, 2 * TOK_DEV * POOL * SLIC...  10.7 us
    pallas_call x2, Pallas kernels, scatter_rows(): pl.pallas_call(body, name='scatter_rows', grid=(steps,), out_shape=struct...  6.94 us
    pallas_call x1, Pallas kernels, forward(): call(body, 'forward', 5, shapes, 2 * TOK_DEV * D * 2 * H, 10 * MIB, [pltp...  3.02 us
  transfers between devices with their start and end apart: 34, of which 17 were waited for; matrix products, arithmetic and copies ran while one was open for 0% of the time, Pallas kernels for 19%

profile of v12, /device:TPU:1, one launch (start us, length us, event | category | flops | bytes accessed | tf_op | source)
XLA Modules:
  0.0 146.4 jit_solution(14233545946653400667)
XLA Ops:
  0.6 2.2 %collective-permute-start.2 = (s32[1,512]{1,0:T(1,128)}, s32[1,512]{1,0:T(1,128)S(1)}, u32[]{:S(2)}, u32[]{:S(2)}) collective-permute-start(s32[1,512]{1,0:T(1,128)} %refs_0_.2), channel_id=1, source_target_pairs={{0,32},{32,64},{64,96},{96,0},{1,33},{33,65},{65,97},{97,1},{2,34}... | collective-permute-start | bytes 6152 | tf_op jit(solution)/shard_map/ppermute | solution.py:393
  2.8 2.6 %collective-permute-start.1 = (s32[1,512]{1,0:T(1,128)}, s32[1,512]{1,0:T(1,128)S(1)}, u32[]{:S(2)}, u32[]{:S(2)}) collective-permute-start(s32[1,512]{1,0:T(1,128)} %refs_0_.2), channel_id=1, source_target_pairs={{0,64},{32,96},{64,0},{96,32},{1,65},{33,97},{65,1},{97,33},{2,66}... | collective-permute-start | bytes 6152 | tf_op jit(solution)/shard_map/ppermute | solution.py:393
  6.5 1.6 %copy-done.9 = bf16[2048,512]{1,0:T(8,128)(2,1)S(1)} copy-done((bf16[2048,512]{1,0:T(8,128)(2,1)S(1)}, bf16[2048,512]{1,0:T(8,128)(2,1)}, u32[]{:S(2)}) %copy-start.9) | copy-done | bytes 2097176
  8.1 1.4 pick_rows.7
  9.6 1.4 pick_rows.6
  11.5 2.3 %collective-permute-start.7 = (bf16[512,512]{1,0:T(8,128)(2,1)S(1)}, bf16[512,512]{1,0:T(8,128)(2,1)S(1)}, u32[]{:S(2)}, u32[]{:S(2)}) collective-permute-start(bf16[512,512]{1,0:T(8,128)(2,1)S(1)} %pick_rows.7), channel_id=1, source_target_pairs={{0,96},{32,0},{64,32},{96,64},{1,97},{33,1},{65,33},{97,65},{2,98}... | collective-permute-start | bytes 1572872 | tf_op jit(solution)/shard_map/ppermute | solution.py:393
  14.3 2.8 %collective-permute-start.5 = (bf16[96,1024]{1,0:T(8,128)(2,1)S(1)}, bf16[96,1024]{1,0:T(8,128)(2,1)S(1)}, u32[]{:S(2)}, u32[]{:S(2)}) collective-permute-start(bf16[96,1024]{1,0:T(8,128)(2,1)S(1)} %pack.1.refs_0_), channel_id=1, source_target_pairs={{0,4},{1,17},{2,6},{3,19},{4,0},{5,21},{6,2},{7,23},{8,12},{9,25},... | collective-permute-start | bytes 589832 | tf_op jit(solution)/shard_map/ppermute | solution.py:393
  17.5 2.3 %collective-permute-start.3 = (bf16[96,1024]{1,0:T(8,128)(2,1)S(1)}, bf16[96,1024]{1,0:T(8,128)(2,1)S(1)}, u32[]{:S(2)}, u32[]{:S(2)}) collective-permute-start(bf16[96,1024]{1,0:T(8,128)(2,1)S(1)} %pack.1.refs_0_), channel_id=1, source_target_pairs={{0,6},{1,25},{2,0},{3,27},{4,2},{5,29},{6,4},{7,31},{8,14},{9,1},{... | collective-permute-start | bytes 589832 | tf_op jit(solution)/shard_map/ppermute | solution.py:393
  19.8 2.5 %pick_rows.8 = bf16[1024,512]{1,0:T(8,128)(2,1)S(1)} custom-call(s32[1,512]{1,0:T(1,128)S(1)} %collective-permute-done.1.refs_0_.refs_2_, bf16[2048,512]{1,0:T(8,128)(2,1)S(1)} %copy-done.9, bf16[2048,512]{1,0:T(8,128)(2,1)S(1)} %copy-done.8), custom_call_target="tpu_custom_call" | custom-call | flops 2147483648 | bytes 3145728 | tf_op jit(solution)/shard_map/pick_rows/pallas_call | solution.py:73
  24.7 3.7 %collective-permute-start.10 = (bf16[4,96,1024]{2,1,0:T(8,128)(2,1)S(1)}, bf16[4,96,1024]{2,1,0:T(8,128)(2,1)S(1)}, u32[]{:S(2)}, u32[]{:S(2)}) collective-permute-start(bf16[4,96,1024]{2,1,0:T(8,128)(2,1)S(1)} %bundle.1.refs_0_), channel_id=1, source_target_pairs={{0,16},{1,5},{2,18},{3,7},{4,20},{5,1},{6,22},{7,3},{8,24},{9,13},... | collective-permute-start | bytes 2359304 | tf_op jit(solution)/shard_map/ppermute | solution.py:393
  29.2 1.9 %collective-permute-start.8 = (bf16[4,96,1024]{2,1,0:T(8,128)(2,1)S(1)}, bf16[4,96,1024]{2,1,0:T(8,128)(2,1)S(1)}, u32[]{:S(2)}, u32[]{:S(2)}) collective-permute-start(bf16[4,96,1024]{2,1,0:T(8,128)(2,1)S(1)} %bundle.1.refs_0_), channel_id=1, source_target_pairs={{0,24},{1,7},{2,26},{3,1},{4,28},{5,3},{6,30},{7,5},{8,0},{9,15},{... | collective-permute-start | bytes 2359304 | tf_op jit(solution)/shard_map/ppermute | solution.py:393
  31.1 1.4 pick_rows.10
  32.6 1.4 pick_rows.11
  34.0 2.5 %pick_rows.9 = (bf16[512,512]{1,0:T(8,128)(2,1)S(1)}, bf16[512,512]{1,0:T(8,128)(2,1)S(1)}) custom-call(s32[1,512]{1,0:T(1,128)S(1)} %copy-done.7, bf16[2048,512]{1,0:T(8,128)(2,1)S(1)} %copy-done.9, bf16[2048,512]{1,0:T(8,128)(2,1)S(1)} %copy-done.8), custom_call_target="tpu_custom_call" | custom-call | flops 2147483648 | bytes 3145728 | tf_op jit(solution)/shard_map/pick_rows/pallas_call | solution.py:73
  36.5 1.6 %collective-permute-done.10.refs_2_ = bf16[4,96,1024]{2,1,0:T(8,128)(2,1)S(1)} collective-permute-done((bf16[4,96,1024]{2,1,0:T(8,128)(2,1)S(1)}, bf16[4,96,1024]{2,1,0:T(8,128)(2,1)S(1)}, u32[]{:S(2)}, u32[]{:S(2)}) %collective-permute-start.10) | collective-permute-done | bytes 786464 | tf_op jit(solution)/shard_map/ppermute | solution.py:393
  38.1 8.4 %collective-permute-done.9.refs_1_ = bf16[4,96,1024]{2,1,0:T(8,128)(2,1)S(1)} collective-permute-done((bf16[4,96,1024]{2,1,0:T(8,128)(2,1)S(1)}, bf16[4,96,1024]{2,1,0:T(8,128)(2,1)S(1)}, u32[]{:S(2)}, u32[]{:S(2)}) %collective-permute-start.9) | collective-permute-done | bytes 786464 | tf_op jit(solution)/shard_map/ppermute | solution.py:393
  47.5 4.2 %collective-permute-start.14 = (bf16[16,96,1024]{2,1,0:T(8,128)(2,1)S(1)}, bf16[16,96,1024]{2,1,0:T(8,128)(2,1)S(1)}, u32[]{:S(2)}, u32[]{:S(2)}) collective-permute-start(bf16[16,96,1024]{2,1,0:T(8,128)(2,1)S(1)} %half_of_weights.1.a), channel_id=1, source_target_pairs={{0,1},{1,0},{2,3},{3,2},{4,5},{5,4},{6,7},{7,6},{8,9},{9,8},{10,11... | collective-permute-start | bytes 9437192 | tf_op jit(solution)/shard_map/ppermute | solution.py:393
  51.8 1.1 collective-permute-start.12
  52.9 1.5 %collective-permute-start.13 = (bf16[512,512]{1,0:T(8,128)(2,1)S(1)}, bf16[512,512]{1,0:T(8,128)(2,1)S(1)}, u32[]{:S(2)}, u32[]{:S(2)}) collective-permute-start(bf16[512,512]{1,0:T(8,128)(2,1)S(1)} %pick_rows.11), channel_id=1, source_target_pairs={{0,96},{32,0},{64,32},{96,64},{1,97},{33,1},{65,33},{97,65},{2,98}... | collective-permute-start | bytes 1572872 | tf_op jit(solution)/shard_map/ppermute | solution.py:393
  54.4 2.6 %collective-permute-done.14.b = bf16[16,96,1024]{2,1,0:T(8,128)(2,1)S(1)} collective-permute-done((bf16[16,96,1024]{2,1,0:T(8,128)(2,1)S(1)}, bf16[16,96,1024]{2,1,0:T(8,128)(2,1)S(1)}, u32[]{:S(2)}, u32[]{:S(2)}) %collective-permute-start.14) | collective-permute-done | bytes 3145760 | tf_op jit(solution)/shard_map/ppermute | solution.py:393
  57.5 3.0 %forward.1 = (bf16[512,512]{1,0:T(8,128)(2,1)S(1)}, f32[512,512]{1,0:T(8,128)S(1)}, f32[512,512]{1,0:T(8,128)S(1)}, bf16[4,512,512]{2,1,0:T(8,128)(2,1)S(1)}) custom-call(bf16[512,512]{1,0:T(8,128)(2,1)S(1)} %get-tuple-element.125.x0, bf16[512,512]{1,0:T(8,128)(2,1)S(1)} %collective-permute-done.6.x1, bf16[1024,512]{1,0:T(8,128)(2,1)S(1)} %collective-permute-done.11.x2.c2, ...), custom_call_target="tpu_custom_call" | custom-call | flops 2147483648 | bytes 10485760 | tf_op jit(solution)/shard_map/forward/pallas_call | solution.py:127
  60.5 1.4 backward_early.1
  62.0 4.5 %collective-permute-done.12.c1 = bf16[512,512]{1,0:T(8,128)(2,1)S(1)} collective-permute-done((bf16[512,512]{1,0:T(8,128)(2,1)S(1)}, bf16[512,512]{1,0:T(8,128)(2,1)S(1)}, u32[]{:S(2)}, u32[]{:S(2)}) %collective-permute-start.12) | collective-permute-done | bytes 524320 | tf_op jit(solution)/shard_map/ppermute | solution.py:393
  66.5 1.5 %backward_down.1 = (bf16[16,64,512]{2,1,0:T(8,128)(2,1)S(1)}, bf16[16,64,512]{2,1,0:T(8,128)(2,1)S(1)}, f32[512,512]{1,0:T(8,128)S(1)}) custom-call(bf16[512,512]{1,0:T(8,128)(2,1)S(1)} %collective-permute-done.12.c1, bf16[512,512]{1,0:T(8,128)(2,1)S(1)} %collective-permute-done.13.c3, f32[1,512]{1,0:T(1,128)S(1)} %copy-done.6, ...), custom_call_target="tpu_custom_call" | custom-call | flops 1073741824 | bytes 10485760 | tf_op jit(solution)/shard_map/backward_down/pallas_call | solution.py:186
  68.9 2.5 %backward_in.1 = (bf16[16,128,512]{2,1,0:T(8,128)(2,1)S(1)}, bf16[16,128,512]{2,1,0:T(8,128)(2,1)S(1)}, bf16[512,1024]{1,0:T(8,128)(2,1)S(1)}) custom-call(f32[512,512]{1,0:T(8,128)S(1)} %get-tuple-element.137.hg, f32[512,512]{1,0:T(8,128)S(1)} %get-tuple-element.138.factor, f32[512,512]{1,0:T(8,128)S(1)} %get-tuple-element.139.act_ref, ...), custom_call_target="tpu_custom_call" | custom-call | flops 2147483648 | bytes 10485760 | tf_op jit(solution)/shard_map/backward_in/pallas_call | solution.py:214
  71.6 2.4 %slot_gradients.1 = (bf16[512,512]{1,0:T(8,128)(2,1)S(1)}, bf16[512,512]{1,0:T(8,128)(2,1)S(1)}, bf16[512,512]{1,0:T(8,128)(2,1)S(1)}, bf16[512,512]{1,0:T(8,128)(2,1)S(1)}) custom-call(bf16[512,1024]{1,0:T(8,128)(2,1)S(1)} %get-tuple-element.147.both_ref, bf16[32,96,1024]{2,1,0:T(8,128)(2,1)S(1)} %whole_weights.1.w), custom_call_target="tpu_custom_call" | custom-call | flops 2147483648 | bytes 9437184 | tf_op jit(solution)/shard_map/slot_gradients/pallas_call | solution.py:224
  73.9 1.8 %collective-permute-done.16.b_in = bf16[16,128,512]{2,1,0:T(8,128)(2,1)S(1)} collective-permute-done((bf16[16,128,512]{2,1,0:T(8,128)(2,1)S(1)}, bf16[16,128,512]{2,1,0:T(8,128)(2,1)S(1)}, u32[]{:S(2)}, u32[]{:S(2)}) %collective-permute-start.16) | collective-permute-done | bytes 2097184 | tf_op jit(solution)/shard_map/ppermute | solution.py:393
  76.7 1.1 collective-permute-done.17.t_ref
  77.8 1.3 pair_merge.1
  79.1 2.8 %collective-permute-start.18 = (bf16[4,192,512]{2,1,0:T(8,128)(2,1)S(1)}, bf16[4,192,512]{2,1,0:T(8,128)(2,1)S(1)}, u32[]{:S(2)}, u32[]{:S(2)}) collective-permute-start(bf16[4,192,512]{2,1,0:T(8,128)(2,1)S(1)} %get-tuple-element.154), channel_id=1, source_target_pairs={{0,4},{1,17},{2,6},{3,19},{4,0},{5,21},{6,2},{7,23},{8,12},{9,25},... | collective-permute-start | bytes 2359304 | tf_op jit(solution)/shard_map/ppermute | solution.py:393
  82.2 2.3 %collective-permute-start.20 = (bf16[4,192,512]{2,1,0:T(8,128)(2,1)S(1)}, bf16[4,192,512]{2,1,0:T(8,128)(2,1)S(1)}, u32[]{:S(2)}, u32[]{:S(2)}) collective-permute-start(bf16[4,192,512]{2,1,0:T(8,128)(2,1)S(1)} %get-tuple-element.156), channel_id=1, source_target_pairs={{0,6},{1,25},{2,0},{3,27},{4,2},{5,29},{6,4},{7,31},{8,14},{9,1},{... | collective-permute-start | bytes 2359304 | tf_op jit(solution)/shard_map/ppermute | solution.py:393
  84.6 2.7 %collective-permute-start.21 = (bf16[512,512]{1,0:T(8,128)(2,1)S(1)}, bf16[512,512]{1,0:T(8,128)(2,1)S(1)}, u32[]{:S(2)}, u32[]{:S(2)}) collective-permute-start(bf16[512,512]{1,0:T(8,128)(2,1)S(1)} %get-tuple-element.158), channel_id=1, source_target_pairs={{0,96},{32,0},{64,32},{96,64},{1,97},{33,1},{65,33},{97,65},{2,98}... | collective-permute-start | bytes 1572872 | tf_op jit(solution)/shard_map/ppermute | solution.py:393
  87.2 9.3 %collective-permute-done.21.refs_5_ = bf16[512,512]{1,0:T(8,128)(2,1)S(1)} collective-permute-done((bf16[512,512]{1,0:T(8,128)(2,1)S(1)}, bf16[512,512]{1,0:T(8,128)(2,1)S(1)}, u32[]{:S(2)}, u32[]{:S(2)}) %collective-permute-start.21) | collective-permute-done | bytes 524320 | tf_op jit(solution)/shard_map/ppermute | solution.py:393
  96.5 3.1 %collective-permute-done.22.refs_7_ = bf16[512,512]{1,0:T(8,128)(2,1)S(1)} collective-permute-done((bf16[512,512]{1,0:T(8,128)(2,1)S(1)}, bf16[512,512]{1,0:T(8,128)(2,1)S(1)}, u32[]{:S(2)}, u32[]{:S(2)}) %collective-permute-start.22) | collective-permute-done | bytes 524320 | tf_op jit(solution)/shard_map/ppermute | solution.py:393
  100.6 4.3 %collective-permute-start.23 = (bf16[4,192,512]{2,1,0:T(8,128)(2,1)S(1)}, bf16[4,192,512]{2,1,0:T(8,128)(2,1)S(1)}, u32[]{:S(2)}, u32[]{:S(2)}) collective-permute-start(bf16[4,192,512]{2,1,0:T(8,128)(2,1)S(1)} %get-tuple-element.169), channel_id=1, source_target_pairs={{0,16},{1,5},{2,18},{3,7},{4,20},{5,1},{6,22},{7,3},{8,24},{9,13},... | collective-permute-start | bytes 2359304 | tf_op jit(solution)/shard_map/ppermute | solution.py:393
  105.8 1.8 %collective-permute-start.25 = (bf16[4,192,512]{2,1,0:T(8,128)(2,1)S(1)}, bf16[4,192,512]{2,1,0:T(8,128)(2,1)S(1)}, u32[]{:S(2)}, u32[]{:S(2)}) collective-permute-start(bf16[4,192,512]{2,1,0:T(8,128)(2,1)S(1)} %get-tuple-element.171), channel_id=1, source_target_pairs={{0,24},{1,7},{2,26},{3,1},{4,28},{5,3},{6,30},{7,5},{8,0},{9,15},{... | collective-permute-start | bytes 2359304 | tf_op jit(solution)/shard_map/ppermute | solution.py:393
  107.5 2.0 %collective-permute-start.26 = (bf16[512,512]{1,0:T(8,128)(2,1)S(1)}, bf16[512,512]{1,0:T(8,128)(2,1)S(1)}, u32[]{:S(2)}, u32[]{:S(2)}) collective-permute-start(bf16[512,512]{1,0:T(8,128)(2,1)S(1)} %get-tuple-element.173), channel_id=1, source_target_pairs={{0,64},{32,96},{64,0},{96,32},{1,65},{33,97},{65,1},{97,33},{2,66}... | collective-permute-start | bytes 1572872 | tf_op jit(solution)/shard_map/ppermute | solution.py:393
  109.5 11.1 %collective-permute-done.26.refs_6_ = bf16[512,512]{1,0:T(8,128)(2,1)S(1)} collective-permute-done((bf16[512,512]{1,0:T(8,128)(2,1)S(1)}, bf16[512,512]{1,0:T(8,128)(2,1)S(1)}, u32[]{:S(2)}, u32[]{:S(2)}) %collective-permute-start.26) | collective-permute-done | bytes 524320 | tf_op jit(solution)/shard_map/ppermute | solution.py:393
  120.6 2.4 %collective-permute-done.24.refs_1_.x1 = bf16[4,192,512]{2,1,0:T(8,128)(2,1)S(1)} collective-permute-done((bf16[4,192,512]{2,1,0:T(8,128)(2,1)S(1)}, bf16[4,192,512]{2,1,0:T(8,128)(2,1)S(1)}, u32[]{:S(2)}, u32[]{:S(2)}) %collective-permute-start.24) | collective-permute-done | bytes 786464 | tf_op jit(solution)/shard_map/ppermute | solution.py:393
  123.9 2.3 %gram.1 = f32[3,16,128]{2,1,0:T(8,128)S(1)} custom-call(bf16[4,192,512]{2,1,0:T(8,128)(2,1)S(1)} %get-tuple-element.174.refs_0_.x0, bf16[4,192,512]{2,1,0:T(8,128)(2,1)S(1)} %collective-permute-done.24.refs_1_.x1, bf16[4,192,512]{2,1,0:T(8,128)(2,1)S(1)} %collective-permute-done.23.refs_2_.x2, bf16[4,192,512]{2,1,0:T(8,128)(2,1)S(1)} %collective-permute-done.25.refs_3_.x3), custom_call_target="tpu_custom_call" | custom-call | flops 805306368 | bytes 3145728 | tf_op jit(solution)/shard_map/gram/pallas_call | solution.py:315
  126.2 2.4 %collective-permute-start.29 = (f32[3,16,128]{2,1,0:T(8,128)S(1)}, f32[3,16,128]{2,1,0:T(8,128)S(1)}, u32[]{:S(2)}, u32[]{:S(2)}) collective-permute-start(f32[3,16,128]{2,1,0:T(8,128)S(1)} %gram.1), channel_id=1, source_target_pairs={{0,6},{1,7},{2,0},{3,1},{4,2},{5,3},{6,4},{7,5},{8,14},{9,15},{10,... | collective-permute-start | bytes 73736 | tf_op jit(solution)/shard_map/ppermute | solution.py:393
  128.6 1.2 collective-permute-start.27
  129.8 3.5 %scatter_rows.2.refs_8_ = f32[2048,512]{1,0:T(8,128)} custom-call(s32[1,512]{1,0:T(1,128)S(1)} %copy-done.7, s32[1,512]{1,0:T(1,128)S(1)} %collective-permute-done.refs_0_.refs_1_, s32[1,512]{1,0:T(1,128)S(1)} %collective-permute-done.1.refs_0_.refs_2_, s32[1,512]{1,0:T(1,128)S(1)} %collective-permute-done.2.refs_0_.refs_3_, ...), custom_call_target="tpu_custom_call" | custom-call | flops 2147483648 | bytes 4194304 | tf_op jit(solution)/shard_map/scatter_rows/pallas_call | solution.py:379
  133.4 1.8 %collective-permute-start.32 = (f32[3,16,128]{2,1,0:T(8,128)S(1)}, f32[3,16,128]{2,1,0:T(8,128)S(1)}, u32[]{:S(2)}, u32[]{:S(2)}) collective-permute-start(f32[3,16,128]{2,1,0:T(8,128)S(1)} %add_add_fusion.1), channel_id=1, source_target_pairs={{0,24},{1,25},{2,26},{3,27},{4,28},{5,29},{6,30},{7,31},{8,0},{9,1... | collective-permute-start | bytes 73736 | tf_op jit(solution)/shard_map/ppermute | solution.py:393
  135.2 1.3 collective-permute-start.30
  136.5 3.5 %scatter_rows.3 = f32[2048,512]{1,0:T(8,128)} custom-call(s32[1,512]{1,0:T(1,128)S(1)} %copy-done.7, s32[1,512]{1,0:T(1,128)S(1)} %collective-permute-done.refs_0_.refs_1_, s32[1,512]{1,0:T(1,128)S(1)} %collective-permute-done.1.refs_0_.refs_2_, s32[1,512]{1,0:T(1,128)S(1)} %collective-permute-done.2.refs_0_.refs_3_, ...), custom_call_target="tpu_custom_call", output_to_operand_aliasing={{}: (8, {})} | custom-call | flops 2147483648 | bytes 4194304 | tf_op jit(solution)/shard_map/scatter_rows/pallas_call | solution.py:379
  140.0 3.7 %collective-permute-start.33 = (f32[3,16,128]{2,1,0:T(8,128)S(1)}, f32[3,16,128]{2,1,0:T(8,128)S(1)}, u32[]{:S(2)}, u32[]{:S(2)}) collective-permute-start(f32[3,16,128]{2,1,0:T(8,128)S(1)} %add_add_fusion.g_ref), channel_id=1, source_target_pairs={{0,1},{1,0},{2,3},{3,2},{4,5},{5,4},{6,7},{7,6},{8,9},{9,8},{10,11... | collective-permute-start | bytes 73736 | tf_op jit(solution)/shard_map/ppermute | solution.py:393
  144.5 1.8 %finish.1 = (f32[64,512]{1,0:T(8,128)}, f32[64,512]{1,0:T(8,128)}, f32[16,2048]{1,0:T(8,128)}, f32[64,512]{1,0:T(8,128)}, f32[64,512]{1,0:T(8,128)}, /*index=5*/f32[16,2048]{1,0:T(8,128)}) custom-call(bf16[4,192,512]{2,1,0:T(8,128)(2,1)S(1)} %get-tuple-element.174.refs_0_.x0, bf16[4,192,512]{2,1,0:T(8,128)(2,1)S(1)} %collective-permute-done.24.refs_1_.x1, ...), custom_call_target="tpu_custom_call" | custom-call | flops 4194304 | bytes 6291456 | tf_op jit(solution)/shard_map/finish/pallas_call | solution.py:361
  (64 shorter events, 13.1 us)
Async XLA Ops:
  0.6 5.9 %collective-permute-start.2 = (s32[1,512]{1,0:T(1,128)}, s32[1,512]{1,0:T(1,128)S(1)}, u32[]{:S(2)}, u32[]{:S(2)}) collective-permute-start(s32[1,512]{1,0:T(1,128)} %refs_0_.2), channel_id=1, source_target_pairs={{0,32},{32,64},{64,96},{96,0},{1,33},{33,65},{65,97},{97,1},{2,34}... | collective-permute-start | bytes 6152 | tf_op jit(solution)/shard_map/ppermute | solution.py:393
  2.8 8.2 %collective-permute-start.1 = (s32[1,512]{1,0:T(1,128)}, s32[1,512]{1,0:T(1,128)S(1)}, u32[]{:S(2)}, u32[]{:S(2)}) collective-permute-start(s32[1,512]{1,0:T(1,128)} %refs_0_.2), channel_id=1, source_target_pairs={{0,64},{32,96},{64,0},{96,32},{1,65},{33,97},{65,1},{97,33},{2,66}... | collective-permute-start | bytes 6152 | tf_op jit(solution)/shard_map/ppermute | solution.py:393
  5.4 4.1 %collective-permute-start = (s32[1,512]{1,0:T(1,128)}, s32[1,512]{1,0:T(1,128)S(1)}, u32[]{:S(2)}, u32[]{:S(2)}) collective-permute-start(s32[1,512]{1,0:T(1,128)} %refs_0_.2), channel_id=1, source_target_pairs={{0,96},{32,0},{64,32},{96,64},{1,97},{33,1},{65,33},{97,65},{2,98}... | collective-permute-start | bytes 6152 | tf_op jit(solution)/shard_map/ppermute | solution.py:393
  6.5 1.6 %copy-start.9 = (bf16[2048,512]{1,0:T(8,128)(2,1)S(1)}, bf16[2048,512]{1,0:T(8,128)(2,1)}, u32[]{:S(2)}) copy-start(bf16[2048,512]{1,0:T(8,128)(2,1)} %refs_1_.9) | copy-start | bytes 6291460
  9.5 4.2 %copy-start = (f32[1,64,512]{2,1,0:T(8,128)S(1)}, f32[1,64,512]{2,1,0:T(8,128)}, u32[]{:S(2)}) copy-start(f32[1,64,512]{2,1,0:T(8,128)} %param.14) | copy-start | bytes 393220
  9.5 4.2 %copy-start.1 = (f32[1,64,512]{2,1,0:T(8,128)S(1)}, f32[1,64,512]{2,1,0:T(8,128)}, u32[]{:S(2)}) copy-start(f32[1,64,512]{2,1,0:T(8,128)} %param.15) | copy-start | bytes 393220
  9.5 4.2 %copy-start.2 = (f32[1,16,2048]{2,1,0:T(8,128)S(1)}, f32[1,16,2048]{2,1,0:T(8,128)}, u32[]{:S(2)}) copy-start(f32[1,16,2048]{2,1,0:T(8,128)} %param.16) | copy-start | bytes 393220
  9.6 10.3 %copy-start.8 = (bf16[2048,512]{1,0:T(8,128)(2,1)S(1)}, bf16[2048,512]{1,0:T(8,128)(2,1)}, u32[]{:S(2)}) copy-start(bf16[2048,512]{1,0:T(8,128)(2,1)} %refs_1_.11) | copy-start | bytes 6291460
  11.0 13.2 %collective-permute-start.6 = (bf16[512,512]{1,0:T(8,128)(2,1)S(1)}, bf16[512,512]{1,0:T(8,128)(2,1)S(1)}, u32[]{:S(2)}, u32[]{:S(2)}) collective-permute-start(bf16[512,512]{1,0:T(8,128)(2,1)S(1)} %pick_rows.6), channel_id=1, source_target_pairs={{0,32},{32,64},{64,96},{96,0},{1,33},{33,65},{65,97},{97,1},{2,34}... | collective-permute-start | bytes 1572872 | tf_op jit(solution)/shard_map/ppermute | solution.py:393
  11.5 12.7 %collective-permute-start.7 = (bf16[512,512]{1,0:T(8,128)(2,1)S(1)}, bf16[512,512]{1,0:T(8,128)(2,1)S(1)}, u32[]{:S(2)}, u32[]{:S(2)}) collective-permute-start(bf16[512,512]{1,0:T(8,128)(2,1)S(1)} %pick_rows.7), channel_id=1, source_target_pairs={{0,96},{32,0},{64,32},{96,64},{1,97},{33,1},{65,33},{97,65},{2,98}... | collective-permute-start | bytes 1572872 | tf_op jit(solution)/shard_map/ppermute | solution.py:393
  14.3 8.0 %collective-permute-start.5 = (bf16[96,1024]{1,0:T(8,128)(2,1)S(1)}, bf16[96,1024]{1,0:T(8,128)(2,1)S(1)}, u32[]{:S(2)}, u32[]{:S(2)}) collective-permute-start(bf16[96,1024]{1,0:T(8,128)(2,1)S(1)} %pack.1.refs_0_), channel_id=1, source_target_pairs={{0,4},{1,17},{2,6},{3,19},{4,0},{5,21},{6,2},{7,23},{8,12},{9,25},... | collective-permute-start | bytes 589832 | tf_op jit(solution)/shard_map/ppermute | solution.py:393
  17.1 6.0 %collective-permute-start.4 = (bf16[96,1024]{1,0:T(8,128)(2,1)S(1)}, bf16[96,1024]{1,0:T(8,128)(2,1)S(1)}, u32[]{:S(2)}, u32[]{:S(2)}) collective-permute-start(bf16[96,1024]{1,0:T(8,128)(2,1)S(1)} %pack.1.refs_0_), channel_id=1, source_target_pairs={{0,2},{1,9},{2,4},{3,11},{4,6},{5,13},{6,0},{7,15},{8,10},{9,17},{... | collective-permute-start | bytes 589832 | tf_op jit(solution)/shard_map/ppermute | solution.py:393
  17.5 5.7 %collective-permute-start.3 = (bf16[96,1024]{1,0:T(8,128)(2,1)S(1)}, bf16[96,1024]{1,0:T(8,128)(2,1)S(1)}, u32[]{:S(2)}, u32[]{:S(2)}) collective-permute-start(bf16[96,1024]{1,0:T(8,128)(2,1)S(1)} %pack.1.refs_0_), channel_id=1, source_target_pairs={{0,6},{1,25},{2,0},{3,27},{4,2},{5,29},{6,4},{7,31},{8,14},{9,1},{... | collective-permute-start | bytes 589832 | tf_op jit(solution)/shard_map/ppermute | solution.py:393
  24.2 23.1 %collective-permute-start.11 = (bf16[1024,512]{1,0:T(8,128)(2,1)S(1)}, bf16[1024,512]{1,0:T(8,128)(2,1)S(1)}, u32[]{:S(2)}, u32[]{:S(2)}) collective-permute-start(bf16[1024,512]{1,0:T(8,128)(2,1)S(1)} %pick_rows.8), channel_id=1, source_target_pairs={{0,64},{32,96},{64,0},{96,32},{1,65},{33,97},{65,1},{97,33},{2,66}... | collective-permute-start | bytes 3145736 | tf_op jit(solution)/shard_map/ppermute | solution.py:393
  24.7 13.5 %collective-permute-start.10 = (bf16[4,96,1024]{2,1,0:T(8,128)(2,1)S(1)}, bf16[4,96,1024]{2,1,0:T(8,128)(2,1)S(1)}, u32[]{:S(2)}, u32[]{:S(2)}) collective-permute-start(bf16[4,96,1024]{2,1,0:T(8,128)(2,1)S(1)} %bundle.1.refs_0_), channel_id=1, source_target_pairs={{0,16},{1,5},{2,18},{3,7},{4,20},{5,1},{6,22},{7,3},{8,24},{9,13},... | collective-permute-start | bytes 2359304 | tf_op jit(solution)/shard_map/ppermute | solution.py:393
  28.4 18.1 %collective-permute-start.9 = (bf16[4,96,1024]{2,1,0:T(8,128)(2,1)S(1)}, bf16[4,96,1024]{2,1,0:T(8,128)(2,1)S(1)}, u32[]{:S(2)}, u32[]{:S(2)}) collective-permute-start(bf16[4,96,1024]{2,1,0:T(8,128)(2,1)S(1)} %bundle.1.refs_0_), channel_id=1, source_target_pairs={{0,8},{1,3},{2,10},{3,5},{4,12},{5,7},{6,14},{7,1},{8,16},{9,11},{... | collective-permute-start | bytes 2359304 | tf_op jit(solution)/shard_map/ppermute | solution.py:393
  29.2 18.1 %collective-permute-start.8 = (bf16[4,96,1024]{2,1,0:T(8,128)(2,1)S(1)}, bf16[4,96,1024]{2,1,0:T(8,128)(2,1)S(1)}, u32[]{:S(2)}, u32[]{:S(2)}) collective-permute-start(bf16[4,96,1024]{2,1,0:T(8,128)(2,1)S(1)} %bundle.1.refs_0_), channel_id=1, source_target_pairs={{0,24},{1,7},{2,26},{3,1},{4,28},{5,3},{6,30},{7,5},{8,0},{9,15},{... | collective-permute-start | bytes 2359304 | tf_op jit(solution)/shard_map/ppermute | solution.py:393
  32.5 1.5 %copy-start.7 = (s32[1,512]{1,0:T(1,128)S(1)}, s32[1,512]{1,0:T(1,128)}, u32[]{:S(2)}) copy-start(s32[1,512]{1,0:T(1,128)} %refs_0_.2) | copy-start | bytes 6148
  47.5 9.5 %collective-permute-start.14 = (bf16[16,96,1024]{2,1,0:T(8,128)(2,1)S(1)}, bf16[16,96,1024]{2,1,0:T(8,128)(2,1)S(1)}, u32[]{:S(2)}, u32[]{:S(2)}) collective-permute-start(bf16[16,96,1024]{2,1,0:T(8,128)(2,1)S(1)} %half_of_weights.1.a), channel_id=1, source_target_pairs={{0,1},{1,0},{2,3},{3,2},{4,5},{5,4},{6,7},{7,6},{8,9},{9,8},{10,11... | collective-permute-start | bytes 9437192 | tf_op jit(solution)/shard_map/ppermute | solution.py:393
  51.8 14.7 %collective-permute-start.12 = (bf16[512,512]{1,0:T(8,128)(2,1)S(1)}, bf16[512,512]{1,0:T(8,128)(2,1)S(1)}, u32[]{:S(2)}, u32[]{:S(2)}) collective-permute-start(bf16[512,512]{1,0:T(8,128)(2,1)S(1)} %pick_rows.10), channel_id=1, source_target_pairs={{0,32},{32,64},{64,96},{96,0},{1,33},{33,65},{65,97},{97,1},{2,34}... | collective-permute-start | bytes 1572872 | tf_op jit(solution)/shard_map/ppermute | solution.py:393
  52.9 13.6 %collective-permute-start.13 = (bf16[512,512]{1,0:T(8,128)(2,1)S(1)}, bf16[512,512]{1,0:T(8,128)(2,1)S(1)}, u32[]{:S(2)}, u32[]{:S(2)}) collective-permute-start(bf16[512,512]{1,0:T(8,128)(2,1)S(1)} %pick_rows.11), channel_id=1, source_target_pairs={{0,96},{32,0},{64,32},{96,64},{1,97},{33,1},{65,33},{97,65},{2,98}... | collective-permute-start | bytes 1572872 | tf_op jit(solution)/shard_map/ppermute | solution.py:393
  57.5 3.0 %copy-start.6 = (f32[1,512]{1,0:T(1,128)S(1)}, f32[1,512]{1,0:T(1,128)}, u32[]{:S(2)}) copy-start(f32[1,512]{1,0:T(1,128)} %route_ref.3) | copy-start | bytes 6148
  68.0 3.5 %collective-permute-start.15 = (bf16[16,64,512]{2,1,0:T(8,128)(2,1)S(1)}, bf16[16,64,512]{2,1,0:T(8,128)(2,1)S(1)}, u32[]{:S(2)}, u32[]{:S(2)}) collective-permute-start(bf16[16,64,512]{2,1,0:T(8,128)(2,1)S(1)} %get-tuple-element.143), channel_id=1, source_target_pairs={{0,1},{1,0},{2,3},{3,2},{4,5},{5,4},{6,7},{7,6},{8,9},{9,8},{10,11... | collective-permute-start | bytes 3145736 | tf_op jit(solution)/shard_map/ppermute | solution.py:393
  71.4 4.2 %collective-permute-start.16 = (bf16[16,128,512]{2,1,0:T(8,128)(2,1)S(1)}, bf16[16,128,512]{2,1,0:T(8,128)(2,1)S(1)}, u32[]{:S(2)}, u32[]{:S(2)}) collective-permute-start(bf16[16,128,512]{2,1,0:T(8,128)(2,1)S(1)} %get-tuple-element.145), channel_id=1, source_target_pairs={{0,1},{1,0},{2,3},{3,2},{4,5},{5,4},{6,7},{7,6},{8,9},{9,8},{10,11... | collective-permute-start | bytes 6291464 | tf_op jit(solution)/shard_map/ppermute | solution.py:393
  76.5 1.3 collective-permute-start.17
  79.1 20.6 %collective-permute-start.18 = (bf16[4,192,512]{2,1,0:T(8,128)(2,1)S(1)}, bf16[4,192,512]{2,1,0:T(8,128)(2,1)S(1)}, u32[]{:S(2)}, u32[]{:S(2)}) collective-permute-start(bf16[4,192,512]{2,1,0:T(8,128)(2,1)S(1)} %get-tuple-element.154), channel_id=1, source_target_pairs={{0,4},{1,17},{2,6},{3,19},{4,0},{5,21},{6,2},{7,23},{8,12},{9,25},... | collective-permute-start | bytes 2359304 | tf_op jit(solution)/shard_map/ppermute | solution.py:393
  81.9 18.3 %collective-permute-start.19 = (bf16[4,192,512]{2,1,0:T(8,128)(2,1)S(1)}, bf16[4,192,512]{2,1,0:T(8,128)(2,1)S(1)}, u32[]{:S(2)}, u32[]{:S(2)}) collective-permute-start(bf16[4,192,512]{2,1,0:T(8,128)(2,1)S(1)} %get-tuple-element.155), channel_id=1, source_target_pairs={{0,2},{1,9},{2,4},{3,11},{4,6},{5,13},{6,0},{7,15},{8,10},{9,17},{... | collective-permute-start | bytes 2359304 | tf_op jit(solution)/shard_map/ppermute | solution.py:393
  82.2 18.1 %collective-permute-start.20 = (bf16[4,192,512]{2,1,0:T(8,128)(2,1)S(1)}, bf16[4,192,512]{2,1,0:T(8,128)(2,1)S(1)}, u32[]{:S(2)}, u32[]{:S(2)}) collective-permute-start(bf16[4,192,512]{2,1,0:T(8,128)(2,1)S(1)} %get-tuple-element.156), channel_id=1, source_target_pairs={{0,6},{1,25},{2,0},{3,27},{4,2},{5,29},{6,4},{7,31},{8,14},{9,1},{... | collective-permute-start | bytes 2359304 | tf_op jit(solution)/shard_map/ppermute | solution.py:393
  84.6 12.0 %collective-permute-start.21 = (bf16[512,512]{1,0:T(8,128)(2,1)S(1)}, bf16[512,512]{1,0:T(8,128)(2,1)S(1)}, u32[]{:S(2)}, u32[]{:S(2)}) collective-permute-start(bf16[512,512]{1,0:T(8,128)(2,1)S(1)} %get-tuple-element.158), channel_id=1, source_target_pairs={{0,96},{32,0},{64,32},{96,64},{1,97},{33,1},{65,33},{97,65},{2,98}... | collective-permute-start | bytes 1572872 | tf_op jit(solution)/shard_map/ppermute | solution.py:393
  87.2 12.4 %collective-permute-start.22 = (bf16[512,512]{1,0:T(8,128)(2,1)S(1)}, bf16[512,512]{1,0:T(8,128)(2,1)S(1)}, u32[]{:S(2)}, u32[]{:S(2)}) collective-permute-start(bf16[512,512]{1,0:T(8,128)(2,1)S(1)} %get-tuple-element.159), channel_id=1, source_target_pairs={{0,32},{32,64},{64,96},{96,0},{1,33},{33,65},{65,97},{97,1},{2,34}... | collective-permute-start | bytes 1572872 | tf_op jit(solution)/shard_map/ppermute | solution.py:393
  100.6 20.0 %collective-permute-start.23 = (bf16[4,192,512]{2,1,0:T(8,128)(2,1)S(1)}, bf16[4,192,512]{2,1,0:T(8,128)(2,1)S(1)}, u32[]{:S(2)}, u32[]{:S(2)}) collective-permute-start(bf16[4,192,512]{2,1,0:T(8,128)(2,1)S(1)} %get-tuple-element.169), channel_id=1, source_target_pairs={{0,16},{1,5},{2,18},{3,7},{4,20},{5,1},{6,22},{7,3},{8,24},{9,13},... | collective-permute-start | bytes 2359304 | tf_op jit(solution)/shard_map/ppermute | solution.py:393
  104.8 18.1 %collective-permute-start.24 = (bf16[4,192,512]{2,1,0:T(8,128)(2,1)S(1)}, bf16[4,192,512]{2,1,0:T(8,128)(2,1)S(1)}, u32[]{:S(2)}, u32[]{:S(2)}) collective-permute-start(bf16[4,192,512]{2,1,0:T(8,128)(2,1)S(1)} %get-tuple-element.170), channel_id=1, source_target_pairs={{0,8},{1,3},{2,10},{3,5},{4,12},{5,7},{6,14},{7,1},{8,16},{9,11},{... | collective-permute-start | bytes 2359304 | tf_op jit(solution)/shard_map/ppermute | solution.py:393
  105.8 18.1 %collective-permute-start.25 = (bf16[4,192,512]{2,1,0:T(8,128)(2,1)S(1)}, bf16[4,192,512]{2,1,0:T(8,128)(2,1)S(1)}, u32[]{:S(2)}, u32[]{:S(2)}) collective-permute-start(bf16[4,192,512]{2,1,0:T(8,128)(2,1)S(1)} %get-tuple-element.171), channel_id=1, source_target_pairs={{0,24},{1,7},{2,26},{3,1},{4,28},{5,3},{6,30},{7,5},{8,0},{9,15},{... | collective-permute-start | bytes 2359304 | tf_op jit(solution)/shard_map/ppermute | solution.py:393
  107.5 13.1 %collective-permute-start.26 = (bf16[512,512]{1,0:T(8,128)(2,1)S(1)}, bf16[512,512]{1,0:T(8,128)(2,1)S(1)}, u32[]{:S(2)}, u32[]{:S(2)}) collective-permute-start(bf16[512,512]{1,0:T(8,128)(2,1)S(1)} %get-tuple-element.173), channel_id=1, source_target_pairs={{0,64},{32,96},{64,0},{96,32},{1,65},{33,97},{65,1},{97,33},{2,66}... | collective-permute-start | bytes 1572872 | tf_op jit(solution)/shard_map/ppermute | solution.py:393
  126.2 7.1 %collective-permute-start.29 = (f32[3,16,128]{2,1,0:T(8,128)S(1)}, f32[3,16,128]{2,1,0:T(8,128)S(1)}, u32[]{:S(2)}, u32[]{:S(2)}) collective-permute-start(f32[3,16,128]{2,1,0:T(8,128)S(1)} %gram.1), channel_id=1, source_target_pairs={{0,6},{1,7},{2,0},{3,1},{4,2},{5,3},{6,4},{7,5},{8,14},{9,15},{10,... | collective-permute-start | bytes 73736 | tf_op jit(solution)/shard_map/ppermute | solution.py:393
  128.6 4.7 %collective-permute-start.28 = (f32[3,16,128]{2,1,0:T(8,128)S(1)}, f32[3,16,128]{2,1,0:T(8,128)S(1)}, u32[]{:S(2)}, u32[]{:S(2)}) collective-permute-start(f32[3,16,128]{2,1,0:T(8,128)S(1)} %gram.1), channel_id=1, source_target_pairs={{0,2},{1,3},{2,4},{3,5},{4,6},{5,7},{6,0},{7,1},{8,10},{9,11},{10,... | collective-permute-start | bytes 73736 | tf_op jit(solution)/shard_map/ppermute | solution.py:393
  128.6 4.7 %collective-permute-start.27 = (f32[3,16,128]{2,1,0:T(8,128)S(1)}, f32[3,16,128]{2,1,0:T(8,128)S(1)}, u32[]{:S(2)}, u32[]{:S(2)}) collective-permute-start(f32[3,16,128]{2,1,0:T(8,128)S(1)} %gram.1), channel_id=1, source_target_pairs={{0,4},{1,5},{2,6},{3,7},{4,0},{5,1},{6,2},{7,3},{8,12},{9,13},{10,... | collective-permute-start | bytes 73736 | tf_op jit(solution)/shard_map/ppermute | solution.py:393
  133.3 11.2 %copy-start.3 = (f32[1,64,512]{2,1,0:T(8,128)S(1)}, f32[1,64,512]{2,1,0:T(8,128)}, u32[]{:S(2)}) copy-start(f32[1,64,512]{2,1,0:T(8,128)} %param.17) | copy-start | bytes 393220
  133.3 11.2 %copy-start.4 = (f32[1,64,512]{2,1,0:T(8,128)S(1)}, f32[1,64,512]{2,1,0:T(8,128)}, u32[]{:S(2)}) copy-start(f32[1,64,512]{2,1,0:T(8,128)} %param.18) | copy-start | bytes 393220
  133.3 11.2 %copy-start.5 = (f32[1,16,2048]{2,1,0:T(8,128)S(1)}, f32[1,16,2048]{2,1,0:T(8,128)}, u32[]{:S(2)}) copy-start(f32[1,16,2048]{2,1,0:T(8,128)} %param.19) | copy-start | bytes 393220
  133.4 6.6 %collective-permute-start.32 = (f32[3,16,128]{2,1,0:T(8,128)S(1)}, f32[3,16,128]{2,1,0:T(8,128)S(1)}, u32[]{:S(2)}, u32[]{:S(2)}) collective-permute-start(f32[3,16,128]{2,1,0:T(8,128)S(1)} %add_add_fusion.1), channel_id=1, source_target_pairs={{0,24},{1,25},{2,26},{3,27},{4,28},{5,29},{6,30},{7,31},{8,0},{9,1... | collective-permute-start | bytes 73736 | tf_op jit(solution)/shard_map/ppermute | solution.py:393
  135.2 4.7 %collective-permute-start.31 = (f32[3,16,128]{2,1,0:T(8,128)S(1)}, f32[3,16,128]{2,1,0:T(8,128)S(1)}, u32[]{:S(2)}, u32[]{:S(2)}) collective-permute-start(f32[3,16,128]{2,1,0:T(8,128)S(1)} %add_add_fusion.1), channel_id=1, source_target_pairs={{0,8},{1,9},{2,10},{3,11},{4,12},{5,13},{6,14},{7,15},{8,16},{9,17... | collective-permute-start | bytes 73736 | tf_op jit(solution)/shard_map/ppermute | solution.py:393
  135.2 4.7 %collective-permute-start.30 = (f32[3,16,128]{2,1,0:T(8,128)S(1)}, f32[3,16,128]{2,1,0:T(8,128)S(1)}, u32[]{:S(2)}, u32[]{:S(2)}) collective-permute-start(f32[3,16,128]{2,1,0:T(8,128)S(1)} %add_add_fusion.1), channel_id=1, source_target_pairs={{0,16},{1,17},{2,18},{3,19},{4,20},{5,21},{6,22},{7,23},{8,24},{9,... | collective-permute-start | bytes 73736 | tf_op jit(solution)/shard_map/ppermute | solution.py:393
  140.0 4.6 %collective-permute-start.33 = (f32[3,16,128]{2,1,0:T(8,128)S(1)}, f32[3,16,128]{2,1,0:T(8,128)S(1)}, u32[]{:S(2)}, u32[]{:S(2)}) collective-permute-start(f32[3,16,128]{2,1,0:T(8,128)S(1)} %add_add_fusion.g_ref), channel_id=1, source_target_pairs={{0,1},{1,0},{2,3},{3,2},{4,5},{5,4},{6,7},{7,6},{8,9},{9,8},{10,11... | collective-permute-start | bytes 73736 | tf_op jit(solution)/shard_map/ppermute | solution.py:393

commit v13 on v12

--- a/solution.py
+++ b/solution.py
@@ -303,12 +303,11 @@
         order = jnp.where(order == lax.broadcasted_iota(jnp.int32, (16, 16), 0), 1.0, 0.0)
         exact = dict(precision=lax.Precision.HIGHEST, preferred_element_type=F32)
         for m in range(3):
-            acc = None
-            for b in range(4):
-                at = 64 * m + 16 * b
-                block = jnp.concatenate([r[:, at : at + 16, :].reshape(64, SLICE) for r in x], axis=0)
-                part = lax.dot_general(block, block, NT, preferred_element_type=F32)
-                acc = part if acc is None else acc + part
+            spans = [slice(64 * m + 16 * b, 64 * m + 16 * (b + 1)) for b in range(4)]
+            block = jnp.concatenate(
+                [jnp.concatenate([r[:, rows, :].reshape(64, SLICE) for rows in spans], axis=1) for r in x], axis=0
+            )
+            acc = lax.dot_general(block, block, NT, preferred_element_type=F32)
             acc = jnp.sum((acc * same).reshape(16, 16, 256), axis=1)
             out[m] = jnp.dot(order, jnp.dot(acc, fold, **exact), **exact)
 
@@ -463,8 +462,8 @@
     return [out[1], out[2], out[3]]
 
 
-def tie_far(items, others, last=False):
-    order = (3, 1, 2, 0) if last else (2, 1, 3, 0)
+def tie_in_order(items, others):
+    order = (3, 1, 2, 0)
     tied, others = lax.optimization_barrier(([items[k] for k in order], others))
     return [tied[order.index(k)] for k in range(4)], others
 
@@ -537,14 +536,14 @@
     blocks = spread(packed, 0)
     x[1], x[3] = around_y(x[1], 1), around_y(x[3], 3)
     (x[2],) = pick_rows(ids[2:3], [pool_tokens, pool_cotangent], stacked=True)
-    blocks, (ids, x[1:]) = tie_far([packed, *blocks], (ids, x[1:]), last=True)
+    blocks, (ids, x[1:]) = tie_in_order([packed, *blocks], (ids, x[1:]))
 
     block = bundle(blocks)
     blocks = spread(block, 1)
     x[2] = c[2] = around_y(x[2], 2)
     c[1], c[3] = picked(1, pool_cotangent), picked(3, pool_cotangent)
     x[0], c[0] = pick_rows(ids[:1], [pool_tokens, pool_cotangent])
-    blocks, (x, c) = tie_far([block, *blocks], (x, [c[0], c[1], c[3]]), last=True)
+    blocks, (x, c) = tie_in_order([block, *blocks], (x, [c[0], c[1], c[3]]))
     c = [c[0], c[1], x[2], c[2]]
 
     mine = half_of_weights(blocks)
@@ -564,11 +563,11 @@
     sent = pair_merge(keep, received, mine, other_core(mine))
     parts = [sent[0], *to_others(sent, 0)]
     back = [slots[0], around_y(slots[1], 3), None, around_y(slots[3], 1)]
-    parts, (back[1], back[3]) = tie_far(parts, (back[1], back[3]))
+    parts, (back[1], back[3]) = tie_in_order(parts, (back[1], back[3]))
     sent, slots[2] = tie((turn_over(parts), slots[2]))
     parts = [sent[0], *to_others(sent, 1)]
     back[2] = around_y(slots[2], 2)
-    parts, back[2] = tie_far(parts, back[2])
+    parts, back[2] = tie_in_order(parts, back[2])
     products, pool_grad = sum_dp(gram(parts), ids, back)
     outs = finish(
         parts,

time: 147 us -> 150 us (1.020)
  waiting for transfers between devices: 50.9 us -> 57.4 us
  starting transfers between devices: 56.6 us -> 53.6 us
    ppermute x34, waiting for transfers between devices: 50.9 us -> 57.4 us  [shift(): lax.ppermute(block, axis, [(i, to(i)) for i in range(lax.axis_size(axis))])]
    ppermute x34, starting transfers between devices: 56.6 us -> 53.6 us  [shift(): lax.ppermute(block, axis, [(i, to(i)) for i in range(lax.axis_size(axis))])]
  transfers between devices with their start and end apart: 34 -> 34, of which waited for: 17 -> 19; matrix products, arithmetic and copies ran while one was open for 0% -> 0% of each run, Pallas kernels for 19% -> 19%
where the time goes in v13:
time: 150 us
  waiting for transfers between devices  57.4 us (38%)
  starting transfers between devices  53.6 us (36%)
  Pallas kernels  36.2 us (24%)
  local copies, waits for them, and re-layouts  1.65 us (1%)
    ppermute x34, waiting for transfers between devices, shift(): lax.ppermute(block, axis, [(i, to(i)) for i in range(lax.axis_size(axis))])  57.4 us
    ppermute x34, starting transfers between devices, shift(): lax.ppermute(block, axis, [(i, to(i)) for i in range(lax.axis_size(axis))])  53.6 us
    pallas_call x6, Pallas kernels, pick_rows(): call(body, 'pick_rows', n_ids + n_pool, shapes, 2 * TOK_DEV * POOL * SLIC...  10.7 us
    pallas_call x2, Pallas kernels, scatter_rows(): pl.pallas_call(body, name='scatter_rows', grid=(steps,), out_shape=struct...  6.94 us
    pallas_call x1, Pallas kernels, forward(): call(body, 'forward', 5, shapes, 2 * TOK_DEV * D * 2 * H, 10 * MIB, [pltp...  3.02 us
  transfers between devices with their start and end apart: 34, of which 19 were waited for; matrix products, arithmetic and copies ran while one was open for 0% of the time, Pallas kernels for 19%

profile of v13, /device:TPU:1, one launch (start us, length us, event | category | flops | bytes accessed | tf_op | source)
XLA Modules:
  0.0 149.8 jit_solution(9249927573913464793)
XLA Ops:
  0.6 2.2 %collective-permute-start.2 = (s32[1,512]{1,0:T(1,128)}, s32[1,512]{1,0:T(1,128)S(1)}, u32[]{:S(2)}, u32[]{:S(2)}) collective-permute-start(s32[1,512]{1,0:T(1,128)} %refs_0_.2), channel_id=1, source_target_pairs={{0,32},{32,64},{64,96},{96,0},{1,33},{33,65},{65,97},{97,1},{2,34}... | collective-permute-start | bytes 6152 | tf_op jit(solution)/shard_map/ppermute | solution.py:392
  2.8 2.6 %collective-permute-start.1 = (s32[1,512]{1,0:T(1,128)}, s32[1,512]{1,0:T(1,128)S(1)}, u32[]{:S(2)}, u32[]{:S(2)}) collective-permute-start(s32[1,512]{1,0:T(1,128)} %refs_0_.2), channel_id=1, source_target_pairs={{0,64},{32,96},{64,0},{96,32},{1,65},{33,97},{65,1},{97,33},{2,66}... | collective-permute-start | bytes 6152 | tf_op jit(solution)/shard_map/ppermute | solution.py:392
  5.4 1.1 collective-permute-start
  6.5 1.6 %copy-done.9 = bf16[2048,512]{1,0:T(8,128)(2,1)S(1)} copy-done((bf16[2048,512]{1,0:T(8,128)(2,1)S(1)}, bf16[2048,512]{1,0:T(8,128)(2,1)}, u32[]{:S(2)}) %copy-start.9) | copy-done | bytes 2097176
  8.1 1.4 pick_rows.7
  9.6 1.4 pick_rows.6
  11.5 2.3 %collective-permute-start.7 = (bf16[512,512]{1,0:T(8,128)(2,1)S(1)}, bf16[512,512]{1,0:T(8,128)(2,1)S(1)}, u32[]{:S(2)}, u32[]{:S(2)}) collective-permute-start(bf16[512,512]{1,0:T(8,128)(2,1)S(1)} %pick_rows.7), channel_id=1, source_target_pairs={{0,96},{32,0},{64,32},{96,64},{1,97},{33,1},{65,33},{97,65},{2,98}... | collective-permute-start | bytes 1572872 | tf_op jit(solution)/shard_map/ppermute | solution.py:392
  14.3 2.8 %collective-permute-start.5 = (bf16[96,1024]{1,0:T(8,128)(2,1)S(1)}, bf16[96,1024]{1,0:T(8,128)(2,1)S(1)}, u32[]{:S(2)}, u32[]{:S(2)}) collective-permute-start(bf16[96,1024]{1,0:T(8,128)(2,1)S(1)} %pack.1.refs_0_), channel_id=1, source_target_pairs={{0,4},{1,17},{2,6},{3,19},{4,0},{5,21},{6,2},{7,23},{8,12},{9,25},... | collective-permute-start | bytes 589832 | tf_op jit(solution)/shard_map/ppermute | solution.py:392
  17.5 2.3 %collective-permute-start.3 = (bf16[96,1024]{1,0:T(8,128)(2,1)S(1)}, bf16[96,1024]{1,0:T(8,128)(2,1)S(1)}, u32[]{:S(2)}, u32[]{:S(2)}) collective-permute-start(bf16[96,1024]{1,0:T(8,128)(2,1)S(1)} %pack.1.refs_0_), channel_id=1, source_target_pairs={{0,6},{1,25},{2,0},{3,27},{4,2},{5,29},{6,4},{7,31},{8,14},{9,1},{... | collective-permute-start | bytes 589832 | tf_op jit(solution)/shard_map/ppermute | solution.py:392
  19.8 2.5 %pick_rows.8 = bf16[1024,512]{1,0:T(8,128)(2,1)S(1)} custom-call(s32[1,512]{1,0:T(1,128)S(1)} %collective-permute-done.1.refs_0_.refs_2_, bf16[2048,512]{1,0:T(8,128)(2,1)S(1)} %copy-done.9, bf16[2048,512]{1,0:T(8,128)(2,1)S(1)} %copy-done.8), custom_call_target="tpu_custom_call" | custom-call | flops 2147483648 | bytes 3145728 | tf_op jit(solution)/shard_map/pick_rows/pallas_call | solution.py:73
  24.7 3.7 %collective-permute-start.10 = (bf16[4,96,1024]{2,1,0:T(8,128)(2,1)S(1)}, bf16[4,96,1024]{2,1,0:T(8,128)(2,1)S(1)}, u32[]{:S(2)}, u32[]{:S(2)}) collective-permute-start(bf16[4,96,1024]{2,1,0:T(8,128)(2,1)S(1)} %bundle.1.refs_0_), channel_id=1, source_target_pairs={{0,16},{1,5},{2,18},{3,7},{4,20},{5,1},{6,22},{7,3},{8,24},{9,13},... | collective-permute-start | bytes 2359304 | tf_op jit(solution)/shard_map/ppermute | solution.py:392
  29.2 1.9 %collective-permute-start.8 = (bf16[4,96,1024]{2,1,0:T(8,128)(2,1)S(1)}, bf16[4,96,1024]{2,1,0:T(8,128)(2,1)S(1)}, u32[]{:S(2)}, u32[]{:S(2)}) collective-permute-start(bf16[4,96,1024]{2,1,0:T(8,128)(2,1)S(1)} %bundle.1.refs_0_), channel_id=1, source_target_pairs={{0,24},{1,7},{2,26},{3,1},{4,28},{5,3},{6,30},{7,5},{8,0},{9,15},{... | collective-permute-start | bytes 2359304 | tf_op jit(solution)/shard_map/ppermute | solution.py:392
  31.1 1.4 pick_rows.10
  32.6 1.4 pick_rows.11
  34.0 2.5 %pick_rows.9 = (bf16[512,512]{1,0:T(8,128)(2,1)S(1)}, bf16[512,512]{1,0:T(8,128)(2,1)S(1)}) custom-call(s32[1,512]{1,0:T(1,128)S(1)} %copy-done.7, bf16[2048,512]{1,0:T(8,128)(2,1)S(1)} %copy-done.9, bf16[2048,512]{1,0:T(8,128)(2,1)S(1)} %copy-done.8), custom_call_target="tpu_custom_call" | custom-call | flops 2147483648 | bytes 3145728 | tf_op jit(solution)/shard_map/pick_rows/pallas_call | solution.py:73
  36.5 1.6 %collective-permute-done.10.refs_2_ = bf16[4,96,1024]{2,1,0:T(8,128)(2,1)S(1)} collective-permute-done((bf16[4,96,1024]{2,1,0:T(8,128)(2,1)S(1)}, bf16[4,96,1024]{2,1,0:T(8,128)(2,1)S(1)}, u32[]{:S(2)}, u32[]{:S(2)}) %collective-permute-start.10) | collective-permute-done | bytes 786464 | tf_op jit(solution)/shard_map/ppermute | solution.py:392
  38.1 8.4 %collective-permute-done.9.refs_1_ = bf16[4,96,1024]{2,1,0:T(8,128)(2,1)S(1)} collective-permute-done((bf16[4,96,1024]{2,1,0:T(8,128)(2,1)S(1)}, bf16[4,96,1024]{2,1,0:T(8,128)(2,1)S(1)}, u32[]{:S(2)}, u32[]{:S(2)}) %collective-permute-start.9) | collective-permute-done | bytes 786464 | tf_op jit(solution)/shard_map/ppermute | solution.py:392
  47.5 4.2 %collective-permute-start.14 = (bf16[16,96,1024]{2,1,0:T(8,128)(2,1)S(1)}, bf16[16,96,1024]{2,1,0:T(8,128)(2,1)S(1)}, u32[]{:S(2)}, u32[]{:S(2)}) collective-permute-start(bf16[16,96,1024]{2,1,0:T(8,128)(2,1)S(1)} %half_of_weights.1.a), channel_id=1, source_target_pairs={{0,1},{1,0},{2,3},{3,2},{4,5},{5,4},{6,7},{7,6},{8,9},{9,8},{10,11... | collective-permute-start | bytes 9437192 | tf_op jit(solution)/shard_map/ppermute | solution.py:392
  51.8 1.1 collective-permute-start.12
  52.9 1.5 %collective-permute-start.13 = (bf16[512,512]{1,0:T(8,128)(2,1)S(1)}, bf16[512,512]{1,0:T(8,128)(2,1)S(1)}, u32[]{:S(2)}, u32[]{:S(2)}) collective-permute-start(bf16[512,512]{1,0:T(8,128)(2,1)S(1)} %pick_rows.11), channel_id=1, source_target_pairs={{0,96},{32,0},{64,32},{96,64},{1,97},{33,1},{65,33},{97,65},{2,98}... | collective-permute-start | bytes 1572872 | tf_op jit(solution)/shard_map/ppermute | solution.py:392
  54.4 2.6 %collective-permute-done.14.b = bf16[16,96,1024]{2,1,0:T(8,128)(2,1)S(1)} collective-permute-done((bf16[16,96,1024]{2,1,0:T(8,128)(2,1)S(1)}, bf16[16,96,1024]{2,1,0:T(8,128)(2,1)S(1)}, u32[]{:S(2)}, u32[]{:S(2)}) %collective-permute-start.14) | collective-permute-done | bytes 3145760 | tf_op jit(solution)/shard_map/ppermute | solution.py:392
  57.5 3.0 %forward.1 = (bf16[512,512]{1,0:T(8,128)(2,1)S(1)}, f32[512,512]{1,0:T(8,128)S(1)}, f32[512,512]{1,0:T(8,128)S(1)}, bf16[4,512,512]{2,1,0:T(8,128)(2,1)S(1)}) custom-call(bf16[512,512]{1,0:T(8,128)(2,1)S(1)} %get-tuple-element.125.x0, bf16[512,512]{1,0:T(8,128)(2,1)S(1)} %collective-permute-done.6.x1, bf16[1024,512]{1,0:T(8,128)(2,1)S(1)} %collective-permute-done.11.x2.c2, ...), custom_call_target="tpu_custom_call" | custom-call | flops 2147483648 | bytes 10485760 | tf_op jit(solution)/shard_map/forward/pallas_call | solution.py:127
  60.5 1.4 backward_early.1
  62.0 4.5 %collective-permute-done.12.c1 = bf16[512,512]{1,0:T(8,128)(2,1)S(1)} collective-permute-done((bf16[512,512]{1,0:T(8,128)(2,1)S(1)}, bf16[512,512]{1,0:T(8,128)(2,1)S(1)}, u32[]{:S(2)}, u32[]{:S(2)}) %collective-permute-start.12) | collective-permute-done | bytes 524320 | tf_op jit(solution)/shard_map/ppermute | solution.py:392
  66.5 1.5 backward_down.1
  68.9 2.5 %backward_in.1 = (bf16[16,128,512]{2,1,0:T(8,128)(2,1)S(1)}, bf16[16,128,512]{2,1,0:T(8,128)(2,1)S(1)}, bf16[512,1024]{1,0:T(8,128)(2,1)S(1)}) custom-call(f32[512,512]{1,0:T(8,128)S(1)} %get-tuple-element.137.hg, f32[512,512]{1,0:T(8,128)S(1)} %get-tuple-element.138.factor, f32[512,512]{1,0:T(8,128)S(1)} %get-tuple-element.139.act_ref, ...), custom_call_target="tpu_custom_call" | custom-call | flops 2147483648 | bytes 10485760 | tf_op jit(solution)/shard_map/backward_in/pallas_call | solution.py:214
  71.6 2.4 %slot_gradients.1 = (bf16[512,512]{1,0:T(8,128)(2,1)S(1)}, bf16[512,512]{1,0:T(8,128)(2,1)S(1)}, bf16[512,512]{1,0:T(8,128)(2,1)S(1)}, bf16[512,512]{1,0:T(8,128)(2,1)S(1)}) custom-call(bf16[512,1024]{1,0:T(8,128)(2,1)S(1)} %get-tuple-element.147.both_ref, bf16[32,96,1024]{2,1,0:T(8,128)(2,1)S(1)} %whole_weights.1.w), custom_call_target="tpu_custom_call" | custom-call | flops 2147483648 | bytes 9437184 | tf_op jit(solution)/shard_map/slot_gradients/pallas_call | solution.py:224
  73.9 1.8 %collective-permute-done.16.b_in = bf16[16,128,512]{2,1,0:T(8,128)(2,1)S(1)} collective-permute-done((bf16[16,128,512]{2,1,0:T(8,128)(2,1)S(1)}, bf16[16,128,512]{2,1,0:T(8,128)(2,1)S(1)}, u32[]{:S(2)}, u32[]{:S(2)}) %collective-permute-start.16) | collective-permute-done | bytes 2097184 | tf_op jit(solution)/shard_map/ppermute | solution.py:392
  76.7 1.1 collective-permute-done.17.t_ref
  77.8 1.3 pair_merge.1
  79.1 2.6 %collective-permute-start.18 = (bf16[4,192,512]{2,1,0:T(8,128)(2,1)S(1)}, bf16[4,192,512]{2,1,0:T(8,128)(2,1)S(1)}, u32[]{:S(2)}, u32[]{:S(2)}) collective-permute-start(bf16[4,192,512]{2,1,0:T(8,128)(2,1)S(1)} %get-tuple-element.154), channel_id=1, source_target_pairs={{0,6},{1,25},{2,0},{3,27},{4,2},{5,29},{6,4},{7,31},{8,14},{9,1},{... | collective-permute-start | bytes 2359304 | tf_op jit(solution)/shard_map/ppermute | solution.py:392
  81.6 1.7 %collective-permute-start.20 = (bf16[4,192,512]{2,1,0:T(8,128)(2,1)S(1)}, bf16[4,192,512]{2,1,0:T(8,128)(2,1)S(1)}, u32[]{:S(2)}, u32[]{:S(2)}) collective-permute-start(bf16[4,192,512]{2,1,0:T(8,128)(2,1)S(1)} %get-tuple-element.156), channel_id=1, source_target_pairs={{0,4},{1,17},{2,6},{3,19},{4,0},{5,21},{6,2},{7,23},{8,12},{9,25},... | collective-permute-start | bytes 2359304 | tf_op jit(solution)/shard_map/ppermute | solution.py:392
  83.3 2.7 %collective-permute-start.21 = (bf16[512,512]{1,0:T(8,128)(2,1)S(1)}, bf16[512,512]{1,0:T(8,128)(2,1)S(1)}, u32[]{:S(2)}, u32[]{:S(2)}) collective-permute-start(bf16[512,512]{1,0:T(8,128)(2,1)S(1)} %get-tuple-element.158), channel_id=1, source_target_pairs={{0,96},{32,0},{64,32},{96,64},{1,97},{33,1},{65,33},{97,65},{2,98}... | collective-permute-start | bytes 1572872 | tf_op jit(solution)/shard_map/ppermute | solution.py:392
  86.0 9.3 %collective-permute-done.21.refs_5_ = bf16[512,512]{1,0:T(8,128)(2,1)S(1)} collective-permute-done((bf16[512,512]{1,0:T(8,128)(2,1)S(1)}, bf16[512,512]{1,0:T(8,128)(2,1)S(1)}, u32[]{:S(2)}, u32[]{:S(2)}) %collective-permute-start.21) | collective-permute-done | bytes 524320 | tf_op jit(solution)/shard_map/ppermute | solution.py:392
  95.3 3.1 %collective-permute-done.22.refs_7_ = bf16[512,512]{1,0:T(8,128)(2,1)S(1)} collective-permute-done((bf16[512,512]{1,0:T(8,128)(2,1)S(1)}, bf16[512,512]{1,0:T(8,128)(2,1)S(1)}, u32[]{:S(2)}, u32[]{:S(2)}) %collective-permute-start.22) | collective-permute-done | bytes 524320 | tf_op jit(solution)/shard_map/ppermute | solution.py:392
  99.0 3.4 %collective-permute-done.19.refs_1_ = bf16[4,192,512]{2,1,0:T(8,128)(2,1)S(1)} collective-permute-done((bf16[4,192,512]{2,1,0:T(8,128)(2,1)S(1)}, bf16[4,192,512]{2,1,0:T(8,128)(2,1)S(1)}, u32[]{:S(2)}, u32[]{:S(2)}) %collective-permute-start.19) | collective-permute-done | bytes 786464 | tf_op jit(solution)/shard_map/ppermute | solution.py:392
  102.6 3.7 %collective-permute-start.23 = (bf16[4,192,512]{2,1,0:T(8,128)(2,1)S(1)}, bf16[4,192,512]{2,1,0:T(8,128)(2,1)S(1)}, u32[]{:S(2)}, u32[]{:S(2)}) collective-permute-start(bf16[4,192,512]{2,1,0:T(8,128)(2,1)S(1)} %get-tuple-element.169), channel_id=1, source_target_pairs={{0,24},{1,7},{2,26},{3,1},{4,28},{5,3},{6,30},{7,5},{8,0},{9,15},{... | collective-permute-start | bytes 2359304 | tf_op jit(solution)/shard_map/ppermute | solution.py:392
  106.3 1.3 collective-permute-start.25
  107.7 2.4 %collective-permute-start.26 = (bf16[512,512]{1,0:T(8,128)(2,1)S(1)}, bf16[512,512]{1,0:T(8,128)(2,1)S(1)}, u32[]{:S(2)}, u32[]{:S(2)}) collective-permute-start(bf16[512,512]{1,0:T(8,128)(2,1)S(1)} %get-tuple-element.173), channel_id=1, source_target_pairs={{0,64},{32,96},{64,0},{96,32},{1,65},{33,97},{65,1},{97,33},{2,66}... | collective-permute-start | bytes 1572872 | tf_op jit(solution)/shard_map/ppermute | solution.py:392
  110.0 9.7 %collective-permute-done.26.refs_6_ = bf16[512,512]{1,0:T(8,128)(2,1)S(1)} collective-permute-done((bf16[512,512]{1,0:T(8,128)(2,1)S(1)}, bf16[512,512]{1,0:T(8,128)(2,1)S(1)}, u32[]{:S(2)}, u32[]{:S(2)}) %collective-permute-start.26) | collective-permute-done | bytes 524320 | tf_op jit(solution)/shard_map/ppermute | solution.py:392
  119.7 4.0 %collective-permute-done.23.refs_3_.x3 = bf16[4,192,512]{2,1,0:T(8,128)(2,1)S(1)} collective-permute-done((bf16[4,192,512]{2,1,0:T(8,128)(2,1)S(1)}, bf16[4,192,512]{2,1,0:T(8,128)(2,1)S(1)}, u32[]{:S(2)}, u32[]{:S(2)}) %collective-permute-start.23) | collective-permute-done | bytes 786464 | tf_op jit(solution)/shard_map/ppermute | solution.py:392
  123.7 3.4 %collective-permute-done.24.refs_1_.x1 = bf16[4,192,512]{2,1,0:T(8,128)(2,1)S(1)} collective-permute-done((bf16[4,192,512]{2,1,0:T(8,128)(2,1)S(1)}, bf16[4,192,512]{2,1,0:T(8,128)(2,1)S(1)}, u32[]{:S(2)}, u32[]{:S(2)}) %collective-permute-start.24) | collective-permute-done | bytes 786464 | tf_op jit(solution)/shard_map/ppermute | solution.py:392
  127.1 2.3 %gram.1 = f32[3,16,128]{2,1,0:T(8,128)S(1)} custom-call(bf16[4,192,512]{2,1,0:T(8,128)(2,1)S(1)} %get-tuple-element.174.refs_0_.x0, bf16[4,192,512]{2,1,0:T(8,128)(2,1)S(1)} %collective-permute-done.24.refs_1_.x1, bf16[4,192,512]{2,1,0:T(8,128)(2,1)S(1)} %collective-permute-done.25.refs_2_.x2, bf16[4,192,512]{2,1,0:T(8,128)(2,1)S(1)} %collective-permute-done.23.refs_3_.x3), custom_call_target="tpu_custom_call" | custom-call | flops 805306368 | bytes 3145728 | tf_op jit(solution)/shard_map/gram/pallas_call | solution.py:314
  129.5 1.5 collective-permute-start.28
  131.2 3.5 %scatter_rows.2.refs_8_ = f32[2048,512]{1,0:T(8,128)} custom-call(s32[1,512]{1,0:T(1,128)S(1)} %copy-done.7, s32[1,512]{1,0:T(1,128)S(1)} %collective-permute-done.refs_0_.refs_1_, s32[1,512]{1,0:T(1,128)S(1)} %collective-permute-done.1.refs_0_.refs_2_, s32[1,512]{1,0:T(1,128)S(1)} %collective-permute-done.2.refs_0_.refs_3_, ...), custom_call_target="tpu_custom_call" | custom-call | flops 2147483648 | bytes 4194304 | tf_op jit(solution)/shard_map/scatter_rows/pallas_call | solution.py:378
  137.3 3.5 %scatter_rows.3 = f32[2048,512]{1,0:T(8,128)} custom-call(s32[1,512]{1,0:T(1,128)S(1)} %copy-done.7, s32[1,512]{1,0:T(1,128)S(1)} %collective-permute-done.refs_0_.refs_1_, s32[1,512]{1,0:T(1,128)S(1)} %collective-permute-done.1.refs_0_.refs_2_, s32[1,512]{1,0:T(1,128)S(1)} %collective-permute-done.2.refs_0_.refs_3_, ...), custom_call_target="tpu_custom_call", output_to_operand_aliasing={{}: (8, {})} | custom-call | flops 2147483648 | bytes 4194304 | tf_op jit(solution)/shard_map/scatter_rows/pallas_call | solution.py:378
  140.9 6.2 %collective-permute-start.33 = (f32[3,16,128]{2,1,0:T(8,128)S(1)}, f32[3,16,128]{2,1,0:T(8,128)S(1)}, u32[]{:S(2)}, u32[]{:S(2)}) collective-permute-start(f32[3,16,128]{2,1,0:T(8,128)S(1)} %add_add_fusion.g_ref), channel_id=1, source_target_pairs={{0,1},{1,0},{2,3},{3,2},{4,5},{5,4},{6,7},{7,6},{8,9},{9,8},{10,11... | collective-permute-start | bytes 73736 | tf_op jit(solution)/shard_map/ppermute | solution.py:392
  148.0 1.8 %finish.1 = (f32[64,512]{1,0:T(8,128)}, f32[64,512]{1,0:T(8,128)}, f32[16,2048]{1,0:T(8,128)}, f32[64,512]{1,0:T(8,128)}, f32[64,512]{1,0:T(8,128)}, /*index=5*/f32[16,2048]{1,0:T(8,128)}) custom-call(bf16[4,192,512]{2,1,0:T(8,128)(2,1)S(1)} %get-tuple-element.174.refs_0_.x0, bf16[4,192,512]{2,1,0:T(8,128)(2,1)S(1)} %collective-permute-done.24.refs_1_.x1, ...), custom_call_target="tpu_custom_call" | custom-call | flops 4194304 | bytes 6291456 | tf_op jit(solution)/shard_map/finish/pallas_call | solution.py:360
  (64 shorter events, 12.6 us)
Async XLA Ops:
  0.6 5.9 %collective-permute-start.2 = (s32[1,512]{1,0:T(1,128)}, s32[1,512]{1,0:T(1,128)S(1)}, u32[]{:S(2)}, u32[]{:S(2)}) collective-permute-start(s32[1,512]{1,0:T(1,128)} %refs_0_.2), channel_id=1, source_target_pairs={{0,32},{32,64},{64,96},{96,0},{1,33},{33,65},{65,97},{97,1},{2,34}... | collective-permute-start | bytes 6152 | tf_op jit(solution)/shard_map/ppermute | solution.py:392
  2.8 8.2 %collective-permute-start.1 = (s32[1,512]{1,0:T(1,128)}, s32[1,512]{1,0:T(1,128)S(1)}, u32[]{:S(2)}, u32[]{:S(2)}) collective-permute-start(s32[1,512]{1,0:T(1,128)} %refs_0_.2), channel_id=1, source_target_pairs={{0,64},{32,96},{64,0},{96,32},{1,65},{33,97},{65,1},{97,33},{2,66}... | collective-permute-start | bytes 6152 | tf_op jit(solution)/shard_map/ppermute | solution.py:392
  5.4 4.1 %collective-permute-start = (s32[1,512]{1,0:T(1,128)}, s32[1,512]{1,0:T(1,128)S(1)}, u32[]{:S(2)}, u32[]{:S(2)}) collective-permute-start(s32[1,512]{1,0:T(1,128)} %refs_0_.2), channel_id=1, source_target_pairs={{0,96},{32,0},{64,32},{96,64},{1,97},{33,1},{65,33},{97,65},{2,98}... | collective-permute-start | bytes 6152 | tf_op jit(solution)/shard_map/ppermute | solution.py:392
  6.5 1.6 %copy-start.9 = (bf16[2048,512]{1,0:T(8,128)(2,1)S(1)}, bf16[2048,512]{1,0:T(8,128)(2,1)}, u32[]{:S(2)}) copy-start(bf16[2048,512]{1,0:T(8,128)(2,1)} %refs_1_.9) | copy-start | bytes 6291460
  9.5 4.2 %copy-start = (f32[1,64,512]{2,1,0:T(8,128)S(1)}, f32[1,64,512]{2,1,0:T(8,128)}, u32[]{:S(2)}) copy-start(f32[1,64,512]{2,1,0:T(8,128)} %param.14) | copy-start | bytes 393220
  9.5 4.2 %copy-start.1 = (f32[1,64,512]{2,1,0:T(8,128)S(1)}, f32[1,64,512]{2,1,0:T(8,128)}, u32[]{:S(2)}) copy-start(f32[1,64,512]{2,1,0:T(8,128)} %param.15) | copy-start | bytes 393220
  9.5 4.2 %copy-start.2 = (f32[1,16,2048]{2,1,0:T(8,128)S(1)}, f32[1,16,2048]{2,1,0:T(8,128)}, u32[]{:S(2)}) copy-start(f32[1,16,2048]{2,1,0:T(8,128)} %param.16) | copy-start | bytes 393220
  9.6 10.3 %copy-start.8 = (bf16[2048,512]{1,0:T(8,128)(2,1)S(1)}, bf16[2048,512]{1,0:T(8,128)(2,1)}, u32[]{:S(2)}) copy-start(bf16[2048,512]{1,0:T(8,128)(2,1)} %refs_1_.11) | copy-start | bytes 6291460
  11.0 13.2 %collective-permute-start.6 = (bf16[512,512]{1,0:T(8,128)(2,1)S(1)}, bf16[512,512]{1,0:T(8,128)(2,1)S(1)}, u32[]{:S(2)}, u32[]{:S(2)}) collective-permute-start(bf16[512,512]{1,0:T(8,128)(2,1)S(1)} %pick_rows.6), channel_id=1, source_target_pairs={{0,32},{32,64},{64,96},{96,0},{1,33},{33,65},{65,97},{97,1},{2,34}... | collective-permute-start | bytes 1572872 | tf_op jit(solution)/shard_map/ppermute | solution.py:392
  11.5 12.7 %collective-permute-start.7 = (bf16[512,512]{1,0:T(8,128)(2,1)S(1)}, bf16[512,512]{1,0:T(8,128)(2,1)S(1)}, u32[]{:S(2)}, u32[]{:S(2)}) collective-permute-start(bf16[512,512]{1,0:T(8,128)(2,1)S(1)} %pick_rows.7), channel_id=1, source_target_pairs={{0,96},{32,0},{64,32},{96,64},{1,97},{33,1},{65,33},{97,65},{2,98}... | collective-permute-start | bytes 1572872 | tf_op jit(solution)/shard_map/ppermute | solution.py:392
  14.3 8.0 %collective-permute-start.5 = (bf16[96,1024]{1,0:T(8,128)(2,1)S(1)}, bf16[96,1024]{1,0:T(8,128)(2,1)S(1)}, u32[]{:S(2)}, u32[]{:S(2)}) collective-permute-start(bf16[96,1024]{1,0:T(8,128)(2,1)S(1)} %pack.1.refs_0_), channel_id=1, source_target_pairs={{0,4},{1,17},{2,6},{3,19},{4,0},{5,21},{6,2},{7,23},{8,12},{9,25},... | collective-permute-start | bytes 589832 | tf_op jit(solution)/shard_map/ppermute | solution.py:392
  17.1 6.0 %collective-permute-start.4 = (bf16[96,1024]{1,0:T(8,128)(2,1)S(1)}, bf16[96,1024]{1,0:T(8,128)(2,1)S(1)}, u32[]{:S(2)}, u32[]{:S(2)}) collective-permute-start(bf16[96,1024]{1,0:T(8,128)(2,1)S(1)} %pack.1.refs_0_), channel_id=1, source_target_pairs={{0,2},{1,9},{2,4},{3,11},{4,6},{5,13},{6,0},{7,15},{8,10},{9,17},{... | collective-permute-start | bytes 589832 | tf_op jit(solution)/shard_map/ppermute | solution.py:392
  17.5 5.7 %collective-permute-start.3 = (bf16[96,1024]{1,0:T(8,128)(2,1)S(1)}, bf16[96,1024]{1,0:T(8,128)(2,1)S(1)}, u32[]{:S(2)}, u32[]{:S(2)}) collective-permute-start(bf16[96,1024]{1,0:T(8,128)(2,1)S(1)} %pack.1.refs_0_), channel_id=1, source_target_pairs={{0,6},{1,25},{2,0},{3,27},{4,2},{5,29},{6,4},{7,31},{8,14},{9,1},{... | collective-permute-start | bytes 589832 | tf_op jit(solution)/shard_map/ppermute | solution.py:392
  24.2 23.1 %collective-permute-start.11 = (bf16[1024,512]{1,0:T(8,128)(2,1)S(1)}, bf16[1024,512]{1,0:T(8,128)(2,1)S(1)}, u32[]{:S(2)}, u32[]{:S(2)}) collective-permute-start(bf16[1024,512]{1,0:T(8,128)(2,1)S(1)} %pick_rows.8), channel_id=1, source_target_pairs={{0,64},{32,96},{64,0},{96,32},{1,65},{33,97},{65,1},{97,33},{2,66}... | collective-permute-start | bytes 3145736 | tf_op jit(solution)/shard_map/ppermute | solution.py:392
  24.7 13.5 %collective-permute-start.10 = (bf16[4,96,1024]{2,1,0:T(8,128)(2,1)S(1)}, bf16[4,96,1024]{2,1,0:T(8,128)(2,1)S(1)}, u32[]{:S(2)}, u32[]{:S(2)}) collective-permute-start(bf16[4,96,1024]{2,1,0:T(8,128)(2,1)S(1)} %bundle.1.refs_0_), channel_id=1, source_target_pairs={{0,16},{1,5},{2,18},{3,7},{4,20},{5,1},{6,22},{7,3},{8,24},{9,13},... | collective-permute-start | bytes 2359304 | tf_op jit(solution)/shard_map/ppermute | solution.py:392
  28.4 18.1 %collective-permute-start.9 = (bf16[4,96,1024]{2,1,0:T(8,128)(2,1)S(1)}, bf16[4,96,1024]{2,1,0:T(8,128)(2,1)S(1)}, u32[]{:S(2)}, u32[]{:S(2)}) collective-permute-start(bf16[4,96,1024]{2,1,0:T(8,128)(2,1)S(1)} %bundle.1.refs_0_), channel_id=1, source_target_pairs={{0,8},{1,3},{2,10},{3,5},{4,12},{5,7},{6,14},{7,1},{8,16},{9,11},{... | collective-permute-start | bytes 2359304 | tf_op jit(solution)/shard_map/ppermute | solution.py:392
  29.2 18.1 %collective-permute-start.8 = (bf16[4,96,1024]{2,1,0:T(8,128)(2,1)S(1)}, bf16[4,96,1024]{2,1,0:T(8,128)(2,1)S(1)}, u32[]{:S(2)}, u32[]{:S(2)}) collective-permute-start(bf16[4,96,1024]{2,1,0:T(8,128)(2,1)S(1)} %bundle.1.refs_0_), channel_id=1, source_target_pairs={{0,24},{1,7},{2,26},{3,1},{4,28},{5,3},{6,30},{7,5},{8,0},{9,15},{... | collective-permute-start | bytes 2359304 | tf_op jit(solution)/shard_map/ppermute | solution.py:392
  32.5 1.5 copy-start.7
  47.5 9.5 %collective-permute-start.14 = (bf16[16,96,1024]{2,1,0:T(8,128)(2,1)S(1)}, bf16[16,96,1024]{2,1,0:T(8,128)(2,1)S(1)}, u32[]{:S(2)}, u32[]{:S(2)}) collective-permute-start(bf16[16,96,1024]{2,1,0:T(8,128)(2,1)S(1)} %half_of_weights.1.a), channel_id=1, source_target_pairs={{0,1},{1,0},{2,3},{3,2},{4,5},{5,4},{6,7},{7,6},{8,9},{9,8},{10,11... | collective-permute-start | bytes 9437192 | tf_op jit(solution)/shard_map/ppermute | solution.py:392
  51.8 14.7 %collective-permute-start.12 = (bf16[512,512]{1,0:T(8,128)(2,1)S(1)}, bf16[512,512]{1,0:T(8,128)(2,1)S(1)}, u32[]{:S(2)}, u32[]{:S(2)}) collective-permute-start(bf16[512,512]{1,0:T(8,128)(2,1)S(1)} %pick_rows.10), channel_id=1, source_target_pairs={{0,32},{32,64},{64,96},{96,0},{1,33},{33,65},{65,97},{97,1},{2,34}... | collective-permute-start | bytes 1572872 | tf_op jit(solution)/shard_map/ppermute | solution.py:392
  52.9 13.6 %collective-permute-start.13 = (bf16[512,512]{1,0:T(8,128)(2,1)S(1)}, bf16[512,512]{1,0:T(8,128)(2,1)S(1)}, u32[]{:S(2)}, u32[]{:S(2)}) collective-permute-start(bf16[512,512]{1,0:T(8,128)(2,1)S(1)} %pick_rows.11), channel_id=1, source_target_pairs={{0,96},{32,0},{64,32},{96,64},{1,97},{33,1},{65,33},{97,65},{2,98}... | collective-permute-start | bytes 1572872 | tf_op jit(solution)/shard_map/ppermute | solution.py:392
  57.5 3.0 %copy-start.6 = (f32[1,512]{1,0:T(1,128)S(1)}, f32[1,512]{1,0:T(1,128)}, u32[]{:S(2)}) copy-start(f32[1,512]{1,0:T(1,128)} %route_ref.3) | copy-start | bytes 6148
  68.0 3.5 %collective-permute-start.15 = (bf16[16,64,512]{2,1,0:T(8,128)(2,1)S(1)}, bf16[16,64,512]{2,1,0:T(8,128)(2,1)S(1)}, u32[]{:S(2)}, u32[]{:S(2)}) collective-permute-start(bf16[16,64,512]{2,1,0:T(8,128)(2,1)S(1)} %get-tuple-element.143), channel_id=1, source_target_pairs={{0,1},{1,0},{2,3},{3,2},{4,5},{5,4},{6,7},{7,6},{8,9},{9,8},{10,11... | collective-permute-start | bytes 3145736 | tf_op jit(solution)/shard_map/ppermute | solution.py:392
  71.4 4.2 %collective-permute-start.16 = (bf16[16,128,512]{2,1,0:T(8,128)(2,1)S(1)}, bf16[16,128,512]{2,1,0:T(8,128)(2,1)S(1)}, u32[]{:S(2)}, u32[]{:S(2)}) collective-permute-start(bf16[16,128,512]{2,1,0:T(8,128)(2,1)S(1)} %get-tuple-element.145), channel_id=1, source_target_pairs={{0,1},{1,0},{2,3},{3,2},{4,5},{5,4},{6,7},{7,6},{8,9},{9,8},{10,11... | collective-permute-start | bytes 6291464 | tf_op jit(solution)/shard_map/ppermute | solution.py:392
  76.5 1.3 collective-permute-start.17
  79.1 19.9 %collective-permute-start.18 = (bf16[4,192,512]{2,1,0:T(8,128)(2,1)S(1)}, bf16[4,192,512]{2,1,0:T(8,128)(2,1)S(1)}, u32[]{:S(2)}, u32[]{:S(2)}) collective-permute-start(bf16[4,192,512]{2,1,0:T(8,128)(2,1)S(1)} %get-tuple-element.154), channel_id=1, source_target_pairs={{0,6},{1,25},{2,0},{3,27},{4,2},{5,29},{6,4},{7,31},{8,14},{9,1},{... | collective-permute-start | bytes 2359304 | tf_op jit(solution)/shard_map/ppermute | solution.py:392
  81.6 20.8 %collective-permute-start.19 = (bf16[4,192,512]{2,1,0:T(8,128)(2,1)S(1)}, bf16[4,192,512]{2,1,0:T(8,128)(2,1)S(1)}, u32[]{:S(2)}, u32[]{:S(2)}) collective-permute-start(bf16[4,192,512]{2,1,0:T(8,128)(2,1)S(1)} %get-tuple-element.155), channel_id=1, source_target_pairs={{0,2},{1,9},{2,4},{3,11},{4,6},{5,13},{6,0},{7,15},{8,10},{9,17},{... | collective-permute-start | bytes 2359304 | tf_op jit(solution)/shard_map/ppermute | solution.py:392
  81.6 20.8 %collective-permute-start.20 = (bf16[4,192,512]{2,1,0:T(8,128)(2,1)S(1)}, bf16[4,192,512]{2,1,0:T(8,128)(2,1)S(1)}, u32[]{:S(2)}, u32[]{:S(2)}) collective-permute-start(bf16[4,192,512]{2,1,0:T(8,128)(2,1)S(1)} %get-tuple-element.156), channel_id=1, source_target_pairs={{0,4},{1,17},{2,6},{3,19},{4,0},{5,21},{6,2},{7,23},{8,12},{9,25},... | collective-permute-start | bytes 2359304 | tf_op jit(solution)/shard_map/ppermute | solution.py:392
  83.3 12.0 %collective-permute-start.21 = (bf16[512,512]{1,0:T(8,128)(2,1)S(1)}, bf16[512,512]{1,0:T(8,128)(2,1)S(1)}, u32[]{:S(2)}, u32[]{:S(2)}) collective-permute-start(bf16[512,512]{1,0:T(8,128)(2,1)S(1)} %get-tuple-element.158), channel_id=1, source_target_pairs={{0,96},{32,0},{64,32},{96,64},{1,97},{33,1},{65,33},{97,65},{2,98}... | collective-permute-start | bytes 1572872 | tf_op jit(solution)/shard_map/ppermute | solution.py:392
  86.0 12.4 %collective-permute-start.22 = (bf16[512,512]{1,0:T(8,128)(2,1)S(1)}, bf16[512,512]{1,0:T(8,128)(2,1)S(1)}, u32[]{:S(2)}, u32[]{:S(2)}) collective-permute-start(bf16[512,512]{1,0:T(8,128)(2,1)S(1)} %get-tuple-element.159), channel_id=1, source_target_pairs={{0,32},{32,64},{64,96},{96,0},{1,33},{33,65},{65,97},{97,1},{2,34}... | collective-permute-start | bytes 1572872 | tf_op jit(solution)/shard_map/ppermute | solution.py:392
  102.6 21.1 %collective-permute-start.23 = (bf16[4,192,512]{2,1,0:T(8,128)(2,1)S(1)}, bf16[4,192,512]{2,1,0:T(8,128)(2,1)S(1)}, u32[]{:S(2)}, u32[]{:S(2)}) collective-permute-start(bf16[4,192,512]{2,1,0:T(8,128)(2,1)S(1)} %get-tuple-element.169), channel_id=1, source_target_pairs={{0,24},{1,7},{2,26},{3,1},{4,28},{5,3},{6,30},{7,5},{8,0},{9,15},{... | collective-permute-start | bytes 2359304 | tf_op jit(solution)/shard_map/ppermute | solution.py:392
  106.3 20.8 %collective-permute-start.24 = (bf16[4,192,512]{2,1,0:T(8,128)(2,1)S(1)}, bf16[4,192,512]{2,1,0:T(8,128)(2,1)S(1)}, u32[]{:S(2)}, u32[]{:S(2)}) collective-permute-start(bf16[4,192,512]{2,1,0:T(8,128)(2,1)S(1)} %get-tuple-element.170), channel_id=1, source_target_pairs={{0,8},{1,3},{2,10},{3,5},{4,12},{5,7},{6,14},{7,1},{8,16},{9,11},{... | collective-permute-start | bytes 2359304 | tf_op jit(solution)/shard_map/ppermute | solution.py:392
  106.3 20.8 %collective-permute-start.25 = (bf16[4,192,512]{2,1,0:T(8,128)(2,1)S(1)}, bf16[4,192,512]{2,1,0:T(8,128)(2,1)S(1)}, u32[]{:S(2)}, u32[]{:S(2)}) collective-permute-start(bf16[4,192,512]{2,1,0:T(8,128)(2,1)S(1)} %get-tuple-element.171), channel_id=1, source_target_pairs={{0,16},{1,5},{2,18},{3,7},{4,20},{5,1},{6,22},{7,3},{8,24},{9,13},... | collective-permute-start | bytes 2359304 | tf_op jit(solution)/shard_map/ppermute | solution.py:392
  107.7 12.1 %collective-permute-start.26 = (bf16[512,512]{1,0:T(8,128)(2,1)S(1)}, bf16[512,512]{1,0:T(8,128)(2,1)S(1)}, u32[]{:S(2)}, u32[]{:S(2)}) collective-permute-start(bf16[512,512]{1,0:T(8,128)(2,1)S(1)} %get-tuple-element.173), channel_id=1, source_target_pairs={{0,64},{32,96},{64,0},{96,32},{1,65},{33,97},{65,1},{97,33},{2,66}... | collective-permute-start | bytes 1572872 | tf_op jit(solution)/shard_map/ppermute | solution.py:392
  129.5 5.2 %collective-permute-start.29 = (f32[3,16,128]{2,1,0:T(8,128)S(1)}, f32[3,16,128]{2,1,0:T(8,128)S(1)}, u32[]{:S(2)}, u32[]{:S(2)}) collective-permute-start(f32[3,16,128]{2,1,0:T(8,128)S(1)} %gram.1), channel_id=1, source_target_pairs={{0,6},{1,7},{2,0},{3,1},{4,2},{5,3},{6,4},{7,5},{8,14},{9,15},{10,... | collective-permute-start | bytes 73736 | tf_op jit(solution)/shard_map/ppermute | solution.py:392
  129.5 5.2 %collective-permute-start.28 = (f32[3,16,128]{2,1,0:T(8,128)S(1)}, f32[3,16,128]{2,1,0:T(8,128)S(1)}, u32[]{:S(2)}, u32[]{:S(2)}) collective-permute-start(f32[3,16,128]{2,1,0:T(8,128)S(1)} %gram.1), channel_id=1, source_target_pairs={{0,2},{1,3},{2,4},{3,5},{4,6},{5,7},{6,0},{7,1},{8,10},{9,11},{10,... | collective-permute-start | bytes 73736 | tf_op jit(solution)/shard_map/ppermute | solution.py:392
  130.9 4.2 %collective-permute-start.27 = (f32[3,16,128]{2,1,0:T(8,128)S(1)}, f32[3,16,128]{2,1,0:T(8,128)S(1)}, u32[]{:S(2)}, u32[]{:S(2)}) collective-permute-start(f32[3,16,128]{2,1,0:T(8,128)S(1)} %gram.1), channel_id=1, source_target_pairs={{0,4},{1,5},{2,6},{3,7},{4,0},{5,1},{6,2},{7,3},{8,12},{9,13},{10,... | collective-permute-start | bytes 73736 | tf_op jit(solution)/shard_map/ppermute | solution.py:392
  135.1 12.8 %copy-start.3 = (f32[1,64,512]{2,1,0:T(8,128)S(1)}, f32[1,64,512]{2,1,0:T(8,128)}, u32[]{:S(2)}) copy-start(f32[1,64,512]{2,1,0:T(8,128)} %param.17) | copy-start | bytes 393220
  135.1 12.8 %copy-start.4 = (f32[1,64,512]{2,1,0:T(8,128)S(1)}, f32[1,64,512]{2,1,0:T(8,128)}, u32[]{:S(2)}) copy-start(f32[1,64,512]{2,1,0:T(8,128)} %param.18) | copy-start | bytes 393220
  135.2 12.8 %copy-start.5 = (f32[1,16,2048]{2,1,0:T(8,128)S(1)}, f32[1,16,2048]{2,1,0:T(8,128)}, u32[]{:S(2)}) copy-start(f32[1,16,2048]{2,1,0:T(8,128)} %param.19) | copy-start | bytes 393220
  135.2 5.6 %collective-permute-start.32 = (f32[3,16,128]{2,1,0:T(8,128)S(1)}, f32[3,16,128]{2,1,0:T(8,128)S(1)}, u32[]{:S(2)}, u32[]{:S(2)}) collective-permute-start(f32[3,16,128]{2,1,0:T(8,128)S(1)} %add_add_fusion.1), channel_id=1, source_target_pairs={{0,24},{1,25},{2,26},{3,27},{4,28},{5,29},{6,30},{7,31},{8,0},{9,1... | collective-permute-start | bytes 73736 | tf_op jit(solution)/shard_map/ppermute | solution.py:392
  135.7 5.0 %collective-permute-start.31 = (f32[3,16,128]{2,1,0:T(8,128)S(1)}, f32[3,16,128]{2,1,0:T(8,128)S(1)}, u32[]{:S(2)}, u32[]{:S(2)}) collective-permute-start(f32[3,16,128]{2,1,0:T(8,128)S(1)} %add_add_fusion.1), channel_id=1, source_target_pairs={{0,8},{1,9},{2,10},{3,11},{4,12},{5,13},{6,14},{7,15},{8,16},{9,17... | collective-permute-start | bytes 73736 | tf_op jit(solution)/shard_map/ppermute | solution.py:392
  136.7 4.2 %collective-permute-start.30 = (f32[3,16,128]{2,1,0:T(8,128)S(1)}, f32[3,16,128]{2,1,0:T(8,128)S(1)}, u32[]{:S(2)}, u32[]{:S(2)}) collective-permute-start(f32[3,16,128]{2,1,0:T(8,128)S(1)} %add_add_fusion.1), channel_id=1, source_target_pairs={{0,16},{1,17},{2,18},{3,19},{4,20},{5,21},{6,22},{7,23},{8,24},{9,... | collective-permute-start | bytes 73736 | tf_op jit(solution)/shard_map/ppermute | solution.py:392
  140.9 7.1 %collective-permute-start.33 = (f32[3,16,128]{2,1,0:T(8,128)S(1)}, f32[3,16,128]{2,1,0:T(8,128)S(1)}, u32[]{:S(2)}, u32[]{:S(2)}) collective-permute-start(f32[3,16,128]{2,1,0:T(8,128)S(1)} %add_add_fusion.g_ref), channel_id=1, source_target_pairs={{0,1},{1,0},{2,3},{3,2},{4,5},{5,4},{6,7},{7,6},{8,9},{9,8},{10,11... | collective-permute-start | bytes 73736 | tf_op jit(solution)/shard_map/ppermute | solution.py:392

commit v14 on v12

--- a/solution.py
+++ b/solution.py
@@ -563,12 +563,12 @@
     mine = pair_moments(keep, received)
     sent = pair_merge(keep, received, mine, other_core(mine))
     parts = [sent[0], *to_others(sent, 0)]
-    back = [slots[0], around_y(slots[1], 3), None, around_y(slots[3], 1)]
+    back = [slots[0], None, around_y(slots[2], 2), None]
+    parts, back[2] = tie_far(parts, back[2])
+    sent, slots[1], slots[3] = tie((turn_over(parts), slots[1], slots[3]))
+    parts = [sent[0], *to_others(sent, 1)]
+    back[1], back[3] = around_y(slots[1], 3), around_y(slots[3], 1)
     parts, (back[1], back[3]) = tie_far(parts, (back[1], back[3]))
-    sent, slots[2] = tie((turn_over(parts), slots[2]))
-    parts = [sent[0], *to_others(sent, 1)]
-    back[2] = around_y(slots[2], 2)
-    parts, back[2] = tie_far(parts, back[2])
     products, pool_grad = sum_dp(gram(parts), ids, back)
     outs = finish(
         parts,

time: 147 us -> 147 us (level)
  no operation moved by 1% of the time
where the time goes in v14:
time: 147 us; the launch traced here: 146 us
  starting transfers between devices  57 us (39%)
  waiting for transfers between devices  50.3 us (34%)
  Pallas kernels  36.2 us (25%)
  local copies, waits for them, and re-layouts  1.65 us (1%)
    ppermute x34, starting transfers between devices, shift(): lax.ppermute(block, axis, [(i, to(i)) for i in range(lax.axis_size(axis))])  57 us
    ppermute x34, waiting for transfers between devices, shift(): lax.ppermute(block, axis, [(i, to(i)) for i in range(lax.axis_size(axis))])  50.3 us
    pallas_call x6, Pallas kernels, pick_rows(): call(body, 'pick_rows', n_ids + n_pool, shapes, 2 * TOK_DEV * POOL * SLIC...  10.7 us
    pallas_call x2, Pallas kernels, scatter_rows(): pl.pallas_call(body, name='scatter_rows', grid=(steps,), out_shape=struct...  6.94 us
    pallas_call x1, Pallas kernels, forward(): call(body, 'forward', 5, shapes, 2 * TOK_DEV * D * 2 * H, 10 * MIB, [pltp...  3.02 us
  transfers between devices with their start and end apart: 34, of which 17 were waited for; matrix products, arithmetic and copies ran while one was open for 0% of the time, Pallas kernels for 19%

profile of v14, /device:TPU:1, one launch (start us, length us, event | category | flops | bytes accessed | tf_op | source)
XLA Modules:
  0.0 146.2 jit_solution(2829848596667591559)
XLA Ops:
  0.6 2.2 %collective-permute-start.2 = (s32[1,512]{1,0:T(1,128)}, s32[1,512]{1,0:T(1,128)S(1)}, u32[]{:S(2)}, u32[]{:S(2)}) collective-permute-start(s32[1,512]{1,0:T(1,128)} %refs_0_.2), channel_id=1, source_target_pairs={{0,32},{32,64},{64,96},{96,0},{1,33},{33,65},{65,97},{97,1},{2,34}... | collective-permute-start | bytes 6152 | tf_op jit(solution)/shard_map/ppermute | solution.py:393
  2.8 2.6 %collective-permute-start.1 = (s32[1,512]{1,0:T(1,128)}, s32[1,512]{1,0:T(1,128)S(1)}, u32[]{:S(2)}, u32[]{:S(2)}) collective-permute-start(s32[1,512]{1,0:T(1,128)} %refs_0_.2), channel_id=1, source_target_pairs={{0,64},{32,96},{64,0},{96,32},{1,65},{33,97},{65,1},{97,33},{2,66}... | collective-permute-start | bytes 6152 | tf_op jit(solution)/shard_map/ppermute | solution.py:393
  6.5 1.6 %copy-done.9 = bf16[2048,512]{1,0:T(8,128)(2,1)S(1)} copy-done((bf16[2048,512]{1,0:T(8,128)(2,1)S(1)}, bf16[2048,512]{1,0:T(8,128)(2,1)}, u32[]{:S(2)}) %copy-start.9) | copy-done | bytes 2097176
  8.1 1.4 pick_rows.7
  9.6 1.4 pick_rows.6
  11.5 2.3 %collective-permute-start.7 = (bf16[512,512]{1,0:T(8,128)(2,1)S(1)}, bf16[512,512]{1,0:T(8,128)(2,1)S(1)}, u32[]{:S(2)}, u32[]{:S(2)}) collective-permute-start(bf16[512,512]{1,0:T(8,128)(2,1)S(1)} %pick_rows.7), channel_id=1, source_target_pairs={{0,96},{32,0},{64,32},{96,64},{1,97},{33,1},{65,33},{97,65},{2,98}... | collective-permute-start | bytes 1572872 | tf_op jit(solution)/shard_map/ppermute | solution.py:393
  14.3 2.8 %collective-permute-start.5 = (bf16[96,1024]{1,0:T(8,128)(2,1)S(1)}, bf16[96,1024]{1,0:T(8,128)(2,1)S(1)}, u32[]{:S(2)}, u32[]{:S(2)}) collective-permute-start(bf16[96,1024]{1,0:T(8,128)(2,1)S(1)} %pack.1.refs_0_), channel_id=1, source_target_pairs={{0,4},{1,17},{2,6},{3,19},{4,0},{5,21},{6,2},{7,23},{8,12},{9,25},... | collective-permute-start | bytes 589832 | tf_op jit(solution)/shard_map/ppermute | solution.py:393
  17.5 2.3 %collective-permute-start.3 = (bf16[96,1024]{1,0:T(8,128)(2,1)S(1)}, bf16[96,1024]{1,0:T(8,128)(2,1)S(1)}, u32[]{:S(2)}, u32[]{:S(2)}) collective-permute-start(bf16[96,1024]{1,0:T(8,128)(2,1)S(1)} %pack.1.refs_0_), channel_id=1, source_target_pairs={{0,6},{1,25},{2,0},{3,27},{4,2},{5,29},{6,4},{7,31},{8,14},{9,1},{... | collective-permute-start | bytes 589832 | tf_op jit(solution)/shard_map/ppermute | solution.py:393
  19.8 2.5 %pick_rows.8 = bf16[1024,512]{1,0:T(8,128)(2,1)S(1)} custom-call(s32[1,512]{1,0:T(1,128)S(1)} %collective-permute-done.1.refs_0_.refs_2_, bf16[2048,512]{1,0:T(8,128)(2,1)S(1)} %copy-done.9, bf16[2048,512]{1,0:T(8,128)(2,1)S(1)} %copy-done.8), custom_call_target="tpu_custom_call" | custom-call | flops 2147483648 | bytes 3145728 | tf_op jit(solution)/shard_map/pick_rows/pallas_call | solution.py:73
  24.7 3.7 %collective-permute-start.10 = (bf16[4,96,1024]{2,1,0:T(8,128)(2,1)S(1)}, bf16[4,96,1024]{2,1,0:T(8,128)(2,1)S(1)}, u32[]{:S(2)}, u32[]{:S(2)}) collective-permute-start(bf16[4,96,1024]{2,1,0:T(8,128)(2,1)S(1)} %bundle.1.refs_0_), channel_id=1, source_target_pairs={{0,16},{1,5},{2,18},{3,7},{4,20},{5,1},{6,22},{7,3},{8,24},{9,13},... | collective-permute-start | bytes 2359304 | tf_op jit(solution)/shard_map/ppermute | solution.py:393
  29.2 1.9 %collective-permute-start.8 = (bf16[4,96,1024]{2,1,0:T(8,128)(2,1)S(1)}, bf16[4,96,1024]{2,1,0:T(8,128)(2,1)S(1)}, u32[]{:S(2)}, u32[]{:S(2)}) collective-permute-start(bf16[4,96,1024]{2,1,0:T(8,128)(2,1)S(1)} %bundle.1.refs_0_), channel_id=1, source_target_pairs={{0,24},{1,7},{2,26},{3,1},{4,28},{5,3},{6,30},{7,5},{8,0},{9,15},{... | collective-permute-start | bytes 2359304 | tf_op jit(solution)/shard_map/ppermute | solution.py:393
  31.1 1.4 pick_rows.10
  32.6 1.4 pick_rows.11
  34.0 2.5 %pick_rows.9 = (bf16[512,512]{1,0:T(8,128)(2,1)S(1)}, bf16[512,512]{1,0:T(8,128)(2,1)S(1)}) custom-call(s32[1,512]{1,0:T(1,128)S(1)} %copy-done.7, bf16[2048,512]{1,0:T(8,128)(2,1)S(1)} %copy-done.9, bf16[2048,512]{1,0:T(8,128)(2,1)S(1)} %copy-done.8), custom_call_target="tpu_custom_call" | custom-call | flops 2147483648 | bytes 3145728 | tf_op jit(solution)/shard_map/pick_rows/pallas_call | solution.py:73
  36.5 1.6 %collective-permute-done.10.refs_2_ = bf16[4,96,1024]{2,1,0:T(8,128)(2,1)S(1)} collective-permute-done((bf16[4,96,1024]{2,1,0:T(8,128)(2,1)S(1)}, bf16[4,96,1024]{2,1,0:T(8,128)(2,1)S(1)}, u32[]{:S(2)}, u32[]{:S(2)}) %collective-permute-start.10) | collective-permute-done | bytes 786464 | tf_op jit(solution)/shard_map/ppermute | solution.py:393
  38.1 8.4 %collective-permute-done.9.refs_1_ = bf16[4,96,1024]{2,1,0:T(8,128)(2,1)S(1)} collective-permute-done((bf16[4,96,1024]{2,1,0:T(8,128)(2,1)S(1)}, bf16[4,96,1024]{2,1,0:T(8,128)(2,1)S(1)}, u32[]{:S(2)}, u32[]{:S(2)}) %collective-permute-start.9) | collective-permute-done | bytes 786464 | tf_op jit(solution)/shard_map/ppermute | solution.py:393
  47.5 4.2 %collective-permute-start.14 = (bf16[16,96,1024]{2,1,0:T(8,128)(2,1)S(1)}, bf16[16,96,1024]{2,1,0:T(8,128)(2,1)S(1)}, u32[]{:S(2)}, u32[]{:S(2)}) collective-permute-start(bf16[16,96,1024]{2,1,0:T(8,128)(2,1)S(1)} %half_of_weights.1.a), channel_id=1, source_target_pairs={{0,1},{1,0},{2,3},{3,2},{4,5},{5,4},{6,7},{7,6},{8,9},{9,8},{10,11... | collective-permute-start | bytes 9437192 | tf_op jit(solution)/shard_map/ppermute | solution.py:393
  51.8 1.1 collective-permute-start.12
  52.9 1.5 %collective-permute-start.13 = (bf16[512,512]{1,0:T(8,128)(2,1)S(1)}, bf16[512,512]{1,0:T(8,128)(2,1)S(1)}, u32[]{:S(2)}, u32[]{:S(2)}) collective-permute-start(bf16[512,512]{1,0:T(8,128)(2,1)S(1)} %pick_rows.11), channel_id=1, source_target_pairs={{0,96},{32,0},{64,32},{96,64},{1,97},{33,1},{65,33},{97,65},{2,98}... | collective-permute-start | bytes 1572872 | tf_op jit(solution)/shard_map/ppermute | solution.py:393
  54.4 2.6 %collective-permute-done.14.b = bf16[16,96,1024]{2,1,0:T(8,128)(2,1)S(1)} collective-permute-done((bf16[16,96,1024]{2,1,0:T(8,128)(2,1)S(1)}, bf16[16,96,1024]{2,1,0:T(8,128)(2,1)S(1)}, u32[]{:S(2)}, u32[]{:S(2)}) %collective-permute-start.14) | collective-permute-done | bytes 3145760 | tf_op jit(solution)/shard_map/ppermute | solution.py:393
  57.5 3.0 %forward.1 = (bf16[512,512]{1,0:T(8,128)(2,1)S(1)}, f32[512,512]{1,0:T(8,128)S(1)}, f32[512,512]{1,0:T(8,128)S(1)}, bf16[4,512,512]{2,1,0:T(8,128)(2,1)S(1)}) custom-call(bf16[512,512]{1,0:T(8,128)(2,1)S(1)} %get-tuple-element.126.x0, bf16[512,512]{1,0:T(8,128)(2,1)S(1)} %collective-permute-done.6.x1, bf16[1024,512]{1,0:T(8,128)(2,1)S(1)} %collective-permute-done.11.x2.c2, ...), custom_call_target="tpu_custom_call" | custom-call | flops 2147483648 | bytes 10485760 | tf_op jit(solution)/shard_map/forward/pallas_call | solution.py:127
  60.5 1.4 backward_early.1
  62.0 4.5 %collective-permute-done.12.c1 = bf16[512,512]{1,0:T(8,128)(2,1)S(1)} collective-permute-done((bf16[512,512]{1,0:T(8,128)(2,1)S(1)}, bf16[512,512]{1,0:T(8,128)(2,1)S(1)}, u32[]{:S(2)}, u32[]{:S(2)}) %collective-permute-start.12) | collective-permute-done | bytes 524320 | tf_op jit(solution)/shard_map/ppermute | solution.py:393
  66.5 1.5 %backward_down.1 = (bf16[16,64,512]{2,1,0:T(8,128)(2,1)S(1)}, bf16[16,64,512]{2,1,0:T(8,128)(2,1)S(1)}, f32[512,512]{1,0:T(8,128)S(1)}) custom-call(bf16[512,512]{1,0:T(8,128)(2,1)S(1)} %collective-permute-done.12.c1, bf16[512,512]{1,0:T(8,128)(2,1)S(1)} %collective-permute-done.13.c3, f32[1,512]{1,0:T(1,128)S(1)} %copy-done.6, ...), custom_call_target="tpu_custom_call" | custom-call | flops 1073741824 | bytes 10485760 | tf_op jit(solution)/shard_map/backward_down/pallas_call | solution.py:186
  68.9 2.5 %backward_in.1 = (bf16[16,128,512]{2,1,0:T(8,128)(2,1)S(1)}, bf16[16,128,512]{2,1,0:T(8,128)(2,1)S(1)}, bf16[512,1024]{1,0:T(8,128)(2,1)S(1)}) custom-call(f32[512,512]{1,0:T(8,128)S(1)} %get-tuple-element.138.hg, f32[512,512]{1,0:T(8,128)S(1)} %get-tuple-element.139.factor, f32[512,512]{1,0:T(8,128)S(1)} %get-tuple-element.140.act_ref, ...), custom_call_target="tpu_custom_call" | custom-call | flops 2147483648 | bytes 10485760 | tf_op jit(solution)/shard_map/backward_in/pallas_call | solution.py:214
  71.6 2.4 %slot_gradients.1 = (bf16[512,512]{1,0:T(8,128)(2,1)S(1)}, bf16[512,512]{1,0:T(8,128)(2,1)S(1)}, bf16[512,512]{1,0:T(8,128)(2,1)S(1)}, bf16[512,512]{1,0:T(8,128)(2,1)S(1)}) custom-call(bf16[512,1024]{1,0:T(8,128)(2,1)S(1)} %get-tuple-element.148.both_ref, bf16[32,96,1024]{2,1,0:T(8,128)(2,1)S(1)} %whole_weights.1.w), custom_call_target="tpu_custom_call" | custom-call | flops 2147483648 | bytes 9437184 | tf_op jit(solution)/shard_map/slot_gradients/pallas_call | solution.py:224
  73.9 1.8 %collective-permute-done.16.b_in = bf16[16,128,512]{2,1,0:T(8,128)(2,1)S(1)} collective-permute-done((bf16[16,128,512]{2,1,0:T(8,128)(2,1)S(1)}, bf16[16,128,512]{2,1,0:T(8,128)(2,1)S(1)}, u32[]{:S(2)}, u32[]{:S(2)}) %collective-permute-start.16) | collective-permute-done | bytes 2097184 | tf_op jit(solution)/shard_map/ppermute | solution.py:393
  76.7 1.1 collective-permute-done.17.t_ref
  77.8 1.3 pair_merge.1
  79.1 2.8 %collective-permute-start.18 = (bf16[4,192,512]{2,1,0:T(8,128)(2,1)S(1)}, bf16[4,192,512]{2,1,0:T(8,128)(2,1)S(1)}, u32[]{:S(2)}, u32[]{:S(2)}) collective-permute-start(bf16[4,192,512]{2,1,0:T(8,128)(2,1)S(1)} %get-tuple-element.155), channel_id=1, source_target_pairs={{0,4},{1,17},{2,6},{3,19},{4,0},{5,21},{6,2},{7,23},{8,12},{9,25},... | collective-permute-start | bytes 2359304 | tf_op jit(solution)/shard_map/ppermute | solution.py:393
  82.2 2.3 %collective-permute-start.20 = (bf16[4,192,512]{2,1,0:T(8,128)(2,1)S(1)}, bf16[4,192,512]{2,1,0:T(8,128)(2,1)S(1)}, u32[]{:S(2)}, u32[]{:S(2)}) collective-permute-start(bf16[4,192,512]{2,1,0:T(8,128)(2,1)S(1)} %get-tuple-element.157), channel_id=1, source_target_pairs={{0,6},{1,25},{2,0},{3,27},{4,2},{5,29},{6,4},{7,31},{8,14},{9,1},{... | collective-permute-start | bytes 2359304 | tf_op jit(solution)/shard_map/ppermute | solution.py:393
  84.6 2.4 %collective-permute-start.21 = (bf16[512,512]{1,0:T(8,128)(2,1)S(1)}, bf16[512,512]{1,0:T(8,128)(2,1)S(1)}, u32[]{:S(2)}, u32[]{:S(2)}) collective-permute-start(bf16[512,512]{1,0:T(8,128)(2,1)S(1)} %get-tuple-element.159), channel_id=1, source_target_pairs={{0,64},{32,96},{64,0},{96,32},{1,65},{33,97},{65,1},{97,33},{2,66}... | collective-permute-start | bytes 1572872 | tf_op jit(solution)/shard_map/ppermute | solution.py:393
  86.9 10.7 %collective-permute-done.21.refs_6_ = bf16[512,512]{1,0:T(8,128)(2,1)S(1)} collective-permute-done((bf16[512,512]{1,0:T(8,128)(2,1)S(1)}, bf16[512,512]{1,0:T(8,128)(2,1)S(1)}, u32[]{:S(2)}, u32[]{:S(2)}) %collective-permute-start.21) | collective-permute-done | bytes 524320 | tf_op jit(solution)/shard_map/ppermute | solution.py:393
  97.6 2.6 %collective-permute-done.19.refs_1_ = bf16[4,192,512]{2,1,0:T(8,128)(2,1)S(1)} collective-permute-done((bf16[4,192,512]{2,1,0:T(8,128)(2,1)S(1)}, bf16[4,192,512]{2,1,0:T(8,128)(2,1)S(1)}, u32[]{:S(2)}, u32[]{:S(2)}) %collective-permute-start.19) | collective-permute-done | bytes 786464 | tf_op jit(solution)/shard_map/ppermute | solution.py:393
  100.6 3.7 %collective-permute-start.22 = (bf16[4,192,512]{2,1,0:T(8,128)(2,1)S(1)}, bf16[4,192,512]{2,1,0:T(8,128)(2,1)S(1)}, u32[]{:S(2)}, u32[]{:S(2)}) collective-permute-start(bf16[4,192,512]{2,1,0:T(8,128)(2,1)S(1)} %get-tuple-element.170), channel_id=1, source_target_pairs={{0,16},{1,5},{2,18},{3,7},{4,20},{5,1},{6,22},{7,3},{8,24},{9,13},... | collective-permute-start | bytes 2359304 | tf_op jit(solution)/shard_map/ppermute | solution.py:393
  104.9 2.0 %collective-permute-start.24 = (bf16[4,192,512]{2,1,0:T(8,128)(2,1)S(1)}, bf16[4,192,512]{2,1,0:T(8,128)(2,1)S(1)}, u32[]{:S(2)}, u32[]{:S(2)}) collective-permute-start(bf16[4,192,512]{2,1,0:T(8,128)(2,1)S(1)} %get-tuple-element.172), channel_id=1, source_target_pairs={{0,24},{1,7},{2,26},{3,1},{4,28},{5,3},{6,30},{7,5},{8,0},{9,15},{... | collective-permute-start | bytes 2359304 | tf_op jit(solution)/shard_map/ppermute | solution.py:393
  106.9 2.7 %collective-permute-start.25 = (bf16[512,512]{1,0:T(8,128)(2,1)S(1)}, bf16[512,512]{1,0:T(8,128)(2,1)S(1)}, u32[]{:S(2)}, u32[]{:S(2)}) collective-permute-start(bf16[512,512]{1,0:T(8,128)(2,1)S(1)} %get-tuple-element.174), channel_id=1, source_target_pairs={{0,96},{32,0},{64,32},{96,64},{1,97},{33,1},{65,33},{97,65},{2,98}... | collective-permute-start | bytes 1572872 | tf_op jit(solution)/shard_map/ppermute | solution.py:393
  109.6 8.9 %collective-permute-done.25.refs_5_ = bf16[512,512]{1,0:T(8,128)(2,1)S(1)} collective-permute-done((bf16[512,512]{1,0:T(8,128)(2,1)S(1)}, bf16[512,512]{1,0:T(8,128)(2,1)S(1)}, u32[]{:S(2)}, u32[]{:S(2)}) %collective-permute-start.25) | collective-permute-done | bytes 524320 | tf_op jit(solution)/shard_map/ppermute | solution.py:393
  118.5 3.1 %collective-permute-done.26.refs_7_ = bf16[512,512]{1,0:T(8,128)(2,1)S(1)} collective-permute-done((bf16[512,512]{1,0:T(8,128)(2,1)S(1)}, bf16[512,512]{1,0:T(8,128)(2,1)S(1)}, u32[]{:S(2)}, u32[]{:S(2)}) %collective-permute-start.26) | collective-permute-done | bytes 524320 | tf_op jit(solution)/shard_map/ppermute | solution.py:393
  123.1 2.3 %gram.1 = f32[3,16,128]{2,1,0:T(8,128)S(1)} custom-call(bf16[4,192,512]{2,1,0:T(8,128)(2,1)S(1)} %get-tuple-element.176.refs_0_.x0, bf16[4,192,512]{2,1,0:T(8,128)(2,1)S(1)} %collective-permute-done.23.refs_1_.x1, bf16[4,192,512]{2,1,0:T(8,128)(2,1)S(1)} %collective-permute-done.22.refs_2_.x2, bf16[4,192,512]{2,1,0:T(8,128)(2,1)S(1)} %collective-permute-done.24.refs_3_.x3), custom_call_target="tpu_custom_call" | custom-call | flops 805306368 | bytes 3145728 | tf_op jit(solution)/shard_map/gram/pallas_call | solution.py:315
  125.4 2.4 %collective-permute-start.29 = (f32[3,16,128]{2,1,0:T(8,128)S(1)}, f32[3,16,128]{2,1,0:T(8,128)S(1)}, u32[]{:S(2)}, u32[]{:S(2)}) collective-permute-start(f32[3,16,128]{2,1,0:T(8,128)S(1)} %gram.1), channel_id=1, source_target_pairs={{0,6},{1,7},{2,0},{3,1},{4,2},{5,3},{6,4},{7,5},{8,14},{9,15},{10,... | collective-permute-start | bytes 73736 | tf_op jit(solution)/shard_map/ppermute | solution.py:393
  127.8 1.2 collective-permute-start.27
  129.0 3.5 %scatter_rows.2.refs_8_ = f32[2048,512]{1,0:T(8,128)} custom-call(s32[1,512]{1,0:T(1,128)S(1)} %copy-done.7, s32[1,512]{1,0:T(1,128)S(1)} %collective-permute-done.refs_0_.refs_1_, s32[1,512]{1,0:T(1,128)S(1)} %collective-permute-done.1.refs_0_.refs_2_, s32[1,512]{1,0:T(1,128)S(1)} %collective-permute-done.2.refs_0_.refs_3_, ...), custom_call_target="tpu_custom_call" | custom-call | flops 2147483648 | bytes 4194304 | tf_op jit(solution)/shard_map/scatter_rows/pallas_call | solution.py:379
  132.5 2.4 %collective-permute-start.32 = (f32[3,16,128]{2,1,0:T(8,128)S(1)}, f32[3,16,128]{2,1,0:T(8,128)S(1)}, u32[]{:S(2)}, u32[]{:S(2)}) collective-permute-start(f32[3,16,128]{2,1,0:T(8,128)S(1)} %add_add_fusion.1), channel_id=1, source_target_pairs={{0,24},{1,25},{2,26},{3,27},{4,28},{5,29},{6,30},{7,31},{8,0},{9,1... | collective-permute-start | bytes 73736 | tf_op jit(solution)/shard_map/ppermute | solution.py:393
  135.0 1.3 collective-permute-start.30
  136.2 3.5 %scatter_rows.3 = f32[2048,512]{1,0:T(8,128)} custom-call(s32[1,512]{1,0:T(1,128)S(1)} %copy-done.7, s32[1,512]{1,0:T(1,128)S(1)} %collective-permute-done.refs_0_.refs_1_, s32[1,512]{1,0:T(1,128)S(1)} %collective-permute-done.1.refs_0_.refs_2_, s32[1,512]{1,0:T(1,128)S(1)} %collective-permute-done.2.refs_0_.refs_3_, ...), custom_call_target="tpu_custom_call", output_to_operand_aliasing={{}: (8, {})} | custom-call | flops 2147483648 | bytes 4194304 | tf_op jit(solution)/shard_map/scatter_rows/pallas_call | solution.py:379
  139.7 3.7 %collective-permute-start.33 = (f32[3,16,128]{2,1,0:T(8,128)S(1)}, f32[3,16,128]{2,1,0:T(8,128)S(1)}, u32[]{:S(2)}, u32[]{:S(2)}) collective-permute-start(f32[3,16,128]{2,1,0:T(8,128)S(1)} %add_add_fusion.g_ref), channel_id=1, source_target_pairs={{0,1},{1,0},{2,3},{3,2},{4,5},{5,4},{6,7},{7,6},{8,9},{9,8},{10,11... | collective-permute-start | bytes 73736 | tf_op jit(solution)/shard_map/ppermute | solution.py:393
  144.3 1.8 %finish.1 = (f32[64,512]{1,0:T(8,128)}, f32[64,512]{1,0:T(8,128)}, f32[16,2048]{1,0:T(8,128)}, f32[64,512]{1,0:T(8,128)}, f32[64,512]{1,0:T(8,128)}, /*index=5*/f32[16,2048]{1,0:T(8,128)}) custom-call(bf16[4,192,512]{2,1,0:T(8,128)(2,1)S(1)} %get-tuple-element.176.refs_0_.x0, bf16[4,192,512]{2,1,0:T(8,128)(2,1)S(1)} %collective-permute-done.23.refs_1_.x1, ...), custom_call_target="tpu_custom_call" | custom-call | flops 4194304 | bytes 6291456 | tf_op jit(solution)/shard_map/finish/pallas_call | solution.py:361
  (64 shorter events, 12.9 us)
Async XLA Ops:
  0.6 5.9 %collective-permute-start.2 = (s32[1,512]{1,0:T(1,128)}, s32[1,512]{1,0:T(1,128)S(1)}, u32[]{:S(2)}, u32[]{:S(2)}) collective-permute-start(s32[1,512]{1,0:T(1,128)} %refs_0_.2), channel_id=1, source_target_pairs={{0,32},{32,64},{64,96},{96,0},{1,33},{33,65},{65,97},{97,1},{2,34}... | collective-permute-start | bytes 6152 | tf_op jit(solution)/shard_map/ppermute | solution.py:393
  2.8 8.2 %collective-permute-start.1 = (s32[1,512]{1,0:T(1,128)}, s32[1,512]{1,0:T(1,128)S(1)}, u32[]{:S(2)}, u32[]{:S(2)}) collective-permute-start(s32[1,512]{1,0:T(1,128)} %refs_0_.2), channel_id=1, source_target_pairs={{0,64},{32,96},{64,0},{96,32},{1,65},{33,97},{65,1},{97,33},{2,66}... | collective-permute-start | bytes 6152 | tf_op jit(solution)/shard_map/ppermute | solution.py:393
  5.4 4.1 %collective-permute-start = (s32[1,512]{1,0:T(1,128)}, s32[1,512]{1,0:T(1,128)S(1)}, u32[]{:S(2)}, u32[]{:S(2)}) collective-permute-start(s32[1,512]{1,0:T(1,128)} %refs_0_.2), channel_id=1, source_target_pairs={{0,96},{32,0},{64,32},{96,64},{1,97},{33,1},{65,33},{97,65},{2,98}... | collective-permute-start | bytes 6152 | tf_op jit(solution)/shard_map/ppermute | solution.py:393
  6.5 1.6 %copy-start.9 = (bf16[2048,512]{1,0:T(8,128)(2,1)S(1)}, bf16[2048,512]{1,0:T(8,128)(2,1)}, u32[]{:S(2)}) copy-start(bf16[2048,512]{1,0:T(8,128)(2,1)} %refs_1_.9) | copy-start | bytes 6291460
  9.5 4.2 %copy-start = (f32[1,64,512]{2,1,0:T(8,128)S(1)}, f32[1,64,512]{2,1,0:T(8,128)}, u32[]{:S(2)}) copy-start(f32[1,64,512]{2,1,0:T(8,128)} %param.14) | copy-start | bytes 393220
  9.5 4.2 %copy-start.1 = (f32[1,64,512]{2,1,0:T(8,128)S(1)}, f32[1,64,512]{2,1,0:T(8,128)}, u32[]{:S(2)}) copy-start(f32[1,64,512]{2,1,0:T(8,128)} %param.15) | copy-start | bytes 393220
  9.5 4.2 %copy-start.2 = (f32[1,16,2048]{2,1,0:T(8,128)S(1)}, f32[1,16,2048]{2,1,0:T(8,128)}, u32[]{:S(2)}) copy-start(f32[1,16,2048]{2,1,0:T(8,128)} %param.16) | copy-start | bytes 393220
  9.6 10.3 %copy-start.8 = (bf16[2048,512]{1,0:T(8,128)(2,1)S(1)}, bf16[2048,512]{1,0:T(8,128)(2,1)}, u32[]{:S(2)}) copy-start(bf16[2048,512]{1,0:T(8,128)(2,1)} %refs_1_.11) | copy-start | bytes 6291460
  11.0 13.2 %collective-permute-start.6 = (bf16[512,512]{1,0:T(8,128)(2,1)S(1)}, bf16[512,512]{1,0:T(8,128)(2,1)S(1)}, u32[]{:S(2)}, u32[]{:S(2)}) collective-permute-start(bf16[512,512]{1,0:T(8,128)(2,1)S(1)} %pick_rows.6), channel_id=1, source_target_pairs={{0,32},{32,64},{64,96},{96,0},{1,33},{33,65},{65,97},{97,1},{2,34}... | collective-permute-start | bytes 1572872 | tf_op jit(solution)/shard_map/ppermute | solution.py:393
  11.5 12.7 %collective-permute-start.7 = (bf16[512,512]{1,0:T(8,128)(2,1)S(1)}, bf16[512,512]{1,0:T(8,128)(2,1)S(1)}, u32[]{:S(2)}, u32[]{:S(2)}) collective-permute-start(bf16[512,512]{1,0:T(8,128)(2,1)S(1)} %pick_rows.7), channel_id=1, source_target_pairs={{0,96},{32,0},{64,32},{96,64},{1,97},{33,1},{65,33},{97,65},{2,98}... | collective-permute-start | bytes 1572872 | tf_op jit(solution)/shard_map/ppermute | solution.py:393
  14.3 8.0 %collective-permute-start.5 = (bf16[96,1024]{1,0:T(8,128)(2,1)S(1)}, bf16[96,1024]{1,0:T(8,128)(2,1)S(1)}, u32[]{:S(2)}, u32[]{:S(2)}) collective-permute-start(bf16[96,1024]{1,0:T(8,128)(2,1)S(1)} %pack.1.refs_0_), channel_id=1, source_target_pairs={{0,4},{1,17},{2,6},{3,19},{4,0},{5,21},{6,2},{7,23},{8,12},{9,25},... | collective-permute-start | bytes 589832 | tf_op jit(solution)/shard_map/ppermute | solution.py:393
  17.1 6.0 %collective-permute-start.4 = (bf16[96,1024]{1,0:T(8,128)(2,1)S(1)}, bf16[96,1024]{1,0:T(8,128)(2,1)S(1)}, u32[]{:S(2)}, u32[]{:S(2)}) collective-permute-start(bf16[96,1024]{1,0:T(8,128)(2,1)S(1)} %pack.1.refs_0_), channel_id=1, source_target_pairs={{0,2},{1,9},{2,4},{3,11},{4,6},{5,13},{6,0},{7,15},{8,10},{9,17},{... | collective-permute-start | bytes 589832 | tf_op jit(solution)/shard_map/ppermute | solution.py:393
  17.5 5.7 %collective-permute-start.3 = (bf16[96,1024]{1,0:T(8,128)(2,1)S(1)}, bf16[96,1024]{1,0:T(8,128)(2,1)S(1)}, u32[]{:S(2)}, u32[]{:S(2)}) collective-permute-start(bf16[96,1024]{1,0:T(8,128)(2,1)S(1)} %pack.1.refs_0_), channel_id=1, source_target_pairs={{0,6},{1,25},{2,0},{3,27},{4,2},{5,29},{6,4},{7,31},{8,14},{9,1},{... | collective-permute-start | bytes 589832 | tf_op jit(solution)/shard_map/ppermute | solution.py:393
  24.2 23.1 %collective-permute-start.11 = (bf16[1024,512]{1,0:T(8,128)(2,1)S(1)}, bf16[1024,512]{1,0:T(8,128)(2,1)S(1)}, u32[]{:S(2)}, u32[]{:S(2)}) collective-permute-start(bf16[1024,512]{1,0:T(8,128)(2,1)S(1)} %pick_rows.8), channel_id=1, source_target_pairs={{0,64},{32,96},{64,0},{96,32},{1,65},{33,97},{65,1},{97,33},{2,66}... | collective-permute-start | bytes 3145736 | tf_op jit(solution)/shard_map/ppermute | solution.py:393
  24.7 13.5 %collective-permute-start.10 = (bf16[4,96,1024]{2,1,0:T(8,128)(2,1)S(1)}, bf16[4,96,1024]{2,1,0:T(8,128)(2,1)S(1)}, u32[]{:S(2)}, u32[]{:S(2)}) collective-permute-start(bf16[4,96,1024]{2,1,0:T(8,128)(2,1)S(1)} %bundle.1.refs_0_), channel_id=1, source_target_pairs={{0,16},{1,5},{2,18},{3,7},{4,20},{5,1},{6,22},{7,3},{8,24},{9,13},... | collective-permute-start | bytes 2359304 | tf_op jit(solution)/shard_map/ppermute | solution.py:393
  28.4 18.1 %collective-permute-start.9 = (bf16[4,96,1024]{2,1,0:T(8,128)(2,1)S(1)}, bf16[4,96,1024]{2,1,0:T(8,128)(2,1)S(1)}, u32[]{:S(2)}, u32[]{:S(2)}) collective-permute-start(bf16[4,96,1024]{2,1,0:T(8,128)(2,1)S(1)} %bundle.1.refs_0_), channel_id=1, source_target_pairs={{0,8},{1,3},{2,10},{3,5},{4,12},{5,7},{6,14},{7,1},{8,16},{9,11},{... | collective-permute-start | bytes 2359304 | tf_op jit(solution)/shard_map/ppermute | solution.py:393
  29.2 18.1 %collective-permute-start.8 = (bf16[4,96,1024]{2,1,0:T(8,128)(2,1)S(1)}, bf16[4,96,1024]{2,1,0:T(8,128)(2,1)S(1)}, u32[]{:S(2)}, u32[]{:S(2)}) collective-permute-start(bf16[4,96,1024]{2,1,0:T(8,128)(2,1)S(1)} %bundle.1.refs_0_), channel_id=1, source_target_pairs={{0,24},{1,7},{2,26},{3,1},{4,28},{5,3},{6,30},{7,5},{8,0},{9,15},{... | collective-permute-start | bytes 2359304 | tf_op jit(solution)/shard_map/ppermute | solution.py:393
  32.5 1.5 %copy-start.7 = (s32[1,512]{1,0:T(1,128)S(1)}, s32[1,512]{1,0:T(1,128)}, u32[]{:S(2)}) copy-start(s32[1,512]{1,0:T(1,128)} %refs_0_.2) | copy-start | bytes 6148
  47.5 9.5 %collective-permute-start.14 = (bf16[16,96,1024]{2,1,0:T(8,128)(2,1)S(1)}, bf16[16,96,1024]{2,1,0:T(8,128)(2,1)S(1)}, u32[]{:S(2)}, u32[]{:S(2)}) collective-permute-start(bf16[16,96,1024]{2,1,0:T(8,128)(2,1)S(1)} %half_of_weights.1.a), channel_id=1, source_target_pairs={{0,1},{1,0},{2,3},{3,2},{4,5},{5,4},{6,7},{7,6},{8,9},{9,8},{10,11... | collective-permute-start | bytes 9437192 | tf_op jit(solution)/shard_map/ppermute | solution.py:393
  51.8 14.7 %collective-permute-start.12 = (bf16[512,512]{1,0:T(8,128)(2,1)S(1)}, bf16[512,512]{1,0:T(8,128)(2,1)S(1)}, u32[]{:S(2)}, u32[]{:S(2)}) collective-permute-start(bf16[512,512]{1,0:T(8,128)(2,1)S(1)} %pick_rows.10), channel_id=1, source_target_pairs={{0,32},{32,64},{64,96},{96,0},{1,33},{33,65},{65,97},{97,1},{2,34}... | collective-permute-start | bytes 1572872 | tf_op jit(solution)/shard_map/ppermute | solution.py:393
  52.9 13.6 %collective-permute-start.13 = (bf16[512,512]{1,0:T(8,128)(2,1)S(1)}, bf16[512,512]{1,0:T(8,128)(2,1)S(1)}, u32[]{:S(2)}, u32[]{:S(2)}) collective-permute-start(bf16[512,512]{1,0:T(8,128)(2,1)S(1)} %pick_rows.11), channel_id=1, source_target_pairs={{0,96},{32,0},{64,32},{96,64},{1,97},{33,1},{65,33},{97,65},{2,98}... | collective-permute-start | bytes 1572872 | tf_op jit(solution)/shard_map/ppermute | solution.py:393
  57.5 3.0 %copy-start.6 = (f32[1,512]{1,0:T(1,128)S(1)}, f32[1,512]{1,0:T(1,128)}, u32[]{:S(2)}) copy-start(f32[1,512]{1,0:T(1,128)} %route_ref.3) | copy-start | bytes 6148
  68.0 3.5 %collective-permute-start.15 = (bf16[16,64,512]{2,1,0:T(8,128)(2,1)S(1)}, bf16[16,64,512]{2,1,0:T(8,128)(2,1)S(1)}, u32[]{:S(2)}, u32[]{:S(2)}) collective-permute-start(bf16[16,64,512]{2,1,0:T(8,128)(2,1)S(1)} %get-tuple-element.144), channel_id=1, source_target_pairs={{0,1},{1,0},{2,3},{3,2},{4,5},{5,4},{6,7},{7,6},{8,9},{9,8},{10,11... | collective-permute-start | bytes 3145736 | tf_op jit(solution)/shard_map/ppermute | solution.py:393
  71.4 4.2 %collective-permute-start.16 = (bf16[16,128,512]{2,1,0:T(8,128)(2,1)S(1)}, bf16[16,128,512]{2,1,0:T(8,128)(2,1)S(1)}, u32[]{:S(2)}, u32[]{:S(2)}) collective-permute-start(bf16[16,128,512]{2,1,0:T(8,128)(2,1)S(1)} %get-tuple-element.146), channel_id=1, source_target_pairs={{0,1},{1,0},{2,3},{3,2},{4,5},{5,4},{6,7},{7,6},{8,9},{9,8},{10,11... | collective-permute-start | bytes 6291464 | tf_op jit(solution)/shard_map/ppermute | solution.py:393
  76.5 1.3 collective-permute-start.17
  79.1 18.5 %collective-permute-start.18 = (bf16[4,192,512]{2,1,0:T(8,128)(2,1)S(1)}, bf16[4,192,512]{2,1,0:T(8,128)(2,1)S(1)}, u32[]{:S(2)}, u32[]{:S(2)}) collective-permute-start(bf16[4,192,512]{2,1,0:T(8,128)(2,1)S(1)} %get-tuple-element.155), channel_id=1, source_target_pairs={{0,4},{1,17},{2,6},{3,19},{4,0},{5,21},{6,2},{7,23},{8,12},{9,25},... | collective-permute-start | bytes 2359304 | tf_op jit(solution)/shard_map/ppermute | solution.py:393
  81.9 18.3 %collective-permute-start.19 = (bf16[4,192,512]{2,1,0:T(8,128)(2,1)S(1)}, bf16[4,192,512]{2,1,0:T(8,128)(2,1)S(1)}, u32[]{:S(2)}, u32[]{:S(2)}) collective-permute-start(bf16[4,192,512]{2,1,0:T(8,128)(2,1)S(1)} %get-tuple-element.156), channel_id=1, source_target_pairs={{0,2},{1,9},{2,4},{3,11},{4,6},{5,13},{6,0},{7,15},{8,10},{9,17},{... | collective-permute-start | bytes 2359304 | tf_op jit(solution)/shard_map/ppermute | solution.py:393
  82.2 18.1 %collective-permute-start.20 = (bf16[4,192,512]{2,1,0:T(8,128)(2,1)S(1)}, bf16[4,192,512]{2,1,0:T(8,128)(2,1)S(1)}, u32[]{:S(2)}, u32[]{:S(2)}) collective-permute-start(bf16[4,192,512]{2,1,0:T(8,128)(2,1)S(1)} %get-tuple-element.157), channel_id=1, source_target_pairs={{0,6},{1,25},{2,0},{3,27},{4,2},{5,29},{6,4},{7,31},{8,14},{9,1},{... | collective-permute-start | bytes 2359304 | tf_op jit(solution)/shard_map/ppermute | solution.py:393
  84.6 13.0 %collective-permute-start.21 = (bf16[512,512]{1,0:T(8,128)(2,1)S(1)}, bf16[512,512]{1,0:T(8,128)(2,1)S(1)}, u32[]{:S(2)}, u32[]{:S(2)}) collective-permute-start(bf16[512,512]{1,0:T(8,128)(2,1)S(1)} %get-tuple-element.159), channel_id=1, source_target_pairs={{0,64},{32,96},{64,0},{96,32},{1,65},{33,97},{65,1},{97,33},{2,66}... | collective-permute-start | bytes 1572872 | tf_op jit(solution)/shard_map/ppermute | solution.py:393
  100.6 21.1 %collective-permute-start.22 = (bf16[4,192,512]{2,1,0:T(8,128)(2,1)S(1)}, bf16[4,192,512]{2,1,0:T(8,128)(2,1)S(1)}, u32[]{:S(2)}, u32[]{:S(2)}) collective-permute-start(bf16[4,192,512]{2,1,0:T(8,128)(2,1)S(1)} %get-tuple-element.170), channel_id=1, source_target_pairs={{0,16},{1,5},{2,18},{3,7},{4,20},{5,1},{6,22},{7,3},{8,24},{9,13},... | collective-permute-start | bytes 2359304 | tf_op jit(solution)/shard_map/ppermute | solution.py:393
  104.2 18.1 %collective-permute-start.23 = (bf16[4,192,512]{2,1,0:T(8,128)(2,1)S(1)}, bf16[4,192,512]{2,1,0:T(8,128)(2,1)S(1)}, u32[]{:S(2)}, u32[]{:S(2)}) collective-permute-start(bf16[4,192,512]{2,1,0:T(8,128)(2,1)S(1)} %get-tuple-element.171), channel_id=1, source_target_pairs={{0,8},{1,3},{2,10},{3,5},{4,12},{5,7},{6,14},{7,1},{8,16},{9,11},{... | collective-permute-start | bytes 2359304 | tf_op jit(solution)/shard_map/ppermute | solution.py:393
  104.9 18.1 %collective-permute-start.24 = (bf16[4,192,512]{2,1,0:T(8,128)(2,1)S(1)}, bf16[4,192,512]{2,1,0:T(8,128)(2,1)S(1)}, u32[]{:S(2)}, u32[]{:S(2)}) collective-permute-start(bf16[4,192,512]{2,1,0:T(8,128)(2,1)S(1)} %get-tuple-element.172), channel_id=1, source_target_pairs={{0,24},{1,7},{2,26},{3,1},{4,28},{5,3},{6,30},{7,5},{8,0},{9,15},{... | collective-permute-start | bytes 2359304 | tf_op jit(solution)/shard_map/ppermute | solution.py:393
  106.9 11.6 %collective-permute-start.25 = (bf16[512,512]{1,0:T(8,128)(2,1)S(1)}, bf16[512,512]{1,0:T(8,128)(2,1)S(1)}, u32[]{:S(2)}, u32[]{:S(2)}) collective-permute-start(bf16[512,512]{1,0:T(8,128)(2,1)S(1)} %get-tuple-element.174), channel_id=1, source_target_pairs={{0,96},{32,0},{64,32},{96,64},{1,97},{33,1},{65,33},{97,65},{2,98}... | collective-permute-start | bytes 1572872 | tf_op jit(solution)/shard_map/ppermute | solution.py:393
  109.6 12.1 %collective-permute-start.26 = (bf16[512,512]{1,0:T(8,128)(2,1)S(1)}, bf16[512,512]{1,0:T(8,128)(2,1)S(1)}, u32[]{:S(2)}, u32[]{:S(2)}) collective-permute-start(bf16[512,512]{1,0:T(8,128)(2,1)S(1)} %get-tuple-element.175), channel_id=1, source_target_pairs={{0,32},{32,64},{64,96},{96,0},{1,33},{33,65},{65,97},{97,1},{2,34}... | collective-permute-start | bytes 1572872 | tf_op jit(solution)/shard_map/ppermute | solution.py:393
  125.4 7.1 %collective-permute-start.29 = (f32[3,16,128]{2,1,0:T(8,128)S(1)}, f32[3,16,128]{2,1,0:T(8,128)S(1)}, u32[]{:S(2)}, u32[]{:S(2)}) collective-permute-start(f32[3,16,128]{2,1,0:T(8,128)S(1)} %gram.1), channel_id=1, source_target_pairs={{0,6},{1,7},{2,0},{3,1},{4,2},{5,3},{6,4},{7,5},{8,14},{9,15},{10,... | collective-permute-start | bytes 73736 | tf_op jit(solution)/shard_map/ppermute | solution.py:393
  127.8 4.7 %collective-permute-start.28 = (f32[3,16,128]{2,1,0:T(8,128)S(1)}, f32[3,16,128]{2,1,0:T(8,128)S(1)}, u32[]{:S(2)}, u32[]{:S(2)}) collective-permute-start(f32[3,16,128]{2,1,0:T(8,128)S(1)} %gram.1), channel_id=1, source_target_pairs={{0,2},{1,3},{2,4},{3,5},{4,6},{5,7},{6,0},{7,1},{8,10},{9,11},{10,... | collective-permute-start | bytes 73736 | tf_op jit(solution)/shard_map/ppermute | solution.py:393
  127.8 4.7 %collective-permute-start.27 = (f32[3,16,128]{2,1,0:T(8,128)S(1)}, f32[3,16,128]{2,1,0:T(8,128)S(1)}, u32[]{:S(2)}, u32[]{:S(2)}) collective-permute-start(f32[3,16,128]{2,1,0:T(8,128)S(1)} %gram.1), channel_id=1, source_target_pairs={{0,4},{1,5},{2,6},{3,7},{4,0},{5,1},{6,2},{7,3},{8,12},{9,13},{10,... | collective-permute-start | bytes 73736 | tf_op jit(solution)/shard_map/ppermute | solution.py:393
  132.5 11.8 %copy-start.3 = (f32[1,64,512]{2,1,0:T(8,128)S(1)}, f32[1,64,512]{2,1,0:T(8,128)}, u32[]{:S(2)}) copy-start(f32[1,64,512]{2,1,0:T(8,128)} %param.17) | copy-start | bytes 393220
  132.5 11.8 %copy-start.4 = (f32[1,64,512]{2,1,0:T(8,128)S(1)}, f32[1,64,512]{2,1,0:T(8,128)}, u32[]{:S(2)}) copy-start(f32[1,64,512]{2,1,0:T(8,128)} %param.18) | copy-start | bytes 393220
  132.5 11.8 %copy-start.5 = (f32[1,16,2048]{2,1,0:T(8,128)S(1)}, f32[1,16,2048]{2,1,0:T(8,128)}, u32[]{:S(2)}) copy-start(f32[1,16,2048]{2,1,0:T(8,128)} %param.19) | copy-start | bytes 393220
  132.5 7.2 %collective-permute-start.32 = (f32[3,16,128]{2,1,0:T(8,128)S(1)}, f32[3,16,128]{2,1,0:T(8,128)S(1)}, u32[]{:S(2)}, u32[]{:S(2)}) collective-permute-start(f32[3,16,128]{2,1,0:T(8,128)S(1)} %add_add_fusion.1), channel_id=1, source_target_pairs={{0,24},{1,25},{2,26},{3,27},{4,28},{5,29},{6,30},{7,31},{8,0},{9,1... | collective-permute-start | bytes 73736 | tf_op jit(solution)/shard_map/ppermute | solution.py:393
  135.0 4.7 %collective-permute-start.31 = (f32[3,16,128]{2,1,0:T(8,128)S(1)}, f32[3,16,128]{2,1,0:T(8,128)S(1)}, u32[]{:S(2)}, u32[]{:S(2)}) collective-permute-start(f32[3,16,128]{2,1,0:T(8,128)S(1)} %add_add_fusion.1), channel_id=1, source_target_pairs={{0,8},{1,9},{2,10},{3,11},{4,12},{5,13},{6,14},{7,15},{8,16},{9,17... | collective-permute-start | bytes 73736 | tf_op jit(solution)/shard_map/ppermute | solution.py:393
  135.0 4.7 %collective-permute-start.30 = (f32[3,16,128]{2,1,0:T(8,128)S(1)}, f32[3,16,128]{2,1,0:T(8,128)S(1)}, u32[]{:S(2)}, u32[]{:S(2)}) collective-permute-start(f32[3,16,128]{2,1,0:T(8,128)S(1)} %add_add_fusion.1), channel_id=1, source_target_pairs={{0,16},{1,17},{2,18},{3,19},{4,20},{5,21},{6,22},{7,23},{8,24},{9,... | collective-permute-start | bytes 73736 | tf_op jit(solution)/shard_map/ppermute | solution.py:393
  139.7 4.6 %collective-permute-start.33 = (f32[3,16,128]{2,1,0:T(8,128)S(1)}, f32[3,16,128]{2,1,0:T(8,128)S(1)}, u32[]{:S(2)}, u32[]{:S(2)}) collective-permute-start(f32[3,16,128]{2,1,0:T(8,128)S(1)} %add_add_fusion.g_ref), channel_id=1, source_target_pairs={{0,1},{1,0},{2,3},{3,2},{4,5},{5,4},{6,7},{7,6},{8,9},{9,8},{10,11... | collective-permute-start | bytes 73736 | tf_op jit(solution)/shard_map/ppermute | solution.py:393

commit v15 on v14

--- a/solution.py
+++ b/solution.py
@@ -568,7 +568,7 @@
     sent, slots[1], slots[3] = tie((turn_over(parts), slots[1], slots[3]))
     parts = [sent[0], *to_others(sent, 1)]
     back[1], back[3] = around_y(slots[1], 3), around_y(slots[3], 1)
-    parts, (back[1], back[3]) = tie_far(parts, (back[1], back[3]))
+    parts, back[1] = tie_far(parts, back[1])
     products, pool_grad = sum_dp(gram(parts), ids, back)
     outs = finish(
         parts,

time: 147 us -> 147 us (level)
  transfers between devices with their start and end apart: 34 -> 34, of which waited for: 17 -> 16; matrix products, arithmetic and copies ran while one was open for 0% -> 0% of each run, Pallas kernels for 19% -> 21%
where the time goes in v15:
time: 147 us; the launch traced here: 146 us
  starting transfers between devices  57 us (39%)
  waiting for transfers between devices  50.3 us (34%)
  Pallas kernels  36.2 us (25%)
  local copies, waits for them, and re-layouts  1.65 us (1%)
    ppermute x34, starting transfers between devices, shift(): lax.ppermute(block, axis, [(i, to(i)) for i in range(lax.axis_size(axis))])  57 us
    ppermute x34, waiting for transfers between devices, shift(): lax.ppermute(block, axis, [(i, to(i)) for i in range(lax.axis_size(axis))])  50.3 us
    pallas_call x6, Pallas kernels, pick_rows(): call(body, 'pick_rows', n_ids + n_pool, shapes, 2 * TOK_DEV * POOL * SLIC...  10.7 us
    pallas_call x2, Pallas kernels, scatter_rows(): pl.pallas_call(body, name='scatter_rows', grid=(steps,), out_shape=struct...  6.94 us
    pallas_call x1, Pallas kernels, forward(): call(body, 'forward', 5, shapes, 2 * TOK_DEV * D * 2 * H, 10 * MIB, [pltp...  3.02 us
  transfers between devices with their start and end apart: 34, of which 16 were waited for; matrix products, arithmetic and copies ran while one was open for 0% of the time, Pallas kernels for 21%

profile of v15, /device:TPU:1, one launch (start us, length us, event | category | flops | bytes accessed | tf_op | source)
XLA Modules:
  0.0 146.2 jit_solution(12657829424512806848)
XLA Ops:
  0.6 2.2 %collective-permute-start.2 = (s32[1,512]{1,0:T(1,128)}, s32[1,512]{1,0:T(1,128)S(1)}, u32[]{:S(2)}, u32[]{:S(2)}) collective-permute-start(s32[1,512]{1,0:T(1,128)} %refs_0_.2), channel_id=1, source_target_pairs={{0,32},{32,64},{64,96},{96,0},{1,33},{33,65},{65,97},{97,1},{2,34}... | collective-permute-start | bytes 6152 | tf_op jit(solution)/shard_map/ppermute | solution.py:393
  2.8 2.6 %collective-permute-start.1 = (s32[1,512]{1,0:T(1,128)}, s32[1,512]{1,0:T(1,128)S(1)}, u32[]{:S(2)}, u32[]{:S(2)}) collective-permute-start(s32[1,512]{1,0:T(1,128)} %refs_0_.2), channel_id=1, source_target_pairs={{0,64},{32,96},{64,0},{96,32},{1,65},{33,97},{65,1},{97,33},{2,66}... | collective-permute-start | bytes 6152 | tf_op jit(solution)/shard_map/ppermute | solution.py:393
  6.5 1.6 %copy-done.9 = bf16[2048,512]{1,0:T(8,128)(2,1)S(1)} copy-done((bf16[2048,512]{1,0:T(8,128)(2,1)S(1)}, bf16[2048,512]{1,0:T(8,128)(2,1)}, u32[]{:S(2)}) %copy-start.9) | copy-done | bytes 2097176
  8.1 1.4 pick_rows.7
  9.6 1.4 pick_rows.6
  11.5 2.3 %collective-permute-start.7 = (bf16[512,512]{1,0:T(8,128)(2,1)S(1)}, bf16[512,512]{1,0:T(8,128)(2,1)S(1)}, u32[]{:S(2)}, u32[]{:S(2)}) collective-permute-start(bf16[512,512]{1,0:T(8,128)(2,1)S(1)} %pick_rows.7), channel_id=1, source_target_pairs={{0,96},{32,0},{64,32},{96,64},{1,97},{33,1},{65,33},{97,65},{2,98}... | collective-permute-start | bytes 1572872 | tf_op jit(solution)/shard_map/ppermute | solution.py:393
  14.3 2.8 %collective-permute-start.5 = (bf16[96,1024]{1,0:T(8,128)(2,1)S(1)}, bf16[96,1024]{1,0:T(8,128)(2,1)S(1)}, u32[]{:S(2)}, u32[]{:S(2)}) collective-permute-start(bf16[96,1024]{1,0:T(8,128)(2,1)S(1)} %pack.1.refs_0_), channel_id=1, source_target_pairs={{0,4},{1,17},{2,6},{3,19},{4,0},{5,21},{6,2},{7,23},{8,12},{9,25},... | collective-permute-start | bytes 589832 | tf_op jit(solution)/shard_map/ppermute | solution.py:393
  17.5 2.3 %collective-permute-start.3 = (bf16[96,1024]{1,0:T(8,128)(2,1)S(1)}, bf16[96,1024]{1,0:T(8,128)(2,1)S(1)}, u32[]{:S(2)}, u32[]{:S(2)}) collective-permute-start(bf16[96,1024]{1,0:T(8,128)(2,1)S(1)} %pack.1.refs_0_), channel_id=1, source_target_pairs={{0,6},{1,25},{2,0},{3,27},{4,2},{5,29},{6,4},{7,31},{8,14},{9,1},{... | collective-permute-start | bytes 589832 | tf_op jit(solution)/shard_map/ppermute | solution.py:393
  19.8 2.5 %pick_rows.8 = bf16[1024,512]{1,0:T(8,128)(2,1)S(1)} custom-call(s32[1,512]{1,0:T(1,128)S(1)} %collective-permute-done.1.refs_0_.refs_2_, bf16[2048,512]{1,0:T(8,128)(2,1)S(1)} %copy-done.9, bf16[2048,512]{1,0:T(8,128)(2,1)S(1)} %copy-done.8), custom_call_target="tpu_custom_call" | custom-call | flops 2147483648 | bytes 3145728 | tf_op jit(solution)/shard_map/pick_rows/pallas_call | solution.py:73
  24.7 3.7 %collective-permute-start.10 = (bf16[4,96,1024]{2,1,0:T(8,128)(2,1)S(1)}, bf16[4,96,1024]{2,1,0:T(8,128)(2,1)S(1)}, u32[]{:S(2)}, u32[]{:S(2)}) collective-permute-start(bf16[4,96,1024]{2,1,0:T(8,128)(2,1)S(1)} %bundle.1.refs_0_), channel_id=1, source_target_pairs={{0,16},{1,5},{2,18},{3,7},{4,20},{5,1},{6,22},{7,3},{8,24},{9,13},... | collective-permute-start | bytes 2359304 | tf_op jit(solution)/shard_map/ppermute | solution.py:393
  29.2 1.9 %collective-permute-start.8 = (bf16[4,96,1024]{2,1,0:T(8,128)(2,1)S(1)}, bf16[4,96,1024]{2,1,0:T(8,128)(2,1)S(1)}, u32[]{:S(2)}, u32[]{:S(2)}) collective-permute-start(bf16[4,96,1024]{2,1,0:T(8,128)(2,1)S(1)} %bundle.1.refs_0_), channel_id=1, source_target_pairs={{0,24},{1,7},{2,26},{3,1},{4,28},{5,3},{6,30},{7,5},{8,0},{9,15},{... | collective-permute-start | bytes 2359304 | tf_op jit(solution)/shard_map/ppermute | solution.py:393
  31.1 1.4 pick_rows.10
  32.6 1.4 pick_rows.11
  34.0 2.5 %pick_rows.9 = (bf16[512,512]{1,0:T(8,128)(2,1)S(1)}, bf16[512,512]{1,0:T(8,128)(2,1)S(1)}) custom-call(s32[1,512]{1,0:T(1,128)S(1)} %copy-done.7, bf16[2048,512]{1,0:T(8,128)(2,1)S(1)} %copy-done.9, bf16[2048,512]{1,0:T(8,128)(2,1)S(1)} %copy-done.8), custom_call_target="tpu_custom_call" | custom-call | flops 2147483648 | bytes 3145728 | tf_op jit(solution)/shard_map/pick_rows/pallas_call | solution.py:73
  36.5 1.6 %collective-permute-done.10.refs_2_ = bf16[4,96,1024]{2,1,0:T(8,128)(2,1)S(1)} collective-permute-done((bf16[4,96,1024]{2,1,0:T(8,128)(2,1)S(1)}, bf16[4,96,1024]{2,1,0:T(8,128)(2,1)S(1)}, u32[]{:S(2)}, u32[]{:S(2)}) %collective-permute-start.10) | collective-permute-done | bytes 786464 | tf_op jit(solution)/shard_map/ppermute | solution.py:393
  38.1 8.4 %collective-permute-done.9.refs_1_ = bf16[4,96,1024]{2,1,0:T(8,128)(2,1)S(1)} collective-permute-done((bf16[4,96,1024]{2,1,0:T(8,128)(2,1)S(1)}, bf16[4,96,1024]{2,1,0:T(8,128)(2,1)S(1)}, u32[]{:S(2)}, u32[]{:S(2)}) %collective-permute-start.9) | collective-permute-done | bytes 786464 | tf_op jit(solution)/shard_map/ppermute | solution.py:393
  47.5 4.2 %collective-permute-start.14 = (bf16[16,96,1024]{2,1,0:T(8,128)(2,1)S(1)}, bf16[16,96,1024]{2,1,0:T(8,128)(2,1)S(1)}, u32[]{:S(2)}, u32[]{:S(2)}) collective-permute-start(bf16[16,96,1024]{2,1,0:T(8,128)(2,1)S(1)} %half_of_weights.1.a), channel_id=1, source_target_pairs={{0,1},{1,0},{2,3},{3,2},{4,5},{5,4},{6,7},{7,6},{8,9},{9,8},{10,11... | collective-permute-start | bytes 9437192 | tf_op jit(solution)/shard_map/ppermute | solution.py:393
  51.8 1.1 collective-permute-start.12
  52.9 1.5 %collective-permute-start.13 = (bf16[512,512]{1,0:T(8,128)(2,1)S(1)}, bf16[512,512]{1,0:T(8,128)(2,1)S(1)}, u32[]{:S(2)}, u32[]{:S(2)}) collective-permute-start(bf16[512,512]{1,0:T(8,128)(2,1)S(1)} %pick_rows.11), channel_id=1, source_target_pairs={{0,96},{32,0},{64,32},{96,64},{1,97},{33,1},{65,33},{97,65},{2,98}... | collective-permute-start | bytes 1572872 | tf_op jit(solution)/shard_map/ppermute | solution.py:393
  54.4 2.6 %collective-permute-done.14.b = bf16[16,96,1024]{2,1,0:T(8,128)(2,1)S(1)} collective-permute-done((bf16[16,96,1024]{2,1,0:T(8,128)(2,1)S(1)}, bf16[16,96,1024]{2,1,0:T(8,128)(2,1)S(1)}, u32[]{:S(2)}, u32[]{:S(2)}) %collective-permute-start.14) | collective-permute-done | bytes 3145760 | tf_op jit(solution)/shard_map/ppermute | solution.py:393
  57.5 3.0 %forward.1 = (bf16[512,512]{1,0:T(8,128)(2,1)S(1)}, f32[512,512]{1,0:T(8,128)S(1)}, f32[512,512]{1,0:T(8,128)S(1)}, bf16[4,512,512]{2,1,0:T(8,128)(2,1)S(1)}) custom-call(bf16[512,512]{1,0:T(8,128)(2,1)S(1)} %get-tuple-element.125.x0, bf16[512,512]{1,0:T(8,128)(2,1)S(1)} %collective-permute-done.6.x1, bf16[1024,512]{1,0:T(8,128)(2,1)S(1)} %collective-permute-done.11.x2.c2, ...), custom_call_target="tpu_custom_call" | custom-call | flops 2147483648 | bytes 10485760 | tf_op jit(solution)/shard_map/forward/pallas_call | solution.py:127
  60.5 1.4 backward_early.1
  62.0 4.5 %collective-permute-done.12.c1 = bf16[512,512]{1,0:T(8,128)(2,1)S(1)} collective-permute-done((bf16[512,512]{1,0:T(8,128)(2,1)S(1)}, bf16[512,512]{1,0:T(8,128)(2,1)S(1)}, u32[]{:S(2)}, u32[]{:S(2)}) %collective-permute-start.12) | collective-permute-done | bytes 524320 | tf_op jit(solution)/shard_map/ppermute | solution.py:393
  66.5 1.5 %backward_down.1 = (bf16[16,64,512]{2,1,0:T(8,128)(2,1)S(1)}, bf16[16,64,512]{2,1,0:T(8,128)(2,1)S(1)}, f32[512,512]{1,0:T(8,128)S(1)}) custom-call(bf16[512,512]{1,0:T(8,128)(2,1)S(1)} %collective-permute-done.12.c1, bf16[512,512]{1,0:T(8,128)(2,1)S(1)} %collective-permute-done.13.c3, f32[1,512]{1,0:T(1,128)S(1)} %copy-done.6, ...), custom_call_target="tpu_custom_call" | custom-call | flops 1073741824 | bytes 10485760 | tf_op jit(solution)/shard_map/backward_down/pallas_call | solution.py:186
  68.9 2.5 %backward_in.1 = (bf16[16,128,512]{2,1,0:T(8,128)(2,1)S(1)}, bf16[16,128,512]{2,1,0:T(8,128)(2,1)S(1)}, bf16[512,1024]{1,0:T(8,128)(2,1)S(1)}) custom-call(f32[512,512]{1,0:T(8,128)S(1)} %get-tuple-element.137.hg, f32[512,512]{1,0:T(8,128)S(1)} %get-tuple-element.138.factor, f32[512,512]{1,0:T(8,128)S(1)} %get-tuple-element.139.act_ref, ...), custom_call_target="tpu_custom_call" | custom-call | flops 2147483648 | bytes 10485760 | tf_op jit(solution)/shard_map/backward_in/pallas_call | solution.py:214
  71.6 2.4 %slot_gradients.1 = (bf16[512,512]{1,0:T(8,128)(2,1)S(1)}, bf16[512,512]{1,0:T(8,128)(2,1)S(1)}, bf16[512,512]{1,0:T(8,128)(2,1)S(1)}, bf16[512,512]{1,0:T(8,128)(2,1)S(1)}) custom-call(bf16[512,1024]{1,0:T(8,128)(2,1)S(1)} %get-tuple-element.147.both_ref, bf16[32,96,1024]{2,1,0:T(8,128)(2,1)S(1)} %whole_weights.1.w), custom_call_target="tpu_custom_call" | custom-call | flops 2147483648 | bytes 9437184 | tf_op jit(solution)/shard_map/slot_gradients/pallas_call | solution.py:224
  73.9 1.8 %collective-permute-done.16.b_in = bf16[16,128,512]{2,1,0:T(8,128)(2,1)S(1)} collective-permute-done((bf16[16,128,512]{2,1,0:T(8,128)(2,1)S(1)}, bf16[16,128,512]{2,1,0:T(8,128)(2,1)S(1)}, u32[]{:S(2)}, u32[]{:S(2)}) %collective-permute-start.16) | collective-permute-done | bytes 2097184 | tf_op jit(solution)/shard_map/ppermute | solution.py:393
  76.7 1.1 collective-permute-done.17.t_ref
  77.8 1.3 pair_merge.1
  79.1 2.8 %collective-permute-start.18 = (bf16[4,192,512]{2,1,0:T(8,128)(2,1)S(1)}, bf16[4,192,512]{2,1,0:T(8,128)(2,1)S(1)}, u32[]{:S(2)}, u32[]{:S(2)}) collective-permute-start(bf16[4,192,512]{2,1,0:T(8,128)(2,1)S(1)} %get-tuple-element.154), channel_id=1, source_target_pairs={{0,4},{1,17},{2,6},{3,19},{4,0},{5,21},{6,2},{7,23},{8,12},{9,25},... | collective-permute-start | bytes 2359304 | tf_op jit(solution)/shard_map/ppermute | solution.py:393
  82.2 2.3 %collective-permute-start.20 = (bf16[4,192,512]{2,1,0:T(8,128)(2,1)S(1)}, bf16[4,192,512]{2,1,0:T(8,128)(2,1)S(1)}, u32[]{:S(2)}, u32[]{:S(2)}) collective-permute-start(bf16[4,192,512]{2,1,0:T(8,128)(2,1)S(1)} %get-tuple-element.156), channel_id=1, source_target_pairs={{0,6},{1,25},{2,0},{3,27},{4,2},{5,29},{6,4},{7,31},{8,14},{9,1},{... | collective-permute-start | bytes 2359304 | tf_op jit(solution)/shard_map/ppermute | solution.py:393
  84.6 2.4 %collective-permute-start.21 = (bf16[512,512]{1,0:T(8,128)(2,1)S(1)}, bf16[512,512]{1,0:T(8,128)(2,1)S(1)}, u32[]{:S(2)}, u32[]{:S(2)}) collective-permute-start(bf16[512,512]{1,0:T(8,128)(2,1)S(1)} %get-tuple-element.158), channel_id=1, source_target_pairs={{0,64},{32,96},{64,0},{96,32},{1,65},{33,97},{65,1},{97,33},{2,66}... | collective-permute-start | bytes 1572872 | tf_op jit(solution)/shard_map/ppermute | solution.py:393
  86.9 10.7 %collective-permute-done.21.refs_6_ = bf16[512,512]{1,0:T(8,128)(2,1)S(1)} collective-permute-done((bf16[512,512]{1,0:T(8,128)(2,1)S(1)}, bf16[512,512]{1,0:T(8,128)(2,1)S(1)}, u32[]{:S(2)}, u32[]{:S(2)}) %collective-permute-start.21) | collective-permute-done | bytes 524320 | tf_op jit(solution)/shard_map/ppermute | solution.py:393
  97.6 2.6 %collective-permute-done.19.refs_1_ = bf16[4,192,512]{2,1,0:T(8,128)(2,1)S(1)} collective-permute-done((bf16[4,192,512]{2,1,0:T(8,128)(2,1)S(1)}, bf16[4,192,512]{2,1,0:T(8,128)(2,1)S(1)}, u32[]{:S(2)}, u32[]{:S(2)}) %collective-permute-start.19) | collective-permute-done | bytes 786464 | tf_op jit(solution)/shard_map/ppermute | solution.py:393
  100.6 3.7 %collective-permute-start.22 = (bf16[4,192,512]{2,1,0:T(8,128)(2,1)S(1)}, bf16[4,192,512]{2,1,0:T(8,128)(2,1)S(1)}, u32[]{:S(2)}, u32[]{:S(2)}) collective-permute-start(bf16[4,192,512]{2,1,0:T(8,128)(2,1)S(1)} %get-tuple-element.169), channel_id=1, source_target_pairs={{0,16},{1,5},{2,18},{3,7},{4,20},{5,1},{6,22},{7,3},{8,24},{9,13},... | collective-permute-start | bytes 2359304 | tf_op jit(solution)/shard_map/ppermute | solution.py:393
  104.9 2.0 %collective-permute-start.24 = (bf16[4,192,512]{2,1,0:T(8,128)(2,1)S(1)}, bf16[4,192,512]{2,1,0:T(8,128)(2,1)S(1)}, u32[]{:S(2)}, u32[]{:S(2)}) collective-permute-start(bf16[4,192,512]{2,1,0:T(8,128)(2,1)S(1)} %get-tuple-element.171), channel_id=1, source_target_pairs={{0,24},{1,7},{2,26},{3,1},{4,28},{5,3},{6,30},{7,5},{8,0},{9,15},{... | collective-permute-start | bytes 2359304 | tf_op jit(solution)/shard_map/ppermute | solution.py:393
  106.9 2.7 %collective-permute-start.25 = (bf16[512,512]{1,0:T(8,128)(2,1)S(1)}, bf16[512,512]{1,0:T(8,128)(2,1)S(1)}, u32[]{:S(2)}, u32[]{:S(2)}) collective-permute-start(bf16[512,512]{1,0:T(8,128)(2,1)S(1)} %get-tuple-element.173), channel_id=1, source_target_pairs={{0,96},{32,0},{64,32},{96,64},{1,97},{33,1},{65,33},{97,65},{2,98}... | collective-permute-start | bytes 1572872 | tf_op jit(solution)/shard_map/ppermute | solution.py:393
  109.6 8.9 %collective-permute-done.25.refs_5_ = bf16[512,512]{1,0:T(8,128)(2,1)S(1)} collective-permute-done((bf16[512,512]{1,0:T(8,128)(2,1)S(1)}, bf16[512,512]{1,0:T(8,128)(2,1)S(1)}, u32[]{:S(2)}, u32[]{:S(2)}) %collective-permute-start.25) | collective-permute-done | bytes 524320 | tf_op jit(solution)/shard_map/ppermute | solution.py:393
  118.5 3.8 %collective-permute-done.23.refs_1_.x1 = bf16[4,192,512]{2,1,0:T(8,128)(2,1)S(1)} collective-permute-done((bf16[4,192,512]{2,1,0:T(8,128)(2,1)S(1)}, bf16[4,192,512]{2,1,0:T(8,128)(2,1)S(1)}, u32[]{:S(2)}, u32[]{:S(2)}) %collective-permute-start.23) | collective-permute-done | bytes 786464 | tf_op jit(solution)/shard_map/ppermute | solution.py:393
  123.1 2.3 %gram.1 = f32[3,16,128]{2,1,0:T(8,128)S(1)} custom-call(bf16[4,192,512]{2,1,0:T(8,128)(2,1)S(1)} %get-tuple-element.174.refs_0_.x0, bf16[4,192,512]{2,1,0:T(8,128)(2,1)S(1)} %collective-permute-done.23.refs_1_.x1, bf16[4,192,512]{2,1,0:T(8,128)(2,1)S(1)} %collective-permute-done.22.refs_2_.x2, bf16[4,192,512]{2,1,0:T(8,128)(2,1)S(1)} %collective-permute-done.24.refs_3_.x3), custom_call_target="tpu_custom_call" | custom-call | flops 805306368 | bytes 3145728 | tf_op jit(solution)/shard_map/gram/pallas_call | solution.py:315
  125.4 2.4 %collective-permute-start.28 = (f32[3,16,128]{2,1,0:T(8,128)S(1)}, f32[3,16,128]{2,1,0:T(8,128)S(1)}, u32[]{:S(2)}, u32[]{:S(2)}) collective-permute-start(f32[3,16,128]{2,1,0:T(8,128)S(1)} %gram.1), channel_id=1, source_target_pairs={{0,6},{1,7},{2,0},{3,1},{4,2},{5,3},{6,4},{7,5},{8,14},{9,15},{10,... | collective-permute-start | bytes 73736 | tf_op jit(solution)/shard_map/ppermute | solution.py:393
  127.8 1.2 collective-permute-start.26
  129.0 3.5 %scatter_rows.2.refs_8_ = f32[2048,512]{1,0:T(8,128)} custom-call(s32[1,512]{1,0:T(1,128)S(1)} %copy-done.7, s32[1,512]{1,0:T(1,128)S(1)} %collective-permute-done.refs_0_.refs_1_, s32[1,512]{1,0:T(1,128)S(1)} %collective-permute-done.1.refs_0_.refs_2_, s32[1,512]{1,0:T(1,128)S(1)} %collective-permute-done.2.refs_0_.refs_3_, ...), custom_call_target="tpu_custom_call" | custom-call | flops 2147483648 | bytes 4194304 | tf_op jit(solution)/shard_map/scatter_rows/pallas_call | solution.py:379
  132.6 2.4 %collective-permute-start.32 = (f32[3,16,128]{2,1,0:T(8,128)S(1)}, f32[3,16,128]{2,1,0:T(8,128)S(1)}, u32[]{:S(2)}, u32[]{:S(2)}) collective-permute-start(f32[3,16,128]{2,1,0:T(8,128)S(1)} %add_add_fusion.1), channel_id=1, source_target_pairs={{0,24},{1,25},{2,26},{3,27},{4,28},{5,29},{6,30},{7,31},{8,0},{9,1... | collective-permute-start | bytes 73736 | tf_op jit(solution)/shard_map/ppermute | solution.py:393
  135.0 1.3 collective-permute-start.30
  136.2 3.5 %scatter_rows.3 = f32[2048,512]{1,0:T(8,128)} custom-call(s32[1,512]{1,0:T(1,128)S(1)} %copy-done.7, s32[1,512]{1,0:T(1,128)S(1)} %collective-permute-done.refs_0_.refs_1_, s32[1,512]{1,0:T(1,128)S(1)} %collective-permute-done.1.refs_0_.refs_2_, s32[1,512]{1,0:T(1,128)S(1)} %collective-permute-done.2.refs_0_.refs_3_, ...), custom_call_target="tpu_custom_call", output_to_operand_aliasing={{}: (8, {})} | custom-call | flops 2147483648 | bytes 4194304 | tf_op jit(solution)/shard_map/scatter_rows/pallas_call | solution.py:379
  139.7 3.7 %collective-permute-start.33 = (f32[3,16,128]{2,1,0:T(8,128)S(1)}, f32[3,16,128]{2,1,0:T(8,128)S(1)}, u32[]{:S(2)}, u32[]{:S(2)}) collective-permute-start(f32[3,16,128]{2,1,0:T(8,128)S(1)} %add_add_fusion.g_ref), channel_id=1, source_target_pairs={{0,1},{1,0},{2,3},{3,2},{4,5},{5,4},{6,7},{7,6},{8,9},{9,8},{10,11... | collective-permute-start | bytes 73736 | tf_op jit(solution)/shard_map/ppermute | solution.py:393
  144.3 1.8 %finish.1 = (f32[64,512]{1,0:T(8,128)}, f32[64,512]{1,0:T(8,128)}, f32[16,2048]{1,0:T(8,128)}, f32[64,512]{1,0:T(8,128)}, f32[64,512]{1,0:T(8,128)}, /*index=5*/f32[16,2048]{1,0:T(8,128)}) custom-call(bf16[4,192,512]{2,1,0:T(8,128)(2,1)S(1)} %get-tuple-element.174.refs_0_.x0, bf16[4,192,512]{2,1,0:T(8,128)(2,1)S(1)} %collective-permute-done.23.refs_1_.x1, ...), custom_call_target="tpu_custom_call" | custom-call | flops 4194304 | bytes 6291456 | tf_op jit(solution)/shard_map/finish/pallas_call | solution.py:361
  (64 shorter events, 12.2 us)
Async XLA Ops:
  0.6 5.9 %collective-permute-start.2 = (s32[1,512]{1,0:T(1,128)}, s32[1,512]{1,0:T(1,128)S(1)}, u32[]{:S(2)}, u32[]{:S(2)}) collective-permute-start(s32[1,512]{1,0:T(1,128)} %refs_0_.2), channel_id=1, source_target_pairs={{0,32},{32,64},{64,96},{96,0},{1,33},{33,65},{65,97},{97,1},{2,34}... | collective-permute-start | bytes 6152 | tf_op jit(solution)/shard_map/ppermute | solution.py:393
  2.8 8.2 %collective-permute-start.1 = (s32[1,512]{1,0:T(1,128)}, s32[1,512]{1,0:T(1,128)S(1)}, u32[]{:S(2)}, u32[]{:S(2)}) collective-permute-start(s32[1,512]{1,0:T(1,128)} %refs_0_.2), channel_id=1, source_target_pairs={{0,64},{32,96},{64,0},{96,32},{1,65},{33,97},{65,1},{97,33},{2,66}... | collective-permute-start | bytes 6152 | tf_op jit(solution)/shard_map/ppermute | solution.py:393
  5.4 4.1 %collective-permute-start = (s32[1,512]{1,0:T(1,128)}, s32[1,512]{1,0:T(1,128)S(1)}, u32[]{:S(2)}, u32[]{:S(2)}) collective-permute-start(s32[1,512]{1,0:T(1,128)} %refs_0_.2), channel_id=1, source_target_pairs={{0,96},{32,0},{64,32},{96,64},{1,97},{33,1},{65,33},{97,65},{2,98}... | collective-permute-start | bytes 6152 | tf_op jit(solution)/shard_map/ppermute | solution.py:393
  6.5 1.6 %copy-start.9 = (bf16[2048,512]{1,0:T(8,128)(2,1)S(1)}, bf16[2048,512]{1,0:T(8,128)(2,1)}, u32[]{:S(2)}) copy-start(bf16[2048,512]{1,0:T(8,128)(2,1)} %refs_1_.9) | copy-start | bytes 6291460
  9.5 4.2 %copy-start = (f32[1,64,512]{2,1,0:T(8,128)S(1)}, f32[1,64,512]{2,1,0:T(8,128)}, u32[]{:S(2)}) copy-start(f32[1,64,512]{2,1,0:T(8,128)} %param.14) | copy-start | bytes 393220
  9.5 4.2 %copy-start.1 = (f32[1,64,512]{2,1,0:T(8,128)S(1)}, f32[1,64,512]{2,1,0:T(8,128)}, u32[]{:S(2)}) copy-start(f32[1,64,512]{2,1,0:T(8,128)} %param.15) | copy-start | bytes 393220
  9.5 4.2 %copy-start.2 = (f32[1,16,2048]{2,1,0:T(8,128)S(1)}, f32[1,16,2048]{2,1,0:T(8,128)}, u32[]{:S(2)}) copy-start(f32[1,16,2048]{2,1,0:T(8,128)} %param.16) | copy-start | bytes 393220
  9.6 10.3 %copy-start.8 = (bf16[2048,512]{1,0:T(8,128)(2,1)S(1)}, bf16[2048,512]{1,0:T(8,128)(2,1)}, u32[]{:S(2)}) copy-start(bf16[2048,512]{1,0:T(8,128)(2,1)} %refs_1_.11) | copy-start | bytes 6291460
  11.0 13.2 %collective-permute-start.6 = (bf16[512,512]{1,0:T(8,128)(2,1)S(1)}, bf16[512,512]{1,0:T(8,128)(2,1)S(1)}, u32[]{:S(2)}, u32[]{:S(2)}) collective-permute-start(bf16[512,512]{1,0:T(8,128)(2,1)S(1)} %pick_rows.6), channel_id=1, source_target_pairs={{0,32},{32,64},{64,96},{96,0},{1,33},{33,65},{65,97},{97,1},{2,34}... | collective-permute-start | bytes 1572872 | tf_op jit(solution)/shard_map/ppermute | solution.py:393
  11.5 12.7 %collective-permute-start.7 = (bf16[512,512]{1,0:T(8,128)(2,1)S(1)}, bf16[512,512]{1,0:T(8,128)(2,1)S(1)}, u32[]{:S(2)}, u32[]{:S(2)}) collective-permute-start(bf16[512,512]{1,0:T(8,128)(2,1)S(1)} %pick_rows.7), channel_id=1, source_target_pairs={{0,96},{32,0},{64,32},{96,64},{1,97},{33,1},{65,33},{97,65},{2,98}... | collective-permute-start | bytes 1572872 | tf_op jit(solution)/shard_map/ppermute | solution.py:393
  14.3 8.0 %collective-permute-start.5 = (bf16[96,1024]{1,0:T(8,128)(2,1)S(1)}, bf16[96,1024]{1,0:T(8,128)(2,1)S(1)}, u32[]{:S(2)}, u32[]{:S(2)}) collective-permute-start(bf16[96,1024]{1,0:T(8,128)(2,1)S(1)} %pack.1.refs_0_), channel_id=1, source_target_pairs={{0,4},{1,17},{2,6},{3,19},{4,0},{5,21},{6,2},{7,23},{8,12},{9,25},... | collective-permute-start | bytes 589832 | tf_op jit(solution)/shard_map/ppermute | solution.py:393
  17.1 6.0 %collective-permute-start.4 = (bf16[96,1024]{1,0:T(8,128)(2,1)S(1)}, bf16[96,1024]{1,0:T(8,128)(2,1)S(1)}, u32[]{:S(2)}, u32[]{:S(2)}) collective-permute-start(bf16[96,1024]{1,0:T(8,128)(2,1)S(1)} %pack.1.refs_0_), channel_id=1, source_target_pairs={{0,2},{1,9},{2,4},{3,11},{4,6},{5,13},{6,0},{7,15},{8,10},{9,17},{... | collective-permute-start | bytes 589832 | tf_op jit(solution)/shard_map/ppermute | solution.py:393
  17.5 5.7 %collective-permute-start.3 = (bf16[96,1024]{1,0:T(8,128)(2,1)S(1)}, bf16[96,1024]{1,0:T(8,128)(2,1)S(1)}, u32[]{:S(2)}, u32[]{:S(2)}) collective-permute-start(bf16[96,1024]{1,0:T(8,128)(2,1)S(1)} %pack.1.refs_0_), channel_id=1, source_target_pairs={{0,6},{1,25},{2,0},{3,27},{4,2},{5,29},{6,4},{7,31},{8,14},{9,1},{... | collective-permute-start | bytes 589832 | tf_op jit(solution)/shard_map/ppermute | solution.py:393
  24.2 23.1 %collective-permute-start.11 = (bf16[1024,512]{1,0:T(8,128)(2,1)S(1)}, bf16[1024,512]{1,0:T(8,128)(2,1)S(1)}, u32[]{:S(2)}, u32[]{:S(2)}) collective-permute-start(bf16[1024,512]{1,0:T(8,128)(2,1)S(1)} %pick_rows.8), channel_id=1, source_target_pairs={{0,64},{32,96},{64,0},{96,32},{1,65},{33,97},{65,1},{97,33},{2,66}... | collective-permute-start | bytes 3145736 | tf_op jit(solution)/shard_map/ppermute | solution.py:393
  24.7 13.5 %collective-permute-start.10 = (bf16[4,96,1024]{2,1,0:T(8,128)(2,1)S(1)}, bf16[4,96,1024]{2,1,0:T(8,128)(2,1)S(1)}, u32[]{:S(2)}, u32[]{:S(2)}) collective-permute-start(bf16[4,96,1024]{2,1,0:T(8,128)(2,1)S(1)} %bundle.1.refs_0_), channel_id=1, source_target_pairs={{0,16},{1,5},{2,18},{3,7},{4,20},{5,1},{6,22},{7,3},{8,24},{9,13},... | collective-permute-start | bytes 2359304 | tf_op jit(solution)/shard_map/ppermute | solution.py:393
  28.4 18.1 %collective-permute-start.9 = (bf16[4,96,1024]{2,1,0:T(8,128)(2,1)S(1)}, bf16[4,96,1024]{2,1,0:T(8,128)(2,1)S(1)}, u32[]{:S(2)}, u32[]{:S(2)}) collective-permute-start(bf16[4,96,1024]{2,1,0:T(8,128)(2,1)S(1)} %bundle.1.refs_0_), channel_id=1, source_target_pairs={{0,8},{1,3},{2,10},{3,5},{4,12},{5,7},{6,14},{7,1},{8,16},{9,11},{... | collective-permute-start | bytes 2359304 | tf_op jit(solution)/shard_map/ppermute | solution.py:393
  29.2 18.1 %collective-permute-start.8 = (bf16[4,96,1024]{2,1,0:T(8,128)(2,1)S(1)}, bf16[4,96,1024]{2,1,0:T(8,128)(2,1)S(1)}, u32[]{:S(2)}, u32[]{:S(2)}) collective-permute-start(bf16[4,96,1024]{2,1,0:T(8,128)(2,1)S(1)} %bundle.1.refs_0_), channel_id=1, source_target_pairs={{0,24},{1,7},{2,26},{3,1},{4,28},{5,3},{6,30},{7,5},{8,0},{9,15},{... | collective-permute-start | bytes 2359304 | tf_op jit(solution)/shard_map/ppermute | solution.py:393
  32.5 1.5 %copy-start.7 = (s32[1,512]{1,0:T(1,128)S(1)}, s32[1,512]{1,0:T(1,128)}, u32[]{:S(2)}) copy-start(s32[1,512]{1,0:T(1,128)} %refs_0_.2) | copy-start | bytes 6148
  47.5 9.5 %collective-permute-start.14 = (bf16[16,96,1024]{2,1,0:T(8,128)(2,1)S(1)}, bf16[16,96,1024]{2,1,0:T(8,128)(2,1)S(1)}, u32[]{:S(2)}, u32[]{:S(2)}) collective-permute-start(bf16[16,96,1024]{2,1,0:T(8,128)(2,1)S(1)} %half_of_weights.1.a), channel_id=1, source_target_pairs={{0,1},{1,0},{2,3},{3,2},{4,5},{5,4},{6,7},{7,6},{8,9},{9,8},{10,11... | collective-permute-start | bytes 9437192 | tf_op jit(solution)/shard_map/ppermute | solution.py:393
  51.8 14.7 %collective-permute-start.12 = (bf16[512,512]{1,0:T(8,128)(2,1)S(1)}, bf16[512,512]{1,0:T(8,128)(2,1)S(1)}, u32[]{:S(2)}, u32[]{:S(2)}) collective-permute-start(bf16[512,512]{1,0:T(8,128)(2,1)S(1)} %pick_rows.10), channel_id=1, source_target_pairs={{0,32},{32,64},{64,96},{96,0},{1,33},{33,65},{65,97},{97,1},{2,34}... | collective-permute-start | bytes 1572872 | tf_op jit(solution)/shard_map/ppermute | solution.py:393
  52.9 13.6 %collective-permute-start.13 = (bf16[512,512]{1,0:T(8,128)(2,1)S(1)}, bf16[512,512]{1,0:T(8,128)(2,1)S(1)}, u32[]{:S(2)}, u32[]{:S(2)}) collective-permute-start(bf16[512,512]{1,0:T(8,128)(2,1)S(1)} %pick_rows.11), channel_id=1, source_target_pairs={{0,96},{32,0},{64,32},{96,64},{1,97},{33,1},{65,33},{97,65},{2,98}... | collective-permute-start | bytes 1572872 | tf_op jit(solution)/shard_map/ppermute | solution.py:393
  57.5 3.0 %copy-start.6 = (f32[1,512]{1,0:T(1,128)S(1)}, f32[1,512]{1,0:T(1,128)}, u32[]{:S(2)}) copy-start(f32[1,512]{1,0:T(1,128)} %route_ref.3) | copy-start | bytes 6148
  68.0 3.5 %collective-permute-start.15 = (bf16[16,64,512]{2,1,0:T(8,128)(2,1)S(1)}, bf16[16,64,512]{2,1,0:T(8,128)(2,1)S(1)}, u32[]{:S(2)}, u32[]{:S(2)}) collective-permute-start(bf16[16,64,512]{2,1,0:T(8,128)(2,1)S(1)} %get-tuple-element.143), channel_id=1, source_target_pairs={{0,1},{1,0},{2,3},{3,2},{4,5},{5,4},{6,7},{7,6},{8,9},{9,8},{10,11... | collective-permute-start | bytes 3145736 | tf_op jit(solution)/shard_map/ppermute | solution.py:393
  71.4 4.2 %collective-permute-start.16 = (bf16[16,128,512]{2,1,0:T(8,128)(2,1)S(1)}, bf16[16,128,512]{2,1,0:T(8,128)(2,1)S(1)}, u32[]{:S(2)}, u32[]{:S(2)}) collective-permute-start(bf16[16,128,512]{2,1,0:T(8,128)(2,1)S(1)} %get-tuple-element.145), channel_id=1, source_target_pairs={{0,1},{1,0},{2,3},{3,2},{4,5},{5,4},{6,7},{7,6},{8,9},{9,8},{10,11... | collective-permute-start | bytes 6291464 | tf_op jit(solution)/shard_map/ppermute | solution.py:393
  76.5 1.3 collective-permute-start.17
  79.1 18.5 %collective-permute-start.18 = (bf16[4,192,512]{2,1,0:T(8,128)(2,1)S(1)}, bf16[4,192,512]{2,1,0:T(8,128)(2,1)S(1)}, u32[]{:S(2)}, u32[]{:S(2)}) collective-permute-start(bf16[4,192,512]{2,1,0:T(8,128)(2,1)S(1)} %get-tuple-element.154), channel_id=1, source_target_pairs={{0,4},{1,17},{2,6},{3,19},{4,0},{5,21},{6,2},{7,23},{8,12},{9,25},... | collective-permute-start | bytes 2359304 | tf_op jit(solution)/shard_map/ppermute | solution.py:393
  81.9 18.3 %collective-permute-start.19 = (bf16[4,192,512]{2,1,0:T(8,128)(2,1)S(1)}, bf16[4,192,512]{2,1,0:T(8,128)(2,1)S(1)}, u32[]{:S(2)}, u32[]{:S(2)}) collective-permute-start(bf16[4,192,512]{2,1,0:T(8,128)(2,1)S(1)} %get-tuple-element.155), channel_id=1, source_target_pairs={{0,2},{1,9},{2,4},{3,11},{4,6},{5,13},{6,0},{7,15},{8,10},{9,17},{... | collective-permute-start | bytes 2359304 | tf_op jit(solution)/shard_map/ppermute | solution.py:393
  82.2 18.1 %collective-permute-start.20 = (bf16[4,192,512]{2,1,0:T(8,128)(2,1)S(1)}, bf16[4,192,512]{2,1,0:T(8,128)(2,1)S(1)}, u32[]{:S(2)}, u32[]{:S(2)}) collective-permute-start(bf16[4,192,512]{2,1,0:T(8,128)(2,1)S(1)} %get-tuple-element.156), channel_id=1, source_target_pairs={{0,6},{1,25},{2,0},{3,27},{4,2},{5,29},{6,4},{7,31},{8,14},{9,1},{... | collective-permute-start | bytes 2359304 | tf_op jit(solution)/shard_map/ppermute | solution.py:393
  84.6 13.0 %collective-permute-start.21 = (bf16[512,512]{1,0:T(8,128)(2,1)S(1)}, bf16[512,512]{1,0:T(8,128)(2,1)S(1)}, u32[]{:S(2)}, u32[]{:S(2)}) collective-permute-start(bf16[512,512]{1,0:T(8,128)(2,1)S(1)} %get-tuple-element.158), channel_id=1, source_target_pairs={{0,64},{32,96},{64,0},{96,32},{1,65},{33,97},{65,1},{97,33},{2,66}... | collective-permute-start | bytes 1572872 | tf_op jit(solution)/shard_map/ppermute | solution.py:393
  100.6 17.9 %collective-permute-start.22 = (bf16[4,192,512]{2,1,0:T(8,128)(2,1)S(1)}, bf16[4,192,512]{2,1,0:T(8,128)(2,1)S(1)}, u32[]{:S(2)}, u32[]{:S(2)}) collective-permute-start(bf16[4,192,512]{2,1,0:T(8,128)(2,1)S(1)} %get-tuple-element.169), channel_id=1, source_target_pairs={{0,16},{1,5},{2,18},{3,7},{4,20},{5,1},{6,22},{7,3},{8,24},{9,13},... | collective-permute-start | bytes 2359304 | tf_op jit(solution)/shard_map/ppermute | solution.py:393
  104.2 18.1 %collective-permute-start.23 = (bf16[4,192,512]{2,1,0:T(8,128)(2,1)S(1)}, bf16[4,192,512]{2,1,0:T(8,128)(2,1)S(1)}, u32[]{:S(2)}, u32[]{:S(2)}) collective-permute-start(bf16[4,192,512]{2,1,0:T(8,128)(2,1)S(1)} %get-tuple-element.170), channel_id=1, source_target_pairs={{0,8},{1,3},{2,10},{3,5},{4,12},{5,7},{6,14},{7,1},{8,16},{9,11},{... | collective-permute-start | bytes 2359304 | tf_op jit(solution)/shard_map/ppermute | solution.py:393
  104.9 18.1 %collective-permute-start.24 = (bf16[4,192,512]{2,1,0:T(8,128)(2,1)S(1)}, bf16[4,192,512]{2,1,0:T(8,128)(2,1)S(1)}, u32[]{:S(2)}, u32[]{:S(2)}) collective-permute-start(bf16[4,192,512]{2,1,0:T(8,128)(2,1)S(1)} %get-tuple-element.171), channel_id=1, source_target_pairs={{0,24},{1,7},{2,26},{3,1},{4,28},{5,3},{6,30},{7,5},{8,0},{9,15},{... | collective-permute-start | bytes 2359304 | tf_op jit(solution)/shard_map/ppermute | solution.py:393
  106.9 11.6 %collective-permute-start.25 = (bf16[512,512]{1,0:T(8,128)(2,1)S(1)}, bf16[512,512]{1,0:T(8,128)(2,1)S(1)}, u32[]{:S(2)}, u32[]{:S(2)}) collective-permute-start(bf16[512,512]{1,0:T(8,128)(2,1)S(1)} %get-tuple-element.173), channel_id=1, source_target_pairs={{0,96},{32,0},{64,32},{96,64},{1,97},{33,1},{65,33},{97,65},{2,98}... | collective-permute-start | bytes 1572872 | tf_op jit(solution)/shard_map/ppermute | solution.py:393
  109.6 19.4 %collective-permute-start.29 = (bf16[512,512]{1,0:T(8,128)(2,1)S(1)}, bf16[512,512]{1,0:T(8,128)(2,1)S(1)}, u32[]{:S(2)}, u32[]{:S(2)}) collective-permute-start(bf16[512,512]{1,0:T(8,128)(2,1)S(1)} %get-tuple-element.182), channel_id=1, source_target_pairs={{0,32},{32,64},{64,96},{96,0},{1,33},{33,65},{65,97},{97,1},{2,34}... | collective-permute-start | bytes 1572872 | tf_op jit(solution)/shard_map/ppermute | solution.py:393
  125.4 7.1 %collective-permute-start.28 = (f32[3,16,128]{2,1,0:T(8,128)S(1)}, f32[3,16,128]{2,1,0:T(8,128)S(1)}, u32[]{:S(2)}, u32[]{:S(2)}) collective-permute-start(f32[3,16,128]{2,1,0:T(8,128)S(1)} %gram.1), channel_id=1, source_target_pairs={{0,6},{1,7},{2,0},{3,1},{4,2},{5,3},{6,4},{7,5},{8,14},{9,15},{10,... | collective-permute-start | bytes 73736 | tf_op jit(solution)/shard_map/ppermute | solution.py:393
  127.8 4.7 %collective-permute-start.27 = (f32[3,16,128]{2,1,0:T(8,128)S(1)}, f32[3,16,128]{2,1,0:T(8,128)S(1)}, u32[]{:S(2)}, u32[]{:S(2)}) collective-permute-start(f32[3,16,128]{2,1,0:T(8,128)S(1)} %gram.1), channel_id=1, source_target_pairs={{0,2},{1,3},{2,4},{3,5},{4,6},{5,7},{6,0},{7,1},{8,10},{9,11},{10,... | collective-permute-start | bytes 73736 | tf_op jit(solution)/shard_map/ppermute | solution.py:393
  127.8 4.7 %collective-permute-start.26 = (f32[3,16,128]{2,1,0:T(8,128)S(1)}, f32[3,16,128]{2,1,0:T(8,128)S(1)}, u32[]{:S(2)}, u32[]{:S(2)}) collective-permute-start(f32[3,16,128]{2,1,0:T(8,128)S(1)} %gram.1), channel_id=1, source_target_pairs={{0,4},{1,5},{2,6},{3,7},{4,0},{5,1},{6,2},{7,3},{8,12},{9,13},{10,... | collective-permute-start | bytes 73736 | tf_op jit(solution)/shard_map/ppermute | solution.py:393
  132.5 11.8 %copy-start.3 = (f32[1,64,512]{2,1,0:T(8,128)S(1)}, f32[1,64,512]{2,1,0:T(8,128)}, u32[]{:S(2)}) copy-start(f32[1,64,512]{2,1,0:T(8,128)} %param.17) | copy-start | bytes 393220
  132.5 11.8 %copy-start.4 = (f32[1,64,512]{2,1,0:T(8,128)S(1)}, f32[1,64,512]{2,1,0:T(8,128)}, u32[]{:S(2)}) copy-start(f32[1,64,512]{2,1,0:T(8,128)} %param.18) | copy-start | bytes 393220
  132.5 11.8 %copy-start.5 = (f32[1,16,2048]{2,1,0:T(8,128)S(1)}, f32[1,16,2048]{2,1,0:T(8,128)}, u32[]{:S(2)}) copy-start(f32[1,16,2048]{2,1,0:T(8,128)} %param.19) | copy-start | bytes 393220
  132.6 7.2 %collective-permute-start.32 = (f32[3,16,128]{2,1,0:T(8,128)S(1)}, f32[3,16,128]{2,1,0:T(8,128)S(1)}, u32[]{:S(2)}, u32[]{:S(2)}) collective-permute-start(f32[3,16,128]{2,1,0:T(8,128)S(1)} %add_add_fusion.1), channel_id=1, source_target_pairs={{0,24},{1,25},{2,26},{3,27},{4,28},{5,29},{6,30},{7,31},{8,0},{9,1... | collective-permute-start | bytes 73736 | tf_op jit(solution)/shard_map/ppermute | solution.py:393
  135.0 4.7 %collective-permute-start.31 = (f32[3,16,128]{2,1,0:T(8,128)S(1)}, f32[3,16,128]{2,1,0:T(8,128)S(1)}, u32[]{:S(2)}, u32[]{:S(2)}) collective-permute-start(f32[3,16,128]{2,1,0:T(8,128)S(1)} %add_add_fusion.1), channel_id=1, source_target_pairs={{0,8},{1,9},{2,10},{3,11},{4,12},{5,13},{6,14},{7,15},{8,16},{9,17... | collective-permute-start | bytes 73736 | tf_op jit(solution)/shard_map/ppermute | solution.py:393
  135.0 4.7 %collective-permute-start.30 = (f32[3,16,128]{2,1,0:T(8,128)S(1)}, f32[3,16,128]{2,1,0:T(8,128)S(1)}, u32[]{:S(2)}, u32[]{:S(2)}) collective-permute-start(f32[3,16,128]{2,1,0:T(8,128)S(1)} %add_add_fusion.1), channel_id=1, source_target_pairs={{0,16},{1,17},{2,18},{3,19},{4,20},{5,21},{6,22},{7,23},{8,24},{9,... | collective-permute-start | bytes 73736 | tf_op jit(solution)/shard_map/ppermute | solution.py:393
  139.7 4.6 %collective-permute-start.33 = (f32[3,16,128]{2,1,0:T(8,128)S(1)}, f32[3,16,128]{2,1,0:T(8,128)S(1)}, u32[]{:S(2)}, u32[]{:S(2)}) collective-permute-start(f32[3,16,128]{2,1,0:T(8,128)S(1)} %add_add_fusion.g_ref), channel_id=1, source_target_pairs={{0,1},{1,0},{2,3},{3,2},{4,5},{5,4},{6,7},{7,6},{8,9},{9,8},{10,11... | collective-permute-start | bytes 73736 | tf_op jit(solution)/shard_map/ppermute | solution.py:393
